TPU v7x, 32 devices: a whole 2x2x4 slice. The times are simulated.
32 devices in a mesh: dp: 16 (over z, y, core), tensor: 2 (over x).
Axes of the slice: x: 2, y: 2, z: 4, core: 2. Of those that a mesh axis runs over, the one named last changes fastest.
Arguments:
- inputs: bfloat16 [2, 4096, 2048], P(None, ('dp', 'tensor')), may hold values from -6 to 6
- out_grad: bfloat16 [2, 4096, 2048], P(None, ('dp', 'tensor')), may hold values from -6 to 6
- deal_order: int32 [2, 4096], replicated, may hold values from 0 to 4095, as said below
- segment: int32 [2, 4096], P(None, 'dp'), may hold values from 0 to 2, as said below
- query_weight: bfloat16 [2048, 1024], P('dp', 'tensor'), may hold values from -0.125 to 0.125
- key_weight: bfloat16 [2048, 256], P('dp', 'tensor'), may hold values from -0.125 to 0.125
- value_weight: bfloat16 [2048, 256], P('dp', 'tensor'), may hold values from -0.125 to 0.125
- attention_out: bfloat16 [2048, 1024], P('dp', 'tensor'), may hold values from -0.75 to 0.75
- mamba_gate: bfloat16 [2048, 3072], P('dp', 'tensor'), may hold values from -0.125 to 0.125
- mamba_input: bfloat16 [2048, 3072], P('dp', 'tensor'), may hold values from -0.125 to 0.125
- step_weight: bfloat16 [2048, 48], P('dp', 'tensor'), may hold values from -0.125 to 0.125
- state_weight: bfloat16 [2048, 512], P('dp'), may hold values from -0.125 to 0.125
- mamba_out: bfloat16 [2048, 3072], P('dp', 'tensor'), may hold values from -0.109375 to 0.109375
- feed_gate: bfloat16 [2048, 4096], P('dp', 'tensor'), may hold values from -0.125 to 0.125
- feed_up: bfloat16 [2048, 4096], P('dp', 'tensor'), may hold values from -0.125 to 0.125
- feed_down: bfloat16 [2048, 4096], P('dp', 'tensor'), may hold values from -0.09375 to 0.09375
- gain_input: float32 [2048], replicated, may hold values from 0.5 to 1.5
- gain_middle: float32 [2048], replicated, may hold values from 0.5 to 1.5
- kernel_inner: float32 [5, 3072], P(None, 'tensor'), may hold values from -0.5 to 0.5
- kernel_state: float32 [5, 512], replicated, may hold values from -0.5 to 0.5
- mixer_gain: float32 [3072], P('tensor'), may hold values from 0.5 to 1.5
- step_bias: float32 [48], P('tensor'), may hold values from -6 to -2
- log_rate: float32 [48], P('tensor'), may hold values from -1 to 2
- skip_gain: float32 [48], P('tensor'), may hold values from 0.5 to 1.5
Outputs:
- block_out: bfloat16 [2, 4096, 2048], P(None, ('dp', 'tensor'))
- grad_input: bfloat16 [2, 4096, 2048], P(None, ('dp', 'tensor'))
- grad_query_weight: float32 [2048, 1024], P('dp', 'tensor')
- grad_key_weight: float32 [2048, 256], P('dp', 'tensor')
- grad_value_weight: float32 [2048, 256], P('dp', 'tensor')
- grad_attention_out: float32 [2048, 1024], P('dp', 'tensor')
- grad_mamba_gate: float32 [2048, 3072], P('dp', 'tensor')
- grad_mamba_input: float32 [2048, 3072], P('dp', 'tensor')
- grad_step_weight: float32 [2048, 48], P('dp', 'tensor')
- grad_state_weight: float32 [2048, 512], P(('dp', 'tensor'))
- grad_mamba_out: float32 [2048, 3072], P('dp', 'tensor')
- grad_feed_gate: float32 [2048, 4096], P('dp', 'tensor')
- grad_feed_up: float32 [2048, 4096], P('dp', 'tensor')
- grad_feed_down: float32 [2048, 4096], P('dp', 'tensor')
- grad_gain_input: float32 [2048], replicated
- grad_gain_middle: float32 [2048], replicated
- grad_kernel_inner: float32 [5, 3072], replicated
- grad_kernel_state: float32 [5, 512], replicated
- grad_mixer_gain: float32 [3072], replicated
- grad_step_bias: float32 [48], replicated
- grad_log_rate: float32 [48], replicated
- grad_skip_gain: float32 [48], replicated
Inputs may be any that keep to these rules, and one draw needn't show every extreme that they name: For each micro-batch a permutation of its rows: initial row r becomes dealt row deal_order[m, r]. The rows that device (i, t) holds in the initial order go to rows of devices (j, t) in the dealt order, exactly 8 to each j. `segment`: within each aligned block of 256 dealt rows the ids start at 0 and never fall.
All inputs are finite; a program needn't handle non-finite values.
Results may differ from a plain program's by a relative error of at most 0.017.
Values may be sent and summed in bfloat16 or wider, within the bound.
No kernel may reach another device: no remote copies, remote signals or barrier semaphores. Data moves between devices by JAX's collectives and lax.ppermute only.
A program may use at most 256 MiB of HBM per device.

v0:
```python
import math

import jax
import jax.numpy as jnp
from jax import lax
from jax.sharding import PartitionSpec as P

HEAD = 128
SH = 48
SHD = 64
NS = 256
CONV = 4


epsilon = 1e-05
rope_base = 100000000000.0


def project(left, right):
    return jnp.dot(left, right, preferred_element_type=jnp.float32)


def project_back(left, right):
    return lax.dot_general(
        left, right, (((1,), (1,)), ((), ())), preferred_element_type=jnp.float32
    )


def outer_sum(left, right):
    return lax.dot_general(
        left, right, (((0,), (0,)), ((), ())), preferred_element_type=jnp.float32
    )


def rms_norm(values, gain):
    return values * lax.rsqrt(jnp.mean(values * values, axis=-1, keepdims=True) + epsilon) * gain


def seq_layout(segment_rows):
    row_count = segment_rows.shape[0]
    before = jnp.sum((segment_rows[None, :] < segment_rows[:, None]).astype(jnp.int32), axis=1)
    places = jnp.arange(row_count, dtype=jnp.int32)
    allowed = (segment_rows[:, None] == segment_rows[None, :]) & (
        places[None, :] <= places[:, None]
    )
    return (places - before, allowed)


def rotate(values, position):
    half_size = values.shape[-1] // 2
    frequency = jnp.exp(
        jnp.arange(half_size, dtype=jnp.float32) * (-2.0 * math.log(rope_base) / values.shape[-1])
    )
    angles = position.astype(jnp.float32)[:, None] * frequency[None, :]
    cosine = jnp.cos(angles)[:, None, :]
    sine_val = jnp.sin(angles)[:, None, :]
    first_half = values[..., :half_size]
    second = values[..., half_size:]
    return jnp.concatenate(
        [first_half * cosine - second * sine_val, second * cosine + first_half * sine_val], axis=-1
    )


def conv_act(signal, kernel, position):
    summed = kernel[CONV][None, :] + signal * kernel[0][None, :]
    for shift_by in range(1, CONV):
        shifted = jnp.concatenate(
            [jnp.zeros((shift_by, signal.shape[1]), signal.dtype), signal[:-shift_by]], axis=0
        )
        summed = (
            summed
            + jnp.where((position >= shift_by)[:, None], shifted, 0.0) * kernel[shift_by][None, :]
        )
    return jax.nn.silu(summed)


def decay_scores(state_inner, raw_step, step_bias, log_rate, allowed):
    step_size = jax.nn.softplus(raw_step + step_bias)
    running = jnp.cumsum(step_size * -jnp.exp(log_rate), axis=0).T
    spread = running[:, :, None] - running[:, None, :]
    decayed = jnp.exp(jnp.where(allowed[None], spread, -jnp.inf))
    return state_inner[None] * decayed * step_size.T[:, None, :]


def swiglu(gate_value, up_value):
    return jax.nn.silu(gate_value) * up_value


def gate_mult(ssm_value, gate_value):
    return ssm_value * jax.nn.silu(gate_value)


def pad_slot(piece, full_size, slot_index, axis_number):
    shape_full = piece.shape[:axis_number] + (full_size,) + piece.shape[axis_number + 1 :]
    zeros_full = jnp.zeros(shape_full, jnp.float32)
    return lax.dynamic_update_slice_in_dim(
        zeros_full, piece, slot_index * piece.shape[axis_number], axis_number
    )


def sum_weights(grads):
    (
        g_query,
        g_key,
        g_value,
        g_attn,
        g_gate,
        g_input,
        g_step,
        g_state,
        g_mix,
        g_fgate,
        g_fup,
        g_fdown,
    ) = grads
    return (
        lax.psum_scatter(g_query, "dp", scatter_dimension=0, tiled=True),
        lax.psum_scatter(g_key, "dp", scatter_dimension=0, tiled=True),
        lax.psum_scatter(g_value, "dp", scatter_dimension=0, tiled=True),
        lax.psum_scatter(g_attn, "dp", scatter_dimension=0, tiled=True),
        lax.psum_scatter(g_gate, "dp", scatter_dimension=0, tiled=True),
        lax.psum_scatter(g_input, "dp", scatter_dimension=0, tiled=True),
        lax.psum_scatter(g_step, "dp", scatter_dimension=0, tiled=True),
        lax.psum_scatter(g_state, "dp", scatter_dimension=0, tiled=True),
        lax.psum_scatter(g_mix, "dp", scatter_dimension=0, tiled=True),
        lax.psum_scatter(g_fgate, "dp", scatter_dimension=0, tiled=True),
        lax.psum_scatter(g_fup, "dp", scatter_dimension=0, tiled=True),
        lax.psum_scatter(g_fdown, "dp", scatter_dimension=0, tiled=True),
    )


def local(
    inputs,
    out_grad,
    deal_order,
    segment,
    query_weight,
    key_weight,
    value_weight,
    attention_out,
    mamba_gate,
    mamba_input,
    step_weight,
    state_weight,
    mamba_out,
    feed_gate,
    feed_up,
    feed_down,
    gain_input,
    gain_middle,
    kernel_inner,
    kernel_state,
    mixer_gain,
    step_bias,
    log_rate,
    skip_gain,
):
    micro_count = inputs.shape[0]
    own_rows = inputs.shape[1]
    model_width = inputs.shape[2]
    group_count = lax.axis_size("dp")
    lane_count = lax.axis_size("tensor")
    lane_index = lax.axis_index("tensor")
    device_index = lax.axis_index("dp") * lane_count + lane_index
    per_group = own_rows // group_count
    all_rows = own_rows * lane_count
    inner_width = SH * SHD
    scale_factor = HEAD ** (-0.5)
    local_places = jnp.arange(own_rows, dtype=jnp.int32)
    outputs = []
    input_grads = []
    weight_totals = None
    small_totals = None
    for micro_step in range(micro_count):
        order_now = deal_order[micro_step]
        own_order = lax.dynamic_slice_in_dim(order_now, device_index * own_rows, own_rows)
        send_order = jnp.argsort(own_order)
        inverse = (
            jnp.zeros_like(order_now)
            .at[order_now]
            .set(jnp.arange(order_now.shape[0], dtype=jnp.int32))
        )
        sources = lax.dynamic_slice_in_dim(inverse, device_index * own_rows, own_rows)
        recv_order = jnp.argsort(sources // (own_rows * lane_count) * own_rows + local_places)
        place_back = jnp.argsort(recv_order)
        got_rows, got_grad = (
            lax.all_to_all(
                inputs[micro_step][send_order].reshape(group_count, per_group, model_width),
                "dp",
                split_axis=0,
                concat_axis=0,
                tiled=True,
            ),
            lax.all_to_all(
                out_grad[micro_step][send_order].reshape(group_count, per_group, model_width),
                "dp",
                split_axis=0,
                concat_axis=0,
                tiled=True,
            ),
        )
        own_in = got_rows.reshape(own_rows, model_width)[place_back]
        own_grad = got_grad.reshape(own_rows, model_width)[place_back]
        (
            full_query,
            full_key,
            full_value,
            full_attn,
            full_gate,
            full_input,
            full_step,
            full_state,
            full_mix,
            full_fgate,
            full_fup,
            full_fdown,
        ) = (
            lax.all_gather(query_weight, "dp", axis=0, tiled=True),
            lax.all_gather(key_weight, "dp", axis=0, tiled=True),
            lax.all_gather(value_weight, "dp", axis=0, tiled=True),
            lax.all_gather(attention_out, "dp", axis=0, tiled=True),
            lax.all_gather(mamba_gate, "dp", axis=0, tiled=True),
            lax.all_gather(mamba_input, "dp", axis=0, tiled=True),
            lax.all_gather(step_weight, "dp", axis=0, tiled=True),
            lax.all_gather(state_weight, "dp", axis=0, tiled=True),
            lax.all_gather(mamba_out, "dp", axis=0, tiled=True),
            lax.all_gather(feed_gate, "dp", axis=0, tiled=True),
            lax.all_gather(feed_up, "dp", axis=0, tiled=True),
            lax.all_gather(feed_down, "dp", axis=0, tiled=True),
        )
        position, allowed = seq_layout(segment[micro_step])
        whole_in, whole_grad = (
            lax.all_gather(own_in, "tensor", axis=0, tiled=True),
            lax.all_gather(own_grad, "tensor", axis=0, tiled=True),
        )
        normed, norm_pull = jax.vjp(rms_norm, whole_in.astype(jnp.float32), gain_input)
        normed_low = normed.astype(jnp.bfloat16)
        gate_z = project(normed_low, full_gate)
        ssm_in = project(normed_low, full_input)
        raw_step = project(normed_low, full_step)
        state_raw = project(normed_low, full_state)
        ssm_cols, inner_pull = jax.vjp(
            lambda signal_in, kernel: conv_act(signal_in, kernel, position), ssm_in, kernel_inner
        )
        state_act, state_pull = jax.vjp(
            lambda signal_in, kernel: conv_act(signal_in, kernel, position), state_raw, kernel_state
        )
        b_state = state_act[:, :NS].astype(jnp.bfloat16)
        c_state = state_act[:, NS:].astype(jnp.bfloat16)
        state_inner = project_back(c_state, b_state)
        mixing, decay_pull = jax.vjp(
            lambda inner_in, raw_in, bias_in, rate_in: decay_scores(
                inner_in, raw_in, bias_in, rate_in, allowed
            ),
            state_inner,
            raw_step,
            step_bias,
            log_rate,
        )
        mixing_low = mixing.astype(jnp.bfloat16)
        heads_here = raw_step.shape[1]
        ssm_heads = ssm_cols.reshape(all_rows, heads_here, SHD)
        heads_low = ssm_heads.astype(jnp.bfloat16)
        ssm_out = (
            jnp.einsum("hij,jhd->ihd", mixing_low, heads_low, preferred_element_type=jnp.float32)
            + skip_gain[None, :, None] * ssm_heads
        ).reshape(all_rows, -1)
        gated, gate_pull = jax.vjp(gate_mult, ssm_out, gate_z)
        square_sum = lax.psum(jnp.sum(gated * gated, axis=1), "tensor")
        inv_rms = lax.rsqrt(square_sum / inner_width + epsilon)[:, None]
        gated_low = (gated * inv_rms * mixer_gain).astype(jnp.bfloat16)
        branch_part = project_back(gated_low, full_mix)
        query_raw = project(normed_low, full_query).reshape(all_rows, -1, HEAD)
        key_raw = project(normed_low, full_key).reshape(all_rows, -1, HEAD)
        value_low = project(normed_low, full_value).astype(jnp.bfloat16).reshape(all_rows, -1, HEAD)
        query_rot, query_pull = jax.vjp(lambda values_in: rotate(values_in, position), query_raw)
        key_rot, key_pull = jax.vjp(lambda values_in: rotate(values_in, position), key_raw)
        kv_here = key_raw.shape[1]
        query_low = query_rot.astype(jnp.bfloat16).reshape(all_rows, kv_here, -1, HEAD)
        key_low = key_rot.astype(jnp.bfloat16)
        logits = (
            jnp.einsum("igkd,jgd->gkij", query_low, key_low, preferred_element_type=jnp.float32)
            * scale_factor
        )
        logits = jnp.where(allowed[None, None], logits, -jnp.inf)
        row_max = jnp.max(logits, axis=-1, keepdims=True)
        exp_scores = jnp.exp(logits - row_max)
        attention_weights = exp_scores / jnp.sum(exp_scores, axis=-1, keepdims=True)
        weights_low = attention_weights.astype(jnp.bfloat16)
        attended_low = (
            jnp.einsum("gkij,jgd->igkd", weights_low, value_low, preferred_element_type=jnp.float32)
            .astype(jnp.bfloat16)
            .reshape(all_rows, -1)
        )
        branch_part = branch_part + project_back(attended_low, full_attn)
        branch = lax.psum_scatter(branch_part, "tensor", scatter_dimension=0, tiled=True)
        middle = (own_in.astype(jnp.float32) + branch).astype(jnp.bfloat16)
        whole_mid = lax.all_gather(middle, "tensor", axis=0, tiled=True)
        normed_mid, mid_pull = jax.vjp(rms_norm, whole_mid.astype(jnp.float32), gain_middle)
        mid_low = normed_mid.astype(jnp.bfloat16)
        gate_ff = project(mid_low, full_fgate)
        up_ff = project(mid_low, full_fup)
        hidden, swiglu_pull = jax.vjp(swiglu, gate_ff, up_ff)
        hidden_low = hidden.astype(jnp.bfloat16)
        ffn_out = lax.psum_scatter(
            project_back(hidden_low, full_fdown).astype(jnp.bfloat16),
            "tensor",
            scatter_dimension=0,
            tiled=True,
        ).astype(jnp.float32)
        out_rows = (middle.astype(jnp.float32) + ffn_out).astype(jnp.bfloat16)
        grad_hidden = project(whole_grad, full_fdown)
        grad_fdown = outer_sum(whole_grad, hidden_low)
        grad_gate_ff, grad_up_ff = swiglu_pull(grad_hidden)
        gate_ff_low = grad_gate_ff.astype(jnp.bfloat16)
        up_ff_low = grad_up_ff.astype(jnp.bfloat16)
        grad_fgate = outer_sum(mid_low, gate_ff_low)
        grad_fup = outer_sum(mid_low, up_ff_low)
        grad_mid_norm = project_back(gate_ff_low, full_fgate) + project_back(up_ff_low, full_fup)
        grad_mid_part, grad_gain_mid = mid_pull(grad_mid_norm)
        grad_middle = lax.psum_scatter(
            grad_mid_part, "tensor", scatter_dimension=0, tiled=True
        ) + own_grad.astype(jnp.float32)
        whole_branch = lax.all_gather(
            grad_middle.astype(jnp.bfloat16), "tensor", axis=0, tiled=True
        )
        grad_gated_norm = project(whole_branch, full_mix)
        grad_mix = outer_sum(whole_branch, gated_low)
        scaled_grad = grad_gated_norm * mixer_gain
        grad_mixer = jnp.sum(grad_gated_norm * gated * inv_rms, axis=0)
        cross_sum = lax.psum(jnp.sum(scaled_grad * gated, axis=1), "tensor")
        grad_gated = inv_rms * scaled_grad - gated * inv_rms**3 * cross_sum[:, None] / inner_width
        grad_ssm_out, grad_gate_z = gate_pull(grad_gated)
        grad_heads = grad_ssm_out.reshape(all_rows, heads_here, SHD)
        grad_heads_low = grad_heads.astype(jnp.bfloat16)
        grad_ssm_cols = (
            jnp.einsum(
                "hij,ihd->jhd", mixing_low, grad_heads_low, preferred_element_type=jnp.float32
            )
            + skip_gain[None, :, None] * grad_heads
        ).reshape(all_rows, -1)
        grad_skip = jnp.sum(grad_heads * ssm_heads, axis=(0, 2))
        grad_mixing = jnp.einsum(
            "ihd,jhd->hij", grad_heads_low, heads_low, preferred_element_type=jnp.float32
        )
        grad_inner, grad_raw_step, grad_bias, grad_rate = decay_pull(grad_mixing)
        inner_low = grad_inner.astype(jnp.bfloat16)
        grad_c_state = project(inner_low, b_state)
        grad_b_state = outer_sum(inner_low, c_state)
        grad_state_raw, grad_kernel_state = state_pull(
            jnp.concatenate([grad_b_state, grad_c_state], axis=1)
        )
        grad_ssm_in, grad_kernel_inner = inner_pull(grad_ssm_cols)
        gate_low = grad_gate_z.astype(jnp.bfloat16)
        input_low = grad_ssm_in.astype(jnp.bfloat16)
        step_low = grad_raw_step.astype(jnp.bfloat16)
        state_low = grad_state_raw.astype(jnp.bfloat16)
        grad_gate_w = outer_sum(normed_low, gate_low)
        grad_input_w = outer_sum(normed_low, input_low)
        grad_step_w = outer_sum(normed_low, step_low)
        grad_state_w = outer_sum(normed_low, state_low)
        grad_normed = project_back(gate_low, full_gate) + project_back(input_low, full_input)
        grad_normed = (
            grad_normed + project_back(step_low, full_step) + project_back(state_low, full_state)
        )
        grad_attended = (
            project(whole_branch, full_attn)
            .astype(jnp.bfloat16)
            .reshape(all_rows, kv_here, -1, HEAD)
        )
        grad_attn = outer_sum(whole_branch, attended_low)
        grad_weights = jnp.einsum(
            "igkd,jgd->gkij", grad_attended, value_low, preferred_element_type=jnp.float32
        )
        grad_value = jnp.einsum(
            "gkij,igkd->jgd", weights_low, grad_attended, preferred_element_type=jnp.float32
        )
        weighted_sum = jnp.sum(attention_weights * grad_weights, axis=-1, keepdims=True)
        grad_logits = (attention_weights * (grad_weights - weighted_sum)).astype(jnp.bfloat16)
        grad_query_rot = (
            jnp.einsum("gkij,jgd->igkd", grad_logits, key_low, preferred_element_type=jnp.float32)
            * scale_factor
        )
        grad_key_rot = (
            jnp.einsum("gkij,igkd->jgd", grad_logits, query_low, preferred_element_type=jnp.float32)
            * scale_factor
        )
        (grad_query_raw,) = query_pull(grad_query_rot.reshape(all_rows, -1, HEAD))
        (grad_key_raw,) = key_pull(grad_key_rot)
        query_grad_low = grad_query_raw.reshape(all_rows, -1).astype(jnp.bfloat16)
        key_grad_low = grad_key_raw.reshape(all_rows, -1).astype(jnp.bfloat16)
        value_grad_low = grad_value.reshape(all_rows, -1).astype(jnp.bfloat16)
        grad_query_w = outer_sum(normed_low, query_grad_low)
        grad_key_w = outer_sum(normed_low, key_grad_low)
        grad_value_w = outer_sum(normed_low, value_grad_low)
        grad_normed = (
            grad_normed
            + project_back(query_grad_low, full_query)
            + project_back(key_grad_low, full_key)
        )
        grad_normed = grad_normed + project_back(value_grad_low, full_value)
        grad_in_part, grad_gain_in = norm_pull(grad_normed)
        state_order = (
            grad_state_w.reshape(group_count, lane_count, -1, grad_state_w.shape[1])
            .transpose(1, 0, 2, 3)
            .reshape(grad_state_w.shape)
        )
        grad_rows, grad_state_lane = (
            lax.psum_scatter(
                grad_in_part.astype(jnp.bfloat16), "tensor", scatter_dimension=0, tiled=True
            ).astype(jnp.float32),
            lax.psum_scatter(
                state_order.astype(jnp.bfloat16), "tensor", scatter_dimension=0, tiled=True
            ).astype(jnp.float32),
        )
        in_grad_rows = (grad_rows + grad_middle).astype(jnp.bfloat16)
        ship_out, ship_grad = (
            lax.all_to_all(
                out_rows[recv_order].reshape(group_count, per_group, model_width),
                "dp",
                split_axis=0,
                concat_axis=0,
                tiled=True,
            ),
            lax.all_to_all(
                in_grad_rows[recv_order].reshape(group_count, per_group, model_width),
                "dp",
                split_axis=0,
                concat_axis=0,
                tiled=True,
            ),
        )
        restore = jnp.argsort(send_order)
        outputs.append(ship_out.reshape(own_rows, model_width)[restore])
        input_grads.append(ship_grad.reshape(own_rows, model_width)[restore])
        small_now = (
            grad_gain_in,
            grad_gain_mid,
            pad_slot(grad_kernel_inner, inner_width, lane_index, 1),
            grad_kernel_state,
            pad_slot(grad_mixer, inner_width, lane_index, 0),
            pad_slot(grad_bias, SH, lane_index, 0),
            pad_slot(grad_rate, SH, lane_index, 0),
            pad_slot(grad_skip, SH, lane_index, 0),
        )
        small_totals = (
            small_now if small_totals is None else jax.tree.map(jnp.add, small_totals, small_now)
        )
        big_now = (
            grad_query_w,
            grad_key_w,
            grad_value_w,
            grad_attn,
            grad_gate_w,
            grad_input_w,
            grad_step_w,
            grad_state_lane,
            grad_mix,
            grad_fgate,
            grad_fup,
            grad_fdown,
        )
        shard_now = sum_weights(big_now)
        weight_totals = (
            shard_now if weight_totals is None else jax.tree.map(jnp.add, weight_totals, shard_now)
        )
    small_gin, small_gmid, small_kin, small_kst, small_mix, small_bias, small_rate, small_skip = (
        small_totals
    )
    sum_gin, sum_gmid, sum_kin, sum_kst, sum_mix, sum_bias, sum_rate, sum_skip = lax.psum(
        (
            small_gin,
            small_gmid,
            small_kin,
            small_kst,
            small_mix,
            small_bias,
            small_rate,
            small_skip,
        ),
        ("dp", "tensor"),
    )
    block_out = jnp.stack(outputs)
    grad_input = jnp.stack(input_grads)
    return (
        block_out,
        grad_input,
        weight_totals[0],
        weight_totals[1],
        weight_totals[2],
        weight_totals[3],
        weight_totals[4],
        weight_totals[5],
        weight_totals[6],
        weight_totals[7],
        weight_totals[8],
        weight_totals[9],
        weight_totals[10],
        weight_totals[11],
        sum_gin,
        sum_gmid,
        sum_kin,
        sum_kst,
        sum_mix,
        sum_bias,
        sum_rate,
        sum_skip,
    )


def solution(mesh):
    in_specs = (
        P(None, ("dp", "tensor"), None),
        P(None, ("dp", "tensor"), None),
        P(),
        P(None, "dp"),
        P("dp", "tensor"),
        P("dp", "tensor"),
        P("dp", "tensor"),
        P("dp", "tensor"),
        P("dp", "tensor"),
        P("dp", "tensor"),
        P("dp", "tensor"),
        P("dp", None),
        P("dp", "tensor"),
        P("dp", "tensor"),
        P("dp", "tensor"),
        P("dp", "tensor"),
        P(),
        P(),
        P(None, "tensor"),
        P(),
        P("tensor"),
        P("tensor"),
        P("tensor"),
        P("tensor"),
    )
    out_specs = (
        P(None, ("dp", "tensor"), None),
        P(None, ("dp", "tensor"), None),
        P("dp", "tensor"),
        P("dp", "tensor"),
        P("dp", "tensor"),
        P("dp", "tensor"),
        P("dp", "tensor"),
        P("dp", "tensor"),
        P("dp", "tensor"),
        P(("dp", "tensor"), None),
        P("dp", "tensor"),
        P("dp", "tensor"),
        P("dp", "tensor"),
        P("dp", "tensor"),
        P(),
        P(),
        P(),
        P(),
        P(),
        P(),
        P(),
        P(),
    )
    return jax.shard_map(local, mesh=mesh, in_specs=in_specs, out_specs=out_specs, check_vma=False)
```

profile of v0, /device:TPU:0, one launch (start us, length us, event | category | flops | bytes accessed | tf_op | source)
XLA Modules:
  0.0 2670.9 jit_solution(5800463079309955428)
XLA Ops:
  13.4 7.4 all-to-all-start
  20.9 15.5 scatter_custom_fusion
  47.7 6.0 all-to-all-start.2
  53.8 15.5 scatter_custom_fusion.1
  82.8 23.3 all_gather.75
  108.3 20.0 all_gather.78
  128.3 20.5 all_gather.79
  197.7 53.0 %all-gather.22.cloned.1.call-done = bf16[2048,1536]{1,0:T(8,128)(2,1)} async-done(((bf16[128,1536]{1,0:T(8,128)(2,1)}), bf16[2048,1536]{1,0:T(8,128)(2,1)}) %all-gather.22.cloned.1.call-update) | async-done | bytes 6291472 | tf_op jit(solution)/shard_map/all_gather | solution.py:223
  257.5 5.5 fusion.67
  284.7 28.5 %all-gather.26.cloned.1.call-done = bf16[2048,1536]{1,0:T(8,128)(2,1)} async-done(((bf16[128,1536]{1,0:T(8,128)(2,1)}), bf16[2048,1536]{1,0:T(8,128)(2,1)}) %all-gather.26.cloned.1.call-update) | async-done | bytes 6291472 | tf_op jit(solution)/shard_map/all_gather | solution.py:222
  313.2 7.0 multiply_reduce_fusion.18
  329.1 46.9 %all-gather.28.cloned.1.call-done = bf16[2048,1536]{1,0:T(8,128)(2,1)} async-done(((bf16[128,1536]{1,0:T(8,128)(2,1)}), bf16[2048,1536]{1,0:T(8,128)(2,1)}) %all-gather.28.cloned.1.call-update) | async-done | bytes 6291472 | tf_op jit(solution)/shard_map/all_gather | solution.py:226
  376.0 6.5 fusion.234
  382.5 35.7 %all-gather.32.cloned.1.call-done = bf16[2048,512]{1,0:T(8,128)(2,1)} async-done(((bf16[128,512]{1,0:T(8,128)(2,1)}), bf16[2048,512]{1,0:T(8,128)(2,1)}) %all-gather.32.cloned.1.call-update) | async-done | bytes 2097168 | tf_op jit(solution)/shard_map/all_gather | solution.py:221
  436.0 17.3 reduce-scatter.27.cloned.1.call-done
  455.5 31.8 %reduce-scatter.23.cloned.1.call-done = f32[128,2048]{1,0:T(8,128)} async-done(((f32[256,2048]{1,0:T(8,128)}), f32[128,2048]{1,0:T(8,128)}) %reduce-scatter.23.cloned.1.call-update) | async-done | bytes 1048592 | tf_op jit(solution)/shard_map/reduce_scatter | solution.py:296
  494.0 20.1 all_to_all.40
  517.6 18.4 all_to_all.41
  541.3 68.8 %all-gather.36.cloned.1.call-done = bf16[2048,2048]{1,0:T(8,128)(2,1)} async-done(((bf16[128,2048]{1,0:T(8,128)(2,1)}), bf16[2048,2048]{1,0:T(8,128)(2,1)}) %all-gather.36.cloned.1.call-update) | async-done | bytes 8388624 | tf_op jit(solution)/shard_map/all_gather | solution.py:227
  610.1 7.2 fusion.251
  617.2 68.0 %all-gather.38.cloned.1.call-done = bf16[2048,2048]{1,0:T(8,128)(2,1)} async-done(((bf16[128,2048]{1,0:T(8,128)(2,1)}), bf16[2048,2048]{1,0:T(8,128)(2,1)}) %all-gather.38.cloned.1.call-update) | async-done | bytes 8388624 | tf_op jit(solution)/shard_map/all_gather | solution.py:228
  685.3 7.2 fusion.249
  696.2 10.0 all-gather.54.cloned.1.call-done
  706.2 77.0 %all-gather.40.cloned.1.call-done = bf16[2048,2048]{1,0:T(8,128)(2,1)} async-done(((bf16[128,2048]{1,0:T(8,128)(2,1)}), bf16[2048,2048]{1,0:T(8,128)(2,1)}) %all-gather.40.cloned.1.call-update) | async-done | bytes 8388624 | tf_op jit(solution)/shard_map/all_gather | solution.py:229
  783.2 9.2 multiply_convert_fusion.6
  792.4 7.6 fusion.315
  800.0 7.5 fusion.243
  807.5 8.9 multiply_convert_fusion.7
  816.3 6.5 fusion.312
  822.9 5.9 convolution_add_fusion.16
  836.8 29.6 %reduce-scatter.35.cloned.1.call-done = f32[128,2048]{1,0:T(8,128)} async-done(((f32[256,2048]{1,0:T(8,128)}), f32[128,2048]{1,0:T(8,128)}) %reduce-scatter.35.cloned.1.call-update) | async-done | bytes 1048592 | tf_op jit(solution)/shard_map/reduce_scatter | solution.py:321
  868.6 31.9 %reduce-scatter.31.cloned.1.call-done = f32[128,2048]{1,0:T(8,128)} async-done(((f32[256,2048]{1,0:T(8,128)}), f32[128,2048]{1,0:T(8,128)}) %reduce-scatter.31.cloned.1.call-update) | async-done | bytes 1048592 | tf_op jit(solution)/shard_map/reduce_scatter | solution.py:321
  906.6 17.2 all-gather.46.cloned.1.call-done
  923.8 6.1 fusion.316
  930.0 17.4 all-gather.44.cloned.1.call-done
  947.3 8.3 multiply_reduce_fusion.7
  960.6 9.0 multiply_reduce_fusion.5
  972.7 6.6 fusion.3
  982.8 6.7 fusion.5
  1000.0 7.4 convolution_convert_fusion.2
  1007.5 7.2 convolution_convert_fusion.3
  1133.0 6.6 convolution_add_fusion.2
  1142.9 6.6 convolution_add_fusion.1
  1154.1 6.5 convolution_add_fusion
  1165.6 9.7 convolution_add_fusion.5
  1179.1 9.6 convolution_add_fusion.4
  1193.6 8.3 convolution_add_fusion.3
  1205.9 5.6 all-to-all-start.3
  1214.5 11.7 all-to-all-done.3
  1233.5 11.6 all-to-all-done.1
  1252.7 11.2 all-to-all-done.7
  1277.1 6.9 all-to-all-done.5
  1289.6 60.0 %reduce-scatter.55.cloned.1.call-done = f32[128,24]{0,1:T(8,128)} async-done(((f32[2048,24]{0,1:T(8,128)}), f32[128,24]{0,1:T(8,128)}) %reduce-scatter.55.cloned.1.call-update) | async-done | bytes 12304 | tf_op jit(solution)/shard_map/reduce_scatter | solution.py:123
  1349.6 60.5 %reduce-scatter.45.cloned.1.call-done = f32[128,128]{1,0:T(8,128)} async-done(((f32[2048,128]{1,0:T(8,128)}), f32[128,128]{1,0:T(8,128)}) %reduce-scatter.45.cloned.1.call-update) | async-done | bytes 65552 | tf_op jit(solution)/shard_map/reduce_scatter | solution.py:118
  1410.2 61.1 %reduce-scatter.47.cloned.1.call-done = f32[128,128]{1,0:T(8,128)} async-done(((f32[2048,128]{1,0:T(8,128)}), f32[128,128]{1,0:T(8,128)}) %reduce-scatter.47.cloned.1.call-update) | async-done | bytes 65552 | tf_op jit(solution)/shard_map/reduce_scatter | solution.py:119
  1471.3 75.9 %reduce-scatter.43.cloned.1.call-done = f32[128,512]{1,0:T(8,128)} async-done(((f32[2048,512]{1,0:T(8,128)}), f32[128,512]{1,0:T(8,128)}) %reduce-scatter.43.cloned.1.call-update) | async-done | bytes 262160 | tf_op jit(solution)/shard_map/reduce_scatter | solution.py:117
  1547.2 76.5 %reduce-scatter.49.cloned.1.call-done = f32[128,512]{1,0:T(8,128)} async-done(((f32[2048,512]{1,0:T(8,128)}), f32[128,512]{1,0:T(8,128)}) %reduce-scatter.49.cloned.1.call-update) | async-done | bytes 262160 | tf_op jit(solution)/shard_map/reduce_scatter | solution.py:120
  1623.7 64.9 %reduce-scatter.57.cloned.1.call-done = f32[64,512]{1,0:T(8,128)} async-done(((f32[1024,512]{1,0:T(8,128)}), f32[64,512]{1,0:T(8,128)}) %reduce-scatter.57.cloned.1.call-update) | async-done | bytes 131088 | tf_op jit(solution)/shard_map/reduce_scatter | solution.py:124
  1688.6 138.8 %reduce-scatter.51.cloned.1.call-done = f32[128,1536]{1,0:T(8,128)} async-done(((f32[2048,1536]{1,0:T(8,128)}), f32[128,1536]{1,0:T(8,128)}) %reduce-scatter.51.cloned.1.call-update) | async-done | bytes 786448 | tf_op jit(solution)/shard_map/reduce_scatter | solution.py:121
  1827.4 138.9 %reduce-scatter.53.cloned.1.call-done = f32[128,1536]{1,0:T(8,128)} async-done(((f32[2048,1536]{1,0:T(8,128)}), f32[128,1536]{1,0:T(8,128)}) %reduce-scatter.53.cloned.1.call-update) | async-done | bytes 786448 | tf_op jit(solution)/shard_map/reduce_scatter | solution.py:122
  1966.4 138.9 %reduce-scatter.59.cloned.1.call-done = f32[128,1536]{1,0:T(8,128)} async-done(((f32[2048,1536]{1,0:T(8,128)}), f32[128,1536]{1,0:T(8,128)}) %reduce-scatter.59.cloned.1.call-update) | async-done | bytes 786448 | tf_op jit(solution)/shard_map/reduce_scatter | solution.py:125
  2105.2 182.9 %reduce-scatter.61.cloned.1.call-done = f32[128,2048]{1,0:T(8,128)} async-done(((f32[2048,2048]{1,0:T(8,128)}), f32[128,2048]{1,0:T(8,128)}) %reduce-scatter.61.cloned.1.call-update) | async-done | bytes 1048592 | tf_op jit(solution)/shard_map/reduce_scatter | solution.py:126
  2288.2 182.7 %reduce-scatter.63.cloned.1.call-done = f32[128,2048]{1,0:T(8,128)} async-done(((f32[2048,2048]{1,0:T(8,128)}), f32[128,2048]{1,0:T(8,128)}) %reduce-scatter.63.cloned.1.call-update) | async-done | bytes 1048592 | tf_op jit(solution)/shard_map/reduce_scatter | solution.py:127
  2470.8 182.8 %reduce-scatter.65.cloned.1.call-done = f32[128,2048]{1,0:T(8,128)} async-done(((f32[2048,2048]{1,0:T(8,128)}), f32[128,2048]{1,0:T(8,128)}) %reduce-scatter.65.cloned.1.call-update) | async-done | bytes 1048592 | tf_op jit(solution)/shard_map/reduce_scatter | solution.py:128
  (1032 shorter events, 383.4 us)
Async XLA Ops:
  13.4 30.8 %all-to-all-start = ((bf16[16,8,2048]{2,1,0:T(8,128)(2,1)}), bf16[16,8,2048]{2,1,0:T(8,128)(2,1)S(1)}, u32[]{:S(2)}, u32[]{:S(2)}) async-start(bf16[16,8,2048]{2,1,0:T(8,128)(2,1)} %bitcast.2), calls=%async_computation | async-start | bytes 1048576 | tf_op jit(solution)/shard_map/all_to_all | solution.py:187
  20.8 129.6 %all-gather.48.cloned.1.call-start = ((), (), s32[]{:S(2)}) async-start(), calls=%async_computation.53 | async-start | bytes 1572864 | tf_op jit(solution)/shard_map/all_gather | solution.py:233
  47.7 26.8 %all-to-all-start.2 = ((bf16[16,8,2048]{2,1,0:T(8,128)(2,1)}), bf16[16,8,2048]{2,1,0:T(8,128)(2,1)S(1)}, u32[]{:S(2)}, u32[]{:S(2)}) async-start(bf16[16,8,2048]{2,1,0:T(8,128)(2,1)} %bitcast.33), calls=%async_computation.4 | async-start | bytes 1048576 | tf_op jit(solution)/shard_map/all_to_all | solution.py:187
  53.7 98.9 %all-gather.50.cloned.1.call-start = ((), (), s32[]{:S(2)}) async-start(), calls=%async_computation.54 | async-start | bytes 1572864 | tf_op jit(solution)/shard_map/all_gather | solution.py:233
  76.3 100.3 %all-gather.24.cloned.1.call-start = ((), (), s32[]{:S(2)}) async-start(), calls=%async_computation.31 | async-start | bytes 2228224 | tf_op jit(solution)/shard_map/all_gather | solution.py:225
  77.1 111.0 %all-gather.30.cloned.1.call-start = ((), (), s32[]{:S(2)}) async-start(), calls=%async_computation.34 | async-start | bytes 2228224 | tf_op jit(solution)/shard_map/all_gather | solution.py:218
  77.6 173.0 %all-gather.22.cloned.1.call-start = ((), (), s32[]{:S(2)}) async-start(), calls=%async_computation.30 | async-start | bytes 6684672 | tf_op jit(solution)/shard_map/all_gather | solution.py:223
  78.2 235.0 %all-gather.26.cloned.1.call-start = ((), (), s32[]{:S(2)}) async-start(), calls=%async_computation.32 | async-start | bytes 6684672 | tf_op jit(solution)/shard_map/all_gather | solution.py:222
  78.8 297.2 %all-gather.28.cloned.1.call-start = ((), (), s32[]{:S(2)}) async-start(), calls=%async_computation.33 | async-start | bytes 6684672 | tf_op jit(solution)/shard_map/all_gather | solution.py:226
  79.5 338.7 %all-gather.32.cloned.1.call-start = ((), (), s32[]{:S(2)}) async-start(), calls=%async_computation.35 | async-start | bytes 2228224 | tf_op jit(solution)/shard_map/all_gather | solution.py:221
  80.3 373.0 %reduce-scatter.27.cloned.1.call-start = ((), (), s32[]{:S(2)}) async-start(), calls=%async_computation.42 | async-start | bytes 3145728 | tf_op jit(solution)/shard_map/reduce_scatter | solution.py:296
  80.6 71.4 %copy-start.111 = (pred[256,256]{0,1:T(8,128)(4,1)}, pred[256,256]{0,1:T(8,128)(4,1)S(1)}, u32[]{:S(2)}) copy-start(pred[256,256]{0,1:T(8,128)(4,1)S(1)} %fusion.124) | copy-start | bytes 196612
  80.8 71.2 %copy-start.109 = (pred[256,256]{0,1:T(8,128)(4,1)}, pred[256,256]{0,1:T(8,128)(4,1)S(1)}, u32[]{:S(2)}) copy-start(pred[256,256]{0,1:T(8,128)(4,1)S(1)} %fusion.125) | copy-start | bytes 196612
  80.9 71.2 %copy-start.269 = (f32[64]{0:T(128)}, f32[64]{0:T(128)S(1)}, u32[]{:S(2)}) copy-start(f32[64]{0:T(128)S(1)} %multiply_exponential_fusion) | copy-start | bytes 772
  81.5 70.6 %copy-start.210 = (f32[256]{0:T(256)}, f32[256]{0:T(256)S(1)}, u32[]{:S(2)}) copy-start(f32[256]{0:T(256)S(1)} %get-tuple-element.252) | copy-start | bytes 3076
  81.5 70.6 %copy-start.212 = (f32[256]{0:T(256)}, f32[256]{0:T(256)S(1)}, u32[]{:S(2)}) copy-start(f32[256]{0:T(256)S(1)} %get-tuple-element.253) | copy-start | bytes 3076
  81.5 72.7 %copy-start.54 = (f32[2048]{0:T(1024)S(1)}, f32[2048]{0:T(1024)}, u32[]{:S(2)}) copy-start(f32[2048]{0:T(1024)} %param.41) | copy-start | bytes 24580
  128.3 294.7 %copy-start.51 = (bf16[2048,128]{1,0:T(8,128)(2,1)}, bf16[2048,128]{1,0:T(8,128)(2,1)S(1)}, u32[]{:S(2)}) copy-start(bf16[2048,128]{1,0:T(8,128)(2,1)S(1)} %all_gather.78) | copy-start | bytes 1572868
  150.3 275.6 %copy-start.79 = (f32[256,64]{1,0:T(8,128)}, f32[256,64]{1,0:T(8,128)S(1)}, u32[]{:S(2)}) copy-start(f32[256,64]{1,0:T(8,128)S(1)} %get-tuple-element.209) | copy-start | bytes 196612
  150.3 275.6 %copy-start.81 = (f32[256,64]{1,0:T(8,128)}, f32[256,64]{1,0:T(8,128)S(1)}, u32[]{:S(2)}) copy-start(f32[256,64]{1,0:T(8,128)S(1)} %get-tuple-element.210) | copy-start | bytes 196612
  196.6 54.0 %copy-start.206 = (f32[4,256]{1,0:T(4,128)}, f32[4,256]{1,0:T(4,128)S(1)}, u32[]{:S(2)}) copy-start(f32[4,256]{1,0:T(4,128)S(1)} %fusion.87) | copy-start | bytes 12292
  320.2 55.8 %copy-start.138 = (f32[1536]{0:T(1024)S(1)}, f32[1536]{0:T(1024)}, u32[]{:S(2)}) copy-start(f32[1536]{0:T(1024)} %param.45) | copy-start | bytes 18436
  329.1 631.5 %copy-start.240 = (f32[256]{0:T(256)}, f32[256]{0:T(256)S(1)}, u32[]{:S(2)}) copy-start(f32[256]{0:T(256)S(1)} %get-tuple-element.216) | copy-start | bytes 3076
  422.5 64.8 %reduce-scatter.23.cloned.1.call-start = ((), (), s32[]{:S(2)}) async-start(), calls=%async_computation.36 | async-start | bytes 3145728 | tf_op jit(solution)/shard_map/reduce_scatter | solution.py:296
  427.8 532.7 %copy-start.242 = (f32[256]{0:T(256)}, f32[256]{0:T(256)S(1)}, u32[]{:S(2)}) copy-start(f32[256]{0:T(256)S(1)} %get-tuple-element.214) | copy-start | bytes 3076
  435.9 102.2 %all-gather.42.cloned.1.call-start = ((), (), s32[]{:S(2)}) async-start(), calls=%async_computation.43 | async-start | bytes 1572864 | tf_op jit(solution)/shard_map/all_gather | solution.py:298
  455.4 84.3 %all-gather.34.cloned.1.call-start = ((), (), s32[]{:S(2)}) async-start(), calls=%async_computation.37 | async-start | bytes 1572864 | tf_op jit(solution)/shard_map/all_gather | solution.py:298
  489.5 120.6 %all-gather.36.cloned.1.call-start = ((), (), s32[]{:S(2)}) async-start(), calls=%async_computation.38 | async-start | bytes 8912896 | tf_op jit(solution)/shard_map/all_gather | solution.py:227
  490.2 195.0 %all-gather.38.cloned.1.call-start = ((), (), s32[]{:S(2)}) async-start(), calls=%async_computation.39 | async-start | bytes 8912896 | tf_op jit(solution)/shard_map/all_gather | solution.py:228
  490.8 215.4 %all-gather.54.cloned.1.call-start = ((), (), s32[]{:S(2)}) async-start(), calls=%async_computation.56 | async-start | bytes 1572864 | tf_op jit(solution)/shard_map/all_gather | solution.py:234
  515.9 267.3 %all-gather.40.cloned.1.call-start = ((), (), s32[]{:S(2)}) async-start(), calls=%async_computation.40 | async-start | bytes 8912896 | tf_op jit(solution)/shard_map/all_gather | solution.py:229
  516.5 290.9 %all-gather.52.cloned.1.call-start = ((), (), s32[]{:S(2)}) async-start(), calls=%async_computation.55 | async-start | bytes 1572864 | tf_op jit(solution)/shard_map/all_gather | solution.py:234
  537.8 72.2 %copy-start.102 = (f32[2048]{0:T(1024)S(1)}, f32[2048]{0:T(1024)}, u32[]{:S(2)}) copy-start(f32[2048]{0:T(1024)} %param.42) | copy-start | bytes 24580
  537.9 328.5 %reduce-scatter.35.cloned.1.call-start = ((), (), s32[]{:S(2)}) async-start(), calls=%async_computation.48 | async-start | bytes 3145728 | tf_op jit(solution)/shard_map/reduce_scatter | solution.py:321
  538.1 72.0 %copy-start.15 = (bf16[256,2048]{1,0:T(8,128)(2,1)S(1)}, bf16[256,2048]{1,0:T(8,128)(2,1)}, u32[]{:S(2)}) copy-start(bf16[256,2048]{1,0:T(8,128)(2,1)} %all-gather.42.cloned.1.call-done) | copy-start | bytes 3145732
  539.7 293.2 %copy-start.160 = (f32[256]{0:T(256)}, f32[256]{0:T(256)S(1)}, u32[]{:S(2)}) copy-start(f32[256]{0:T(256)S(1)} %fusion.213) | copy-start | bytes 3076
  541.3 291.7 %copy-start.162 = (f32[256]{0:T(256)}, f32[256]{0:T(256)S(1)}, u32[]{:S(2)}) copy-start(f32[256]{0:T(256)S(1)} %fusion.211) | copy-start | bytes 3076
  836.0 64.6 %reduce-scatter.31.cloned.1.call-start = ((), (), s32[]{:S(2)}) async-start(), calls=%async_computation.45 | async-start | bytes 3145728 | tf_op jit(solution)/shard_map/reduce_scatter | solution.py:321
  836.0 64.5 %copy-start.37 = (bf16[128,2048]{1,0:T(8,128)(2,1)S(1)}, bf16[128,2048]{1,0:T(8,128)(2,1)}, u32[]{:S(2)}) copy-start(bf16[128,2048]{1,0:T(8,128)(2,1)} %gather_fusion.9) | copy-start | bytes 1572868
  836.7 87.1 %all-gather.46.cloned.1.call-start = ((), (), s32[]{:S(2)}) async-start(), calls=%async_computation.49 | async-start | bytes 1572864 | tf_op jit(solution)/shard_map/all_gather | solution.py:324
  868.5 78.8 %all-gather.44.cloned.1.call-start = ((), (), s32[]{:S(2)}) async-start(), calls=%async_computation.46 | async-start | bytes 1572864 | tf_op jit(solution)/shard_map/all_gather | solution.py:324
  902.7 223.5 %reduce-scatter.41.cloned.1.call-start = ((), (), s32[]{:S(2)}) async-start(), calls=%async_computation.52 | async-start | bytes 3145728 | tf_op jit(solution)/shard_map/reduce_scatter | solution.py:412
  996.3 130.0 %reduce-scatter.39.cloned.1.call-start = ((), (), s32[]{:S(2)}) async-start(), calls=%async_computation.51 | async-start | bytes 3145728 | tf_op jit(solution)/shard_map/reduce_scatter | solution.py:412
  998.8 203.8 %reduce-scatter.29.cloned.1.call-start = ((), (), s32[]{:S(2)}) async-start(), calls=%async_computation.44 | async-start | bytes 1572864 | tf_op jit(solution)/shard_map/reduce_scatter | solution.py:305
  1007.4 204.2 %reduce-scatter.25.cloned.1.call-start = ((), (), s32[]{:S(2)}) async-start(), calls=%async_computation.41 | async-start | bytes 1572864 | tf_op jit(solution)/shard_map/reduce_scatter | solution.py:305
  1014.7 215.8 %reduce-scatter.37.cloned.1.call-start = ((), (), s32[]{:S(2)}) async-start(), calls=%async_computation.50 | async-start | bytes 1572864 | tf_op jit(solution)/shard_map/reduce_scatter | solution.py:409
  1105.1 144.2 %reduce-scatter.33.cloned.1.call-start = ((), (), s32[]{:S(2)}) async-start(), calls=%async_computation.47 | async-start | bytes 1572864 | tf_op jit(solution)/shard_map/reduce_scatter | solution.py:409
  1105.7 183.9 %all-reduce.57.cloned.1.call-start = ((), (), s32[]{:S(2)}) async-start(), calls=%async_computation.69 | async-start | bytes 289792 | tf_op jit(solution)/shard_map/psum | solution.py:470
  1110.7 238.9 %reduce-scatter.55.cloned.1.call-start = ((), (), s32[]{:S(2)}) async-start(), calls=%async_computation.63 | async-start | bytes 208896 | tf_op jit(solution)/shard_map/reduce_scatter | solution.py:123
  1112.4 297.8 %reduce-scatter.45.cloned.1.call-start = ((), (), s32[]{:S(2)}) async-start(), calls=%async_computation.58 | async-start | bytes 1114112 | tf_op jit(solution)/shard_map/reduce_scatter | solution.py:118
  1114.7 356.6 %reduce-scatter.47.cloned.1.call-start = ((), (), s32[]{:S(2)}) async-start(), calls=%async_computation.59 | async-start | bytes 1114112 | tf_op jit(solution)/shard_map/reduce_scatter | solution.py:119
  1117.1 430.1 %reduce-scatter.43.cloned.1.call-start = ((), (), s32[]{:S(2)}) async-start(), calls=%async_computation.57 | async-start | bytes 4456448 | tf_op jit(solution)/shard_map/reduce_scatter | solution.py:117
  1121.0 502.8 %reduce-scatter.49.cloned.1.call-start = ((), (), s32[]{:S(2)}) async-start(), calls=%async_computation.60 | async-start | bytes 4456448 | tf_op jit(solution)/shard_map/reduce_scatter | solution.py:120
  1126.1 562.5 %reduce-scatter.57.cloned.1.call-start = ((), (), s32[]{:S(2)}) async-start(), calls=%async_computation.64 | async-start | bytes 2228224 | tf_op jit(solution)/shard_map/reduce_scatter | solution.py:124
  1129.4 698.0 %reduce-scatter.51.cloned.1.call-start = ((), (), s32[]{:S(2)}) async-start(), calls=%async_computation.61 | async-start | bytes 13369344 | tf_op jit(solution)/shard_map/reduce_scatter | solution.py:121
  1139.7 826.7 %reduce-scatter.53.cloned.1.call-start = ((), (), s32[]{:S(2)}) async-start(), calls=%async_computation.62 | async-start | bytes 13369344 | tf_op jit(solution)/shard_map/reduce_scatter | solution.py:122
  1149.5 955.7 %reduce-scatter.59.cloned.1.call-start = ((), (), s32[]{:S(2)}) async-start(), calls=%async_computation.65 | async-start | bytes 13369344 | tf_op jit(solution)/shard_map/reduce_scatter | solution.py:125
  1160.7 1127.4 %reduce-scatter.61.cloned.1.call-start = ((), (), s32[]{:S(2)}) async-start(), calls=%async_computation.66 | async-start | bytes 17825792 | tf_op jit(solution)/shard_map/reduce_scatter | solution.py:126
  1175.4 1295.5 %reduce-scatter.63.cloned.1.call-start = ((), (), s32[]{:S(2)}) async-start(), calls=%async_computation.67 | async-start | bytes 17825792 | tf_op jit(solution)/shard_map/reduce_scatter | solution.py:127
  1188.8 1464.9 %reduce-scatter.65.cloned.1.call-start = ((), (), s32[]{:S(2)}) async-start(), calls=%async_computation.68 | async-start | bytes 17825792 | tf_op jit(solution)/shard_map/reduce_scatter | solution.py:128
  1205.9 20.3 all-to-all-start.3
  1226.2 18.8 all-to-all-start.1
  1245.0 18.8 all-to-all-start.7
  1263.9 20.1 all-to-all-start.5
  (303 other events, 1605.3 us)
Sparse Core Ops, SparseCore 0:
  46.1 22.6 all-gather.47
  76.4 22.6 all-gather.49
  101.3 44.4 all-gather.23
  147.8 40.1 all-gather.29
  190.2 60.4 all-gather.21
  252.8 60.4 all-gather.25
  315.5 60.4 all-gather.27
  378.2 39.9 all-gather.31
  422.7 30.5 reduce-scatter.26
  455.5 31.8 reduce-scatter.22
  488.9 21.2 all-gather.41
  511.6 21.2 all-gather.33
  535.1 74.9 all-gather.35
  612.1 73.1 all-gather.37
  686.7 19.5 all-gather.53
  708.3 74.9 all-gather.39
  784.6 19.5 all-gather.51
  836.1 30.2 reduce-scatter.34
  868.7 31.8 reduce-scatter.30
  902.5 21.3 all-gather.45
  926.0 21.2 all-gather.43
  996.4 31.8 reduce-scatter.40
  1030.6 31.8 reduce-scatter.38
  1065.1 20.3 reduce-scatter.28
  1087.8 20.3 reduce-scatter.24
  1110.3 20.3 reduce-scatter.36
  1132.8 20.3 reduce-scatter.32
  1160.7 128.8 all-reduce.56
  1293.7 55.8 reduce-scatter.54
  1353.7 56.4 reduce-scatter.44
  1414.8 56.4 reduce-scatter.46
  1475.7 71.4 reduce-scatter.42
  1552.0 71.7 reduce-scatter.48
  1628.0 60.5 reduce-scatter.56
  1693.8 133.6 reduce-scatter.50
  1832.4 133.8 reduce-scatter.52
  1971.4 133.7 reduce-scatter.58
  2110.4 177.6 reduce-scatter.60
  2293.3 177.5 reduce-scatter.62
  2476.1 177.5 reduce-scatter.64
where the time goes:
time: 2680 us; the launch traced here: 2670 us
  waiting for transfers between devices  1950 us (73%)
  matrix products  297 us (11%)
  local copies, waits for them, and re-layouts  134 us (5%)
  other arithmetic  121 us (5%)
  blocking collectives  112 us (4%)
  starting transfers between devices  35.2 us (1%)
    reduce_scatter x1, waiting for transfers between devices, sum_weights(): lax.psum_scatter(g_fgate, 'dp', scatter_dimension=0, tiled=True)  183 us
    reduce_scatter x1, waiting for transfers between devices, sum_weights(): lax.psum_scatter(g_fdown, 'dp', scatter_dimension=0, tiled=True)  183 us
    reduce_scatter x1, waiting for transfers between devices, sum_weights(): lax.psum_scatter(g_fup, 'dp', scatter_dimension=0, tiled=True)  183 us
    reduce_scatter x1, waiting for transfers between devices, sum_weights(): lax.psum_scatter(g_input, 'dp', scatter_dimension=0, tiled=True)  139 us
    reduce_scatter x1, waiting for transfers between devices, sum_weights(): lax.psum_scatter(g_mix, 'dp', scatter_dimension=0, tiled=True)  139 us
    reduce_scatter x1, waiting for transfers between devices, sum_weights(): lax.psum_scatter(g_gate, 'dp', scatter_dimension=0, tiled=True)  139 us
    dot_general x26, matrix products, project(): return jnp.dot(left, right, preferred_element_type=jnp.float32)  91.7 us
    dot_general x26, matrix products, outer_sum(): lax.dot_general(left, right, (((0,), (0,)), ((), ())), preferred_element_...  84.9 us
  transfers between devices with their start and end apart: 46, of which 32 were waited for; matrix products, arithmetic and copies ran while one was open for 16% of the time, Pallas kernels for 0%

commit v1 on v0

v1 whole, which is shorter than its diff:
```python
import math

import jax
import jax.numpy as jnp
from jax import lax
from jax.sharding import PartitionSpec as P

HEAD = 128
SH = 48
SHD = 64
NS = 256
CONV = 4
STEP_PAD = 128

epsilon = 1e-05
rope_base = 100000000000.0
f32 = jnp.float32
bf16 = jnp.bfloat16


def project(left, right):
    return jnp.dot(left, right, preferred_element_type=f32)


def project_back(left, right):
    return lax.dot_general(left, right, (((1,), (1,)), ((), ())), preferred_element_type=f32)


def outer_sum(left, right):
    return lax.dot_general(left, right, (((0,), (0,)), ((), ())), preferred_element_type=f32)


def rms_scale(values):
    return lax.rsqrt(jnp.mean(values * values, axis=-1, keepdims=True) + epsilon)


def rms_back(grad, values, scale, gain):
    weighted = grad * gain
    inner = jnp.sum(weighted * values, axis=-1, keepdims=True)
    return scale * weighted - values * (scale * scale * scale * inner / values.shape[-1])


def shift_down(values, count):
    return jnp.concatenate([jnp.zeros((count, values.shape[1]), values.dtype), values[:-count]], axis=0)


def shift_up(values, count):
    return jnp.concatenate([values[count:], jnp.zeros((count, values.shape[1]), values.dtype)], axis=0)


def conv_sum(signal, kernel, position):
    summed = kernel[CONV][None, :] + signal * kernel[0][None, :]
    for tap in range(1, CONV):
        moved = jnp.where(position >= tap, shift_down(signal, tap), 0.0)
        summed = summed + moved * kernel[tap][None, :]
    return summed


def silu_back(values):
    sig = jax.nn.sigmoid(values)
    return sig * (1.0 + values * (1.0 - sig))


def conv_back(grad, signal, kernel, position):
    grad_sum = grad * silu_back(conv_sum(signal, kernel, position))
    grad_signal = grad_sum * kernel[0][None, :]
    grad_taps = [jnp.sum(grad_sum * signal, axis=0)]
    for tap in range(1, CONV):
        kept = jnp.where(position >= tap, grad_sum, 0.0)
        grad_signal = grad_signal + shift_up(kept, tap) * kernel[tap][None, :]
        grad_taps.append(jnp.sum(kept * shift_down(signal, tap), axis=0))
    grad_taps.append(jnp.sum(grad_sum, axis=0))
    return grad_signal, jnp.stack(grad_taps)


def rope_tables(position):
    half_size = HEAD // 2
    frequency = jnp.exp(jnp.arange(half_size, dtype=f32) * (-2.0 * math.log(rope_base) / HEAD))
    angles = position.astype(f32) * frequency[None, :]
    return jnp.cos(angles)[:, None, :], jnp.sin(angles)[:, None, :]


def rotate(values, cosine, sine):
    half_size = HEAD // 2
    first, second = values[..., :half_size], values[..., half_size:]
    return jnp.concatenate([first * cosine - second * sine, second * cosine + first * sine], axis=-1)


def rotate_back(values, cosine, sine):
    return rotate(values, cosine, -sine)


def local(
    inputs,
    out_grad,
    deal_order,
    segment,
    query_weight,
    key_weight,
    value_weight,
    attention_out,
    mamba_gate,
    mamba_input,
    step_weight,
    state_weight,
    mamba_out,
    feed_gate,
    feed_up,
    feed_down,
    gain_input,
    gain_middle,
    kernel_inner,
    kernel_state,
    mixer_gain,
    step_bias,
    log_rate,
    skip_gain,
):
    micro, own, width = inputs.shape
    groups = lax.axis_size("dp")
    lanes = lax.axis_size("tensor")
    lane = lax.axis_index("tensor")
    group = lax.axis_index("dp")
    device = group * lanes + lane
    per = own // groups
    rows = own * lanes
    total = micro * rows
    inner_width = SH * SHD
    scale_factor = HEAD ** (-0.5)
    outer_count = groups // 4
    shard = width // groups

    swap_lane = [(0, 1), (1, 0)]

    def other_lane(values):
        return lax.ppermute(values, "tensor", swap_lane)

    def other_group(values, bits):
        return lax.ppermute(values, "dp", [(i, i ^ bits) for i in range(groups)])

    step_padded = jnp.pad(step_weight, ((0, 0), (0, STEP_PAD - step_weight.shape[1])))
    early = [mamba_gate, mamba_input, state_weight, step_padded, query_weight, key_weight, value_weight, mamba_out, attention_out]
    late = [feed_gate, feed_up, feed_down]

    def gather(pieces):
        whole = lax.all_gather(jnp.concatenate(pieces, axis=1), "dp", axis=0, tiled=True)
        found, start = [], 0
        for piece in pieces:
            found.append(whole[:, start : start + piece.shape[1]])
            start += piece.shape[1]
        return found

    full_gate, full_input, full_state, full_step, full_query, full_key, full_value, full_mix, full_attn = gather(early)
    full_fgate, full_fup, full_fdown = gather(late)

    own_places = jnp.arange(own, dtype=jnp.int32)
    own_order = lax.dynamic_slice_in_dim(deal_order, device * own, own, 1)
    micro_index = jnp.arange(micro, dtype=jnp.int32)[:, None]

    def buffer_place(destination, rank):
        return destination * (micro * per) + micro_index * per + rank

    send_rank = jnp.sum((own_order[:, None, :] < own_order[:, :, None]).astype(jnp.int32), axis=2)
    send_place = buffer_place(send_rank // per, send_rank % per).reshape(-1)
    lane_order = lax.dynamic_index_in_dim(deal_order.reshape(micro, groups, lanes, own), lane, 2, keepdims=False)
    slots = device * own + own_places
    found = lane_order[:, None, :, :] == slots[None, :, None, None]
    source = jnp.sum(
        jnp.where(found, jnp.arange(groups, dtype=jnp.int32)[None, None, :, None], 0), axis=(2, 3)
    )
    recv_rank = jnp.sum(
        ((source[:, None, :] == source[:, :, None]) & (own_places[None, None, :] < own_places[None, :, None])).astype(jnp.int32),
        axis=2,
    )
    recv_place = buffer_place(source, recv_rank).reshape(-1)
    buffer_places = jnp.arange(micro * own, dtype=jnp.int32)
    send_pick = (buffer_places[:, None] == send_place[None, :]).astype(bf16)
    recv_pick = (recv_place[:, None] == buffer_places[None, :]).astype(bf16)

    def exchange(buffer):
        return lax.all_to_all(
            buffer.reshape(groups, micro * per, width), "dp", split_axis=0, concat_axis=0, tiled=True
        ).reshape(micro * own, width)

    def deal(values):
        sent = project(send_pick, values.reshape(micro * own, width)).astype(bf16)
        return project(recv_pick, exchange(sent)).astype(bf16)

    def deal_back(values):
        sent = outer_sum(recv_pick, values).astype(bf16)
        return outer_sum(send_pick, exchange(sent)).astype(bf16).reshape(micro, own, width)

    def join_lanes(values):
        mine = values.reshape(micro, 1, own, -1)
        theirs = other_lane(values).reshape(micro, 1, own, -1)
        low = jnp.where(lane == 0, mine, theirs)
        high = jnp.where(lane == 0, theirs, mine)
        return jnp.concatenate([low, high], axis=1).reshape(total, -1)

    def lane_rows(values, which):
        return lax.dynamic_index_in_dim(
            values.reshape(micro, lanes, own, -1), which, 1, keepdims=False
        ).reshape(micro * own, -1)

    own_in = deal(inputs)
    own_grad = deal(out_grad)
    whole_in = join_lanes(own_in)
    whole_grad = join_lanes(own_grad)

    before = jnp.sum((segment[:, None, :] < segment[:, :, None]).astype(jnp.int32), axis=2)
    places = jnp.arange(rows, dtype=jnp.int32)
    allowed = (segment[:, :, None] == segment[:, None, :]) & (places[None, None, :] <= places[None, :, None])
    position = (places[None, :] - before).reshape(total, 1)

    core_bit = group & 1
    y_bit = (group >> 1) & 1
    outer_index = group >> 2

    def split_left(left):
        blocks = left.reshape(left.shape[0], outer_count, 2, 2, shard)

        def part(core, y):
            picked = lax.dynamic_index_in_dim(blocks, core, 3, keepdims=False)
            picked = lax.dynamic_index_in_dim(picked, y, 2, keepdims=False)
            return picked.reshape(left.shape[0], outer_count * shard)

        send = jnp.concatenate([part(1 - core_bit, 1 - y_bit), part(1 - core_bit, y_bit)], axis=1)
        return send, part(core_bit, 1 - y_bit), part(core_bit, y_bit)

    quarter = outer_count * shard

    def reduce_weight(left_parts, right):
        send, keep_send, keep = left_parts
        from_core = other_group(outer_sum(send, right).astype(bf16), 1)
        to_y = (outer_sum(keep_send, right) + from_core[:quarter].astype(f32)).astype(bf16)
        from_y = other_group(to_y, 2).reshape(outer_count, shard, -1)
        mine = (outer_sum(keep, right) + from_core[quarter:].astype(f32)).astype(bf16).reshape(outer_count, shard, -1)

        def pair_sum(index):
            a = lax.dynamic_index_in_dim(mine, index, 0, keepdims=False).astype(f32)
            b = lax.dynamic_index_in_dim(from_y, index, 0, keepdims=False).astype(f32)
            return a + b

        result = pair_sum(outer_index)
        for step in range(1, outer_count):
            got = other_group(pair_sum(outer_index ^ step).astype(bf16), step << 2)
            result = result + got.astype(f32)
        return result

    in32 = whole_in.astype(f32)
    in_scale = rms_scale(in32)
    normed_low = (in32 * in_scale * gain_input).astype(bf16)
    gate_z = project(normed_low, full_gate)
    ssm_in = project(normed_low, full_input)
    state_raw = project(normed_low, full_state)
    heads = step_weight.shape[1]
    raw_step = project(normed_low, full_step)[:, :heads]
    ssm_cols = jax.nn.silu(conv_sum(ssm_in, kernel_inner, position))
    state_act = jax.nn.silu(conv_sum(state_raw, kernel_state, position)).astype(bf16)
    b_state = state_act[:, :NS].reshape(micro, rows, NS)
    c_state = state_act[:, NS:].reshape(micro, rows, NS)
    state_inner = jnp.einsum("mis,mjs->mij", c_state, b_state, preferred_element_type=f32)
    rate = -jnp.exp(log_rate)
    step_size = jax.nn.softplus(raw_step + step_bias)
    step_heads = step_size.reshape(micro, rows, heads).transpose(0, 2, 1)
    lower = (places[None, :] <= places[:, None]).astype(f32)
    running = jnp.einsum(
        "mhj,ij->mhi", step_heads * rate[None, :, None], lower, precision=lax.Precision.HIGHEST, preferred_element_type=f32
    )
    decay = jnp.exp(jnp.where(allowed[:, None], running[:, :, :, None] - running[:, :, None, :], -jnp.inf))
    mixing_low = (state_inner[:, None] * decay * step_heads[:, :, None, :]).astype(bf16)
    ssm_heads = ssm_cols.reshape(micro, rows, heads, SHD)
    heads_low = ssm_heads.astype(bf16)
    skip_wide = jnp.repeat(skip_gain, SHD)[None, :]
    ssm_out = (
        jnp.einsum("mhij,mjhd->mihd", mixing_low, heads_low, preferred_element_type=f32).reshape(total, -1)
        + skip_wide * ssm_cols
    )
    silu_z = jax.nn.silu(gate_z)
    gated = ssm_out * silu_z
    square_own = jnp.sum(gated * gated, axis=1)
    square_sum = square_own + other_lane(square_own)
    inv_rms = lax.rsqrt(square_sum / inner_width + epsilon)[:, None]
    gated_low = (gated * inv_rms * mixer_gain).astype(bf16)

    cosine, sine = rope_tables(position)
    query_low = rotate(project(normed_low, full_query).reshape(total, -1, HEAD), cosine, sine).astype(bf16)
    key_low = rotate(project(normed_low, full_key).reshape(total, -1, HEAD), cosine, sine).astype(bf16)
    value_low = project(normed_low, full_value).astype(bf16)
    kv_here = key_low.shape[1]
    query_low = query_low.reshape(micro, rows, kv_here, -1, HEAD)
    key_low = key_low.reshape(micro, rows, kv_here, HEAD)
    value_low = value_low.reshape(micro, rows, kv_here, HEAD)
    logits = jnp.einsum("migkd,mjgd->mgkij", query_low, key_low, preferred_element_type=f32) * scale_factor
    logits = jnp.where(allowed[:, None, None], logits, -jnp.inf)
    exp_scores = jnp.exp(logits - jnp.max(logits, axis=-1, keepdims=True))
    probs = exp_scores / jnp.sum(exp_scores, axis=-1, keepdims=True)
    probs_low = probs.astype(bf16)
    attended_low = (
        jnp.einsum("mgkij,mjgd->migkd", probs_low, value_low, preferred_element_type=f32).astype(bf16).reshape(total, -1)
    )
    branch_part = (project_back(gated_low, full_mix) + project_back(attended_low, full_attn)).astype(bf16)
    branch = branch_part.astype(f32) + other_lane(branch_part).astype(f32)
    whole_mid = (in32 + branch).astype(bf16)
    mid32 = whole_mid.astype(f32)
    mid_scale = rms_scale(mid32)
    mid_low = (mid32 * mid_scale * gain_middle).astype(bf16)
    gate_ff = project(mid_low, full_fgate)
    up_ff = project(mid_low, full_fup)
    sig_ff = jax.nn.sigmoid(gate_ff)
    hidden_low = (gate_ff * sig_ff * up_ff).astype(bf16)

    grad_left = split_left(whole_grad)
    mid_left = split_left(mid_low)
    total_fdown = reduce_weight(grad_left, hidden_low)
    grad_hidden = project(whole_grad, full_fdown)
    gate_ff_low = (grad_hidden * up_ff * (sig_ff * (1.0 + gate_ff * (1.0 - sig_ff)))).astype(bf16)
    up_ff_low = (grad_hidden * (gate_ff * sig_ff)).astype(bf16)
    total_fgate = reduce_weight(mid_left, gate_ff_low)
    total_fup = reduce_weight(mid_left, up_ff_low)
    grad_mid_norm = project_back(gate_ff_low, full_fgate) + project_back(up_ff_low, full_fup)
    grad_gain_mid = jnp.sum(grad_mid_norm * mid32 * mid_scale, axis=0)
    mid_part = rms_back(grad_mid_norm, mid32, mid_scale, gain_middle).astype(bf16)
    grad_middle = whole_grad.astype(f32) + (mid_part.astype(f32) + other_lane(mid_part).astype(f32))
    whole_branch = grad_middle.astype(bf16)

    ffn_part = project_back(hidden_low, full_fdown).astype(bf16)
    ffn_out = lane_rows(ffn_part, lane).astype(f32) + other_lane(lane_rows(ffn_part, 1 - lane)).astype(f32)
    out_rows = (lane_rows(whole_mid, lane).astype(f32) + ffn_out).astype(bf16)
    block_out = deal_back(out_rows)

    branch_left = split_left(whole_branch)
    total_mix = reduce_weight(branch_left, gated_low)
    total_attn = reduce_weight(branch_left, attended_low)
    grad_gated_norm = project(whole_branch, full_mix)
    scaled_grad = grad_gated_norm * mixer_gain
    grad_mixer = jnp.sum(grad_gated_norm * gated * inv_rms, axis=0)
    cross_own = jnp.sum(scaled_grad * gated, axis=1)
    cross_sum = cross_own + other_lane(cross_own)
    grad_gated = inv_rms * scaled_grad - gated * (inv_rms**3 * cross_sum[:, None] / inner_width)
    grad_ssm_out = grad_gated * silu_z
    gate_low = (grad_gated * ssm_out * silu_back(gate_z)).astype(bf16)
    normed_left = split_left(normed_low)
    total_gate = reduce_weight(normed_left, gate_low)

    grad_attended = project(whole_branch, full_attn).astype(bf16).reshape(micro, rows, kv_here, -1, HEAD)
    grad_probs = jnp.einsum("migkd,mjgd->mgkij", grad_attended, value_low, preferred_element_type=f32)
    grad_value = jnp.einsum("mgkij,migkd->mjgd", probs_low, grad_attended, preferred_element_type=f32)
    weighted_sum = jnp.sum(probs * grad_probs, axis=-1, keepdims=True)
    grad_logits = (probs * (grad_probs - weighted_sum)).astype(bf16)
    grad_query_rot = jnp.einsum("mgkij,mjgd->migkd", grad_logits, key_low, preferred_element_type=f32) * scale_factor
    grad_key_rot = jnp.einsum("mgkij,migkd->mjgd", grad_logits, query_low, preferred_element_type=f32) * scale_factor
    query_grad_low = rotate_back(grad_query_rot.reshape(total, -1, HEAD), cosine, sine).astype(bf16).reshape(total, -1)
    key_grad_low = rotate_back(grad_key_rot.reshape(total, -1, HEAD), cosine, sine).astype(bf16).reshape(total, -1)
    value_grad_low = grad_value.astype(bf16).reshape(total, -1)
    qkv_low = jnp.concatenate([query_grad_low, key_grad_low, value_grad_low], axis=1)
    total_qkv = reduce_weight(normed_left, qkv_low)

    grad_heads_low = grad_ssm_out.astype(bf16).reshape(micro, rows, heads, SHD)
    grad_ssm_cols = (
        jnp.einsum("mhij,mihd->mjhd", mixing_low, grad_heads_low, preferred_element_type=f32).reshape(total, -1)
        + skip_wide * grad_ssm_out
    )
    grad_skip = jnp.sum((grad_ssm_out * ssm_cols).reshape(total, heads, SHD), axis=(0, 2))
    grad_mixing = jnp.einsum("mihd,mjhd->mhij", grad_heads_low, heads_low, preferred_element_type=f32)
    grad_decay = grad_mixing * decay
    inner_low = jnp.sum(grad_decay * step_heads[:, :, None, :], axis=1).astype(bf16)
    grad_direct = jnp.sum(grad_decay * state_inner[:, None], axis=2)
    grad_rows = jnp.sum(grad_decay * state_inner[:, None] * step_heads[:, :, None, :], axis=3)
    grad_running = grad_rows - step_heads * grad_direct
    grad_product = jnp.einsum(
        "mhi,ij->mhj", grad_running, lower, precision=lax.Precision.HIGHEST, preferred_element_type=f32
    )
    grad_step = (grad_direct + grad_product * rate[None, :, None]).transpose(0, 2, 1).reshape(total, heads)
    grad_rate = jnp.sum(grad_product * step_heads, axis=(0, 2)) * rate
    grad_raw_step = grad_step * jax.nn.sigmoid(raw_step + step_bias)
    grad_bias = jnp.sum(grad_raw_step, axis=0)
    grad_c = jnp.einsum("mij,mjs->mis", inner_low, b_state, preferred_element_type=f32)
    grad_b = jnp.einsum("mij,mis->mjs", inner_low, c_state, preferred_element_type=f32)
    grad_state_act = jnp.concatenate([grad_b, grad_c], axis=2).reshape(total, 2 * NS)
    grad_state_raw, grad_kernel_state = conv_back(grad_state_act, state_raw, kernel_state, position)
    grad_ssm_in, grad_kernel_inner = conv_back(grad_ssm_cols, ssm_in, kernel_inner, position)
    input_low = grad_ssm_in.astype(bf16)
    step_low = jnp.pad(grad_raw_step.astype(bf16), ((0, 0), (0, STEP_PAD - heads)))
    state_low = jnp.concatenate([grad_state_raw.astype(bf16), step_low], axis=1)
    total_input = reduce_weight(normed_left, input_low)
    total_state = reduce_weight(normed_left, state_low)

    grad_normed = project_back(gate_low, full_gate) + project_back(query_grad_low, full_query)
    grad_normed = grad_normed + project_back(key_grad_low, full_key) + project_back(value_grad_low, full_value)
    grad_normed = grad_normed + project_back(input_low, full_input)
    grad_normed = grad_normed + project_back(state_low[:, : 2 * NS], full_state) + project_back(step_low, full_step)
    grad_gain_in = jnp.sum(grad_normed * in32 * in_scale, axis=0)
    in_part = rms_back(grad_normed, in32, in_scale, gain_input).astype(bf16)
    in_sum = lane_rows(in_part, lane).astype(f32) + other_lane(lane_rows(in_part, 1 - lane)).astype(f32)
    in_grad_rows = (in_sum + lane_rows(grad_middle, lane)).astype(bf16)
    grad_input = deal_back(in_grad_rows)

    shared = [grad_gain_in, grad_gain_mid, grad_kernel_state.reshape(-1)]
    split = [grad_kernel_inner.reshape(-1), grad_mixer, grad_bias, grad_rate, grad_skip]
    both_flat = jnp.concatenate(shared + split)
    flat_size = both_flat.shape[0]
    padded = -(-flat_size // 1024) * 1024
    flat = jnp.pad(both_flat, (0, padded - flat_size)).reshape(padded // 128, 128)
    bits = 1
    while bits < groups:
        flat = flat + other_group(flat, bits)
        bits *= 2
    theirs = other_lane(flat).reshape(-1)
    flat = flat.reshape(-1)
    pieces = []
    start = 0
    for item in shared:
        pieces.append(flat[start : start + item.shape[0]] + theirs[start : start + item.shape[0]])
        start += item.shape[0]
    for item in split:
        mine, other = flat[start : start + item.shape[0]], theirs[start : start + item.shape[0]]
        pieces.append((jnp.where(lane == 0, mine, other), jnp.where(lane == 0, other, mine)))
        start += item.shape[0]
    sum_gin, sum_gmid, sum_kst = pieces[0], pieces[1], pieces[2].reshape(CONV + 1, -1)
    sum_kin = jnp.concatenate([half.reshape(CONV + 1, -1) for half in pieces[3]], axis=1)
    sum_mix, sum_bias, sum_rate, sum_skip = [jnp.concatenate(pair) for pair in pieces[4:]]

    query_cols = query_weight.shape[1]
    key_cols = key_weight.shape[1]
    total_query = total_qkv[:, :query_cols]
    total_key = total_qkv[:, query_cols : query_cols + key_cols]
    total_value = total_qkv[:, query_cols + key_cols :]
    total_step = total_state[:, 2 * NS : 2 * NS + heads]
    state_rows = total_state[:, : 2 * NS].reshape(lanes, shard // lanes, 2 * NS)
    state_own = lax.dynamic_index_in_dim(state_rows, lane, 0, keepdims=False)
    state_send = lax.dynamic_index_in_dim(state_rows, 1 - lane, 0, keepdims=False)
    state_lane = state_own + other_lane(state_send)
    return (
        block_out,
        grad_input,
        total_query,
        total_key,
        total_value,
        total_attn,
        total_gate,
        total_input,
        total_step,
        state_lane,
        total_mix,
        total_fgate,
        total_fup,
        total_fdown,
        sum_gin,
        sum_gmid,
        sum_kin,
        sum_kst,
        sum_mix,
        sum_bias,
        sum_rate,
        sum_skip,
    )


def solution(mesh):
    both = P("dp", "tensor")
    in_specs = (
        P(None, ("dp", "tensor"), None),
        P(None, ("dp", "tensor"), None),
        P(),
        P(None, "dp"),
        both,
        both,
        both,
        both,
        both,
        both,
        both,
        P("dp", None),
        both,
        both,
        both,
        both,
        P(),
        P(),
        P(None, "tensor"),
        P(),
        P("tensor"),
        P("tensor"),
        P("tensor"),
        P("tensor"),
    )
    out_specs = (
        P(None, ("dp", "tensor"), None),
        P(None, ("dp", "tensor"), None),
        both,
        both,
        both,
        both,
        both,
        both,
        both,
        P(("dp", "tensor"), None),
        both,
        both,
        both,
        both,
        P(),
        P(),
        P(),
        P(),
        P(),
        P(),
        P(),
        P(),
    )
    return jax.shard_map(local, mesh=mesh, in_specs=in_specs, out_specs=out_specs, check_vma=False)
```

time: 2680 us -> 1220 us (0.46)
  waiting for transfers between devices: 1950 us -> 434 us
  starting transfers between devices: 35.2 us -> 173 us
  blocking collectives: 112 us -> 0 us
  local copies, waits for them, and re-layouts: 134 us -> 195 us
    reduce_scatter x22 -> x0, waiting for transfers between devices: 1470 us -> none  [the longest x1 183 us: sum_weights(): lax.psum_scatter(g_fgate, 'dp', scatter_dimension=0, tiled=True)]
    all_gather x17 -> x2, waiting for transfers between devices: 426 us -> 36.8 us  [gather(): lax.all_gather(jnp.concatenate(pieces, axis=1), 'dp', axis=0, tiled=True)]
    ppermute x0 -> x59, waiting for transfers between devices: none -> 327 us  [the longest x49 272 us: other_group(): return lax.ppermute(values, 'dp', [(i, i ^ bits) for i in range(groups)])]
    ppermute x0 -> x59, starting transfers between devices: none -> 151 us  [the longest x49 137 us: other_group(): return lax.ppermute(values, 'dp', [(i, i ^ bits) for i in range(groups)])]
    all_gather x3 -> x0, blocking collectives: 63.8 us -> none  [the longest x1 23.3 us: local(): lax.all_gather(step_weight, 'dp', axis=0, tiled=True)]
    dynamic_slice x1 -> x17, local copies, waits for them, and re-layouts: 0.01 us -> 56.5 us  [the longest x12 50.5 us: part(): picked = lax.dynamic_index_in_dim(picked, y, 2, keepdims=False)]
    all_to_all x2 -> x0, blocking collectives: 38.5 us -> none  [local(): lax.all_to_all(out_grad[micro_step][send_order].reshape(group_count, per_...]
    scatter x2 -> x0, local copies, waits for them, and re-layouts: 31.1 us -> none  [local(): inverse = jnp.zeros_like(order_now).at[order_now].set(jnp.arange(order_no...]
  transfers between devices with their start and end apart: 46 -> 65, of which waited for: 32 -> 28; matrix products, arithmetic and copies ran while one was open for 16% -> 41% of each run, Pallas kernels for 0% -> 0%
where the time goes in v1:
time: 1220 us; the launch traced here: 1210 us
  waiting for transfers between devices  434 us (36%)
  matrix products  283 us (23%)
  local copies, waits for them, and re-layouts  195 us (16%)
  starting transfers between devices  173 us (14%)
  other arithmetic  112 us (9%)
  between operations  17 us (1%)
    ppermute x49, waiting for transfers between devices, other_group(): return lax.ppermute(values, 'dp', [(i, i ^ bits) for i in range(groups)])  272 us
    ppermute x49, starting transfers between devices, other_group(): return lax.ppermute(values, 'dp', [(i, i ^ bits) for i in range(groups)])  137 us
    dot_general x31, matrix products, outer_sum(): lax.dot_general(left, right, (((0,), (0,)), ((), ())), preferred_element_...  103 us
    dot_general x16, matrix products, project(): return jnp.dot(left, right, preferred_element_type=f32)  77.6 us
    dot_general x12, matrix products, project_back(): lax.dot_general(left, right, (((1,), (1,)), ((), ())), preferred_element_...  74.5 us
    all_to_all x4, waiting for transfers between devices, exchange(): lax.all_to_all(buffer.reshape(groups, micro * per, width), 'dp', split_ax...  69.3 us
    ppermute x10, waiting for transfers between devices, other_lane(): return lax.ppermute(values, 'tensor', swap_lane)  55.5 us
    dynamic_slice x12, local copies, waits for them, and re-layouts, part(): picked = lax.dynamic_index_in_dim(picked, y, 2, keepdims=False)  50.5 us
  transfers between devices with their start and end apart: 65, of which 28 were waited for; matrix products, arithmetic and copies ran while one was open for 41% of the time, Pallas kernels for 0%

profile of v1, /device:TPU:0, one launch (start us, length us, event | category | flops | bytes accessed | tf_op | source)
XLA Modules:
  0.0 1214.0 jit_solution(1615003080232475013)
XLA Ops:
  18.9 4.9 select_reduce_fusion
  25.4 7.5 all-to-all-start
  34.6 38.2 %all-to-all-done = bf16[16,16,2048]{2,1,0:T(8,128)(2,1)S(1)} async-done(((bf16[16,16,2048]{2,1,0:T(8,128)(2,1)}), bf16[16,16,2048]{2,1,0:T(8,128)(2,1)S(1)}, u32[]{:S(2)}, u32[]{:S(2)}) %all-to-all-start) | async-done | bytes 1048608 | tf_op jit(solution)/shard_map/all_to_all | solution.py:181
  85.7 31.0 %all-to-all-done.2 = bf16[16,16,2048]{2,1,0:T(8,128)(2,1)S(1)} async-done(((bf16[16,16,2048]{2,1,0:T(8,128)(2,1)}), bf16[16,16,2048]{2,1,0:T(8,128)(2,1)S(1)}, u32[]{:S(2)}, u32[]{:S(2)}) %all-to-all-start.2) | async-done | bytes 1048608 | tf_op jit(solution)/shard_map/all_to_all | solution.py:181
  123.8 6.6 reshape.1249
  135.5 5.3 constant_dynamic-slice_fusion.15
  157.5 31.5 %all-gather.3.cloned.1.call-done = bf16[2048,6528]{1,0:T(8,128)(2,1)} async-done(((bf16[128,6528]{1,0:T(8,128)(2,1)}), bf16[2048,6528]{1,0:T(8,128)(2,1)}) %all-gather.3.cloned.1.call-update) | async-done | bytes 26738704 | tf_op jit(solution)/shard_map/all_gather | solution.py:146
  192.2 6.2 fusion.23
  198.5 5.6 fusion.243
  204.2 5.0 reshape.1260
  221.0 4.9 fusion.62
  225.9 6.0 copy.222
  231.9 6.3 reshape.1258
  238.1 13.1 %multiply_reduce_fusion.10 = (f32[512]{0:T(512)}, f32[512,1536]{1,0:T(8,128)}, f32[512,1536]{1,0:T(8,128)}) fusion(f32[512,1536]{1,0:T(8,128)} %reshape.1258, f32[512,1536]{1,0:T(8,128)} %get-tuple-element.109, f32[1536]{0:T(1024)S(1)} %copy-done.128, bf16[512,2048]{1,0:T(8,128)(2,1)} %fusion.39, bf16[2048,6528]{1,0:T(8,128)(2,1)} %all-gather.3.cloned.1.call-done), kind=kOutput, calls=%fused_computation.102 | convolution fusion | flops 3231448576 | bytes 20979712 | tf_op jit(solution)/shard_map/dot_general | solution.py:22
  283.7 6.2 fusion.15
  302.2 7.2 constant_dynamic-slice_fusion.10
  323.7 5.3 all-gather.5.cloned.1.call-done
  329.0 10.6 fusion.1
  351.8 5.5 constant_dynamic-slice_fusion.2
  368.0 7.0 fusion.7
  375.1 8.8 multiply_convert_fusion.5
  399.6 7.1 fusion.5
  406.7 8.7 fusion.34
  432.4 9.6 fusion.52
  442.0 22.4 %collective-permute-done.5 = bf16[512,2048]{1,0:T(8,128)(2,1)} collective-permute-done((bf16[512,2048]{1,0:T(8,128)(2,1)}, bf16[512,2048]{1,0:T(8,128)(2,1)}, u32[]{:S(2)}, u32[]{:S(2)}) %collective-permute-start.5) | collective-permute-done | bytes 2097184 | tf_op jit(solution)/shard_map/ppermute | solution.py:136
  464.4 5.6 fusion.247
  487.9 5.4 constant_dynamic-slice_fusion.9
  507.1 8.7 multiply_reduce_fusion.4
  537.0 4.9 fusion.69
  552.1 8.4 multiply_reduce_fusion.3
  570.7 8.8 multiply_reduce_fusion
  580.2 4.9 fusion.63
  598.8 6.3 reshape.1259
  605.2 5.3 multiply_reduce_fusion.5
  622.1 8.4 fusion.17
  633.4 8.0 fusion.21
  641.6 6.7 fusion.45
  660.4 11.8 collective-permute-start.56
  684.0 18.9 %collective-permute-done.58 = f32[128,128]{1,0:T(8,128)S(1)} collective-permute-done((f32[128,128]{1,0:T(8,128)S(1)}, f32[128,128]{1,0:T(8,128)S(1)}, u32[]{:S(2)}, u32[]{:S(2)}) %collective-permute-start.58) | collective-permute-done | bytes 65568 | tf_op jit(solution)/shard_map/ppermute | solution.py:136
  714.0 12.0 collective-permute-done.7
  741.6 17.7 %collective-permute-done.14 = bf16[512,512]{1,0:T(8,128)(2,1)S(1)} collective-permute-done((bf16[512,512]{1,0:T(8,128)(2,1)S(1)}, bf16[512,512]{1,0:T(8,128)(2,1)S(1)}, u32[]{:S(2)}, u32[]{:S(2)}) %collective-permute-start.14) | collective-permute-done | bytes 524320 | tf_op jit(solution)/shard_map/ppermute | solution.py:139
  784.6 4.9 collective-permute-done.32
  789.6 6.0 collective-permute-start.30
  795.6 5.7 add_convert_fusion.5
  803.4 5.6 add_convert_fusion.3
  809.0 12.3 %collective-permute-done.9 = bf16[512,768]{1,0:T(8,128)(2,1)S(1)} collective-permute-done((bf16[512,768]{1,0:T(8,128)(2,1)S(1)}, bf16[512,768]{1,0:T(8,128)(2,1)S(1)}, u32[]{:S(2)}, u32[]{:S(2)}) %collective-permute-start.9) | collective-permute-done | bytes 786464 | tf_op jit(solution)/shard_map/ppermute | solution.py:139
  832.0 7.4 add_convert_fusion.1
  840.0 14.0 %collective-permute-done.12 = bf16[128,768]{1,0:T(8,128)(2,1)} collective-permute-done((bf16[128,768]{1,0:T(8,128)(2,1)}, bf16[128,768]{1,0:T(8,128)(2,1)}, u32[]{:S(2)}, u32[]{:S(2)}) %collective-permute-start.12) | collective-permute-done | bytes 196640 | tf_op jit(solution)/shard_map/ppermute | solution.py:139
  855.6 15.2 %collective-permute-done.11 = bf16[128,768]{1,0:T(8,128)(2,1)} collective-permute-done((bf16[128,768]{1,0:T(8,128)(2,1)}, bf16[128,768]{1,0:T(8,128)(2,1)}, u32[]{:S(2)}, u32[]{:S(2)}) %collective-permute-start.11) | collective-permute-done | bytes 196640 | tf_op jit(solution)/shard_map/ppermute | solution.py:139
  872.4 5.0 collective-permute-done.10
  898.2 5.2 collective-permute-done.40
  909.7 13.6 %collective-permute-start.42 = (bf16[128,2048]{1,0:T(8,128)(2,1)S(1)}, bf16[128,2048]{1,0:T(8,128)(2,1)S(1)}, u32[]{:S(2)}, u32[]{:S(2)}) collective-permute-start(bf16[128,2048]{1,0:T(8,128)(2,1)S(1)} %get-tuple-element.126), channel_id=1, source_target_pairs={{0,16},{2,18},{4,20},{6,22},{8,24},{10,26},{12,28},{14,30},{16,0},... | collective-permute-start | bytes 1572872 | tf_op jit(solution)/shard_map/ppermute | solution.py:139
  923.2 25.0 %collective-permute-done.45 = bf16[512,2048]{1,0:T(8,128)(2,1)} collective-permute-done((bf16[512,2048]{1,0:T(8,128)(2,1)}, bf16[512,2048]{1,0:T(8,128)(2,1)}, u32[]{:S(2)}, u32[]{:S(2)}) %collective-permute-start.45) | collective-permute-done | bytes 2097184 | tf_op jit(solution)/shard_map/ppermute | solution.py:139
  948.3 13.1 %collective-permute-start.41 = (bf16[128,2048]{1,0:T(8,128)(2,1)S(1)}, bf16[128,2048]{1,0:T(8,128)(2,1)S(1)}, u32[]{:S(2)}, u32[]{:S(2)}) collective-permute-start(bf16[128,2048]{1,0:T(8,128)(2,1)S(1)} %get-tuple-element.124), channel_id=1, source_target_pairs={{0,8},{2,10},{4,12},{6,14},{8,0},{10,2},{12,4},{14,6},{16,24},{18,... | collective-permute-start | bytes 1572872 | tf_op jit(solution)/shard_map/ppermute | solution.py:139
  963.3 29.9 %collective-permute-done.50 = bf16[512,2048]{1,0:T(8,128)(2,1)} collective-permute-done((bf16[512,2048]{1,0:T(8,128)(2,1)}, bf16[512,2048]{1,0:T(8,128)(2,1)}, u32[]{:S(2)}, u32[]{:S(2)}) %collective-permute-start.50) | collective-permute-done | bytes 2097184 | tf_op jit(solution)/shard_map/ppermute | solution.py:139
  994.3 30.6 %collective-permute-done.35 = bf16[512,1536]{1,0:T(8,128)(2,1)S(1)} collective-permute-done((bf16[512,1536]{1,0:T(8,128)(2,1)}, bf16[512,1536]{1,0:T(8,128)(2,1)S(1)}, u32[]{:S(2)}, u32[]{:S(2)}) %collective-permute-start.35) | collective-permute-done | bytes 1572896 | tf_op jit(solution)/shard_map/ppermute | solution.py:139
  1025.0 13.1 %collective-permute-start.47 = (bf16[128,2048]{1,0:T(8,128)(2,1)S(1)}, bf16[128,2048]{1,0:T(8,128)(2,1)S(1)}, u32[]{:S(2)}, u32[]{:S(2)}) collective-permute-start(bf16[128,2048]{1,0:T(8,128)(2,1)S(1)} %get-tuple-element.121), channel_id=1, source_target_pairs={{0,16},{2,18},{4,20},{6,22},{8,24},{10,26},{12,28},{14,30},{16,0},... | collective-permute-start | bytes 1572872 | tf_op jit(solution)/shard_map/ppermute | solution.py:139
  1047.1 31.7 %collective-permute-done.47 = bf16[128,2048]{1,0:T(8,128)(2,1)S(1)} collective-permute-done((bf16[128,2048]{1,0:T(8,128)(2,1)S(1)}, bf16[128,2048]{1,0:T(8,128)(2,1)S(1)}, u32[]{:S(2)}, u32[]{:S(2)}) %collective-permute-start.47) | collective-permute-done | bytes 524320 | tf_op jit(solution)/shard_map/ppermute | solution.py:139
  1085.9 33.6 %collective-permute-done.52 = bf16[128,2048]{1,0:T(8,128)(2,1)S(1)} collective-permute-done((bf16[128,2048]{1,0:T(8,128)(2,1)S(1)}, bf16[128,2048]{1,0:T(8,128)(2,1)S(1)}, u32[]{:S(2)}, u32[]{:S(2)}) %collective-permute-start.52) | collective-permute-done | bytes 524320 | tf_op jit(solution)/shard_map/ppermute | solution.py:139
  1127.0 15.2 %collective-permute-start.20 = (bf16[128,1536]{1,0:T(8,128)(2,1)S(1)}, bf16[128,1536]{1,0:T(8,128)(2,1)S(1)}, u32[]{:S(2)}, u32[]{:S(2)}) collective-permute-start(bf16[128,1536]{1,0:T(8,128)(2,1)S(1)} %get-tuple-element.143), channel_id=1, source_target_pairs={{0,8},{2,10},{4,12},{6,14},{8,0},{10,2},{12,4},{14,6},{16,24},{18,... | collective-permute-start | bytes 1179656 | tf_op jit(solution)/shard_map/ppermute | solution.py:139
  1142.2 15.2 %collective-permute-done.37 = bf16[128,1536]{1,0:T(8,128)(2,1)S(1)} collective-permute-done((bf16[128,1536]{1,0:T(8,128)(2,1)S(1)}, bf16[128,1536]{1,0:T(8,128)(2,1)S(1)}, u32[]{:S(2)}, u32[]{:S(2)}) %collective-permute-start.37) | collective-permute-done | bytes 393248 | tf_op jit(solution)/shard_map/ppermute | solution.py:139
  1160.1 23.2 %collective-permute-start.25 = (bf16[128,1536]{1,0:T(8,128)(2,1)S(1)}, bf16[128,1536]{1,0:T(8,128)(2,1)S(1)}, u32[]{:S(2)}, u32[]{:S(2)}) collective-permute-start(bf16[128,1536]{1,0:T(8,128)(2,1)S(1)} %get-tuple-element.138), channel_id=1, source_target_pairs={{0,8},{2,10},{4,12},{6,14},{8,0},{10,2},{12,4},{14,6},{16,24},{18,... | collective-permute-start | bytes 1179656 | tf_op jit(solution)/shard_map/ppermute | solution.py:139
  1183.2 7.9 collective-permute-done.21
  1192.3 13.4 %collective-permute-done.26 = bf16[128,1536]{1,0:T(8,128)(2,1)S(1)} collective-permute-done((bf16[128,1536]{1,0:T(8,128)(2,1)S(1)}, bf16[128,1536]{1,0:T(8,128)(2,1)S(1)}, u32[]{:S(2)}, u32[]{:S(2)}) %collective-permute-start.26) | collective-permute-done | bytes 393248 | tf_op jit(solution)/shard_map/ppermute | solution.py:139
  (717 shorter events, 438.0 us)
Async XLA Ops:
  7.2 181.7 %all-gather.3.cloned.1.call-start = ((), (), s32[]{:S(2)}) async-start(), calls=%async_computation.4 | async-start | bytes 28409856 | tf_op jit(solution)/shard_map/all_gather | solution.py:146
  15.9 313.1 %all-gather.5.cloned.1.call-start = ((), (), s32[]{:S(2)}) async-start(), calls=%async_computation.5 | async-start | bytes 26738688 | tf_op jit(solution)/shard_map/all_gather | solution.py:146
  25.4 47.4 %all-to-all-start = ((bf16[16,16,2048]{2,1,0:T(8,128)(2,1)}), bf16[16,16,2048]{2,1,0:T(8,128)(2,1)S(1)}, u32[]{:S(2)}, u32[]{:S(2)}) async-start(bf16[16,16,2048]{2,1,0:T(8,128)(2,1)} %bitcast.6), calls=%async_computation | async-start | bytes 2097152 | tf_op jit(solution)/shard_map/all_to_all | solution.py:181
  72.8 43.9 %all-to-all-start.2 = ((bf16[16,16,2048]{2,1,0:T(8,128)(2,1)}), bf16[16,16,2048]{2,1,0:T(8,128)(2,1)S(1)}, u32[]{:S(2)}, u32[]{:S(2)}) async-start(bf16[16,16,2048]{2,1,0:T(8,128)(2,1)} %bitcast.50), calls=%async_computation.2 | async-start | bytes 2097152 | tf_op jit(solution)/shard_map/all_to_all | solution.py:181
  81.8 37.9 %collective-permute-start = (bf16[256,2048]{1,0:T(8,128)(2,1)S(1)}, bf16[256,2048]{1,0:T(8,128)(2,1)}, u32[]{:S(2)}, u32[]{:S(2)}) collective-permute-start(bf16[256,2048]{1,0:T(8,128)(2,1)S(1)} %convolution_convert_fusion.12), channel_id=1, source_target_pairs={{0,1},{1,0},{2,3},{3,2},{4,5},{5,4},{6,7},{7,6},{8,9},{9,8},{10,11... | collective-permute-start | bytes 3145736 | tf_op jit(solution)/shard_map/ppermute | solution.py:136
  118.2 176.4 %collective-permute-start.4 = (bf16[256,2048]{1,0:T(8,128)(2,1)}, bf16[256,2048]{1,0:T(8,128)(2,1)}, u32[]{:S(2)}, u32[]{:S(2)}) collective-permute-start(bf16[256,2048]{1,0:T(8,128)(2,1)} %convolution_convert_fusion.8), channel_id=1, source_target_pairs={{0,1},{1,0},{2,3},{3,2},{4,5},{5,4},{6,7},{7,6},{8,9},{9,8},{10,11... | collective-permute-start | bytes 3145736 | tf_op jit(solution)/shard_map/ppermute | solution.py:136
  251.2 29.4 %collective-permute-start.1 = (f32[512]{0:T(512)}, f32[512]{0:T(512)}, u32[]{:S(2)}, u32[]{:S(2)}) collective-permute-start(f32[512]{0:T(512)} %get-tuple-element.104), channel_id=1, source_target_pairs={{0,1},{1,0},{2,3},{3,2},{4,5},{5,4},{6,7},{7,6},{8,9},{9,8},{10,11... | collective-permute-start | bytes 6152 | tf_op jit(solution)/shard_map/ppermute | solution.py:136
  294.3 47.5 %collective-permute-start.2 = (bf16[512,2048]{1,0:T(8,128)(2,1)}, bf16[512,2048]{1,0:T(8,128)(2,1)}, u32[]{:S(2)}, u32[]{:S(2)}) collective-permute-start(bf16[512,2048]{1,0:T(8,128)(2,1)} %add_convert_fusion.6), channel_id=1, source_target_pairs={{0,1},{1,0},{2,3},{3,2},{4,5},{5,4},{6,7},{7,6},{8,9},{9,8},{10,11... | collective-permute-start | bytes 6291464 | tf_op jit(solution)/shard_map/ppermute | solution.py:136
  417.5 46.9 %collective-permute-start.5 = (bf16[512,2048]{1,0:T(8,128)(2,1)}, bf16[512,2048]{1,0:T(8,128)(2,1)}, u32[]{:S(2)}, u32[]{:S(2)}) collective-permute-start(bf16[512,2048]{1,0:T(8,128)(2,1)} %fusion.32), channel_id=1, source_target_pairs={{0,1},{1,0},{2,3},{3,2},{4,5},{5,4},{6,7},{7,6},{8,9},{9,8},{10,11... | collective-permute-start | bytes 6291464 | tf_op jit(solution)/shard_map/ppermute | solution.py:136
  419.6 365.0 %collective-permute-start.39 = (bf16[1024,2048]{1,0:T(8,128)(2,1)}, bf16[1024,2048]{1,0:T(8,128)(2,1)}, u32[]{:S(2)}, u32[]{:S(2)}) collective-permute-start(bf16[1024,2048]{1,0:T(8,128)(2,1)} %convolution_convert_fusion.2), channel_id=1, source_target_pairs={{0,2},{2,0},{4,6},{6,4},{8,10},{10,8},{12,14},{14,12},{16,18},{18,... | collective-permute-start | bytes 12582920 | tf_op jit(solution)/shard_map/ppermute | solution.py:139
  423.1 378.4 %collective-permute-start.44 = (bf16[1024,2048]{1,0:T(8,128)(2,1)}, bf16[1024,2048]{1,0:T(8,128)(2,1)}, u32[]{:S(2)}, u32[]{:S(2)}) collective-permute-start(bf16[1024,2048]{1,0:T(8,128)(2,1)} %convolution_convert_fusion.1), channel_id=1, source_target_pairs={{0,2},{2,0},{4,6},{6,4},{8,10},{10,8},{12,14},{14,12},{16,18},{18,... | collective-permute-start | bytes 12582920 | tf_op jit(solution)/shard_map/ppermute | solution.py:139
  515.7 35.7 %collective-permute-start.6 = (f32[512]{0:T(512)}, f32[512]{0:T(512)}, u32[]{:S(2)}, u32[]{:S(2)}) collective-permute-start(f32[512]{0:T(512)} %get-tuple-element.70), channel_id=1, source_target_pairs={{0,1},{1,0},{2,3},{3,2},{4,5},{5,4},{6,7},{7,6},{8,9},{9,8},{10,11... | collective-permute-start | bytes 6152 | tf_op jit(solution)/shard_map/ppermute | solution.py:136
  528.8 179.5 %collective-permute-start.13 = (bf16[1024,512]{1,0:T(8,128)(2,1)}, bf16[1024,512]{1,0:T(8,128)(2,1)}, u32[]{:S(2)}, u32[]{:S(2)}) collective-permute-start(bf16[1024,512]{1,0:T(8,128)(2,1)} %convolution_convert_fusion.16), channel_id=1, source_target_pairs={{0,2},{2,0},{4,6},{6,4},{8,10},{10,8},{12,14},{14,12},{16,18},{18,... | collective-permute-start | bytes 3145736 | tf_op jit(solution)/shard_map/ppermute | solution.py:139
  648.9 7.2 collective-permute-start.54
  660.4 14.4 %collective-permute-start.56 = (f32[128,128]{1,0:T(8,128)S(1)}, f32[128,128]{1,0:T(8,128)S(1)}, u32[]{:S(2)}, u32[]{:S(2)}) collective-permute-start(f32[128,128]{1,0:T(8,128)S(1)} %fusion.350), channel_id=1, source_target_pairs={{0,8},{2,10},{4,12},{6,14},{8,0},{10,2},{12,4},{14,6},{16,24},{18,... | collective-permute-start | bytes 196616 | tf_op jit(solution)/shard_map/ppermute | solution.py:139
  674.8 5.2 collective-permute-start.57
  677.9 35.6 %collective-permute-start.3 = (bf16[256,2048]{1,0:T(8,128)(2,1)}, bf16[256,2048]{1,0:T(8,128)(2,1)}, u32[]{:S(2)}, u32[]{:S(2)}) collective-permute-start(bf16[256,2048]{1,0:T(8,128)(2,1)} %bitcast.45), channel_id=1, source_target_pairs={{0,1},{1,0},{2,3},{3,2},{4,5},{5,4},{6,7},{7,6},{8,9},{9,8},{10,11... | collective-permute-start | bytes 3145736 | tf_op jit(solution)/shard_map/ppermute | solution.py:136
  680.1 22.8 %collective-permute-start.58 = (f32[128,128]{1,0:T(8,128)S(1)}, f32[128,128]{1,0:T(8,128)S(1)}, u32[]{:S(2)}, u32[]{:S(2)}) collective-permute-start(f32[128,128]{1,0:T(8,128)S(1)} %add.1060), channel_id=1, source_target_pairs={{0,1},{1,0},{2,3},{3,2},{4,5},{5,4},{6,7},{7,6},{8,9},{9,8},{10,11... | collective-permute-start | bytes 196616 | tf_op jit(solution)/shard_map/ppermute | solution.py:136
  702.9 23.1 %collective-permute-start.7 = (bf16[256,2048]{1,0:T(8,128)(2,1)}, bf16[256,2048]{1,0:T(8,128)(2,1)}, u32[]{:S(2)}, u32[]{:S(2)}) collective-permute-start(bf16[256,2048]{1,0:T(8,128)(2,1)} %bitcast.84), channel_id=1, source_target_pairs={{0,1},{1,0},{2,3},{3,2},{4,5},{5,4},{6,7},{7,6},{8,9},{9,8},{10,11... | collective-permute-start | bytes 3145736 | tf_op jit(solution)/shard_map/ppermute | solution.py:136
  708.3 27.9 %collective-permute-start.28 = (bf16[1024,640]{1,0:T(8,128)(2,1)}, bf16[1024,640]{1,0:T(8,128)(2,1)}, u32[]{:S(2)}, u32[]{:S(2)}) collective-permute-start(bf16[1024,640]{1,0:T(8,128)(2,1)} %convolution_convert_fusion.15), channel_id=1, source_target_pairs={{0,2},{2,0},{4,6},{6,4},{8,10},{10,8},{12,14},{14,12},{16,18},{18,... | collective-permute-start | bytes 3932168 | tf_op jit(solution)/shard_map/ppermute | solution.py:139
  713.5 114.2 %collective-permute-start.49 = (bf16[1024,2048]{1,0:T(8,128)(2,1)}, bf16[1024,2048]{1,0:T(8,128)(2,1)}, u32[]{:S(2)}, u32[]{:S(2)}) collective-permute-start(bf16[1024,2048]{1,0:T(8,128)(2,1)} %convolution_convert_fusion), channel_id=1, source_target_pairs={{0,2},{2,0},{4,6},{6,4},{8,10},{10,8},{12,14},{14,12},{16,18},{18,... | collective-permute-start | bytes 12582920 | tf_op jit(solution)/shard_map/ppermute | solution.py:139
  726.0 36.5 %collective-permute-start.8 = (bf16[1024,768]{1,0:T(8,128)(2,1)}, bf16[1024,768]{1,0:T(8,128)(2,1)}, u32[]{:S(2)}, u32[]{:S(2)}) collective-permute-start(bf16[1024,768]{1,0:T(8,128)(2,1)} %convolution_convert_fusion.14), channel_id=1, source_target_pairs={{0,2},{2,0},{4,6},{6,4},{8,10},{10,8},{12,14},{14,12},{16,18},{18,... | collective-permute-start | bytes 4718600 | tf_op jit(solution)/shard_map/ppermute | solution.py:139
  728.9 94.1 %all-to-all-start.1 = ((bf16[16,16,2048]{2,1,0:T(8,128)(2,1)}), bf16[16,16,2048]{2,1,0:T(8,128)(2,1)}, u32[]{:S(2)}, u32[]{:S(2)}) async-start(bf16[16,16,2048]{2,1,0:T(8,128)(2,1)} %bitcast.571), calls=%async_computation.1 | async-start | bytes 2097152 | tf_op jit(solution)/shard_map/all_to_all | solution.py:181
  736.2 23.1 %collective-permute-start.14 = (bf16[512,512]{1,0:T(8,128)(2,1)S(1)}, bf16[512,512]{1,0:T(8,128)(2,1)S(1)}, u32[]{:S(2)}, u32[]{:S(2)}) collective-permute-start(bf16[512,512]{1,0:T(8,128)(2,1)S(1)} %copy-done.181), channel_id=1, source_target_pairs={{0,4},{2,6},{4,0},{6,2},{8,12},{10,14},{12,8},{14,10},{16,20},{18,... | collective-permute-start | bytes 1572872 | tf_op jit(solution)/shard_map/ppermute | solution.py:139
  759.3 16.3 %collective-permute-start.29 = (bf16[512,640]{1,0:T(8,128)(2,1)S(1)}, bf16[512,640]{1,0:T(8,128)(2,1)S(1)}, u32[]{:S(2)}, u32[]{:S(2)}) collective-permute-start(bf16[512,640]{1,0:T(8,128)(2,1)S(1)} %add_convert_fusion.16), channel_id=1, source_target_pairs={{0,4},{2,6},{4,0},{6,2},{8,12},{10,14},{12,8},{14,10},{16,20},{18,... | collective-permute-start | bytes 1966088 | tf_op jit(solution)/shard_map/ppermute | solution.py:139
  762.4 6.9 collective-permute-start.17
  769.3 10.0 collective-permute-start.16
  775.6 5.0 collective-permute-start.15
  779.4 105.0 %collective-permute-start.34 = (bf16[1024,1536]{1,0:T(8,128)(2,1)}, bf16[1024,1536]{1,0:T(8,128)(2,1)}, u32[]{:S(2)}, u32[]{:S(2)}) collective-permute-start(bf16[1024,1536]{1,0:T(8,128)(2,1)} %convolution_convert_fusion.3), channel_id=1, source_target_pairs={{0,2},{2,0},{4,6},{6,4},{8,10},{10,8},{12,14},{14,12},{16,18},{18,... | collective-permute-start | bytes 9437192 | tf_op jit(solution)/shard_map/ppermute | solution.py:139
  780.6 9.0 collective-permute-start.32
  784.6 16.7 %collective-permute-start.31 = (bf16[128,640]{1,0:T(8,128)(2,1)S(1)}, bf16[128,640]{1,0:T(8,128)(2,1)S(1)}, u32[]{:S(2)}, u32[]{:S(2)}) collective-permute-start(bf16[128,640]{1,0:T(8,128)(2,1)S(1)} %get-tuple-element.177), channel_id=1, source_target_pairs={{0,16},{2,18},{4,20},{6,22},{8,24},{10,26},{12,28},{14,30},{16,0},... | collective-permute-start | bytes 491528 | tf_op jit(solution)/shard_map/ppermute | solution.py:139
  789.6 11.7 collective-permute-start.30
  801.3 88.3 %collective-permute-start.18 = (bf16[1024,1536]{1,0:T(8,128)(2,1)}, bf16[1024,1536]{1,0:T(8,128)(2,1)}, u32[]{:S(2)}, u32[]{:S(2)}) collective-permute-start(bf16[1024,1536]{1,0:T(8,128)(2,1)} %convolution_convert_fusion.5), channel_id=1, source_target_pairs={{0,2},{2,0},{4,6},{6,4},{8,10},{10,8},{12,14},{14,12},{16,18},{18,... | collective-permute-start | bytes 9437192 | tf_op jit(solution)/shard_map/ppermute | solution.py:139
  801.3 20.0 %collective-permute-start.9 = (bf16[512,768]{1,0:T(8,128)(2,1)S(1)}, bf16[512,768]{1,0:T(8,128)(2,1)S(1)}, u32[]{:S(2)}, u32[]{:S(2)}) collective-permute-start(bf16[512,768]{1,0:T(8,128)(2,1)S(1)} %add_convert_fusion.14), channel_id=1, source_target_pairs={{0,4},{2,6},{4,0},{6,2},{8,12},{10,14},{12,8},{14,10},{16,20},{18,... | collective-permute-start | bytes 2359304 | tf_op jit(solution)/shard_map/ppermute | solution.py:139
  801.6 29.8 %collective-permute-start.33 = (f32[64,512]{1,0:T(8,128)S(1)}, f32[64,512]{1,0:T(8,128)S(1)}, u32[]{:S(2)}, u32[]{:S(2)}) collective-permute-start(f32[64,512]{1,0:T(8,128)S(1)} %dynamic-slice_bitcast_fusion), channel_id=1, source_target_pairs={{0,1},{1,0},{2,3},{3,2},{4,5},{5,4},{6,7},{7,6},{8,9},{9,8},{10,11... | collective-permute-start | bytes 393224 | tf_op jit(solution)/shard_map/ppermute | solution.py:136
  821.2 85.2 %collective-permute-start.23 = (bf16[1024,1536]{1,0:T(8,128)(2,1)}, bf16[1024,1536]{1,0:T(8,128)(2,1)}, u32[]{:S(2)}, u32[]{:S(2)}) collective-permute-start(bf16[1024,1536]{1,0:T(8,128)(2,1)} %convolution_convert_fusion.4), channel_id=1, source_target_pairs={{0,2},{2,0},{4,6},{6,4},{8,10},{10,8},{12,14},{14,12},{16,18},{18,... | collective-permute-start | bytes 9437192 | tf_op jit(solution)/shard_map/ppermute | solution.py:139
  823.0 68.0 %all-to-all-start.3 = ((bf16[16,16,2048]{2,1,0:T(8,128)(2,1)}), bf16[16,16,2048]{2,1,0:T(8,128)(2,1)}, u32[]{:S(2)}, u32[]{:S(2)}) async-start(bf16[16,16,2048]{2,1,0:T(8,128)(2,1)} %bitcast.87), calls=%async_computation.3 | async-start | bytes 2097152 | tf_op jit(solution)/shard_map/all_to_all | solution.py:181
  827.7 26.4 %collective-permute-start.12 = (bf16[128,768]{1,0:T(8,128)(2,1)}, bf16[128,768]{1,0:T(8,128)(2,1)}, u32[]{:S(2)}, u32[]{:S(2)}) collective-permute-start(bf16[128,768]{1,0:T(8,128)(2,1)} %get-tuple-element.173), channel_id=1, source_target_pairs={{0,24},{2,26},{4,28},{6,30},{8,16},{10,18},{12,20},{14,22},{16,8},... | collective-permute-start | bytes 589832 | tf_op jit(solution)/shard_map/ppermute | solution.py:139
  831.3 39.4 %collective-permute-start.11 = (bf16[128,768]{1,0:T(8,128)(2,1)}, bf16[128,768]{1,0:T(8,128)(2,1)}, u32[]{:S(2)}, u32[]{:S(2)}) collective-permute-start(bf16[128,768]{1,0:T(8,128)(2,1)} %get-tuple-element.174), channel_id=1, source_target_pairs={{0,16},{2,18},{4,20},{6,22},{8,24},{10,26},{12,28},{14,30},{16,0},... | collective-permute-start | bytes 589832 | tf_op jit(solution)/shard_map/ppermute | solution.py:139
  854.1 49.3 %collective-permute-start.40 = (bf16[512,2048]{1,0:T(8,128)(2,1)}, bf16[512,2048]{1,0:T(8,128)(2,1)}, u32[]{:S(2)}, u32[]{:S(2)}) collective-permute-start(bf16[512,2048]{1,0:T(8,128)(2,1)} %get-tuple-element.128), channel_id=1, source_target_pairs={{0,4},{2,6},{4,0},{6,2},{8,12},{10,14},{12,8},{14,10},{16,20},{18,... | collective-permute-start | bytes 6291464 | tf_op jit(solution)/shard_map/ppermute | solution.py:139
  870.8 6.7 collective-permute-start.10
  877.4 70.9 %collective-permute-start.45 = (bf16[512,2048]{1,0:T(8,128)(2,1)}, bf16[512,2048]{1,0:T(8,128)(2,1)}, u32[]{:S(2)}, u32[]{:S(2)}) collective-permute-start(bf16[512,2048]{1,0:T(8,128)(2,1)} %get-tuple-element.123), channel_id=1, source_target_pairs={{0,4},{2,6},{4,0},{6,2},{8,12},{10,14},{12,8},{14,10},{16,20},{18,... | collective-permute-start | bytes 6291464 | tf_op jit(solution)/shard_map/ppermute | solution.py:139
  884.3 108.9 %collective-permute-start.50 = (bf16[512,2048]{1,0:T(8,128)(2,1)}, bf16[512,2048]{1,0:T(8,128)(2,1)}, u32[]{:S(2)}, u32[]{:S(2)}) collective-permute-start(bf16[512,2048]{1,0:T(8,128)(2,1)} %get-tuple-element.118), channel_id=1, source_target_pairs={{0,4},{2,6},{4,0},{6,2},{8,12},{10,14},{12,8},{14,10},{16,20},{18,... | collective-permute-start | bytes 6291464 | tf_op jit(solution)/shard_map/ppermute | solution.py:139
  889.6 135.4 %collective-permute-start.35 = (bf16[512,1536]{1,0:T(8,128)(2,1)}, bf16[512,1536]{1,0:T(8,128)(2,1)S(1)}, u32[]{:S(2)}, u32[]{:S(2)}) collective-permute-start(bf16[512,1536]{1,0:T(8,128)(2,1)} %get-tuple-element.137), channel_id=1, source_target_pairs={{0,4},{2,6},{4,0},{6,2},{8,12},{10,14},{12,8},{14,10},{16,20},{18,... | collective-permute-start | bytes 4718600 | tf_op jit(solution)/shard_map/ppermute | solution.py:139
  905.3 132.7 %collective-permute-start.43 = (bf16[128,2048]{1,0:T(8,128)(2,1)S(1)}, bf16[128,2048]{1,0:T(8,128)(2,1)S(1)}, u32[]{:S(2)}, u32[]{:S(2)}) collective-permute-start(bf16[128,2048]{1,0:T(8,128)(2,1)S(1)} %get-tuple-element.125), channel_id=1, source_target_pairs={{0,24},{2,26},{4,28},{6,30},{8,16},{10,18},{12,20},{14,22},{16,8},... | collective-permute-start | bytes 1572872 | tf_op jit(solution)/shard_map/ppermute | solution.py:139
  909.7 130.5 %collective-permute-start.42 = (bf16[128,2048]{1,0:T(8,128)(2,1)S(1)}, bf16[128,2048]{1,0:T(8,128)(2,1)S(1)}, u32[]{:S(2)}, u32[]{:S(2)}) collective-permute-start(bf16[128,2048]{1,0:T(8,128)(2,1)S(1)} %get-tuple-element.126), channel_id=1, source_target_pairs={{0,16},{2,18},{4,20},{6,22},{8,24},{10,26},{12,28},{14,30},{16,0},... | collective-permute-start | bytes 1572872 | tf_op jit(solution)/shard_map/ppermute | solution.py:139
  948.3 93.4 %collective-permute-start.41 = (bf16[128,2048]{1,0:T(8,128)(2,1)S(1)}, bf16[128,2048]{1,0:T(8,128)(2,1)S(1)}, u32[]{:S(2)}, u32[]{:S(2)}) collective-permute-start(bf16[128,2048]{1,0:T(8,128)(2,1)S(1)} %get-tuple-element.124), channel_id=1, source_target_pairs={{0,8},{2,10},{4,12},{6,14},{8,0},{10,2},{12,4},{14,6},{16,24},{18,... | collective-permute-start | bytes 1572872 | tf_op jit(solution)/shard_map/ppermute | solution.py:139
  993.2 51.5 %collective-permute-start.48 = (bf16[128,2048]{1,0:T(8,128)(2,1)S(1)}, bf16[128,2048]{1,0:T(8,128)(2,1)S(1)}, u32[]{:S(2)}, u32[]{:S(2)}) collective-permute-start(bf16[128,2048]{1,0:T(8,128)(2,1)S(1)} %get-tuple-element.120), channel_id=1, source_target_pairs={{0,24},{2,26},{4,28},{6,30},{8,16},{10,18},{12,20},{14,22},{16,8},... | collective-permute-start | bytes 1572872 | tf_op jit(solution)/shard_map/ppermute | solution.py:139
  1025.0 53.8 %collective-permute-start.47 = (bf16[128,2048]{1,0:T(8,128)(2,1)S(1)}, bf16[128,2048]{1,0:T(8,128)(2,1)S(1)}, u32[]{:S(2)}, u32[]{:S(2)}) collective-permute-start(bf16[128,2048]{1,0:T(8,128)(2,1)S(1)} %get-tuple-element.121), channel_id=1, source_target_pairs={{0,16},{2,18},{4,20},{6,22},{8,24},{10,26},{12,28},{14,30},{16,0},... | collective-permute-start | bytes 1572872 | tf_op jit(solution)/shard_map/ppermute | solution.py:139
  1038.1 40.7 %collective-permute-start.46 = (bf16[128,2048]{1,0:T(8,128)(2,1)S(1)}, bf16[128,2048]{1,0:T(8,128)(2,1)S(1)}, u32[]{:S(2)}, u32[]{:S(2)}) collective-permute-start(bf16[128,2048]{1,0:T(8,128)(2,1)S(1)} %get-tuple-element.119), channel_id=1, source_target_pairs={{0,8},{2,10},{4,12},{6,14},{8,0},{10,2},{12,4},{14,6},{16,24},{18,... | collective-permute-start | bytes 1572872 | tf_op jit(solution)/shard_map/ppermute | solution.py:139
  1040.2 83.8 %collective-permute-start.19 = (bf16[512,1536]{1,0:T(8,128)(2,1)S(1)}, bf16[512,1536]{1,0:T(8,128)(2,1)S(1)}, u32[]{:S(2)}, u32[]{:S(2)}) collective-permute-start(bf16[512,1536]{1,0:T(8,128)(2,1)S(1)} %get-tuple-element.147), channel_id=1, source_target_pairs={{0,4},{2,6},{4,0},{6,2},{8,12},{10,14},{12,8},{14,10},{16,20},{18,... | collective-permute-start | bytes 4718600 | tf_op jit(solution)/shard_map/ppermute | solution.py:139
  1041.7 85.0 %collective-permute-start.24 = (bf16[512,1536]{1,0:T(8,128)(2,1)S(1)}, bf16[512,1536]{1,0:T(8,128)(2,1)S(1)}, u32[]{:S(2)}, u32[]{:S(2)}) collective-permute-start(bf16[512,1536]{1,0:T(8,128)(2,1)S(1)} %get-tuple-element.142), channel_id=1, source_target_pairs={{0,4},{2,6},{4,0},{6,2},{8,12},{10,14},{12,8},{14,10},{16,20},{18,... | collective-permute-start | bytes 4718600 | tf_op jit(solution)/shard_map/ppermute | solution.py:139
  1044.7 38.8 %collective-permute-start.53 = (bf16[128,2048]{1,0:T(8,128)(2,1)S(1)}, bf16[128,2048]{1,0:T(8,128)(2,1)S(1)}, u32[]{:S(2)}, u32[]{:S(2)}) collective-permute-start(bf16[128,2048]{1,0:T(8,128)(2,1)S(1)} %get-tuple-element.115), channel_id=1, source_target_pairs={{0,24},{2,26},{4,28},{6,30},{8,16},{10,18},{12,20},{14,22},{16,8},... | collective-permute-start | bytes 1572872 | tf_op jit(solution)/shard_map/ppermute | solution.py:139
  1078.7 40.7 %collective-permute-start.52 = (bf16[128,2048]{1,0:T(8,128)(2,1)S(1)}, bf16[128,2048]{1,0:T(8,128)(2,1)S(1)}, u32[]{:S(2)}, u32[]{:S(2)}) collective-permute-start(bf16[128,2048]{1,0:T(8,128)(2,1)S(1)} %get-tuple-element.116), channel_id=1, source_target_pairs={{0,16},{2,18},{4,20},{6,22},{8,24},{10,26},{12,28},{14,30},{16,0},... | collective-permute-start | bytes 1572872 | tf_op jit(solution)/shard_map/ppermute | solution.py:139
  1078.8 40.7 %collective-permute-start.51 = (bf16[128,2048]{1,0:T(8,128)(2,1)S(1)}, bf16[128,2048]{1,0:T(8,128)(2,1)S(1)}, u32[]{:S(2)}, u32[]{:S(2)}) collective-permute-start(bf16[128,2048]{1,0:T(8,128)(2,1)S(1)} %get-tuple-element.114), channel_id=1, source_target_pairs={{0,8},{2,10},{4,12},{6,14},{8,0},{10,2},{12,4},{14,6},{16,24},{18,... | collective-permute-start | bytes 1572872 | tf_op jit(solution)/shard_map/ppermute | solution.py:139
  1083.5 43.5 %collective-permute-start.38 = (bf16[128,1536]{1,0:T(8,128)(2,1)S(1)}, bf16[128,1536]{1,0:T(8,128)(2,1)S(1)}, u32[]{:S(2)}, u32[]{:S(2)}) collective-permute-start(bf16[128,1536]{1,0:T(8,128)(2,1)S(1)} %get-tuple-element.134), channel_id=1, source_target_pairs={{0,24},{2,26},{4,28},{6,30},{8,16},{10,18},{12,20},{14,22},{16,8},... | collective-permute-start | bytes 1179656 | tf_op jit(solution)/shard_map/ppermute | solution.py:139
  1119.5 37.9 %collective-permute-start.37 = (bf16[128,1536]{1,0:T(8,128)(2,1)S(1)}, bf16[128,1536]{1,0:T(8,128)(2,1)S(1)}, u32[]{:S(2)}, u32[]{:S(2)}) collective-permute-start(bf16[128,1536]{1,0:T(8,128)(2,1)S(1)} %get-tuple-element.135), channel_id=1, source_target_pairs={{0,16},{2,18},{4,20},{6,22},{8,24},{10,26},{12,28},{14,30},{16,0},... | collective-permute-start | bytes 1179656 | tf_op jit(solution)/shard_map/ppermute | solution.py:139
  1119.5 39.4 %collective-permute-start.36 = (bf16[128,1536]{1,0:T(8,128)(2,1)S(1)}, bf16[128,1536]{1,0:T(8,128)(2,1)S(1)}, u32[]{:S(2)}, u32[]{:S(2)}) collective-permute-start(bf16[128,1536]{1,0:T(8,128)(2,1)S(1)} %get-tuple-element.133), channel_id=1, source_target_pairs={{0,8},{2,10},{4,12},{6,14},{8,0},{10,2},{12,4},{14,6},{16,24},{18,... | collective-permute-start | bytes 1179656 | tf_op jit(solution)/shard_map/ppermute | solution.py:139
  1124.3 35.8 %collective-permute-start.22 = (bf16[128,1536]{1,0:T(8,128)(2,1)S(1)}, bf16[128,1536]{1,0:T(8,128)(2,1)S(1)}, u32[]{:S(2)}, u32[]{:S(2)}) collective-permute-start(bf16[128,1536]{1,0:T(8,128)(2,1)S(1)} %get-tuple-element.144), channel_id=1, source_target_pairs={{0,24},{2,26},{4,28},{6,30},{8,16},{10,18},{12,20},{14,22},{16,8},... | collective-permute-start | bytes 1179656 | tf_op jit(solution)/shard_map/ppermute | solution.py:139
  1126.7 64.5 %collective-permute-start.21 = (bf16[128,1536]{1,0:T(8,128)(2,1)S(1)}, bf16[128,1536]{1,0:T(8,128)(2,1)S(1)}, u32[]{:S(2)}, u32[]{:S(2)}) collective-permute-start(bf16[128,1536]{1,0:T(8,128)(2,1)S(1)} %get-tuple-element.145), channel_id=1, source_target_pairs={{0,16},{2,18},{4,20},{6,22},{8,24},{10,26},{12,28},{14,30},{16,0},... | collective-permute-start | bytes 1179656 | tf_op jit(solution)/shard_map/ppermute | solution.py:139
  1127.0 64.1 %collective-permute-start.20 = (bf16[128,1536]{1,0:T(8,128)(2,1)S(1)}, bf16[128,1536]{1,0:T(8,128)(2,1)S(1)}, u32[]{:S(2)}, u32[]{:S(2)}) collective-permute-start(bf16[128,1536]{1,0:T(8,128)(2,1)S(1)} %get-tuple-element.143), channel_id=1, source_target_pairs={{0,8},{2,10},{4,12},{6,14},{8,0},{10,2},{12,4},{14,6},{16,24},{18,... | collective-permute-start | bytes 1179656 | tf_op jit(solution)/shard_map/ppermute | solution.py:139
  1157.4 34.9 %collective-permute-start.27 = (bf16[128,1536]{1,0:T(8,128)(2,1)S(1)}, bf16[128,1536]{1,0:T(8,128)(2,1)S(1)}, u32[]{:S(2)}, u32[]{:S(2)}) collective-permute-start(bf16[128,1536]{1,0:T(8,128)(2,1)S(1)} %get-tuple-element.139), channel_id=1, source_target_pairs={{0,24},{2,26},{4,28},{6,30},{8,16},{10,18},{12,20},{14,22},{16,8},... | collective-permute-start | bytes 1179656 | tf_op jit(solution)/shard_map/ppermute | solution.py:139
  1158.9 46.8 %collective-permute-start.26 = (bf16[128,1536]{1,0:T(8,128)(2,1)S(1)}, bf16[128,1536]{1,0:T(8,128)(2,1)S(1)}, u32[]{:S(2)}, u32[]{:S(2)}) collective-permute-start(bf16[128,1536]{1,0:T(8,128)(2,1)S(1)} %get-tuple-element.140), channel_id=1, source_target_pairs={{0,16},{2,18},{4,20},{6,22},{8,24},{10,26},{12,28},{14,30},{16,0},... | collective-permute-start | bytes 1179656 | tf_op jit(solution)/shard_map/ppermute | solution.py:139
  1160.1 45.6 %collective-permute-start.25 = (bf16[128,1536]{1,0:T(8,128)(2,1)S(1)}, bf16[128,1536]{1,0:T(8,128)(2,1)S(1)}, u32[]{:S(2)}, u32[]{:S(2)}) collective-permute-start(bf16[128,1536]{1,0:T(8,128)(2,1)S(1)} %get-tuple-element.138), channel_id=1, source_target_pairs={{0,8},{2,10},{4,12},{6,14},{8,0},{10,2},{12,4},{14,6},{16,24},{18,... | collective-permute-start | bytes 1179656 | tf_op jit(solution)/shard_map/ppermute | solution.py:139
  (191 other events, 2959.1 us)
Sparse Core Ops, SparseCore 0:
  16.1 172.8 all-gather.2
  190.5 138.4 all-gather.4

commit v2 on v1

v2 whole, which is shorter than its diff:
```python
import math

import jax
import jax.numpy as jnp
from jax import lax
from jax.experimental import pallas as pl
from jax.experimental.pallas import tpu as pltpu
from jax.sharding import PartitionSpec as P

HEAD = 128
SH = 48
SHD = 64
NS = 256
CONV = 4
STEP_PAD = 128

epsilon = 1e-05
rope_base = 100000000000.0
f32 = jnp.float32
bf16 = jnp.bfloat16


def project(left, right):
    return jnp.dot(left, right, preferred_element_type=f32)


def project_back(left, right):
    return lax.dot_general(left, right, (((1,), (1,)), ((), ())), preferred_element_type=f32)


def outer_sum(left, right):
    return lax.dot_general(left, right, (((0,), (0,)), ((), ())), preferred_element_type=f32)


def rms_scale(values):
    return lax.rsqrt(jnp.mean(values * values, axis=-1, keepdims=True) + epsilon)


def rms_back(grad, values, scale, gain):
    weighted = grad * gain
    inner = jnp.sum(weighted * values, axis=-1, keepdims=True)
    return scale * weighted - values * (scale * scale * scale * inner / values.shape[-1])


def shift_down(values, count):
    return jnp.concatenate([jnp.zeros((count, values.shape[1]), values.dtype), values[:-count]], axis=0)


def shift_up(values, count):
    return jnp.concatenate([values[count:], jnp.zeros((count, values.shape[1]), values.dtype)], axis=0)


def conv_sum(signal, kernel, position):
    summed = kernel[CONV][None, :] + signal * kernel[0][None, :]
    for tap in range(1, CONV):
        moved = jnp.where(position >= tap, shift_down(signal, tap), 0.0)
        summed = summed + moved * kernel[tap][None, :]
    return summed


def silu_back(values):
    sig = jax.nn.sigmoid(values)
    return sig * (1.0 + values * (1.0 - sig))


def conv_back(grad, signal, kernel, position):
    grad_sum = grad * silu_back(conv_sum(signal, kernel, position))
    grad_signal = grad_sum * kernel[0][None, :]
    grad_taps = [jnp.sum(grad_sum * signal, axis=0)]
    for tap in range(1, CONV):
        kept = jnp.where(position >= tap, grad_sum, 0.0)
        grad_signal = grad_signal + shift_up(kept, tap) * kernel[tap][None, :]
        grad_taps.append(jnp.sum(kept * shift_down(signal, tap), axis=0))
    grad_taps.append(jnp.sum(grad_sum, axis=0))
    return grad_signal, jnp.stack(grad_taps)


def rope_tables(position):
    half_size = HEAD // 2
    frequency = jnp.exp(jnp.arange(half_size, dtype=f32) * (-2.0 * math.log(rope_base) / HEAD))
    angles = position.astype(f32) * frequency[None, :]
    return jnp.cos(angles)[:, None, :], jnp.sin(angles)[:, None, :]


def rotate(values, cosine, sine):
    half_size = HEAD // 2
    first, second = values[..., :half_size], values[..., half_size:]
    return jnp.concatenate([first * cosine - second * sine, second * cosine + first * sine], axis=-1)


def copy_block(order_ref, source_ref, target_ref):
    target_ref[...] = source_ref[...]


def pick_blocks(values, order, block):
    height, width = values.shape
    if block % 128:
        return jnp.take(values.reshape(height, -1, block), order, axis=1).reshape(height, width)
    return pl.pallas_call(
        copy_block,
        out_shape=jax.ShapeDtypeStruct(values.shape, values.dtype),
        grid_spec=pltpu.PrefetchScalarGridSpec(
            num_scalar_prefetch=1,
            grid=(width // block,),
            in_specs=[pl.BlockSpec((height, block), lambda i, order: (0, order[i]))],
            out_specs=pl.BlockSpec((height, block), lambda i, order: (0, i)),
        ),
        cost_estimate=pl.CostEstimate(flops=0, transcendentals=0, bytes_accessed=4 * height * width),
    )(order, values)


def rotate_back(values, cosine, sine):
    return rotate(values, cosine, -sine)


NEGATIVE = -1e30


def sigmoid_of(values):
    return 1.0 / (1.0 + jnp.exp(-values))


def block_mask(rows, segment_col, segment_row):
    row_index = lax.broadcasted_iota(jnp.int32, (rows, rows), 0)
    col_index = lax.broadcasted_iota(jnp.int32, (rows, rows), 1)
    return jnp.where((segment_col == segment_row) & (col_index <= row_index), 0.0, NEGATIVE)


def conv_block(signal, taps_ref, position):
    summed = taps_ref[CONV : CONV + 1, :] + signal * taps_ref[0:1, :]
    moved = []
    for tap in range(1, CONV):
        shifted = jnp.where(position >= tap, pltpu.roll(signal, tap, 0), 0.0)
        moved.append(shifted)
        summed = summed + shifted * taps_ref[tap : tap + 1, :]
    return summed, moved


def mixing_block(inner, mask, run_col, run_row, step_row):
    decay = jnp.exp(run_col - run_row + mask)
    return decay, (inner * decay * step_row).astype(bf16)


def state_forward_kernel(
    signal_ref, gate_ref, taps_ref, skip_ref, state_ref, seg_col_ref, seg_row_ref, position_ref,
    run_row_ref, run_col_ref, step_ref, out_ref, square_ref, inner_ref, mask_ref,
):
    rows = signal_ref.shape[0]

    @pl.when(pl.program_id(1) == 0)
    def _():
        inner_ref[...] = lax.dot_general(
            state_ref[:, NS:], state_ref[:, :NS], (((1,), (1,)), ((), ())), preferred_element_type=f32
        )
        mask_ref[...] = block_mask(rows, seg_col_ref[...], seg_row_ref[0])
        square_ref[...] = jnp.zeros_like(square_ref)

    summed, _ = conv_block(signal_ref[...], taps_ref, position_ref[...])
    cols = summed * sigmoid_of(summed)
    cols_low = cols.astype(bf16)
    mixed = []
    for head in range(2):
        _, mixing = mixing_block(
            inner_ref[...], mask_ref[...], run_col_ref[0, 0, :, head : head + 1],
            run_row_ref[0, 0, head : head + 1, :], step_ref[0, 0, head : head + 1, :],
        )
        mixed.append(jnp.dot(mixing, cols_low, preferred_element_type=f32))
    lanes = lax.broadcasted_iota(jnp.int32, cols.shape, 1)
    out = jnp.where(lanes < SHD, mixed[0], mixed[1]) + skip_ref[...] * cols
    out_ref[...] = out
    gate = gate_ref[...]
    gated = out * (gate * sigmoid_of(gate))
    square_ref[...] += gated * gated


def state_backward_kernel(
    grad_ref, out_ref, gate_ref, signal_ref, taps_ref, skip_ref, gain_ref, scale_ref, cross_ref, state_ref,
    seg_col_ref, seg_row_ref, position_ref, run_row_ref, run_col_ref, step_ref,
    gate_low_ref, input_low_ref, sums_ref, direct_ref, along_ref, state_grad_ref, inner_ref, mask_ref, grad_inner_ref,
):
    rows = signal_ref.shape[0]

    @pl.when(pl.program_id(1) == 0)
    def _():
        inner_ref[...] = lax.dot_general(
            state_ref[:, NS:], state_ref[:, :NS], (((1,), (1,)), ((), ())), preferred_element_type=f32
        )
        mask_ref[...] = block_mask(rows, seg_col_ref[...], seg_row_ref[0])
        grad_inner_ref[...] = jnp.zeros_like(grad_inner_ref)

    grad, out, gate, signal = grad_ref[...], out_ref[...], gate_ref[...], signal_ref[...]
    position = position_ref[...]
    sig = sigmoid_of(gate)
    silu = gate * sig
    gated = out * silu
    scaled = grad * scale_ref[...]
    grad_gated = scaled * gain_ref[...] - gated * cross_ref[...]
    grad_out = grad_gated * silu
    gate_low_ref[...] = (grad_gated * out * (sig * (1.0 + gate * (1.0 - sig)))).astype(bf16)
    summed, moved = conv_block(signal, taps_ref, position)
    sig = sigmoid_of(summed)
    cols = summed * sig
    cols_low = cols.astype(bf16)
    grad_low = grad_out.astype(bf16)
    lanes = lax.broadcasted_iota(jnp.int32, cols.shape, 1)
    zero = jnp.zeros_like(grad_low)
    grad_cols = []
    for head in range(2):
        step_row = step_ref[0, 0, head : head + 1, :]
        inner = inner_ref[...]
        decay, mixing = mixing_block(
            inner, mask_ref[...], run_col_ref[0, 0, :, head : head + 1], run_row_ref[0, 0, head : head + 1, :], step_row
        )
        grad_cols.append(
            lax.dot_general(mixing, grad_low, (((0,), (0,)), ((), ())), preferred_element_type=f32)
        )
        grad_head = jnp.where((lanes < SHD) == (head == 0), grad_low, zero)
        grad_decay = lax.dot_general(
            grad_head, cols_low, (((1,), (1,)), ((), ())), preferred_element_type=f32
        ) * decay
        stepped = grad_decay * step_row
        grad_inner_ref[...] += stepped
        direct_ref[0, 0, head : head + 1, :] = jnp.sum(grad_decay * inner, axis=0, keepdims=True)
        along_ref[0, 0, :, head : head + 1] = jnp.sum(stepped * inner, axis=1, keepdims=True)
    grad_cols = jnp.where(lanes < SHD, grad_cols[0], grad_cols[1]) + skip_ref[...] * grad_out
    grad_sum = grad_cols * (sig * (1.0 + summed * (1.0 - sig)))
    grad_signal = grad_sum * taps_ref[0:1, :]
    sums_ref[0, 0:1, :] = jnp.sum(grad_sum * signal, axis=0, keepdims=True)
    for tap in range(1, CONV):
        kept = jnp.where(position >= tap, grad_sum, 0.0)
        grad_signal = grad_signal + pltpu.roll(kept, rows - tap, 0) * taps_ref[tap : tap + 1, :]
        sums_ref[0, tap : tap + 1, :] = jnp.sum(grad_sum * moved[tap - 1], axis=0, keepdims=True)
    sums_ref[0, CONV : CONV + 1, :] = jnp.sum(grad_sum, axis=0, keepdims=True)
    sums_ref[0, CONV + 1 : CONV + 2, :] = jnp.sum(scaled * gated, axis=0, keepdims=True)
    sums_ref[0, CONV + 2 : CONV + 3, :] = jnp.sum(grad_out * cols, axis=0, keepdims=True)
    sums_ref[0, CONV + 3 : CONV + 4, :] = jnp.zeros((1, cols.shape[1]), f32)
    input_low_ref[...] = grad_signal.astype(bf16)

    @pl.when(pl.program_id(1) == pl.num_programs(1) - 1)
    def _():
        inner_low = grad_inner_ref[...].astype(bf16)
        state_grad_ref[:, :NS] = lax.dot_general(
            inner_low, state_ref[:, NS:], (((0,), (0,)), ((), ())), preferred_element_type=f32
        )
        state_grad_ref[:, NS:] = jnp.dot(inner_low, state_ref[:, :NS], preferred_element_type=f32)


def state_specs(rows, pairs):
    block = pl.BlockSpec((rows, 2 * SHD), lambda m, p: (m, p))
    return {
        "block": block,
        "taps": pl.BlockSpec((CONV + 1, 2 * SHD), lambda m, p: (0, p)),
        "vector": pl.BlockSpec((1, 2 * SHD), lambda m, p: (0, p)),
        "state": pl.BlockSpec((rows, 2 * NS), lambda m, p: (m, 0)),
        "column": pl.BlockSpec((rows, 1), lambda m, p: (m, 0)),
        "row": pl.BlockSpec((1, 1, rows), lambda m, p: (m, 0, 0)),
        "head_row": pl.BlockSpec((1, 1, 2, rows), lambda m, p: (m, p, 0, 0)),
        "head_col": pl.BlockSpec((1, 1, rows, 2), lambda m, p: (m, p, 0, 0)),
    }


def state_forward(signal, gate, taps, skip, state, seg_col, seg_row, position, run_row, run_col, step):
    micro, pairs, _, rows = run_row.shape
    spec = state_specs(rows, pairs)
    total, width = signal.shape
    return pl.pallas_call(
        state_forward_kernel,
        out_shape=(jax.ShapeDtypeStruct((total, width), f32), jax.ShapeDtypeStruct((total, 2 * SHD), f32)),
        grid=(micro, pairs),
        in_specs=[spec[name] for name in (
            "block", "block", "taps", "vector", "state", "column", "row", "column", "head_row", "head_col", "head_row")],
        out_specs=(spec["block"], pl.BlockSpec((rows, 2 * SHD), lambda m, p: (m, 0))),
        scratch_shapes=[pltpu.VMEM((rows, rows), f32), pltpu.VMEM((rows, rows), f32)],
        cost_estimate=pl.CostEstimate(
            flops=8 * total * rows * width // SHD * SHD, transcendentals=total * rows * width // SHD, bytes_accessed=12 * total * width
        ),
        name="state_forward",
    )(signal, gate, taps, skip, state, seg_col, seg_row, position, run_row, run_col, step)


def state_backward(grad, out, gate, signal, taps, skip, gain, scale, cross, state, seg_col, seg_row, position, run_row, run_col, step):
    micro, pairs, _, rows = run_row.shape
    spec = state_specs(rows, pairs)
    total, width = signal.shape
    return pl.pallas_call(
        state_backward_kernel,
        out_shape=(
            jax.ShapeDtypeStruct((total, width), bf16),
            jax.ShapeDtypeStruct((total, width), bf16),
            jax.ShapeDtypeStruct((micro, 8, width), f32),
            jax.ShapeDtypeStruct(run_row.shape, f32),
            jax.ShapeDtypeStruct(run_col.shape, f32),
            jax.ShapeDtypeStruct((total, 2 * NS), f32),
        ),
        grid=(micro, pairs),
        in_specs=[spec[name] for name in (
            "block", "block", "block", "block", "taps", "vector", "vector", "column", "column", "state",
            "column", "row", "column", "head_row", "head_col", "head_row")],
        out_specs=(
            spec["block"], spec["block"], pl.BlockSpec((1, 8, 2 * SHD), lambda m, p: (m, 0, p)),
            spec["head_row"], spec["head_col"], spec["state"],
        ),
        scratch_shapes=[pltpu.VMEM((rows, rows), f32)] * 3,
        cost_estimate=pl.CostEstimate(
            flops=20 * total * rows * width, transcendentals=total * rows * width // SHD, bytes_accessed=20 * total * width
        ),
        name="state_backward",
    )(grad, out, gate, signal, taps, skip, gain, scale, cross, state, seg_col, seg_row, position, run_row, run_col, step)


def local(
    inputs,
    out_grad,
    deal_order,
    segment,
    query_weight,
    key_weight,
    value_weight,
    attention_out,
    mamba_gate,
    mamba_input,
    step_weight,
    state_weight,
    mamba_out,
    feed_gate,
    feed_up,
    feed_down,
    gain_input,
    gain_middle,
    kernel_inner,
    kernel_state,
    mixer_gain,
    step_bias,
    log_rate,
    skip_gain,
):
    micro, own, width = inputs.shape
    groups = lax.axis_size("dp")
    lanes = lax.axis_size("tensor")
    lane = lax.axis_index("tensor")
    group = lax.axis_index("dp")
    device = group * lanes + lane
    per = own // groups
    rows = own * lanes
    total = micro * rows
    inner_width = SH * SHD
    scale_factor = HEAD ** (-0.5)
    outer_count = groups // 4
    shard = width // groups

    swap_lane = [(0, 1), (1, 0)]

    def other_lane(values):
        return lax.ppermute(values, "tensor", swap_lane)

    def other_group(values, bits):
        return lax.ppermute(values, "dp", [(i, i ^ bits) for i in range(groups)])

    step_padded = jnp.pad(step_weight, ((0, 0), (0, STEP_PAD - step_weight.shape[1])))
    early = [mamba_gate, mamba_input, state_weight, step_padded, query_weight, key_weight, value_weight, mamba_out, attention_out]
    late = [feed_gate, feed_up, feed_down]

    def gather(pieces):
        whole = lax.all_gather(jnp.concatenate(pieces, axis=1), "dp", axis=0, tiled=True)
        found, start = [], 0
        for piece in pieces:
            found.append(whole[:, start : start + piece.shape[1]])
            start += piece.shape[1]
        return found

    full_gate, full_input, full_state, full_step, full_query, full_key, full_value, full_mix, full_attn = gather(early)
    full_fgate, full_fup, full_fdown = gather(late)

    own_places = jnp.arange(own, dtype=jnp.int32)
    own_order = lax.dynamic_slice_in_dim(deal_order, device * own, own, 1)
    micro_index = jnp.arange(micro, dtype=jnp.int32)[:, None]

    def buffer_place(destination, rank):
        return destination * (micro * per) + micro_index * per + rank

    send_rank = jnp.sum((own_order[:, None, :] < own_order[:, :, None]).astype(jnp.int32), axis=2)
    send_place = buffer_place(send_rank // per, send_rank % per).reshape(-1)
    lane_order = lax.dynamic_index_in_dim(deal_order.reshape(micro, groups, lanes, own), lane, 2, keepdims=False)
    slots = device * own + own_places
    found = lane_order[:, None, :, :] == slots[None, :, None, None]
    source = jnp.sum(
        jnp.where(found, jnp.arange(groups, dtype=jnp.int32)[None, None, :, None], 0), axis=(2, 3)
    )
    recv_rank = jnp.sum(
        ((source[:, None, :] == source[:, :, None]) & (own_places[None, None, :] < own_places[None, :, None])).astype(jnp.int32),
        axis=2,
    )
    recv_place = buffer_place(source, recv_rank).reshape(-1)
    buffer_places = jnp.arange(micro * own, dtype=jnp.int32)
    send_pick = (buffer_places[:, None] == send_place[None, :]).astype(bf16)
    recv_pick = (recv_place[:, None] == buffer_places[None, :]).astype(bf16)

    def exchange(buffer):
        return lax.all_to_all(
            buffer.reshape(groups, micro * per, width), "dp", split_axis=0, concat_axis=0, tiled=True
        ).reshape(micro * own, width)

    def deal(values):
        sent = project(send_pick, values.reshape(micro * own, width)).astype(bf16)
        return project(recv_pick, exchange(sent)).astype(bf16)

    def deal_order_rows(values):
        return outer_sum(recv_pick, values).astype(bf16)

    def deal_take(moved):
        return outer_sum(send_pick, moved).astype(bf16).reshape(micro, own, width)

    def join_lanes(values):
        mine = values.reshape(micro, 1, own, -1)
        theirs = other_lane(values).reshape(micro, 1, own, -1)
        low = jnp.where(lane == 0, mine, theirs)
        high = jnp.where(lane == 0, theirs, mine)
        return jnp.concatenate([low, high], axis=1).reshape(total, -1)

    def lane_rows(values, which):
        return lax.dynamic_index_in_dim(
            values.reshape(micro, lanes, own, -1), which, 1, keepdims=False
        ).reshape(micro * own, -1)

    own_in = deal(inputs)
    own_grad = deal(out_grad)
    whole_in = join_lanes(own_in)
    whole_grad = join_lanes(own_grad)

    before = jnp.sum((segment[:, None, :] < segment[:, :, None]).astype(jnp.int32), axis=2)
    places = jnp.arange(rows, dtype=jnp.int32)
    allowed = (segment[:, :, None] == segment[:, None, :]) & (places[None, None, :] <= places[None, :, None])
    position = (places[None, :] - before).reshape(total, 1)

    masks = [1, 2] + [4, 12][: max(0, groups.bit_length() - 3)]
    while 1 << len(masks) < groups:
        masks.append(1 << len(masks))
    relative = []
    for block in range(groups):
        flip = 0
        for place, mask in enumerate(masks):
            if block >> (len(masks) - 1 - place) & 1:
                flip ^= mask
        relative.append(flip)
    block_order = jnp.bitwise_xor(group.astype(jnp.int32), jnp.array(relative, jnp.int32))
    half_width = width // 2

    def split_left(left):
        mixed = pick_blocks(left, block_order, shard)
        return mixed[:, :half_width], mixed[:, half_width:]

    inner_places = list(range(1, len(masks)))

    def core_send(left_parts, right):
        return outer_sum(left_parts[1], right).astype(bf16)

    def halve(kept, place):
        return (
            lax.slice_in_dim(kept, 1, 2, axis=place - 1).reshape(-1, kept.shape[-1]),
            lax.slice_in_dim(kept, 0, 1, axis=place - 1),
        )

    class Reduction:
        def __init__(self, first):
            self.places = [place for place in first if place in inner_places]
            self.places += [place for place in inner_places if place not in first]
            self.stage = 0

        def move(self, send, kept):
            self.came = other_group(send, masks[self.places[self.stage]])
            self.kept = kept
            self.stage += 1

        def first(self, left_parts, right, from_core):
            kept = (outer_sum(left_parts[0], right) + from_core.astype(f32)).astype(bf16)
            kept = kept.reshape((2,) * len(inner_places) + (shard, -1))
            return halve(kept, self.places[0])

        def added(self):
            return self.kept.astype(f32) + self.came.reshape(self.kept.shape).astype(f32)

        def next(self):
            return halve(self.added().astype(bf16), self.places[self.stage])

        def last(self):
            return self.added().reshape(shard, -1)

        def step(self):
            return self.next() if self.stage < len(self.places) else self.last()

    def advance(reductions, *others):
        steps, results = unit(lambda: ([red.step() for red in reductions], [work() for work in others]))
        for red, step in zip(reductions, steps):
            if red.stage < len(red.places):
                red.move(*step)
            else:
                red.result = step
        return results

    order = [deal_order[0, 0] >= 0]

    def unit(work):
        shapes = jax.eval_shape(work)
        results = lax.cond(
            order[0], work, lambda: jax.tree.map(lambda leaf: jnp.zeros(leaf.shape, leaf.dtype), shapes)
        )
        results, order[0] = lax.optimization_barrier((results, order[0]))
        return results

    in32 = whole_in.astype(f32)
    in_scale = rms_scale(in32)
    normed_low = (in32 * in_scale * gain_input).astype(bf16)
    gate_z = project(normed_low, full_gate)
    ssm_in = project(normed_low, full_input)
    state_raw = project(normed_low, full_state)
    heads = step_weight.shape[1]
    raw_step = project(normed_low, full_step)[:, :heads]
    state_low = jax.nn.silu(conv_sum(state_raw, kernel_state, position)).astype(bf16)
    rate = -jnp.exp(log_rate)
    step_size = jax.nn.softplus(raw_step + step_bias)
    step_heads = step_size.reshape(micro, rows, heads).transpose(0, 2, 1)
    lower = (places[None, :] <= places[:, None]).astype(f32)
    running = jnp.einsum(
        "mhj,ij->mhi", step_heads * rate[None, :, None], lower, precision=lax.Precision.HIGHEST, preferred_element_type=f32
    )
    pairs = heads // 2
    run_row = running.reshape(micro, pairs, 2, rows)
    run_col = run_row.transpose(0, 1, 3, 2)
    step_row = step_heads.reshape(micro, pairs, 2, rows)
    skip_wide = jnp.repeat(skip_gain, SHD)[None, :]
    layout = (state_low, segment.reshape(total, 1), segment.reshape(micro, 1, rows), position, run_row, run_col, step_row)
    ssm_out, squares = state_forward(ssm_in, gate_z, kernel_inner, skip_wide, *layout)
    square_own = jnp.sum(squares, axis=1)
    square_sum = square_own + other_lane(square_own)
    inv_rms = lax.rsqrt(square_sum / inner_width + epsilon)[:, None]
    gated_low = (ssm_out * jax.nn.silu(gate_z) * inv_rms * mixer_gain).astype(bf16)

    cosine, sine = rope_tables(position)
    query_low = rotate(project(normed_low, full_query).reshape(total, -1, HEAD), cosine, sine).astype(bf16)
    key_low = rotate(project(normed_low, full_key).reshape(total, -1, HEAD), cosine, sine).astype(bf16)
    value_low = project(normed_low, full_value).astype(bf16)
    kv_here = key_low.shape[1]
    query_low = query_low.reshape(micro, rows, kv_here, -1, HEAD)
    key_low = key_low.reshape(micro, rows, kv_here, HEAD)
    value_low = value_low.reshape(micro, rows, kv_here, HEAD)
    logits = jnp.einsum("migkd,mjgd->mgkij", query_low, key_low, preferred_element_type=f32) * scale_factor
    logits = jnp.where(allowed[:, None, None], logits, -jnp.inf)
    exp_scores = jnp.exp(logits - jnp.max(logits, axis=-1, keepdims=True))
    probs = exp_scores / jnp.sum(exp_scores, axis=-1, keepdims=True)
    probs_low = probs.astype(bf16)
    attended_low = (
        jnp.einsum("mgkij,mjgd->migkd", probs_low, value_low, preferred_element_type=f32).astype(bf16).reshape(total, -1)
    )
    branch_part = (project_back(gated_low, full_mix) + project_back(attended_low, full_attn)).astype(bf16)
    branch = branch_part.astype(f32) + other_lane(branch_part).astype(f32)
    whole_mid = (in32 + branch).astype(bf16)
    mid32 = whole_mid.astype(f32)
    mid_scale = rms_scale(mid32)
    mid_low = (mid32 * mid_scale * gain_middle).astype(bf16)
    grad_left = split_left(whole_grad)
    mid_left = split_left(mid_low)
    normed_left = split_left(normed_low)
    red_down, red_fgate, red_fup, red_branch, red_gate, red_input, red_rest = [
        Reduction(order) for order in ((1, 2, 3), (2, 3, 1), (3, 2, 1), (1, 3, 2), (2, 3, 1), (3, 2, 1), (1, 3, 2))
    ]
    ff_cols = feed_gate.shape[1]
    gate_cols = mamba_gate.shape[1]

    def feed_forward():
        gate_ff = project(mid_low, full_fgate)
        up_ff = project(mid_low, full_fup)
        sig_ff = jax.nn.sigmoid(gate_ff)
        hidden_low = (gate_ff * sig_ff * up_ff).astype(bf16)
        grad_hidden = project(whole_grad, full_fdown)
        gate_ff_low = (grad_hidden * up_ff * (sig_ff * (1.0 + gate_ff * (1.0 - sig_ff)))).astype(bf16)
        up_ff_low = (grad_hidden * (gate_ff * sig_ff)).astype(bf16)
        grad_mid_norm = project_back(gate_ff_low, full_fgate) + project_back(up_ff_low, full_fup)
        grad_gain_mid = jnp.sum(grad_mid_norm * mid32 * mid_scale, axis=0)
        mid_part = rms_back(grad_mid_norm, mid32, mid_scale, gain_middle).astype(bf16)
        return hidden_low, gate_ff_low, up_ff_low, mid_part, grad_gain_mid, core_send(grad_left, hidden_low)

    hidden_low, gate_ff_low, up_ff_low, mid_part, grad_gain_mid, send_down = unit(feed_forward)
    mid_other = other_lane(mid_part)
    from_core_down = other_group(send_down, 1)

    def feed_sends():
        ffn_part = project_back(hidden_low, full_fdown).astype(bf16)
        send = jnp.concatenate([core_send(mid_left, gate_ff_low), core_send(mid_left, up_ff_low)], axis=1)
        return lane_rows(ffn_part, lane), lane_rows(ffn_part, 1 - lane), send

    ffn_own, ffn_send, send_feed = unit(feed_sends)
    from_core_feed = other_group(send_feed, 1)
    red_down.move(*unit(lambda: red_down.first(grad_left, hidden_low, from_core_down)))
    moves = unit(
        lambda: (
            red_fgate.first(mid_left, gate_ff_low, from_core_feed[:, :ff_cols]),
            red_fup.first(mid_left, up_ff_low, from_core_feed[:, ff_cols:]),
        )
    )
    red_fgate.move(*moves[0])
    red_fup.move(*moves[1])

    def branch_start():
        grad_middle = whole_grad.astype(f32) + (mid_part.astype(f32) + mid_other.astype(f32))
        whole_branch = grad_middle.astype(bf16)
        grad_gated_norm = project(whole_branch, full_mix)
        cross_own = jnp.sum(grad_gated_norm * mixer_gain * (ssm_out * jax.nn.silu(gate_z)), axis=1)
        return lane_rows(grad_middle, lane), whole_branch, grad_gated_norm, cross_own

    grad_middle_own, whole_branch, grad_gated_norm, cross_own = unit(branch_start)
    cross_other = other_lane(cross_own)
    ffn_other = other_lane(ffn_send)

    def attention_backward():
        branch_left = split_left(whole_branch)
        branch_right = jnp.concatenate([gated_low, attended_low], axis=1)
        grad_attended = project(whole_branch, full_attn).astype(bf16).reshape(micro, rows, kv_here, -1, HEAD)
        grad_probs = jnp.einsum("migkd,mjgd->mgkij", grad_attended, value_low, preferred_element_type=f32)
        grad_value = jnp.einsum("mgkij,migkd->mjgd", probs_low, grad_attended, preferred_element_type=f32)
        weighted_sum = jnp.sum(probs * grad_probs, axis=-1, keepdims=True)
        grad_logits = (probs * (grad_probs - weighted_sum)).astype(bf16)
        grad_query_rot = jnp.einsum("mgkij,mjgd->migkd", grad_logits, key_low, preferred_element_type=f32) * scale_factor
        grad_key_rot = jnp.einsum("mgkij,migkd->mjgd", grad_logits, query_low, preferred_element_type=f32) * scale_factor
        query_grad_low = rotate_back(grad_query_rot.reshape(total, -1, HEAD), cosine, sine).astype(bf16).reshape(total, -1)
        key_grad_low = rotate_back(grad_key_rot.reshape(total, -1, HEAD), cosine, sine).astype(bf16).reshape(total, -1)
        value_grad_low = grad_value.astype(bf16).reshape(total, -1)
        return (
            branch_left, branch_right, core_send(branch_left, branch_right), query_grad_low, key_grad_low, value_grad_low
        )

    branch_left, branch_right, send_branch, query_grad_low, key_grad_low, value_grad_low = unit(attention_backward)
    from_core_branch = other_group(send_branch, 1)

    def state_space_backward():
        cross = (inv_rms**3) * ((cross_own + cross_other)[:, None] / inner_width)
        gate_low, input_low, column_sums, direct, along, grad_state_act = state_backward(
            grad_gated_norm, ssm_out, gate_z, ssm_in, kernel_inner, skip_wide, mixer_gain[None, :], inv_rms, cross, *layout
        )
        column_sums = jnp.sum(column_sums, axis=0)
        grad_kernel_inner = column_sums[: CONV + 1]
        grad_mixer = column_sums[CONV + 1]
        grad_skip = jnp.sum(column_sums[CONV + 2].reshape(heads, SHD), axis=1)
        grad_direct = direct.reshape(micro, heads, rows)
        grad_running = along.transpose(0, 1, 3, 2).reshape(micro, heads, rows) - step_heads * grad_direct
        grad_product = jnp.einsum(
            "mhi,ij->mhj", grad_running, lower, precision=lax.Precision.HIGHEST, preferred_element_type=f32
        )
        grad_step = (grad_direct + grad_product * rate[None, :, None]).transpose(0, 2, 1).reshape(total, heads)
        grad_rate = jnp.sum(grad_product * step_heads, axis=(0, 2)) * rate
        grad_raw_step = grad_step * jax.nn.sigmoid(raw_step + step_bias)
        grad_bias = jnp.sum(grad_raw_step, axis=0)
        grad_state_raw, grad_kernel_state = conv_back(grad_state_act, state_raw, kernel_state, position)
        step_low = jnp.pad(grad_raw_step.astype(bf16), ((0, 0), (0, STEP_PAD - heads)))
        rest_low = jnp.concatenate(
            [grad_state_raw.astype(bf16), step_low, query_grad_low, key_grad_low, value_grad_low], axis=1
        )
        send = jnp.concatenate([core_send(normed_left, part) for part in (gate_low, input_low, rest_low)], axis=1)
        small = (grad_kernel_state, grad_kernel_inner, grad_mixer, grad_bias, grad_rate, grad_skip)
        return gate_low, input_low, rest_low, send, small

    gate_low, input_low, rest_low, send_first, small = unit(state_space_backward)
    grad_kernel_state, grad_kernel_inner, grad_mixer, grad_bias, grad_rate, grad_skip = small
    from_core_first = other_group(send_first, 1)

    def middle_moves():
        ffn_out = ffn_own.astype(f32) + ffn_other.astype(f32)
        out_rows = (lane_rows(whole_mid, lane).astype(f32) + ffn_out).astype(bf16)
        return (
            red_branch.first(branch_left, branch_right, from_core_branch),
            red_down.next(), red_fgate.next(), red_fup.next(), deal_order_rows(out_rows),
        )

    moves = unit(middle_moves)
    for red, move in zip((red_branch, red_down, red_fgate, red_fup), moves):
        red.move(*move)
    out_moved = exchange(moves[4])

    def input_gradient():
        grad_normed = project_back(gate_low, full_gate) + project_back(input_low, full_input)
        columns = [2 * NS, STEP_PAD, query_weight.shape[1], key_weight.shape[1], value_weight.shape[1]]
        start = 0
        for size, weight in zip(columns, (full_state, full_step, full_query, full_key, full_value)):
            grad_normed = grad_normed + project_back(rest_low[:, start : start + size], weight)
            start += size
        grad_gain_in = jnp.sum(grad_normed * in32 * in_scale, axis=0)
        in_part = rms_back(grad_normed, in32, in_scale, gain_input).astype(bf16)
        return grad_gain_in, lane_rows(in_part, lane), lane_rows(in_part, 1 - lane)

    grad_gain_in, in_own, in_send = unit(input_gradient)
    in_other = other_lane(in_send)

    advance([red_down, red_fgate, red_fup])
    moves = unit(
        lambda: (
            red_gate.first(normed_left, gate_low, from_core_first[:, :gate_cols]),
            red_input.first(normed_left, input_low, from_core_first[:, gate_cols : 2 * gate_cols]),
            red_rest.first(normed_left, rest_low, from_core_first[:, 2 * gate_cols :]),
        )
    )
    early = [red_down, red_fgate, red_fup, red_branch]
    late = [red_gate, red_input, red_rest]
    for red, move in zip(late, moves):
        red.move(*move)


    shared = [grad_gain_in, grad_gain_mid, grad_kernel_state.reshape(-1)]
    split = [grad_kernel_inner.reshape(-1), grad_mixer, grad_bias, grad_rate, grad_skip]
    used = sum(item.shape[0] for item in shared + split)
    padded = -(-used // 1024) * 1024

    def send_input():
        in_sum = in_own.astype(f32) + in_other.astype(f32)
        return deal_order_rows((in_sum + grad_middle_own).astype(bf16))

    in_sent, flat = advance(
        early,
        send_input,
        lambda: jnp.pad(jnp.concatenate(shared + split), (0, padded - used)).reshape(padded // 128, 128),
    )
    in_moved = exchange(in_sent)
    flat_moved = other_group(flat, masks[0])
    flat, block_out = advance(late, lambda: flat + flat_moved, lambda: deal_take(out_moved))
    pending = early + late
    bits = 1
    pending = [red for red in pending if not hasattr(red, "result")]
    while pending:
        work = []
        if bits < len(masks):
            flat_moved = other_group(flat, masks[bits])
            work.append(lambda: flat + flat_moved)
        results = advance(pending, *work)
        if bits < len(masks):
            flat = results[0]
            bits += 1
        pending = [red for red in pending if not hasattr(red, "result")]
    while bits < len(masks):
        flat = flat + other_group(flat, masks[bits])
        bits += 1
    grad_input = deal_take(in_moved)
    theirs = other_lane(flat).reshape(-1)
    flat = flat.reshape(-1)
    pieces = []
    start = 0
    for item in shared:
        pieces.append(flat[start : start + item.shape[0]] + theirs[start : start + item.shape[0]])
        start += item.shape[0]
    for item in split:
        mine, other = flat[start : start + item.shape[0]], theirs[start : start + item.shape[0]]
        pieces.append((jnp.where(lane == 0, mine, other), jnp.where(lane == 0, other, mine)))
        start += item.shape[0]
    sum_gin, sum_gmid, sum_kst = pieces[0], pieces[1], pieces[2].reshape(CONV + 1, -1)
    sum_kin = jnp.concatenate([half.reshape(CONV + 1, -1) for half in pieces[3]], axis=1)
    sum_mix, sum_bias, sum_rate, sum_skip = [jnp.concatenate(pair) for pair in pieces[4:]]

    query_cols, key_cols = query_weight.shape[1], key_weight.shape[1]
    total_fdown, total_fgate, total_fup = red_down.result, red_fgate.result, red_fup.result
    total_mix, total_attn = red_branch.result[:, :gate_cols], red_branch.result[:, gate_cols:]
    total_gate, total_input = red_gate.result, red_input.result
    rest = red_rest.result
    total_step = rest[:, 2 * NS : 2 * NS + heads]
    start = 2 * NS + STEP_PAD
    total_query = rest[:, start : start + query_cols]
    total_key = rest[:, start + query_cols : start + query_cols + key_cols]
    total_value = rest[:, start + query_cols + key_cols :]
    state_rows = rest[:, : 2 * NS].reshape(lanes, shard // lanes, 2 * NS)
    state_own = lax.dynamic_index_in_dim(state_rows, lane, 0, keepdims=False)
    state_send = lax.dynamic_index_in_dim(state_rows, 1 - lane, 0, keepdims=False)
    state_lane = state_own + other_lane(state_send)
    return (
        block_out,
        grad_input,
        total_query,
        total_key,
        total_value,
        total_attn,
        total_gate,
        total_input,
        total_step,
        state_lane,
        total_mix,
        total_fgate,
        total_fup,
        total_fdown,
        sum_gin,
        sum_gmid,
        sum_kin,
        sum_kst,
        sum_mix,
        sum_bias,
        sum_rate,
        sum_skip,
    )


def solution(mesh):
    both = P("dp", "tensor")
    in_specs = (
        P(None, ("dp", "tensor"), None),
        P(None, ("dp", "tensor"), None),
        P(),
        P(None, "dp"),
        both,
        both,
        both,
        both,
        both,
        both,
        both,
        P("dp", None),
        both,
        both,
        both,
        both,
        P(),
        P(),
        P(None, "tensor"),
        P(),
        P("tensor"),
        P("tensor"),
        P("tensor"),
        P("tensor"),
    )
    out_specs = (
        P(None, ("dp", "tensor"), None),
        P(None, ("dp", "tensor"), None),
        both,
        both,
        both,
        both,
        both,
        both,
        both,
        P(("dp", "tensor"), None),
        both,
        both,
        both,
        both,
        P(),
        P(),
        P(),
        P(),
        P(),
        P(),
        P(),
        P(),
    )
    return jax.shard_map(local, mesh=mesh, in_specs=in_specs, out_specs=out_specs, check_vma=False)
```

time: 1220 us -> 1230 us (level)
  Pallas kernels: 0 us -> 88.1 us
  matrix products: 283 us -> 212 us
  waiting for transfers between devices: 434 us -> 472 us
  local copies, waits for them, and re-layouts: 195 us -> 170 us
  starting transfers between devices: 173 us -> 150 us
    pallas_call x0 -> x6, Pallas kernels: none -> 88.1 us  [the longest x4 37.1 us: pick_blocks(): pl.pallas_call(copy_block, out_shape=jax.ShapeDtypeStruct(values.shape, v...]
    slice x5 -> x31, local copies, waits for them, and re-layouts: 1.44 us -> 69 us  [the longest x4 31.7 us: gather(): found.append(whole[:, start:start + piece.shape[1]])]
    ppermute x10, waiting for transfers between devices: 55.5 us -> 117 us  [other_lane(): return lax.ppermute(values, 'tensor', swap_lane)]
    dynamic_slice x12 -> x0, local copies, waits for them, and re-layouts: 50.5 us -> none  [part(): picked = lax.dynamic_index_in_dim(picked, y, 2, keepdims=False)]
    all_gather x2, waiting for transfers between devices: 36.8 us -> 81.1 us  [gather(): lax.all_gather(jnp.concatenate(pieces, axis=1), 'dp', axis=0, tiled=True)]
    ppermute x49 -> x29, waiting for transfers between devices: 272 us -> 235 us  [other_group(): return lax.ppermute(values, 'dp', [(i, i ^ bits) for i in range(groups)])]
    reshape x12 -> x6, local copies, waits for them, and re-layouts: 40 us -> 5.2 us  [the longest x2 2.85 us: local(): run_row = running.reshape(micro, pairs, 2, rows)]
    dot_general x31 -> x18, matrix products: 103 us -> 72.3 us  [outer_sum(): lax.dot_general(left, right, (((0,), (0,)), ((), ())), preferred_element_...]
  transfers between devices with their start and end apart: 65 -> 45, of which waited for: 28 -> 20; matrix products, arithmetic and copies ran while one was open for 41% -> 24% of each run, Pallas kernels for 0% -> 4%
where the time goes in v2:
time: 1230 us; the launch traced here: 1220 us
  waiting for transfers between devices  472 us (38%)
  matrix products  212 us (17%)
  local copies, waits for them, and re-layouts  170 us (14%)
  starting transfers between devices  150 us (12%)
  other arithmetic  108 us (9%)
  Pallas kernels  88.1 us (7%)
  between operations  16.1 us (1%)
    ppermute x29, waiting for transfers between devices, other_group(): return lax.ppermute(values, 'dp', [(i, i ^ bits) for i in range(groups)])  235 us
    ppermute x29, starting transfers between devices, other_group(): return lax.ppermute(values, 'dp', [(i, i ^ bits) for i in range(groups)])  119 us
    ppermute x10, waiting for transfers between devices, other_lane(): return lax.ppermute(values, 'tensor', swap_lane)  117 us
    all_gather x2, waiting for transfers between devices, gather(): lax.all_gather(jnp.concatenate(pieces, axis=1), 'dp', axis=0, tiled=True)  81.1 us
    dot_general x18, matrix products, outer_sum(): lax.dot_general(left, right, (((0,), (0,)), ((), ())), preferred_element_...  72.3 us
    dot_general x16, matrix products, project(): return jnp.dot(left, right, preferred_element_type=f32)  68.7 us
    dot_general x12, matrix products, project_back(): lax.dot_general(left, right, (((1,), (1,)), ((), ())), preferred_element_...  64.6 us
    all_to_all x4, waiting for transfers between devices, exchange(): lax.all_to_all(buffer.reshape(groups, micro * per, width), 'dp', split_ax...  38.2 us
  transfers between devices with their start and end apart: 45, of which 20 were waited for; matrix products, arithmetic and copies ran while one was open for 24% of the time, Pallas kernels for 4%

profile of v2, /device:TPU:0, one launch (start us, length us, event | category | flops | bytes accessed | tf_op | source)
XLA Modules:
  0.0 1219.5 jit_solution(14350340762923307158)
XLA Ops:
  22.9 7.4 all-to-all-start
  31.9 38.2 %all-to-all-done = bf16[16,16,2048]{2,1,0:T(8,128)(2,1)S(1)} async-done(((bf16[16,16,2048]{2,1,0:T(8,128)(2,1)}), bf16[16,16,2048]{2,1,0:T(8,128)(2,1)S(1)}, u32[]{:S(2)}, u32[]{:S(2)}) %all-to-all-start) | async-done | bytes 1048608 | tf_op jit(solution)/shard_map/all_to_all | solution.py:399
  81.4 19.6 %collective-permute-done = bf16[256,2048]{1,0:T(8,128)(2,1)S(1)} collective-permute-done((bf16[256,2048]{1,0:T(8,128)(2,1)S(1)}, bf16[256,2048]{1,0:T(8,128)(2,1)S(1)}, u32[]{:S(2)}, u32[]{:S(2)}) %collective-permute-start) | collective-permute-done | bytes 1048608 | tf_op jit(solution)/shard_map/ppermute | solution.py:354
  105.5 81.1 %all-gather.5.cloned.1.call-done = bf16[2048,6528]{1,0:T(8,128)(2,1)} async-done(((bf16[128,6528]{1,0:T(8,128)(2,1)}), bf16[2048,6528]{1,0:T(8,128)(2,1)}) %all-gather.5.cloned.1.call-update) | async-done | bytes 26738704 | tf_op jit(solution)/shard_map/all_gather | solution.py:364
  202.0 8.1 fusion.120.gate_ref
  210.0 8.1 fusion.122.signal_ref
  218.2 21.1 %state_forward.1 = (f32[512,1536]{1,0:T(8,128)}, f32[512,128]{1,0:T(8,128)}) custom-call(f32[512,1536]{1,0:T(8,128)} %fusion.122.signal_ref, f32[512,1536]{1,0:T(8,128)} %fusion.120.gate_ref, f32[5,1536]{1,0:T(8,128)S(1)} %copy-done.95, f32[1,1536]{1,0:T(1,128)S(1)} %broadcast_in_dim_reshape.2.skip_ref, bf16[512,512]{1,0:T(8,128)(2,1)S(1)} %copy-done.29, ...), custom_call_target="tpu_custom_call" | custom-call | flops 1610612736 | bytes 9437184 | tf_op jit(solution)/shard_map/state_forward/pallas_call | solution.py:266
  241.9 6.7 fusion.153
  271.7 6.1 fusion.118
  287.7 64.9 %collective-permute-done.3 = bf16[256,2048]{1,0:T(8,128)(2,1)S(1)} collective-permute-done((bf16[256,2048]{1,0:T(8,128)(2,1)S(1)}, bf16[256,2048]{1,0:T(8,128)(2,1)S(1)}, u32[]{:S(2)}, u32[]{:S(2)}) %collective-permute-start.3) | collective-permute-done | bytes 1048608 | tf_op jit(solution)/shard_map/ppermute | solution.py:354
  352.9 6.6 shard_map.408
  359.6 8.4 slice.543
  376.6 10.2 shard_map.409
  387.4 48.4 %conditional.15 = (bf16[512,2048]{1,0:T(8,128)(2,1)}, bf16[512,2048]{1,0:T(8,128)(2,1)}, bf16[512,2048]{1,0:T(8,128)(2,1)}, bf16[512,2048]{1,0:T(8,128)(2,1)}, f...) conditional(s32[]{:T(128)} %convert_element_type.700, () %tuple.148, (bf16[2048,6144]{1,0:T(8,128)(2,1)}, ...), branch_computations={%region_9.10_spmd, %region_10.13_spmd} | conditional | flops 23652728832 | bytes 168868016 | solution.py:504
  387.4 8.5 fusion.2
  396.0 7.1 fusion.6
  403.1 8.0 multiply_convert_fusion
  411.2 6.0 convert_bitcast_fusion
  417.1 7.8 fusion
  424.9 8.5 multiply_reduce_fusion
  436.5 30.3 %conditional.16 = (bf16[256,2048]{1,0:T(8,128)(2,1)S(1)}, bf16[256,2048]{1,0:T(8,128)(2,1)}, bf16[1024,4096]{1,0:T(8,128)(2,1)}) conditional(s32[]{:T(128)} %convert_element_type.729, () %tuple.151, (bf16[512,2048]{1,0:T(8,128)(2,1)}, bf16[2048,2048]{1,0:T(8,128)(2,1)}, s32[]{:T(128)}, bf16[512,2048]{1,0:T(8,128)(2,1)}, ...), branch_computations={%region_13.14_spmd, %region_14.15_spmd} | conditional | flops 8611954688 | bytes 56623244 | solution.py:504
  436.5 8.5 convolution_convert_fusion.2
  447.0 6.0 convolution_convert_fusion.1
  453.0 5.9 convolution_convert_fusion
  459.0 7.8 pad_maximum_fusion
  466.8 6.9 copy.216
  474.9 10.2 shard_map.410
  488.6 14.0 %fusion.154 = (bf16[2048,1536]{1,0:T(8,128)(2,1)}, bf16[2048,1536]{1,0:T(8,128)(2,1)}, bf16[2048,1536]{1,0:T(8,128)(2,1)}) fusion(bf16[2048,6528]{1,0:T(8,128)(2,1)} %all-gather.5.cloned.1.call-done), kind=kLoop, calls=%fused_computation.365 | loop fusion | bytes 37748736 | tf_op jit(solution)/shard_map/slice | solution.py:367
  502.6 19.3 %collective-permute-done.6 = bf16[512,2048]{1,0:T(8,128)(2,1)S(1)} collective-permute-done((bf16[512,2048]{1,0:T(8,128)(2,1)}, bf16[512,2048]{1,0:T(8,128)(2,1)S(1)}, u32[]{:S(2)}, u32[]{:S(2)}) %collective-permute-start.6) | collective-permute-done | bytes 2097184 | tf_op jit(solution)/shard_map/ppermute | solution.py:354
  523.2 8.3 conditional.17
  531.6 15.5 %conditional.18 = (bf16[512,2048]{1,0:T(8,128)(2,1)}, bf16[2,1,2,128,2048]{4,3,2,1,0:T(8,128)(2,1)}, bf16[512,2048]{1,0:T(8,128)(2,1)}, bf16[2,2,1,128,2048]{4,3,2,1,0:T(8,128)(2,1)}) conditional(s32[]{:T(128)} %convert_element_type.731, () %tuple.157, (bf16[512,2048]{1,0:T(8,128)(2,1)S(1)}, bf16[512,2048]{1,0:T(8,128)(2,1)}, ...), branch_computations={%region_17.18_spmd, %region_18.19_spmd} | conditional | flops 4307550208 | bytes 39845920 | solution.py:504
  547.1 16.2 %conditional.19 = (f32[256,2048]{1,0:T(8,128)}, bf16[512,2048]{1,0:T(8,128)(2,1)}, f32[512,1536]{1,0:T(8,128)}, f32[512]{0:T(512)S(1)}) conditional(s32[]{:T(128)} %convert_element_type.732, () %tuple.160, (bf16[512,2048]{1,0:T(8,128)(2,1)}, bf16[512,2048]{1,0:T(8,128)(2,1)}, bf16[512,2048]{1,0:T(8,128)(2,1)}, s32[]{:T(128)}, ...), branch_computations={%region_19.20_spmd, %region_20.22_spmd} | conditional | flops 3233807872 | bytes 84943008 | solution.py:504
  547.4 5.9 fusion.125
  554.8 7.1 multiply_reduce_fusion.2
  564.7 44.1 %conditional.20 = (bf16[512,1024]{1,0:T(8,128)(2,1)}, bf16[512,2048]{1,0:T(8,128)(2,1)}, bf16[1024,2048]{1,0:T(8,128)(2,1)}, bf16[512,512]{0,1:T(8,128)(2,1)}, b...) conditional(s32[]{:T(128)} %convert_element_type.733, () %tuple.163, (s32[16]{0:T(128)S(1)}, ...), branch_computations={%region_22.23_spmd, %region_23.25_spmd} | conditional | flops 3766122496 | bytes 70664456 | solution.py:504
  571.8 10.1 branch_1_fun.2
  602.8 5.9 convolution_convert_fusion.3
  608.8 68.4 %conditional.21 = (bf16[512,1536]{1,0:T(8,128)(2,1)}, bf16[512,1536]{1,0:T(8,128)(2,1)S(1)}, bf16[512,1408]{1,0:T(8,128)(2,1)S(1)}, bf16[1024,4480]{0,1:T(8,128)...) conditional(s32[]{:T(128)} %convert_element_type.734, ...), branch_computations={%region_25.26_spmd, %region_26.36_spmd} | conditional | flops 8804412416 | bytes 132862032 | solution.py:504
  619.6 29.9 %state_backward.1 = (bf16[512,1536]{1,0:T(8,128)(2,1)}, bf16[512,1536]{1,0:T(8,128)(2,1)}, f32[2,8,1536]{2,1,0:T(8,128)}, f32[2,12,2,256]{3,2,1,0:T(2,128)}, f32...) custom-call(f32[512,1536]{1,0:T(8,128)} %get-tuple-element.411.grad_ref, f32[512,1536]{1,0:T(8,128)} %get-tuple-element.412.out_ref, ...), custom_call_target="tpu_custom_call" | custom-call | flops 4026531840 | bytes 15728640 | tf_op jit(solution)/shard_map/cond/branch_1_fun/state_backward/pallas_call | solution.py:285
  678.8 12.6 %copy.229 = bf16[1024,4480]{1,0:T(8,128)(2,1)} copy(bf16[1024,4480]{0,1:T(8,128)(2,1)} %get-tuple-element.847) | data formatting | bytes 18350080 | tf_op jit(solution)/shard_map/optimization_barrier | solution.py:507
  694.5 12.4 %collective-permute-start.10 = (bf16[512,2048]{1,0:T(8,128)(2,1)}, bf16[512,2048]{1,0:T(8,128)(2,1)}, u32[]{:S(2)}, u32[]{:S(2)}) collective-permute-start(bf16[512,2048]{1,0:T(8,128)(2,1)} %get-tuple-element.812), channel_id=1, source_target_pairs={{0,8},{2,10},{4,12},{6,14},{8,0},{10,2},{12,4},{14,6},{16,24},{18,... | collective-permute-start | bytes 6291464 | tf_op jit(solution)/shard_map/ppermute | solution.py:357
  706.9 10.3 collective-permute-done.12
  719.1 22.0 %collective-permute-done.9 = bf16[512,2048]{1,0:T(8,128)(2,1)} collective-permute-done((bf16[512,2048]{1,0:T(8,128)(2,1)}, bf16[512,2048]{1,0:T(8,128)(2,1)}, u32[]{:S(2)}, u32[]{:S(2)}) %collective-permute-start.9) | collective-permute-done | bytes 2097184 | tf_op jit(solution)/shard_map/ppermute | solution.py:357
  741.1 12.2 %collective-permute-done.10 = bf16[512,2048]{1,0:T(8,128)(2,1)} collective-permute-done((bf16[512,2048]{1,0:T(8,128)(2,1)}, bf16[512,2048]{1,0:T(8,128)(2,1)}, u32[]{:S(2)}, u32[]{:S(2)}) %collective-permute-start.10) | collective-permute-done | bytes 2097184 | tf_op jit(solution)/shard_map/ppermute | solution.py:357
  753.3 45.8 %collective-permute-done.11 = bf16[512,2048]{1,0:T(8,128)(2,1)} collective-permute-done((bf16[512,2048]{1,0:T(8,128)(2,1)}, bf16[512,2048]{1,0:T(8,128)(2,1)}, u32[]{:S(2)}, u32[]{:S(2)}) %collective-permute-start.11) | collective-permute-done | bytes 2097184 | tf_op jit(solution)/shard_map/ppermute | solution.py:357
  799.1 24.5 %conditional.22 = (bf16[512,2048]{1,0:T(8,128)(2,1)}, bf16[1,2,2,128,2048]{4,3,2,1,0:T(8,128)(2,1)}, bf16[256,2048]{1,0:T(8,128)(2,1)}, bf16[1,1,2,128,2048]{4,3...) conditional(s32[]{:T(128)} %convert_element_type.736, ...), branch_computations={%region_36.37_spmd, %region_37.38_spmd} | conditional | flops 2438463488 | bytes 70385856 | solution.py:504
  823.6 22.6 %collective-permute-start.13 = (bf16[256,2048]{1,0:T(8,128)(2,1)}, bf16[256,2048]{1,0:T(8,128)(2,1)}, u32[]{:S(2)}, u32[]{:S(2)}) collective-permute-start(bf16[256,2048]{1,0:T(8,128)(2,1)} %get-tuple-element.835), channel_id=1, source_target_pairs={{0,8},{2,10},{4,12},{6,14},{8,0},{10,2},{12,4},{14,6},{16,24},{18,... | collective-permute-start | bytes 3145736 | tf_op jit(solution)/shard_map/ppermute | solution.py:357
  860.7 32.9 %conditional.23 = (f32[2048]{0:T(1024)S(1)}, bf16[256,2048]{1,0:T(8,128)(2,1)}, bf16[256,2048]{1,0:T(8,128)(2,1)}) conditional(s32[]{:T(128)} %convert_element_type.738, () %tuple.172, (bf16[512,1536]{1,0:T(8,128)(2,1)}, bf16[2048,1536]{1,0:T(8,128)(2,1)}, bf16[512,1536]{1,0:T(8,128)(2,1)}, bf16[2048,1536]{1,0:T(8,128)(2,1)}, ...), branch_computations={%region_38.39_spmd, %region_39.42_spmd} | conditional | flops 9413066752 | bytes 165067136 | solution.py:504
  860.9 8.9 fusion.161
  884.2 7.3 multiply_reduce_fusion.3
  895.1 16.2 %collective-permute-done.14 = bf16[256,2048]{1,0:T(8,128)(2,1)} collective-permute-done((bf16[256,2048]{1,0:T(8,128)(2,1)}, bf16[256,2048]{1,0:T(8,128)(2,1)}, u32[]{:S(2)}, u32[]{:S(2)}) %collective-permute-start.14) | collective-permute-done | bytes 1048608 | tf_op jit(solution)/shard_map/ppermute | solution.py:357
  911.3 18.7 %collective-permute-done.15 = bf16[256,2048]{1,0:T(8,128)(2,1)} collective-permute-done((bf16[256,2048]{1,0:T(8,128)(2,1)}, bf16[256,2048]{1,0:T(8,128)(2,1)}, u32[]{:S(2)}, u32[]{:S(2)}) %collective-permute-start.15) | collective-permute-done | bytes 1048608 | tf_op jit(solution)/shard_map/ppermute | solution.py:357
  930.0 7.6 conditional.24
  940.4 18.4 %conditional.25 = (bf16[512,1536]{1,0:T(8,128)(2,1)}, bf16[2,1,2,128,1536]{4,3,2,1,0:T(8,128)(2,1)}, bf16[512,1536]{1,0:T(8,128)(2,1)}, bf16[2,2,1,128,1536]{4,3...) conditional(s32[]{:T(128)} %convert_element_type.740, () %tuple.178, ...), branch_computations={%region_44.45_spmd, %region_45.46_spmd} | conditional | flops 4711383040 | bytes 59113576 | solution.py:504
  963.9 13.1 %collective-permute-done.19 = bf16[128,2048]{1,0:T(8,128)(2,1)} collective-permute-done((bf16[128,2048]{1,0:T(8,128)(2,1)}, bf16[128,2048]{1,0:T(8,128)(2,1)}, u32[]{:S(2)}, u32[]{:S(2)}) %collective-permute-start.19) | collective-permute-done | bytes 524320 | tf_op jit(solution)/shard_map/ppermute | solution.py:357
  977.1 12.0 conditional.26
  1004.7 26.5 %collective-permute-done.23 = bf16[512,1536]{1,0:T(8,128)(2,1)} collective-permute-done((bf16[512,1536]{1,0:T(8,128)(2,1)}, bf16[512,1536]{1,0:T(8,128)(2,1)}, u32[]{:S(2)}, u32[]{:S(2)}) %collective-permute-start.23) | collective-permute-done | bytes 1572896 | tf_op jit(solution)/shard_map/ppermute | solution.py:357
  1031.3 13.0 %conditional.27 = (bf16[256,1536]{1,0:T(8,128)(2,1)}, bf16[2,1,1,128,1536]{4,3,2,1,0:T(8,128)(2,1)}, bf16[256,1536]{1,0:T(8,128)(2,1)}, bf16[2,1,1,128,1536]{4,3...) conditional(s32[]{:T(128)} %convert_element_type.742, ...), branch_computations={%region_48.49_spmd, %region_49.50_spmd} | conditional | flops 278151168 | bytes 25362496 | solution.py:504
  1046.2 6.8 collective-permute-start.28
  1057.2 13.5 %collective-permute-done.26 = bf16[256,2048]{1,0:T(8,128)(2,1)} collective-permute-done((bf16[256,2048]{1,0:T(8,128)(2,1)}, bf16[256,2048]{1,0:T(8,128)(2,1)}, u32[]{:S(2)}, u32[]{:S(2)}) %collective-permute-start.26) | collective-permute-done | bytes 1048608 | tf_op jit(solution)/shard_map/ppermute | solution.py:357
  1070.7 45.1 %collective-permute-done.29 = bf16[256,1408]{1,0:T(8,128)(2,1)} collective-permute-done((bf16[256,1408]{1,0:T(8,128)(2,1)}, bf16[256,1408]{1,0:T(8,128)(2,1)}, u32[]{:S(2)}, u32[]{:S(2)}) %collective-permute-start.29) | collective-permute-done | bytes 720928 | tf_op jit(solution)/shard_map/ppermute | solution.py:357
  1116.7 9.4 conditional.28
  1126.2 44.9 %collective-permute-start.31 = (bf16[128,2048]{1,0:T(8,128)(2,1)}, bf16[128,2048]{1,0:T(8,128)(2,1)S(1)}, u32[]{:S(2)}, u32[]{:S(2)}) collective-permute-start(bf16[128,2048]{1,0:T(8,128)(2,1)} %get-tuple-element.921), channel_id=1, source_target_pairs={{0,8},{2,10},{4,12},{6,14},{8,0},{10,2},{12,4},{14,6},{16,24},{18,... | collective-permute-start | bytes 1572872 | tf_op jit(solution)/shard_map/ppermute | solution.py:357
  1176.6 14.2 %collective-permute-done.35 = f32[128,128]{1,0:T(8,128)S(1)} collective-permute-done((f32[128,128]{1,0:T(8,128)S(1)}, f32[128,128]{1,0:T(8,128)S(1)}, u32[]{:S(2)}, u32[]{:S(2)}) %collective-permute-start.35) | collective-permute-done | bytes 65568 | tf_op jit(solution)/shard_map/ppermute | solution.py:357
  (606 shorter events, 381.8 us)
Async XLA Ops:
  7.2 179.3 %all-gather.5.cloned.1.call-start = ((), (), s32[]{:S(2)}) async-start(), calls=%async_computation.5 | async-start | bytes 28409856 | tf_op jit(solution)/shard_map/all_gather | solution.py:364
  13.6 346.1 %all-gather.3.cloned.1.call-start = ((), (), s32[]{:S(2)}) async-start(), calls=%async_computation.4 | async-start | bytes 26738688 | tf_op jit(solution)/shard_map/all_gather | solution.py:364
  21.5 261.3 %copy-start.127 = (s32[256]{0:T(256)}, s32[256]{0:T(256)S(1)}, u32[]{:S(2)}) copy-start(s32[256]{0:T(256)S(1)} %get-tuple-element.1323) | copy-start | bytes 3076
  22.9 47.3 %all-to-all-start = ((bf16[16,16,2048]{2,1,0:T(8,128)(2,1)}), bf16[16,16,2048]{2,1,0:T(8,128)(2,1)S(1)}, u32[]{:S(2)}, u32[]{:S(2)}) async-start(bf16[16,16,2048]{2,1,0:T(8,128)(2,1)} %bitcast.141), calls=%async_computation | async-start | bytes 2097152 | tf_op jit(solution)/shard_map/all_to_all | solution.py:399
  70.2 212.6 %all-to-all-start.1 = ((bf16[16,16,2048]{2,1,0:T(8,128)(2,1)}), bf16[16,16,2048]{2,1,0:T(8,128)(2,1)}, u32[]{:S(2)}, u32[]{:S(2)}) async-start(bf16[16,16,2048]{2,1,0:T(8,128)(2,1)} %bitcast.175), calls=%async_computation.1 | async-start | bytes 2097152 | tf_op jit(solution)/shard_map/all_to_all | solution.py:399
  75.5 25.5 %collective-permute-start = (bf16[256,2048]{1,0:T(8,128)(2,1)S(1)}, bf16[256,2048]{1,0:T(8,128)(2,1)S(1)}, u32[]{:S(2)}, u32[]{:S(2)}) collective-permute-start(bf16[256,2048]{1,0:T(8,128)(2,1)S(1)} %convolution_convert_fusion.14), channel_id=1, source_target_pairs={{0,1},{1,0},{2,3},{3,2},{4,5},{5,4},{6,7},{7,6},{8,9},{9,8},{10,11... | collective-permute-start | bytes 3145736 | tf_op jit(solution)/shard_map/ppermute | solution.py:354
  77.1 141.1 %copy-start.118 = (s32[2,1,256]{2,1,0:T(1,128)}, s32[2,1,256]{2,1,0:T(1,128)S(1)}, u32[]{:S(2)}) copy-start(s32[2,1,256]{2,1,0:T(1,128)S(1)} %broadcast_in_dim.152.seg_row_ref) | copy-start | bytes 6148
  77.1 24.0 %copy-start.119 = (s32[1,1,2,256]{3,1,2,0:T(1,128)}, s32[1,1,2,256]{3,1,2,0:T(1,128)S(1)}, u32[]{:S(2)}) copy-start(s32[1,1,2,256]{3,1,2,0:T(1,128)S(1)} %copy.249) | copy-start | bytes 6148
  77.2 23.9 %copy-start.120 = (s32[1,1,2,256]{3,1,2,0:T(1,128)}, s32[1,1,2,256]{3,1,2,0:T(1,128)S(1)}, u32[]{:S(2)}) copy-start(s32[1,1,2,256]{3,1,2,0:T(1,128)S(1)} %copy.250) | copy-start | bytes 6148
  77.4 140.8 %copy-start.102 = (f32[1,1536]{1,0:T(1,128)}, f32[1,1536]{1,0:T(1,128)S(1)}, u32[]{:S(2)}) copy-start(f32[1,1536]{1,0:T(1,128)S(1)} %broadcast_in_dim_reshape.2.skip_ref) | copy-start | bytes 18436
  79.3 109.6 %copy-start.131 = (f32[24]{0:T(128)}, f32[24]{0:T(128)S(1)}, u32[]{:S(2)}) copy-start(f32[24]{0:T(128)S(1)} %exponential_negate_fusion) | copy-start | bytes 292
  105.0 81.5 %copy-start.129 = (f32[24]{0:T(128)S(1)}, f32[24]{0:T(128)}, u32[]{:S(2)}) copy-start(f32[24]{0:T(128)} %param.76) | copy-start | bytes 292
  105.4 157.9 %copy-start.7 = (bf16[512,2048]{1,0:T(8,128)(2,1)}, bf16[512,2048]{1,0:T(8,128)(2,1)S(1)}, u32[]{:S(2)}) copy-start(bf16[512,2048]{1,0:T(8,128)(2,1)S(1)} %multiply_convert_fusion.5.source_ref) | copy-start | bytes 6291460
  192.1 26.1 %copy-start.87 = (f32[2,12,2,256]{3,2,1,0:T(2,128)}, f32[2,12,2,256]{3,2,1,0:T(2,128)S(1)}, u32[]{:S(2)}) copy-start(f32[2,12,2,256]{3,2,1,0:T(2,128)S(1)} %reshape.1221.step_ref) | copy-start | bytes 147460
  195.4 65.8 %copy-start.60 = (bf16[512,1,64]{2,0,1:T(8,128)(2,1)}, bf16[512,1,64]{2,0,1:T(8,128)(2,1)S(1)}, u32[]{:S(2)}) copy-start(bf16[512,1,64]{2,0,1:T(8,128)(2,1)S(1)} %copy.243) | copy-start | bytes 196612
  240.4 27.0 %collective-permute-start.1 = (f32[512]{0:T(512)S(1)}, f32[512]{0:T(512)S(1)}, u32[]{:S(2)}, u32[]{:S(2)}) collective-permute-start(f32[512]{0:T(512)S(1)} %reduce_sum.222), channel_id=1, source_target_pairs={{0,1},{1,0},{2,3},{3,2},{4,5},{5,4},{6,7},{7,6},{8,9},{9,8},{10,11... | collective-permute-start | bytes 6152 | tf_op jit(solution)/shard_map/ppermute | solution.py:354
  282.1 86.0 %collective-permute-start.2 = (bf16[512,2048]{1,0:T(8,128)(2,1)}, bf16[512,2048]{1,0:T(8,128)(2,1)}, u32[]{:S(2)}, u32[]{:S(2)}) collective-permute-start(bf16[512,2048]{1,0:T(8,128)(2,1)} %add_convert_fusion.13), channel_id=1, source_target_pairs={{0,1},{1,0},{2,3},{3,2},{4,5},{5,4},{6,7},{7,6},{8,9},{9,8},{10,11... | collective-permute-start | bytes 6291464 | tf_op jit(solution)/shard_map/ppermute | solution.py:354
  284.6 68.0 %collective-permute-start.3 = (bf16[256,2048]{1,0:T(8,128)(2,1)S(1)}, bf16[256,2048]{1,0:T(8,128)(2,1)S(1)}, u32[]{:S(2)}, u32[]{:S(2)}) collective-permute-start(bf16[256,2048]{1,0:T(8,128)(2,1)S(1)} %convolution_convert_fusion.12), channel_id=1, source_target_pairs={{0,1},{1,0},{2,3},{3,2},{4,5},{5,4},{6,7},{7,6},{8,9},{9,8},{10,11... | collective-permute-start | bytes 3145736 | tf_op jit(solution)/shard_map/ppermute | solution.py:354
  466.8 64.8 %collective-permute-start.5 = (bf16[1024,4096]{1,0:T(8,128)(2,1)}, bf16[1024,4096]{1,0:T(8,128)(2,1)}, u32[]{:S(2)}, u32[]{:S(2)}) collective-permute-start(bf16[1024,4096]{1,0:T(8,128)(2,1)} %get-tuple-element.770), channel_id=1, source_target_pairs={{0,2},{2,0},{4,6},{6,4},{8,10},{10,8},{12,14},{14,12},{16,18},{18,... | collective-permute-start | bytes 25165832 | tf_op jit(solution)/shard_map/ppermute | solution.py:357
  473.7 48.3 %collective-permute-start.4 = (bf16[1024,2048]{1,0:T(8,128)(2,1)}, bf16[1024,2048]{1,0:T(8,128)(2,1)}, u32[]{:S(2)}, u32[]{:S(2)}) collective-permute-start(bf16[1024,2048]{1,0:T(8,128)(2,1)} %copy.216), channel_id=1, source_target_pairs={{0,2},{2,0},{4,6},{6,4},{8,10},{10,8},{12,14},{14,12},{16,18},{18,... | collective-permute-start | bytes 12582920 | tf_op jit(solution)/shard_map/ppermute | solution.py:357
  473.8 48.1 %collective-permute-start.6 = (bf16[512,2048]{1,0:T(8,128)(2,1)}, bf16[512,2048]{1,0:T(8,128)(2,1)S(1)}, u32[]{:S(2)}, u32[]{:S(2)}) collective-permute-start(bf16[512,2048]{1,0:T(8,128)(2,1)} %get-tuple-element.776), channel_id=1, source_target_pairs={{0,1},{1,0},{2,3},{3,2},{4,5},{5,4},{6,7},{7,6},{8,9},{9,8},{10,11... | collective-permute-start | bytes 6291464 | tf_op jit(solution)/shard_map/ppermute | solution.py:354
  547.1 16.6 %copy-start.61 = (bf16[512,1,64]{2,0,1:T(8,128)(2,1)S(1)}, bf16[512,1,64]{2,0,1:T(8,128)(2,1)}, u32[]{:S(2)}) copy-start(bf16[512,1,64]{2,0,1:T(8,128)(2,1)} %copy-done.60) | copy-start | bytes 196612
  547.1 16.6 %copy-start.63 = (bf16[512,1,64]{2,0,1:T(8,128)(2,1)S(1)}, bf16[512,1,64]{2,0,1:T(8,128)(2,1)}, u32[]{:S(2)}) copy-start(bf16[512,1,64]{2,0,1:T(8,128)(2,1)} %copy.244) | copy-start | bytes 196612
  547.1 16.7 %copy-start.32 = (bf16[2,256,1,4,128]{4,3,1,0,2:T(4,128)(2,1)S(1)}, bf16[2,256,1,4,128]{4,3,1,0,2:T(4,128)(2,1)}, u32[]{:S(2)}) copy-start(bf16[2,256,1,4,128]{4,3,1,0,2:T(4,128)(2,1)} %copy-done.31) | copy-start | bytes 1572868
  547.1 17.6 %copy-start.11 = (f32[2,1,4,256,256]{3,4,2,0,1:T(8,128)S(1)}, f32[2,1,4,256,256]{3,4,2,0,1:T(8,128)}, u32[]{:S(2)}) copy-start(f32[2,1,4,256,256]{3,4,2,0,1:T(8,128)} %get-tuple-element.1191) | copy-start | bytes 6291460
  563.3 45.5 %collective-permute-start.7 = (f32[512]{0:T(512)S(1)}, f32[512]{0:T(512)S(1)}, u32[]{:S(2)}, u32[]{:S(2)}) collective-permute-start(f32[512]{0:T(512)S(1)} %get-tuple-element.790), channel_id=1, source_target_pairs={{0,1},{1,0},{2,3},{3,2},{4,5},{5,4},{6,7},{7,6},{8,9},{9,8},{10,11... | collective-permute-start | bytes 6152 | tf_op jit(solution)/shard_map/ppermute | solution.py:354
  564.7 44.1 %copy-start.3 = (f32[512,512]{1,0:T(8,128)S(1)}, f32[512,512]{1,0:T(8,128)}, u32[]{:S(2)}) copy-start(f32[512,512]{1,0:T(8,128)} %copy-done.2) | copy-start | bytes 3145732
  678.8 40.2 %copy-start.128 = (s32[256]{0:T(256)S(1)}, s32[256]{0:T(256)}, u32[]{:S(2)}) copy-start(s32[256]{0:T(256)} %copy-done.127) | copy-start | bytes 3076
  678.8 120.3 %copy-start.10 = (bf16[512,2048]{1,0:T(8,128)(2,1)S(1)}, bf16[512,2048]{1,0:T(8,128)(2,1)}, u32[]{:S(2)}) copy-start(bf16[512,2048]{1,0:T(8,128)(2,1)} %copy-done.9) | copy-start | bytes 6291460
  691.4 249.1 %collective-permute-start.16 = (bf16[1024,4480]{1,0:T(8,128)(2,1)}, bf16[1024,4480]{1,0:T(8,128)(2,1)}, u32[]{:S(2)}, u32[]{:S(2)}) collective-permute-start(bf16[1024,4480]{1,0:T(8,128)(2,1)} %copy.229), channel_id=1, source_target_pairs={{0,2},{2,0},{4,6},{6,4},{8,10},{10,8},{12,14},{14,12},{16,18},{18,... | collective-permute-start | bytes 27525128 | tf_op jit(solution)/shard_map/ppermute | solution.py:357
  691.4 107.8 %collective-permute-start.8 = (bf16[1024,2048]{1,0:T(8,128)(2,1)}, bf16[1024,2048]{1,0:T(8,128)(2,1)}, u32[]{:S(2)}, u32[]{:S(2)}) collective-permute-start(bf16[1024,2048]{1,0:T(8,128)(2,1)} %get-tuple-element.808), channel_id=1, source_target_pairs={{0,2},{2,0},{4,6},{6,4},{8,10},{10,8},{12,14},{14,12},{16,18},{18,... | collective-permute-start | bytes 12582920 | tf_op jit(solution)/shard_map/ppermute | solution.py:357
  691.9 25.3 %collective-permute-start.12 = (bf16[256,2048]{1,0:T(8,128)(2,1)}, bf16[256,2048]{1,0:T(8,128)(2,1)S(1)}, u32[]{:S(2)}, u32[]{:S(2)}) collective-permute-start(bf16[256,2048]{1,0:T(8,128)(2,1)} %get-tuple-element.816), channel_id=1, source_target_pairs={{0,1},{1,0},{2,3},{3,2},{4,5},{5,4},{6,7},{7,6},{8,9},{9,8},{10,11... | collective-permute-start | bytes 3145736 | tf_op jit(solution)/shard_map/ppermute | solution.py:354
  693.5 47.6 %collective-permute-start.9 = (bf16[512,2048]{1,0:T(8,128)(2,1)}, bf16[512,2048]{1,0:T(8,128)(2,1)}, u32[]{:S(2)}, u32[]{:S(2)}) collective-permute-start(bf16[512,2048]{1,0:T(8,128)(2,1)} %get-tuple-element.810), channel_id=1, source_target_pairs={{0,4},{2,6},{4,0},{6,2},{8,12},{10,14},{12,8},{14,10},{16,20},{18,... | collective-permute-start | bytes 6291464 | tf_op jit(solution)/shard_map/ppermute | solution.py:357
  694.5 58.8 %collective-permute-start.10 = (bf16[512,2048]{1,0:T(8,128)(2,1)}, bf16[512,2048]{1,0:T(8,128)(2,1)}, u32[]{:S(2)}, u32[]{:S(2)}) collective-permute-start(bf16[512,2048]{1,0:T(8,128)(2,1)} %get-tuple-element.812), channel_id=1, source_target_pairs={{0,8},{2,10},{4,12},{6,14},{8,0},{10,2},{12,4},{14,6},{16,24},{18,... | collective-permute-start | bytes 6291464 | tf_op jit(solution)/shard_map/ppermute | solution.py:357
  717.1 82.0 %collective-permute-start.11 = (bf16[512,2048]{1,0:T(8,128)(2,1)}, bf16[512,2048]{1,0:T(8,128)(2,1)}, u32[]{:S(2)}, u32[]{:S(2)}) collective-permute-start(bf16[512,2048]{1,0:T(8,128)(2,1)} %get-tuple-element.814), channel_id=1, source_target_pairs={{0,24},{2,26},{4,28},{6,30},{8,16},{10,18},{12,20},{14,22},{16,8},... | collective-permute-start | bytes 6291464 | tf_op jit(solution)/shard_map/ppermute | solution.py:357
  719.1 80.1 %copy-start.64 = (bf16[256,256]{1,0:T(8,128)(2,1)}, bf16[256,256]{1,0:T(8,128)(2,1)S(1)}, u32[]{:S(2)}) copy-start(bf16[256,256]{1,0:T(8,128)(2,1)S(1)} %fusion.94) | copy-start | bytes 393220
  823.6 70.0 %collective-permute-start.13 = (bf16[256,2048]{1,0:T(8,128)(2,1)}, bf16[256,2048]{1,0:T(8,128)(2,1)}, u32[]{:S(2)}, u32[]{:S(2)}) collective-permute-start(bf16[256,2048]{1,0:T(8,128)(2,1)} %get-tuple-element.835), channel_id=1, source_target_pairs={{0,8},{2,10},{4,12},{6,14},{8,0},{10,2},{12,4},{14,6},{16,24},{18,... | collective-permute-start | bytes 3145736 | tf_op jit(solution)/shard_map/ppermute | solution.py:357
  848.5 141.9 %all-to-all-start.2 = ((bf16[16,16,2048]{2,1,0:T(8,128)(2,1)}), bf16[16,16,2048]{2,1,0:T(8,128)(2,1)}, u32[]{:S(2)}, u32[]{:S(2)}) async-start(bf16[16,16,2048]{2,1,0:T(8,128)(2,1)} %bitcast.184), calls=%async_computation.2 | async-start | bytes 2097152 | tf_op jit(solution)/shard_map/all_to_all | solution.py:399
  852.9 58.3 %collective-permute-start.14 = (bf16[256,2048]{1,0:T(8,128)(2,1)}, bf16[256,2048]{1,0:T(8,128)(2,1)}, u32[]{:S(2)}, u32[]{:S(2)}) collective-permute-start(bf16[256,2048]{1,0:T(8,128)(2,1)} %get-tuple-element.837), channel_id=1, source_target_pairs={{0,24},{2,26},{4,28},{6,30},{8,16},{10,18},{12,20},{14,22},{16,8},... | collective-permute-start | bytes 3145736 | tf_op jit(solution)/shard_map/ppermute | solution.py:357
  856.6 73.4 %collective-permute-start.15 = (bf16[256,2048]{1,0:T(8,128)(2,1)}, bf16[256,2048]{1,0:T(8,128)(2,1)}, u32[]{:S(2)}, u32[]{:S(2)}) collective-permute-start(bf16[256,2048]{1,0:T(8,128)(2,1)} %get-tuple-element.839), channel_id=1, source_target_pairs={{0,8},{2,10},{4,12},{6,14},{8,0},{10,2},{12,4},{14,6},{16,24},{18,... | collective-permute-start | bytes 3145736 | tf_op jit(solution)/shard_map/ppermute | solution.py:357
  856.6 120.5 %collective-permute-start.20 = (bf16[512,2048]{1,0:T(8,128)(2,1)}, bf16[512,2048]{1,0:T(8,128)(2,1)}, u32[]{:S(2)}, u32[]{:S(2)}) collective-permute-start(bf16[512,2048]{1,0:T(8,128)(2,1)} %get-tuple-element.862), channel_id=1, source_target_pairs={{0,4},{2,6},{4,0},{6,2},{8,12},{10,14},{12,8},{14,10},{16,20},{18,... | collective-permute-start | bytes 6291464 | tf_op jit(solution)/shard_map/ppermute | solution.py:357
  893.6 36.4 %copy-start.110 = (f32[2048]{0:T(1024)}, f32[2048]{0:T(1024)S(1)}, u32[]{:S(2)}) copy-start(f32[2048]{0:T(1024)S(1)} %get-tuple-element.868) | copy-start | bytes 24580
  893.6 66.2 %collective-permute-start.21 = (bf16[256,2048]{1,0:T(8,128)(2,1)}, bf16[256,2048]{1,0:T(8,128)(2,1)}, u32[]{:S(2)}, u32[]{:S(2)}) collective-permute-start(bf16[256,2048]{1,0:T(8,128)(2,1)} %get-tuple-element.864), channel_id=1, source_target_pairs={{0,1},{1,0},{2,3},{3,2},{4,5},{5,4},{6,7},{7,6},{8,9},{9,8},{10,11... | collective-permute-start | bytes 3145736 | tf_op jit(solution)/shard_map/ppermute | solution.py:354
  937.6 24.3 %collective-permute-start.17 = (bf16[128,2048]{1,0:T(8,128)(2,1)}, bf16[128,2048]{1,0:T(8,128)(2,1)S(1)}, u32[]{:S(2)}, u32[]{:S(2)}) collective-permute-start(bf16[128,2048]{1,0:T(8,128)(2,1)} %get-tuple-element.856), channel_id=1, source_target_pairs={{0,24},{2,26},{4,28},{6,30},{8,16},{10,18},{12,20},{14,22},{16,8},... | collective-permute-start | bytes 1572872 | tf_op jit(solution)/shard_map/ppermute | solution.py:357
  938.9 23.9 %collective-permute-start.18 = (bf16[128,2048]{1,0:T(8,128)(2,1)}, bf16[128,2048]{1,0:T(8,128)(2,1)S(1)}, u32[]{:S(2)}, u32[]{:S(2)}) collective-permute-start(bf16[128,2048]{1,0:T(8,128)(2,1)} %get-tuple-element.858), channel_id=1, source_target_pairs={{0,4},{2,6},{4,0},{6,2},{8,12},{10,14},{12,8},{14,10},{16,20},{18,... | collective-permute-start | bytes 1572872 | tf_op jit(solution)/shard_map/ppermute | solution.py:357
  958.9 45.8 %collective-permute-start.22 = (bf16[512,1536]{1,0:T(8,128)(2,1)}, bf16[512,1536]{1,0:T(8,128)(2,1)}, u32[]{:S(2)}, u32[]{:S(2)}) collective-permute-start(bf16[512,1536]{1,0:T(8,128)(2,1)} %get-tuple-element.883), channel_id=1, source_target_pairs={{0,8},{2,10},{4,12},{6,14},{8,0},{10,2},{12,4},{14,6},{16,24},{18,... | collective-permute-start | bytes 4718600 | tf_op jit(solution)/shard_map/ppermute | solution.py:357
  959.8 71.5 %collective-permute-start.23 = (bf16[512,1536]{1,0:T(8,128)(2,1)}, bf16[512,1536]{1,0:T(8,128)(2,1)}, u32[]{:S(2)}, u32[]{:S(2)}) collective-permute-start(bf16[512,1536]{1,0:T(8,128)(2,1)} %get-tuple-element.885), channel_id=1, source_target_pairs={{0,24},{2,26},{4,28},{6,30},{8,16},{10,18},{12,20},{14,22},{16,8},... | collective-permute-start | bytes 4718600 | tf_op jit(solution)/shard_map/ppermute | solution.py:357
  961.9 15.2 %collective-permute-start.19 = (bf16[128,2048]{1,0:T(8,128)(2,1)}, bf16[128,2048]{1,0:T(8,128)(2,1)}, u32[]{:S(2)}, u32[]{:S(2)}) collective-permute-start(bf16[128,2048]{1,0:T(8,128)(2,1)} %get-tuple-element.860), channel_id=1, source_target_pairs={{0,4},{2,6},{4,0},{6,2},{8,12},{10,14},{12,8},{14,10},{16,20},{18,... | collective-permute-start | bytes 1572872 | tf_op jit(solution)/shard_map/ppermute | solution.py:357
  962.8 42.0 %collective-permute-start.24 = (bf16[512,1408]{1,0:T(8,128)(2,1)}, bf16[512,1408]{1,0:T(8,128)(2,1)}, u32[]{:S(2)}, u32[]{:S(2)}) collective-permute-start(bf16[512,1408]{1,0:T(8,128)(2,1)} %get-tuple-element.887), channel_id=1, source_target_pairs={{0,4},{2,6},{4,0},{6,2},{8,12},{10,14},{12,8},{14,10},{16,20},{18,... | collective-permute-start | bytes 4325384 | tf_op jit(solution)/shard_map/ppermute | solution.py:357
  990.5 184.6 %all-to-all-start.3 = ((bf16[16,16,2048]{2,1,0:T(8,128)(2,1)}), bf16[16,16,2048]{2,1,0:T(8,128)(2,1)S(1)}, u32[]{:S(2)}, u32[]{:S(2)}) async-start(bf16[16,16,2048]{2,1,0:T(8,128)(2,1)} %bitcast.185), calls=%async_computation.3 | async-start | bytes 2097152 | tf_op jit(solution)/shard_map/all_to_all | solution.py:399
  994.1 76.6 %collective-permute-start.26 = (bf16[256,2048]{1,0:T(8,128)(2,1)}, bf16[256,2048]{1,0:T(8,128)(2,1)}, u32[]{:S(2)}, u32[]{:S(2)}) collective-permute-start(bf16[256,2048]{1,0:T(8,128)(2,1)} %get-tuple-element.902), channel_id=1, source_target_pairs={{0,24},{2,26},{4,28},{6,30},{8,16},{10,18},{12,20},{14,22},{16,8},... | collective-permute-start | bytes 3145736 | tf_op jit(solution)/shard_map/ppermute | solution.py:357
  997.8 1.5 collective-permute-start.25
  1044.3 71.5 %collective-permute-start.27 = (bf16[256,1536]{1,0:T(8,128)(2,1)}, bf16[256,1536]{1,0:T(8,128)(2,1)}, u32[]{:S(2)}, u32[]{:S(2)}) collective-permute-start(bf16[256,1536]{1,0:T(8,128)(2,1)} %get-tuple-element.904), channel_id=1, source_target_pairs={{0,24},{2,26},{4,28},{6,30},{8,16},{10,18},{12,20},{14,22},{16,8},... | collective-permute-start | bytes 2359304 | tf_op jit(solution)/shard_map/ppermute | solution.py:357
  1046.2 70.6 %collective-permute-start.28 = (bf16[256,1536]{1,0:T(8,128)(2,1)}, bf16[256,1536]{1,0:T(8,128)(2,1)}, u32[]{:S(2)}, u32[]{:S(2)}) collective-permute-start(bf16[256,1536]{1,0:T(8,128)(2,1)} %get-tuple-element.906), channel_id=1, source_target_pairs={{0,8},{2,10},{4,12},{6,14},{8,0},{10,2},{12,4},{14,6},{16,24},{18,... | collective-permute-start | bytes 2359304 | tf_op jit(solution)/shard_map/ppermute | solution.py:357
  1052.9 62.9 %collective-permute-start.29 = (bf16[256,1408]{1,0:T(8,128)(2,1)}, bf16[256,1408]{1,0:T(8,128)(2,1)}, u32[]{:S(2)}, u32[]{:S(2)}) collective-permute-start(bf16[256,1408]{1,0:T(8,128)(2,1)} %get-tuple-element.908), channel_id=1, source_target_pairs={{0,24},{2,26},{4,28},{6,30},{8,16},{10,18},{12,20},{14,22},{16,8},... | collective-permute-start | bytes 2162696 | tf_op jit(solution)/shard_map/ppermute | solution.py:357
  1055.8 14.9 %collective-permute-start.30 = (f32[128,128]{1,0:T(8,128)S(1)}, f32[128,128]{1,0:T(8,128)S(1)}, u32[]{:S(2)}, u32[]{:S(2)}) collective-permute-start(f32[128,128]{1,0:T(8,128)S(1)} %get-tuple-element.909), channel_id=1, source_target_pairs={{0,4},{2,6},{4,0},{6,2},{8,12},{10,14},{12,8},{14,10},{16,20},{18,... | collective-permute-start | bytes 196616 | tf_op jit(solution)/shard_map/ppermute | solution.py:357
  1126.2 64.6 %collective-permute-start.31 = (bf16[128,2048]{1,0:T(8,128)(2,1)}, bf16[128,2048]{1,0:T(8,128)(2,1)S(1)}, u32[]{:S(2)}, u32[]{:S(2)}) collective-permute-start(bf16[128,2048]{1,0:T(8,128)(2,1)} %get-tuple-element.921), channel_id=1, source_target_pairs={{0,8},{2,10},{4,12},{6,14},{8,0},{10,2},{12,4},{14,6},{16,24},{18,... | collective-permute-start | bytes 1572872 | tf_op jit(solution)/shard_map/ppermute | solution.py:357
  1171.0 19.8 %collective-permute-start.32 = (bf16[128,1536]{1,0:T(8,128)(2,1)}, bf16[128,1536]{1,0:T(8,128)(2,1)S(1)}, u32[]{:S(2)}, u32[]{:S(2)}) collective-permute-start(bf16[128,1536]{1,0:T(8,128)(2,1)} %get-tuple-element.923), channel_id=1, source_target_pairs={{0,4},{2,6},{4,0},{6,2},{8,12},{10,14},{12,8},{14,10},{16,20},{18,... | collective-permute-start | bytes 1179656 | tf_op jit(solution)/shard_map/ppermute | solution.py:357
  1172.2 18.6 %collective-permute-start.33 = (bf16[128,1536]{1,0:T(8,128)(2,1)}, bf16[128,1536]{1,0:T(8,128)(2,1)S(1)}, u32[]{:S(2)}, u32[]{:S(2)}) collective-permute-start(bf16[128,1536]{1,0:T(8,128)(2,1)} %get-tuple-element.925), channel_id=1, source_target_pairs={{0,4},{2,6},{4,0},{6,2},{8,12},{10,14},{12,8},{14,10},{16,20},{18,... | collective-permute-start | bytes 1179656 | tf_op jit(solution)/shard_map/ppermute | solution.py:357
  1173.1 17.7 %collective-permute-start.34 = (bf16[128,1408]{1,0:T(8,128)(2,1)}, bf16[128,1408]{1,0:T(8,128)(2,1)}, u32[]{:S(2)}, u32[]{:S(2)}) collective-permute-start(bf16[128,1408]{1,0:T(8,128)(2,1)} %get-tuple-element.927), channel_id=1, source_target_pairs={{0,8},{2,10},{4,12},{6,14},{8,0},{10,2},{12,4},{14,6},{16,24},{18,... | collective-permute-start | bytes 1081352 | tf_op jit(solution)/shard_map/ppermute | solution.py:357
  1173.1 17.7 %collective-permute-start.35 = (f32[128,128]{1,0:T(8,128)S(1)}, f32[128,128]{1,0:T(8,128)S(1)}, u32[]{:S(2)}, u32[]{:S(2)}) collective-permute-start(f32[128,128]{1,0:T(8,128)S(1)} %get-tuple-element.928), channel_id=1, source_target_pairs={{0,8},{2,10},{4,12},{6,14},{8,0},{10,2},{12,4},{14,6},{16,24},{18,... | collective-permute-start | bytes 196616 | tf_op jit(solution)/shard_map/ppermute | solution.py:357
  1196.5 7.3 collective-permute-start.37
  1198.9 5.4 collective-permute-start.36
  1203.7 4.3 collective-permute-start.38
  (122 other events, 580.8 us)
Sparse Core Ops, SparseCore 0:
  13.7 172.8 all-gather.4
  188.1 138.4 all-gather.2

commit v3 on v2

--- a/solution.py
+++ b/solution.py
@@ -88,25 +88,34 @@
     return jnp.concatenate([first * cosine - second * sine, second * cosine + first * sine], axis=-1)
 
 
-def copy_block(order_ref, source_ref, target_ref):
-    target_ref[...] = source_ref[...]
-
-
-def pick_blocks(values, order, block):
+def copy_blocks(order_ref, first_ref, second_ref, first_out_ref, second_out_ref):
+    first_out_ref[...] = first_ref[...]
+    second_out_ref[...] = second_ref[...]
+
+
+def pick_halves(values, order, block):
     height, width = values.shape
+    count = width // block // 2
     if block % 128:
-        return jnp.take(values.reshape(height, -1, block), order, axis=1).reshape(height, width)
+        mixed = jnp.take(values.reshape(height, -1, block), order, axis=1).reshape(height, width)
+        return mixed[:, : width // 2], mixed[:, width // 2 :]
+    half = jax.ShapeDtypeStruct((height, width // 2), values.dtype)
+    out_spec = pl.BlockSpec((height, block), lambda i, order: (0, i))
     return pl.pallas_call(
-        copy_block,
-        out_shape=jax.ShapeDtypeStruct(values.shape, values.dtype),
+        copy_blocks,
+        out_shape=(half, half),
         grid_spec=pltpu.PrefetchScalarGridSpec(
             num_scalar_prefetch=1,
-            grid=(width // block,),
-            in_specs=[pl.BlockSpec((height, block), lambda i, order: (0, order[i]))],
-            out_specs=pl.BlockSpec((height, block), lambda i, order: (0, i)),
+            grid=(count,),
+            in_specs=[
+                pl.BlockSpec((height, block), lambda i, order: (0, order[i])),
+                pl.BlockSpec((height, block), lambda i, order: (0, order[i + count])),
+            ],
+            out_specs=(out_spec, out_spec),
         ),
         cost_estimate=pl.CostEstimate(flops=0, transcendentals=0, bytes_accessed=4 * height * width),
-    )(order, values)
+        name="pick_halves",
+    )(order, values, values)
 
 
 def rotate_back(values, cosine, sine):
@@ -443,11 +452,9 @@
                 flip ^= mask
         relative.append(flip)
     block_order = jnp.bitwise_xor(group.astype(jnp.int32), jnp.array(relative, jnp.int32))
-    half_width = width // 2
 
     def split_left(left):
-        mixed = pick_blocks(left, block_order, shard)
-        return mixed[:, :half_width], mixed[:, half_width:]
+        return pick_halves(left, block_order, shard)
 
     inner_places = list(range(1, len(masks)))
 
@@ -488,15 +495,6 @@
         def step(self):
             return self.next() if self.stage < len(self.places) else self.last()
 
-    def advance(reductions, *others):
-        steps, results = unit(lambda: ([red.step() for red in reductions], [work() for work in others]))
-        for red, step in zip(reductions, steps):
-            if red.stage < len(red.places):
-                red.move(*step)
-            else:
-                red.result = step
-        return results
-
     order = [deal_order[0, 0] >= 0]
 
     def unit(work):
@@ -504,12 +502,20 @@
         results = lax.cond(
             order[0], work, lambda: jax.tree.map(lambda leaf: jnp.zeros(leaf.shape, leaf.dtype), shapes)
         )
-        results, order[0] = lax.optimization_barrier((results, order[0]))
-        return results
+        leaves, form = jax.tree.flatten(results)
+        least = min(range(len(leaves)), key=lambda place: leaves[place].size)
+        leaves[least], order[0] = lax.optimization_barrier((leaves[least], order[0]))
+        return jax.tree.unflatten(form, leaves)
+
+    def after(value, *others):
+        return lax.optimization_barrier((value, others))[0]
 
     in32 = whole_in.astype(f32)
     in_scale = rms_scale(in32)
     normed_low = (in32 * in_scale * gain_input).astype(bf16)
+    grad_left = split_left(whole_grad)
+    normed_left = split_left(normed_low)
+    full_gate = after(full_gate, whole_grad, grad_left, normed_left)
     gate_z = project(normed_low, full_gate)
     ssm_in = project(normed_low, full_input)
     state_raw = project(normed_low, full_state)
@@ -557,16 +563,14 @@
     mid32 = whole_mid.astype(f32)
     mid_scale = rms_scale(mid32)
     mid_low = (mid32 * mid_scale * gain_middle).astype(bf16)
-    grad_left = split_left(whole_grad)
-    mid_left = split_left(mid_low)
-    normed_left = split_left(normed_low)
     red_down, red_fgate, red_fup, red_branch, red_gate, red_input, red_rest = [
-        Reduction(order) for order in ((1, 2, 3), (2, 3, 1), (3, 2, 1), (1, 3, 2), (2, 3, 1), (3, 2, 1), (1, 3, 2))
+        Reduction(places) for places in ((1, 2, 3), (2, 3, 1), (3, 1, 2), (1, 3, 2), (2, 3, 1), (3, 1, 2), (1, 2, 3))
     ]
-    ff_cols = feed_gate.shape[1]
     gate_cols = mamba_gate.shape[1]
+    rest_cols = 2 * NS + STEP_PAD + query_weight.shape[1] + key_weight.shape[1] + value_weight.shape[1]
 
     def feed_forward():
+        mid_left = split_left(mid_low)
         gate_ff = project(mid_low, full_fgate)
         up_ff = project(mid_low, full_fup)
         sig_ff = jax.nn.sigmoid(gate_ff)
@@ -577,43 +581,31 @@
         grad_mid_norm = project_back(gate_ff_low, full_fgate) + project_back(up_ff_low, full_fup)
         grad_gain_mid = jnp.sum(grad_mid_norm * mid32 * mid_scale, axis=0)
         mid_part = rms_back(grad_mid_norm, mid32, mid_scale, gain_middle).astype(bf16)
-        return hidden_low, gate_ff_low, up_ff_low, mid_part, grad_gain_mid, core_send(grad_left, hidden_low)
-
-    hidden_low, gate_ff_low, up_ff_low, mid_part, grad_gain_mid, send_down = unit(feed_forward)
+        rights = (hidden_low, gate_ff_low, up_ff_low)
+        sends = [core_send(left, right) for left, right in zip((grad_left, mid_left, mid_left), rights)]
+        return grad_gain_mid, mid_part, mid_left, rights, sends
+
+    grad_gain_mid, mid_part, mid_left, feed_rights, sends = unit(feed_forward)
+    hidden_low = feed_rights[0]
     mid_other = other_lane(mid_part)
-    from_core_down = other_group(send_down, 1)
-
-    def feed_sends():
+    feed_lefts = (grad_left, mid_left, mid_left)
+    feed_came = [other_group(send, 1) for send in sends]
+    feeds = (red_down, red_fgate, red_fup)
+
+    def feed_output():
         ffn_part = project_back(hidden_low, full_fdown).astype(bf16)
-        send = jnp.concatenate([core_send(mid_left, gate_ff_low), core_send(mid_left, up_ff_low)], axis=1)
-        return lane_rows(ffn_part, lane), lane_rows(ffn_part, 1 - lane), send
-
-    ffn_own, ffn_send, send_feed = unit(feed_sends)
-    from_core_feed = other_group(send_feed, 1)
-    red_down.move(*unit(lambda: red_down.first(grad_left, hidden_low, from_core_down)))
-    moves = unit(
-        lambda: (
-            red_fgate.first(mid_left, gate_ff_low, from_core_feed[:, :ff_cols]),
-            red_fup.first(mid_left, up_ff_low, from_core_feed[:, ff_cols:]),
-        )
-    )
-    red_fgate.move(*moves[0])
-    red_fup.move(*moves[1])
-
-    def branch_start():
+        return lane_rows(ffn_part, lane), lane_rows(ffn_part, 1 - lane)
+
+    ffn_own, ffn_send = unit(feed_output)
+    moves = unit(lambda: [red.first(*given) for red, *given in zip(feeds, feed_lefts, feed_rights, feed_came)])
+    for red, move in zip(feeds, moves):
+        red.move(*move)
+
+    def branch_backward():
         grad_middle = whole_grad.astype(f32) + (mid_part.astype(f32) + mid_other.astype(f32))
         whole_branch = grad_middle.astype(bf16)
         grad_gated_norm = project(whole_branch, full_mix)
         cross_own = jnp.sum(grad_gated_norm * mixer_gain * (ssm_out * jax.nn.silu(gate_z)), axis=1)
-        return lane_rows(grad_middle, lane), whole_branch, grad_gated_norm, cross_own
-
-    grad_middle_own, whole_branch, grad_gated_norm, cross_own = unit(branch_start)
-    cross_other = other_lane(cross_own)
-    ffn_other = other_lane(ffn_send)
-
-    def attention_backward():
-        branch_left = split_left(whole_branch)
-        branch_right = jnp.concatenate([gated_low, attended_low], axis=1)
         grad_attended = project(whole_branch, full_attn).astype(bf16).reshape(micro, rows, kv_here, -1, HEAD)
         grad_probs = jnp.einsum("migkd,mjgd->mgkij", grad_attended, value_low, preferred_element_type=f32)
         grad_value = jnp.einsum("mgkij,migkd->mjgd", probs_low, grad_attended, preferred_element_type=f32)
@@ -624,12 +616,23 @@
         query_grad_low = rotate_back(grad_query_rot.reshape(total, -1, HEAD), cosine, sine).astype(bf16).reshape(total, -1)
         key_grad_low = rotate_back(grad_key_rot.reshape(total, -1, HEAD), cosine, sine).astype(bf16).reshape(total, -1)
         value_grad_low = grad_value.astype(bf16).reshape(total, -1)
+        branch_right = jnp.concatenate([gated_low, attended_low], axis=1)
         return (
-            branch_left, branch_right, core_send(branch_left, branch_right), query_grad_low, key_grad_low, value_grad_low
-        )
-
-    branch_left, branch_right, send_branch, query_grad_low, key_grad_low, value_grad_low = unit(attention_backward)
-    from_core_branch = other_group(send_branch, 1)
+            cross_own, lane_rows(grad_middle, lane), grad_gated_norm, split_left(whole_branch), branch_right,
+            (query_grad_low, key_grad_low, value_grad_low),
+        )
+
+    cross_own, grad_middle_own, grad_gated_norm, branch_left, branch_right, qkv_low = unit(branch_backward)
+
+    def second_moves():
+        return core_send(branch_left, branch_right), [red.next() for red in feeds], lax.optimization_barrier(ffn_send)
+
+    cross_other = other_lane(cross_own)
+    send_branch, moves, ffn_send = unit(second_moves)
+    branch_came = other_group(send_branch, 1)
+    ffn_other = other_lane(ffn_send)
+    for red, move in zip(feeds, moves):
+        red.move(*move)
 
     def state_space_backward():
         cross = (inv_rms**3) * ((cross_own + cross_other)[:, None] / inner_width)
@@ -651,106 +654,105 @@
         grad_bias = jnp.sum(grad_raw_step, axis=0)
         grad_state_raw, grad_kernel_state = conv_back(grad_state_act, state_raw, kernel_state, position)
         step_low = jnp.pad(grad_raw_step.astype(bf16), ((0, 0), (0, STEP_PAD - heads)))
-        rest_low = jnp.concatenate(
-            [grad_state_raw.astype(bf16), step_low, query_grad_low, key_grad_low, value_grad_low], axis=1
-        )
-        send = jnp.concatenate([core_send(normed_left, part) for part in (gate_low, input_low, rest_low)], axis=1)
+        first_right = jnp.concatenate([gate_low, input_low, grad_state_raw.astype(bf16), step_low, *qkv_low], axis=1)
         small = (grad_kernel_state, grad_kernel_inner, grad_mixer, grad_bias, grad_rate, grad_skip)
-        return gate_low, input_low, rest_low, send, small
-
-    gate_low, input_low, rest_low, send_first, small = unit(state_space_backward)
+        return small, first_right
+
+    small, first_right = unit(state_space_backward)
     grad_kernel_state, grad_kernel_inner, grad_mixer, grad_bias, grad_rate, grad_skip = small
-    from_core_first = other_group(send_first, 1)
-
-    def middle_moves():
+
+    def third_moves():
         ffn_out = ffn_own.astype(f32) + ffn_other.astype(f32)
         out_rows = (lane_rows(whole_mid, lane).astype(f32) + ffn_out).astype(bf16)
         return (
-            red_branch.first(branch_left, branch_right, from_core_branch),
-            red_down.next(), red_fgate.next(), red_fup.next(), deal_order_rows(out_rows),
-        )
-
-    moves = unit(middle_moves)
-    for red, move in zip((red_branch, red_down, red_fgate, red_fup), moves):
-        red.move(*move)
-    out_moved = exchange(moves[4])
+            core_send(normed_left, first_right),
+            red_branch.first(branch_left, branch_right, branch_came),
+            [red.step() for red in feeds],
+            deal_order_rows(out_rows),
+        )
+
+    def settle(reductions, steps):
+        for red, step in zip(reductions, steps):
+            if red.stage < len(red.places):
+                red.move(*step)
+            else:
+                red.result = step
+
+    send_first, move, moves, out_sent = unit(third_moves)
+    first_came = other_group(send_first, 1)
+    red_branch.move(*move)
+    settle(feeds, moves)
+    out_moved = exchange(out_sent)
 
     def input_gradient():
-        grad_normed = project_back(gate_low, full_gate) + project_back(input_low, full_input)
-        columns = [2 * NS, STEP_PAD, query_weight.shape[1], key_weight.shape[1], value_weight.shape[1]]
-        start = 0
-        for size, weight in zip(columns, (full_state, full_step, full_query, full_key, full_value)):
-            grad_normed = grad_normed + project_back(rest_low[:, start : start + size], weight)
-            start += size
+        weights = (full_gate, full_input, full_state, full_step, full_query, full_key, full_value)
+        grad_normed, start = 0.0, 0
+        for weight in weights:
+            grad_normed = grad_normed + project_back(first_right[:, start : start + weight.shape[1]], weight)
+            start += weight.shape[1]
         grad_gain_in = jnp.sum(grad_normed * in32 * in_scale, axis=0)
         in_part = rms_back(grad_normed, in32, in_scale, gain_input).astype(bf16)
         return grad_gain_in, lane_rows(in_part, lane), lane_rows(in_part, 1 - lane)
 
     grad_gain_in, in_own, in_send = unit(input_gradient)
-    in_other = other_lane(in_send)
-
-    advance([red_down, red_fgate, red_fup])
-    moves = unit(
-        lambda: (
-            red_gate.first(normed_left, gate_low, from_core_first[:, :gate_cols]),
-            red_input.first(normed_left, input_low, from_core_first[:, gate_cols : 2 * gate_cols]),
-            red_rest.first(normed_left, rest_low, from_core_first[:, 2 * gate_cols :]),
-        )
-    )
-    early = [red_down, red_fgate, red_fup, red_branch]
-    late = [red_gate, red_input, red_rest]
-    for red, move in zip(late, moves):
-        red.move(*move)
-
 
     shared = [grad_gain_in, grad_gain_mid, grad_kernel_state.reshape(-1)]
     split = [grad_kernel_inner.reshape(-1), grad_mixer, grad_bias, grad_rate, grad_skip]
-    used = sum(item.shape[0] for item in shared + split)
+    used = sum(item.shape[0] for item in shared) + lanes * sum(item.shape[0] for item in split)
     padded = -(-used // 1024) * 1024
+    firsts = (red_gate, red_input, red_rest)
+
+    def first_moves():
+        kept = (outer_sum(normed_left[0], first_right) + first_came.astype(f32)).astype(bf16)
+        kept = kept.reshape((2,) * len(inner_places) + (shard, -1))
+        moves, start = [], 0
+        for red, size in zip(firsts, (gate_cols, gate_cols, rest_cols)):
+            moves.append(halve(kept[..., start : start + size], red.places[0]))
+            start += size
+        return moves, lax.optimization_barrier(in_send), [red.step() for red in feeds if not hasattr(red, "result")]
+
+    moves, in_send, steps = unit(first_moves)
+    for red, move in zip(firsts, moves):
+        red.move(*move)
+    settle([red for red in feeds if not hasattr(red, "result")], steps)
+    in_other = other_lane(in_send)
+    block_out = unit(lambda: deal_take(out_moved))
 
     def send_input():
         in_sum = in_own.astype(f32) + in_other.astype(f32)
-        return deal_order_rows((in_sum + grad_middle_own).astype(bf16))
-
-    in_sent, flat = advance(
-        early,
-        send_input,
-        lambda: jnp.pad(jnp.concatenate(shared + split), (0, padded - used)).reshape(padded // 128, 128),
-    )
-    in_moved = exchange(in_sent)
-    flat_moved = other_group(flat, masks[0])
-    flat, block_out = advance(late, lambda: flat + flat_moved, lambda: deal_take(out_moved))
-    pending = early + late
-    bits = 1
-    pending = [red for red in pending if not hasattr(red, "result")]
-    while pending:
-        work = []
-        if bits < len(masks):
-            flat_moved = other_group(flat, masks[bits])
-            work.append(lambda: flat + flat_moved)
-        results = advance(pending, *work)
-        if bits < len(masks):
-            flat = results[0]
-            bits += 1
-        pending = [red for red in pending if not hasattr(red, "result")]
-    while bits < len(masks):
-        flat = flat + other_group(flat, masks[bits])
-        bits += 1
-    grad_input = deal_take(in_moved)
-    theirs = other_lane(flat).reshape(-1)
-    flat = flat.reshape(-1)
-    pieces = []
-    start = 0
-    for item in shared:
-        pieces.append(flat[start : start + item.shape[0]] + theirs[start : start + item.shape[0]])
-        start += item.shape[0]
-    for item in split:
-        mine, other = flat[start : start + item.shape[0]], theirs[start : start + item.shape[0]]
-        pieces.append((jnp.where(lane == 0, mine, other), jnp.where(lane == 0, other, mine)))
-        start += item.shape[0]
-    sum_gin, sum_gmid, sum_kst = pieces[0], pieces[1], pieces[2].reshape(CONV + 1, -1)
-    sum_kin = jnp.concatenate([half.reshape(CONV + 1, -1) for half in pieces[3]], axis=1)
-    sum_mix, sum_bias, sum_rate, sum_skip = [jnp.concatenate(pair) for pair in pieces[4:]]
+        zero = [jnp.zeros_like(item) for item in split]
+        low = [jnp.where(lane == 0, item, none) for item, none in zip(split, zero)]
+        high = [jnp.where(lane == 0, none, item) for item, none in zip(split, zero)]
+        flat = jnp.pad(jnp.concatenate(shared + low + high), (0, padded - used)).reshape(padded // 128, 128)
+        return deal_order_rows((in_sum + grad_middle_own).astype(bf16)), flat
+
+    everything = [*feeds, red_branch, *firsts]
+    in_moved = None
+    def small_sums():
+        pieces, start = [], 0
+        for item in shared + split + split:
+            pieces.append(flat.reshape(-1)[start : start + item.shape[0]])
+            start += item.shape[0]
+        halves = list(zip(pieces[3 : 3 + len(split)], pieces[3 + len(split) :]))
+        return (
+            pieces[0], pieces[1], pieces[2].reshape(CONV + 1, -1),
+            jnp.concatenate([half.reshape(CONV + 1, -1) for half in halves[0]], axis=1),
+            *[jnp.concatenate(pair) for pair in halves[1:]],
+        )
+
+    while pending := [red for red in everything if not hasattr(red, "result")]:
+        last = all(red.stage == len(red.places) for red in pending)
+        steps, other = unit(
+            lambda: (
+                [red.step() for red in pending],
+                (deal_take(in_moved), small_sums()) if last else send_input() if in_moved is None else (),
+            )
+        )
+        settle(pending, steps)
+        if in_moved is None:
+            in_moved = exchange(other[0])
+            flat = lax.psum(other[1], ("dp", "tensor"))
+    grad_input, (sum_gin, sum_gmid, sum_kst, sum_kin, sum_mix, sum_bias, sum_rate, sum_skip) = other
 
     query_cols, key_cols = query_weight.shape[1], key_weight.shape[1]
     total_fdown, total_fgate, total_fup = red_down.result, red_fgate.result, red_fup.result

time: 1230 us -> 1150 us (0.935)
  starting transfers between devices: 150 us -> 97.8 us
  Pallas kernels: 88.1 us -> 74.1 us
  waiting for transfers between devices: 472 us -> 458 us
    psum x0 -> x1, waiting for transfers between devices: none -> 120 us  [local(): flat = lax.psum(other[1], ('dp', 'tensor'))]
    ppermute x29 -> x26, waiting for transfers between devices: 235 us -> 157 us  [other_group(): return lax.ppermute(values, 'dp', [(i, i ^ bits) for i in range(groups)])]
    ppermute x10 -> x9, waiting for transfers between devices: 117 us -> 41.2 us  [other_lane(): return lax.ppermute(values, 'tensor', swap_lane)]
    ppermute x29 -> x26, starting transfers between devices: 119 us -> 67.9 us  [other_group(): return lax.ppermute(values, 'dp', [(i, i ^ bits) for i in range(groups)])]
    all_to_all x4, waiting for transfers between devices: 38.2 us -> 70.2 us  [exchange(): lax.all_to_all(buffer.reshape(groups, micro * per, width), 'dp', split_ax...]
    optimization_barrier x5 -> x0, local copies, waits for them, and re-layouts: 23.4 us -> none  [unit(): results, order[0] = lax.optimization_barrier((results, order[0]))]
    cond x128 -> x101, local copies, waits for them, and re-layouts: 10.6 us -> 26.3 us
    pallas_call x4, Pallas kernels: 37.1 us -> 23 us  [pick_halves(): pl.pallas_call(copy_blocks, out_shape=(half, half), grid_spec=pltpu.Prefe...]
  transfers between devices with their start and end apart: 45 -> 42, of which waited for: 20 -> 16; matrix products, arithmetic and copies ran while one was open for 24% -> 27% of each run, Pallas kernels for 4% -> 6%
where the time goes in v3:
time: 1150 us; the launch traced here: 1140 us
  waiting for transfers between devices  458 us (40%)
  matrix products  218 us (19%)
  local copies, waits for them, and re-layouts  165 us (14%)
  other arithmetic  108 us (9%)
  starting transfers between devices  97.8 us (9%)
  Pallas kernels  74.1 us (6%)
  between operations  16 us (1%)
    ppermute x26, waiting for transfers between devices, other_group(): return lax.ppermute(values, 'dp', [(i, i ^ bits) for i in range(groups)])  157 us
    psum x1, waiting for transfers between devices, local(): flat = lax.psum(other[1], ('dp', 'tensor'))  120 us
    dot_general x14, matrix products, outer_sum(): lax.dot_general(left, right, (((0,), (0,)), ((), ())), preferred_element_...  75.7 us
    dot_general x12, matrix products, project_back(): lax.dot_general(left, right, (((1,), (1,)), ((), ())), preferred_element_...  70.5 us
    all_to_all x4, waiting for transfers between devices, exchange(): lax.all_to_all(buffer.reshape(groups, micro * per, width), 'dp', split_ax...  70.2 us
    all_gather x2, waiting for transfers between devices, gather(): lax.all_gather(jnp.concatenate(pieces, axis=1), 'dp', axis=0, tiled=True)  70.1 us
    ppermute x26, starting transfers between devices, other_group(): return lax.ppermute(values, 'dp', [(i, i ^ bits) for i in range(groups)])  67.9 us
    dot_general x16, matrix products, project(): return jnp.dot(left, right, preferred_element_type=f32)  63.2 us
  transfers between devices with their start and end apart: 42, of which 16 were waited for; matrix products, arithmetic and copies ran while one was open for 27% of the time, Pallas kernels for 6%

profile of v3, /device:TPU:0, one launch (start us, length us, event | category | flops | bytes accessed | tf_op | source)
XLA Modules:
  0.0 1140.0 jit_solution(8035253666427723119)
XLA Ops:
  16.3 4.9 select_reduce_fusion
  23.0 7.4 all-to-all-start.1
  32.0 38.2 %all-to-all-done.1 = bf16[16,16,2048]{2,1,0:T(8,128)(2,1)S(1)} async-done(((bf16[16,16,2048]{2,1,0:T(8,128)(2,1)}), bf16[16,16,2048]{2,1,0:T(8,128)(2,1)S(1)}, u32[]{:S(2)}, u32[]{:S(2)}) %all-to-all-start.1) | async-done | bytes 1048608 | tf_op jit(solution)/shard_map/all_to_all | solution.py:408
  82.0 31.9 %all-to-all-done = bf16[16,16,2048]{2,1,0:T(8,128)(2,1)S(1)} async-done(((bf16[16,16,2048]{2,1,0:T(8,128)(2,1)}), bf16[16,16,2048]{2,1,0:T(8,128)(2,1)S(1)}, u32[]{:S(2)}, u32[]{:S(2)}) %all-to-all-start) | async-done | bytes 1048608 | tf_op jit(solution)/shard_map/all_to_all | solution.py:408
  122.3 6.4 pick_halves.7
  128.7 10.6 collective-permute-done
  149.4 37.2 %all-gather.5.cloned.1.call-done = bf16[2048,6528]{1,0:T(8,128)(2,1)} async-done(((bf16[128,6528]{1,0:T(8,128)(2,1)}), bf16[2048,6528]{1,0:T(8,128)(2,1)}) %all-gather.5.cloned.1.call-update) | async-done | bytes 26738704 | tf_op jit(solution)/shard_map/all_gather | solution.py:373
  196.2 6.6 fusion.139
  212.7 12.7 %fusion.140 = (bf16[2048,1536]{1,0:T(8,128)(2,1)}, bf16[2048,1536]{1,0:T(8,128)(2,1)}, bf16[2048,1536]{1,0:T(8,128)(2,1)S(1)}) fusion(bf16[2048,6528]{1,0:T(8,128)(2,1)} %all-gather.5.cloned.1.call-done), kind=kLoop, calls=%fused_computation.346 | loop fusion | bytes 37748736 | tf_op jit(solution)/shard_map/slice | solution.py:376
  225.5 4.7 fusion.101
  233.6 5.0 fusion.146.gate_ref
  238.6 8.0 fusion.105.signal_ref
  246.6 20.9 %state_forward.1 = (f32[512,1536]{1,0:T(8,128)}, f32[512,128]{1,0:T(8,128)}) custom-call(f32[512,1536]{1,0:T(8,128)} %fusion.105.signal_ref, f32[512,1536]{1,0:T(8,128)} %fusion.146.gate_ref, f32[5,1536]{1,0:T(8,128)} %taps_ref.1, f32[1,1536]{1,0:T(1,128)S(1)} %broadcast_in_dim_reshape.2.skip_ref, bf16[512,512]{1,0:T(8,128)(2,1)S(1)} %copy-done.28, ...), custom_call_target="tpu_custom_call" | custom-call | flops 1610612736 | bytes 9437184 | tf_op jit(solution)/shard_map/state_forward/pallas_call | solution.py:275
  280.6 6.4 fusion.103
  293.7 33.0 %all-gather.3.cloned.1.call-done = bf16[2048,6144]{1,0:T(8,128)(2,1)} async-done(((bf16[128,6144]{1,0:T(8,128)(2,1)}), bf16[2048,6144]{1,0:T(8,128)(2,1)}) %all-gather.3.cloned.1.call-update) | async-done | bytes 25165840 | tf_op jit(solution)/shard_map/all_gather | solution.py:373
  326.7 8.4 slice.516
  335.1 4.5 collective-permute-done.3
  339.6 5.6 fusion.110
  348.4 67.8 %conditional.13 = (f32[2048]{0:T(1024)S(1)}, bf16[512,2048]{1,0:T(8,128)(2,1)}, bf16[512,1024]{1,0:T(8,128)(2,1)}, bf16[512,2048]{1,0:T(8,128)(2,1)}, bf16[512,2...) conditional(s32[]{:T(128)} %convert_element_type.670, ...), branch_computations={%region_9.10_spmd, %region_10.13_spmd} | conditional | flops 27951890432 | bytes 179353824 | solution.py:502
  348.4 6.5 fusion.145
  355.0 6.4 pick_halves.4
  361.4 7.7 fusion.2
  369.1 10.4 multiply_convert_fusion
  379.6 6.1 convert_bitcast_fusion
  385.7 6.1 convolution_convert_fusion.1
  391.8 6.0 convolution_convert_fusion
  397.8 7.8 fusion
  405.5 8.5 multiply_reduce_fusion
  416.3 6.5 copy.218
  423.3 10.0 conditional.14
  423.3 8.5 convolution_convert_fusion.2
  436.3 6.0 collective-permute-done.6
  442.3 24.6 %conditional.15 = (bf16[512,2048]{1,0:T(8,128)(2,1)}, bf16[1,2,2,128,2048]{4,3,2,1,0:T(8,128)(2,1)}, bf16[512,2048]{1,0:T(8,128)(2,1)}, bf16[2,1,2,128,2048]{4,3...) conditional(s32[]{:T(128)} %convert_element_type.700, () %tuple.143, ...), branch_computations={%region_15.16_spmd, %region_16.17_spmd} | conditional | flops 6461325312 | bytes 59768880 | solution.py:502
  442.7 5.5 add_convert_fusion.2
  450.7 5.5 add_convert_fusion.1
  456.3 5.5 add_convert_fusion
  468.0 12.3 %collective-permute-start.9 = (bf16[512,2048]{1,0:T(8,128)(2,1)}, bf16[512,2048]{1,0:T(8,128)(2,1)}, u32[]{:S(2)}, u32[]{:S(2)}) collective-permute-start(bf16[512,2048]{1,0:T(8,128)(2,1)} %get-tuple-element.743), channel_id=1, source_target_pairs={{0,8},{2,10},{4,12},{6,14},{8,0},{10,2},{12,4},{14,6},{16,24},{18,... | collective-permute-start | bytes 6291464 | tf_op jit(solution)/shard_map/ppermute | solution.py:366
  493.5 42.1 %conditional.16 = (f32[512]{0:T(512)S(1)}, f32[256,2048]{1,0:T(8,128)}, f32[512,1536]{1,0:T(8,128)}, bf16[512,1024]{1,0:T(8,128)(2,1)}, bf16[512,1024]{1,0:T(8,1...) conditional(s32[]{:T(128)} %convert_element_type.701, ...), branch_computations={%region_17.18_spmd, %region_18.21_spmd} | conditional | flops 4854543872 | bytes 152723840 | solution.py:502
  506.3 5.4 multiply_reduce_fusion.2
  529.3 6.3 pick_halves.5
  535.7 37.1 %collective-permute-done.10 = bf16[512,2048]{1,0:T(8,128)(2,1)} collective-permute-done((bf16[512,2048]{1,0:T(8,128)(2,1)}, bf16[512,2048]{1,0:T(8,128)(2,1)}, u32[]{:S(2)}, u32[]{:S(2)}) %collective-permute-start.10) | collective-permute-done | bytes 2097184 | tf_op jit(solution)/shard_map/ppermute | solution.py:366
  572.8 22.4 %conditional.17 = (bf16[1024,2048]{1,0:T(8,128)(2,1)}, bf16[256,2048]{1,0:T(8,128)(2,1)}, bf16[1,1,2,128,2048]{4,3,2,1,0:T(8,128)(2,1)}, bf16[256,2048]{1,0:T(8,...) conditional(s32[]{:T(128)} %convert_element_type.702, ...), branch_computations={%region_21.22_spmd, %region_22.23_spmd} | conditional | flops 2162163712 | bytes 40894528 | solution.py:502
  573.0 6.4 convolution_convert_fusion.4
  600.9 74.7 %conditional.18 = (f32[1536]{0:T(1024)}, f32[24]{0:T(128)}, f32[24]{0:T(128)}, f32[24]{0:T(128)}, bf16[512,4480]{1,0:T(8,128)(2,1)}, /*index=5*/f32[2560]{0:T(1024)}, f32[7680]{0:T(1024)}) conditional(s32[]{:T(128)} %convert_element_type.703, () %tuple.152, (f32[1536]{0:T(1024)S(1)}, f32[512]{0:T(512)S(1)}, f32[512]{0:T(512)S(1)}, ...), branch_computations={%region_23.24_spmd, %region_24.34_spmd} | conditional | flops 4074679296 | bytes 83959152 | solution.py:502
  610.0 30.2 %state_backward.1 = (bf16[512,1536]{1,0:T(8,128)(2,1)}, bf16[512,1536]{1,0:T(8,128)(2,1)}, f32[2,8,1536]{2,1,0:T(8,128)}, f32[2,12,2,256]{3,2,1,0:T(2,128)}, f32...) custom-call(f32[512,1536]{1,0:T(8,128)} %get-tuple-element.446.grad_ref, f32[512,1536]{1,0:T(8,128)} %get-tuple-element.447.out_ref, ...), custom_call_target="tpu_custom_call" | custom-call | flops 4026531840 | bytes 15728640 | tf_op jit(solution)/shard_map/cond/branch_1_fun/state_backward/pallas_call | solution.py:294
  675.7 30.4 %conditional.19 = (bf16[1024,4480]{1,0:T(8,128)(2,1)}, bf16[512,2048]{1,0:T(8,128)(2,1)}, bf16[1,2,2,128,2048]{4,3,2,1,0:T(8,128)(2,1)}, bf16[128,2048]{1,0:T(8,...) conditional(s32[]{:T(128)} %convert_element_type.705, ...), branch_computations={%region_34.35_spmd, %region_35.36_spmd} | conditional | flops 7134380032 | bytes 69468360 | solution.py:502
  688.4 9.9 convolution_convert_fusion.5
  698.3 5.2 add_convert_fusion.5
  711.3 4.7 all-to-all-start.2
  718.8 37.4 %conditional.20 = (f32[2048]{0:T(1024)S(1)}, bf16[256,2048]{1,0:T(8,128)(2,1)}, bf16[256,2048]{1,0:T(8,128)(2,1)}) conditional(s32[]{:T(128)} %convert_element_type.707, () %tuple.158, (bf16[512,4480]{1,0:T(8,128)(2,1)}, bf16[2048,1536]{1,0:T(8,128)(2,1)}, bf16[2048,1536]{1,0:T(8,128)(2,1)}, bf16[2048,512]{1,0:T(8,128)(2,1)}, ...), branch_computations={%region_36.37_spmd, %region_37.40_spmd} | conditional | flops 9413066752 | bytes 153008448 | solution.py:502
  719.0 8.9 fusion.38
  727.9 6.6 fusion.36
  746.7 7.3 multiply_reduce_fusion.3
  756.2 20.2 %conditional.21 = (bf16[512,1536]{1,0:T(8,128)(2,1)}, bf16[2,1,2,128,1536]{4,3,2,1,0:T(8,128)(2,1)}, bf16[512,1536]{1,0:T(8,128)(2,1)}, bf16[2,2,1,128,1536]{4,3...) conditional(s32[]{:T(128)} %convert_element_type.708, ...), branch_computations={%region_40.41_spmd, %region_41.42_spmd} | conditional | flops 4713742336 | bytes 50724944 | solution.py:502
  756.4 9.2 add_convert_fusion.6
  784.4 22.5 %collective-permute-done.25 = bf16[256,2048]{1,0:T(8,128)(2,1)} collective-permute-done((bf16[256,2048]{1,0:T(8,128)(2,1)}, bf16[256,2048]{1,0:T(8,128)(2,1)}, u32[]{:S(2)}, u32[]{:S(2)}) %collective-permute-start.25) | collective-permute-done | bytes 1048608 | tf_op jit(solution)/shard_map/ppermute | solution.py:363
  806.9 7.2 collective-permute-done.24
  814.1 35.1 %collective-permute-done.23 = bf16[512,1536]{1,0:T(8,128)(2,1)} collective-permute-done((bf16[512,1536]{1,0:T(8,128)(2,1)}, bf16[512,1536]{1,0:T(8,128)(2,1)}, u32[]{:S(2)}, u32[]{:S(2)}) %collective-permute-start.23) | collective-permute-done | bytes 1572896 | tf_op jit(solution)/shard_map/ppermute | solution.py:366
  849.2 24.3 %conditional.23 = (bf16[256,2048]{1,0:T(8,128)(2,1)}, bf16[1,2,1,128,2048]{4,3,2,1,0:T(8,128)(2,1)S(1)}, bf16[256,1536]{1,0:T(8,128)(2,1)}, bf16[2,1,1,128,1536]...) conditional(s32[]{:T(128)} %convert_element_type.711, ...), branch_computations={%region_44.45_spmd, %region_45.46_spmd} | conditional | flops 284969120 | bytes 41935508 | solution.py:502
  883.4 69.0 %collective-permute-done.29 = bf16[256,1408]{1,0:T(8,128)(2,1)} collective-permute-done((bf16[256,1408]{1,0:T(8,128)(2,1)}, bf16[256,1408]{1,0:T(8,128)(2,1)}, u32[]{:S(2)}, u32[]{:S(2)}) %collective-permute-start.29) | collective-permute-done | bytes 720928 | tf_op jit(solution)/shard_map/ppermute | solution.py:366
  952.4 9.0 conditional.24
  961.4 31.0 %collective-permute-start.32 = (bf16[128,2048]{1,0:T(8,128)(2,1)}, bf16[128,2048]{1,0:T(8,128)(2,1)S(1)}, u32[]{:S(2)}, u32[]{:S(2)}) collective-permute-start(bf16[128,2048]{1,0:T(8,128)(2,1)} %get-tuple-element.822), channel_id=1, source_target_pairs={{0,8},{2,10},{4,12},{6,14},{8,0},{10,2},{12,4},{14,6},{16,24},{18,... | collective-permute-start | bytes 1572872 | tf_op jit(solution)/shard_map/ppermute | solution.py:366
  995.3 119.8 %all-reduce.14.cloned.1.call-done = f32[200,128]{1,0:T(8,128)} async-done(((f32[200,128]{1,0:T(8,128)}), f32[200,128]{1,0:T(8,128)}) %all-reduce.14.cloned.1.call-update) | async-done | bytes 102416 | tf_op jit(solution)/shard_map/psum | solution.py:754
  1115.2 12.4 %conditional.25 = (f32[128,1536]{1,0:T(8,128)}, f32[128,1536]{1,0:T(8,128)}, bf16[2,128,2048]{2,1,0:T(8,128)(2,1)}, f32[2048]{0:T(1024)}, f32[2048]{0:T(1024)}, ...) conditional(s32[]{:T(128)} %convert_element_type.713, ...), branch_computations={%region_49.50_spmd, %region_50.51_spmd} | conditional | flops 271485056 | bytes 13273516 | solution.py:502
  (583 shorter events, 333.4 us)
Async XLA Ops:
  7.2 179.3 %all-gather.5.cloned.1.call-start = ((), (), s32[]{:S(2)}) async-start(), calls=%async_computation.5 | async-start | bytes 28409856 | tf_op jit(solution)/shard_map/all_gather | solution.py:373
  13.6 313.1 %all-gather.3.cloned.1.call-start = ((), (), s32[]{:S(2)}) async-start(), calls=%async_computation.4 | async-start | bytes 26738688 | tf_op jit(solution)/shard_map/all_gather | solution.py:373
  21.5 92.5 %copy-start.109 = (s32[256]{0:T(256)}, s32[256]{0:T(256)S(1)}, u32[]{:S(2)}) copy-start(s32[256]{0:T(256)S(1)} %get-tuple-element.1360) | copy-start | bytes 3076
  23.0 47.2 %all-to-all-start.1 = ((bf16[16,16,2048]{2,1,0:T(8,128)(2,1)}), bf16[16,16,2048]{2,1,0:T(8,128)(2,1)S(1)}, u32[]{:S(2)}, u32[]{:S(2)}) async-start(bf16[16,16,2048]{2,1,0:T(8,128)(2,1)} %bitcast.152), calls=%async_computation.1 | async-start | bytes 2097152 | tf_op jit(solution)/shard_map/all_to_all | solution.py:408
  30.5 45.3 %copy-start.127 = (f32[24]{0:T(128)S(1)}, f32[24]{0:T(128)}, u32[]{:S(2)}) copy-start(f32[24]{0:T(128)} %param.74) | copy-start | bytes 292
  30.5 47.4 %copy-start.132 = (s32[16]{0:T(128)S(1)}, s32[16]{0:T(128)}, u32[]{:S(2)}) copy-start(s32[16]{0:T(128)} %constant.223.clone) | copy-start | bytes 196
  30.6 47.4 %copy-start.131 = (f32[24]{0:T(128)S(1)}, f32[24]{0:T(128)}, u32[]{:S(2)}) copy-start(f32[24]{0:T(128)} %param.73) | copy-start | bytes 292
  70.2 43.8 %all-to-all-start = ((bf16[16,16,2048]{2,1,0:T(8,128)(2,1)}), bf16[16,16,2048]{2,1,0:T(8,128)(2,1)S(1)}, u32[]{:S(2)}, u32[]{:S(2)}) async-start(bf16[16,16,2048]{2,1,0:T(8,128)(2,1)} %bitcast.144), calls=%async_computation | async-start | bytes 2097152 | tf_op jit(solution)/shard_map/all_to_all | solution.py:408
  74.2 172.3 %copy-start.98 = (s32[2,1,256]{2,1,0:T(1,128)}, s32[2,1,256]{2,1,0:T(1,128)S(1)}, u32[]{:S(2)}) copy-start(s32[2,1,256]{2,1,0:T(1,128)S(1)} %broadcast_in_dim.152.seg_row_ref) | copy-start | bytes 6148
  74.2 40.2 %copy-start.99 = (s32[1,1,2,256]{3,1,2,0:T(1,128)}, s32[1,1,2,256]{3,1,2,0:T(1,128)S(1)}, u32[]{:S(2)}) copy-start(s32[1,1,2,256]{3,1,2,0:T(1,128)S(1)} %copy.254) | copy-start | bytes 6148
  75.8 38.7 %copy-start.100 = (s32[1,1,2,256]{3,1,2,0:T(1,128)}, s32[1,1,2,256]{3,1,2,0:T(1,128)S(1)}, u32[]{:S(2)}) copy-start(s32[1,1,2,256]{3,1,2,0:T(1,128)S(1)} %copy.255) | copy-start | bytes 6148
  76.0 170.6 %copy-start.80 = (f32[1,1536]{1,0:T(1,128)}, f32[1,1536]{1,0:T(1,128)S(1)}, u32[]{:S(2)}) copy-start(f32[1,1536]{1,0:T(1,128)S(1)} %broadcast_in_dim_reshape.2.skip_ref) | copy-start | bytes 18436
  77.9 63.0 %copy-start.116 = (s32[16]{0:T(128)}, s32[16]{0:T(128)S(1)}, u32[]{:S(2)}) copy-start(s32[16]{0:T(128)S(1)} %broadcast_xor_fusion.order_ref) | copy-start | bytes 196
  77.9 111.0 %copy-start.123 = (f32[24]{0:T(128)}, f32[24]{0:T(128)S(1)}, u32[]{:S(2)}) copy-start(f32[24]{0:T(128)S(1)} %exponential_negate_fusion) | copy-start | bytes 292
  78.4 37.6 %collective-permute-start.1 = (bf16[256,2048]{1,0:T(8,128)(2,1)S(1)}, bf16[256,2048]{1,0:T(8,128)(2,1)}, u32[]{:S(2)}, u32[]{:S(2)}) collective-permute-start(bf16[256,2048]{1,0:T(8,128)(2,1)S(1)} %convolution_convert_fusion.10), channel_id=1, source_target_pairs={{0,1},{1,0},{2,3},{3,2},{4,5},{5,4},{6,7},{7,6},{8,9},{9,8},{10,11... | collective-permute-start | bytes 3145736 | tf_op jit(solution)/shard_map/ppermute | solution.py:363
  114.5 24.8 %collective-permute-start = (bf16[256,2048]{1,0:T(8,128)(2,1)S(1)}, bf16[256,2048]{1,0:T(8,128)(2,1)}, u32[]{:S(2)}, u32[]{:S(2)}) collective-permute-start(bf16[256,2048]{1,0:T(8,128)(2,1)S(1)} %convolution_convert_fusion.12), channel_id=1, source_target_pairs={{0,1},{1,0},{2,3},{3,2},{4,5},{5,4},{6,7},{7,6},{8,9},{9,8},{10,11... | collective-permute-start | bytes 3145736 | tf_op jit(solution)/shard_map/ppermute | solution.py:363
  146.1 40.4 %copy-start.7 = (bf16[512,2048]{1,0:T(8,128)(2,1)S(1)}, bf16[512,2048]{1,0:T(8,128)(2,1)}, u32[]{:S(2)}) copy-start(bf16[512,2048]{1,0:T(8,128)(2,1)} %multiply_convert_fusion.5.first_ref.second_ref) | copy-start | bytes 6291460
  146.2 40.4 %copy-start.122 = (f32[24]{0:T(128)S(1)}, f32[24]{0:T(128)}, u32[]{:S(2)}) copy-start(f32[24]{0:T(128)} %param.72) | copy-start | bytes 292
  196.0 74.1 %copy-start.47 = (bf16[512,1,64]{2,0,1:T(8,128)(2,1)}, bf16[512,1,64]{2,0,1:T(8,128)(2,1)S(1)}, u32[]{:S(2)}) copy-start(bf16[512,1,64]{2,0,1:T(8,128)(2,1)S(1)} %copy.244) | copy-start | bytes 196612
  196.2 74.0 %copy-start.49 = (bf16[512,1,64]{2,0,1:T(8,128)(2,1)}, bf16[512,1,64]{2,0,1:T(8,128)(2,1)S(1)}, u32[]{:S(2)}) copy-start(bf16[512,1,64]{2,0,1:T(8,128)(2,1)S(1)} %copy.245) | copy-start | bytes 196612
  268.6 7.8 collective-permute-start.2
  291.4 48.2 %collective-permute-start.3 = (bf16[512,2048]{1,0:T(8,128)(2,1)}, bf16[512,2048]{1,0:T(8,128)(2,1)}, u32[]{:S(2)}, u32[]{:S(2)}) collective-permute-start(bf16[512,2048]{1,0:T(8,128)(2,1)} %add_convert_fusion.11), channel_id=1, source_target_pairs={{0,1},{1,0},{2,3},{3,2},{4,5},{5,4},{6,7},{7,6},{8,9},{9,8},{10,11... | collective-permute-start | bytes 6291464 | tf_op jit(solution)/shard_map/ppermute | solution.py:363
  422.8 11.0 collective-permute-start.4
  422.8 13.5 %collective-permute-start.5 = (bf16[1024,2048]{1,0:T(8,128)(2,1)}, bf16[1024,2048]{1,0:T(8,128)(2,1)}, u32[]{:S(2)}, u32[]{:S(2)}) collective-permute-start(bf16[1024,2048]{1,0:T(8,128)(2,1)} %get-tuple-element.730), channel_id=1, source_target_pairs={{0,2},{2,0},{4,6},{6,4},{8,10},{10,8},{12,14},{14,12},{16,18},{18,... | collective-permute-start | bytes 12582920 | tf_op jit(solution)/shard_map/ppermute | solution.py:366
  423.3 19.0 %collective-permute-start.6 = (bf16[1024,2048]{1,0:T(8,128)(2,1)}, bf16[1024,2048]{1,0:T(8,128)(2,1)}, u32[]{:S(2)}, u32[]{:S(2)}) collective-permute-start(bf16[1024,2048]{1,0:T(8,128)(2,1)} %get-tuple-element.732), channel_id=1, source_target_pairs={{0,2},{2,0},{4,6},{6,4},{8,10},{10,8},{12,14},{14,12},{16,18},{18,... | collective-permute-start | bytes 12582920 | tf_op jit(solution)/shard_map/ppermute | solution.py:366
  433.3 60.2 %collective-permute-start.7 = (bf16[512,2048]{1,0:T(8,128)(2,1)}, bf16[512,2048]{1,0:T(8,128)(2,1)}, u32[]{:S(2)}, u32[]{:S(2)}) collective-permute-start(bf16[512,2048]{1,0:T(8,128)(2,1)} %get-tuple-element.735), channel_id=1, source_target_pairs={{0,1},{1,0},{2,3},{3,2},{4,5},{5,4},{6,7},{7,6},{8,9},{9,8},{10,11... | collective-permute-start | bytes 6291464 | tf_op jit(solution)/shard_map/ppermute | solution.py:363
  442.3 41.5 %copy-start.36 = (bf16[512,4,64]{0,2,1:T(8,128)(2,1)S(1)}, bf16[512,4,64]{0,2,1:T(8,128)(2,1)}, u32[]{:S(2)}) copy-start(bf16[512,4,64]{0,2,1:T(8,128)(2,1)} %copy-done.35) | copy-start | bytes 786436
  466.9 68.8 %collective-permute-start.8 = (bf16[512,2048]{1,0:T(8,128)(2,1)}, bf16[512,2048]{1,0:T(8,128)(2,1)}, u32[]{:S(2)}, u32[]{:S(2)}) collective-permute-start(bf16[512,2048]{1,0:T(8,128)(2,1)} %get-tuple-element.741), channel_id=1, source_target_pairs={{0,4},{2,6},{4,0},{6,2},{8,12},{10,14},{12,8},{14,10},{16,20},{18,... | collective-permute-start | bytes 6291464 | tf_op jit(solution)/shard_map/ppermute | solution.py:366
  468.0 67.7 %collective-permute-start.9 = (bf16[512,2048]{1,0:T(8,128)(2,1)}, bf16[512,2048]{1,0:T(8,128)(2,1)}, u32[]{:S(2)}, u32[]{:S(2)}) collective-permute-start(bf16[512,2048]{1,0:T(8,128)(2,1)} %get-tuple-element.743), channel_id=1, source_target_pairs={{0,8},{2,10},{4,12},{6,14},{8,0},{10,2},{12,4},{14,6},{16,24},{18,... | collective-permute-start | bytes 6291464 | tf_op jit(solution)/shard_map/ppermute | solution.py:366
  480.3 92.4 %collective-permute-start.10 = (bf16[512,2048]{1,0:T(8,128)(2,1)}, bf16[512,2048]{1,0:T(8,128)(2,1)}, u32[]{:S(2)}, u32[]{:S(2)}) collective-permute-start(bf16[512,2048]{1,0:T(8,128)(2,1)} %get-tuple-element.745), channel_id=1, source_target_pairs={{0,24},{2,26},{4,28},{6,30},{8,16},{10,18},{12,20},{14,22},{16,8},... | collective-permute-start | bytes 6291464 | tf_op jit(solution)/shard_map/ppermute | solution.py:366
  535.6 37.1 %copy-start.67 = (bf16[512,128]{1,0:T(8,128)(2,1)}, bf16[512,128]{1,0:T(8,128)(2,1)S(1)}, u32[]{:S(2)}) copy-start(bf16[512,128]{1,0:T(8,128)(2,1)S(1)} %get-tuple-element.752) | copy-start | bytes 393220
  535.6 37.1 %copy-start.118 = (f32[512]{0:T(512)}, f32[512]{0:T(512)S(1)}, u32[]{:S(2)}) copy-start(f32[512]{0:T(512)S(1)} %get-tuple-element.749) | copy-start | bytes 6148
  572.7 28.1 %copy-start.3 = (f32[512,512]{1,0:T(8,128)S(1)}, f32[512,512]{1,0:T(8,128)}, u32[]{:S(2)}) copy-start(f32[512,512]{1,0:T(8,128)} %copy-done.2) | copy-start | bytes 3145732
  572.7 28.1 %copy-start.61 = (f32[2,24,256]{2,0,1:T(2,128)S(1)}, f32[2,24,256]{2,0,1:T(2,128)}, u32[]{:S(2)}) copy-start(f32[2,24,256]{2,0,1:T(2,128)} %copy-done.60) | copy-start | bytes 147460
  595.2 80.4 %collective-permute-start.12 = (bf16[1024,2048]{1,0:T(8,128)(2,1)}, bf16[1024,2048]{1,0:T(8,128)(2,1)}, u32[]{:S(2)}, u32[]{:S(2)}) collective-permute-start(bf16[1024,2048]{1,0:T(8,128)(2,1)} %get-tuple-element.758), channel_id=1, source_target_pairs={{0,2},{2,0},{4,6},{6,4},{8,10},{10,8},{12,14},{14,12},{16,18},{18,... | collective-permute-start | bytes 12582920 | tf_op jit(solution)/shard_map/ppermute | solution.py:366
  595.2 3.6 collective-permute-start.11
  595.9 79.7 %collective-permute-start.13 = (bf16[256,2048]{1,0:T(8,128)(2,1)}, bf16[256,2048]{1,0:T(8,128)(2,1)}, u32[]{:S(2)}, u32[]{:S(2)}) collective-permute-start(bf16[256,2048]{1,0:T(8,128)(2,1)} %get-tuple-element.760), channel_id=1, source_target_pairs={{0,8},{2,10},{4,12},{6,14},{8,0},{10,2},{12,4},{14,6},{16,24},{18,... | collective-permute-start | bytes 3145736 | tf_op jit(solution)/shard_map/ppermute | solution.py:366
  595.9 79.7 %collective-permute-start.14 = (bf16[256,2048]{1,0:T(8,128)(2,1)}, bf16[256,2048]{1,0:T(8,128)(2,1)}, u32[]{:S(2)}, u32[]{:S(2)}) collective-permute-start(bf16[256,2048]{1,0:T(8,128)(2,1)} %get-tuple-element.762), channel_id=1, source_target_pairs={{0,24},{2,26},{4,28},{6,30},{8,16},{10,18},{12,20},{14,22},{16,8},... | collective-permute-start | bytes 3145736 | tf_op jit(solution)/shard_map/ppermute | solution.py:366
  597.9 77.7 %collective-permute-start.15 = (bf16[256,2048]{1,0:T(8,128)(2,1)}, bf16[256,2048]{1,0:T(8,128)(2,1)}, u32[]{:S(2)}, u32[]{:S(2)}) collective-permute-start(bf16[256,2048]{1,0:T(8,128)(2,1)} %get-tuple-element.764), channel_id=1, source_target_pairs={{0,4},{2,6},{4,0},{6,2},{8,12},{10,14},{12,8},{14,10},{16,20},{18,... | collective-permute-start | bytes 3145736 | tf_op jit(solution)/shard_map/ppermute | solution.py:366
  598.8 76.8 %collective-permute-start.16 = (bf16[256,2048]{1,0:T(8,128)(2,1)}, bf16[256,2048]{1,0:T(8,128)(2,1)}, u32[]{:S(2)}, u32[]{:S(2)}) collective-permute-start(bf16[256,2048]{1,0:T(8,128)(2,1)} %get-tuple-element.766), channel_id=1, source_target_pairs={{0,1},{1,0},{2,3},{3,2},{4,5},{5,4},{6,7},{7,6},{8,9},{9,8},{10,11... | collective-permute-start | bytes 3145736 | tf_op jit(solution)/shard_map/ppermute | solution.py:363
  600.8 74.8 %copy-start.51 = (bf16[256,256]{1,0:T(8,128)(2,1)}, bf16[256,256]{1,0:T(8,128)(2,1)S(1)}, u32[]{:S(2)}) copy-start(bf16[256,256]{1,0:T(8,128)(2,1)S(1)} %fusion.82) | copy-start | bytes 393220
  600.9 74.7 %copy-start.12 = (bf16[512,2048]{1,0:T(8,128)(2,1)S(1)}, bf16[512,2048]{1,0:T(8,128)(2,1)}, u32[]{:S(2)}) copy-start(bf16[512,2048]{1,0:T(8,128)(2,1)} %copy-done.11) | copy-start | bytes 6291460
  706.0 50.2 %collective-permute-start.17 = (bf16[1024,4480]{1,0:T(8,128)(2,1)}, bf16[1024,4480]{1,0:T(8,128)(2,1)}, u32[]{:S(2)}, u32[]{:S(2)}) collective-permute-start(bf16[1024,4480]{1,0:T(8,128)(2,1)} %get-tuple-element.771), channel_id=1, source_target_pairs={{0,2},{2,0},{4,6},{6,4},{8,10},{10,8},{12,14},{14,12},{16,18},{18,... | collective-permute-start | bytes 27525128 | tf_op jit(solution)/shard_map/ppermute | solution.py:366
  706.0 50.2 %collective-permute-start.18 = (bf16[128,2048]{1,0:T(8,128)(2,1)}, bf16[128,2048]{1,0:T(8,128)(2,1)}, u32[]{:S(2)}, u32[]{:S(2)}) collective-permute-start(bf16[128,2048]{1,0:T(8,128)(2,1)} %get-tuple-element.774), channel_id=1, source_target_pairs={{0,24},{2,26},{4,28},{6,30},{8,16},{10,18},{12,20},{14,22},{16,8},... | collective-permute-start | bytes 1572872 | tf_op jit(solution)/shard_map/ppermute | solution.py:366
  707.6 48.6 %collective-permute-start.19 = (bf16[128,2048]{1,0:T(8,128)(2,1)}, bf16[128,2048]{1,0:T(8,128)(2,1)}, u32[]{:S(2)}, u32[]{:S(2)}) collective-permute-start(bf16[128,2048]{1,0:T(8,128)(2,1)} %get-tuple-element.776), channel_id=1, source_target_pairs={{0,4},{2,6},{4,0},{6,2},{8,12},{10,14},{12,8},{14,10},{16,20},{18,... | collective-permute-start | bytes 1572872 | tf_op jit(solution)/shard_map/ppermute | solution.py:366
  709.1 47.1 %collective-permute-start.20 = (bf16[128,2048]{1,0:T(8,128)(2,1)}, bf16[128,2048]{1,0:T(8,128)(2,1)}, u32[]{:S(2)}, u32[]{:S(2)}) collective-permute-start(bf16[128,2048]{1,0:T(8,128)(2,1)} %get-tuple-element.778), channel_id=1, source_target_pairs={{0,8},{2,10},{4,12},{6,14},{8,0},{10,2},{12,4},{14,6},{16,24},{18,... | collective-permute-start | bytes 1572872 | tf_op jit(solution)/shard_map/ppermute | solution.py:366
  709.4 75.0 %collective-permute-start.21 = (bf16[512,2048]{1,0:T(8,128)(2,1)}, bf16[512,2048]{1,0:T(8,128)(2,1)}, u32[]{:S(2)}, u32[]{:S(2)}) collective-permute-start(bf16[512,2048]{1,0:T(8,128)(2,1)} %get-tuple-element.785), channel_id=1, source_target_pairs={{0,4},{2,6},{4,0},{6,2},{8,12},{10,14},{12,8},{14,10},{16,20},{18,... | collective-permute-start | bytes 6291464 | tf_op jit(solution)/shard_map/ppermute | solution.py:366
  711.3 71.6 %all-to-all-start.2 = ((bf16[16,16,2048]{2,1,0:T(8,128)(2,1)}), bf16[16,16,2048]{2,1,0:T(8,128)(2,1)S(1)}, u32[]{:S(2)}, u32[]{:S(2)}) async-start(bf16[16,16,2048]{2,1,0:T(8,128)(2,1)} %bitcast.187), calls=%async_computation.2 | async-start | bytes 2097152 | tf_op jit(solution)/shard_map/all_to_all | solution.py:408
  776.4 72.8 %copy-start.91 = (f32[2048]{0:T(1024)S(1)}, f32[2048]{0:T(1024)}, u32[]{:S(2)}) copy-start(f32[2048]{0:T(1024)} %copy-done.90) | copy-start | bytes 24580
  776.4 37.8 %collective-permute-start.22 = (bf16[512,1536]{1,0:T(8,128)(2,1)}, bf16[512,1536]{1,0:T(8,128)(2,1)}, u32[]{:S(2)}, u32[]{:S(2)}) collective-permute-start(bf16[512,1536]{1,0:T(8,128)(2,1)} %get-tuple-element.787), channel_id=1, source_target_pairs={{0,8},{2,10},{4,12},{6,14},{8,0},{10,2},{12,4},{14,6},{16,24},{18,... | collective-permute-start | bytes 4718600 | tf_op jit(solution)/shard_map/ppermute | solution.py:366
  778.4 70.8 %collective-permute-start.23 = (bf16[512,1536]{1,0:T(8,128)(2,1)}, bf16[512,1536]{1,0:T(8,128)(2,1)}, u32[]{:S(2)}, u32[]{:S(2)}) collective-permute-start(bf16[512,1536]{1,0:T(8,128)(2,1)} %get-tuple-element.789), channel_id=1, source_target_pairs={{0,24},{2,26},{4,28},{6,30},{8,16},{10,18},{12,20},{14,22},{16,8},... | collective-permute-start | bytes 4718600 | tf_op jit(solution)/shard_map/ppermute | solution.py:366
  780.7 33.4 %collective-permute-start.24 = (bf16[512,1408]{1,0:T(8,128)(2,1)}, bf16[512,1408]{1,0:T(8,128)(2,1)}, u32[]{:S(2)}, u32[]{:S(2)}) collective-permute-start(bf16[512,1408]{1,0:T(8,128)(2,1)} %get-tuple-element.791), channel_id=1, source_target_pairs={{0,4},{2,6},{4,0},{6,2},{8,12},{10,14},{12,8},{14,10},{16,20},{18,... | collective-permute-start | bytes 4325384 | tf_op jit(solution)/shard_map/ppermute | solution.py:366
  782.2 24.7 %collective-permute-start.25 = (bf16[256,2048]{1,0:T(8,128)(2,1)}, bf16[256,2048]{1,0:T(8,128)(2,1)}, u32[]{:S(2)}, u32[]{:S(2)}) collective-permute-start(bf16[256,2048]{1,0:T(8,128)(2,1)} %get-tuple-element.793), channel_id=1, source_target_pairs={{0,1},{1,0},{2,3},{3,2},{4,5},{5,4},{6,7},{7,6},{8,9},{9,8},{10,11... | collective-permute-start | bytes 3145736 | tf_op jit(solution)/shard_map/ppermute | solution.py:363
  873.5 241.7 %all-to-all-start.3 = ((bf16[16,16,2048]{2,1,0:T(8,128)(2,1)}), bf16[16,16,2048]{2,1,0:T(8,128)(2,1)S(1)}, u32[]{:S(2)}, u32[]{:S(2)}) async-start(bf16[16,16,2048]{2,1,0:T(8,128)(2,1)} %bitcast.188), calls=%async_computation.3 | async-start | bytes 2097152 | tf_op jit(solution)/shard_map/all_to_all | solution.py:408
  877.5 237.6 %all-reduce.14.cloned.1.call-start = ((), (), s32[]{:S(2)}) async-start(), calls=%async_computation.6 | async-start | bytes 204800 | tf_op jit(solution)/shard_map/psum | solution.py:754
  877.5 74.9 %collective-permute-start.26 = (bf16[256,2048]{1,0:T(8,128)(2,1)}, bf16[256,2048]{1,0:T(8,128)(2,1)}, u32[]{:S(2)}, u32[]{:S(2)}) collective-permute-start(bf16[256,2048]{1,0:T(8,128)(2,1)} %get-tuple-element.806), channel_id=1, source_target_pairs={{0,24},{2,26},{4,28},{6,30},{8,16},{10,18},{12,20},{14,22},{16,8},... | collective-permute-start | bytes 3145736 | tf_op jit(solution)/shard_map/ppermute | solution.py:366
  881.3 71.1 %collective-permute-start.27 = (bf16[256,1536]{1,0:T(8,128)(2,1)}, bf16[256,1536]{1,0:T(8,128)(2,1)}, u32[]{:S(2)}, u32[]{:S(2)}) collective-permute-start(bf16[256,1536]{1,0:T(8,128)(2,1)} %get-tuple-element.808), channel_id=1, source_target_pairs={{0,24},{2,26},{4,28},{6,30},{8,16},{10,18},{12,20},{14,22},{16,8},... | collective-permute-start | bytes 2359304 | tf_op jit(solution)/shard_map/ppermute | solution.py:366
  881.4 71.0 %collective-permute-start.28 = (bf16[256,1536]{1,0:T(8,128)(2,1)}, bf16[256,1536]{1,0:T(8,128)(2,1)}, u32[]{:S(2)}, u32[]{:S(2)}) collective-permute-start(bf16[256,1536]{1,0:T(8,128)(2,1)} %get-tuple-element.810), channel_id=1, source_target_pairs={{0,4},{2,6},{4,0},{6,2},{8,12},{10,14},{12,8},{14,10},{16,20},{18,... | collective-permute-start | bytes 2359304 | tf_op jit(solution)/shard_map/ppermute | solution.py:366
  883.4 69.0 %collective-permute-start.29 = (bf16[256,1408]{1,0:T(8,128)(2,1)}, bf16[256,1408]{1,0:T(8,128)(2,1)}, u32[]{:S(2)}, u32[]{:S(2)}) collective-permute-start(bf16[256,1408]{1,0:T(8,128)(2,1)} %get-tuple-element.812), channel_id=1, source_target_pairs={{0,8},{2,10},{4,12},{6,14},{8,0},{10,2},{12,4},{14,6},{16,24},{18,... | collective-permute-start | bytes 2162696 | tf_op jit(solution)/shard_map/ppermute | solution.py:366
  961.4 153.7 %collective-permute-start.32 = (bf16[128,2048]{1,0:T(8,128)(2,1)}, bf16[128,2048]{1,0:T(8,128)(2,1)S(1)}, u32[]{:S(2)}, u32[]{:S(2)}) collective-permute-start(bf16[128,2048]{1,0:T(8,128)(2,1)} %get-tuple-element.822), channel_id=1, source_target_pairs={{0,8},{2,10},{4,12},{6,14},{8,0},{10,2},{12,4},{14,6},{16,24},{18,... | collective-permute-start | bytes 1572872 | tf_op jit(solution)/shard_map/ppermute | solution.py:366
  992.4 122.7 %collective-permute-start.30 = (bf16[128,1536]{1,0:T(8,128)(2,1)}, bf16[128,1536]{1,0:T(8,128)(2,1)S(1)}, u32[]{:S(2)}, u32[]{:S(2)}) collective-permute-start(bf16[128,1536]{1,0:T(8,128)(2,1)} %get-tuple-element.816), channel_id=1, source_target_pairs={{0,4},{2,6},{4,0},{6,2},{8,12},{10,14},{12,8},{14,10},{16,20},{18,... | collective-permute-start | bytes 1179656 | tf_op jit(solution)/shard_map/ppermute | solution.py:366
  993.9 121.3 %collective-permute-start.31 = (bf16[128,1536]{1,0:T(8,128)(2,1)}, bf16[128,1536]{1,0:T(8,128)(2,1)S(1)}, u32[]{:S(2)}, u32[]{:S(2)}) collective-permute-start(bf16[128,1536]{1,0:T(8,128)(2,1)} %get-tuple-element.818), channel_id=1, source_target_pairs={{0,8},{2,10},{4,12},{6,14},{8,0},{10,2},{12,4},{14,6},{16,24},{18,... | collective-permute-start | bytes 1179656 | tf_op jit(solution)/shard_map/ppermute | solution.py:366
  993.9 121.3 %collective-permute-start.33 = (bf16[128,1408]{1,0:T(8,128)(2,1)}, bf16[128,1408]{1,0:T(8,128)(2,1)}, u32[]{:S(2)}, u32[]{:S(2)}) collective-permute-start(bf16[128,1408]{1,0:T(8,128)(2,1)} %get-tuple-element.824), channel_id=1, source_target_pairs={{0,24},{2,26},{4,28},{6,30},{8,16},{10,18},{12,20},{14,22},{16,8},... | collective-permute-start | bytes 1081352 | tf_op jit(solution)/shard_map/ppermute | solution.py:366
  1127.6 5.0 collective-permute-start.34
  (112 other events, 730.0 us)
Sparse Core Ops, SparseCore 0:
  13.7 172.8 all-gather.4
  188.2 138.4 all-gather.2
  995.4 119.6 all-reduce.13

commit v4 on v3

--- a/solution.py
+++ b/solution.py
@@ -116,6 +116,21 @@
         cost_estimate=pl.CostEstimate(flops=0, transcendentals=0, bytes_accessed=4 * height * width),
         name="pick_halves",
     )(order, values, values)
+
+
+def hand_over(values, microseconds):
+    def idle(values_ref, out_ref):
+        pass
+
+    return pl.pallas_call(
+        idle,
+        out_shape=jax.ShapeDtypeStruct(values.shape, values.dtype),
+        in_specs=[pl.BlockSpec(memory_space=pl.ANY)],
+        out_specs=pl.BlockSpec(memory_space=pl.ANY),
+        input_output_aliases={0: 0},
+        cost_estimate=pl.CostEstimate(flops=microseconds * 1150000000, transcendentals=0, bytes_accessed=0),
+        name="hand_over",
+    )(values)
 
 
 def rotate_back(values, cosine, sine):
@@ -366,19 +381,22 @@
         return lax.ppermute(values, "dp", [(i, i ^ bits) for i in range(groups)])
 
     step_padded = jnp.pad(step_weight, ((0, 0), (0, STEP_PAD - step_weight.shape[1])))
-    early = [mamba_gate, mamba_input, state_weight, step_padded, query_weight, key_weight, value_weight, mamba_out, attention_out]
-    late = [feed_gate, feed_up, feed_down]
-
-    def gather(pieces):
-        whole = lax.all_gather(jnp.concatenate(pieces, axis=1), "dp", axis=0, tiled=True)
-        found, start = [], 0
-        for piece in pieces:
-            found.append(whole[:, start : start + piece.shape[1]])
-            start += piece.shape[1]
-        return found
-
-    full_gate, full_input, full_state, full_step, full_query, full_key, full_value, full_mix, full_attn = gather(early)
-    full_fgate, full_fup, full_fdown = gather(late)
+    early = dict(
+        gate=mamba_gate, input=mamba_input, state=state_weight, step=step_padded, query=query_weight, key=key_weight,
+        value=value_weight, mix=mamba_out, attn=attention_out,
+    )
+    late = dict(fgate=feed_gate, fup=feed_up, fdown=feed_down)
+    whole, places_of = {}, {}
+    for label, group_weights in (("early", early), ("late", late)):
+        start = 0
+        for name, weight in group_weights.items():
+            places_of[name] = (label, start, weight.shape[1])
+            start += weight.shape[1]
+        whole[label] = lax.all_gather(jnp.concatenate(list(group_weights.values()), axis=1), "dp", axis=0, tiled=True)
+
+    def full(name):
+        label, start, size = places_of[name]
+        return lax.slice_in_dim(whole[label], start, start + size, axis=1)
 
     own_places = jnp.arange(own, dtype=jnp.int32)
     own_order = lax.dynamic_slice_in_dim(deal_order, device * own, own, 1)
@@ -441,9 +459,7 @@
     allowed = (segment[:, :, None] == segment[:, None, :]) & (places[None, None, :] <= places[None, :, None])
     position = (places[None, :] - before).reshape(total, 1)
 
-    masks = [1, 2] + [4, 12][: max(0, groups.bit_length() - 3)]
-    while 1 << len(masks) < groups:
-        masks.append(1 << len(masks))
+    masks = [1 << place for place in range(groups.bit_length() - 1)]
     relative = []
     for block in range(groups):
         flip = 0
@@ -513,14 +529,13 @@
     in32 = whole_in.astype(f32)
     in_scale = rms_scale(in32)
     normed_low = (in32 * in_scale * gain_input).astype(bf16)
-    grad_left = split_left(whole_grad)
     normed_left = split_left(normed_low)
-    full_gate = after(full_gate, whole_grad, grad_left, normed_left)
-    gate_z = project(normed_low, full_gate)
-    ssm_in = project(normed_low, full_input)
-    state_raw = project(normed_low, full_state)
+    whole["early"] = after(whole["early"], whole_grad, normed_left)
+    gate_z = project(normed_low, full("gate"))
+    ssm_in = project(normed_low, full("input"))
+    state_raw = project(normed_low, full("state"))
     heads = step_weight.shape[1]
-    raw_step = project(normed_low, full_step)[:, :heads]
+    raw_step = project(normed_low, full("step"))[:, :heads]
     state_low = jax.nn.silu(conv_sum(state_raw, kernel_state, position)).astype(bf16)
     rate = -jnp.exp(log_rate)
     step_size = jax.nn.softplus(raw_step + step_bias)
@@ -542,9 +557,9 @@
     gated_low = (ssm_out * jax.nn.silu(gate_z) * inv_rms * mixer_gain).astype(bf16)
 
     cosine, sine = rope_tables(position)
-    query_low = rotate(project(normed_low, full_query).reshape(total, -1, HEAD), cosine, sine).astype(bf16)
-    key_low = rotate(project(normed_low, full_key).reshape(total, -1, HEAD), cosine, sine).astype(bf16)
-    value_low = project(normed_low, full_value).astype(bf16)
+    query_low = rotate(project(normed_low, full("query")).reshape(total, -1, HEAD), cosine, sine).astype(bf16)
+    key_low = rotate(project(normed_low, full("key")).reshape(total, -1, HEAD), cosine, sine).astype(bf16)
+    value_low = project(normed_low, full("value")).astype(bf16)
     kv_here = key_low.shape[1]
     query_low = query_low.reshape(micro, rows, kv_here, -1, HEAD)
     key_low = key_low.reshape(micro, rows, kv_here, HEAD)
@@ -557,56 +572,74 @@
     attended_low = (
         jnp.einsum("mgkij,mjgd->migkd", probs_low, value_low, preferred_element_type=f32).astype(bf16).reshape(total, -1)
     )
-    branch_part = (project_back(gated_low, full_mix) + project_back(attended_low, full_attn)).astype(bf16)
+    branch_part = (project_back(gated_low, full("mix")) + project_back(attended_low, full("attn"))).astype(bf16)
     branch = branch_part.astype(f32) + other_lane(branch_part).astype(f32)
     whole_mid = (in32 + branch).astype(bf16)
     mid32 = whole_mid.astype(f32)
     mid_scale = rms_scale(mid32)
     mid_low = (mid32 * mid_scale * gain_middle).astype(bf16)
-    red_down, red_fgate, red_fup, red_branch, red_gate, red_input, red_rest = [
-        Reduction(places) for places in ((1, 2, 3), (2, 3, 1), (3, 1, 2), (1, 3, 2), (2, 3, 1), (3, 1, 2), (1, 2, 3))
+    red_fgate, red_fup, red_branch, red_low, red_high = [
+        Reduction(places) for places in ((1, 2), (2, 1), (1, 2), (1, 2), (2, 1))
     ]
+    feeds = (red_fgate, red_fup)
+    ff_cols = feed_gate.shape[1]
     gate_cols = mamba_gate.shape[1]
-    rest_cols = 2 * NS + STEP_PAD + query_weight.shape[1] + key_weight.shape[1] + value_weight.shape[1]
 
     def feed_forward():
-        mid_left = split_left(mid_low)
-        gate_ff = project(mid_low, full_fgate)
-        up_ff = project(mid_low, full_fup)
+        gate_ff = project(mid_low, full("fgate"))
+        up_ff = project(mid_low, full("fup"))
         sig_ff = jax.nn.sigmoid(gate_ff)
         hidden_low = (gate_ff * sig_ff * up_ff).astype(bf16)
-        grad_hidden = project(whole_grad, full_fdown)
+        grad_hidden = project(whole_grad, full("fdown"))
         gate_ff_low = (grad_hidden * up_ff * (sig_ff * (1.0 + gate_ff * (1.0 - sig_ff)))).astype(bf16)
         up_ff_low = (grad_hidden * (gate_ff * sig_ff)).astype(bf16)
-        grad_mid_norm = project_back(gate_ff_low, full_fgate) + project_back(up_ff_low, full_fup)
+        grad_mid_norm = project_back(gate_ff_low, full("fgate")) + project_back(up_ff_low, full("fup"))
         grad_gain_mid = jnp.sum(grad_mid_norm * mid32 * mid_scale, axis=0)
         mid_part = rms_back(grad_mid_norm, mid32, mid_scale, gain_middle).astype(bf16)
-        rights = (hidden_low, gate_ff_low, up_ff_low)
-        sends = [core_send(left, right) for left, right in zip((grad_left, mid_left, mid_left), rights)]
-        return grad_gain_mid, mid_part, mid_left, rights, sends
-
-    grad_gain_mid, mid_part, mid_left, feed_rights, sends = unit(feed_forward)
-    hidden_low = feed_rights[0]
-    mid_other = other_lane(mid_part)
-    feed_lefts = (grad_left, mid_left, mid_left)
-    feed_came = [other_group(send, 1) for send in sends]
-    feeds = (red_down, red_fgate, red_fup)
+        return grad_gain_mid, mid_part, hidden_low, jnp.concatenate([gate_ff_low, up_ff_low], axis=1)
+
+    grad_gain_mid, mid_part, hidden_low, feed_low = unit(feed_forward)
+    mid_other = hand_over(other_lane(mid_part), 3000)
 
     def feed_output():
-        ffn_part = project_back(hidden_low, full_fdown).astype(bf16)
-        return lane_rows(ffn_part, lane), lane_rows(ffn_part, 1 - lane)
-
-    ffn_own, ffn_send = unit(feed_output)
-    moves = unit(lambda: [red.first(*given) for red, *given in zip(feeds, feed_lefts, feed_rights, feed_came)])
+        ffn_part = project_back(hidden_low, full("fdown")).astype(bf16)
+        mid_left = split_left(mid_low)
+        return (
+            lane_rows(ffn_part, lane), lane_rows(ffn_part, 1 - lane), mid_left[0], core_send(mid_left, feed_low),
+            outer_sum(whole_grad, hidden_low).astype(bf16),
+        )
+
+    ffn_own, ffn_send, mid_keep, send_feed, part_fdown = unit(feed_output)
+    sum_fdown = lax.psum_scatter(part_fdown, "dp", scatter_dimension=0, tiled=True)
+    feed_came = other_group(send_feed, 1)
+
+    def keep_first(keep, right, came, reductions, sizes):
+        kept = (outer_sum(keep, right) + came.astype(f32)).astype(bf16)
+        kept = kept.reshape((2,) * len(inner_places) + (shard, -1))
+        moves, start = [], 0
+        for red, size in zip(reductions, sizes):
+            moves.append(halve(kept[..., start : start + size], red.places[0]))
+            start += size
+        return moves
+
+    def settle(reductions, steps):
+        for red, step in zip(reductions, steps):
+            if red.stage < len(red.places):
+                red.move(*step)
+            else:
+                red.result = step
+
+    mid_other, feed_came = lax.optimization_barrier((mid_other, feed_came))
+    moves = unit(lambda: keep_first(mid_keep, feed_low, feed_came, feeds, (ff_cols, ff_cols)))
     for red, move in zip(feeds, moves):
         red.move(*move)
 
     def branch_backward():
         grad_middle = whole_grad.astype(f32) + (mid_part.astype(f32) + mid_other.astype(f32))
         whole_branch = grad_middle.astype(bf16)
-        grad_gated_norm = project(whole_branch, full_mix)
+        grad_gated_norm = project(whole_branch, full("mix"))
         cross_own = jnp.sum(grad_gated_norm * mixer_gain * (ssm_out * jax.nn.silu(gate_z)), axis=1)
-        grad_attended = project(whole_branch, full_attn).astype(bf16).reshape(micro, rows, kv_here, -1, HEAD)
+        grad_attended = project(whole_branch, full("attn")).astype(bf16).reshape(micro, rows, kv_here, -1, HEAD)
         grad_probs = jnp.einsum("migkd,mjgd->mgkij", grad_attended, value_low, preferred_element_type=f32)
         grad_value = jnp.einsum("mgkij,migkd->mjgd", probs_low, grad_attended, preferred_element_type=f32)
         weighted_sum = jnp.sum(probs * grad_probs, axis=-1, keepdims=True)
@@ -617,22 +650,18 @@
         key_grad_low = rotate_back(grad_key_rot.reshape(total, -1, HEAD), cosine, sine).astype(bf16).reshape(total, -1)
         value_grad_low = grad_value.astype(bf16).reshape(total, -1)
         branch_right = jnp.concatenate([gated_low, attended_low], axis=1)
+        branch_left = split_left(whole_branch)
         return (
-            cross_own, lane_rows(grad_middle, lane), grad_gated_norm, split_left(whole_branch), branch_right,
+            cross_own, lane_rows(grad_middle, lane), grad_gated_norm, branch_left, branch_right,
             (query_grad_low, key_grad_low, value_grad_low),
         )
 
     cross_own, grad_middle_own, grad_gated_norm, branch_left, branch_right, qkv_low = unit(branch_backward)
 
-    def second_moves():
-        return core_send(branch_left, branch_right), [red.next() for red in feeds], lax.optimization_barrier(ffn_send)
-
     cross_other = other_lane(cross_own)
-    send_branch, moves, ffn_send = unit(second_moves)
+    send_branch, steps = unit(lambda: (core_send(branch_left, branch_right), [red.step() for red in feeds]))
     branch_came = other_group(send_branch, 1)
-    ffn_other = other_lane(ffn_send)
-    for red, move in zip(feeds, moves):
-        red.move(*move)
+    settle(feeds, steps)
 
     def state_space_backward():
         cross = (inv_rms**3) * ((cross_own + cross_other)[:, None] / inner_width)
@@ -662,30 +691,22 @@
     grad_kernel_state, grad_kernel_inner, grad_mixer, grad_bias, grad_rate, grad_skip = small
 
     def third_moves():
-        ffn_out = ffn_own.astype(f32) + ffn_other.astype(f32)
-        out_rows = (lane_rows(whole_mid, lane).astype(f32) + ffn_out).astype(bf16)
         return (
             core_send(normed_left, first_right),
             red_branch.first(branch_left, branch_right, branch_came),
+            lax.optimization_barrier(ffn_send),
             [red.step() for red in feeds],
-            deal_order_rows(out_rows),
-        )
-
-    def settle(reductions, steps):
-        for red, step in zip(reductions, steps):
-            if red.stage < len(red.places):
-                red.move(*step)
-            else:
-                red.result = step
-
-    send_first, move, moves, out_sent = unit(third_moves)
+            sum_fdown.astype(f32),
+        )
+
+    send_first, move, ffn_send, steps, total_fdown = unit(third_moves)
+    settle(feeds, steps)
     first_came = other_group(send_first, 1)
     red_branch.move(*move)
-    settle(feeds, moves)
-    out_moved = exchange(out_sent)
+    ffn_other = other_lane(ffn_send)
 
     def input_gradient():
-        weights = (full_gate, full_input, full_state, full_step, full_query, full_key, full_value)
+        weights = [full(name) for name in ("gate", "input", "state", "step", "query", "key", "value")]
         grad_normed, start = 0.0, 0
         for weight in weights:
             grad_normed = grad_normed + project_back(first_right[:, start : start + weight.shape[1]], weight)
@@ -698,67 +719,70 @@
 
     shared = [grad_gain_in, grad_gain_mid, grad_kernel_state.reshape(-1)]
     split = [grad_kernel_inner.reshape(-1), grad_mixer, grad_bias, grad_rate, grad_skip]
-    used = sum(item.shape[0] for item in shared) + lanes * sum(item.shape[0] for item in split)
+    used = sum(item.shape[0] for item in shared + split)
     padded = -(-used // 1024) * 1024
-    firsts = (red_gate, red_input, red_rest)
+    firsts = (red_low, red_high)
+    first_sizes = (first_right.shape[1] // 256 * 128, first_right.shape[1] - first_right.shape[1] // 256 * 128)
 
     def first_moves():
-        kept = (outer_sum(normed_left[0], first_right) + first_came.astype(f32)).astype(bf16)
-        kept = kept.reshape((2,) * len(inner_places) + (shard, -1))
-        moves, start = [], 0
-        for red, size in zip(firsts, (gate_cols, gate_cols, rest_cols)):
-            moves.append(halve(kept[..., start : start + size], red.places[0]))
-            start += size
-        return moves, lax.optimization_barrier(in_send), [red.step() for red in feeds if not hasattr(red, "result")]
-
-    moves, in_send, steps = unit(first_moves)
+        moves = keep_first(normed_left[0], first_right, first_came, firsts, first_sizes)
+        flat = jnp.pad(jnp.concatenate(shared + split), (0, padded - used)).reshape(padded // 128, 128)
+        ffn_out = ffn_own.astype(f32) + ffn_other.astype(f32)
+        out_rows = (lane_rows(whole_mid, lane).astype(f32) + ffn_out).astype(bf16)
+        return moves, lax.optimization_barrier(in_send), flat, deal_order_rows(out_rows), [red.step() for red in (*feeds, red_branch)]
+
+    moves, in_send, flat, out_sent, steps = unit(first_moves)
+    settle((*feeds, red_branch), steps)
+    out_moved = exchange(out_sent)
     for red, move in zip(firsts, moves):
         red.move(*move)
-    settle([red for red in feeds if not hasattr(red, "result")], steps)
     in_other = other_lane(in_send)
-    block_out = unit(lambda: deal_take(out_moved))
+    flat_moved = other_group(flat, masks[0])
+    flat = unit(lambda: flat + flat_moved)
+    flat_moved = other_group(flat, masks[1])
 
     def send_input():
         in_sum = in_own.astype(f32) + in_other.astype(f32)
-        zero = [jnp.zeros_like(item) for item in split]
-        low = [jnp.where(lane == 0, item, none) for item, none in zip(split, zero)]
-        high = [jnp.where(lane == 0, none, item) for item, none in zip(split, zero)]
-        flat = jnp.pad(jnp.concatenate(shared + low + high), (0, padded - used)).reshape(padded // 128, 128)
-        return deal_order_rows((in_sum + grad_middle_own).astype(bf16)), flat
+        return deal_order_rows((in_sum + grad_middle_own).astype(bf16))
 
     everything = [*feeds, red_branch, *firsts]
     in_moved = None
-    def small_sums():
-        pieces, start = [], 0
-        for item in shared + split + split:
-            pieces.append(flat.reshape(-1)[start : start + item.shape[0]])
-            start += item.shape[0]
-        halves = list(zip(pieces[3 : 3 + len(split)], pieces[3 + len(split) :]))
-        return (
-            pieces[0], pieces[1], pieces[2].reshape(CONV + 1, -1),
-            jnp.concatenate([half.reshape(CONV + 1, -1) for half in halves[0]], axis=1),
-            *[jnp.concatenate(pair) for pair in halves[1:]],
-        )
-
+    bits = 2
     while pending := [red for red in everything if not hasattr(red, "result")]:
         last = all(red.stage == len(red.places) for red in pending)
-        steps, other = unit(
+        steps, flat, other = unit(
             lambda: (
                 [red.step() for red in pending],
-                (deal_take(in_moved), small_sums()) if last else send_input() if in_moved is None else (),
+                flat + flat_moved if bits <= len(masks) else flat,
+                (deal_take(in_moved), deal_take(out_moved)) if last else send_input() if in_moved is None else (),
             )
         )
         settle(pending, steps)
+        if bits < len(masks):
+            flat_moved = other_group(flat, masks[bits])
+        bits += 1
         if in_moved is None:
-            in_moved = exchange(other[0])
-            flat = lax.psum(other[1], ("dp", "tensor"))
-    grad_input, (sum_gin, sum_gmid, sum_kst, sum_kin, sum_mix, sum_bias, sum_rate, sum_skip) = other
+            in_moved = exchange(other)
+    grad_input, block_out = other
+    theirs = other_lane(flat).reshape(-1)
+    flat = flat.reshape(-1)
+    pieces, start = [], 0
+    for item in shared:
+        pieces.append(flat[start : start + item.shape[0]] + theirs[start : start + item.shape[0]])
+        start += item.shape[0]
+    for item in split:
+        mine, other = flat[start : start + item.shape[0]], theirs[start : start + item.shape[0]]
+        pieces.append((jnp.where(lane == 0, mine, other), jnp.where(lane == 0, other, mine)))
+        start += item.shape[0]
+    sum_gin, sum_gmid, sum_kst = pieces[0], pieces[1], pieces[2].reshape(CONV + 1, -1)
+    sum_kin = jnp.concatenate([half.reshape(CONV + 1, -1) for half in pieces[3]], axis=1)
+    sum_mix, sum_bias, sum_rate, sum_skip = [jnp.concatenate(pair) for pair in pieces[4:]]
 
     query_cols, key_cols = query_weight.shape[1], key_weight.shape[1]
-    total_fdown, total_fgate, total_fup = red_down.result, red_fgate.result, red_fup.result
+    total_fgate, total_fup = red_fgate.result, red_fup.result
     total_mix, total_attn = red_branch.result[:, :gate_cols], red_branch.result[:, gate_cols:]
-    total_gate, total_input = red_gate.result, red_input.result
-    rest = red_rest.result
+    rest = jnp.concatenate([red.result for red in firsts], axis=1)
+    total_gate, total_input, rest = rest[:, :gate_cols], rest[:, gate_cols : 2 * gate_cols], rest[:, 2 * gate_cols :]
     total_step = rest[:, 2 * NS : 2 * NS + heads]
     start = 2 * NS + STEP_PAD
     total_query = rest[:, start : start + query_cols]

time: 1150 us -> 1020 us (0.89)
  waiting for transfers between devices: 458 us -> 400 us
  local copies, waits for them, and re-layouts: 165 us -> 116 us
  starting transfers between devices: 97.8 us -> 66.8 us
    psum x1 -> x0, waiting for transfers between devices: 120 us -> none  [local(): flat = lax.psum(other[1], ('dp', 'tensor'))]
    ppermute x26 -> x22, waiting for transfers between devices: 157 us -> 217 us  [other_group(): return lax.ppermute(values, 'dp', [(i, i ^ bits) for i in range(groups)])]
    ppermute x9 -> x10, waiting for transfers between devices: 41.2 us -> 81.3 us  [other_lane(): return lax.ppermute(values, 'tensor', swap_lane)]
    all_gather x2, waiting for transfers between devices: 70.1 us -> 32.4 us  [local(): lax.all_gather(jnp.concatenate(list(group_weights.values()), axis=1), 'dp...]
    ppermute x26 -> x22, starting transfers between devices: 67.9 us -> 36 us  [other_group(): return lax.ppermute(values, 'dp', [(i, i ^ bits) for i in range(groups)])]
    slice x11 -> x1, local copies, waits for them, and re-layouts: 31.2 us -> 2.07 us  [local(): rest[:, :gate_cols]]
    pallas_call x1, Pallas kernels: 20.9 us -> 35.8 us  [state_forward(): pl.pallas_call(state_forward_kernel, out_shape=(jax.ShapeDtypeStruct((tot...]
    convert_element_type x14 -> x9, other arithmetic: 30 us -> 22.3 us  [next(): return halve(self.added().astype(bf16), self.places[self.stage])]
  transfers between devices with their start and end apart: 42 -> 39, of which waited for: 16 -> 15; matrix products, arithmetic and copies ran while one was open for 27% -> 30% of each run, Pallas kernels for 6% -> 8%
where the time goes in v4:
time: 1020 us; the launch traced here: 1010 us
  waiting for transfers between devices  400 us (39%)
  matrix products  225 us (22%)
  local copies, waits for them, and re-layouts  116 us (11%)
  other arithmetic  101 us (10%)
  Pallas kernels  82.9 us (8%)
  starting transfers between devices  66.8 us (7%)
  between operations  16.2 us (2%)
    ppermute x22, waiting for transfers between devices, other_group(): return lax.ppermute(values, 'dp', [(i, i ^ bits) for i in range(groups)])  217 us
    ppermute x10, waiting for transfers between devices, other_lane(): return lax.ppermute(values, 'tensor', swap_lane)  81.3 us
    dot_general x12, matrix products, project_back(): lax.dot_general(left, right, (((1,), (1,)), ((), ())), preferred_element_...  78 us
    dot_general x11, matrix products, outer_sum(): lax.dot_general(left, right, (((0,), (0,)), ((), ())), preferred_element_...  72 us
    dot_general x16, matrix products, project(): return jnp.dot(left, right, preferred_element_type=f32)  70.4 us
    all_to_all x4, waiting for transfers between devices, exchange(): lax.all_to_all(buffer.reshape(groups, micro * per, width), 'dp', split_ax...  69 us
    ppermute x22, starting transfers between devices, other_group(): return lax.ppermute(values, 'dp', [(i, i ^ bits) for i in range(groups)])  36 us
    pallas_call x1, Pallas kernels, state_forward(): pl.pallas_call(state_forward_kernel, out_shape=(jax.ShapeDtypeStruct((tot...  35.8 us
  transfers between devices with their start and end apart: 39, of which 15 were waited for; matrix products, arithmetic and copies ran while one was open for 30% of the time, Pallas kernels for 8%

profile of v4, /device:TPU:0, one launch (start us, length us, event | category | flops | bytes accessed | tf_op | source)
XLA Modules:
  0.0 1010.5 jit_solution(17841836697458168776)
XLA Ops:
  18.7 4.9 select_reduce_fusion
  25.3 7.4 all-to-all-start
  34.7 37.8 %all-to-all-done = bf16[16,16,2048]{2,1,0:T(8,128)(2,1)S(1)} async-done(((bf16[16,16,2048]{2,1,0:T(8,128)(2,1)}), bf16[16,16,2048]{2,1,0:T(8,128)(2,1)S(1)}, u32[]{:S(2)}, u32[]{:S(2)}) %all-to-all-start) | async-done | bytes 1048608 | tf_op jit(solution)/shard_map/all_to_all | solution.py:426
  72.6 3.7 all-to-all-start.1
  84.9 31.1 %all-to-all-done.1 = bf16[16,16,2048]{2,1,0:T(8,128)(2,1)S(1)} async-done(((bf16[16,16,2048]{2,1,0:T(8,128)(2,1)}), bf16[16,16,2048]{2,1,0:T(8,128)(2,1)S(1)}, u32[]{:S(2)}, u32[]{:S(2)}) %all-to-all-start.1) | async-done | bytes 1048608 | tf_op jit(solution)/shard_map/all_to_all | solution.py:426
  121.1 20.2 %collective-permute-done.1 = bf16[256,2048]{1,0:T(8,128)(2,1)S(1)} collective-permute-done((bf16[256,2048]{1,0:T(8,128)(2,1)S(1)}, bf16[256,2048]{1,0:T(8,128)(2,1)S(1)}, u32[]{:S(2)}, u32[]{:S(2)}) %collective-permute-start.1) | collective-permute-done | bytes 1048608 | tf_op jit(solution)/shard_map/ppermute | solution.py:378
  146.5 6.7 pick_halves.5
  153.2 3.3 multiply_convert_fusion.4
  156.5 32.4 %all-gather.5.cloned.1.call-done = bf16[2048,6528]{1,0:T(8,128)(2,1)} async-done(((bf16[128,6528]{1,0:T(8,128)(2,1)}), bf16[2048,6528]{1,0:T(8,128)(2,1)}) %all-gather.5.cloned.1.call-update) | async-done | bytes 26738704 | tf_op jit(solution)/shard_map/all_gather | solution.py:395
  197.5 4.0 copy.198
  201.5 3.5 fusion.154
  217.7 8.1 fusion.89.gate_ref
  225.8 8.1 fusion.91.signal_ref
  234.0 35.8 %state_forward.1 = (f32[512,1536]{1,0:T(8,128)}, f32[512,128]{1,0:T(8,128)}) custom-call(f32[512,1536]{1,0:T(8,128)} %fusion.91.signal_ref, f32[512,1536]{1,0:T(8,128)} %fusion.89.gate_ref, f32[5,1536]{1,0:T(8,128)} %taps_ref.1, f32[1,1536]{1,0:T(1,128)S(1)} %broadcast_in_dim_reshape.2.skip_ref, bf16[512,512]{1,0:T(8,128)(2,1)S(1)} %copy-done.22, ...), custom_call_target="tpu_custom_call" | custom-call | flops 1610612736 | bytes 9437184 | tf_op jit(solution)/shard_map/state_forward/pallas_call | solution.py:290
  280.0 4.2 multiply_convert_fusion.6
  284.2 6.3 fusion.87
  295.7 45.5 %collective-permute-done.3 = bf16[512,2048]{1,0:T(8,128)(2,1)} collective-permute-done((bf16[512,2048]{1,0:T(8,128)(2,1)S(1)}, bf16[512,2048]{1,0:T(8,128)(2,1)}, u32[]{:S(2)}, u32[]{:S(2)}) %collective-permute-start.3) | collective-permute-done | bytes 2097184 | tf_op jit(solution)/shard_map/ppermute | solution.py:378
  341.3 6.0 fusion.129
  349.9 54.5 %conditional.13 = (f32[2048]{0:T(1024)}, bf16[512,2048]{1,0:T(8,128)(2,1)}, bf16[512,2048]{1,0:T(8,128)(2,1)}, bf16[512,4096]{1,0:T(8,128)(2,1)}) conditional(s32[]{:T(128)} %convert_element_type.562, () %tuple.143, (bf16[2048,6144]{1,0:T(8,128)(2,1)}, bf16[512,2048]{1,0:T(8,128)(2,1)}, bf16[512,2048]{1,0:T(8,128)(2,1)S(1)}, ...), branch_computations={%region_9.10_spmd, %region_10.13_spmd} | conditional | flops 21511536640 | bytes 237025392 | solution.py:518
  349.9 9.5 fusion.4
  362.6 6.2 fusion
  368.7 10.5 %multiply_convert_fusion = (bf16[512,2048]{1,0:T(8,128)(2,1)}, bf16[512,2048]{1,0:T(8,128)(2,1)S(1)}, bf16[512,2048]{1,0:T(8,128)(2,1)S(1)}) fusion(f32[512,2048]{1,0:T(8,128)} %fusion.4, f32[512,2048]{1,0:T(8,128)} %fusion, bf16[512,2048]{1,0:T(8,128)(2,1)S(1)} %get-tuple-element.365, bf16[2048,6144]{1,0:T(8,128)(2,1)} %get-tuple-element.364), kind=kOutput, calls=%fused_computation.11 | convolution fusion | flops 4310695936 | bytes 25165824 | tf_op jit(solution)/shard_map/cond/branch_1_fun/dot_general | solution.py:24
  381.8 9.8 fusion.2
  391.6 10.3 %multiply_reduce_fusion = (f32[512]{0:T(512)S(1)}, f32[2048]{0:T(1024)}, f32[512,2048]{1,0:T(8,128)S(1)}) fusion(f32[512,2048]{1,0:T(8,128)S(1)} %copy-done.12, f32[2048]{0:T(1024)S(1)} %get-tuple-element.370, f32[512]{0:T(512)S(1)} %bitcast.487, f32[512,2048]{1,0:T(8,128)} %fusion.2, bf16[512,2048]{1,0:T(8,128)(2,1)S(1)} %get-tuple-element.1109, ...), kind=kOutput, calls=%fused_computation.13 | convolution fusion | flops 4302304768 | bytes 23089152 | tf_op jit(solution)/shard_map/cond/branch_1_fun/dot_general | solution.py:28
  404.7 32.5 %conditional.14 = (bf16[256,2048]{1,0:T(8,128)(2,1)}, bf16[256,2048]{1,0:T(8,128)(2,1)S(1)}, bf16[512,1024]{1,0:T(8,128)(2,1)}, bf16[1024,4096]{1,0:T(8,128)(2,1)}, bf16[2048,2048]{1,0:T(8,128)(2,1)}) conditional(s32[]{:T(128)} %convert_element_type.591, () %tuple.147, (bf16[2048,6144]{1,0:T(8,128)(2,1)}, bf16[512,2048]{1,0:T(8,128)(2,1)}, ...), branch_computations={%region_13.14_spmd, %region_14.15_spmd} | conditional | flops 12894339072 | bytes 55574684 | solution.py:518
  404.7 8.5 fusion.18
  414.4 3.9 pick_halves.3
  418.3 10.4 %convolution_convert_fusion.1 = bf16[1024,4096]{1,0:T(8,128)(2,1)} fusion(bf16[512,1024]{1,0:T(8,128)(2,1)} %get-tuple-element.377, bf16[512,4096]{1,0:T(8,128)(2,1)} %get-tuple-element.378), kind=kOutput, calls=%fused_computation.27 | convolution fusion | flops 4299161600 | bytes 13631488 | tf_op jit(solution)/shard_map/cond/branch_1_fun/dot_general | solution.py:32
  428.7 8.4 convolution_convert_fusion
  438.3 13.3 %collective-permute-done.4.values_ref = bf16[512,2048]{1,0:T(8,128)(2,1)} collective-permute-done((bf16[512,2048]{1,0:T(8,128)(2,1)}, bf16[512,2048]{1,0:T(8,128)(2,1)}, u32[]{:S(2)}, u32[]{:S(2)}) %collective-permute-start.4) | collective-permute-done | bytes 2097184 | tf_op jit(solution)/shard_map/ppermute | solution.py:378
  451.6 15.9 %conditional.15 = (bf16[512,2048]{1,0:T(8,128)(2,1)}, bf16[1,2,2,128,2048]{4,3,2,1,0:T(8,128)(2,1)}, bf16[512,2048]{1,0:T(8,128)(2,1)}, bf16[2,1,2,128,2048]{4,3,2,1,0:T(8,128)(2,1)}) conditional(s32[]{:T(128)} %convert_element_type.592, () %tuple.150, (bf16[512,1024]{1,0:T(8,128)(2,1)}, bf16[512,4096]{1,0:T(8,128)(2,1)}, ...), branch_computations={%region_15.16_spmd, %region_16.17_spmd} | conditional | flops 4307550208 | bytes 38797344 | solution.py:518
  451.6 10.8 %add_convert_fusion = bf16[1024,4096]{1,0:T(8,128)(2,1)S(1)} fusion(bf16[1024,4096]{1,0:T(8,128)(2,1)} %get-tuple-element.382, bf16[512,1024]{1,0:T(8,128)(2,1)} %get-tuple-element.380, bf16[512,4096]{1,0:T(8,128)(2,1)} %get-tuple-element.381), kind=kOutput, calls=%fused_computation.31 | convolution fusion | flops 4307550208 | bytes 22020096 | tf_op jit(solution)/shard_map/cond/branch_1_fun/dot_general | solution.py:32
  467.7 13.5 %collective-permute-start.7 = (bf16[512,2048]{1,0:T(8,128)(2,1)}, bf16[512,2048]{1,0:T(8,128)(2,1)}, u32[]{:S(2)}, u32[]{:S(2)}) collective-permute-start(bf16[512,2048]{1,0:T(8,128)(2,1)} %get-tuple-element.677), channel_id=1, source_target_pairs={{0,8},{2,10},{4,12},{6,14},{8,0},{10,2},{12,4},{14,6},{16,24},{18,... | collective-permute-start | bytes 6291464 | tf_op jit(solution)/shard_map/ppermute | solution.py:381
  487.4 38.2 %conditional.16 = (f32[512]{0:T(512)S(1)}, f32[256,2048]{1,0:T(8,128)}, f32[512,1536]{1,0:T(8,128)}, bf16[512,1024]{1,0:T(8,128)(2,1)}, bf16[512,1024]{1,0:T(8,1...) conditional(s32[]{:T(128)} %convert_element_type.593, ...), branch_computations={%region_17.18_spmd, %region_18.21_spmd} | conditional | flops 4854543872 | bytes 110780848 | solution.py:518
  487.6 6.2 fusion.127
  507.5 8.8 multiply_reduce_fusion.2
  517.6 6.3 pick_halves.4
  525.7 34.3 %collective-permute-done.7 = bf16[512,2048]{1,0:T(8,128)(2,1)} collective-permute-done((bf16[512,2048]{1,0:T(8,128)(2,1)}, bf16[512,2048]{1,0:T(8,128)(2,1)}, u32[]{:S(2)}, u32[]{:S(2)}) %collective-permute-start.7) | collective-permute-done | bytes 2097184 | tf_op jit(solution)/shard_map/ppermute | solution.py:381
  560.1 15.7 %conditional.17 = (bf16[1024,2048]{1,0:T(8,128)(2,1)}, bf16[256,2048]{1,0:T(8,128)(2,1)}, bf16[1,1,2,128,2048]{4,3,2,1,0:T(8,128)(2,1)}, bf16[256,2048]{1,0:T(8,128)(2,1)}, bf16[1,1,2,128,2048]{4,3,2,1,0:T(8,128)(2,1)}) conditional(s32[]{:T(128)} %convert_element_type.594, () %tuple.157, (bf16[512,1024]{1,0:T(8,128)(2,1)}, ...), branch_computations={%region_21.22_spmd, %region_22.23_spmd} | conditional | flops 2157969408 | bytes 28311592 | solution.py:518
  569.2 6.6 convolution_convert_fusion.2
  582.0 58.4 %conditional.18 = (f32[1536]{0:T(1024)}, f32[24]{0:T(128)}, f32[24]{0:T(128)}, f32[24]{0:T(128)}, bf16[512,4480]{1,0:T(8,128)(2,1)}, /*index=5*/f32[2560]{0:T(1024)}, f32[7680]{0:T(1024)}) conditional(s32[]{:T(128)} %convert_element_type.595, () %tuple.160, (f32[1536]{0:T(1024)S(1)}, f32[512]{0:T(512)S(1)}, f32[512]{0:T(512)S(1)}, ...), branch_computations={%region_23.24_spmd, %region_24.34_spmd} | conditional | flops 4074679296 | bytes 70610784 | solution.py:518
  586.7 30.2 %state_backward.1 = (bf16[512,1536]{1,0:T(8,128)(2,1)}, bf16[512,1536]{1,0:T(8,128)(2,1)}, f32[2,8,1536]{2,1,0:T(8,128)}, f32[2,12,2,256]{3,2,1,0:T(2,128)}, f32...) custom-call(f32[512,1536]{1,0:T(8,128)} %get-tuple-element.409.grad_ref, f32[512,1536]{1,0:T(8,128)} %get-tuple-element.410.out_ref, ...), custom_call_target="tpu_custom_call" | custom-call | flops 4026531840 | bytes 15728640 | tf_op jit(solution)/shard_map/cond/branch_1_fun/state_backward/pallas_call | solution.py:309
  640.5 24.4 %conditional.19 = (bf16[1024,4480]{1,0:T(8,128)(2,1)}, bf16[512,2048]{1,0:T(8,128)(2,1)}, bf16[1,2,2,128,2048]{4,3,2,1,0:T(8,128)(2,1)}, bf16[256,2048]{1,0:T(8,...) conditional(s32[]{:T(128)} %convert_element_type.597, ...), branch_computations={%region_35.36_spmd, %region_36.37_spmd} | conditional | flops 6860439552 | bytes 59375772 | solution.py:518
  645.8 5.5 add_convert_fusion.3
  653.9 10.0 convolution_convert_fusion.3
  670.8 45.0 %conditional.20 = (f32[2048]{0:T(1024)S(1)}, bf16[256,2048]{1,0:T(8,128)(2,1)}, bf16[256,2048]{1,0:T(8,128)(2,1)S(1)}) conditional(s32[]{:T(128)} %convert_element_type.598, () %tuple.166, (bf16[512,4480]{1,0:T(8,128)(2,1)}, bf16[2048,6528]{1,0:T(8,128)(2,1)}, f32[512,2048]{1,0:T(8,128)}, f32[2,2,128]{2,1,0:T(2,128)S(1)}, f32[512,1]{0,1:T(1,128)S(1)}, ...), branch_computations={%region_37.38_spmd, %region_38.41_spmd} | conditional | flops 9413066752 | bytes 113162384 | solution.py:518
  670.8 8.8 fusion.45
  679.6 8.8 fusion.47
  694.6 3.8 fusion.56
  698.3 4.0 fusion.59
  702.3 8.6 multiply_reduce_fusion.3
  716.2 28.0 %conditional.21 = (bf16[512,2176]{1,0:T(8,128)(2,1)}, bf16[1,2,2,128,2176]{4,3,2,1,0:T(8,128)(2,1)}, bf16[512,2304]{1,0:T(8,128)(2,1)}, bf16[2,1,2,128,2304]{4,3...) conditional(s32[]{:T(128)} %convert_element_type.599, ...), branch_computations={%region_41.42_spmd, %region_42.43_spmd} | conditional | flops 4989255680 | bytes 80473128 | solution.py:518
  720.8 9.1 add_convert_fusion.4
  739.0 3.3 fusion.71
  745.2 4.5 all-to-all-start.3
  756.8 45.7 %collective-permute-done.21 = f32[128,128]{1,0:T(8,128)} collective-permute-done((f32[128,128]{1,0:T(8,128)}, f32[128,128]{1,0:T(8,128)}, u32[]{:S(2)}, u32[]{:S(2)}) %collective-permute-start.21) | collective-permute-done | bytes 65568 | tf_op jit(solution)/shard_map/ppermute | solution.py:381
  802.5 35.1 %collective-permute-done.18 = bf16[256,2048]{1,0:T(8,128)(2,1)} collective-permute-done((bf16[256,2048]{1,0:T(8,128)(2,1)}, bf16[256,2048]{1,0:T(8,128)(2,1)}, u32[]{:S(2)}, u32[]{:S(2)}) %collective-permute-start.18) | collective-permute-done | bytes 1048608 | tf_op jit(solution)/shard_map/ppermute | solution.py:381
  837.6 15.6 %conditional.23 = (bf16[128,2048]{1,0:T(8,128)(2,1)}, bf16[1,1,1,128,2048]{4,3,2,1,0:T(8,128)(2,1)}, bf16[256,2176]{1,0:T(8,128)(2,1)}, bf16[1,1,2,128,2176]{4,3...) conditional(s32[]{:T(128)} %convert_element_type.602, ...), branch_computations={%region_45.46_spmd, %region_46.47_spmd} | conditional | flops 282869760 | bytes 34013276 | solution.py:518
  847.7 4.0 fusion.75
  855.5 4.3 all-to-all-start.2
  866.1 50.1 %collective-permute-done.25 = f32[128,128]{1,0:T(8,128)S(1)} collective-permute-done((f32[128,128]{1,0:T(8,128)}, f32[128,128]{1,0:T(8,128)S(1)}, u32[]{:S(2)}, u32[]{:S(2)}) %collective-permute-start.25) | collective-permute-done | bytes 65568 | tf_op jit(solution)/shard_map/ppermute | solution.py:381
  916.2 7.8 conditional.24
  929.7 49.8 %collective-permute-done.29 = f32[128,128]{1,0:T(8,128)S(1)} collective-permute-done((f32[128,128]{1,0:T(8,128)S(1)}, f32[128,128]{1,0:T(8,128)S(1)}, u32[]{:S(2)}, u32[]{:S(2)}) %collective-permute-start.29) | collective-permute-done | bytes 65568 | tf_op jit(solution)/shard_map/ppermute | solution.py:381
  979.5 12.5 %conditional.25 = (f32[128,2176]{1,0:T(8,128)}, f32[128,2304]{1,0:T(8,128)S(1)}, f32[128,128]{1,0:T(8,128)S(1)}, bf16[2,128,2048]{2,1,0:T(8,128)(2,1)S(1)}, bf16...) conditional(s32[]{:T(128)} %convert_element_type.604, ...), branch_computations={%region_49.50_spmd, %region_50.51_spmd} | conditional | flops 539656192 | bytes 26067144 | solution.py:518
  (561 shorter events, 261.2 us)
Async XLA Ops:
  7.2 181.6 %all-gather.5.cloned.1.call-start = ((), (), s32[]{:S(2)}) async-start(), calls=%async_computation.6 | async-start | bytes 28409856 | tf_op jit(solution)/shard_map/all_gather | solution.py:395
  15.9 333.3 %all-gather.3.cloned.1.call-start = ((), (), s32[]{:S(2)}) async-start(), calls=%async_computation.5 | async-start | bytes 26738688 | tf_op jit(solution)/shard_map/all_gather | solution.py:395
  23.9 92.2 %copy-start.107 = (s32[256]{0:T(256)}, s32[256]{0:T(256)S(1)}, u32[]{:S(2)}) copy-start(s32[256]{0:T(256)S(1)} %get-tuple-element.1210) | copy-start | bytes 3076
  25.3 47.3 %all-to-all-start = ((bf16[16,16,2048]{2,1,0:T(8,128)(2,1)}), bf16[16,16,2048]{2,1,0:T(8,128)(2,1)S(1)}, u32[]{:S(2)}, u32[]{:S(2)}) async-start(bf16[16,16,2048]{2,1,0:T(8,128)(2,1)} %bitcast.124), calls=%async_computation | async-start | bytes 2097152 | tf_op jit(solution)/shard_map/all_to_all | solution.py:426
  33.3 47.3 %copy-start.128 = (f32[24]{0:T(128)S(1)}, f32[24]{0:T(128)}, u32[]{:S(2)}) copy-start(f32[24]{0:T(128)} %param.74) | copy-start | bytes 292
  33.3 47.4 %copy-start.132 = (s32[16]{0:T(128)S(1)}, s32[16]{0:T(128)}, u32[]{:S(2)}) copy-start(s32[16]{0:T(128)} %constant.256.clone) | copy-start | bytes 196
  33.3 47.9 %copy-start.88 = (f32[5,512]{1,0:T(8,128)S(1)}, f32[5,512]{1,0:T(8,128)}, u32[]{:S(2)}) copy-start(f32[5,512]{1,0:T(8,128)} %param.70) | copy-start | bytes 30724
  72.6 43.5 %all-to-all-start.1 = ((bf16[16,16,2048]{2,1,0:T(8,128)(2,1)}), bf16[16,16,2048]{2,1,0:T(8,128)(2,1)S(1)}, u32[]{:S(2)}, u32[]{:S(2)}) async-start(bf16[16,16,2048]{2,1,0:T(8,128)(2,1)} %bitcast.130), calls=%async_computation.1 | async-start | bytes 2097152 | tf_op jit(solution)/shard_map/all_to_all | solution.py:426
  76.2 564.2 %reduce-scatter.2.cloned.1.call-start = ((), (), s32[]{:S(2)}) async-start(), calls=%async_computation.7 | async-start | bytes 8912896 | tf_op jit(solution)/shard_map/reduce_scatter | solution.py:613
  76.4 40.1 %copy-start.96 = (f32[1,2,2,128]{3,1,2,0:T(2,128)}, f32[1,2,2,128]{3,1,2,0:T(2,128)S(1)}, u32[]{:S(2)}) copy-start(f32[1,2,2,128]{3,1,2,0:T(2,128)S(1)} %copy.241) | copy-start | bytes 6148
  80.7 153.2 %copy-start.78 = (f32[1,1536]{1,0:T(1,128)}, f32[1,1536]{1,0:T(1,128)S(1)}, u32[]{:S(2)}) copy-start(f32[1,1536]{1,0:T(1,128)S(1)} %broadcast_in_dim_reshape.2.skip_ref) | copy-start | bytes 18436
  82.3 36.9 %collective-permute-start = (bf16[256,2048]{1,0:T(8,128)(2,1)S(1)}, bf16[256,2048]{1,0:T(8,128)(2,1)S(1)}, u32[]{:S(2)}, u32[]{:S(2)}) collective-permute-start(bf16[256,2048]{1,0:T(8,128)(2,1)S(1)} %convolution_convert_fusion.10), channel_id=1, source_target_pairs={{0,1},{1,0},{2,3},{3,2},{4,5},{5,4},{6,7},{7,6},{8,9},{9,8},{10,11... | collective-permute-start | bytes 3145736 | tf_op jit(solution)/shard_map/ppermute | solution.py:378
  116.5 24.7 %collective-permute-start.1 = (bf16[256,2048]{1,0:T(8,128)(2,1)S(1)}, bf16[256,2048]{1,0:T(8,128)(2,1)S(1)}, u32[]{:S(2)}, u32[]{:S(2)}) collective-permute-start(bf16[256,2048]{1,0:T(8,128)(2,1)S(1)} %convolution_convert_fusion.8), channel_id=1, source_target_pairs={{0,1},{1,0},{2,3},{3,2},{4,5},{5,4},{6,7},{7,6},{8,9},{9,8},{10,11... | collective-permute-start | bytes 3145736 | tf_op jit(solution)/shard_map/ppermute | solution.py:378
  153.2 35.7 %copy-start.6 = (bf16[512,2048]{1,0:T(8,128)(2,1)S(1)}, bf16[512,2048]{1,0:T(8,128)(2,1)}, u32[]{:S(2)}) copy-start(bf16[512,2048]{1,0:T(8,128)(2,1)} %multiply_convert_fusion.5.first_ref.second_ref) | copy-start | bytes 6291460
  156.5 34.8 %copy-start.123 = (f32[24]{0:T(128)S(1)}, f32[24]{0:T(128)}, u32[]{:S(2)}) copy-start(f32[24]{0:T(128)} %exponential_negate_fusion) | copy-start | bytes 292
  210.8 61.6 %copy-start.45 = (bf16[512,1,64]{2,0,1:T(8,128)(2,1)}, bf16[512,1,64]{2,0,1:T(8,128)(2,1)S(1)}, u32[]{:S(2)}) copy-start(bf16[512,1,64]{2,0,1:T(8,128)(2,1)S(1)} %copy.229) | copy-start | bytes 196612
  210.9 61.5 %copy-start.47 = (bf16[512,1,64]{2,0,1:T(8,128)(2,1)}, bf16[512,1,64]{2,0,1:T(8,128)(2,1)S(1)}, u32[]{:S(2)}) copy-start(bf16[512,1,64]{2,0,1:T(8,128)(2,1)S(1)} %copy.230) | copy-start | bytes 196612
  234.0 38.5 %copy-start.40 = (bf16[2,256,4,64]{3,1,2,0:T(8,128)(2,1)S(1)}, bf16[2,256,4,64]{3,1,2,0:T(8,128)(2,1)}, u32[]{:S(2)}) copy-start(bf16[2,256,4,64]{3,1,2,0:T(8,128)(2,1)} %copy.199) | copy-start | bytes 786436
  270.9 8.5 collective-permute-start.2
  293.5 47.8 %collective-permute-start.3 = (bf16[512,2048]{1,0:T(8,128)(2,1)S(1)}, bf16[512,2048]{1,0:T(8,128)(2,1)}, u32[]{:S(2)}, u32[]{:S(2)}) collective-permute-start(bf16[512,2048]{1,0:T(8,128)(2,1)S(1)} %add_convert_fusion.9), channel_id=1, source_target_pairs={{0,1},{1,0},{2,3},{3,2},{4,5},{5,4},{6,7},{7,6},{8,9},{9,8},{10,11... | collective-permute-start | bytes 6291464 | tf_op jit(solution)/shard_map/ppermute | solution.py:378
  295.7 52.9 %copy-start.87 = (f32[2048]{0:T(1024)S(1)}, f32[2048]{0:T(1024)}, u32[]{:S(2)}) copy-start(f32[2048]{0:T(1024)} %param.68) | copy-start | bytes 24580
  349.3 55.4 %copy-start.118 = (s32[16]{0:T(128)S(1)}, s32[16]{0:T(128)}, u32[]{:S(2)}) copy-start(s32[16]{0:T(128)} %broadcast_xor_fusion.order_ref) | copy-start | bytes 196
  404.4 47.2 %collective-permute-start.4 = (bf16[512,2048]{1,0:T(8,128)(2,1)}, bf16[512,2048]{1,0:T(8,128)(2,1)}, u32[]{:S(2)}, u32[]{:S(2)}) collective-permute-start(bf16[512,2048]{1,0:T(8,128)(2,1)} %get-tuple-element.664), channel_id=1, source_target_pairs={{0,1},{1,0},{2,3},{3,2},{4,5},{5,4},{6,7},{7,6},{8,9},{9,8},{10,11... | collective-permute-start | bytes 6291464 | tf_op jit(solution)/shard_map/ppermute | solution.py:378
  437.3 14.3 %collective-permute-start.5 = (bf16[1024,4096]{1,0:T(8,128)(2,1)}, bf16[1024,4096]{1,0:T(8,128)(2,1)}, u32[]{:S(2)}, u32[]{:S(2)}) collective-permute-start(bf16[1024,4096]{1,0:T(8,128)(2,1)} %get-tuple-element.665), channel_id=1, source_target_pairs={{0,2},{2,0},{4,6},{6,4},{8,10},{10,8},{12,14},{14,12},{16,18},{18,... | collective-permute-start | bytes 25165832 | tf_op jit(solution)/shard_map/ppermute | solution.py:381
  451.6 29.6 %copy-start.38 = (bf16[512,4,64]{0,2,1:T(8,128)(2,1)S(1)}, bf16[512,4,64]{0,2,1:T(8,128)(2,1)}, u32[]{:S(2)}) copy-start(bf16[512,4,64]{0,2,1:T(8,128)(2,1)} %copy-done.37) | copy-start | bytes 786436
  451.6 30.4 %copy-start.36 = (bf16[512,4,64]{0,2,1:T(8,128)(2,1)S(1)}, bf16[512,4,64]{0,2,1:T(8,128)(2,1)}, u32[]{:S(2)}) copy-start(bf16[512,4,64]{0,2,1:T(8,128)(2,1)} %copy-done.35) | copy-start | bytes 786436
  451.6 31.1 %copy-start.25 = (bf16[2,256,1,4,128]{4,3,1,0,2:T(4,128)(2,1)S(1)}, bf16[2,256,1,4,128]{4,3,1,0,2:T(4,128)(2,1)}, u32[]{:S(2)}) copy-start(bf16[2,256,1,4,128]{4,3,1,0,2:T(4,128)(2,1)} %copy.203) | copy-start | bytes 1572868
  467.5 58.2 %collective-permute-start.6 = (bf16[512,2048]{1,0:T(8,128)(2,1)}, bf16[512,2048]{1,0:T(8,128)(2,1)}, u32[]{:S(2)}, u32[]{:S(2)}) collective-permute-start(bf16[512,2048]{1,0:T(8,128)(2,1)} %get-tuple-element.675), channel_id=1, source_target_pairs={{0,4},{2,6},{4,0},{6,2},{8,12},{10,14},{12,8},{14,10},{16,20},{18,... | collective-permute-start | bytes 6291464 | tf_op jit(solution)/shard_map/ppermute | solution.py:381
  467.7 92.2 %collective-permute-start.7 = (bf16[512,2048]{1,0:T(8,128)(2,1)}, bf16[512,2048]{1,0:T(8,128)(2,1)}, u32[]{:S(2)}, u32[]{:S(2)}) collective-permute-start(bf16[512,2048]{1,0:T(8,128)(2,1)} %get-tuple-element.677), channel_id=1, source_target_pairs={{0,8},{2,10},{4,12},{6,14},{8,0},{10,2},{12,4},{14,6},{16,24},{18,... | collective-permute-start | bytes 6291464 | tf_op jit(solution)/shard_map/ppermute | solution.py:381
  525.6 34.4 %copy-start.115 = (f32[512]{0:T(512)}, f32[512]{0:T(512)S(1)}, u32[]{:S(2)}) copy-start(f32[512]{0:T(512)S(1)} %get-tuple-element.680) | copy-start | bytes 6148
  559.9 21.9 %copy-start.23 = (bf16[512,512]{1,0:T(8,128)(2,1)S(1)}, bf16[512,512]{1,0:T(8,128)(2,1)}, u32[]{:S(2)}) copy-start(bf16[512,512]{1,0:T(8,128)(2,1)} %multiply_convert_fusion.7.state_ref) | copy-start | bytes 1572868
  575.8 64.6 %collective-permute-start.9 = (bf16[1024,2048]{1,0:T(8,128)(2,1)}, bf16[1024,2048]{1,0:T(8,128)(2,1)}, u32[]{:S(2)}, u32[]{:S(2)}) collective-permute-start(bf16[1024,2048]{1,0:T(8,128)(2,1)} %get-tuple-element.689), channel_id=1, source_target_pairs={{0,2},{2,0},{4,6},{6,4},{8,10},{10,8},{12,14},{14,12},{16,18},{18,... | collective-permute-start | bytes 12582920 | tf_op jit(solution)/shard_map/ppermute | solution.py:381
  575.8 64.6 %collective-permute-start.10 = (bf16[256,2048]{1,0:T(8,128)(2,1)}, bf16[256,2048]{1,0:T(8,128)(2,1)}, u32[]{:S(2)}, u32[]{:S(2)}) collective-permute-start(bf16[256,2048]{1,0:T(8,128)(2,1)} %get-tuple-element.692), channel_id=1, source_target_pairs={{0,8},{2,10},{4,12},{6,14},{8,0},{10,2},{12,4},{14,6},{16,24},{18,... | collective-permute-start | bytes 3145736 | tf_op jit(solution)/shard_map/ppermute | solution.py:381
  577.5 62.9 %collective-permute-start.11 = (bf16[256,2048]{1,0:T(8,128)(2,1)}, bf16[256,2048]{1,0:T(8,128)(2,1)}, u32[]{:S(2)}, u32[]{:S(2)}) collective-permute-start(bf16[256,2048]{1,0:T(8,128)(2,1)} %get-tuple-element.694), channel_id=1, source_target_pairs={{0,4},{2,6},{4,0},{6,2},{8,12},{10,14},{12,8},{14,10},{16,20},{18,... | collective-permute-start | bytes 3145736 | tf_op jit(solution)/shard_map/ppermute | solution.py:381
  578.3 3.6 collective-permute-start.8
  586.7 30.2 %copy-start.34 = (s32[512,1]{1,0:T(8,128)S(1)}, s32[512,1]{1,0:T(8,128)}, u32[]{:S(2)}) copy-start(s32[512,1]{1,0:T(8,128)} %copy.212.position_ref) | copy-start | bytes 6148 | tf_op jit(solution)/shard_map/cond
  640.4 30.2 %copy-start.108 = (s32[256]{0:T(256)S(1)}, s32[256]{0:T(256)}, u32[]{:S(2)}) copy-start(s32[256]{0:T(256)} %copy-done.107) | copy-start | bytes 3076
  640.4 30.3 %copy-start.75 = (f32[2048]{0:T(1024)S(1)}, f32[2048]{0:T(1024)}, u32[]{:S(2)}) copy-start(f32[2048]{0:T(1024)} %param.67) | copy-start | bytes 24580
  640.4 30.3 %copy-start.100 = (f32[2,2,128]{2,1,0:T(2,128)S(1)}, f32[2,2,128]{2,1,0:T(2,128)}, u32[]{:S(2)}) copy-start(f32[2,2,128]{2,1,0:T(2,128)} %copy-done.99) | copy-start | bytes 6148
  640.5 30.3 %copy-start.102 = (f32[512,1]{0,1:T(1,128)S(1)}, f32[512,1]{0,1:T(1,128)}, u32[]{:S(2)}) copy-start(f32[512,1]{0,1:T(1,128)} %copy-done.101) | copy-start | bytes 6148
  640.5 30.3 %copy-start.104 = (f32[512,1]{0,1:T(1,128)S(1)}, f32[512,1]{0,1:T(1,128)}, u32[]{:S(2)}) copy-start(f32[512,1]{0,1:T(1,128)} %copy-done.103) | copy-start | bytes 6148
  664.9 51.2 %collective-permute-start.12 = (bf16[1024,4480]{1,0:T(8,128)(2,1)}, bf16[1024,4480]{1,0:T(8,128)(2,1)}, u32[]{:S(2)}, u32[]{:S(2)}) collective-permute-start(bf16[1024,4480]{1,0:T(8,128)(2,1)} %get-tuple-element.700), channel_id=1, source_target_pairs={{0,2},{2,0},{4,6},{6,4},{8,10},{10,8},{12,14},{14,12},{16,18},{18,... | collective-permute-start | bytes 27525128 | tf_op jit(solution)/shard_map/ppermute | solution.py:381
  664.9 51.2 %collective-permute-start.16 = (bf16[512,2048]{1,0:T(8,128)(2,1)}, bf16[512,2048]{1,0:T(8,128)(2,1)}, u32[]{:S(2)}, u32[]{:S(2)}) collective-permute-start(bf16[512,2048]{1,0:T(8,128)(2,1)} %get-tuple-element.717), channel_id=1, source_target_pairs={{0,4},{2,6},{4,0},{6,2},{8,12},{10,14},{12,8},{14,10},{16,20},{18,... | collective-permute-start | bytes 6291464 | tf_op jit(solution)/shard_map/ppermute | solution.py:381
  666.2 49.9 %collective-permute-start.13 = (bf16[256,2048]{1,0:T(8,128)(2,1)}, bf16[256,2048]{1,0:T(8,128)(2,1)}, u32[]{:S(2)}, u32[]{:S(2)}) collective-permute-start(bf16[256,2048]{1,0:T(8,128)(2,1)} %get-tuple-element.711), channel_id=1, source_target_pairs={{0,1},{1,0},{2,3},{3,2},{4,5},{5,4},{6,7},{7,6},{8,9},{9,8},{10,11... | collective-permute-start | bytes 3145736 | tf_op jit(solution)/shard_map/ppermute | solution.py:378
  667.7 48.1 %collective-permute-start.14 = (bf16[128,2048]{1,0:T(8,128)(2,1)}, bf16[128,2048]{1,0:T(8,128)(2,1)}, u32[]{:S(2)}, u32[]{:S(2)}) collective-permute-start(bf16[128,2048]{1,0:T(8,128)(2,1)} %get-tuple-element.713), channel_id=1, source_target_pairs={{0,16},{2,18},{4,20},{6,22},{8,24},{10,26},{12,28},{14,30},{16,0},... | collective-permute-start | bytes 1572872 | tf_op jit(solution)/shard_map/ppermute | solution.py:381
  667.7 48.4 %collective-permute-start.15 = (bf16[128,2048]{1,0:T(8,128)(2,1)}, bf16[128,2048]{1,0:T(8,128)(2,1)}, u32[]{:S(2)}, u32[]{:S(2)}) collective-permute-start(bf16[128,2048]{1,0:T(8,128)(2,1)} %get-tuple-element.715), channel_id=1, source_target_pairs={{0,16},{2,18},{4,20},{6,22},{8,24},{10,26},{12,28},{14,30},{16,0},... | collective-permute-start | bytes 1572872 | tf_op jit(solution)/shard_map/ppermute | solution.py:381
  670.8 45.4 %copy-start.8 = (bf16[512,2048]{1,0:T(8,128)(2,1)S(1)}, bf16[512,2048]{1,0:T(8,128)(2,1)}, u32[]{:S(2)}) copy-start(bf16[512,2048]{1,0:T(8,128)(2,1)} %copy-done.7) | copy-start | bytes 6291460
  744.8 92.8 %collective-permute-start.20 = (bf16[512,2304]{1,0:T(8,128)(2,1)}, bf16[512,2304]{1,0:T(8,128)(2,1)S(1)}, u32[]{:S(2)}, u32[]{:S(2)}) collective-permute-start(bf16[512,2304]{1,0:T(8,128)(2,1)} %get-tuple-element.727), channel_id=1, source_target_pairs={{0,8},{2,10},{4,12},{6,14},{8,0},{10,2},{12,4},{14,6},{16,24},{18,... | collective-permute-start | bytes 7077896 | tf_op jit(solution)/shard_map/ppermute | solution.py:381
  744.8 92.8 %collective-permute-start.19 = (bf16[512,2176]{1,0:T(8,128)(2,1)}, bf16[512,2176]{1,0:T(8,128)(2,1)}, u32[]{:S(2)}, u32[]{:S(2)}) collective-permute-start(bf16[512,2176]{1,0:T(8,128)(2,1)} %get-tuple-element.725), channel_id=1, source_target_pairs={{0,4},{2,6},{4,0},{6,2},{8,12},{10,14},{12,8},{14,10},{16,20},{18,... | collective-permute-start | bytes 6684680 | tf_op jit(solution)/shard_map/ppermute | solution.py:381
  745.2 110.3 %all-to-all-start.3 = ((bf16[16,16,2048]{2,1,0:T(8,128)(2,1)}), bf16[16,16,2048]{2,1,0:T(8,128)(2,1)}, u32[]{:S(2)}, u32[]{:S(2)}) async-start(bf16[16,16,2048]{2,1,0:T(8,128)(2,1)} %bitcast.166), calls=%async_computation.4 | async-start | bytes 2097152 | tf_op jit(solution)/shard_map/all_to_all | solution.py:426
  749.7 87.9 %collective-permute-start.18 = (bf16[256,2048]{1,0:T(8,128)(2,1)}, bf16[256,2048]{1,0:T(8,128)(2,1)}, u32[]{:S(2)}, u32[]{:S(2)}) collective-permute-start(bf16[256,2048]{1,0:T(8,128)(2,1)} %get-tuple-element.723), channel_id=1, source_target_pairs={{0,8},{2,10},{4,12},{6,14},{8,0},{10,2},{12,4},{14,6},{16,24},{18,... | collective-permute-start | bytes 3145736 | tf_op jit(solution)/shard_map/ppermute | solution.py:381
  751.6 86.0 %collective-permute-start.22 = (bf16[256,2048]{1,0:T(8,128)(2,1)}, bf16[256,2048]{1,0:T(8,128)(2,1)}, u32[]{:S(2)}, u32[]{:S(2)}) collective-permute-start(bf16[256,2048]{1,0:T(8,128)(2,1)} %get-tuple-element.730), channel_id=1, source_target_pairs={{0,1},{1,0},{2,3},{3,2},{4,5},{5,4},{6,7},{7,6},{8,9},{9,8},{10,11... | collective-permute-start | bytes 3145736 | tf_op jit(solution)/shard_map/ppermute | solution.py:378
  752.2 1.6 collective-permute-start.17
  755.3 47.2 %collective-permute-start.21 = (f32[128,128]{1,0:T(8,128)}, f32[128,128]{1,0:T(8,128)}, u32[]{:S(2)}, u32[]{:S(2)}) collective-permute-start(f32[128,128]{1,0:T(8,128)} %get-tuple-element.1384), channel_id=1, source_target_pairs={{0,4},{2,6},{4,0},{6,2},{8,12},{10,14},{12,8},{14,10},{16,20},{18,... | collective-permute-start | bytes 196616 | tf_op jit(solution)/shard_map/ppermute | solution.py:381
  855.5 124.0 %all-to-all-start.2 = ((bf16[16,16,2048]{2,1,0:T(8,128)(2,1)}), bf16[16,16,2048]{2,1,0:T(8,128)(2,1)}, u32[]{:S(2)}, u32[]{:S(2)}) async-start(bf16[16,16,2048]{2,1,0:T(8,128)(2,1)} %bitcast.165), calls=%async_computation.3 | async-start | bytes 2097152 | tf_op jit(solution)/shard_map/all_to_all | solution.py:426
  859.9 56.3 %collective-permute-start.24 = (bf16[256,2304]{1,0:T(8,128)(2,1)}, bf16[256,2304]{1,0:T(8,128)(2,1)}, u32[]{:S(2)}, u32[]{:S(2)}) collective-permute-start(bf16[256,2304]{1,0:T(8,128)(2,1)} %get-tuple-element.737), channel_id=1, source_target_pairs={{0,4},{2,6},{4,0},{6,2},{8,12},{10,14},{12,8},{14,10},{16,20},{18,... | collective-permute-start | bytes 3538952 | tf_op jit(solution)/shard_map/ppermute | solution.py:381
  861.6 54.6 %collective-permute-start.23 = (bf16[256,2176]{1,0:T(8,128)(2,1)}, bf16[256,2176]{1,0:T(8,128)(2,1)}, u32[]{:S(2)}, u32[]{:S(2)}) collective-permute-start(bf16[256,2176]{1,0:T(8,128)(2,1)} %get-tuple-element.735), channel_id=1, source_target_pairs={{0,8},{2,10},{4,12},{6,14},{8,0},{10,2},{12,4},{14,6},{16,24},{18,... | collective-permute-start | bytes 3342344 | tf_op jit(solution)/shard_map/ppermute | solution.py:381
  863.1 53.1 %collective-permute-start.26 = (bf16[128,2048]{1,0:T(8,128)(2,1)}, bf16[128,2048]{1,0:T(8,128)(2,1)S(1)}, u32[]{:S(2)}, u32[]{:S(2)}) collective-permute-start(bf16[128,2048]{1,0:T(8,128)(2,1)} %get-tuple-element.740), channel_id=1, source_target_pairs={{0,16},{2,18},{4,20},{6,22},{8,24},{10,26},{12,28},{14,30},{16,0},... | collective-permute-start | bytes 1572872 | tf_op jit(solution)/shard_map/ppermute | solution.py:381
  865.5 50.7 %collective-permute-start.25 = (f32[128,128]{1,0:T(8,128)}, f32[128,128]{1,0:T(8,128)S(1)}, u32[]{:S(2)}, u32[]{:S(2)}) collective-permute-start(f32[128,128]{1,0:T(8,128)} %get-tuple-element.738), channel_id=1, source_target_pairs={{0,8},{2,10},{4,12},{6,14},{8,0},{10,2},{12,4},{14,6},{16,24},{18,... | collective-permute-start | bytes 196616 | tf_op jit(solution)/shard_map/ppermute | solution.py:381
  924.1 55.4 %collective-permute-start.28 = (bf16[128,2304]{1,0:T(8,128)(2,1)}, bf16[128,2304]{1,0:T(8,128)(2,1)S(1)}, u32[]{:S(2)}, u32[]{:S(2)}) collective-permute-start(bf16[128,2304]{1,0:T(8,128)(2,1)} %get-tuple-element.746), channel_id=1, source_target_pairs={{0,16},{2,18},{4,20},{6,22},{8,24},{10,26},{12,28},{14,30},{16,0},... | collective-permute-start | bytes 1769480 | tf_op jit(solution)/shard_map/ppermute | solution.py:381
  926.7 52.8 %collective-permute-start.27 = (bf16[128,2176]{1,0:T(8,128)(2,1)}, bf16[128,2176]{1,0:T(8,128)(2,1)S(1)}, u32[]{:S(2)}, u32[]{:S(2)}) collective-permute-start(bf16[128,2176]{1,0:T(8,128)(2,1)} %get-tuple-element.744), channel_id=1, source_target_pairs={{0,16},{2,18},{4,20},{6,22},{8,24},{10,26},{12,28},{14,30},{16,0},... | collective-permute-start | bytes 1671176 | tf_op jit(solution)/shard_map/ppermute | solution.py:381
  927.1 52.4 %collective-permute-start.29 = (f32[128,128]{1,0:T(8,128)S(1)}, f32[128,128]{1,0:T(8,128)S(1)}, u32[]{:S(2)}, u32[]{:S(2)}) collective-permute-start(f32[128,128]{1,0:T(8,128)S(1)} %get-tuple-element.747), channel_id=1, source_target_pairs={{0,16},{2,18},{4,20},{6,22},{8,24},{10,26},{12,28},{14,30},{16,0},... | collective-permute-start | bytes 196616 | tf_op jit(solution)/shard_map/ppermute | solution.py:381
  992.0 5.6 collective-permute-start.31
  994.3 7.7 collective-permute-start.30
  (108 other events, 772.8 us)
Sparse Core Ops, SparseCore 0:
  16.0 172.8 all-gather.4
  190.5 138.4 all-gather.2
  437.5 159.5 reduce-scatter.1

commit v5 on v4

--- a/solution.py
+++ b/solution.py
@@ -160,6 +160,18 @@
     return summed, moved
 
 
+def conv_block_back(grad_sum, signal, moved, taps_ref, position, sums_ref):
+    rows = signal.shape[0]
+    grad_signal = grad_sum * taps_ref[0:1, :]
+    sums_ref[0, 0:1, :] = jnp.sum(grad_sum * signal, axis=0, keepdims=True)
+    for tap in range(1, CONV):
+        kept = jnp.where(position >= tap, grad_sum, 0.0)
+        grad_signal = grad_signal + pltpu.roll(kept, rows - tap, 0) * taps_ref[tap : tap + 1, :]
+        sums_ref[0, tap : tap + 1, :] = jnp.sum(grad_sum * moved[tap - 1], axis=0, keepdims=True)
+    sums_ref[0, CONV : CONV + 1, :] = jnp.sum(grad_sum, axis=0, keepdims=True)
+    return grad_signal
+
+
 def mixing_block(inner, mask, run_col, run_row, step_row):
     decay = jnp.exp(run_col - run_row + mask)
     return decay, (inner * decay * step_row).astype(bf16)
@@ -200,12 +212,16 @@
 def state_backward_kernel(
     grad_ref, out_ref, gate_ref, signal_ref, taps_ref, skip_ref, gain_ref, scale_ref, cross_ref, state_ref,
     seg_col_ref, seg_row_ref, position_ref, run_row_ref, run_col_ref, step_ref,
-    gate_low_ref, input_low_ref, sums_ref, direct_ref, along_ref, state_grad_ref, inner_ref, mask_ref, grad_inner_ref,
+    state_raw_ref, state_taps_ref, step_all_ref, step_sig_ref, rate_ref,
+    gate_low_ref, input_low_ref, sums_ref, rest_low_ref, state_sums_ref, head_sums_ref,
+    inner_ref, mask_ref, grad_inner_ref, direct_ref, along_ref,
 ):
     rows = signal_ref.shape[0]
-
-    @pl.when(pl.program_id(1) == 0)
+    pair = pl.program_id(1)
+
+    @pl.when(pair == 0)
     def _():
+        along_ref[...] = jnp.zeros_like(along_ref)
         inner_ref[...] = lax.dot_general(
             state_ref[:, NS:], state_ref[:, :NS], (((1,), (1,)), ((), ())), preferred_element_type=f32
         )
@@ -244,29 +260,46 @@
         ) * decay
         stepped = grad_decay * step_row
         grad_inner_ref[...] += stepped
-        direct_ref[0, 0, head : head + 1, :] = jnp.sum(grad_decay * inner, axis=0, keepdims=True)
-        along_ref[0, 0, :, head : head + 1] = jnp.sum(stepped * inner, axis=1, keepdims=True)
+        direct_ref[pl.ds(2 * pair + head, 1), :] = jnp.sum(grad_decay * inner, axis=0, keepdims=True)
+        along = jnp.sum(stepped * inner, axis=1, keepdims=True)
+        along_ref[...] = jnp.where(lanes == 2 * pair + head, along, along_ref[...])
     grad_cols = jnp.where(lanes < SHD, grad_cols[0], grad_cols[1]) + skip_ref[...] * grad_out
     grad_sum = grad_cols * (sig * (1.0 + summed * (1.0 - sig)))
-    grad_signal = grad_sum * taps_ref[0:1, :]
-    sums_ref[0, 0:1, :] = jnp.sum(grad_sum * signal, axis=0, keepdims=True)
-    for tap in range(1, CONV):
-        kept = jnp.where(position >= tap, grad_sum, 0.0)
-        grad_signal = grad_signal + pltpu.roll(kept, rows - tap, 0) * taps_ref[tap : tap + 1, :]
-        sums_ref[0, tap : tap + 1, :] = jnp.sum(grad_sum * moved[tap - 1], axis=0, keepdims=True)
-    sums_ref[0, CONV : CONV + 1, :] = jnp.sum(grad_sum, axis=0, keepdims=True)
+    grad_signal = conv_block_back(grad_sum, signal, moved, taps_ref, position, sums_ref)
     sums_ref[0, CONV + 1 : CONV + 2, :] = jnp.sum(scaled * gated, axis=0, keepdims=True)
     sums_ref[0, CONV + 2 : CONV + 3, :] = jnp.sum(grad_out * cols, axis=0, keepdims=True)
     sums_ref[0, CONV + 3 : CONV + 4, :] = jnp.zeros((1, cols.shape[1]), f32)
     input_low_ref[...] = grad_signal.astype(bf16)
 
-    @pl.when(pl.program_id(1) == pl.num_programs(1) - 1)
+    @pl.when(pair == pl.num_programs(1) - 1)
     def _():
         inner_low = grad_inner_ref[...].astype(bf16)
-        state_grad_ref[:, :NS] = lax.dot_general(
-            inner_low, state_ref[:, NS:], (((0,), (0,)), ((), ())), preferred_element_type=f32
-        )
-        state_grad_ref[:, NS:] = jnp.dot(inner_low, state_ref[:, :NS], preferred_element_type=f32)
+        for part, (mine, other) in enumerate((((0, NS), (NS, 2 * NS)), ((NS, 2 * NS), (0, NS)))):
+            raw = state_raw_ref[:, mine[0] : mine[1]]
+            taps = state_taps_ref.at[:, mine[0] : mine[1]]
+            summed, moved = conv_block(raw, taps, position)
+            sig = sigmoid_of(summed)
+            grad = lax.dot_general(
+                inner_low, state_ref[:, other[0] : other[1]], (((part,), (0,)), ((), ())), preferred_element_type=f32
+            )
+            grad_sum = grad * (sig * (1.0 + summed * (1.0 - sig)))
+            back = conv_block_back(grad_sum, raw, moved, taps, position, state_sums_ref.at[:, :, mine[0] : mine[1]])
+            rest_low_ref[:, mine[0] : mine[1]] = back.astype(bf16)
+        state_sums_ref[0, CONV + 1 :, :] = jnp.zeros((7 - CONV, 2 * NS), f32)
+        heads = step_all_ref.shape[1]
+        direct, step = direct_ref[...], step_all_ref[0]
+        grad_running = along_ref[...].T[:heads] - step * direct
+        row_index = lax.broadcasted_iota(jnp.int32, (rows, rows), 0)
+        col_index = lax.broadcasted_iota(jnp.int32, (rows, rows), 1)
+        lower = jnp.where(col_index <= row_index, 1.0, 0.0)
+        grad_product = jnp.dot(
+            grad_running, lower, precision=lax.Precision.HIGHEST, preferred_element_type=f32
+        )
+        grad_raw = (direct + grad_product * rate_ref[...]) * step_sig_ref[0]
+        head_sums_ref[0, :, 0:1] = jnp.sum(grad_product * step, axis=1, keepdims=True)
+        head_sums_ref[0, :, 1:2] = jnp.sum(grad_raw, axis=1, keepdims=True)
+        wide = jnp.concatenate([grad_raw, jnp.zeros((STEP_PAD - heads, rows), f32)], axis=0)
+        rest_low_ref[:, 2 * NS :] = wide.T.astype(bf16)
 
 
 def state_specs(rows, pairs):
@@ -302,34 +335,48 @@
     )(signal, gate, taps, skip, state, seg_col, seg_row, position, run_row, run_col, step)
 
 
-def state_backward(grad, out, gate, signal, taps, skip, gain, scale, cross, state, seg_col, seg_row, position, run_row, run_col, step):
+def state_backward(
+    grad, out, gate, signal, taps, skip, gain, scale, cross, state, seg_col, seg_row, position, run_row, run_col, step,
+    state_raw, state_taps, step_all, step_sig, rate,
+):
     micro, pairs, _, rows = run_row.shape
+    heads = 2 * pairs
     spec = state_specs(rows, pairs)
     total, width = signal.shape
+    heads_block = pl.BlockSpec((1, heads, rows), lambda m, p: (m, 0, 0))
     return pl.pallas_call(
         state_backward_kernel,
         out_shape=(
             jax.ShapeDtypeStruct((total, width), bf16),
             jax.ShapeDtypeStruct((total, width), bf16),
             jax.ShapeDtypeStruct((micro, 8, width), f32),
-            jax.ShapeDtypeStruct(run_row.shape, f32),
-            jax.ShapeDtypeStruct(run_col.shape, f32),
-            jax.ShapeDtypeStruct((total, 2 * NS), f32),
+            jax.ShapeDtypeStruct((total, 2 * NS + STEP_PAD), bf16),
+            jax.ShapeDtypeStruct((micro, 8, 2 * NS), f32),
+            jax.ShapeDtypeStruct((micro, heads, 2), f32),
         ),
         grid=(micro, pairs),
         in_specs=[spec[name] for name in (
             "block", "block", "block", "block", "taps", "vector", "vector", "column", "column", "state",
-            "column", "row", "column", "head_row", "head_col", "head_row")],
+            "column", "row", "column", "head_row", "head_col", "head_row", "state")]
+        + [
+            pl.BlockSpec((CONV + 1, 2 * NS), lambda m, p: (0, 0)), heads_block, heads_block,
+            pl.BlockSpec((heads, 1), lambda m, p: (0, 0)),
+        ],
         out_specs=(
             spec["block"], spec["block"], pl.BlockSpec((1, 8, 2 * SHD), lambda m, p: (m, 0, p)),
-            spec["head_row"], spec["head_col"], spec["state"],
+            pl.BlockSpec((rows, 2 * NS + STEP_PAD), lambda m, p: (m, 0)),
+            pl.BlockSpec((1, 8, 2 * NS), lambda m, p: (m, 0, 0)),
+            pl.BlockSpec((1, heads, 2), lambda m, p: (m, 0, 0)),
         ),
-        scratch_shapes=[pltpu.VMEM((rows, rows), f32)] * 3,
+        scratch_shapes=[pltpu.VMEM((rows, rows), f32)] * 3 + [pltpu.VMEM((heads, rows), f32), pltpu.VMEM((rows, 2 * SHD), f32)],
         cost_estimate=pl.CostEstimate(
             flops=20 * total * rows * width, transcendentals=total * rows * width // SHD, bytes_accessed=20 * total * width
         ),
         name="state_backward",
-    )(grad, out, gate, signal, taps, skip, gain, scale, cross, state, seg_col, seg_row, position, run_row, run_col, step)
+    )(
+        grad, out, gate, signal, taps, skip, gain, scale, cross, state, seg_col, seg_row, position, run_row, run_col, step,
+        state_raw, state_taps, step_all, step_sig, rate,
+    )
 
 
 def local(
@@ -578,9 +625,7 @@
     mid32 = whole_mid.astype(f32)
     mid_scale = rms_scale(mid32)
     mid_low = (mid32 * mid_scale * gain_middle).astype(bf16)
-    red_fgate, red_fup, red_branch, red_low, red_high = [
-        Reduction(places) for places in ((1, 2), (2, 1), (1, 2), (1, 2), (2, 1))
-    ]
+    red_fgate, red_fup, red_low, red_high = [Reduction(places) for places in ((1, 2), (2, 1), (1, 2), (2, 1))]
     feeds = (red_fgate, red_fup)
     ff_cols = feed_gate.shape[1]
     gate_cols = mamba_gate.shape[1]
@@ -628,11 +673,6 @@
                 red.move(*step)
             else:
                 red.result = step
-
-    mid_other, feed_came = lax.optimization_barrier((mid_other, feed_came))
-    moves = unit(lambda: keep_first(mid_keep, feed_low, feed_came, feeds, (ff_cols, ff_cols)))
-    for red, move in zip(feeds, moves):
-        red.move(*move)
 
     def branch_backward():
         grad_middle = whole_grad.astype(f32) + (mid_part.astype(f32) + mid_other.astype(f32))
@@ -649,105 +689,95 @@
         query_grad_low = rotate_back(grad_query_rot.reshape(total, -1, HEAD), cosine, sine).astype(bf16).reshape(total, -1)
         key_grad_low = rotate_back(grad_key_rot.reshape(total, -1, HEAD), cosine, sine).astype(bf16).reshape(total, -1)
         value_grad_low = grad_value.astype(bf16).reshape(total, -1)
+        return (
+            cross_own, lane_rows(grad_middle, lane), grad_gated_norm, whole_branch,
+            (query_grad_low, key_grad_low, value_grad_low),
+        )
+
+    cross_own, grad_middle_own, grad_gated_norm, whole_branch, qkv_low = unit(branch_backward)
+    cross_other = other_lane(cross_own)
+
+    def second_moves():
+        moves = keep_first(mid_keep, feed_low, feed_came, feeds, (ff_cols, ff_cols))
         branch_right = jnp.concatenate([gated_low, attended_low], axis=1)
-        branch_left = split_left(whole_branch)
-        return (
-            cross_own, lane_rows(grad_middle, lane), grad_gated_norm, branch_left, branch_right,
-            (query_grad_low, key_grad_low, value_grad_low),
-        )
-
-    cross_own, grad_middle_own, grad_gated_norm, branch_left, branch_right, qkv_low = unit(branch_backward)
-
-    cross_other = other_lane(cross_own)
-    send_branch, steps = unit(lambda: (core_send(branch_left, branch_right), [red.step() for red in feeds]))
-    branch_came = other_group(send_branch, 1)
-    settle(feeds, steps)
+        return moves, outer_sum(whole_branch, branch_right).astype(bf16)
+
+    moves, part_branch = unit(second_moves)
+    for red, move in zip(feeds, moves):
+        red.move(*move)
+    sum_branch = lax.psum_scatter(part_branch, "dp", scatter_dimension=0, tiled=True)
 
     def state_space_backward():
         cross = (inv_rms**3) * ((cross_own + cross_other)[:, None] / inner_width)
-        gate_low, input_low, column_sums, direct, along, grad_state_act = state_backward(
-            grad_gated_norm, ssm_out, gate_z, ssm_in, kernel_inner, skip_wide, mixer_gain[None, :], inv_rms, cross, *layout
-        )
-        column_sums = jnp.sum(column_sums, axis=0)
-        grad_kernel_inner = column_sums[: CONV + 1]
-        grad_mixer = column_sums[CONV + 1]
-        grad_skip = jnp.sum(column_sums[CONV + 2].reshape(heads, SHD), axis=1)
-        grad_direct = direct.reshape(micro, heads, rows)
-        grad_running = along.transpose(0, 1, 3, 2).reshape(micro, heads, rows) - step_heads * grad_direct
-        grad_product = jnp.einsum(
-            "mhi,ij->mhj", grad_running, lower, precision=lax.Precision.HIGHEST, preferred_element_type=f32
-        )
-        grad_step = (grad_direct + grad_product * rate[None, :, None]).transpose(0, 2, 1).reshape(total, heads)
-        grad_rate = jnp.sum(grad_product * step_heads, axis=(0, 2)) * rate
-        grad_raw_step = grad_step * jax.nn.sigmoid(raw_step + step_bias)
-        grad_bias = jnp.sum(grad_raw_step, axis=0)
-        grad_state_raw, grad_kernel_state = conv_back(grad_state_act, state_raw, kernel_state, position)
-        step_low = jnp.pad(grad_raw_step.astype(bf16), ((0, 0), (0, STEP_PAD - heads)))
-        first_right = jnp.concatenate([gate_low, input_low, grad_state_raw.astype(bf16), step_low, *qkv_low], axis=1)
-        small = (grad_kernel_state, grad_kernel_inner, grad_mixer, grad_bias, grad_rate, grad_skip)
-        return small, first_right
-
-    small, first_right = unit(state_space_backward)
-    grad_kernel_state, grad_kernel_inner, grad_mixer, grad_bias, grad_rate, grad_skip = small
+        step_sig = jax.nn.sigmoid(raw_step + step_bias).reshape(micro, rows, heads).transpose(0, 2, 1)
+        gate_low, input_low, column_sums, rest_low, state_sums, head_sums = state_backward(
+            grad_gated_norm, ssm_out, gate_z, ssm_in, kernel_inner, skip_wide, mixer_gain[None, :], inv_rms, cross, *layout,
+            state_raw, kernel_state, step_heads, step_sig, rate[:, None],
+        )
+        return column_sums, state_sums, head_sums, jnp.concatenate([gate_low, input_low, rest_low, *qkv_low], axis=1)
+
+    column_sums, state_sums, head_sums, first_right = unit(state_space_backward)
 
     def third_moves():
         return (
             core_send(normed_left, first_right),
-            red_branch.first(branch_left, branch_right, branch_came),
             lax.optimization_barrier(ffn_send),
             [red.step() for red in feeds],
             sum_fdown.astype(f32),
         )
 
-    send_first, move, ffn_send, steps, total_fdown = unit(third_moves)
+    send_first, ffn_send, steps, total_fdown = unit(third_moves)
     settle(feeds, steps)
     first_came = other_group(send_first, 1)
-    red_branch.move(*move)
     ffn_other = other_lane(ffn_send)
 
     def input_gradient():
-        weights = [full(name) for name in ("gate", "input", "state", "step", "query", "key", "value")]
-        grad_normed, start = 0.0, 0
-        for weight in weights:
-            grad_normed = grad_normed + project_back(first_right[:, start : start + weight.shape[1]], weight)
-            start += weight.shape[1]
+        grad_normed = project_back(first_right, lax.slice_in_dim(whole["early"], 0, first_right.shape[1], axis=1))
         grad_gain_in = jnp.sum(grad_normed * in32 * in_scale, axis=0)
         in_part = rms_back(grad_normed, in32, in_scale, gain_input).astype(bf16)
         return grad_gain_in, lane_rows(in_part, lane), lane_rows(in_part, 1 - lane)
 
     grad_gain_in, in_own, in_send = unit(input_gradient)
 
-    shared = [grad_gain_in, grad_gain_mid, grad_kernel_state.reshape(-1)]
-    split = [grad_kernel_inner.reshape(-1), grad_mixer, grad_bias, grad_rate, grad_skip]
-    used = sum(item.shape[0] for item in shared + split)
+    small_sizes = (width, width, (CONV + 1) * 2 * NS, (CONV + 1) * inner_width // lanes, inner_width // lanes, heads, heads, heads)
+    used = sum(small_sizes)
     padded = -(-used // 1024) * 1024
     firsts = (red_low, red_high)
     first_sizes = (first_right.shape[1] // 256 * 128, first_right.shape[1] - first_right.shape[1] // 256 * 128)
 
     def first_moves():
         moves = keep_first(normed_left[0], first_right, first_came, firsts, first_sizes)
-        flat = jnp.pad(jnp.concatenate(shared + split), (0, padded - used)).reshape(padded // 128, 128)
         ffn_out = ffn_own.astype(f32) + ffn_other.astype(f32)
         out_rows = (lane_rows(whole_mid, lane).astype(f32) + ffn_out).astype(bf16)
-        return moves, lax.optimization_barrier(in_send), flat, deal_order_rows(out_rows), [red.step() for red in (*feeds, red_branch)]
-
-    moves, in_send, flat, out_sent, steps = unit(first_moves)
-    settle((*feeds, red_branch), steps)
+        return moves, lax.optimization_barrier(in_send), deal_order_rows(out_rows), [red.step() for red in feeds]
+
+    moves, in_send, out_sent, steps = unit(first_moves)
+    settle(feeds, steps)
     out_moved = exchange(out_sent)
     for red, move in zip(firsts, moves):
         red.move(*move)
     in_other = other_lane(in_send)
+
+    def small_flat():
+        columns = jnp.sum(column_sums, axis=0)
+        head_totals = jnp.sum(head_sums, axis=0)
+        parts = (
+            grad_gain_in, grad_gain_mid, jnp.sum(state_sums, axis=0)[: CONV + 1].reshape(-1), columns[: CONV + 1].reshape(-1),
+            columns[CONV + 1], head_totals[:, 1], head_totals[:, 0] * rate,
+            jnp.sum(columns[CONV + 2].reshape(heads, SHD), axis=1),
+        )
+        return jnp.pad(jnp.concatenate(parts), (0, padded - used)).reshape(padded // 128, 128)
+
+    flat = unit(small_flat)
     flat_moved = other_group(flat, masks[0])
-    flat = unit(lambda: flat + flat_moved)
-    flat_moved = other_group(flat, masks[1])
 
     def send_input():
         in_sum = in_own.astype(f32) + in_other.astype(f32)
-        return deal_order_rows((in_sum + grad_middle_own).astype(bf16))
-
-    everything = [*feeds, red_branch, *firsts]
+        return deal_order_rows((in_sum + grad_middle_own).astype(bf16)), sum_branch.astype(f32)
+
+    everything = [*feeds, *firsts]
     in_moved = None
-    bits = 2
+    bits = 1
     while pending := [red for red in everything if not hasattr(red, "result")]:
         last = all(red.stage == len(red.places) for red in pending)
         steps, flat, other = unit(
@@ -762,25 +792,28 @@
             flat_moved = other_group(flat, masks[bits])
         bits += 1
         if in_moved is None:
-            in_moved = exchange(other)
+            in_moved = exchange(other[0])
+            total_branch = other[1]
     grad_input, block_out = other
+    while bits <= len(masks):
+        flat = flat + flat_moved
+        if bits < len(masks):
+            flat_moved = other_group(flat, masks[bits])
+        bits += 1
     theirs = other_lane(flat).reshape(-1)
     flat = flat.reshape(-1)
     pieces, start = [], 0
-    for item in shared:
-        pieces.append(flat[start : start + item.shape[0]] + theirs[start : start + item.shape[0]])
-        start += item.shape[0]
-    for item in split:
-        mine, other = flat[start : start + item.shape[0]], theirs[start : start + item.shape[0]]
-        pieces.append((jnp.where(lane == 0, mine, other), jnp.where(lane == 0, other, mine)))
-        start += item.shape[0]
+    for place, size in enumerate(small_sizes):
+        mine, other = flat[start : start + size], theirs[start : start + size]
+        pieces.append(mine + other if place < 3 else (jnp.where(lane == 0, mine, other), jnp.where(lane == 0, other, mine)))
+        start += size
     sum_gin, sum_gmid, sum_kst = pieces[0], pieces[1], pieces[2].reshape(CONV + 1, -1)
     sum_kin = jnp.concatenate([half.reshape(CONV + 1, -1) for half in pieces[3]], axis=1)
     sum_mix, sum_bias, sum_rate, sum_skip = [jnp.concatenate(pair) for pair in pieces[4:]]
 
     query_cols, key_cols = query_weight.shape[1], key_weight.shape[1]
     total_fgate, total_fup = red_fgate.result, red_fup.result
-    total_mix, total_attn = red_branch.result[:, :gate_cols], red_branch.result[:, gate_cols:]
+    total_mix, total_attn = total_branch[:, :gate_cols], total_branch[:, gate_cols:]
     rest = jnp.concatenate([red.result for red in firsts], axis=1)
     total_gate, total_input, rest = rest[:, :gate_cols], rest[:, gate_cols : 2 * gate_cols], rest[:, 2 * gate_cols :]
     total_step = rest[:, 2 * NS : 2 * NS + heads]

time: 1020 us -> 947 us (0.928)
  waiting for transfers between devices: 400 us -> 360 us
  matrix products: 225 us -> 199 us
  Pallas kernels: 82.9 us -> 65.1 us
  local copies, waits for them, and re-layouts: 116 us -> 129 us
    ppermute x22 -> x18, waiting for transfers between devices: 217 us -> 127 us  [other_group(): return lax.ppermute(values, 'dp', [(i, i ^ bits) for i in range(groups)])]
    reduce_scatter x0 -> x1, waiting for transfers between devices: none -> 51.8 us  [local(): lax.psum_scatter(part_branch, 'dp', scatter_dimension=0, tiled=True)]
    dot_general x12 -> x6, matrix products: 78 us -> 56.6 us  [project_back(): lax.dot_general(left, right, (((1,), (1,)), ((), ())), preferred_element_...]
    pallas_call x1, Pallas kernels: 35.8 us -> 20.7 us  [state_forward(): pl.pallas_call(state_forward_kernel, out_shape=(jax.ShapeDtypeStruct((tot...]
    cond x2 -> x3, local copies, waits for them, and re-layouts: 3.71 us -> 15.2 us  [unit(): lax.cond(order[0], work, lambda: jax.tree.map(lambda leaf: jnp.zeros(leaf...]
    dot_general x11 -> x10, matrix products: 72 us -> 64.6 us  [outer_sum(): lax.dot_general(left, right, (((0,), (0,)), ((), ())), preferred_element_...]
    slice x14 -> x11, local copies, waits for them, and re-layouts: 23.7 us -> 18.2 us  [halve(): lax.slice_in_dim(kept, 0, 1, axis=place - 1)]
    ppermute x22 -> x18, starting transfers between devices: 36 us -> 30.5 us  [other_group(): return lax.ppermute(values, 'dp', [(i, i ^ bits) for i in range(groups)])]
  transfers between devices with their start and end apart: 39 -> 36, of which waited for: 15 -> 16; matrix products, arithmetic and copies ran while one was open for 30% -> 36% of each run, Pallas kernels for 8% -> 7%
where the time goes in v5:
time: 947 us; the launch traced here: 936 us
  waiting for transfers between devices  360 us (38%)
  matrix products  199 us (21%)
  local copies, waits for them, and re-layouts  129 us (14%)
  other arithmetic  102 us (11%)
  Pallas kernels  65.1 us (7%)
  starting transfers between devices  62.6 us (7%)
  between operations  16 us (2%)
    ppermute x18, waiting for transfers between devices, other_group(): return lax.ppermute(values, 'dp', [(i, i ^ bits) for i in range(groups)])  127 us
    ppermute x10, waiting for transfers between devices, other_lane(): return lax.ppermute(values, 'tensor', swap_lane)  75.9 us
    dot_general x16, matrix products, project(): return jnp.dot(left, right, preferred_element_type=f32)  72.1 us
    all_to_all x4, waiting for transfers between devices, exchange(): lax.all_to_all(buffer.reshape(groups, micro * per, width), 'dp', split_ax...  71.7 us
    dot_general x10, matrix products, outer_sum(): lax.dot_general(left, right, (((0,), (0,)), ((), ())), preferred_element_...  64.6 us
    dot_general x6, matrix products, project_back(): lax.dot_general(left, right, (((1,), (1,)), ((), ())), preferred_element_...  56.6 us
    reduce_scatter x1, waiting for transfers between devices, local(): lax.psum_scatter(part_branch, 'dp', scatter_dimension=0, tiled=True)  51.8 us
    pallas_call x1, Pallas kernels, state_backward(): pl.pallas_call(state_backward_kernel, out_shape=(jax.ShapeDtypeStruct((to...  33.7 us
  transfers between devices with their start and end apart: 36, of which 16 were waited for; matrix products, arithmetic and copies ran while one was open for 36% of the time, Pallas kernels for 7%

profile of v5, /device:TPU:0, one launch (start us, length us, event | category | flops | bytes accessed | tf_op | source)
XLA Modules:
  0.0 935.5 jit_solution(14705341742385477324)
XLA Ops:
  18.0 4.9 select_reduce_fusion
  24.6 7.4 all-to-all-start
  33.7 38.2 %all-to-all-done = bf16[16,16,2048]{2,1,0:T(8,128)(2,1)S(1)} async-done(((bf16[16,16,2048]{2,1,0:T(8,128)(2,1)}), bf16[16,16,2048]{2,1,0:T(8,128)(2,1)S(1)}, u32[]{:S(2)}, u32[]{:S(2)}) %all-to-all-start) | async-done | bytes 1048608 | tf_op jit(solution)/shard_map/all_to_all | solution.py:473
  71.9 3.7 all-to-all-start.1
  81.9 33.5 %all-to-all-done.1 = bf16[16,16,2048]{2,1,0:T(8,128)(2,1)S(1)} async-done(((bf16[16,16,2048]{2,1,0:T(8,128)(2,1)}), bf16[16,16,2048]{2,1,0:T(8,128)(2,1)S(1)}, u32[]{:S(2)}, u32[]{:S(2)}) %all-to-all-start.1) | async-done | bytes 1048608 | tf_op jit(solution)/shard_map/all_to_all | solution.py:473
  119.3 21.3 %collective-permute-done.1 = bf16[256,2048]{1,0:T(8,128)(2,1)S(1)} collective-permute-done((bf16[256,2048]{1,0:T(8,128)(2,1)S(1)}, bf16[256,2048]{1,0:T(8,128)(2,1)S(1)}, u32[]{:S(2)}, u32[]{:S(2)}) %collective-permute-start.1) | collective-permute-done | bytes 1048608 | tf_op jit(solution)/shard_map/ppermute | solution.py:425
  145.5 6.6 pick_halves.3
  155.4 32.8 %all-gather.5.cloned.1.call-done = bf16[2048,6528]{1,0:T(8,128)(2,1)} async-done(((bf16[128,6528]{1,0:T(8,128)(2,1)}), bf16[2048,6528]{1,0:T(8,128)(2,1)}) %all-gather.5.cloned.1.call-update) | async-done | bytes 26738704 | tf_op jit(solution)/shard_map/all_gather | solution.py:442
  198.7 7.9 fusion.70.signal_ref
  206.7 8.3 fusion.68.gate_ref
  215.0 20.7 %state_forward.1 = (f32[512,1536]{1,0:T(8,128)}, f32[512,128]{1,0:T(8,128)}) custom-call(f32[512,1536]{1,0:T(8,128)} %fusion.70.signal_ref, f32[512,1536]{1,0:T(8,128)} %fusion.68.gate_ref, f32[5,1536]{1,0:T(8,128)S(1)} %copy-done.61, f32[1,1536]{1,0:T(1,128)S(1)} %broadcast_in_dim_reshape.2.skip_ref, bf16[512,512]{1,0:T(8,128)(2,1)S(1)} %copy-done.23, ...), custom_call_target="tpu_custom_call" | custom-call | flops 1610612736 | bytes 9437184 | tf_op jit(solution)/shard_map/state_forward/pallas_call | solution.py:323
  241.6 4.1 copy.198
  245.8 3.7 fusion.125
  263.4 4.2 multiply_convert_fusion.6
  267.7 6.2 fusion.66
  278.8 45.4 %collective-permute-done.3 = bf16[512,2048]{1,0:T(8,128)(2,1)} collective-permute-done((bf16[512,2048]{1,0:T(8,128)(2,1)S(1)}, bf16[512,2048]{1,0:T(8,128)(2,1)}, u32[]{:S(2)}, u32[]{:S(2)}) %collective-permute-start.3) | collective-permute-done | bytes 2097184 | tf_op jit(solution)/shard_map/ppermute | solution.py:425
  324.3 6.0 fusion.105
  332.9 54.1 %conditional.12 = (f32[2048]{0:T(1024)S(1)}, bf16[512,2048]{1,0:T(8,128)(2,1)}, bf16[512,2048]{1,0:T(8,128)(2,1)}, bf16[512,4096]{1,0:T(8,128)(2,1)}) conditional(s32[]{:T(128)} %convert_element_type.507, () %tuple.129, (bf16[2048,6144]{1,0:T(8,128)(2,1)}, bf16[512,2048]{1,0:T(8,128)(2,1)}, bf16[512,2048]{1,0:T(8,128)(2,1)S(1)}, ...), branch_computations={%region_9.10_spmd, %region_10.13_spmd} | conditional | flops 21511536640 | bytes 237025392 | solution.py:565
  333.0 9.8 %fusion.4 = f32[512,2048]{1,0:T(8,128)} fusion(bf16[512,2048]{1,0:T(8,128)(2,1)S(1)} %get-tuple-element.346, bf16[2048,6144]{1,0:T(8,128)(2,1)} %get-tuple-element.345), kind=kOutput, calls=%fused_computation.4 | convolution fusion | flops 4294967296 | bytes 14680064 | tf_op jit(solution)/shard_map/cond/branch_1_fun/dot_general | solution.py:24
  345.7 6.1 fusion
  351.7 10.5 %multiply_convert_fusion = (bf16[512,2048]{1,0:T(8,128)(2,1)}, bf16[512,2048]{1,0:T(8,128)(2,1)S(1)}, bf16[512,2048]{1,0:T(8,128)(2,1)S(1)}) fusion(f32[512,2048]{1,0:T(8,128)} %fusion.4, f32[512,2048]{1,0:T(8,128)} %fusion, bf16[512,2048]{1,0:T(8,128)(2,1)S(1)} %get-tuple-element.346, bf16[2048,6144]{1,0:T(8,128)(2,1)} %get-tuple-element.345), kind=kOutput, calls=%fused_computation.11 | convolution fusion | flops 4310695936 | bytes 25165824 | tf_op jit(solution)/shard_map/cond/branch_1_fun/dot_general | solution.py:24
  362.3 10.1 %fusion.2 = f32[512,2048]{1,0:T(8,128)} fusion(bf16[512,2048]{1,0:T(8,128)(2,1)S(1)} %get-tuple-element.1030, bf16[2048,6144]{1,0:T(8,128)(2,1)} %get-tuple-element.345), kind=kOutput, calls=%fused_computation.2 | convolution fusion | flops 4294967296 | bytes 14680064 | tf_op jit(solution)/shard_map/cond/branch_1_fun/dot_general | solution.py:28
  372.4 9.7 %multiply_reduce_fusion = (f32[512]{0:T(512)S(1)}, f32[2048]{0:T(1024)S(1)}, f32[512,2048]{1,0:T(8,128)S(1)}) fusion(f32[512,2048]{1,0:T(8,128)S(1)} %copy-done.10, f32[2048]{0:T(1024)S(1)} %get-tuple-element.351, f32[512]{0:T(512)S(1)} %bitcast.452, f32[512,2048]{1,0:T(8,128)} %fusion.2, bf16[512,2048]{1,0:T(8,128)(2,1)S(1)} %get-tuple-element.1031, ...), kind=kOutput, calls=%fused_computation.13 | convolution fusion | flops 4302304768 | bytes 23089152 | tf_op jit(solution)/shard_map/cond/branch_1_fun/dot_general | solution.py:28
  393.7 36.9 %conditional.13 = (bf16[256,2048]{1,0:T(8,128)(2,1)}, bf16[256,2048]{1,0:T(8,128)(2,1)S(1)}, bf16[512,1024]{1,0:T(8,128)(2,1)}, bf16[1024,4096]{1,0:T(8,128)(2,1)}, bf16[2048,2048]{1,0:T(8,128)(2,1)}) conditional(s32[]{:T(128)} %convert_element_type.536, () %tuple.133, (bf16[2048,6144]{1,0:T(8,128)(2,1)}, bf16[512,2048]{1,0:T(8,128)(2,1)}, ...), branch_computations={%region_13.14_spmd, %region_14.15_spmd} | conditional | flops 12894339072 | bytes 55574684 | solution.py:565
  395.1 9.9 %fusion.18 = bf16[512,2048]{1,0:T(8,128)(2,1)} fusion(bf16[512,2048]{1,0:T(8,128)(2,1)} %get-tuple-element.352, bf16[2048,6144]{1,0:T(8,128)(2,1)} %get-tuple-element.353), kind=kOutput, calls=%fused_computation.28 | convolution fusion | flops 4296015872 | bytes 12582912 | tf_op jit(solution)/shard_map/cond/branch_1_fun/dot_general | solution.py:28
  407.7 4.1 pick_halves.2
  411.8 10.4 %convolution_convert_fusion.1 = bf16[1024,4096]{1,0:T(8,128)(2,1)} fusion(bf16[512,1024]{1,0:T(8,128)(2,1)} %get-tuple-element.358, bf16[512,4096]{1,0:T(8,128)(2,1)} %get-tuple-element.359), kind=kOutput, calls=%fused_computation.27 | convolution fusion | flops 4299161600 | bytes 13631488 | tf_op jit(solution)/shard_map/cond/branch_1_fun/dot_general | solution.py:32
  422.3 8.3 convolution_convert_fusion
  435.4 33.2 %conditional.14 = (f32[512]{0:T(512)S(1)}, f32[256,2048]{1,0:T(8,128)}, f32[512,1536]{1,0:T(8,128)}, bf16[512,2048]{1,0:T(8,128)(2,1)}, bf16[512,512]{0,1:T(8,12...) conditional(s32[]{:T(128)} %convert_element_type.537, () %tuple.136, ...), branch_computations={%region_15.16_spmd, %region_16.19_spmd} | conditional | flops 4850349568 | bytes 109207888 | solution.py:565
  435.6 7.3 fusion.104
  442.9 9.3 multiply_reduce_fusion.2
  452.2 3.4 constant_dynamic-slice_fusion.2
  455.6 3.9 fusion.29
  469.3 22.4 %conditional.15 = (bf16[512,2048]{1,0:T(8,128)(2,1)}, bf16[1,2,2,128,2048]{4,3,2,1,0:T(8,128)(2,1)S(1)}, bf16[512,2048]{1,0:T(8,128)(2,1)}, bf16[2,1,2,128,2048]{4,3,2,1,0:T(8,128)(2,1)}, bf16[2048,2048]{0,1:T(8,128)(2,1)}) conditional(s32[]{:T(128)} %convert_element_type.538, () %tuple.139, (bf16[512,1024]{1,0:T(8,128)(2,1)}, ...), branch_computations={%region_19.20_spmd, %region_20.21_spmd} | conditional | flops 8610906112 | bytes 59768928 | solution.py:565
  469.7 9.5 %add_convert_fusion.2 = bf16[1024,4096]{1,0:T(8,128)(2,1)S(1)} fusion(bf16[1024,4096]{1,0:T(8,128)(2,1)} %get-tuple-element.378, bf16[512,1024]{1,0:T(8,128)(2,1)} %get-tuple-element.376, bf16[512,4096]{1,0:T(8,128)(2,1)} %get-tuple-element.377), kind=kOutput, calls=%fused_computation.64 | convolution fusion | flops 4307550208 | bytes 22020096 | tf_op jit(solution)/shard_map/cond/branch_1_fun/dot_general | solution.py:32
  483.4 8.3 convert_bitcast_fusion
  493.3 12.0 %collective-permute-start.8 = (bf16[512,2048]{1,0:T(8,128)(2,1)}, bf16[512,2048]{1,0:T(8,128)(2,1)}, u32[]{:S(2)}, u32[]{:S(2)}) collective-permute-start(bf16[512,2048]{1,0:T(8,128)(2,1)} %get-tuple-element.631), channel_id=1, source_target_pairs={{0,8},{2,10},{4,12},{6,14},{8,0},{10,2},{12,4},{14,6},{16,24},{18,... | collective-permute-start | bytes 6291464 | tf_op jit(solution)/shard_map/ppermute | solution.py:428
  505.2 12.3 %copy.216 = bf16[2048,2048]{1,0:T(8,128)(2,1)} copy(bf16[2048,2048]{0,1:T(8,128)(2,1)} %get-tuple-element.665) | data formatting | bytes 16777216 | tf_op jit(solution)/shard_map/cond | solution.py:565
  517.7 3.9 collective-permute-done.6
  521.7 53.2 %conditional.16 = (f32[2,8,1536]{2,1,0:T(8,128)}, f32[2,8,512]{2,1,0:T(8,128)}, f32[2,24,2]{2,1,0:T(8,128)}, bf16[512,4480]{1,0:T(8,128)(2,1)}) conditional(s32[]{:T(128)} %convert_element_type.539, () %tuple.142, (f32[1536]{0:T(1024)S(1)}, f32[512]{0:T(512)}, f32[512]{0:T(512)}, f32[512]{0:T(512)}, f32[24]{0:T(128)}, ...), branch_computations={%region_21.22_spmd, %region_22.23_spmd} | conditional | flops 4026583552 | bytes 35197304 | solution.py:565
  531.8 33.7 %state_backward.1 = (bf16[512,1536]{1,0:T(8,128)(2,1)}, bf16[512,1536]{1,0:T(8,128)(2,1)}, f32[2,8,1536]{2,1,0:T(8,128)}, bf16[512,640]{1,0:T(8,128)(2,1)}, f32[2,8,512]{2,1,0:T(8,128)}, /*index=5*/f32[2,24,2]{2,1,0:T(8,128)}) custom-call(f32[512,1536]{1,0:T(8,128)} %get-tuple-element.382.grad_ref, f32[512,1536]{1,0:T(8,128)} %get-tuple-element.383.out_ref, ...), custom_call_target="tpu_custom_call" | custom-call | flops 4026531840 | bytes 15728640 | tf_op jit(solution)/shard_map/cond/branch_1_fun/state_backward/pallas_call | solution.py:347
  574.9 19.8 %conditional.17 = (bf16[1024,4480]{1,0:T(8,128)(2,1)}, bf16[256,2048]{1,0:T(8,128)(2,1)}, bf16[256,2048]{1,0:T(8,128)(2,1)}, bf16[1,1,2,128,2048]{4,3,2,1,0:T(8,...) conditional(s32[]{:T(128)} %convert_element_type.540, ...), branch_computations={%region_24.25_spmd, %region_25.26_spmd} | conditional | flops 4710858752 | bytes 45744240 | solution.py:565
  575.1 10.1 %convolution_convert_fusion.2 = bf16[1024,4480]{1,0:T(8,128)(2,1)} fusion(bf16[512,1024]{1,0:T(8,128)(2,1)} %get-tuple-element.414, bf16[512,4480]{1,0:T(8,128)(2,1)} %get-tuple-element.415), kind=kOutput, calls=%fused_computation.80 | convolution fusion | flops 4702208000 | bytes 14811136 | tf_op jit(solution)/shard_map/cond/branch_1_fun/dot_general | solution.py:32
  586.2 3.6 fusion.46
  600.7 26.1 %conditional.18 = (f32[2048]{0:T(1024)S(1)}, bf16[256,2048]{1,0:T(8,128)(2,1)}, bf16[256,2048]{1,0:T(8,128)(2,1)S(1)}) conditional(s32[]{:T(128)} %convert_element_type.541, () %tuple.148, (bf16[2048,6528]{1,0:T(8,128)(2,1)}, bf16[512,4480]{1,0:T(8,128)(2,1)}, f32[512,2048]{1,0:T(8,128)}, f32[2,2,128]{2,1,0:T(2,128)S(1)}, f32[512,1]{0,1:T(1,128)S(1)}, ...), branch_computations={%region_26.27_spmd, %region_27.30_spmd} | conditional | flops 9406776320 | bytes 46053484 | solution.py:565
  600.7 17.8 %multiply_reduce_fusion.3 = (f32[512]{0:T(512)S(1)}, f32[2048]{0:T(1024)S(1)}, f32[512,2048]{1,0:T(8,128)}) fusion(f32[512,2048]{1,0:T(8,128)} %get-tuple-element.424, f32[2048]{0:T(1024)S(1)} %get-tuple-element.428, f32[512]{0:T(512)S(1)} %bitcast.454, bf16[512,4480]{1,0:T(8,128)(2,1)} %get-tuple-element.422, bf16[2048,6528]{1,0:T(8,128)(2,1)} %get-tuple-element.423), kind=kOutput, calls=%fused_computation.88 | convolution fusion | flops 9401530368 | bytes 31346688 | tf_op jit(solution)/shard_map/cond/branch_1_fun/dot_general | solution.py:28
  618.5 5.5 subtract_convert_fusion.3
  627.4 24.1 %conditional.19 = (bf16[512,2176]{1,0:T(8,128)(2,1)}, bf16[1,2,2,128,2176]{4,3,2,1,0:T(8,128)(2,1)}, bf16[512,2304]{1,0:T(8,128)(2,1)}, bf16[2,1,2,128,2304]{4,3...) conditional(s32[]{:T(128)} %convert_element_type.542, ...), branch_computations={%region_30.31_spmd, %region_31.32_spmd} | conditional | flops 4987682816 | bytes 63438964 | solution.py:565
  627.6 9.2 add_convert_fusion.3
  652.5 4.7 all-to-all-start.3
  658.0 14.4 %conditional.20 = (f32[128,128]{1,0:T(8,128)}) conditional(s32[]{:T(128)} %convert_element_type.544, () %tuple.154, (f32[2,8,512]{2,1,0:T(8,128)}, f32[2,8,1536]{2,1,0:T(8,128)}, f32[2,24,2]{2,1,0:T(8,128)}, f32[24]{0:T(128)}, f32[2048]{0:T(1024)}, /*index=5*/f32[2048]{0:T(1024)}) %tuple.324), branch_computations={%region_32.33_spmd, %region_33.38_spmd} | conditional | flops 17968 | bytes 580152 | solution.py:565
  676.8 51.8 %reduce-scatter.5.cloned.1.call-done = bf16[128,2048]{1,0:T(8,128)(2,1)} async-done(((bf16[2048,2048]{1,0:T(8,128)(2,1)}), bf16[128,2048]{1,0:T(8,128)(2,1)}) %reduce-scatter.5.cloned.1.call-update) | async-done | bytes 524304 | tf_op jit(solution)/shard_map/reduce_scatter | solution.py:708
  728.5 24.1 %collective-permute-done.13 = bf16[128,2048]{1,0:T(8,128)(2,1)} collective-permute-done((bf16[128,2048]{1,0:T(8,128)(2,1)}, bf16[128,2048]{1,0:T(8,128)(2,1)}, u32[]{:S(2)}, u32[]{:S(2)}) %collective-permute-start.13) | collective-permute-done | bytes 524320 | tf_op jit(solution)/shard_map/ppermute | solution.py:428
  752.6 11.0 %collective-permute-done.14 = bf16[128,2048]{1,0:T(8,128)(2,1)} collective-permute-done((bf16[128,2048]{1,0:T(8,128)(2,1)}, bf16[128,2048]{1,0:T(8,128)(2,1)}, u32[]{:S(2)}, u32[]{:S(2)}) %collective-permute-start.14) | collective-permute-done | bytes 524320 | tf_op jit(solution)/shard_map/ppermute | solution.py:428
  763.6 19.6 %conditional.21 = (f32[128,2048]{1,0:T(8,128)}, f32[128,2048]{1,0:T(8,128)}, bf16[256,2176]{1,0:T(8,128)(2,1)}, bf16[1,1,2,128,2176]{4,3,2,1,0:T(8,128)(2,1)S(1)...) conditional(s32[]{:T(128)} %convert_element_type.545, ...), branch_computations={%region_39.40_spmd, %region_40.41_spmd} | conditional | flops 282345472 | bytes 56033472 | solution.py:565
  763.6 4.1 fusion.60
  777.4 4.0 fusion.59
  785.4 6.5 all-to-all-start.2
  795.9 37.0 %collective-permute-done.21 = f32[128,128]{1,0:T(8,128)S(1)} collective-permute-done((f32[128,128]{1,0:T(8,128)}, f32[128,128]{1,0:T(8,128)S(1)}, u32[]{:S(2)}, u32[]{:S(2)}) %collective-permute-start.21) | collective-permute-done | bytes 65568 | tf_op jit(solution)/shard_map/ppermute | solution.py:428
  835.9 6.1 conditional.22
  845.7 24.8 %collective-permute-done.24 = f32[128,128]{1,0:T(8,128)S(1)} collective-permute-done((f32[128,128]{1,0:T(8,128)S(1)}, f32[128,128]{1,0:T(8,128)S(1)}, u32[]{:S(2)}, u32[]{:S(2)}) %collective-permute-start.24) | collective-permute-done | bytes 65568 | tf_op jit(solution)/shard_map/ppermute | solution.py:428
  870.5 24.0 %collective-permute-done.22 = bf16[128,2176]{1,0:T(8,128)(2,1)S(1)} collective-permute-done((bf16[128,2176]{1,0:T(8,128)(2,1)}, bf16[128,2176]{1,0:T(8,128)(2,1)S(1)}, u32[]{:S(2)}, u32[]{:S(2)}) %collective-permute-start.22) | collective-permute-done | bytes 557088 | tf_op jit(solution)/shard_map/ppermute | solution.py:428
  894.5 12.8 %conditional.23 = (f32[128,2176]{1,0:T(8,128)}, f32[128,2304]{1,0:T(8,128)}, f32[128,128]{1,0:T(8,128)}, bf16[2,128,2048]{2,1,0:T(8,128)(2,1)S(1)}, bf16[2,128,2...) conditional(s32[]{:T(128)} %convert_element_type.547, ...), branch_computations={%region_43.44_spmd, %region_44.45_spmd} | conditional | flops 539656192 | bytes 12173400 | solution.py:565
  912.2 3.5 collective-permute-done.26
  (476 shorter events, 237.1 us)
Async XLA Ops:
  7.2 16.0 %copy-start = (bf16[2,128,2048]{2,1,0:T(8,128)(2,1)S(1)}, bf16[2,128,2048]{2,1,0:T(8,128)(2,1)}, u32[]{:S(2)}) copy-start(bf16[2,128,2048]{2,1,0:T(8,128)(2,1)} %param.50) | copy-start | bytes 3145732
  7.2 180.9 %all-gather.5.cloned.1.call-start = ((), (), s32[]{:S(2)}) async-start(), calls=%async_computation.7 | async-start | bytes 28409856 | tf_op jit(solution)/shard_map/all_gather | solution.py:442
  15.2 317.1 %all-gather.3.cloned.1.call-start = ((), (), s32[]{:S(2)}) async-start(), calls=%async_computation.6 | async-start | bytes 26738688 | tf_op jit(solution)/shard_map/all_gather | solution.py:442
  17.8 14.4 %copy-start.41 = (bf16[2,128,2048]{2,1,0:T(8,128)(2,1)S(1)}, bf16[2,128,2048]{2,1,0:T(8,128)(2,1)}, u32[]{:S(2)}) copy-start(bf16[2,128,2048]{2,1,0:T(8,128)(2,1)} %param.49) | copy-start | bytes 3145732
  23.2 92.2 %copy-start.93 = (s32[256]{0:T(256)}, s32[256]{0:T(256)S(1)}, u32[]{:S(2)}) copy-start(s32[256]{0:T(256)S(1)} %get-tuple-element.1117) | copy-start | bytes 3076
  24.6 47.3 %all-to-all-start = ((bf16[16,16,2048]{2,1,0:T(8,128)(2,1)}), bf16[16,16,2048]{2,1,0:T(8,128)(2,1)S(1)}, u32[]{:S(2)}, u32[]{:S(2)}) async-start(bf16[16,16,2048]{2,1,0:T(8,128)(2,1)} %bitcast.107), calls=%async_computation | async-start | bytes 2097152 | tf_op jit(solution)/shard_map/all_to_all | solution.py:473
  32.2 182.8 %copy-start.70 = (f32[1,1536]{1,0:T(1,128)}, f32[1,1536]{1,0:T(1,128)S(1)}, u32[]{:S(2)}) copy-start(f32[1,1536]{1,0:T(1,128)S(1)} %broadcast_in_dim_reshape.2.skip_ref) | copy-start | bytes 18436
  32.2 182.8 %copy-start.90 = (s32[2,1,256]{2,1,0:T(1,128)}, s32[2,1,256]{2,1,0:T(1,128)S(1)}, u32[]{:S(2)}) copy-start(s32[2,1,256]{2,1,0:T(1,128)S(1)} %broadcast_in_dim.74.seg_row_ref) | copy-start | bytes 6148
  32.2 45.5 %copy-start.104 = (s32[16]{0:T(128)S(1)}, s32[16]{0:T(128)}, u32[]{:S(2)}) copy-start(s32[16]{0:T(128)} %constant.230.clone) | copy-start | bytes 196
  32.2 45.5 %copy-start.72 = (f32[5,512]{1,0:T(8,128)S(1)}, f32[5,512]{1,0:T(8,128)}, u32[]{:S(2)}) copy-start(f32[5,512]{1,0:T(8,128)} %param.68) | copy-start | bytes 30724
  71.9 43.5 %all-to-all-start.1 = ((bf16[16,16,2048]{2,1,0:T(8,128)(2,1)}), bf16[16,16,2048]{2,1,0:T(8,128)(2,1)S(1)}, u32[]{:S(2)}, u32[]{:S(2)}) async-start(bf16[16,16,2048]{2,1,0:T(8,128)(2,1)} %bitcast.113), calls=%async_computation.1 | async-start | bytes 2097152 | tf_op jit(solution)/shard_map/all_to_all | solution.py:473
  75.5 499.3 %reduce-scatter.3.cloned.1.call-start = ((), (), s32[]{:S(2)}) async-start(), calls=%async_computation.8 | async-start | bytes 8912896 | tf_op jit(solution)/shard_map/reduce_scatter | solution.py:658
  75.8 40.0 %copy-start.82 = (s32[1,1,2,256]{3,1,2,0:T(1,128)}, s32[1,1,2,256]{3,1,2,0:T(1,128)S(1)}, u32[]{:S(2)}) copy-start(s32[1,1,2,256]{3,1,2,0:T(1,128)S(1)} %copy.244) | copy-start | bytes 6148
  76.7 39.2 %copy-start.83 = (s32[1,1,2,256]{3,1,2,0:T(1,128)}, s32[1,1,2,256]{3,1,2,0:T(1,128)S(1)}, u32[]{:S(2)}) copy-start(s32[1,1,2,256]{3,1,2,0:T(1,128)S(1)} %copy.245) | copy-start | bytes 6148
  77.8 39.6 %copy-start.103 = (f32[24]{0:T(128)S(1)}, f32[24]{0:T(128)}, u32[]{:S(2)}) copy-start(f32[24]{0:T(128)} %param.71) | copy-start | bytes 292
  78.3 39.1 %collective-permute-start = (bf16[256,2048]{1,0:T(8,128)(2,1)S(1)}, bf16[256,2048]{1,0:T(8,128)(2,1)S(1)}, u32[]{:S(2)}, u32[]{:S(2)}) collective-permute-start(bf16[256,2048]{1,0:T(8,128)(2,1)S(1)} %convolution_convert_fusion.9), channel_id=1, source_target_pairs={{0,1},{1,0},{2,3},{3,2},{4,5},{5,4},{6,7},{7,6},{8,9},{9,8},{10,11... | collective-permute-start | bytes 3145736 | tf_op jit(solution)/shard_map/ppermute | solution.py:425
  79.9 37.7 %copy-start.98 = (f32[64]{0:T(128)}, f32[64]{0:T(128)S(1)}, u32[]{:S(2)}) copy-start(f32[64]{0:T(128)S(1)} %multiply_exponential_fusion) | copy-start | bytes 772
  115.9 24.7 %collective-permute-start.1 = (bf16[256,2048]{1,0:T(8,128)(2,1)S(1)}, bf16[256,2048]{1,0:T(8,128)(2,1)S(1)}, u32[]{:S(2)}, u32[]{:S(2)}) collective-permute-start(bf16[256,2048]{1,0:T(8,128)(2,1)S(1)} %convolution_convert_fusion.7), channel_id=1, source_target_pairs={{0,1},{1,0},{2,3},{3,2},{4,5},{5,4},{6,7},{7,6},{8,9},{9,8},{10,11... | collective-permute-start | bytes 3145736 | tf_op jit(solution)/shard_map/ppermute | solution.py:425
  117.4 73.1 %copy-start.101 = (f32[24]{0:T(128)}, f32[24]{0:T(128)S(1)}, u32[]{:S(2)}) copy-start(f32[24]{0:T(128)S(1)} %exponential_negate_fusion) | copy-start | bytes 292
  152.1 36.1 %copy-start.3 = (bf16[512,2048]{1,0:T(8,128)(2,1)S(1)}, bf16[512,2048]{1,0:T(8,128)(2,1)}, u32[]{:S(2)}) copy-start(bf16[512,2048]{1,0:T(8,128)(2,1)} %multiply_convert_fusion.5.first_ref.second_ref) | copy-start | bytes 6291460
  152.1 36.1 %copy-start.97 = (f32[24]{0:T(128)S(1)}, f32[24]{0:T(128)}, u32[]{:S(2)}) copy-start(f32[24]{0:T(128)} %param.70) | copy-start | bytes 292
  193.8 21.2 %copy-start.55 = (f32[2,12,2,256]{3,2,1,0:T(2,128)}, f32[2,12,2,256]{3,2,1,0:T(2,128)S(1)}, u32[]{:S(2)}) copy-start(f32[2,12,2,256]{3,2,1,0:T(2,128)S(1)} %reshape.1074.step_ref) | copy-start | bytes 147460
  236.8 26.6 %collective-permute-start.2 = (f32[512]{0:T(512)S(1)}, f32[512]{0:T(512)S(1)}, u32[]{:S(2)}, u32[]{:S(2)}) collective-permute-start(f32[512]{0:T(512)S(1)} %reduce_sum.177), channel_id=1, source_target_pairs={{0,1},{1,0},{2,3},{3,2},{4,5},{5,4},{6,7},{7,6},{8,9},{9,8},{10,11... | collective-permute-start | bytes 6152 | tf_op jit(solution)/shard_map/ppermute | solution.py:425
  276.9 47.4 %collective-permute-start.3 = (bf16[512,2048]{1,0:T(8,128)(2,1)S(1)}, bf16[512,2048]{1,0:T(8,128)(2,1)}, u32[]{:S(2)}, u32[]{:S(2)}) collective-permute-start(bf16[512,2048]{1,0:T(8,128)(2,1)S(1)} %add_convert_fusion.7), channel_id=1, source_target_pairs={{0,1},{1,0},{2,3},{3,2},{4,5},{5,4},{6,7},{7,6},{8,9},{9,8},{10,11... | collective-permute-start | bytes 6291464 | tf_op jit(solution)/shard_map/ppermute | solution.py:425
  278.8 52.9 %copy-start.81 = (f32[2048]{0:T(1024)S(1)}, f32[2048]{0:T(1024)}, u32[]{:S(2)}) copy-start(f32[2048]{0:T(1024)} %param.66) | copy-start | bytes 24580
  332.4 55.3 %copy-start.31 = (bf16[512,4,64]{0,2,1:T(8,128)(2,1)S(1)}, bf16[512,4,64]{0,2,1:T(8,128)(2,1)}, u32[]{:S(2)}) copy-start(bf16[512,4,64]{0,2,1:T(8,128)(2,1)} %copy-done.30) | copy-start | bytes 786436
  332.4 56.1 %copy-start.20 = (bf16[2,256,1,4,128]{4,3,1,0,2:T(4,128)(2,1)S(1)}, bf16[2,256,1,4,128]{4,3,1,0,2:T(4,128)(2,1)}, u32[]{:S(2)}) copy-start(bf16[2,256,1,4,128]{4,3,1,0,2:T(4,128)(2,1)} %copy.203) | copy-start | bytes 1572868
  387.1 46.7 %collective-permute-start.4 = (bf16[512,2048]{1,0:T(8,128)(2,1)}, bf16[512,2048]{1,0:T(8,128)(2,1)}, u32[]{:S(2)}, u32[]{:S(2)}) collective-permute-start(bf16[512,2048]{1,0:T(8,128)(2,1)} %get-tuple-element.611), channel_id=1, source_target_pairs={{0,1},{1,0},{2,3},{3,2},{4,5},{5,4},{6,7},{7,6},{8,9},{9,8},{10,11... | collective-permute-start | bytes 6291464 | tf_op jit(solution)/shard_map/ppermute | solution.py:425
  430.6 38.0 %collective-permute-start.5 = (bf16[1024,4096]{1,0:T(8,128)(2,1)}, bf16[1024,4096]{1,0:T(8,128)(2,1)}, u32[]{:S(2)}, u32[]{:S(2)}) collective-permute-start(bf16[1024,4096]{1,0:T(8,128)(2,1)} %get-tuple-element.615), channel_id=1, source_target_pairs={{0,2},{2,0},{4,6},{6,4},{8,10},{10,8},{12,14},{14,12},{16,18},{18,... | collective-permute-start | bytes 25165832 | tf_op jit(solution)/shard_map/ppermute | solution.py:428
  431.6 296.9 %reduce-scatter.5.cloned.1.call-start = ((), (), s32[]{:S(2)}) async-start(), calls=%async_computation.9 | async-start | bytes 8912896 | tf_op jit(solution)/shard_map/reduce_scatter | solution.py:708
  491.7 83.2 %collective-permute-start.7 = (bf16[512,2048]{1,0:T(8,128)(2,1)}, bf16[512,2048]{1,0:T(8,128)(2,1)}, u32[]{:S(2)}, u32[]{:S(2)}) collective-permute-start(bf16[512,2048]{1,0:T(8,128)(2,1)} %get-tuple-element.629), channel_id=1, source_target_pairs={{0,4},{2,6},{4,0},{6,2},{8,12},{10,14},{12,8},{14,10},{16,20},{18,... | collective-permute-start | bytes 6291464 | tf_op jit(solution)/shard_map/ppermute | solution.py:428
  493.3 81.6 %collective-permute-start.8 = (bf16[512,2048]{1,0:T(8,128)(2,1)}, bf16[512,2048]{1,0:T(8,128)(2,1)}, u32[]{:S(2)}, u32[]{:S(2)}) collective-permute-start(bf16[512,2048]{1,0:T(8,128)(2,1)} %get-tuple-element.631), channel_id=1, source_target_pairs={{0,8},{2,10},{4,12},{6,14},{8,0},{10,2},{12,4},{14,6},{16,24},{18,... | collective-permute-start | bytes 6291464 | tf_op jit(solution)/shard_map/ppermute | solution.py:428
  517.7 4.0 collective-permute-start.6
  574.9 25.6 %copy-start.94 = (s32[256]{0:T(256)S(1)}, s32[256]{0:T(256)}, u32[]{:S(2)}) copy-start(s32[256]{0:T(256)} %copy-done.93) | copy-start | bytes 3076
  574.9 25.7 %copy-start.67 = (f32[2048]{0:T(1024)S(1)}, f32[2048]{0:T(1024)}, u32[]{:S(2)}) copy-start(f32[2048]{0:T(1024)} %param.65) | copy-start | bytes 24580
  574.9 25.7 %copy-start.85 = (f32[2,2,128]{2,1,0:T(2,128)S(1)}, f32[2,2,128]{2,1,0:T(2,128)}, u32[]{:S(2)}) copy-start(f32[2,2,128]{2,1,0:T(2,128)} %copy-done.84) | copy-start | bytes 6148
  574.9 25.7 %copy-start.87 = (f32[512,1]{0,1:T(1,128)S(1)}, f32[512,1]{0,1:T(1,128)}, u32[]{:S(2)}) copy-start(f32[512,1]{0,1:T(1,128)} %copy-done.86) | copy-start | bytes 6148
  574.9 25.7 %copy-start.89 = (f32[512,1]{0,1:T(1,128)S(1)}, f32[512,1]{0,1:T(1,128)}, u32[]{:S(2)}) copy-start(f32[512,1]{0,1:T(1,128)} %copy-done.88) | copy-start | bytes 6148
  594.7 32.1 %collective-permute-start.9 = (bf16[1024,4480]{1,0:T(8,128)(2,1)}, bf16[1024,4480]{1,0:T(8,128)(2,1)}, u32[]{:S(2)}, u32[]{:S(2)}) collective-permute-start(bf16[1024,4480]{1,0:T(8,128)(2,1)} %get-tuple-element.637), channel_id=1, source_target_pairs={{0,2},{2,0},{4,6},{6,4},{8,10},{10,8},{12,14},{14,12},{16,18},{18,... | collective-permute-start | bytes 27525128 | tf_op jit(solution)/shard_map/ppermute | solution.py:428
  594.8 32.0 %collective-permute-start.10 = (bf16[256,2048]{1,0:T(8,128)(2,1)}, bf16[256,2048]{1,0:T(8,128)(2,1)}, u32[]{:S(2)}, u32[]{:S(2)}) collective-permute-start(bf16[256,2048]{1,0:T(8,128)(2,1)} %get-tuple-element.640), channel_id=1, source_target_pairs={{0,1},{1,0},{2,3},{3,2},{4,5},{5,4},{6,7},{7,6},{8,9},{9,8},{10,11... | collective-permute-start | bytes 3145736 | tf_op jit(solution)/shard_map/ppermute | solution.py:425
  596.2 30.6 %collective-permute-start.11 = (bf16[256,2048]{1,0:T(8,128)(2,1)}, bf16[256,2048]{1,0:T(8,128)(2,1)}, u32[]{:S(2)}, u32[]{:S(2)}) collective-permute-start(bf16[256,2048]{1,0:T(8,128)(2,1)} %get-tuple-element.642), channel_id=1, source_target_pairs={{0,8},{2,10},{4,12},{6,14},{8,0},{10,2},{12,4},{14,6},{16,24},{18,... | collective-permute-start | bytes 3145736 | tf_op jit(solution)/shard_map/ppermute | solution.py:428
  599.0 27.8 %collective-permute-start.12 = (bf16[256,2048]{1,0:T(8,128)(2,1)}, bf16[256,2048]{1,0:T(8,128)(2,1)}, u32[]{:S(2)}, u32[]{:S(2)}) collective-permute-start(bf16[256,2048]{1,0:T(8,128)(2,1)} %get-tuple-element.644), channel_id=1, source_target_pairs={{0,4},{2,6},{4,0},{6,2},{8,12},{10,14},{12,8},{14,10},{16,20},{18,... | collective-permute-start | bytes 3145736 | tf_op jit(solution)/shard_map/ppermute | solution.py:428
  600.7 26.2 %copy-start.8 = (bf16[512,2048]{1,0:T(8,128)(2,1)S(1)}, bf16[512,2048]{1,0:T(8,128)(2,1)}, u32[]{:S(2)}) copy-start(bf16[512,2048]{1,0:T(8,128)(2,1)} %copy-done.7) | copy-start | bytes 6291460
  651.5 112.1 %collective-permute-start.16 = (bf16[512,2304]{1,0:T(8,128)(2,1)}, bf16[512,2304]{1,0:T(8,128)(2,1)S(1)}, u32[]{:S(2)}, u32[]{:S(2)}) collective-permute-start(bf16[512,2304]{1,0:T(8,128)(2,1)} %get-tuple-element.660), channel_id=1, source_target_pairs={{0,8},{2,10},{4,12},{6,14},{8,0},{10,2},{12,4},{14,6},{16,24},{18,... | collective-permute-start | bytes 7077896 | tf_op jit(solution)/shard_map/ppermute | solution.py:428
  652.1 111.5 %collective-permute-start.15 = (bf16[512,2176]{1,0:T(8,128)(2,1)}, bf16[512,2176]{1,0:T(8,128)(2,1)}, u32[]{:S(2)}, u32[]{:S(2)}) collective-permute-start(bf16[512,2176]{1,0:T(8,128)(2,1)} %get-tuple-element.658), channel_id=1, source_target_pairs={{0,4},{2,6},{4,0},{6,2},{8,12},{10,14},{12,8},{14,10},{16,20},{18,... | collective-permute-start | bytes 6684680 | tf_op jit(solution)/shard_map/ppermute | solution.py:428
  652.5 132.9 %all-to-all-start.3 = ((bf16[16,16,2048]{2,1,0:T(8,128)(2,1)}), bf16[16,16,2048]{2,1,0:T(8,128)(2,1)S(1)}, u32[]{:S(2)}, u32[]{:S(2)}) async-start(bf16[16,16,2048]{2,1,0:T(8,128)(2,1)} %bitcast.401), calls=%async_computation.5 | async-start | bytes 2097152 | tf_op jit(solution)/shard_map/all_to_all | solution.py:473
  657.3 106.3 %collective-permute-start.18 = (bf16[256,2048]{1,0:T(8,128)(2,1)}, bf16[256,2048]{1,0:T(8,128)(2,1)}, u32[]{:S(2)}, u32[]{:S(2)}) collective-permute-start(bf16[256,2048]{1,0:T(8,128)(2,1)} %get-tuple-element.663), channel_id=1, source_target_pairs={{0,1},{1,0},{2,3},{3,2},{4,5},{5,4},{6,7},{7,6},{8,9},{9,8},{10,11... | collective-permute-start | bytes 3145736 | tf_op jit(solution)/shard_map/ppermute | solution.py:425
  672.4 2.8 collective-permute-start.17
  672.5 80.2 %collective-permute-start.13 = (bf16[128,2048]{1,0:T(8,128)(2,1)}, bf16[128,2048]{1,0:T(8,128)(2,1)}, u32[]{:S(2)}, u32[]{:S(2)}) collective-permute-start(bf16[128,2048]{1,0:T(8,128)(2,1)} %get-tuple-element.654), channel_id=1, source_target_pairs={{0,16},{2,18},{4,20},{6,22},{8,24},{10,26},{12,28},{14,30},{16,0},... | collective-permute-start | bytes 1572872 | tf_op jit(solution)/shard_map/ppermute | solution.py:428
  675.2 88.4 %collective-permute-start.14 = (bf16[128,2048]{1,0:T(8,128)(2,1)}, bf16[128,2048]{1,0:T(8,128)(2,1)}, u32[]{:S(2)}, u32[]{:S(2)}) collective-permute-start(bf16[128,2048]{1,0:T(8,128)(2,1)} %get-tuple-element.656), channel_id=1, source_target_pairs={{0,16},{2,18},{4,20},{6,22},{8,24},{10,26},{12,28},{14,30},{16,0},... | collective-permute-start | bytes 1572872 | tf_op jit(solution)/shard_map/ppermute | solution.py:428
  785.4 109.1 %all-to-all-start.2 = ((bf16[16,16,2048]{2,1,0:T(8,128)(2,1)}), bf16[16,16,2048]{2,1,0:T(8,128)(2,1)}, u32[]{:S(2)}, u32[]{:S(2)}) async-start(bf16[16,16,2048]{2,1,0:T(8,128)(2,1)} %bitcast.400), calls=%async_computation.4 | async-start | bytes 2097152 | tf_op jit(solution)/shard_map/all_to_all | solution.py:473
  791.9 43.9 %collective-permute-start.20 = (bf16[256,2304]{1,0:T(8,128)(2,1)}, bf16[256,2304]{1,0:T(8,128)(2,1)}, u32[]{:S(2)}, u32[]{:S(2)}) collective-permute-start(bf16[256,2304]{1,0:T(8,128)(2,1)} %get-tuple-element.671), channel_id=1, source_target_pairs={{0,4},{2,6},{4,0},{6,2},{8,12},{10,14},{12,8},{14,10},{16,20},{18,... | collective-permute-start | bytes 3538952 | tf_op jit(solution)/shard_map/ppermute | solution.py:428
  793.8 42.0 %collective-permute-start.19 = (bf16[256,2176]{1,0:T(8,128)(2,1)}, bf16[256,2176]{1,0:T(8,128)(2,1)}, u32[]{:S(2)}, u32[]{:S(2)}) collective-permute-start(bf16[256,2176]{1,0:T(8,128)(2,1)} %get-tuple-element.669), channel_id=1, source_target_pairs={{0,8},{2,10},{4,12},{6,14},{8,0},{10,2},{12,4},{14,6},{16,24},{18,... | collective-permute-start | bytes 3342344 | tf_op jit(solution)/shard_map/ppermute | solution.py:428
  795.4 37.6 %collective-permute-start.21 = (f32[128,128]{1,0:T(8,128)}, f32[128,128]{1,0:T(8,128)S(1)}, u32[]{:S(2)}, u32[]{:S(2)}) collective-permute-start(f32[128,128]{1,0:T(8,128)} %get-tuple-element.672), channel_id=1, source_target_pairs={{0,4},{2,6},{4,0},{6,2},{8,12},{10,14},{12,8},{14,10},{16,20},{18,... | collective-permute-start | bytes 196616 | tf_op jit(solution)/shard_map/ppermute | solution.py:428
  841.9 52.6 %collective-permute-start.23 = (bf16[128,2304]{1,0:T(8,128)(2,1)}, bf16[128,2304]{1,0:T(8,128)(2,1)S(1)}, u32[]{:S(2)}, u32[]{:S(2)}) collective-permute-start(bf16[128,2304]{1,0:T(8,128)(2,1)} %get-tuple-element.678), channel_id=1, source_target_pairs={{0,16},{2,18},{4,20},{6,22},{8,24},{10,26},{12,28},{14,30},{16,0},... | collective-permute-start | bytes 1769480 | tf_op jit(solution)/shard_map/ppermute | solution.py:428
  844.5 50.0 %collective-permute-start.22 = (bf16[128,2176]{1,0:T(8,128)(2,1)}, bf16[128,2176]{1,0:T(8,128)(2,1)S(1)}, u32[]{:S(2)}, u32[]{:S(2)}) collective-permute-start(bf16[128,2176]{1,0:T(8,128)(2,1)} %get-tuple-element.676), channel_id=1, source_target_pairs={{0,16},{2,18},{4,20},{6,22},{8,24},{10,26},{12,28},{14,30},{16,0},... | collective-permute-start | bytes 1671176 | tf_op jit(solution)/shard_map/ppermute | solution.py:428
  844.9 25.6 %collective-permute-start.24 = (f32[128,128]{1,0:T(8,128)S(1)}, f32[128,128]{1,0:T(8,128)S(1)}, u32[]{:S(2)}, u32[]{:S(2)}) collective-permute-start(f32[128,128]{1,0:T(8,128)S(1)} %get-tuple-element.679), channel_id=1, source_target_pairs={{0,8},{2,10},{4,12},{6,14},{8,0},{10,2},{12,4},{14,6},{16,24},{18,... | collective-permute-start | bytes 196616 | tf_op jit(solution)/shard_map/ppermute | solution.py:428
  908.6 14.9 %copy-start.38 = (bf16[2,128,2048]{2,1,0:T(8,128)(2,1)}, bf16[2,128,2048]{2,1,0:T(8,128)(2,1)S(1)}, u32[]{:S(2)}) copy-start(bf16[2,128,2048]{2,1,0:T(8,128)(2,1)S(1)} %get-tuple-element.994) | copy-start | bytes 3145732
  908.6 14.9 %copy-start.39 = (bf16[2,128,2048]{2,1,0:T(8,128)(2,1)}, bf16[2,128,2048]{2,1,0:T(8,128)(2,1)S(1)}, u32[]{:S(2)}) copy-start(bf16[2,128,2048]{2,1,0:T(8,128)(2,1)S(1)} %get-tuple-element.993) | copy-start | bytes 3145732
  908.6 14.9 %copy-start.95 = (f32[128,24]{0,1:T(8,128)}, f32[128,24]{0,1:T(8,128)S(1)}, u32[]{:S(2)}) copy-start(f32[128,24]{0,1:T(8,128)S(1)} %get-tuple-element.1016) | copy-start | bytes 36868
  908.6 20.2 %copy-start.1 = (bf16[2,128,2048]{2,1,0:T(8,128)(2,1)S(1)}, bf16[2,128,2048]{2,1,0:T(8,128)(2,1)}, u32[]{:S(2)}) copy-start(bf16[2,128,2048]{2,1,0:T(8,128)(2,1)} %param.50) | copy-start | bytes 3145732
  908.6 8.6 collective-permute-start.25
  910.2 5.6 collective-permute-start.26
  916.6 4.3 collective-permute-start.27
  (77 other events, 299.4 us)
Sparse Core Ops, SparseCore 0:
  15.3 172.8 all-gather.4
  189.8 138.4 all-gather.2
  430.8 143.3 reduce-scatter.2
  578.0 150.4 reduce-scatter.4

commit v6 on v5

--- a/solution.py
+++ b/solution.py
@@ -178,20 +178,21 @@
 
 
 def state_forward_kernel(
-    signal_ref, gate_ref, taps_ref, skip_ref, state_ref, seg_col_ref, seg_row_ref, position_ref,
-    run_row_ref, run_col_ref, step_ref, out_ref, square_ref, inner_ref, mask_ref,
+    signal_ref, gate_ref, taps_ref, skip_ref, state_ref, seg_row_ref, run_row_ref, run_col_ref, step_ref, columns_ref,
+    out_ref, square_ref, inner_ref, mask_ref,
 ):
     rows = signal_ref.shape[0]
+    position = columns_ref[:, 1:2]
 
     @pl.when(pl.program_id(1) == 0)
     def _():
         inner_ref[...] = lax.dot_general(
             state_ref[:, NS:], state_ref[:, :NS], (((1,), (1,)), ((), ())), preferred_element_type=f32
         )
-        mask_ref[...] = block_mask(rows, seg_col_ref[...], seg_row_ref[0])
+        mask_ref[...] = block_mask(rows, columns_ref[:, 0:1], seg_row_ref[0])
         square_ref[...] = jnp.zeros_like(square_ref)
 
-    summed, _ = conv_block(signal_ref[...], taps_ref, position_ref[...])
+    summed, _ = conv_block(signal_ref[...], taps_ref, position)
     cols = summed * sigmoid_of(summed)
     cols_low = cols.astype(bf16)
     mixed = []
@@ -210,10 +211,9 @@
 
 
 def state_backward_kernel(
-    grad_ref, out_ref, gate_ref, signal_ref, taps_ref, skip_ref, gain_ref, scale_ref, cross_ref, state_ref,
-    seg_col_ref, seg_row_ref, position_ref, run_row_ref, run_col_ref, step_ref,
-    state_raw_ref, state_taps_ref, step_all_ref, step_sig_ref, rate_ref,
-    gate_low_ref, input_low_ref, sums_ref, rest_low_ref, state_sums_ref, head_sums_ref,
+    grad_ref, out_ref, gate_ref, signal_ref, taps_ref, skip_ref, gain_ref, state_ref, seg_row_ref, run_row_ref, run_col_ref,
+    step_ref, columns_ref, state_raw_ref, state_taps_ref, step_all_ref, step_sig_ref, rate_ref, others_ref,
+    first_ref, sums_ref, state_sums_ref, head_sums_ref,
     inner_ref, mask_ref, grad_inner_ref, direct_ref, along_ref,
 ):
     rows = signal_ref.shape[0]
@@ -225,18 +225,21 @@
         inner_ref[...] = lax.dot_general(
             state_ref[:, NS:], state_ref[:, :NS], (((1,), (1,)), ((), ())), preferred_element_type=f32
         )
-        mask_ref[...] = block_mask(rows, seg_col_ref[...], seg_row_ref[0])
+        mask_ref[...] = block_mask(rows, columns_ref[:, 0:1], seg_row_ref[0])
         grad_inner_ref[...] = jnp.zeros_like(grad_inner_ref)
 
     grad, out, gate, signal = grad_ref[...], out_ref[...], gate_ref[...], signal_ref[...]
-    position = position_ref[...]
+    position, scale, cross = columns_ref[:, 1:2], columns_ref[:, 2:3], columns_ref[:, 3:4]
+    gate_cols = pl.num_programs(1) * 2 * SHD
+    here = pl.multiple_of(pair * 2 * SHD, 2 * SHD)
+    rest = first_ref.shape[1] - others_ref.shape[1] - 2 * NS - STEP_PAD
     sig = sigmoid_of(gate)
     silu = gate * sig
     gated = out * silu
-    scaled = grad * scale_ref[...]
-    grad_gated = scaled * gain_ref[...] - gated * cross_ref[...]
+    scaled = grad * scale
+    grad_gated = scaled * gain_ref[...] - gated * cross
     grad_out = grad_gated * silu
-    gate_low_ref[...] = (grad_gated * out * (sig * (1.0 + gate * (1.0 - sig)))).astype(bf16)
+    first_ref[:, pl.ds(here, 2 * SHD)] = (grad_gated * out * (sig * (1.0 + gate * (1.0 - sig)))).astype(bf16)
     summed, moved = conv_block(signal, taps_ref, position)
     sig = sigmoid_of(summed)
     cols = summed * sig
@@ -269,7 +272,7 @@
     sums_ref[0, CONV + 1 : CONV + 2, :] = jnp.sum(scaled * gated, axis=0, keepdims=True)
     sums_ref[0, CONV + 2 : CONV + 3, :] = jnp.sum(grad_out * cols, axis=0, keepdims=True)
     sums_ref[0, CONV + 3 : CONV + 4, :] = jnp.zeros((1, cols.shape[1]), f32)
-    input_low_ref[...] = grad_signal.astype(bf16)
+    first_ref[:, pl.ds(pl.multiple_of(gate_cols + here, 2 * SHD), 2 * SHD)] = grad_signal.astype(bf16)
 
     @pl.when(pair == pl.num_programs(1) - 1)
     def _():
@@ -284,7 +287,7 @@
             )
             grad_sum = grad * (sig * (1.0 + summed * (1.0 - sig)))
             back = conv_block_back(grad_sum, raw, moved, taps, position, state_sums_ref.at[:, :, mine[0] : mine[1]])
-            rest_low_ref[:, mine[0] : mine[1]] = back.astype(bf16)
+            first_ref[:, rest + mine[0] : rest + mine[1]] = back.astype(bf16)
         state_sums_ref[0, CONV + 1 :, :] = jnp.zeros((7 - CONV, 2 * NS), f32)
         heads = step_all_ref.shape[1]
         direct, step = direct_ref[...], step_all_ref[0]
@@ -299,7 +302,8 @@
         head_sums_ref[0, :, 0:1] = jnp.sum(grad_product * step, axis=1, keepdims=True)
         head_sums_ref[0, :, 1:2] = jnp.sum(grad_raw, axis=1, keepdims=True)
         wide = jnp.concatenate([grad_raw, jnp.zeros((STEP_PAD - heads, rows), f32)], axis=0)
-        rest_low_ref[:, 2 * NS :] = wide.T.astype(bf16)
+        first_ref[:, rest + 2 * NS : rest + 2 * NS + STEP_PAD] = wide.T.astype(bf16)
+        first_ref[:, rest + 2 * NS + STEP_PAD :] = others_ref[...]
 
 
 def state_specs(rows, pairs):
@@ -309,14 +313,14 @@
         "taps": pl.BlockSpec((CONV + 1, 2 * SHD), lambda m, p: (0, p)),
         "vector": pl.BlockSpec((1, 2 * SHD), lambda m, p: (0, p)),
         "state": pl.BlockSpec((rows, 2 * NS), lambda m, p: (m, 0)),
-        "column": pl.BlockSpec((rows, 1), lambda m, p: (m, 0)),
+        "columns": pl.BlockSpec((rows, 8), lambda m, p: (m, 0)),
         "row": pl.BlockSpec((1, 1, rows), lambda m, p: (m, 0, 0)),
         "head_row": pl.BlockSpec((1, 1, 2, rows), lambda m, p: (m, p, 0, 0)),
         "head_col": pl.BlockSpec((1, 1, rows, 2), lambda m, p: (m, p, 0, 0)),
     }
 
 
-def state_forward(signal, gate, taps, skip, state, seg_col, seg_row, position, run_row, run_col, step):
+def state_forward(signal, gate, taps, skip, state, seg_row, run_row, run_col, step, columns):
     micro, pairs, _, rows = run_row.shape
     spec = state_specs(rows, pairs)
     total, width = signal.shape
@@ -325,46 +329,44 @@
         out_shape=(jax.ShapeDtypeStruct((total, width), f32), jax.ShapeDtypeStruct((total, 2 * SHD), f32)),
         grid=(micro, pairs),
         in_specs=[spec[name] for name in (
-            "block", "block", "taps", "vector", "state", "column", "row", "column", "head_row", "head_col", "head_row")],
+            "block", "block", "taps", "vector", "state", "row", "head_row", "head_col", "head_row", "columns")],
         out_specs=(spec["block"], pl.BlockSpec((rows, 2 * SHD), lambda m, p: (m, 0))),
         scratch_shapes=[pltpu.VMEM((rows, rows), f32), pltpu.VMEM((rows, rows), f32)],
         cost_estimate=pl.CostEstimate(
             flops=8 * total * rows * width // SHD * SHD, transcendentals=total * rows * width // SHD, bytes_accessed=12 * total * width
         ),
         name="state_forward",
-    )(signal, gate, taps, skip, state, seg_col, seg_row, position, run_row, run_col, step)
+    )(signal, gate, taps, skip, state, seg_row, run_row, run_col, step, columns)
 
 
 def state_backward(
-    grad, out, gate, signal, taps, skip, gain, scale, cross, state, seg_col, seg_row, position, run_row, run_col, step,
-    state_raw, state_taps, step_all, step_sig, rate,
+    grad, out, gate, signal, taps, skip, gain, state, seg_row, run_row, run_col, step, columns,
+    state_raw, state_taps, step_all, step_sig, rate, others,
 ):
     micro, pairs, _, rows = run_row.shape
     heads = 2 * pairs
     spec = state_specs(rows, pairs)
     total, width = signal.shape
+    joint = 2 * width + 2 * NS + STEP_PAD + others.shape[1]
     heads_block = pl.BlockSpec((1, heads, rows), lambda m, p: (m, 0, 0))
     return pl.pallas_call(
         state_backward_kernel,
         out_shape=(
-            jax.ShapeDtypeStruct((total, width), bf16),
-            jax.ShapeDtypeStruct((total, width), bf16),
+            jax.ShapeDtypeStruct((total, joint), bf16),
             jax.ShapeDtypeStruct((micro, 8, width), f32),
-            jax.ShapeDtypeStruct((total, 2 * NS + STEP_PAD), bf16),
             jax.ShapeDtypeStruct((micro, 8, 2 * NS), f32),
             jax.ShapeDtypeStruct((micro, heads, 2), f32),
         ),
         grid=(micro, pairs),
         in_specs=[spec[name] for name in (
-            "block", "block", "block", "block", "taps", "vector", "vector", "column", "column", "state",
-            "column", "row", "column", "head_row", "head_col", "head_row", "state")]
+            "block", "block", "block", "block", "taps", "vector", "vector", "state",
+            "row", "head_row", "head_col", "head_row", "columns", "state")]
         + [
             pl.BlockSpec((CONV + 1, 2 * NS), lambda m, p: (0, 0)), heads_block, heads_block,
-            pl.BlockSpec((heads, 1), lambda m, p: (0, 0)),
+            pl.BlockSpec((heads, 1), lambda m, p: (0, 0)), pl.BlockSpec((rows, others.shape[1]), lambda m, p: (m, 0)),
         ],
         out_specs=(
-            spec["block"], spec["block"], pl.BlockSpec((1, 8, 2 * SHD), lambda m, p: (m, 0, p)),
-            pl.BlockSpec((rows, 2 * NS + STEP_PAD), lambda m, p: (m, 0)),
+            pl.BlockSpec((rows, joint), lambda m, p: (m, 0)), pl.BlockSpec((1, 8, 2 * SHD), lambda m, p: (m, 0, p)),
             pl.BlockSpec((1, 8, 2 * NS), lambda m, p: (m, 0, 0)),
             pl.BlockSpec((1, heads, 2), lambda m, p: (m, 0, 0)),
         ),
@@ -374,8 +376,8 @@
         ),
         name="state_backward",
     )(
-        grad, out, gate, signal, taps, skip, gain, scale, cross, state, seg_col, seg_row, position, run_row, run_col, step,
-        state_raw, state_taps, step_all, step_sig, rate,
+        grad, out, gate, signal, taps, skip, gain, state, seg_row, run_row, run_col, step, columns,
+        state_raw, state_taps, step_all, step_sig, rate, others,
     )
 
 
@@ -596,8 +598,9 @@
     run_col = run_row.transpose(0, 1, 3, 2)
     step_row = step_heads.reshape(micro, pairs, 2, rows)
     skip_wide = jnp.repeat(skip_gain, SHD)[None, :]
-    layout = (state_low, segment.reshape(total, 1), segment.reshape(micro, 1, rows), position, run_row, run_col, step_row)
-    ssm_out, squares = state_forward(ssm_in, gate_z, kernel_inner, skip_wide, *layout)
+    layout = (state_low, segment.reshape(micro, 1, rows).astype(f32), run_row, run_col, step_row)
+    row_facts = jnp.concatenate([segment.reshape(total, 1).astype(f32), position.astype(f32)], axis=1)
+    ssm_out, squares = state_forward(ssm_in, gate_z, kernel_inner, skip_wide, *layout, jnp.pad(row_facts, ((0, 0), (0, 6))))
     square_own = jnp.sum(squares, axis=1)
     square_sum = square_own + other_lane(square_own)
     inv_rms = lax.rsqrt(square_sum / inner_width + epsilon)[:, None]
@@ -699,22 +702,21 @@
 
     def second_moves():
         moves = keep_first(mid_keep, feed_low, feed_came, feeds, (ff_cols, ff_cols))
-        branch_right = jnp.concatenate([gated_low, attended_low], axis=1)
-        return moves, outer_sum(whole_branch, branch_right).astype(bf16)
-
-    moves, part_branch = unit(second_moves)
+        return moves
+
+    moves = unit(second_moves)
     for red, move in zip(feeds, moves):
         red.move(*move)
-    sum_branch = lax.psum_scatter(part_branch, "dp", scatter_dimension=0, tiled=True)
 
     def state_space_backward():
         cross = (inv_rms**3) * ((cross_own + cross_other)[:, None] / inner_width)
         step_sig = jax.nn.sigmoid(raw_step + step_bias).reshape(micro, rows, heads).transpose(0, 2, 1)
-        gate_low, input_low, column_sums, rest_low, state_sums, head_sums = state_backward(
-            grad_gated_norm, ssm_out, gate_z, ssm_in, kernel_inner, skip_wide, mixer_gain[None, :], inv_rms, cross, *layout,
-            state_raw, kernel_state, step_heads, step_sig, rate[:, None],
-        )
-        return column_sums, state_sums, head_sums, jnp.concatenate([gate_low, input_low, rest_low, *qkv_low], axis=1)
+        columns = jnp.pad(jnp.concatenate([row_facts, inv_rms, cross], axis=1), ((0, 0), (0, 4)))
+        first_right, column_sums, state_sums, head_sums = state_backward(
+            grad_gated_norm, ssm_out, gate_z, ssm_in, kernel_inner, skip_wide, mixer_gain[None, :], *layout, columns,
+            state_raw, kernel_state, step_heads, step_sig, rate[:, None], jnp.concatenate(qkv_low, axis=1),
+        )
+        return column_sums, state_sums, head_sums, first_right
 
     column_sums, state_sums, head_sums, first_right = unit(state_space_backward)
 
@@ -724,9 +726,11 @@
             lax.optimization_barrier(ffn_send),
             [red.step() for red in feeds],
             sum_fdown.astype(f32),
-        )
-
-    send_first, ffn_send, steps, total_fdown = unit(third_moves)
+            outer_sum(whole_branch, jnp.concatenate([gated_low, attended_low], axis=1)).astype(bf16),
+        )
+
+    send_first, ffn_send, steps, total_fdown, part_branch = unit(third_moves)
+    sum_branch = lax.psum_scatter(part_branch, "dp", scatter_dimension=0, tiled=True)
     settle(feeds, steps)
     first_came = other_group(send_first, 1)
     ffn_other = other_lane(ffn_send)
@@ -739,9 +743,6 @@
 
     grad_gain_in, in_own, in_send = unit(input_gradient)
 
-    small_sizes = (width, width, (CONV + 1) * 2 * NS, (CONV + 1) * inner_width // lanes, inner_width // lanes, heads, heads, heads)
-    used = sum(small_sizes)
-    padded = -(-used // 1024) * 1024
     firsts = (red_low, red_high)
     first_sizes = (first_right.shape[1] // 256 * 128, first_right.shape[1] - first_right.shape[1] // 256 * 128)
 
@@ -749,31 +750,26 @@
         moves = keep_first(normed_left[0], first_right, first_came, firsts, first_sizes)
         ffn_out = ffn_own.astype(f32) + ffn_other.astype(f32)
         out_rows = (lane_rows(whole_mid, lane).astype(f32) + ffn_out).astype(bf16)
-        return moves, lax.optimization_barrier(in_send), deal_order_rows(out_rows), [red.step() for red in feeds]
-
-    moves, in_send, out_sent, steps = unit(first_moves)
+        head_row = (jnp.sum(head_sums, axis=0).T * jnp.stack([rate, jnp.ones_like(rate)])).reshape(1, -1)
+        flat = jnp.concatenate(
+            [
+                jnp.concatenate([jnp.sum(column_sums, axis=0), jnp.sum(state_sums, axis=0)], axis=1),
+                grad_gain_in[None, :], grad_gain_mid[None, :], jnp.pad(head_row, ((0, 5), (0, width - head_row.shape[1]))),
+            ]
+        )
+        return moves, lax.optimization_barrier(in_send), deal_order_rows(out_rows), [red.step() for red in feeds], flat
+
+    moves, in_send, out_sent, steps, flat = unit(first_moves)
+    flat_moved = other_group(flat, masks[0])
     settle(feeds, steps)
     out_moved = exchange(out_sent)
     for red, move in zip(firsts, moves):
         red.move(*move)
     in_other = other_lane(in_send)
 
-    def small_flat():
-        columns = jnp.sum(column_sums, axis=0)
-        head_totals = jnp.sum(head_sums, axis=0)
-        parts = (
-            grad_gain_in, grad_gain_mid, jnp.sum(state_sums, axis=0)[: CONV + 1].reshape(-1), columns[: CONV + 1].reshape(-1),
-            columns[CONV + 1], head_totals[:, 1], head_totals[:, 0] * rate,
-            jnp.sum(columns[CONV + 2].reshape(heads, SHD), axis=1),
-        )
-        return jnp.pad(jnp.concatenate(parts), (0, padded - used)).reshape(padded // 128, 128)
-
-    flat = unit(small_flat)
-    flat_moved = other_group(flat, masks[0])
-
     def send_input():
         in_sum = in_own.astype(f32) + in_other.astype(f32)
-        return deal_order_rows((in_sum + grad_middle_own).astype(bf16)), sum_branch.astype(f32)
+        return deal_order_rows((in_sum + grad_middle_own).astype(bf16))
 
     everything = [*feeds, *firsts]
     in_moved = None
@@ -784,7 +780,7 @@
             lambda: (
                 [red.step() for red in pending],
                 flat + flat_moved if bits <= len(masks) else flat,
-                (deal_take(in_moved), deal_take(out_moved)) if last else send_input() if in_moved is None else (),
+                (deal_take(in_moved), deal_take(out_moved), sum_branch.astype(f32)) if last else send_input() if in_moved is None else (),
             )
         )
         settle(pending, steps)
@@ -792,24 +788,28 @@
             flat_moved = other_group(flat, masks[bits])
         bits += 1
         if in_moved is None:
-            in_moved = exchange(other[0])
-            total_branch = other[1]
-    grad_input, block_out = other
+            in_moved = exchange(other)
+    grad_input, block_out, total_branch = other
     while bits <= len(masks):
         flat = flat + flat_moved
         if bits < len(masks):
             flat_moved = other_group(flat, masks[bits])
         bits += 1
-    theirs = other_lane(flat).reshape(-1)
-    flat = flat.reshape(-1)
-    pieces, start = [], 0
-    for place, size in enumerate(small_sizes):
-        mine, other = flat[start : start + size], theirs[start : start + size]
-        pieces.append(mine + other if place < 3 else (jnp.where(lane == 0, mine, other), jnp.where(lane == 0, other, mine)))
-        start += size
-    sum_gin, sum_gmid, sum_kst = pieces[0], pieces[1], pieces[2].reshape(CONV + 1, -1)
-    sum_kin = jnp.concatenate([half.reshape(CONV + 1, -1) for half in pieces[3]], axis=1)
-    sum_mix, sum_bias, sum_rate, sum_skip = [jnp.concatenate(pair) for pair in pieces[4:]]
+    theirs = other_lane(flat)
+    low, high = jnp.where(lane == 0, flat, theirs), jnp.where(lane == 0, theirs, flat)
+    both = flat + theirs
+
+    def joined(row, start, count):
+        return jnp.concatenate([low[row, start : start + count], high[row, start : start + count]])
+
+    gate_width = mamba_gate.shape[1]
+    sum_gin, sum_gmid = both[8], both[9]
+    sum_kst = both[: CONV + 1, gate_width : gate_width + 2 * NS]
+    sum_kin = jnp.concatenate([low[: CONV + 1, :gate_width], high[: CONV + 1, :gate_width]], axis=1)
+    sum_mix = joined(CONV + 1, 0, gate_width)
+    sum_skip = jnp.sum(joined(CONV + 2, 0, gate_width).reshape(SH, SHD), axis=1)
+    sum_bias = joined(10, heads, heads)
+    sum_rate = joined(10, 0, heads)
 
     query_cols, key_cols = query_weight.shape[1], key_weight.shape[1]
     total_fgate, total_fup = red_fgate.result, red_fup.result

time: 947 us -> 971 us (1.025)
  waiting for transfers between devices: 360 us -> 407 us
  local copies, waits for them, and re-layouts: 129 us -> 108 us
    ppermute x18, waiting for transfers between devices: 127 us -> 223 us  [other_group(): return lax.ppermute(values, 'dp', [(i, i ^ bits) for i in range(groups)])]
    reduce_scatter x1, waiting for transfers between devices: 51.8 us -> 0.02 us  [local(): lax.psum_scatter(part_branch, 'dp', scatter_dimension=0, tiled=True)]
  transfers between devices with their start and end apart: 36 -> 36, of which waited for: 16 -> 18; matrix products, arithmetic and copies ran while one was open for 36% -> 29% of each run, Pallas kernels for 7% -> 7%
where the time goes in v6:
time: 971 us; the launch traced here: 960 us
  waiting for transfers between devices  407 us (42%)
  matrix products  201 us (21%)
  local copies, waits for them, and re-layouts  108 us (11%)
  other arithmetic  96 us (10%)
  Pallas kernels  65.3 us (7%)
  starting transfers between devices  62.6 us (6%)
  between operations  16 us (2%)
    ppermute x18, waiting for transfers between devices, other_group(): return lax.ppermute(values, 'dp', [(i, i ^ bits) for i in range(groups)])  223 us
    ppermute x10, waiting for transfers between devices, other_lane(): return lax.ppermute(values, 'tensor', swap_lane)  73.2 us
    all_to_all x4, waiting for transfers between devices, exchange(): lax.all_to_all(buffer.reshape(groups, micro * per, width), 'dp', split_ax...  72.5 us
    dot_general x16, matrix products, project(): return jnp.dot(left, right, preferred_element_type=f32)  72.1 us
    dot_general x10, matrix products, outer_sum(): lax.dot_general(left, right, (((0,), (0,)), ((), ())), preferred_element_...  66.8 us
    dot_general x6, matrix products, project_back(): lax.dot_general(left, right, (((1,), (1,)), ((), ())), preferred_element_...  57.4 us
    pallas_call x1, Pallas kernels, state_backward(): pl.pallas_call(state_backward_kernel, out_shape=(jax.ShapeDtypeStruct((to...  34.3 us
    all_gather x2, waiting for transfers between devices, local(): lax.all_gather(jnp.concatenate(list(group_weights.values()), axis=1), 'dp...  32.8 us
  transfers between devices with their start and end apart: 36, of which 18 were waited for; matrix products, arithmetic and copies ran while one was open for 29% of the time, Pallas kernels for 7%

profile of v6, /device:TPU:0, one launch (start us, length us, event | category | flops | bytes accessed | tf_op | source)
XLA Modules:
  0.0 960.3 jit_solution(4794992185558036609)
XLA Ops:
  18.0 4.9 select_reduce_fusion
  24.6 7.4 all-to-all-start
  33.8 38.0 %all-to-all-done = bf16[16,16,2048]{2,1,0:T(8,128)(2,1)S(1)} async-done(((bf16[16,16,2048]{2,1,0:T(8,128)(2,1)}), bf16[16,16,2048]{2,1,0:T(8,128)(2,1)S(1)}, u32[]{:S(2)}, u32[]{:S(2)}) %all-to-all-start) | async-done | bytes 1048608 | tf_op jit(solution)/shard_map/all_to_all | solution.py:475
  71.9 3.7 all-to-all-start.1
  80.9 34.5 %all-to-all-done.1 = bf16[16,16,2048]{2,1,0:T(8,128)(2,1)S(1)} async-done(((bf16[16,16,2048]{2,1,0:T(8,128)(2,1)}), bf16[16,16,2048]{2,1,0:T(8,128)(2,1)S(1)}, u32[]{:S(2)}, u32[]{:S(2)}) %all-to-all-start.1) | async-done | bytes 1048608 | tf_op jit(solution)/shard_map/all_to_all | solution.py:475
  119.3 21.3 %collective-permute-done.1 = bf16[256,2048]{1,0:T(8,128)(2,1)S(1)} collective-permute-done((bf16[256,2048]{1,0:T(8,128)(2,1)S(1)}, bf16[256,2048]{1,0:T(8,128)(2,1)S(1)}, u32[]{:S(2)}, u32[]{:S(2)}) %collective-permute-start.1) | collective-permute-done | bytes 1048608 | tf_op jit(solution)/shard_map/ppermute | solution.py:427
  145.5 6.7 pick_halves.3
  155.5 32.7 %all-gather.5.cloned.1.call-done = bf16[2048,6528]{1,0:T(8,128)(2,1)} async-done(((bf16[128,6528]{1,0:T(8,128)(2,1)}), bf16[2048,6528]{1,0:T(8,128)(2,1)}) %all-gather.5.cloned.1.call-update) | async-done | bytes 26738704 | tf_op jit(solution)/shard_map/all_gather | solution.py:444
  198.7 7.9 fusion.70.signal_ref
  206.6 8.2 fusion.68.gate_ref
  214.9 20.5 %state_forward.1 = (f32[512,1536]{1,0:T(8,128)}, f32[512,128]{1,0:T(8,128)}) custom-call(f32[512,1536]{1,0:T(8,128)} %fusion.70.signal_ref, f32[512,1536]{1,0:T(8,128)} %fusion.68.gate_ref, f32[5,1536]{1,0:T(8,128)S(1)} %copy-done.61, f32[1,1536]{1,0:T(1,128)S(1)} %broadcast_in_dim_reshape.2.skip_ref, bf16[512,512]{1,0:T(8,128)(2,1)S(1)} %copy-done.24, ...), custom_call_target="tpu_custom_call" | custom-call | flops 1610612736 | bytes 9437184 | tf_op jit(solution)/shard_map/state_forward/pallas_call | solution.py:327
  241.2 4.4 copy.235
  245.6 3.6 fusion.122
  263.3 4.2 multiply_convert_fusion.6
  267.5 6.2 fusion.66
  278.6 45.7 %collective-permute-done.3 = bf16[512,2048]{1,0:T(8,128)(2,1)} collective-permute-done((bf16[512,2048]{1,0:T(8,128)(2,1)S(1)}, bf16[512,2048]{1,0:T(8,128)(2,1)}, u32[]{:S(2)}, u32[]{:S(2)}) %collective-permute-start.3) | collective-permute-done | bytes 2097184 | tf_op jit(solution)/shard_map/ppermute | solution.py:427
  324.3 6.1 fusion.102
  332.9 53.9 %conditional.11 = (f32[2048]{0:T(1024)S(1)}, bf16[512,2048]{1,0:T(8,128)(2,1)}, bf16[512,2048]{1,0:T(8,128)(2,1)}, bf16[512,4096]{1,0:T(8,128)(2,1)}) conditional(s32[]{:T(128)} %convert_element_type.519, () %tuple.118, (bf16[2048,6144]{1,0:T(8,128)(2,1)}, bf16[512,2048]{1,0:T(8,128)(2,1)}, bf16[512,2048]{1,0:T(8,128)(2,1)S(1)}, ...), branch_computations={%region_9.10_spmd, %region_10.13_spmd} | conditional | flops 21511536640 | bytes 237025392 | solution.py:567
  333.0 9.7 %fusion.4 = f32[512,2048]{1,0:T(8,128)} fusion(bf16[512,2048]{1,0:T(8,128)(2,1)S(1)} %get-tuple-element.311, bf16[2048,6144]{1,0:T(8,128)(2,1)} %get-tuple-element.310), kind=kOutput, calls=%fused_computation.4 | convolution fusion | flops 4294967296 | bytes 14680064 | tf_op jit(solution)/shard_map/cond/branch_1_fun/dot_general | solution.py:24
  345.7 6.1 fusion
  351.8 10.5 %multiply_convert_fusion = (bf16[512,2048]{1,0:T(8,128)(2,1)}, bf16[512,2048]{1,0:T(8,128)(2,1)S(1)}, bf16[512,2048]{1,0:T(8,128)(2,1)S(1)}) fusion(f32[512,2048]{1,0:T(8,128)} %fusion.4, f32[512,2048]{1,0:T(8,128)} %fusion, bf16[512,2048]{1,0:T(8,128)(2,1)S(1)} %get-tuple-element.311, bf16[2048,6144]{1,0:T(8,128)(2,1)} %get-tuple-element.310), kind=kOutput, calls=%fused_computation.11 | convolution fusion | flops 4310695936 | bytes 25165824 | tf_op jit(solution)/shard_map/cond/branch_1_fun/dot_general | solution.py:24
  362.3 10.0 %fusion.2 = f32[512,2048]{1,0:T(8,128)} fusion(bf16[512,2048]{1,0:T(8,128)(2,1)S(1)} %get-tuple-element.1136, bf16[2048,6144]{1,0:T(8,128)(2,1)} %get-tuple-element.310), kind=kOutput, calls=%fused_computation.2 | convolution fusion | flops 4294967296 | bytes 14680064 | tf_op jit(solution)/shard_map/cond/branch_1_fun/dot_general | solution.py:28
  372.4 9.7 %multiply_reduce_fusion = (f32[512]{0:T(512)S(1)}, f32[2048]{0:T(1024)S(1)}, f32[512,2048]{1,0:T(8,128)S(1)}) fusion(f32[512,2048]{1,0:T(8,128)S(1)} %copy-done.10, f32[2048]{0:T(1024)S(1)} %get-tuple-element.316, f32[512]{0:T(512)S(1)} %bitcast.442, f32[512,2048]{1,0:T(8,128)} %fusion.2, bf16[512,2048]{1,0:T(8,128)(2,1)S(1)} %get-tuple-element.1137, ...), kind=kOutput, calls=%fused_computation.13 | convolution fusion | flops 4302304768 | bytes 23089152 | tf_op jit(solution)/shard_map/cond/branch_1_fun/dot_general | solution.py:28
  392.6 38.0 %conditional.12 = (bf16[256,2048]{1,0:T(8,128)(2,1)}, bf16[256,2048]{1,0:T(8,128)(2,1)S(1)}, bf16[512,1024]{1,0:T(8,128)(2,1)}, bf16[1024,4096]{1,0:T(8,128)(2,1)}, bf16[2048,2048]{1,0:T(8,128)(2,1)}) conditional(s32[]{:T(128)} %convert_element_type.552, () %tuple.122, (bf16[2048,6144]{1,0:T(8,128)(2,1)}, bf16[512,2048]{1,0:T(8,128)(2,1)}, ...), branch_computations={%region_13.14_spmd, %region_14.15_spmd} | conditional | flops 12894339072 | bytes 55574684 | solution.py:567
  395.2 9.9 %fusion.18 = bf16[512,2048]{1,0:T(8,128)(2,1)} fusion(bf16[512,2048]{1,0:T(8,128)(2,1)} %get-tuple-element.317, bf16[2048,6144]{1,0:T(8,128)(2,1)} %get-tuple-element.318), kind=kOutput, calls=%fused_computation.28 | convolution fusion | flops 4296015872 | bytes 12582912 | tf_op jit(solution)/shard_map/cond/branch_1_fun/dot_general | solution.py:28
  407.8 3.9 pick_halves.2
  411.8 10.4 %convolution_convert_fusion.1 = bf16[1024,4096]{1,0:T(8,128)(2,1)} fusion(bf16[512,1024]{1,0:T(8,128)(2,1)} %get-tuple-element.323, bf16[512,4096]{1,0:T(8,128)(2,1)} %get-tuple-element.324), kind=kOutput, calls=%fused_computation.27 | convolution fusion | flops 4299161600 | bytes 13631488 | tf_op jit(solution)/shard_map/cond/branch_1_fun/dot_general | solution.py:32
  422.2 8.5 convolution_convert_fusion
  435.4 31.8 %conditional.13 = (f32[512]{0:T(512)S(1)}, f32[256,2048]{1,0:T(8,128)}, f32[512,1536]{1,0:T(8,128)}, bf16[512,2048]{1,0:T(8,128)(2,1)}, bf16[512,512]{0,1:T(8,12...) conditional(s32[]{:T(128)} %convert_element_type.553, () %tuple.125, ...), branch_computations={%region_15.16_spmd, %region_16.19_spmd} | conditional | flops 4850349568 | bytes 110780848 | solution.py:567
  435.6 7.3 fusion.101
  442.9 9.3 multiply_reduce_fusion.2
  452.2 3.4 constant_dynamic-slice_fusion.2
  455.6 3.9 fusion.29
  468.0 14.2 %conditional.14 = (bf16[512,2048]{1,0:T(8,128)(2,1)}, bf16[1,2,2,128,2048]{4,3,2,1,0:T(8,128)(2,1)S(1)}, bf16[512,2048]{1,0:T(8,128)(2,1)}, bf16[2,1,2,128,2048]{4,3,2,1,0:T(8,128)(2,1)}) conditional(s32[]{:T(128)} %convert_element_type.554, () %tuple.128, (bf16[512,1024]{1,0:T(8,128)(2,1)}, bf16[512,4096]{1,0:T(8,128)(2,1)}, ...), branch_computations={%region_19.20_spmd, %region_20.21_spmd} | conditional | flops 4307550208 | bytes 38797344 | solution.py:567
  468.2 9.7 %add_convert_fusion.2 = bf16[1024,4096]{1,0:T(8,128)(2,1)S(1)} fusion(bf16[1024,4096]{1,0:T(8,128)(2,1)} %get-tuple-element.343, bf16[512,1024]{1,0:T(8,128)(2,1)} %get-tuple-element.341, bf16[512,4096]{1,0:T(8,128)(2,1)} %get-tuple-element.342), kind=kOutput, calls=%fused_computation.64 | convolution fusion | flops 4307550208 | bytes 22020096 | tf_op jit(solution)/shard_map/cond/branch_1_fun/dot_general | solution.py:32
  483.5 11.2 %collective-permute-start.8 = (bf16[512,2048]{1,0:T(8,128)(2,1)}, bf16[512,2048]{1,0:T(8,128)(2,1)}, u32[]{:S(2)}, u32[]{:S(2)}) collective-permute-start(bf16[512,2048]{1,0:T(8,128)(2,1)} %get-tuple-element.591), channel_id=1, source_target_pairs={{0,8},{2,10},{4,12},{6,14},{8,0},{10,2},{12,4},{14,6},{16,24},{18,... | collective-permute-start | bytes 6291464 | tf_op jit(solution)/shard_map/ppermute | solution.py:430
  498.4 44.8 %conditional.15 = (f32[2,8,1536]{2,1,0:T(8,128)}, f32[2,8,512]{2,1,0:T(8,128)}, f32[2,24,2]{2,1,0:T(8,128)}, bf16[512,4480]{1,0:T(8,128)(2,1)}) conditional(s32[]{:T(128)} %convert_element_type.555, () %tuple.131, (f32[1536]{0:T(1024)S(1)}, f32[512]{0:T(512)S(1)}, f32[512]{0:T(512)S(1)}, f32[512]{0:T(512)S(1)}, f32[512,2]{0,1:T(2,128)S(1)}, ...), branch_computations={%region_21.22_spmd, %region_22.23_spmd} | conditional | flops 4028946944 | bytes 19444176 | solution.py:567
  508.9 34.3 %state_backward.1 = (bf16[512,4480]{1,0:T(8,128)(2,1)}, f32[2,8,1536]{2,1,0:T(8,128)}, f32[2,8,512]{2,1,0:T(8,128)}, f32[2,24,2]{2,1,0:T(8,128)}) custom-call(f32[512,1536]{1,0:T(8,128)} %get-tuple-element.344.grad_ref, f32[512,1536]{1,0:T(8,128)} %get-tuple-element.345.out_ref, f32[512,1536]{1,0:T(8,128)} %get-tuple-element.346.gate_ref, ...), custom_call_target="tpu_custom_call" | custom-call | flops 4026531840 | bytes 15728640 | tf_op jit(solution)/shard_map/cond/branch_1_fun/state_backward/pallas_call | solution.py:352
  543.2 3.4 collective-permute-done.7
  546.6 23.5 %collective-permute-done.8 = bf16[512,2048]{1,0:T(8,128)(2,1)} collective-permute-done((bf16[512,2048]{1,0:T(8,128)(2,1)}, bf16[512,2048]{1,0:T(8,128)(2,1)}, u32[]{:S(2)}, u32[]{:S(2)}) %collective-permute-start.8) | collective-permute-done | bytes 2097184 | tf_op jit(solution)/shard_map/ppermute | solution.py:430
  570.1 5.6 reduce-scatter.3.cloned.1.call-done
  575.7 28.7 %conditional.16 = (bf16[1024,4480]{1,0:T(8,128)(2,1)}, bf16[256,2048]{1,0:T(8,128)(2,1)}, bf16[256,2048]{1,0:T(8,128)(2,1)}, bf16[1,1,2,128,2048]{4,3,2,1,0:T(8,...) conditional(s32[]{:T(128)} %convert_element_type.556, ...), branch_computations={%region_24.25_spmd, %region_25.26_spmd} | conditional | flops 9014214656 | bytes 66715824 | solution.py:567
  576.1 10.1 %convolution_convert_fusion.2 = bf16[1024,4480]{1,0:T(8,128)(2,1)} fusion(bf16[512,1024]{1,0:T(8,128)(2,1)} %get-tuple-element.373, bf16[512,4480]{1,0:T(8,128)(2,1)} %get-tuple-element.374), kind=kOutput, calls=%fused_computation.71 | convolution fusion | flops 4702208000 | bytes 14811136 | tf_op jit(solution)/shard_map/cond/branch_1_fun/dot_general | solution.py:32
  596.0 8.4 convert_bitcast_fusion
  604.5 12.2 %copy.253 = bf16[2048,2048]{1,0:T(8,128)(2,1)} copy(bf16[2048,2048]{0,1:T(8,128)(2,1)} %get-tuple-element.641) | data formatting | bytes 16777216 | tf_op jit(solution)/shard_map/cond | solution.py:567
  621.7 27.0 %conditional.17 = (f32[2048]{0:T(1024)S(1)}, bf16[256,2048]{1,0:T(8,128)(2,1)}, bf16[256,2048]{1,0:T(8,128)(2,1)S(1)}) conditional(s32[]{:T(128)} %convert_element_type.557, () %tuple.137, (bf16[2048,6528]{1,0:T(8,128)(2,1)}, bf16[512,4480]{1,0:T(8,128)(2,1)}, f32[512,2048]{1,0:T(8,128)}, f32[2,2,128]{2,1,0:T(2,128)S(1)}, f32[512,1]{0,1:T(1,128)S(1)}, ...), branch_computations={%region_26.27_spmd, %region_27.30_spmd} | conditional | flops 9406776320 | bytes 46053484 | solution.py:567
  621.8 18.7 %multiply_reduce_fusion.3 = (f32[512]{0:T(512)S(1)}, f32[2048]{0:T(1024)S(1)}, f32[512,2048]{1,0:T(8,128)}) fusion(f32[512,2048]{1,0:T(8,128)} %get-tuple-element.386, f32[2048]{0:T(1024)S(1)} %get-tuple-element.390, f32[512]{0:T(512)S(1)} %bitcast.444, bf16[512,4480]{1,0:T(8,128)(2,1)} %get-tuple-element.384, bf16[2048,6528]{1,0:T(8,128)(2,1)} %get-tuple-element.385), kind=kOutput, calls=%fused_computation.84 | convolution fusion | flops 9401530368 | bytes 31346688 | tf_op jit(solution)/shard_map/cond/branch_1_fun/dot_general | solution.py:28
  640.4 5.5 subtract_convert_fusion.3
  648.8 26.6 %conditional.18 = (bf16[512,2176]{1,0:T(8,128)(2,1)}, bf16[1,2,2,128,2176]{4,3,2,1,0:T(8,128)(2,1)}, bf16[512,2304]{1,0:T(8,128)(2,1)}, bf16[2,1,2,128,2304]{4,3...) conditional(s32[]{:T(128)} %convert_element_type.558, ...), branch_computations={%region_30.31_spmd, %region_31.35_spmd} | conditional | flops 4987895808 | bytes 63850600 | solution.py:567
  648.9 9.2 add_convert_fusion.3
  677.4 4.8 all-to-all-start.3
  687.3 91.4 %collective-permute-done.13 = bf16[128,2048]{1,0:T(8,128)(2,1)} collective-permute-done((bf16[128,2048]{1,0:T(8,128)(2,1)}, bf16[128,2048]{1,0:T(8,128)(2,1)}, u32[]{:S(2)}, u32[]{:S(2)}) %collective-permute-start.13) | collective-permute-done | bytes 524320 | tf_op jit(solution)/shard_map/ppermute | solution.py:430
  778.6 10.8 %collective-permute-done.14 = bf16[128,2048]{1,0:T(8,128)(2,1)} collective-permute-done((bf16[128,2048]{1,0:T(8,128)(2,1)}, bf16[128,2048]{1,0:T(8,128)(2,1)}, u32[]{:S(2)}, u32[]{:S(2)}) %collective-permute-start.14) | collective-permute-done | bytes 524320 | tf_op jit(solution)/shard_map/ppermute | solution.py:430
  789.4 18.0 %conditional.19 = (f32[128,2048]{1,0:T(8,128)}, f32[128,2048]{1,0:T(8,128)}, bf16[256,2176]{1,0:T(8,128)(2,1)}, bf16[1,1,2,128,2176]{4,3,2,1,0:T(8,128)(2,1)S(1)...) conditional(s32[]{:T(128)} %convert_element_type.560, ...), branch_computations={%region_35.36_spmd, %region_36.37_spmd} | conditional | flops 282361856 | bytes 52297876 | solution.py:567
  789.4 4.1 fusion.60
  803.4 3.9 fusion.59
  809.7 6.6 all-to-all-start.2
  820.2 38.4 %collective-permute-done.21 = f32[16,2048]{1,0:T(8,128)S(1)} collective-permute-done((f32[16,2048]{1,0:T(8,128)}, f32[16,2048]{1,0:T(8,128)S(1)}, u32[]{:S(2)}, u32[]{:S(2)}) %collective-permute-start.21) | collective-permute-done | bytes 131104 | tf_op jit(solution)/shard_map/ppermute | solution.py:430
  860.2 6.4 conditional.20
  870.4 26.2 %collective-permute-done.24 = f32[16,2048]{1,0:T(8,128)S(1)} collective-permute-done((f32[16,2048]{1,0:T(8,128)S(1)}, f32[16,2048]{1,0:T(8,128)S(1)}, u32[]{:S(2)}, u32[]{:S(2)}) %collective-permute-start.24) | collective-permute-done | bytes 131104 | tf_op jit(solution)/shard_map/ppermute | solution.py:430
  896.6 22.6 %collective-permute-done.22 = bf16[128,2176]{1,0:T(8,128)(2,1)S(1)} collective-permute-done((bf16[128,2176]{1,0:T(8,128)(2,1)}, bf16[128,2176]{1,0:T(8,128)(2,1)S(1)}, u32[]{:S(2)}, u32[]{:S(2)}) %collective-permute-start.22) | collective-permute-done | bytes 557088 | tf_op jit(solution)/shard_map/ppermute | solution.py:430
  919.2 15.5 %conditional.21 = (f32[128,2176]{1,0:T(8,128)S(1)}, f32[128,2304]{1,0:T(8,128)}, f32[16,2048]{1,0:T(8,128)S(1)}, bf16[2,128,2048]{2,1,0:T(8,128)(2,1)}, bf16[2,1...) conditional(s32[]{:T(128)} %convert_element_type.562, ...), branch_computations={%region_40.41_spmd, %region_41.42_spmd} | conditional | flops 539672576 | bytes 32424208 | solution.py:567
  938.3 5.5 collective-permute-done.26
  945.1 3.7 collective-permute-done.27
  (479 shorter events, 211.5 us)
Async XLA Ops:
  7.2 16.0 %copy-start = (bf16[2,128,2048]{2,1,0:T(8,128)(2,1)S(1)}, bf16[2,128,2048]{2,1,0:T(8,128)(2,1)}, u32[]{:S(2)}) copy-start(bf16[2,128,2048]{2,1,0:T(8,128)(2,1)} %param.48) | copy-start | bytes 3145732
  7.2 181.0 %all-gather.5.cloned.1.call-start = ((), (), s32[]{:S(2)}) async-start(), calls=%async_computation.7 | async-start | bytes 28409856 | tf_op jit(solution)/shard_map/all_gather | solution.py:444
  15.2 317.1 %all-gather.3.cloned.1.call-start = ((), (), s32[]{:S(2)}) async-start(), calls=%async_computation.6 | async-start | bytes 26738688 | tf_op jit(solution)/shard_map/all_gather | solution.py:444
  17.8 14.6 %copy-start.38 = (bf16[2,128,2048]{2,1,0:T(8,128)(2,1)S(1)}, bf16[2,128,2048]{2,1,0:T(8,128)(2,1)}, u32[]{:S(2)}) copy-start(bf16[2,128,2048]{2,1,0:T(8,128)(2,1)} %param.47) | copy-start | bytes 3145732
  23.2 92.2 %copy-start.97 = (s32[256]{0:T(256)}, s32[256]{0:T(256)S(1)}, u32[]{:S(2)}) copy-start(s32[256]{0:T(256)S(1)} %get-tuple-element.1220) | copy-start | bytes 3076
  24.6 47.3 %all-to-all-start = ((bf16[16,16,2048]{2,1,0:T(8,128)(2,1)}), bf16[16,16,2048]{2,1,0:T(8,128)(2,1)S(1)}, u32[]{:S(2)}, u32[]{:S(2)}) async-start(bf16[16,16,2048]{2,1,0:T(8,128)(2,1)} %bitcast.108), calls=%async_computation | async-start | bytes 2097152 | tf_op jit(solution)/shard_map/all_to_all | solution.py:475
  32.2 182.7 %copy-start.70 = (f32[1,1536]{1,0:T(1,128)}, f32[1,1536]{1,0:T(1,128)S(1)}, u32[]{:S(2)}) copy-start(f32[1,1536]{1,0:T(1,128)S(1)} %broadcast_in_dim_reshape.2.skip_ref) | copy-start | bytes 18436
  32.4 44.4 %copy-start.110 = (s32[16]{0:T(128)S(1)}, s32[16]{0:T(128)}, u32[]{:S(2)}) copy-start(s32[16]{0:T(128)} %constant.235.clone) | copy-start | bytes 196
  32.4 44.4 %copy-start.73 = (f32[5,512]{1,0:T(8,128)S(1)}, f32[5,512]{1,0:T(8,128)}, u32[]{:S(2)}) copy-start(f32[5,512]{1,0:T(8,128)} %param.66) | copy-start | bytes 30724
  71.9 43.5 %all-to-all-start.1 = ((bf16[16,16,2048]{2,1,0:T(8,128)(2,1)}), bf16[16,16,2048]{2,1,0:T(8,128)(2,1)S(1)}, u32[]{:S(2)}, u32[]{:S(2)}) async-start(bf16[16,16,2048]{2,1,0:T(8,128)(2,1)} %bitcast.114), calls=%async_computation.1 | async-start | bytes 2097152 | tf_op jit(solution)/shard_map/all_to_all | solution.py:475
  75.5 500.2 %reduce-scatter.3.cloned.1.call-start = ((), (), s32[]{:S(2)}) async-start(), calls=%async_computation.8 | async-start | bytes 8912896 | tf_op jit(solution)/shard_map/reduce_scatter | solution.py:661
  75.6 139.2 %copy-start.93 = (f32[2,1,256]{2,1,0:T(1,128)}, f32[2,1,256]{2,1,0:T(1,128)S(1)}, u32[]{:S(2)}) copy-start(f32[2,1,256]{2,1,0:T(1,128)S(1)} %convert_element_type.533.seg_row_ref) | copy-start | bytes 6148
  75.7 40.2 %copy-start.75 = (f32[512,2]{0,1:T(2,128)}, f32[512,2]{0,1:T(2,128)S(1)}, u32[]{:S(2)}) copy-start(f32[512,2]{0,1:T(2,128)S(1)} %pad_maximum_fusion.12) | copy-start | bytes 12292
  76.8 40.6 %copy-start.109 = (f32[24]{0:T(128)S(1)}, f32[24]{0:T(128)}, u32[]{:S(2)}) copy-start(f32[24]{0:T(128)} %param.69) | copy-start | bytes 292
  77.3 40.1 %collective-permute-start = (bf16[256,2048]{1,0:T(8,128)(2,1)S(1)}, bf16[256,2048]{1,0:T(8,128)(2,1)S(1)}, u32[]{:S(2)}, u32[]{:S(2)}) collective-permute-start(bf16[256,2048]{1,0:T(8,128)(2,1)S(1)} %convolution_convert_fusion.9), channel_id=1, source_target_pairs={{0,1},{1,0},{2,3},{3,2},{4,5},{5,4},{6,7},{7,6},{8,9},{9,8},{10,11... | collective-permute-start | bytes 3145736 | tf_op jit(solution)/shard_map/ppermute | solution.py:427
  78.9 38.7 %copy-start.105 = (f32[64]{0:T(128)}, f32[64]{0:T(128)S(1)}, u32[]{:S(2)}) copy-start(f32[64]{0:T(128)S(1)} %multiply_exponential_fusion) | copy-start | bytes 772
  115.9 24.7 %collective-permute-start.1 = (bf16[256,2048]{1,0:T(8,128)(2,1)S(1)}, bf16[256,2048]{1,0:T(8,128)(2,1)S(1)}, u32[]{:S(2)}, u32[]{:S(2)}) collective-permute-start(bf16[256,2048]{1,0:T(8,128)(2,1)S(1)} %convolution_convert_fusion.7), channel_id=1, source_target_pairs={{0,1},{1,0},{2,3},{3,2},{4,5},{5,4},{6,7},{7,6},{8,9},{9,8},{10,11... | collective-permute-start | bytes 3145736 | tf_op jit(solution)/shard_map/ppermute | solution.py:427
  117.4 73.1 %copy-start.103 = (f32[24]{0:T(128)}, f32[24]{0:T(128)S(1)}, u32[]{:S(2)}) copy-start(f32[24]{0:T(128)S(1)} %exponential_negate_fusion) | copy-start | bytes 292
  152.1 36.1 %copy-start.3 = (bf16[512,2048]{1,0:T(8,128)(2,1)S(1)}, bf16[512,2048]{1,0:T(8,128)(2,1)}, u32[]{:S(2)}) copy-start(bf16[512,2048]{1,0:T(8,128)(2,1)} %multiply_convert_fusion.5.first_ref.second_ref) | copy-start | bytes 6291460
  152.1 36.1 %copy-start.102 = (f32[24]{0:T(128)S(1)}, f32[24]{0:T(128)}, u32[]{:S(2)}) copy-start(f32[24]{0:T(128)} %param.68) | copy-start | bytes 292
  193.8 21.1 %copy-start.57 = (f32[2,12,2,256]{3,2,1,0:T(2,128)}, f32[2,12,2,256]{3,2,1,0:T(2,128)S(1)}, u32[]{:S(2)}) copy-start(f32[2,12,2,256]{3,2,1,0:T(2,128)S(1)} %reshape.1037.step_ref) | copy-start | bytes 147460
  236.5 26.8 %collective-permute-start.2 = (f32[512]{0:T(512)S(1)}, f32[512]{0:T(512)S(1)}, u32[]{:S(2)}, u32[]{:S(2)}) collective-permute-start(f32[512]{0:T(512)S(1)} %reduce_sum.177), channel_id=1, source_target_pairs={{0,1},{1,0},{2,3},{3,2},{4,5},{5,4},{6,7},{7,6},{8,9},{9,8},{10,11... | collective-permute-start | bytes 6152 | tf_op jit(solution)/shard_map/ppermute | solution.py:427
  276.7 47.6 %collective-permute-start.3 = (bf16[512,2048]{1,0:T(8,128)(2,1)S(1)}, bf16[512,2048]{1,0:T(8,128)(2,1)}, u32[]{:S(2)}, u32[]{:S(2)}) collective-permute-start(bf16[512,2048]{1,0:T(8,128)(2,1)S(1)} %add_convert_fusion.7), channel_id=1, source_target_pairs={{0,1},{1,0},{2,3},{3,2},{4,5},{5,4},{6,7},{7,6},{8,9},{9,8},{10,11... | collective-permute-start | bytes 6291464 | tf_op jit(solution)/shard_map/ppermute | solution.py:427
  278.6 53.1 %copy-start.86 = (f32[2048]{0:T(1024)S(1)}, f32[2048]{0:T(1024)}, u32[]{:S(2)}) copy-start(f32[2048]{0:T(1024)} %param.64) | copy-start | bytes 24580
  332.3 55.1 %copy-start.32 = (bf16[512,4,64]{0,2,1:T(8,128)(2,1)S(1)}, bf16[512,4,64]{0,2,1:T(8,128)(2,1)}, u32[]{:S(2)}) copy-start(bf16[512,4,64]{0,2,1:T(8,128)(2,1)} %copy-done.31) | copy-start | bytes 786436
  386.9 47.0 %collective-permute-start.4 = (bf16[512,2048]{1,0:T(8,128)(2,1)}, bf16[512,2048]{1,0:T(8,128)(2,1)}, u32[]{:S(2)}, u32[]{:S(2)}) collective-permute-start(bf16[512,2048]{1,0:T(8,128)(2,1)} %get-tuple-element.572), channel_id=1, source_target_pairs={{0,1},{1,0},{2,3},{3,2},{4,5},{5,4},{6,7},{7,6},{8,9},{9,8},{10,11... | collective-permute-start | bytes 6291464 | tf_op jit(solution)/shard_map/ppermute | solution.py:427
  430.6 36.6 %collective-permute-start.5 = (bf16[1024,4096]{1,0:T(8,128)(2,1)}, bf16[1024,4096]{1,0:T(8,128)(2,1)}, u32[]{:S(2)}, u32[]{:S(2)}) collective-permute-start(bf16[1024,4096]{1,0:T(8,128)(2,1)} %get-tuple-element.576), channel_id=1, source_target_pairs={{0,2},{2,0},{4,6},{6,4},{8,10},{10,8},{12,14},{14,12},{16,18},{18,... | collective-permute-start | bytes 25165832 | tf_op jit(solution)/shard_map/ppermute | solution.py:430
  431.6 438.7 %reduce-scatter.5.cloned.1.call-start = ((), (), s32[]{:S(2)}) async-start(), calls=%async_computation.9 | async-start | bytes 8912896 | tf_op jit(solution)/shard_map/reduce_scatter | solution.py:733
  467.9 26.8 %copy-start.101 = (f32[512]{0:T(512)S(1)}, f32[512]{0:T(512)}, u32[]{:S(2)}) copy-start(f32[512]{0:T(512)} %copy-done.100) | copy-start | bytes 6148
  467.9 30.4 %copy-start.6 = (f32[512,512]{1,0:T(8,128)S(1)}, f32[512,512]{1,0:T(8,128)}, u32[]{:S(2)}) copy-start(f32[512,512]{1,0:T(8,128)} %copy-done.5) | copy-start | bytes 3145732
  467.9 30.4 %copy-start.40 = (f32[2,24,256]{2,0,1:T(2,128)S(1)}, f32[2,24,256]{2,0,1:T(2,128)}, u32[]{:S(2)}) copy-start(f32[2,24,256]{2,0,1:T(2,128)} %copy-done.39) | copy-start | bytes 147460
  467.9 30.4 %copy-start.58 = (f32[2,12,2,256]{3,2,1,0:T(2,128)S(1)}, f32[2,12,2,256]{3,2,1,0:T(2,128)}, u32[]{:S(2)}) copy-start(f32[2,12,2,256]{3,2,1,0:T(2,128)} %copy-done.57) | copy-start | bytes 147460
  467.9 30.4 %copy-start.60 = (f32[3,2,8,256]{3,2,0,1:T(8,128)S(1)}, f32[3,2,8,256]{3,2,0,1:T(8,128)}, u32[]{:S(2)}) copy-start(f32[3,2,8,256]{3,2,0,1:T(8,128)} %copy-done.59) | copy-start | bytes 147460
  467.9 30.4 %copy-start.76 = (f32[512,2]{0,1:T(2,128)S(1)}, f32[512,2]{0,1:T(2,128)}, u32[]{:S(2)}) copy-start(f32[512,2]{0,1:T(2,128)} %copy-done.75) | copy-start | bytes 12292
  467.9 30.4 %copy-start.80 = (f32[1536]{0:T(1024)S(1)}, f32[1536]{0:T(1024)}, u32[]{:S(2)}) copy-start(f32[1536]{0:T(1024)} %param.67) | copy-start | bytes 18436
  468.0 30.4 %copy-start.82 = (f32[512]{0:T(512)S(1)}, f32[512]{0:T(512)}, u32[]{:S(2)}) copy-start(f32[512]{0:T(512)} %copy-done.81) | copy-start | bytes 6148
  482.2 64.4 %collective-permute-start.7 = (bf16[512,2048]{1,0:T(8,128)(2,1)}, bf16[512,2048]{1,0:T(8,128)(2,1)}, u32[]{:S(2)}, u32[]{:S(2)}) collective-permute-start(bf16[512,2048]{1,0:T(8,128)(2,1)} %get-tuple-element.589), channel_id=1, source_target_pairs={{0,4},{2,6},{4,0},{6,2},{8,12},{10,14},{12,8},{14,10},{16,20},{18,... | collective-permute-start | bytes 6291464 | tf_op jit(solution)/shard_map/ppermute | solution.py:430
  483.5 86.6 %collective-permute-start.8 = (bf16[512,2048]{1,0:T(8,128)(2,1)}, bf16[512,2048]{1,0:T(8,128)(2,1)}, u32[]{:S(2)}, u32[]{:S(2)}) collective-permute-start(bf16[512,2048]{1,0:T(8,128)(2,1)} %get-tuple-element.591), channel_id=1, source_target_pairs={{0,8},{2,10},{4,12},{6,14},{8,0},{10,2},{12,4},{14,6},{16,24},{18,... | collective-permute-start | bytes 6291464 | tf_op jit(solution)/shard_map/ppermute | solution.py:430
  494.7 3.6 collective-permute-start.6
  604.4 44.3 %collective-permute-start.9 = (bf16[1024,4480]{1,0:T(8,128)(2,1)}, bf16[1024,4480]{1,0:T(8,128)(2,1)}, u32[]{:S(2)}, u32[]{:S(2)}) collective-permute-start(bf16[1024,4480]{1,0:T(8,128)(2,1)} %get-tuple-element.598), channel_id=1, source_target_pairs={{0,2},{2,0},{4,6},{6,4},{8,10},{10,8},{12,14},{14,12},{16,18},{18,... | collective-permute-start | bytes 27525128 | tf_op jit(solution)/shard_map/ppermute | solution.py:430
  616.8 31.9 %collective-permute-start.10 = (bf16[256,2048]{1,0:T(8,128)(2,1)}, bf16[256,2048]{1,0:T(8,128)(2,1)}, u32[]{:S(2)}, u32[]{:S(2)}) collective-permute-start(bf16[256,2048]{1,0:T(8,128)(2,1)} %get-tuple-element.601), channel_id=1, source_target_pairs={{0,1},{1,0},{2,3},{3,2},{4,5},{5,4},{6,7},{7,6},{8,9},{9,8},{10,11... | collective-permute-start | bytes 3145736 | tf_op jit(solution)/shard_map/ppermute | solution.py:427
  618.3 30.4 %collective-permute-start.11 = (bf16[256,2048]{1,0:T(8,128)(2,1)}, bf16[256,2048]{1,0:T(8,128)(2,1)}, u32[]{:S(2)}, u32[]{:S(2)}) collective-permute-start(bf16[256,2048]{1,0:T(8,128)(2,1)} %get-tuple-element.603), channel_id=1, source_target_pairs={{0,8},{2,10},{4,12},{6,14},{8,0},{10,2},{12,4},{14,6},{16,24},{18,... | collective-permute-start | bytes 3145736 | tf_op jit(solution)/shard_map/ppermute | solution.py:430
  620.1 28.6 %collective-permute-start.12 = (bf16[256,2048]{1,0:T(8,128)(2,1)}, bf16[256,2048]{1,0:T(8,128)(2,1)}, u32[]{:S(2)}, u32[]{:S(2)}) collective-permute-start(bf16[256,2048]{1,0:T(8,128)(2,1)} %get-tuple-element.605), channel_id=1, source_target_pairs={{0,4},{2,6},{4,0},{6,2},{8,12},{10,14},{12,8},{14,10},{16,20},{18,... | collective-permute-start | bytes 3145736 | tf_op jit(solution)/shard_map/ppermute | solution.py:430
  621.7 27.0 %copy-start.8 = (bf16[512,2048]{1,0:T(8,128)(2,1)S(1)}, bf16[512,2048]{1,0:T(8,128)(2,1)}, u32[]{:S(2)}) copy-start(bf16[512,2048]{1,0:T(8,128)(2,1)} %copy-done.7) | copy-start | bytes 6291460
  621.7 27.0 %copy-start.85 = (f32[2048]{0:T(1024)S(1)}, f32[2048]{0:T(1024)}, u32[]{:S(2)}) copy-start(f32[2048]{0:T(1024)} %copy-done.84) | copy-start | bytes 24580
  621.7 27.0 %copy-start.104 = (f32[24]{0:T(128)S(1)}, f32[24]{0:T(128)}, u32[]{:S(2)}) copy-start(f32[24]{0:T(128)} %copy-done.103) | copy-start | bytes 292
  676.0 113.4 %collective-permute-start.16 = (bf16[512,2304]{1,0:T(8,128)(2,1)}, bf16[512,2304]{1,0:T(8,128)(2,1)S(1)}, u32[]{:S(2)}, u32[]{:S(2)}) collective-permute-start(bf16[512,2304]{1,0:T(8,128)(2,1)} %get-tuple-element.620), channel_id=1, source_target_pairs={{0,8},{2,10},{4,12},{6,14},{8,0},{10,2},{12,4},{14,6},{16,24},{18,... | collective-permute-start | bytes 7077896 | tf_op jit(solution)/shard_map/ppermute | solution.py:430
  676.9 112.5 %collective-permute-start.15 = (bf16[512,2176]{1,0:T(8,128)(2,1)}, bf16[512,2176]{1,0:T(8,128)(2,1)}, u32[]{:S(2)}, u32[]{:S(2)}) collective-permute-start(bf16[512,2176]{1,0:T(8,128)(2,1)} %get-tuple-element.618), channel_id=1, source_target_pairs={{0,4},{2,6},{4,0},{6,2},{8,12},{10,14},{12,8},{14,10},{16,20},{18,... | collective-permute-start | bytes 6684680 | tf_op jit(solution)/shard_map/ppermute | solution.py:430
  677.4 132.2 %all-to-all-start.3 = ((bf16[16,16,2048]{2,1,0:T(8,128)(2,1)}), bf16[16,16,2048]{2,1,0:T(8,128)(2,1)S(1)}, u32[]{:S(2)}, u32[]{:S(2)}) async-start(bf16[16,16,2048]{2,1,0:T(8,128)(2,1)} %bitcast.400), calls=%async_computation.4 | async-start | bytes 2097152 | tf_op jit(solution)/shard_map/all_to_all | solution.py:475
  682.2 107.2 %collective-permute-start.18 = (bf16[256,2048]{1,0:T(8,128)(2,1)}, bf16[256,2048]{1,0:T(8,128)(2,1)}, u32[]{:S(2)}, u32[]{:S(2)}) collective-permute-start(bf16[256,2048]{1,0:T(8,128)(2,1)} %get-tuple-element.623), channel_id=1, source_target_pairs={{0,1},{1,0},{2,3},{3,2},{4,5},{5,4},{6,7},{7,6},{8,9},{9,8},{10,11... | collective-permute-start | bytes 3145736 | tf_op jit(solution)/shard_map/ppermute | solution.py:427
  682.8 2.8 collective-permute-start.17
  682.9 95.8 %collective-permute-start.13 = (bf16[128,2048]{1,0:T(8,128)(2,1)}, bf16[128,2048]{1,0:T(8,128)(2,1)}, u32[]{:S(2)}, u32[]{:S(2)}) collective-permute-start(bf16[128,2048]{1,0:T(8,128)(2,1)} %get-tuple-element.614), channel_id=1, source_target_pairs={{0,16},{2,18},{4,20},{6,22},{8,24},{10,26},{12,28},{14,30},{16,0},... | collective-permute-start | bytes 1572872 | tf_op jit(solution)/shard_map/ppermute | solution.py:430
  685.6 103.8 %collective-permute-start.14 = (bf16[128,2048]{1,0:T(8,128)(2,1)}, bf16[128,2048]{1,0:T(8,128)(2,1)}, u32[]{:S(2)}, u32[]{:S(2)}) collective-permute-start(bf16[128,2048]{1,0:T(8,128)(2,1)} %get-tuple-element.616), channel_id=1, source_target_pairs={{0,16},{2,18},{4,20},{6,22},{8,24},{10,26},{12,28},{14,30},{16,0},... | collective-permute-start | bytes 1572872 | tf_op jit(solution)/shard_map/ppermute | solution.py:430
  809.7 109.5 %all-to-all-start.2 = ((bf16[16,16,2048]{2,1,0:T(8,128)(2,1)}), bf16[16,16,2048]{2,1,0:T(8,128)(2,1)}, u32[]{:S(2)}, u32[]{:S(2)}) async-start(bf16[16,16,2048]{2,1,0:T(8,128)(2,1)} %bitcast.399), calls=%async_computation.3 | async-start | bytes 2097152 | tf_op jit(solution)/shard_map/all_to_all | solution.py:475
  816.2 43.9 %collective-permute-start.20 = (bf16[256,2304]{1,0:T(8,128)(2,1)}, bf16[256,2304]{1,0:T(8,128)(2,1)}, u32[]{:S(2)}, u32[]{:S(2)}) collective-permute-start(bf16[256,2304]{1,0:T(8,128)(2,1)} %get-tuple-element.630), channel_id=1, source_target_pairs={{0,4},{2,6},{4,0},{6,2},{8,12},{10,14},{12,8},{14,10},{16,20},{18,... | collective-permute-start | bytes 3538952 | tf_op jit(solution)/shard_map/ppermute | solution.py:430
  818.1 42.0 %collective-permute-start.19 = (bf16[256,2176]{1,0:T(8,128)(2,1)}, bf16[256,2176]{1,0:T(8,128)(2,1)}, u32[]{:S(2)}, u32[]{:S(2)}) collective-permute-start(bf16[256,2176]{1,0:T(8,128)(2,1)} %get-tuple-element.628), channel_id=1, source_target_pairs={{0,8},{2,10},{4,12},{6,14},{8,0},{10,2},{12,4},{14,6},{16,24},{18,... | collective-permute-start | bytes 3342344 | tf_op jit(solution)/shard_map/ppermute | solution.py:430
  819.7 39.0 %collective-permute-start.21 = (f32[16,2048]{1,0:T(8,128)}, f32[16,2048]{1,0:T(8,128)S(1)}, u32[]{:S(2)}, u32[]{:S(2)}) collective-permute-start(f32[16,2048]{1,0:T(8,128)} %get-tuple-element.631), channel_id=1, source_target_pairs={{0,4},{2,6},{4,0},{6,2},{8,12},{10,14},{12,8},{14,10},{16,20},{18,... | collective-permute-start | bytes 393224 | tf_op jit(solution)/shard_map/ppermute | solution.py:430
  866.6 52.6 %collective-permute-start.23 = (bf16[128,2304]{1,0:T(8,128)(2,1)}, bf16[128,2304]{1,0:T(8,128)(2,1)S(1)}, u32[]{:S(2)}, u32[]{:S(2)}) collective-permute-start(bf16[128,2304]{1,0:T(8,128)(2,1)} %get-tuple-element.637), channel_id=1, source_target_pairs={{0,16},{2,18},{4,20},{6,22},{8,24},{10,26},{12,28},{14,30},{16,0},... | collective-permute-start | bytes 1769480 | tf_op jit(solution)/shard_map/ppermute | solution.py:430
  869.2 50.0 %collective-permute-start.22 = (bf16[128,2176]{1,0:T(8,128)(2,1)}, bf16[128,2176]{1,0:T(8,128)(2,1)S(1)}, u32[]{:S(2)}, u32[]{:S(2)}) collective-permute-start(bf16[128,2176]{1,0:T(8,128)(2,1)} %get-tuple-element.635), channel_id=1, source_target_pairs={{0,16},{2,18},{4,20},{6,22},{8,24},{10,26},{12,28},{14,30},{16,0},... | collective-permute-start | bytes 1671176 | tf_op jit(solution)/shard_map/ppermute | solution.py:430
  869.6 27.0 %collective-permute-start.24 = (f32[16,2048]{1,0:T(8,128)S(1)}, f32[16,2048]{1,0:T(8,128)S(1)}, u32[]{:S(2)}, u32[]{:S(2)}) collective-permute-start(f32[16,2048]{1,0:T(8,128)S(1)} %get-tuple-element.638), channel_id=1, source_target_pairs={{0,8},{2,10},{4,12},{6,14},{8,0},{10,2},{12,4},{14,6},{16,24},{18,... | collective-permute-start | bytes 393224 | tf_op jit(solution)/shard_map/ppermute | solution.py:430
  934.7 9.7 %collective-permute-start.25 = (f32[64,512]{1,0:T(8,128)S(1)}, f32[64,512]{1,0:T(8,128)S(1)}, u32[]{:S(2)}, u32[]{:S(2)}) collective-permute-start(f32[64,512]{1,0:T(8,128)S(1)} %dynamic-slice_bitcast_fusion), channel_id=1, source_target_pairs={{0,1},{1,0},{2,3},{3,2},{4,5},{5,4},{6,7},{7,6},{8,9},{9,8},{10,11... | collective-permute-start | bytes 393224 | tf_op jit(solution)/shard_map/ppermute | solution.py:427
  936.2 7.6 collective-permute-start.26
  936.2 17.3 %copy-start.1 = (bf16[2,128,2048]{2,1,0:T(8,128)(2,1)S(1)}, bf16[2,128,2048]{2,1,0:T(8,128)(2,1)}, u32[]{:S(2)}) copy-start(bf16[2,128,2048]{2,1,0:T(8,128)(2,1)} %param.48) | copy-start | bytes 3145732
  943.8 5.0 collective-permute-start.27
  (83 other events, 376.9 us)
Sparse Core Ops, SparseCore 0:
  15.3 172.8 all-gather.4
  189.8 138.4 all-gather.2
  430.8 144.8 reduce-scatter.2
  616.9 133.7 reduce-scatter.4

commit v7 on v6

--- a/solution.py
+++ b/solution.py
@@ -4,6 +4,7 @@
 import jax.numpy as jnp
 from jax import lax
 from jax.experimental import pallas as pl
+from jax.experimental.layout import Layout, with_layout_constraint
 from jax.experimental.pallas import tpu as pltpu
 from jax.sharding import PartitionSpec as P
 
@@ -30,6 +31,10 @@
 
 def outer_sum(left, right):
     return lax.dot_general(left, right, (((0,), (0,)), ((), ())), preferred_element_type=f32)
+
+
+def outer_low(left, right):
+    return with_layout_constraint(outer_sum(left, right).astype(bf16), Layout(major_to_minor=(0, 1)))
 
 
 def rms_scale(values):
@@ -230,9 +235,9 @@
 
     grad, out, gate, signal = grad_ref[...], out_ref[...], gate_ref[...], signal_ref[...]
     position, scale, cross = columns_ref[:, 1:2], columns_ref[:, 2:3], columns_ref[:, 3:4]
-    gate_cols = pl.num_programs(1) * 2 * SHD
     here = pl.multiple_of(pair * 2 * SHD, 2 * SHD)
-    rest = first_ref.shape[1] - others_ref.shape[1] - 2 * NS - STEP_PAD
+    rest = first_ref.shape[1] // 2 - others_ref.shape[1] // 2 - NS - STEP_PAD // 2
+    after_rest = rest + 2 * NS + STEP_PAD
     sig = sigmoid_of(gate)
     silu = gate * sig
     gated = out * silu
@@ -272,7 +277,7 @@
     sums_ref[0, CONV + 1 : CONV + 2, :] = jnp.sum(scaled * gated, axis=0, keepdims=True)
     sums_ref[0, CONV + 2 : CONV + 3, :] = jnp.sum(grad_out * cols, axis=0, keepdims=True)
     sums_ref[0, CONV + 3 : CONV + 4, :] = jnp.zeros((1, cols.shape[1]), f32)
-    first_ref[:, pl.ds(pl.multiple_of(gate_cols + here, 2 * SHD), 2 * SHD)] = grad_signal.astype(bf16)
+    first_ref[:, pl.ds(pl.multiple_of(after_rest + here, 2 * SHD), 2 * SHD)] = grad_signal.astype(bf16)
 
     @pl.when(pair == pl.num_programs(1) - 1)
     def _():
@@ -302,8 +307,8 @@
         head_sums_ref[0, :, 0:1] = jnp.sum(grad_product * step, axis=1, keepdims=True)
         head_sums_ref[0, :, 1:2] = jnp.sum(grad_raw, axis=1, keepdims=True)
         wide = jnp.concatenate([grad_raw, jnp.zeros((STEP_PAD - heads, rows), f32)], axis=0)
-        first_ref[:, rest + 2 * NS : rest + 2 * NS + STEP_PAD] = wide.T.astype(bf16)
-        first_ref[:, rest + 2 * NS + STEP_PAD :] = others_ref[...]
+        first_ref[:, rest + 2 * NS : after_rest] = wide.T.astype(bf16)
+        first_ref[:, first_ref.shape[1] - others_ref.shape[1] :] = others_ref[...]
 
 
 def state_specs(rows, pairs):
@@ -431,7 +436,7 @@
 
     step_padded = jnp.pad(step_weight, ((0, 0), (0, STEP_PAD - step_weight.shape[1])))
     early = dict(
-        gate=mamba_gate, input=mamba_input, state=state_weight, step=step_padded, query=query_weight, key=key_weight,
+        gate=mamba_gate, state=state_weight, step=step_padded, input=mamba_input, query=query_weight, key=key_weight,
         value=value_weight, mix=mamba_out, attn=attention_out,
     )
     late = dict(fgate=feed_gate, fup=feed_up, fdown=feed_down)
@@ -524,7 +529,7 @@
     inner_places = list(range(1, len(masks)))
 
     def core_send(left_parts, right):
-        return outer_sum(left_parts[1], right).astype(bf16)
+        return outer_low(left_parts[1], right)
 
     def halve(kept, place):
         return (
@@ -644,22 +649,22 @@
         grad_mid_norm = project_back(gate_ff_low, full("fgate")) + project_back(up_ff_low, full("fup"))
         grad_gain_mid = jnp.sum(grad_mid_norm * mid32 * mid_scale, axis=0)
         mid_part = rms_back(grad_mid_norm, mid32, mid_scale, gain_middle).astype(bf16)
-        return grad_gain_mid, mid_part, hidden_low, jnp.concatenate([gate_ff_low, up_ff_low], axis=1)
-
-    grad_gain_mid, mid_part, hidden_low, feed_low = unit(feed_forward)
-    mid_other = hand_over(other_lane(mid_part), 3000)
+        return grad_gain_mid, mid_part, hidden_low, (gate_ff_low, up_ff_low), outer_low(whole_grad, hidden_low)
+
+    grad_gain_mid, mid_part, hidden_low, feed_low, part_fdown = unit(feed_forward)
+    sum_fdown = lax.psum_scatter(part_fdown, "dp", scatter_dimension=0, tiled=True)
+    mid_other = hand_over(other_lane(mid_part), 45)
 
     def feed_output():
         ffn_part = project_back(hidden_low, full("fdown")).astype(bf16)
         mid_left = split_left(mid_low)
         return (
-            lane_rows(ffn_part, lane), lane_rows(ffn_part, 1 - lane), mid_left[0], core_send(mid_left, feed_low),
-            outer_sum(whole_grad, hidden_low).astype(bf16),
-        )
-
-    ffn_own, ffn_send, mid_keep, send_feed, part_fdown = unit(feed_output)
-    sum_fdown = lax.psum_scatter(part_fdown, "dp", scatter_dimension=0, tiled=True)
-    feed_came = other_group(send_feed, 1)
+            lane_rows(ffn_part, lane), lane_rows(ffn_part, 1 - lane), mid_left[0],
+            [core_send(mid_left, right) for right in feed_low],
+        )
+
+    ffn_own, ffn_send, mid_keep, send_feed = unit(feed_output)
+    feed_came = [other_group(send, 1) for send in send_feed]
 
     def keep_first(keep, right, came, reductions, sizes):
         kept = (outer_sum(keep, right) + came.astype(f32)).astype(bf16)
@@ -676,6 +681,15 @@
                 red.move(*step)
             else:
                 red.result = step
+
+    mid_other, feed_came = lax.optimization_barrier((mid_other, feed_came))
+    moves = unit(
+        lambda: [
+            keep_first(mid_keep, right, came, (red,), (ff_cols,))[0] for red, right, came in zip(feeds, feed_low, feed_came)
+        ]
+    )
+    for red, move in zip(feeds, moves):
+        red.move(*move)
 
     def branch_backward():
         grad_middle = whole_grad.astype(f32) + (mid_part.astype(f32) + mid_other.astype(f32))
@@ -700,13 +714,16 @@
     cross_own, grad_middle_own, grad_gated_norm, whole_branch, qkv_low = unit(branch_backward)
     cross_other = other_lane(cross_own)
 
-    def second_moves():
-        moves = keep_first(mid_keep, feed_low, feed_came, feeds, (ff_cols, ff_cols))
-        return moves
-
-    moves = unit(second_moves)
-    for red, move in zip(feeds, moves):
-        red.move(*move)
+    ffn_other = other_lane(ffn_send)
+
+    def branch_partial():
+        ffn_out = ffn_own.astype(f32) + ffn_other.astype(f32)
+        out_rows = (lane_rows(whole_mid, lane).astype(f32) + ffn_out).astype(bf16)
+        return outer_low(whole_branch, jnp.concatenate([gated_low, attended_low], axis=1)), deal_order_rows(out_rows)
+
+    part_branch, out_sent = unit(branch_partial)
+    out_moved = exchange(out_sent)
+    sum_branch = lax.psum_scatter(part_branch, "dp", scatter_dimension=0, tiled=True)
 
     def state_space_backward():
         cross = (inv_rms**3) * ((cross_own + cross_other)[:, None] / inner_width)
@@ -720,20 +737,13 @@
 
     column_sums, state_sums, head_sums, first_right = unit(state_space_backward)
 
-    def third_moves():
-        return (
-            core_send(normed_left, first_right),
-            lax.optimization_barrier(ffn_send),
-            [red.step() for red in feeds],
-            sum_fdown.astype(f32),
-            outer_sum(whole_branch, jnp.concatenate([gated_low, attended_low], axis=1)).astype(bf16),
-        )
-
-    send_first, ffn_send, steps, total_fdown, part_branch = unit(third_moves)
-    sum_branch = lax.psum_scatter(part_branch, "dp", scatter_dimension=0, tiled=True)
+    total_fdown_low = [sum_fdown]
+    order[0], total_fdown_low = lax.optimization_barrier((order[0], total_fdown_low))
+    send_first, steps, block_out = unit(
+        lambda: (core_send(normed_left, first_right), [red.step() for red in feeds], deal_take(out_moved))
+    )
     settle(feeds, steps)
     first_came = other_group(send_first, 1)
-    ffn_other = other_lane(ffn_send)
 
     def input_gradient():
         grad_normed = project_back(first_right, lax.slice_in_dim(whole["early"], 0, first_right.shape[1], axis=1))
@@ -744,12 +754,11 @@
     grad_gain_in, in_own, in_send = unit(input_gradient)
 
     firsts = (red_low, red_high)
-    first_sizes = (first_right.shape[1] // 256 * 128, first_right.shape[1] - first_right.shape[1] // 256 * 128)
+    low_size = gate_cols + 2 * NS + STEP_PAD
+    first_sizes = (low_size, first_right.shape[1] - low_size)
 
     def first_moves():
         moves = keep_first(normed_left[0], first_right, first_came, firsts, first_sizes)
-        ffn_out = ffn_own.astype(f32) + ffn_other.astype(f32)
-        out_rows = (lane_rows(whole_mid, lane).astype(f32) + ffn_out).astype(bf16)
         head_row = (jnp.sum(head_sums, axis=0).T * jnp.stack([rate, jnp.ones_like(rate)])).reshape(1, -1)
         flat = jnp.concatenate(
             [
@@ -757,39 +766,74 @@
                 grad_gain_in[None, :], grad_gain_mid[None, :], jnp.pad(head_row, ((0, 5), (0, width - head_row.shape[1]))),
             ]
         )
-        return moves, lax.optimization_barrier(in_send), deal_order_rows(out_rows), [red.step() for red in feeds], flat
-
-    moves, in_send, out_sent, steps, flat = unit(first_moves)
+        return moves, lax.optimization_barrier(in_send), [red.step() for red in feeds], flat
+
+    moves, in_send, steps, flat = unit(first_moves)
     flat_moved = other_group(flat, masks[0])
     settle(feeds, steps)
-    out_moved = exchange(out_sent)
     for red, move in zip(firsts, moves):
         red.move(*move)
-    in_other = other_lane(in_send)
+    in_other = hand_over(other_lane(in_send), 6)
+
+    flat = unit(lambda: flat + flat_moved)
+    flat_moved = other_group(flat, masks[1])
 
     def send_input():
         in_sum = in_own.astype(f32) + in_other.astype(f32)
         return deal_order_rows((in_sum + grad_middle_own).astype(bf16))
 
+    in_moved = None
     everything = [*feeds, *firsts]
-    in_moved = None
-    bits = 1
+    query_cols, key_cols = query_weight.shape[1], key_weight.shape[1]
+
+    bits = 2
+
+    def finish():
+        low, high = red_low.result, red_high.result
+        state_rows = low[:, gate_cols : gate_cols + 2 * NS].reshape(lanes, shard // lanes, 2 * NS)
+        cut = [0, gate_cols, gate_cols + query_cols, gate_cols + query_cols + key_cols, high.shape[1]]
+        pieces = (
+            low[:, :gate_cols], low[:, gate_cols + 2 * NS : gate_cols + 2 * NS + heads],
+            [high[:, start:stop] for start, stop in zip(cut, cut[1:])],
+            [lax.dynamic_index_in_dim(state_rows, which, 0, keepdims=False) for which in (lane, 1 - lane)],
+        )
+        return pieces, deal_take(in_moved)
+
+    arrived = [red.came for red in feeds] + [sum_branch]
+    order[0], arrived = lax.optimization_barrier((order[0], arrived))
+    for red, came in zip(feeds, arrived):
+        red.came = came
+    wides = None
     while pending := [red for red in everything if not hasattr(red, "result")]:
-        last = all(red.stage == len(red.places) for red in pending)
-        steps, flat, other = unit(
-            lambda: (
-                [red.step() for red in pending],
-                flat + flat_moved if bits <= len(masks) else flat,
-                (deal_take(in_moved), deal_take(out_moved), sum_branch.astype(f32)) if last else send_input() if in_moved is None else (),
-            )
-        )
-        settle(pending, steps)
+        if in_moved is None:
+            pending = list(firsts)
+        widen = in_moved is not None and wides is None
+        last = all(red.stage == len(red.places) for red in pending) and in_moved is not None
+
+        def round_work():
+            steps = [red.step() for red in pending]
+            added = flat + flat_moved if bits <= len(masks) else flat
+            wide = [arrived[-1].astype(f32), total_fdown_low[0].astype(f32)] if widen else ()
+            if last:
+                for red, step in zip(pending, steps):
+                    red.result = step
+                return steps, added, wide, finish()
+            return steps, added, wide, send_input() if in_moved is None else ()
+
+        steps, flat, wide, other = unit(round_work)
+        if widen:
+            wides = wide
         if bits < len(masks):
             flat_moved = other_group(flat, masks[bits])
         bits += 1
+        if last:
+            break
+        settle(pending, steps)
         if in_moved is None:
             in_moved = exchange(other)
-    grad_input, block_out, total_branch = other
+    for red, step in zip(pending, steps):
+        red.result = step
+    (total_gate, total_step, (total_input, total_query, total_key, total_value), states), grad_input = other
     while bits <= len(masks):
         flat = flat + flat_moved
         if bits < len(masks):
@@ -802,29 +846,18 @@
     def joined(row, start, count):
         return jnp.concatenate([low[row, start : start + count], high[row, start : start + count]])
 
-    gate_width = mamba_gate.shape[1]
     sum_gin, sum_gmid = both[8], both[9]
-    sum_kst = both[: CONV + 1, gate_width : gate_width + 2 * NS]
-    sum_kin = jnp.concatenate([low[: CONV + 1, :gate_width], high[: CONV + 1, :gate_width]], axis=1)
-    sum_mix = joined(CONV + 1, 0, gate_width)
-    sum_skip = jnp.sum(joined(CONV + 2, 0, gate_width).reshape(SH, SHD), axis=1)
+    sum_kst = both[: CONV + 1, gate_cols : gate_cols + 2 * NS]
+    sum_kin = jnp.concatenate([low[: CONV + 1, :gate_cols], high[: CONV + 1, :gate_cols]], axis=1)
+    sum_mix = joined(CONV + 1, 0, gate_cols)
+    sum_skip = jnp.sum(joined(CONV + 2, 0, gate_cols).reshape(SH, SHD), axis=1)
     sum_bias = joined(10, heads, heads)
     sum_rate = joined(10, 0, heads)
 
-    query_cols, key_cols = query_weight.shape[1], key_weight.shape[1]
     total_fgate, total_fup = red_fgate.result, red_fup.result
+    total_branch, total_fdown = wides
     total_mix, total_attn = total_branch[:, :gate_cols], total_branch[:, gate_cols:]
-    rest = jnp.concatenate([red.result for red in firsts], axis=1)
-    total_gate, total_input, rest = rest[:, :gate_cols], rest[:, gate_cols : 2 * gate_cols], rest[:, 2 * gate_cols :]
-    total_step = rest[:, 2 * NS : 2 * NS + heads]
-    start = 2 * NS + STEP_PAD
-    total_query = rest[:, start : start + query_cols]
-    total_key = rest[:, start + query_cols : start + query_cols + key_cols]
-    total_value = rest[:, start + query_cols + key_cols :]
-    state_rows = rest[:, : 2 * NS].reshape(lanes, shard // lanes, 2 * NS)
-    state_own = lax.dynamic_index_in_dim(state_rows, lane, 0, keepdims=False)
-    state_send = lax.dynamic_index_in_dim(state_rows, 1 - lane, 0, keepdims=False)
-    state_lane = state_own + other_lane(state_send)
+    state_lane = states[0] + other_lane(states[1])
     return (
         block_out,
         grad_input,

time: 971 us -> 924 us (0.952)
  waiting for transfers between devices: 407 us -> 368 us
  local copies, waits for them, and re-layouts: 108 us -> 88.6 us
  Pallas kernels: 65.3 us -> 81.6 us
    ppermute x18 -> x19, waiting for transfers between devices: 223 us -> 175 us  [other_group(): return lax.ppermute(values, 'dp', [(i, i ^ bits) for i in range(groups)])]
    ppermute x10, waiting for transfers between devices: 73.2 us -> 91.4 us  [other_lane(): return lax.ppermute(values, 'tensor', swap_lane)]
    pallas_call x1, Pallas kernels: 20.5 us -> 36.3 us  [state_forward(): pl.pallas_call(state_forward_kernel, out_shape=(jax.ShapeDtypeStruct((tot...]
    cond x3 -> x1, local copies, waits for them, and re-layouts: 15.2 us -> 1.41 us  [unit(): lax.cond(order[0], work, lambda: jax.tree.map(lambda leaf: jnp.zeros(leaf...]
    ppermute x18 -> x19, starting transfers between devices: 29.4 us -> 33.8 us  [other_group(): return lax.ppermute(values, 'dp', [(i, i ^ bits) for i in range(groups)])]
    dot_general x10 -> x12, matrix products: 66.8 us -> 68.6 us  [outer_sum(): lax.dot_general(left, right, (((0,), (0,)), ((), ())), preferred_element_...]
  transfers between devices with their start and end apart: 36 -> 37, of which waited for: 18 -> 14; matrix products, arithmetic and copies ran while one was open for 29% -> 31% of each run, Pallas kernels for 7% -> 9%
where the time goes in v7:
time: 924 us; the launch traced here: 914 us
  waiting for transfers between devices  368 us (40%)
  matrix products  199 us (22%)
  other arithmetic  93.2 us (10%)
  local copies, waits for them, and re-layouts  88.6 us (10%)
  Pallas kernels  81.6 us (9%)
  starting transfers between devices  64.7 us (7%)
  between operations  16 us (2%)
    ppermute x19, waiting for transfers between devices, other_group(): return lax.ppermute(values, 'dp', [(i, i ^ bits) for i in range(groups)])  175 us
    ppermute x10, waiting for transfers between devices, other_lane(): return lax.ppermute(values, 'tensor', swap_lane)  91.4 us
    dot_general x16, matrix products, project(): return jnp.dot(left, right, preferred_element_type=f32)  70.9 us
    all_to_all x4, waiting for transfers between devices, exchange(): lax.all_to_all(buffer.reshape(groups, micro * per, width), 'dp', split_ax...  69.8 us
    dot_general x12, matrix products, outer_sum(): lax.dot_general(left, right, (((0,), (0,)), ((), ())), preferred_element_...  68.6 us
    dot_general x6, matrix products, project_back(): lax.dot_general(left, right, (((1,), (1,)), ((), ())), preferred_element_...  51.6 us
    pallas_call x1, Pallas kernels, state_forward(): pl.pallas_call(state_forward_kernel, out_shape=(jax.ShapeDtypeStruct((tot...  36.3 us
    pallas_call x1, Pallas kernels, state_backward(): pl.pallas_call(state_backward_kernel, out_shape=(jax.ShapeDtypeStruct((to...  34.5 us
  transfers between devices with their start and end apart: 37, of which 14 were waited for; matrix products, arithmetic and copies ran while one was open for 31% of the time, Pallas kernels for 9%

profile of v7, /device:TPU:0, one launch (start us, length us, event | category | flops | bytes accessed | tf_op | source)
XLA Modules:
  0.0 913.7 jit_solution(8524597690648973683)
XLA Ops:
  18.0 4.9 select_reduce_fusion
  24.6 7.4 all-to-all-start
  33.7 38.2 %all-to-all-done = bf16[16,16,2048]{2,1,0:T(8,128)(2,1)S(1)} async-done(((bf16[16,16,2048]{2,1,0:T(8,128)(2,1)}), bf16[16,16,2048]{2,1,0:T(8,128)(2,1)S(1)}, u32[]{:S(2)}, u32[]{:S(2)}) %all-to-all-start) | async-done | bytes 1048608 | tf_op jit(solution)/shard_map/all_to_all | solution.py:480
  71.9 3.7 all-to-all-start.1
  83.8 31.6 %all-to-all-done.1 = bf16[16,16,2048]{2,1,0:T(8,128)(2,1)S(1)} async-done(((bf16[16,16,2048]{2,1,0:T(8,128)(2,1)}), bf16[16,16,2048]{2,1,0:T(8,128)(2,1)S(1)}, u32[]{:S(2)}, u32[]{:S(2)}) %all-to-all-start.1) | async-done | bytes 1048608 | tf_op jit(solution)/shard_map/all_to_all | solution.py:480
  121.2 20.0 %collective-permute-done.1 = bf16[256,2048]{1,0:T(8,128)(2,1)S(1)} collective-permute-done((bf16[256,2048]{1,0:T(8,128)(2,1)S(1)}, bf16[256,2048]{1,0:T(8,128)(2,1)S(1)}, u32[]{:S(2)}, u32[]{:S(2)}) %collective-permute-start.1) | collective-permute-done | bytes 1048608 | tf_op jit(solution)/shard_map/ppermute | solution.py:432
  146.5 6.7 pick_halves.3
  153.2 3.3 multiply_convert_fusion.4
  156.5 31.7 %all-gather.5.cloned.1.call-done = bf16[2048,6528]{1,0:T(8,128)(2,1)} async-done(((bf16[128,6528]{1,0:T(8,128)(2,1)}), bf16[2048,6528]{1,0:T(8,128)(2,1)}) %all-gather.5.cloned.1.call-update) | async-done | bytes 26738704 | tf_op jit(solution)/shard_map/all_gather | solution.py:449
  196.8 4.0 copy.227
  200.8 3.5 fusion.121
  216.0 8.0 fusion.68.gate_ref
  224.0 8.0 fusion.70.signal_ref
  232.1 36.3 %state_forward.1 = (f32[512,1536]{1,0:T(8,128)}, f32[512,128]{1,0:T(8,128)}) custom-call(f32[512,1536]{1,0:T(8,128)} %fusion.70.signal_ref, f32[512,1536]{1,0:T(8,128)} %fusion.68.gate_ref, f32[5,1536]{1,0:T(8,128)} %taps_ref.1, f32[1,1536]{1,0:T(1,128)S(1)} %broadcast_in_dim_reshape.2.skip_ref, bf16[512,512]{1,0:T(8,128)(2,1)S(1)} %copy-done.19, ...), custom_call_target="tpu_custom_call" | custom-call | flops 1610612736 | bytes 9437184 | tf_op jit(solution)/shard_map/state_forward/pallas_call | solution.py:332
  278.6 4.0 multiply_convert_fusion.6
  282.6 6.2 fusion.66
  294.3 45.6 %collective-permute-done.3 = bf16[512,2048]{1,0:T(8,128)(2,1)} collective-permute-done((bf16[512,2048]{1,0:T(8,128)(2,1)S(1)}, bf16[512,2048]{1,0:T(8,128)(2,1)}, u32[]{:S(2)}, u32[]{:S(2)}) %collective-permute-start.3) | collective-permute-done | bytes 2097184 | tf_op jit(solution)/shard_map/ppermute | solution.py:432
  339.9 6.1 fusion.102
  348.5 55.3 %conditional.13 = (f32[2048]{0:T(1024)S(1)}, bf16[512,2048]{1,0:T(8,128)(2,1)}, bf16[512,2048]{1,0:T(8,128)(2,1)}, bf16[512,2048]{1,0:T(8,128)(2,1)}, bf16[512,2...) conditional(s32[]{:T(128)} %convert_element_type.542, () %tuple.133, (bf16[2048,6144]{1,0:T(8,128)(2,1)}, ...), branch_computations={%region_9.10_spmd, %region_10.13_spmd} | conditional | flops 25802309632 | bytes 241219728 | solution.py:572
  348.5 7.7 fusion
  356.2 3.5 copy-done.114
  359.7 6.1 fusion.4
  365.8 10.8 %multiply_convert_fusion = (bf16[512,2048]{1,0:T(8,128)(2,1)}, bf16[512,2048]{1,0:T(8,128)(2,1)}, bf16[512,2048]{1,0:T(8,128)(2,1)}) fusion(f32[512,2048]{1,0:T(8,128)} %fusion.4, f32[512,2048]{1,0:T(8,128)S(1)} %fusion, bf16[512,2048]{1,0:T(8,128)(2,1)S(1)} %get-tuple-element.313, bf16[2048,6144]{1,0:T(8,128)(2,1)} %get-tuple-element.312), kind=kOutput, calls=%fused_computation.11 | convolution fusion | flops 4310695936 | bytes 25165824 | tf_op jit(solution)/shard_map/cond/branch_1_fun/dot_general | solution.py:25
  376.6 7.8 fusion.2
  384.4 8.5 multiply_reduce_fusion
  395.0 8.4 convert_bitcast_fusion
  404.9 26.4 %conditional.14 = (bf16[256,2048]{1,0:T(8,128)(2,1)S(1)}, bf16[256,2048]{1,0:T(8,128)(2,1)}, bf16[512,1024]{1,0:T(8,128)(2,1)}, bf16[1024,2048]{1,0:T(8,128)(2,1)}, bf16[1024,2048]{1,0:T(8,128)(2,1)}) conditional(s32[]{:T(128)} %convert_element_type.575, () %tuple.137, (bf16[2048,6144]{1,0:T(8,128)(2,1)}, bf16[512,2048]{1,0:T(8,128)(2,1)}, ...), branch_computations={%region_13.14_spmd, %region_14.15_spmd} | conditional | flops 8595177472 | bytes 39846044 | solution.py:572
  405.0 8.6 fusion.18
  414.6 4.0 pick_halves.2
  418.7 6.5 convolution_convert_fusion
  425.2 6.2 convolution_convert_fusion.1
  433.4 19.9 %collective-permute-done.4.values_ref = bf16[512,2048]{1,0:T(8,128)(2,1)} collective-permute-done((bf16[512,2048]{1,0:T(8,128)(2,1)}, bf16[512,2048]{1,0:T(8,128)(2,1)}, u32[]{:S(2)}, u32[]{:S(2)}) %collective-permute-start.4) | collective-permute-done | bytes 2097184 | tf_op jit(solution)/shard_map/ppermute | solution.py:432
  453.4 17.3 %conditional.15 = (bf16[512,2048]{1,0:T(8,128)(2,1)}, bf16[1,2,2,128,2048]{4,3,2,1,0:T(8,128)(2,1)}, bf16[512,2048]{1,0:T(8,128)(2,1)}, bf16[2,1,2,128,2048]{4,3,2,1,0:T(8,128)(2,1)}) conditional(s32[]{:T(128)} %convert_element_type.576, () %tuple.140, (bf16[512,1024]{1,0:T(8,128)(2,1)}, bf16[512,2048]{1,0:T(8,128)(2,1)}, ...), branch_computations={%region_15.16_spmd, %region_16.17_spmd} | conditional | flops 4307550208 | bytes 39845920 | solution.py:572
  453.6 6.4 add_convert_fusion
  462.5 5.5 add_convert_fusion.1
  471.8 11.5 %collective-permute-start.10 = (bf16[512,2048]{1,0:T(8,128)(2,1)}, bf16[512,2048]{1,0:T(8,128)(2,1)}, u32[]{:S(2)}, u32[]{:S(2)}) collective-permute-start(bf16[512,2048]{1,0:T(8,128)(2,1)} %get-tuple-element.623), channel_id=1, source_target_pairs={{0,8},{2,10},{4,12},{6,14},{8,0},{10,2},{12,4},{14,6},{16,24},{18,... | collective-permute-start | bytes 6291464 | tf_op jit(solution)/shard_map/ppermute | solution.py:435
  486.8 38.7 %conditional.16 = (f32[512]{0:T(512)S(1)}, f32[256,2048]{1,0:T(8,128)}, f32[512,1536]{1,0:T(8,128)}, bf16[512,2048]{1,0:T(8,128)(2,1)}, bf16[512,512]{0,1:T(8,12...) conditional(s32[]{:T(128)} %convert_element_type.577, () %tuple.144, ...), branch_computations={%region_17.18_spmd, %region_18.21_spmd} | conditional | flops 4850349568 | bytes 97149264 | solution.py:572
  487.0 7.2 fusion.101
  494.2 3.5 fusion.29
  511.5 3.3 constant_dynamic-slice_fusion.2
  514.9 10.0 %multiply_reduce_fusion.2 = (f32[512]{0:T(512)S(1)}, f32[512,1536]{1,0:T(8,128)}) fusion(f32[512,1536]{1,0:T(8,128)S(1)} %copy-done.11, f32[512,1536]{1,0:T(8,128)} %get-tuple-element.339, f32[1536]{0:T(1024)S(1)} %get-tuple-element.337, bf16[512,2048]{1,0:T(8,128)(2,1)} %get-tuple-element.1221, bf16[2048,6528]{1,0:T(8,128)(2,1)} %get-tuple-element.336), kind=kOutput, calls=%fused_computation.36 | convolution fusion | flops 3227516416 | bytes 17833984 | tf_op jit(solution)/shard_map/cond/branch_1_fun/dot_general | solution.py:25
  526.1 12.2 %conditional.17 = (bf16[2048,2048]{1,0:T(8,128)(2,1)}, bf16[256,2048]{0,1:T(8,128)(2,1)S(1)}) conditional(s32[]{:T(128)} %convert_element_type.578, () %tuple.147, (bf16[512,1536]{1,0:T(8,128)(2,1)}, bf16[512,512]{1,0:T(8,128)(2,1)}, bf16[512,2048]{1,0:T(8,128)(2,1)}, bf16[512,2048]{1,0:T(8,128)(2,1)S(1)}, s32[]{:T(128)}, ...), branch_computations={%region_21.22_spmd, %region_22.23_spmd} | conditional | flops 4575461376 | bytes 31588488 | solution.py:572
  529.8 8.5 convert_bitcast_fusion.1
  539.7 3.7 all-to-all-start.2
  547.7 42.0 %conditional.18 = (f32[2,8,1536]{2,1,0:T(8,128)}, f32[2,8,512]{2,1,0:T(8,128)}, f32[2,24,2]{2,1,0:T(8,128)}, bf16[512,4480]{1,0:T(8,128)(2,1)}) conditional(s32[]{:T(128)} %convert_element_type.580, () %tuple.150, (f32[1536]{0:T(1024)S(1)}, f32[512]{0:T(512)S(1)}, f32[512]{0:T(512)S(1)}, f32[512]{0:T(512)S(1)}, f32[512,2]{0,1:T(2,128)S(1)}, ...), branch_computations={%region_23.24_spmd, %region_24.25_spmd} | conditional | flops 4028946944 | bytes 18723964 | solution.py:572
  555.2 34.5 %state_backward.1 = (bf16[512,4480]{1,0:T(8,128)(2,1)}, f32[2,8,1536]{2,1,0:T(8,128)}, f32[2,8,512]{2,1,0:T(8,128)}, f32[2,24,2]{2,1,0:T(8,128)}) custom-call(f32[512,1536]{1,0:T(8,128)} %get-tuple-element.356.grad_ref, f32[512,1536]{1,0:T(8,128)} %get-tuple-element.357.out_ref, f32[512,1536]{1,0:T(8,128)} %get-tuple-element.358.gate_ref, ...), custom_call_target="tpu_custom_call" | custom-call | flops 4026531840 | bytes 15728640 | tf_op jit(solution)/shard_map/cond/branch_1_fun/state_backward/pallas_call | solution.py:357
  589.9 20.7 %conditional.19 = (bf16[1024,4480]{1,0:T(8,128)(2,1)}, bf16[256,2048]{1,0:T(8,128)(2,1)}, bf16[1,1,2,128,2048]{4,3,2,1,0:T(8,128)(2,1)S(1)}, bf16[256,2048]{1,0:...) conditional(s32[]{:T(128)} %convert_element_type.581, () %tuple.154, ...), branch_computations={%region_26.27_spmd, %region_27.28_spmd} | conditional | flops 4979556352 | bytes 42205260 | solution.py:572
  590.3 3.8 fusion.49
  599.2 9.9 %convolution_convert_fusion.3 = bf16[1024,4480]{1,0:T(8,128)(2,1)} fusion(bf16[512,1024]{1,0:T(8,128)(2,1)S(1)} %copy-done.115, bf16[512,4480]{1,0:T(8,128)(2,1)} %get-tuple-element.386), kind=kOutput, calls=%fused_computation.82 | convolution fusion | flops 4702208000 | bytes 14811136 | tf_op jit(solution)/shard_map/cond/branch_1_fun/dot_general | solution.py:33
  613.9 23.0 %conditional.20 = (f32[2048]{0:T(1024)S(1)}, bf16[256,2048]{1,0:T(8,128)(2,1)}, bf16[256,2048]{1,0:T(8,128)(2,1)S(1)}) conditional(s32[]{:T(128)} %convert_element_type.583, () %tuple.157, (bf16[2048,6528]{1,0:T(8,128)(2,1)}, bf16[512,4480]{1,0:T(8,128)(2,1)}, f32[512,2048]{1,0:T(8,128)}, f32[2,2,128]{2,1,0:T(2,128)S(1)}, f32[512,1]{0,1:T(1,128)S(1)}, ...), branch_computations={%region_28.29_spmd, %region_29.32_spmd} | conditional | flops 9406776320 | bytes 46053484 | solution.py:572
  613.9 17.5 %multiply_reduce_fusion.3 = (f32[512]{0:T(512)S(1)}, f32[2048]{0:T(1024)S(1)}, f32[512,2048]{1,0:T(8,128)}) fusion(f32[512,2048]{1,0:T(8,128)} %get-tuple-element.395, f32[2048]{0:T(1024)S(1)} %get-tuple-element.399, f32[512]{0:T(512)S(1)} %bitcast.447, bf16[512,4480]{1,0:T(8,128)(2,1)} %get-tuple-element.393, bf16[2048,6528]{1,0:T(8,128)(2,1)} %get-tuple-element.394), kind=kOutput, calls=%fused_computation.91 | convolution fusion | flops 9401530368 | bytes 31346688 | tf_op jit(solution)/shard_map/cond/branch_1_fun/dot_general | solution.py:29
  631.5 4.3 subtract_convert_fusion.3
  636.9 13.0 %collective-permute-done.12 = bf16[256,2048]{1,0:T(8,128)(2,1)} collective-permute-done((bf16[256,2048]{1,0:T(8,128)(2,1)}, bf16[256,2048]{1,0:T(8,128)(2,1)}, u32[]{:S(2)}, u32[]{:S(2)}) %collective-permute-start.12) | collective-permute-done | bytes 1048608 | tf_op jit(solution)/shard_map/ppermute | solution.py:435
  649.9 22.8 %conditional.21 = (bf16[512,2176]{1,0:T(8,128)(2,1)}, bf16[1,2,2,128,2176]{4,3,2,1,0:T(8,128)(2,1)}, bf16[512,2304]{1,0:T(8,128)(2,1)}, bf16[2,1,2,128,2304]{4,3...) conditional(s32[]{:T(128)} %convert_element_type.584, ...), branch_computations={%region_32.33_spmd, %region_33.37_spmd} | conditional | flops 4715790336 | bytes 59525208 | solution.py:572
  650.1 9.4 %add_convert_fusion.4 = bf16[1024,4480]{1,0:T(8,128)(2,1)S(1)} fusion(bf16[1024,4480]{1,0:T(8,128)(2,1)} %get-tuple-element.403, bf16[512,1024]{1,0:T(8,128)(2,1)} %get-tuple-element.401, bf16[512,4480]{1,0:T(8,128)(2,1)} %get-tuple-element.402), kind=kOutput, calls=%fused_computation.99 | convolution fusion | flops 4711383040 | bytes 23986176 | tf_op jit(solution)/shard_map/cond/branch_1_fun/dot_general | solution.py:33
  681.9 55.3 %collective-permute-done.15 = bf16[128,2048]{1,0:T(8,128)(2,1)} collective-permute-done((bf16[128,2048]{1,0:T(8,128)(2,1)}, bf16[128,2048]{1,0:T(8,128)(2,1)}, u32[]{:S(2)}, u32[]{:S(2)}) %collective-permute-start.15) | collective-permute-done | bytes 524320 | tf_op jit(solution)/shard_map/ppermute | solution.py:435
  739.0 9.2 %collective-permute-done.16 = bf16[128,2048]{1,0:T(8,128)(2,1)} collective-permute-done((bf16[128,2048]{1,0:T(8,128)(2,1)}, bf16[128,2048]{1,0:T(8,128)(2,1)}, u32[]{:S(2)}, u32[]{:S(2)}) %collective-permute-start.16) | collective-permute-done | bytes 524320 | tf_op jit(solution)/shard_map/ppermute | solution.py:435
  750.4 13.1 %conditional.23 = (bf16[256,2176]{1,0:T(8,128)(2,1)}, bf16[1,1,2,128,2176]{4,3,2,1,0:T(8,128)(2,1)}, bf16[256,2304]{1,0:T(8,128)(2,1)}, bf16[1,1,2,128,2304]{4,3...) conditional(s32[]{:T(128)} %convert_element_type.586, () %tuple.167, ...), branch_computations={%region_40.41_spmd, %region_41.42_spmd} | conditional | flops 280788992 | bytes 38142112 | solution.py:572
  764.8 4.8 all-to-all-start.3
  773.6 42.7 %collective-permute-done.23 = f32[16,2048]{1,0:T(8,128)S(1)} collective-permute-done((f32[16,2048]{1,0:T(8,128)}, f32[16,2048]{1,0:T(8,128)S(1)}, u32[]{:S(2)}, u32[]{:S(2)}) %collective-permute-start.23) | collective-permute-done | bytes 131104 | tf_op jit(solution)/shard_map/ppermute | solution.py:435
  816.3 11.5 %conditional.24 = (f32[128,2048]{1,0:T(8,128)}, f32[128,2048]{1,0:T(8,128)}, bf16[128,2176]{1,0:T(8,128)(2,1)}, bf16[1,1,1,128,2176]{4,3,2,1,0:T(8,128)(2,1)S(1)...) conditional(s32[]{:T(128)} %convert_element_type.587, ...), branch_computations={%region_42.43_spmd, %region_43.44_spmd} | conditional | flops 6455296 | bytes 24969408 | solution.py:572
  821.5 3.3 fusion.62
  833.3 52.7 %collective-permute-done.24 = f32[16,2048]{1,0:T(8,128)S(1)} collective-permute-done((f32[16,2048]{1,0:T(8,128)S(1)}, f32[16,2048]{1,0:T(8,128)S(1)}, u32[]{:S(2)}, u32[]{:S(2)}) %collective-permute-start.24) | collective-permute-done | bytes 131104 | tf_op jit(solution)/shard_map/ppermute | solution.py:435
  886.0 8.1 conditional.25
  (498 shorter events, 209.9 us)
Async XLA Ops:
  7.2 16.0 %copy-start = (bf16[2,128,2048]{2,1,0:T(8,128)(2,1)S(1)}, bf16[2,128,2048]{2,1,0:T(8,128)(2,1)}, u32[]{:S(2)}) copy-start(bf16[2,128,2048]{2,1,0:T(8,128)(2,1)} %param.52) | copy-start | bytes 3145732
  7.2 180.9 %all-gather.5.cloned.1.call-start = ((), (), s32[]{:S(2)}) async-start(), calls=%async_computation.7 | async-start | bytes 28409856 | tf_op jit(solution)/shard_map/all_gather | solution.py:449
  15.2 332.6 %all-gather.3.cloned.1.call-start = ((), (), s32[]{:S(2)}) async-start(), calls=%async_computation.6 | async-start | bytes 26738688 | tf_op jit(solution)/shard_map/all_gather | solution.py:449
  23.2 57.5 %copy-start.96 = (s32[256]{0:T(256)}, s32[256]{0:T(256)S(1)}, u32[]{:S(2)}) copy-start(s32[256]{0:T(256)S(1)} %get-tuple-element.1173) | copy-start | bytes 3076
  24.6 47.3 %all-to-all-start = ((bf16[16,16,2048]{2,1,0:T(8,128)(2,1)}), bf16[16,16,2048]{2,1,0:T(8,128)(2,1)S(1)}, u32[]{:S(2)}, u32[]{:S(2)}) async-start(bf16[16,16,2048]{2,1,0:T(8,128)(2,1)} %bitcast.111), calls=%async_computation | async-start | bytes 2097152 | tf_op jit(solution)/shard_map/all_to_all | solution.py:480
  32.2 50.7 %copy-start.83 = (f32[1,2,2,128]{3,1,2,0:T(2,128)}, f32[1,2,2,128]{3,1,2,0:T(2,128)S(1)}, u32[]{:S(2)}) copy-start(f32[1,2,2,128]{3,1,2,0:T(2,128)S(1)} %copy.266) | copy-start | bytes 6148
  32.2 46.5 %copy-start.113 = (f32[24]{0:T(128)S(1)}, f32[24]{0:T(128)}, u32[]{:S(2)}) copy-start(f32[24]{0:T(128)} %param.74) | copy-start | bytes 292
  32.2 47.3 %copy-start.117 = (s32[16]{0:T(128)S(1)}, s32[16]{0:T(128)}, u32[]{:S(2)}) copy-start(s32[16]{0:T(128)} %constant.243.clone) | copy-start | bytes 196
  32.2 47.8 %copy-start.70 = (f32[5,512]{1,0:T(8,128)S(1)}, f32[5,512]{1,0:T(8,128)}, u32[]{:S(2)}) copy-start(f32[5,512]{1,0:T(8,128)} %param.70) | copy-start | bytes 30724
  71.9 43.5 %all-to-all-start.1 = ((bf16[16,16,2048]{2,1,0:T(8,128)(2,1)}), bf16[16,16,2048]{2,1,0:T(8,128)(2,1)S(1)}, u32[]{:S(2)}, u32[]{:S(2)}) async-start(bf16[16,16,2048]{2,1,0:T(8,128)(2,1)} %bitcast.117), calls=%async_computation.1 | async-start | bytes 2097152 | tf_op jit(solution)/shard_map/all_to_all | solution.py:480
  75.5 514.3 %reduce-scatter.3.cloned.1.call-start = ((), (), s32[]{:S(2)}) async-start(), calls=%async_computation.8 | async-start | bytes 8912896 | tf_op jit(solution)/shard_map/reduce_scatter | solution.py:655
  78.8 153.2 %copy-start.67 = (f32[1,1536]{1,0:T(1,128)}, f32[1,1536]{1,0:T(1,128)S(1)}, u32[]{:S(2)}) copy-start(f32[1,1536]{1,0:T(1,128)S(1)} %broadcast_in_dim_reshape.2.skip_ref) | copy-start | bytes 18436
  81.1 38.2 %collective-permute-start = (bf16[256,2048]{1,0:T(8,128)(2,1)S(1)}, bf16[256,2048]{1,0:T(8,128)(2,1)S(1)}, u32[]{:S(2)}, u32[]{:S(2)}) collective-permute-start(bf16[256,2048]{1,0:T(8,128)(2,1)S(1)} %convolution_convert_fusion.9), channel_id=1, source_target_pairs={{0,1},{1,0},{2,3},{3,2},{4,5},{5,4},{6,7},{7,6},{8,9},{9,8},{10,11... | collective-permute-start | bytes 3145736 | tf_op jit(solution)/shard_map/ppermute | solution.py:432
  116.5 24.7 %collective-permute-start.1 = (bf16[256,2048]{1,0:T(8,128)(2,1)S(1)}, bf16[256,2048]{1,0:T(8,128)(2,1)S(1)}, u32[]{:S(2)}, u32[]{:S(2)}) collective-permute-start(bf16[256,2048]{1,0:T(8,128)(2,1)S(1)} %convolution_convert_fusion.7), channel_id=1, source_target_pairs={{0,1},{1,0},{2,3},{3,2},{4,5},{5,4},{6,7},{7,6},{8,9},{9,8},{10,11... | collective-permute-start | bytes 3145736 | tf_op jit(solution)/shard_map/ppermute | solution.py:432
  153.2 35.0 %copy-start.3 = (bf16[512,2048]{1,0:T(8,128)(2,1)S(1)}, bf16[512,2048]{1,0:T(8,128)(2,1)}, u32[]{:S(2)}) copy-start(bf16[512,2048]{1,0:T(8,128)(2,1)} %multiply_convert_fusion.5.first_ref.second_ref) | copy-start | bytes 6291460
  156.5 34.0 %copy-start.106 = (f32[24]{0:T(128)S(1)}, f32[24]{0:T(128)}, u32[]{:S(2)}) copy-start(f32[24]{0:T(128)} %exponential_negate_fusion) | copy-start | bytes 292
  193.7 16.5 %copy-start.60 = (f32[3,2,8,256]{3,2,0,1:T(8,128)}, f32[3,2,8,256]{3,2,0,1:T(8,128)S(1)}, u32[]{:S(2)}) copy-start(f32[3,2,8,256]{3,2,0,1:T(8,128)S(1)} %copy.277) | copy-start | bytes 147460
  210.1 61.0 %copy-start.35 = (bf16[512,1,64]{2,0,1:T(8,128)(2,1)}, bf16[512,1,64]{2,0,1:T(8,128)(2,1)S(1)}, u32[]{:S(2)}) copy-start(bf16[512,1,64]{2,0,1:T(8,128)(2,1)S(1)} %copy.256) | copy-start | bytes 196612
  210.2 60.9 %copy-start.37 = (bf16[512,1,64]{2,0,1:T(8,128)(2,1)}, bf16[512,1,64]{2,0,1:T(8,128)(2,1)S(1)}, u32[]{:S(2)}) copy-start(bf16[512,1,64]{2,0,1:T(8,128)(2,1)S(1)} %copy.257) | copy-start | bytes 196612
  232.1 39.0 %copy-start.31 = (bf16[2,256,4,64]{3,1,2,0:T(8,128)(2,1)S(1)}, bf16[2,256,4,64]{3,1,2,0:T(8,128)(2,1)}, u32[]{:S(2)}) copy-start(bf16[2,256,4,64]{3,1,2,0:T(8,128)(2,1)} %copy.228) | copy-start | bytes 786436
  269.5 8.5 collective-permute-start.2
  291.9 48.0 %collective-permute-start.3 = (bf16[512,2048]{1,0:T(8,128)(2,1)S(1)}, bf16[512,2048]{1,0:T(8,128)(2,1)}, u32[]{:S(2)}, u32[]{:S(2)}) collective-permute-start(bf16[512,2048]{1,0:T(8,128)(2,1)S(1)} %add_convert_fusion.8), channel_id=1, source_target_pairs={{0,1},{1,0},{2,3},{3,2},{4,5},{5,4},{6,7},{7,6},{8,9},{9,8},{10,11... | collective-permute-start | bytes 6291464 | tf_op jit(solution)/shard_map/ppermute | solution.py:432
  294.3 53.0 %copy-start.82 = (f32[2048]{0:T(1024)S(1)}, f32[2048]{0:T(1024)}, u32[]{:S(2)}) copy-start(f32[2048]{0:T(1024)} %param.68) | copy-start | bytes 24580
  404.4 48.9 %collective-permute-start.4 = (bf16[512,2048]{1,0:T(8,128)(2,1)}, bf16[512,2048]{1,0:T(8,128)(2,1)}, u32[]{:S(2)}, u32[]{:S(2)}) collective-permute-start(bf16[512,2048]{1,0:T(8,128)(2,1)} %get-tuple-element.595), channel_id=1, source_target_pairs={{0,1},{1,0},{2,3},{3,2},{4,5},{5,4},{6,7},{7,6},{8,9},{9,8},{10,11... | collective-permute-start | bytes 6291464 | tf_op jit(solution)/shard_map/ppermute | solution.py:432
  404.9 120.6 %copy-start.39 = (bf16[256,256]{1,0:T(8,128)(2,1)}, bf16[256,256]{1,0:T(8,128)(2,1)S(1)}, u32[]{:S(2)}) copy-start(bf16[256,256]{1,0:T(8,128)(2,1)S(1)} %fusion.87) | copy-start | bytes 393220
  431.4 22.0 %copy-start.21 = (bf16[256,2048]{1,0:T(8,128)(2,1)}, bf16[256,2048]{1,0:T(8,128)(2,1)S(1)}, u32[]{:S(2)}) copy-start(bf16[256,2048]{1,0:T(8,128)(2,1)S(1)} %get-tuple-element.606) | copy-start | bytes 3145732
  431.4 22.0 %collective-permute-start.5 = (bf16[1024,2048]{1,0:T(8,128)(2,1)}, bf16[1024,2048]{1,0:T(8,128)(2,1)}, u32[]{:S(2)}, u32[]{:S(2)}) collective-permute-start(bf16[1024,2048]{1,0:T(8,128)(2,1)} %get-tuple-element.596), channel_id=1, source_target_pairs={{0,2},{2,0},{4,6},{6,4},{8,10},{10,8},{12,14},{14,12},{16,18},{18,... | collective-permute-start | bytes 12582920 | tf_op jit(solution)/shard_map/ppermute | solution.py:435
  431.4 22.0 %collective-permute-start.6 = (bf16[1024,2048]{1,0:T(8,128)(2,1)}, bf16[1024,2048]{1,0:T(8,128)(2,1)}, u32[]{:S(2)}, u32[]{:S(2)}) collective-permute-start(bf16[1024,2048]{1,0:T(8,128)(2,1)} %get-tuple-element.597), channel_id=1, source_target_pairs={{0,2},{2,0},{4,6},{6,4},{8,10},{10,8},{12,14},{14,12},{16,18},{18,... | collective-permute-start | bytes 12582920 | tf_op jit(solution)/shard_map/ppermute | solution.py:435
  431.9 93.6 %collective-permute-start.7 = (bf16[256,2048]{1,0:T(8,128)(2,1)}, bf16[256,2048]{1,0:T(8,128)(2,1)}, u32[]{:S(2)}, u32[]{:S(2)}) collective-permute-start(bf16[256,2048]{1,0:T(8,128)(2,1)} %get-tuple-element.607), channel_id=1, source_target_pairs={{0,1},{1,0},{2,3},{3,2},{4,5},{5,4},{6,7},{7,6},{8,9},{9,8},{10,11... | collective-permute-start | bytes 3145736 | tf_op jit(solution)/shard_map/ppermute | solution.py:432
  453.3 29.9 %copy-start.36 = (bf16[512,1,64]{2,0,1:T(8,128)(2,1)S(1)}, bf16[512,1,64]{2,0,1:T(8,128)(2,1)}, u32[]{:S(2)}) copy-start(bf16[512,1,64]{2,0,1:T(8,128)(2,1)} %copy-done.35) | copy-start | bytes 196612
  453.3 29.9 %copy-start.38 = (bf16[512,1,64]{2,0,1:T(8,128)(2,1)S(1)}, bf16[512,1,64]{2,0,1:T(8,128)(2,1)}, u32[]{:S(2)}) copy-start(bf16[512,1,64]{2,0,1:T(8,128)(2,1)} %copy-done.37) | copy-start | bytes 196612
  453.3 30.7 %copy-start.29 = (bf16[512,4,64]{0,2,1:T(8,128)(2,1)S(1)}, bf16[512,4,64]{0,2,1:T(8,128)(2,1)}, u32[]{:S(2)}) copy-start(bf16[512,4,64]{0,2,1:T(8,128)(2,1)} %copy-done.28) | copy-start | bytes 786436
  453.3 30.8 %copy-start.27 = (bf16[512,4,64]{0,2,1:T(8,128)(2,1)S(1)}, bf16[512,4,64]{0,2,1:T(8,128)(2,1)}, u32[]{:S(2)}) copy-start(bf16[512,4,64]{0,2,1:T(8,128)(2,1)} %copy-done.26) | copy-start | bytes 786436
  453.4 30.8 %copy-start.16 = (bf16[2,256,1,4,128]{4,3,1,0,2:T(4,128)(2,1)S(1)}, bf16[2,256,1,4,128]{4,3,1,0,2:T(4,128)(2,1)}, u32[]{:S(2)}) copy-start(bf16[2,256,1,4,128]{4,3,1,0,2:T(4,128)(2,1)} %copy.232) | copy-start | bytes 1572868
  470.6 119.1 %collective-permute-start.9 = (bf16[512,2048]{1,0:T(8,128)(2,1)}, bf16[512,2048]{1,0:T(8,128)(2,1)}, u32[]{:S(2)}, u32[]{:S(2)}) collective-permute-start(bf16[512,2048]{1,0:T(8,128)(2,1)} %get-tuple-element.621), channel_id=1, source_target_pairs={{0,4},{2,6},{4,0},{6,2},{8,12},{10,14},{12,8},{14,10},{16,20},{18,... | collective-permute-start | bytes 6291464 | tf_op jit(solution)/shard_map/ppermute | solution.py:435
  471.8 118.0 %collective-permute-start.10 = (bf16[512,2048]{1,0:T(8,128)(2,1)}, bf16[512,2048]{1,0:T(8,128)(2,1)}, u32[]{:S(2)}, u32[]{:S(2)}) collective-permute-start(bf16[512,2048]{1,0:T(8,128)(2,1)} %get-tuple-element.623), channel_id=1, source_target_pairs={{0,8},{2,10},{4,12},{6,14},{8,0},{10,2},{12,4},{14,6},{16,24},{18,... | collective-permute-start | bytes 6291464 | tf_op jit(solution)/shard_map/ppermute | solution.py:435
  486.8 38.7 %copy-start.7 = (bf16[512,2048]{1,0:T(8,128)(2,1)S(1)}, bf16[512,2048]{1,0:T(8,128)(2,1)}, u32[]{:S(2)}) copy-start(bf16[512,2048]{1,0:T(8,128)(2,1)} %copy-done.6) | copy-start | bytes 6291460
  539.7 50.0 %all-to-all-start.2 = ((bf16[16,16,2048]{2,1,0:T(8,128)(2,1)}), bf16[16,16,2048]{2,1,0:T(8,128)(2,1)S(1)}, u32[]{:S(2)}, u32[]{:S(2)}) async-start(bf16[16,16,2048]{2,1,0:T(8,128)(2,1)} %bitcast.152), calls=%async_computation.3 | async-start | bytes 2097152 | tf_op jit(solution)/shard_map/all_to_all | solution.py:480
  543.4 195.6 %reduce-scatter.5.cloned.1.call-start = ((), (), s32[]{:S(2)}) async-start(), calls=%async_computation.9 | async-start | bytes 8912896 | tf_op jit(solution)/shard_map/reduce_scatter | solution.py:726
  544.0 3.7 collective-permute-start.8
  589.8 24.1 %copy-start.66 = (f32[2048]{0:T(1024)S(1)}, f32[2048]{0:T(1024)}, u32[]{:S(2)}) copy-start(f32[2048]{0:T(1024)} %param.67) | copy-start | bytes 24580
  589.8 24.1 %copy-start.87 = (f32[2,2,128]{2,1,0:T(2,128)S(1)}, f32[2,2,128]{2,1,0:T(2,128)}, u32[]{:S(2)}) copy-start(f32[2,2,128]{2,1,0:T(2,128)} %copy-done.86) | copy-start | bytes 6148
  589.8 24.1 %copy-start.89 = (f32[512,1]{0,1:T(1,128)S(1)}, f32[512,1]{0,1:T(1,128)}, u32[]{:S(2)}) copy-start(f32[512,1]{0,1:T(1,128)} %copy-done.88) | copy-start | bytes 6148
  589.8 24.0 %copy-start.91 = (f32[512,1]{0,1:T(1,128)S(1)}, f32[512,1]{0,1:T(1,128)}, u32[]{:S(2)}) copy-start(f32[512,1]{0,1:T(1,128)} %copy-done.90) | copy-start | bytes 6148
  610.5 39.4 %collective-permute-start.11 = (bf16[1024,4480]{1,0:T(8,128)(2,1)}, bf16[1024,4480]{1,0:T(8,128)(2,1)}, u32[]{:S(2)}, u32[]{:S(2)}) collective-permute-start(bf16[1024,4480]{1,0:T(8,128)(2,1)} %get-tuple-element.630), channel_id=1, source_target_pairs={{0,2},{2,0},{4,6},{6,4},{8,10},{10,8},{12,14},{14,12},{16,18},{18,... | collective-permute-start | bytes 27525128 | tf_op jit(solution)/shard_map/ppermute | solution.py:435
  610.5 39.4 %collective-permute-start.12 = (bf16[256,2048]{1,0:T(8,128)(2,1)}, bf16[256,2048]{1,0:T(8,128)(2,1)}, u32[]{:S(2)}, u32[]{:S(2)}) collective-permute-start(bf16[256,2048]{1,0:T(8,128)(2,1)} %get-tuple-element.633), channel_id=1, source_target_pairs={{0,8},{2,10},{4,12},{6,14},{8,0},{10,2},{12,4},{14,6},{16,24},{18,... | collective-permute-start | bytes 3145736 | tf_op jit(solution)/shard_map/ppermute | solution.py:435
  612.4 37.5 %collective-permute-start.13 = (bf16[256,2048]{1,0:T(8,128)(2,1)}, bf16[256,2048]{1,0:T(8,128)(2,1)}, u32[]{:S(2)}, u32[]{:S(2)}) collective-permute-start(bf16[256,2048]{1,0:T(8,128)(2,1)} %get-tuple-element.635), channel_id=1, source_target_pairs={{0,4},{2,6},{4,0},{6,2},{8,12},{10,14},{12,8},{14,10},{16,20},{18,... | collective-permute-start | bytes 3145736 | tf_op jit(solution)/shard_map/ppermute | solution.py:435
  613.9 36.0 %copy-start.81 = (f32[2048]{0:T(1024)S(1)}, f32[2048]{0:T(1024)}, u32[]{:S(2)}) copy-start(f32[2048]{0:T(1024)} %copy-done.80) | copy-start | bytes 24580
  672.8 77.6 %collective-permute-start.18 = (bf16[512,2304]{1,0:T(8,128)(2,1)}, bf16[512,2304]{1,0:T(8,128)(2,1)}, u32[]{:S(2)}, u32[]{:S(2)}) collective-permute-start(bf16[512,2304]{1,0:T(8,128)(2,1)} %get-tuple-element.652), channel_id=1, source_target_pairs={{0,8},{2,10},{4,12},{6,14},{8,0},{10,2},{12,4},{14,6},{16,24},{18,... | collective-permute-start | bytes 7077896 | tf_op jit(solution)/shard_map/ppermute | solution.py:435
  673.4 74.8 %collective-permute-start.17 = (bf16[512,2176]{1,0:T(8,128)(2,1)}, bf16[512,2176]{1,0:T(8,128)(2,1)}, u32[]{:S(2)}, u32[]{:S(2)}) collective-permute-start(bf16[512,2176]{1,0:T(8,128)(2,1)} %get-tuple-element.650), channel_id=1, source_target_pairs={{0,4},{2,6},{4,0},{6,2},{8,12},{10,14},{12,8},{14,10},{16,20},{18,... | collective-permute-start | bytes 6684680 | tf_op jit(solution)/shard_map/ppermute | solution.py:435
  674.8 73.4 %collective-permute-start.20 = (bf16[256,2048]{1,0:T(8,128)(2,1)}, bf16[256,2048]{1,0:T(8,128)(2,1)S(1)}, u32[]{:S(2)}, u32[]{:S(2)}) collective-permute-start(bf16[256,2048]{1,0:T(8,128)(2,1)} %get-tuple-element.655), channel_id=1, source_target_pairs={{0,1},{1,0},{2,3},{3,2},{4,5},{5,4},{6,7},{7,6},{8,9},{9,8},{10,11... | collective-permute-start | bytes 3145736 | tf_op jit(solution)/shard_map/ppermute | solution.py:432
  676.2 2.4 collective-permute-start.14
  676.2 61.0 %collective-permute-start.15 = (bf16[128,2048]{1,0:T(8,128)(2,1)}, bf16[128,2048]{1,0:T(8,128)(2,1)}, u32[]{:S(2)}, u32[]{:S(2)}) collective-permute-start(bf16[128,2048]{1,0:T(8,128)(2,1)} %get-tuple-element.645), channel_id=1, source_target_pairs={{0,16},{2,18},{4,20},{6,22},{8,24},{10,26},{12,28},{14,30},{16,0},... | collective-permute-start | bytes 1572872 | tf_op jit(solution)/shard_map/ppermute | solution.py:435
  678.6 69.6 %collective-permute-start.16 = (bf16[128,2048]{1,0:T(8,128)(2,1)}, bf16[128,2048]{1,0:T(8,128)(2,1)}, u32[]{:S(2)}, u32[]{:S(2)}) collective-permute-start(bf16[128,2048]{1,0:T(8,128)(2,1)} %get-tuple-element.646), channel_id=1, source_target_pairs={{0,16},{2,18},{4,20},{6,22},{8,24},{10,26},{12,28},{14,30},{16,0},... | collective-permute-start | bytes 1572872 | tf_op jit(solution)/shard_map/ppermute | solution.py:435
  737.2 11.0 %collective-permute-start.19 = (f32[16,2048]{1,0:T(8,128)}, f32[16,2048]{1,0:T(8,128)}, u32[]{:S(2)}, u32[]{:S(2)}) collective-permute-start(f32[16,2048]{1,0:T(8,128)} %get-tuple-element.1327), channel_id=1, source_target_pairs={{0,4},{2,6},{4,0},{6,2},{8,12},{10,14},{12,8},{14,10},{16,20},{18,... | collective-permute-start | bytes 393224 | tf_op jit(solution)/shard_map/ppermute | solution.py:435
  764.8 121.2 %all-to-all-start.3 = ((bf16[16,16,2048]{2,1,0:T(8,128)(2,1)}), bf16[16,16,2048]{2,1,0:T(8,128)(2,1)S(1)}, u32[]{:S(2)}, u32[]{:S(2)}) async-start(bf16[16,16,2048]{2,1,0:T(8,128)(2,1)} %bitcast.153), calls=%async_computation.5 | async-start | bytes 2097152 | tf_op jit(solution)/shard_map/all_to_all | solution.py:480
  769.6 46.7 %collective-permute-start.22 = (bf16[256,2304]{1,0:T(8,128)(2,1)}, bf16[256,2304]{1,0:T(8,128)(2,1)S(1)}, u32[]{:S(2)}, u32[]{:S(2)}) collective-permute-start(bf16[256,2304]{1,0:T(8,128)(2,1)} %get-tuple-element.666), channel_id=1, source_target_pairs={{0,4},{2,6},{4,0},{6,2},{8,12},{10,14},{12,8},{14,10},{16,20},{18,... | collective-permute-start | bytes 3538952 | tf_op jit(solution)/shard_map/ppermute | solution.py:435
  771.5 44.7 %collective-permute-start.21 = (bf16[256,2176]{1,0:T(8,128)(2,1)}, bf16[256,2176]{1,0:T(8,128)(2,1)}, u32[]{:S(2)}, u32[]{:S(2)}) collective-permute-start(bf16[256,2176]{1,0:T(8,128)(2,1)} %get-tuple-element.664), channel_id=1, source_target_pairs={{0,8},{2,10},{4,12},{6,14},{8,0},{10,2},{12,4},{14,6},{16,24},{18,... | collective-permute-start | bytes 3342344 | tf_op jit(solution)/shard_map/ppermute | solution.py:435
  773.0 43.3 %collective-permute-start.23 = (f32[16,2048]{1,0:T(8,128)}, f32[16,2048]{1,0:T(8,128)S(1)}, u32[]{:S(2)}, u32[]{:S(2)}) collective-permute-start(f32[16,2048]{1,0:T(8,128)} %get-tuple-element.667), channel_id=1, source_target_pairs={{0,8},{2,10},{4,12},{6,14},{8,0},{10,2},{12,4},{14,6},{16,24},{18,... | collective-permute-start | bytes 393224 | tf_op jit(solution)/shard_map/ppermute | solution.py:435
  827.8 58.2 %collective-permute-start.26 = (bf16[128,2304]{1,0:T(8,128)(2,1)}, bf16[128,2304]{1,0:T(8,128)(2,1)S(1)}, u32[]{:S(2)}, u32[]{:S(2)}) collective-permute-start(bf16[128,2304]{1,0:T(8,128)(2,1)} %get-tuple-element.676), channel_id=1, source_target_pairs={{0,16},{2,18},{4,20},{6,22},{8,24},{10,26},{12,28},{14,30},{16,0},... | collective-permute-start | bytes 1769480 | tf_op jit(solution)/shard_map/ppermute | solution.py:435
  830.4 55.6 %collective-permute-start.25 = (bf16[128,2176]{1,0:T(8,128)(2,1)}, bf16[128,2176]{1,0:T(8,128)(2,1)}, u32[]{:S(2)}, u32[]{:S(2)}) collective-permute-start(bf16[128,2176]{1,0:T(8,128)(2,1)} %get-tuple-element.674), channel_id=1, source_target_pairs={{0,16},{2,18},{4,20},{6,22},{8,24},{10,26},{12,28},{14,30},{16,0},... | collective-permute-start | bytes 1671176 | tf_op jit(solution)/shard_map/ppermute | solution.py:435
  830.8 55.2 %collective-permute-start.24 = (f32[16,2048]{1,0:T(8,128)S(1)}, f32[16,2048]{1,0:T(8,128)S(1)}, u32[]{:S(2)}, u32[]{:S(2)}) collective-permute-start(f32[16,2048]{1,0:T(8,128)S(1)} %get-tuple-element.672), channel_id=1, source_target_pairs={{0,16},{2,18},{4,20},{6,22},{8,24},{10,26},{12,28},{14,30},{16,0},... | collective-permute-start | bytes 393224 | tf_op jit(solution)/shard_map/ppermute | solution.py:435
  894.1 6.5 collective-permute-start.28
  895.6 10.7 %collective-permute-start.27 = (f32[64,512]{1,0:T(8,128)}, f32[64,512]{1,0:T(8,128)S(1)}, u32[]{:S(2)}, u32[]{:S(2)}) collective-permute-start(f32[64,512]{1,0:T(8,128)} %get-tuple-element.688), channel_id=1, source_target_pairs={{0,1},{1,0},{2,3},{3,2},{4,5},{5,4},{6,7},{7,6},{8,9},{9,8},{10,11... | collective-permute-start | bytes 393224 | tf_op jit(solution)/shard_map/ppermute | solution.py:432
  (91 other events, 339.7 us)
Sparse Core Ops, SparseCore 0:
  15.3 172.8 all-gather.4
  189.8 138.4 all-gather.2
  404.0 149.9 reduce-scatter.2
  557.9 120.8 reduce-scatter.4

commit v8 on v7

--- a/solution.py
+++ b/solution.py
@@ -1,3 +1,4 @@
+import functools
 import math
 
 import jax
@@ -84,13 +85,8 @@
     half_size = HEAD // 2
     frequency = jnp.exp(jnp.arange(half_size, dtype=f32) * (-2.0 * math.log(rope_base) / HEAD))
     angles = position.astype(f32) * frequency[None, :]
-    return jnp.cos(angles)[:, None, :], jnp.sin(angles)[:, None, :]
-
-
-def rotate(values, cosine, sine):
-    half_size = HEAD // 2
-    first, second = values[..., :half_size], values[..., half_size:]
-    return jnp.concatenate([first * cosine - second * sine, second * cosine + first * sine], axis=-1)
+    cosine, sine = jnp.cos(angles), jnp.sin(angles)
+    return jnp.concatenate([cosine, cosine], axis=1), jnp.concatenate([-sine, sine], axis=1)
 
 
 def copy_blocks(order_ref, first_ref, second_ref, first_out_ref, second_out_ref):
@@ -138,10 +134,6 @@
     )(values)
 
 
-def rotate_back(values, cosine, sine):
-    return rotate(values, cosine, -sine)
-
-
 NEGATIVE = -1e30
 
 
@@ -182,12 +174,137 @@
     return decay, (inner * decay * step_row).astype(bf16)
 
 
+def turn(values, cosine_ref, sine_ref, sign):
+    return values * cosine_ref[...] + sign * (pltpu.roll(values, HEAD // 2, 1) * sine_ref[...])
+
+
+def head_probs(query_low, key_low, mask):
+    logits = lax.dot_general(query_low, key_low, (((1,), (1,)), ((), ())), preferred_element_type=f32) * HEAD ** (-0.5)
+    logits = logits + mask
+    weights = jnp.exp(logits - jnp.max(logits, axis=1, keepdims=True))
+    return weights / jnp.sum(weights, axis=1, keepdims=True)
+
+
+def attention_forward_kernel(
+    query_ref, key_ref, value_ref, cosine_ref, sine_ref, columns_ref, seg_row_ref,
+    attended_ref, query_low_ref, key_low_ref, value_low_ref, mask_ref,
+):
+    rows = query_ref.shape[0]
+
+    @pl.when(pl.program_id(1) == 0)
+    def _():
+        mask_ref[...] = block_mask(rows, columns_ref[:, 0:1], seg_row_ref[0])
+
+    query_low = turn(query_ref[...], cosine_ref, sine_ref, 1.0).astype(bf16)
+    key_low = turn(key_ref[...], cosine_ref, sine_ref, 1.0).astype(bf16)
+    value_low = value_ref[...].astype(bf16)
+    probs_low = head_probs(query_low, key_low, mask_ref[...]).astype(bf16)
+    attended_ref[...] = jnp.dot(probs_low, value_low, preferred_element_type=f32).astype(bf16)
+    query_low_ref[...] = query_low
+    key_low_ref[...] = key_low
+    value_low_ref[...] = value_low
+
+
+def attention_backward_kernel(
+    grad_ref, query_ref, key_ref, value_ref, cosine_ref, sine_ref, columns_ref, seg_row_ref,
+    joint_ref, mask_ref, grad_key_ref, grad_value_ref, *, group, query_cols, key_cols,
+):
+    rows = query_ref.shape[0]
+    head = pl.program_id(1)
+
+    @pl.when(head == 0)
+    def _():
+        mask_ref[...] = block_mask(rows, columns_ref[:, 0:1], seg_row_ref[0])
+
+    @pl.when(head % group == 0)
+    def _():
+        grad_key_ref[...] = jnp.zeros_like(grad_key_ref)
+        grad_value_ref[...] = jnp.zeros_like(grad_value_ref)
+
+    grad, query_low, key_low = grad_ref[...], query_ref[...], key_ref[...]
+    probs = head_probs(query_low, key_low, mask_ref[...])
+    grad_probs = lax.dot_general(grad, value_ref[...], (((1,), (1,)), ((), ())), preferred_element_type=f32)
+    grad_value_ref[...] += lax.dot_general(
+        probs.astype(bf16), grad, (((0,), (0,)), ((), ())), preferred_element_type=f32
+    )
+    grad_logits = (probs * (grad_probs - jnp.sum(probs * grad_probs, axis=1, keepdims=True))).astype(bf16)
+    grad_query = jnp.dot(grad_logits, key_low, preferred_element_type=f32) * HEAD ** (-0.5)
+    grad_key_ref[...] += lax.dot_general(
+        grad_logits, query_low, (((0,), (0,)), ((), ())), preferred_element_type=f32
+    ) * HEAD ** (-0.5)
+    joint_ref[:, pl.ds(pl.multiple_of(head * HEAD, HEAD), HEAD)] = turn(
+        grad_query, cosine_ref, sine_ref, -1.0
+    ).astype(bf16)
+
+    @pl.when(head % group == group - 1)
+    def _():
+        place = head // group * HEAD
+        joint_ref[:, pl.ds(pl.multiple_of(query_cols + place, HEAD), HEAD)] = turn(
+            grad_key_ref[...], cosine_ref, sine_ref, -1.0
+        ).astype(bf16)
+        joint_ref[:, pl.ds(pl.multiple_of(query_cols + key_cols + place, HEAD), HEAD)] = grad_value_ref[...].astype(bf16)
+
+
+def attention_specs(rows, group):
+    table = pl.BlockSpec((rows, HEAD), lambda m, h: (m, 0))
+    return (
+        lambda start: pl.BlockSpec((rows, HEAD), lambda m, h: (m, start + h)),
+        lambda start: pl.BlockSpec((rows, HEAD), lambda m, h: (m, start + h // group)),
+        [table, table, pl.BlockSpec((rows, 8), lambda m, h: (m, 0)), pl.BlockSpec((1, 1, rows), lambda m, h: (m, 0, 0))],
+    )
+
+
+def attention_forward(joint, query_cols, key_cols, tables):
+    micro, _, rows = tables[3].shape
+    total = joint.shape[0]
+    heads, kv_heads = query_cols // HEAD, key_cols // HEAD
+    by_head, by_kv, table_specs = attention_specs(rows, heads // kv_heads)
+    return pl.pallas_call(
+        attention_forward_kernel,
+        out_shape=tuple(jax.ShapeDtypeStruct((total, size), bf16) for size in (query_cols, query_cols, key_cols, key_cols)),
+        grid=(micro, heads),
+        in_specs=[by_head(0), by_kv(heads), by_kv(heads + kv_heads)] + table_specs,
+        out_specs=(by_head(0), by_head(0), by_kv(0), by_kv(0)),
+        scratch_shapes=[pltpu.VMEM((rows, rows), f32)],
+        cost_estimate=pl.CostEstimate(
+            flops=4 * total * rows * query_cols, transcendentals=total * rows * heads, bytes_accessed=8 * total * query_cols
+        ),
+        name="attention_forward",
+    )(joint, joint, joint, *tables)
+
+
+def attention_backward(grad, query, key, value, tables):
+    micro, _, rows = tables[3].shape
+    total, query_cols = query.shape
+    key_cols = key.shape[1]
+    heads, kv_heads = query_cols // HEAD, key_cols // HEAD
+    by_head, by_kv, table_specs = attention_specs(rows, heads // kv_heads)
+    joint_cols = query_cols + 2 * key_cols
+    return pl.pallas_call(
+        functools.partial(
+            attention_backward_kernel, group=heads // kv_heads, query_cols=query_cols, key_cols=key_cols
+        ),
+        out_shape=jax.ShapeDtypeStruct((total, joint_cols), bf16),
+        grid=(micro, heads),
+        in_specs=[by_head(0), by_head(0), by_kv(0), by_kv(0)] + table_specs,
+        out_specs=pl.BlockSpec((rows, joint_cols), lambda m, h: (m, 0)),
+        scratch_shapes=[pltpu.VMEM((rows, rows), f32), pltpu.VMEM((rows, HEAD), f32), pltpu.VMEM((rows, HEAD), f32)],
+        cost_estimate=pl.CostEstimate(
+            flops=10 * total * rows * query_cols, transcendentals=total * rows * heads, bytes_accessed=8 * total * query_cols
+        ),
+        name="attention_backward",
+    )(grad, query, key, value, *tables)
+
+
 def state_forward_kernel(
     signal_ref, gate_ref, taps_ref, skip_ref, state_ref, seg_row_ref, run_row_ref, run_col_ref, step_ref, columns_ref,
     out_ref, square_ref, inner_ref, mask_ref,
 ):
     rows = signal_ref.shape[0]
     position = columns_ref[:, 1:2]
+    pair = pl.program_id(1)
+    here = pl.ds(pl.multiple_of(pair * 2 * SHD, 2 * SHD), 2 * SHD)
+    taps_ref, skip_ref = taps_ref.at[:, here], skip_ref.at[:, here]
 
     @pl.when(pl.program_id(1) == 0)
     def _():
@@ -203,8 +320,8 @@
     mixed = []
     for head in range(2):
         _, mixing = mixing_block(
-            inner_ref[...], mask_ref[...], run_col_ref[0, 0, :, head : head + 1],
-            run_row_ref[0, 0, head : head + 1, :], step_ref[0, 0, head : head + 1, :],
+            inner_ref[...], mask_ref[...], run_col_ref[0, pair, :, head : head + 1],
+            run_row_ref[0, pair, head : head + 1, :], step_ref[0, pair, head : head + 1, :],
         )
         mixed.append(jnp.dot(mixing, cols_low, preferred_element_type=f32))
     lanes = lax.broadcasted_iota(jnp.int32, cols.shape, 1)
@@ -223,6 +340,8 @@
 ):
     rows = signal_ref.shape[0]
     pair = pl.program_id(1)
+    block = pl.ds(pl.multiple_of(pair * 2 * SHD, 2 * SHD), 2 * SHD)
+    taps_ref, skip_ref, gain_ref = taps_ref.at[:, block], skip_ref.at[:, block], gain_ref.at[:, block]
 
     @pl.when(pair == 0)
     def _():
@@ -254,10 +373,10 @@
     zero = jnp.zeros_like(grad_low)
     grad_cols = []
     for head in range(2):
-        step_row = step_ref[0, 0, head : head + 1, :]
+        step_row = step_ref[0, pair, head : head + 1, :]
         inner = inner_ref[...]
         decay, mixing = mixing_block(
-            inner, mask_ref[...], run_col_ref[0, 0, :, head : head + 1], run_row_ref[0, 0, head : head + 1, :], step_row
+            inner, mask_ref[...], run_col_ref[0, pair, :, head : head + 1], run_row_ref[0, pair, head : head + 1, :], step_row
         )
         grad_cols.append(
             lax.dot_general(mixing, grad_low, (((0,), (0,)), ((), ())), preferred_element_type=f32)
@@ -315,13 +434,13 @@
     block = pl.BlockSpec((rows, 2 * SHD), lambda m, p: (m, p))
     return {
         "block": block,
-        "taps": pl.BlockSpec((CONV + 1, 2 * SHD), lambda m, p: (0, p)),
-        "vector": pl.BlockSpec((1, 2 * SHD), lambda m, p: (0, p)),
+        "taps": pl.BlockSpec((CONV + 1, 2 * SHD * pairs), lambda m, p: (0, 0)),
+        "vector": pl.BlockSpec((1, 2 * SHD * pairs), lambda m, p: (0, 0)),
         "state": pl.BlockSpec((rows, 2 * NS), lambda m, p: (m, 0)),
         "columns": pl.BlockSpec((rows, 8), lambda m, p: (m, 0)),
         "row": pl.BlockSpec((1, 1, rows), lambda m, p: (m, 0, 0)),
-        "head_row": pl.BlockSpec((1, 1, 2, rows), lambda m, p: (m, p, 0, 0)),
-        "head_col": pl.BlockSpec((1, 1, rows, 2), lambda m, p: (m, p, 0, 0)),
+        "head_row": pl.BlockSpec((1, pairs, 2, rows), lambda m, p: (m, 0, 0, 0)),
+        "head_col": pl.BlockSpec((1, pairs, rows, 2), lambda m, p: (m, 0, 0, 0)),
     }
 
 
@@ -422,7 +541,6 @@
     rows = own * lanes
     total = micro * rows
     inner_width = SH * SHD
-    scale_factor = HEAD ** (-0.5)
     outer_count = groups // 4
     shard = width // groups
 
@@ -510,7 +628,6 @@
 
     before = jnp.sum((segment[:, None, :] < segment[:, :, None]).astype(jnp.int32), axis=2)
     places = jnp.arange(rows, dtype=jnp.int32)
-    allowed = (segment[:, :, None] == segment[:, None, :]) & (places[None, None, :] <= places[None, :, None])
     position = (places[None, :] - before).reshape(total, 1)
 
     masks = [1 << place for place in range(groups.bit_length() - 1)]
@@ -605,28 +722,20 @@
     skip_wide = jnp.repeat(skip_gain, SHD)[None, :]
     layout = (state_low, segment.reshape(micro, 1, rows).astype(f32), run_row, run_col, step_row)
     row_facts = jnp.concatenate([segment.reshape(total, 1).astype(f32), position.astype(f32)], axis=1)
-    ssm_out, squares = state_forward(ssm_in, gate_z, kernel_inner, skip_wide, *layout, jnp.pad(row_facts, ((0, 0), (0, 6))))
+    row_columns = jnp.pad(row_facts, ((0, 0), (0, 6)))
+    query_cols, key_cols = query_weight.shape[1], key_weight.shape[1]
+    attention_tables = (*rope_tables(position), row_columns, layout[1])
+    joint_start = places_of["query"][1]
+    joint_weight = lax.slice_in_dim(whole["early"], joint_start, joint_start + query_cols + 2 * key_cols, axis=1)
+    ssm_out, squares = state_forward(ssm_in, gate_z, kernel_inner, skip_wide, *layout, row_columns)
+    attended_low, query_low, key_low, value_low = attention_forward(
+        project(normed_low, joint_weight), query_cols, key_cols, attention_tables
+    )
     square_own = jnp.sum(squares, axis=1)
     square_sum = square_own + other_lane(square_own)
     inv_rms = lax.rsqrt(square_sum / inner_width + epsilon)[:, None]
     gated_low = (ssm_out * jax.nn.silu(gate_z) * inv_rms * mixer_gain).astype(bf16)
 
-    cosine, sine = rope_tables(position)
-    query_low = rotate(project(normed_low, full("query")).reshape(total, -1, HEAD), cosine, sine).astype(bf16)
-    key_low = rotate(project(normed_low, full("key")).reshape(total, -1, HEAD), cosine, sine).astype(bf16)
-    value_low = project(normed_low, full("value")).astype(bf16)
-    kv_here = key_low.shape[1]
-    query_low = query_low.reshape(micro, rows, kv_here, -1, HEAD)
-    key_low = key_low.reshape(micro, rows, kv_here, HEAD)
-    value_low = value_low.reshape(micro, rows, kv_here, HEAD)
-    logits = jnp.einsum("migkd,mjgd->mgkij", query_low, key_low, preferred_element_type=f32) * scale_factor
-    logits = jnp.where(allowed[:, None, None], logits, -jnp.inf)
-    exp_scores = jnp.exp(logits - jnp.max(logits, axis=-1, keepdims=True))
-    probs = exp_scores / jnp.sum(exp_scores, axis=-1, keepdims=True)
-    probs_low = probs.astype(bf16)
-    attended_low = (
-        jnp.einsum("mgkij,mjgd->migkd", probs_low, value_low, preferred_element_type=f32).astype(bf16).reshape(total, -1)
-    )
     branch_part = (project_back(gated_low, full("mix")) + project_back(attended_low, full("attn"))).astype(bf16)
     branch = branch_part.astype(f32) + other_lane(branch_part).astype(f32)
     whole_mid = (in32 + branch).astype(bf16)
@@ -696,22 +805,14 @@
         whole_branch = grad_middle.astype(bf16)
         grad_gated_norm = project(whole_branch, full("mix"))
         cross_own = jnp.sum(grad_gated_norm * mixer_gain * (ssm_out * jax.nn.silu(gate_z)), axis=1)
-        grad_attended = project(whole_branch, full("attn")).astype(bf16).reshape(micro, rows, kv_here, -1, HEAD)
-        grad_probs = jnp.einsum("migkd,mjgd->mgkij", grad_attended, value_low, preferred_element_type=f32)
-        grad_value = jnp.einsum("mgkij,migkd->mjgd", probs_low, grad_attended, preferred_element_type=f32)
-        weighted_sum = jnp.sum(probs * grad_probs, axis=-1, keepdims=True)
-        grad_logits = (probs * (grad_probs - weighted_sum)).astype(bf16)
-        grad_query_rot = jnp.einsum("mgkij,mjgd->migkd", grad_logits, key_low, preferred_element_type=f32) * scale_factor
-        grad_key_rot = jnp.einsum("mgkij,migkd->mjgd", grad_logits, query_low, preferred_element_type=f32) * scale_factor
-        query_grad_low = rotate_back(grad_query_rot.reshape(total, -1, HEAD), cosine, sine).astype(bf16).reshape(total, -1)
-        key_grad_low = rotate_back(grad_key_rot.reshape(total, -1, HEAD), cosine, sine).astype(bf16).reshape(total, -1)
-        value_grad_low = grad_value.astype(bf16).reshape(total, -1)
+        grad_attended = project(whole_branch, full("attn")).astype(bf16)
+        joint_low = attention_backward(grad_attended, query_low, key_low, value_low, attention_tables)
         return (
             cross_own, lane_rows(grad_middle, lane), grad_gated_norm, whole_branch,
-            (query_grad_low, key_grad_low, value_grad_low),
-        )
-
-    cross_own, grad_middle_own, grad_gated_norm, whole_branch, qkv_low = unit(branch_backward)
+            joint_low,
+        )
+
+    cross_own, grad_middle_own, grad_gated_norm, whole_branch, joint_low = unit(branch_backward)
     cross_other = other_lane(cross_own)
 
     ffn_other = other_lane(ffn_send)
@@ -731,7 +832,7 @@
         columns = jnp.pad(jnp.concatenate([row_facts, inv_rms, cross], axis=1), ((0, 0), (0, 4)))
         first_right, column_sums, state_sums, head_sums = state_backward(
             grad_gated_norm, ssm_out, gate_z, ssm_in, kernel_inner, skip_wide, mixer_gain[None, :], *layout, columns,
-            state_raw, kernel_state, step_heads, step_sig, rate[:, None], jnp.concatenate(qkv_low, axis=1),
+            state_raw, kernel_state, step_heads, step_sig, rate[:, None], joint_low,
         )
         return column_sums, state_sums, head_sums, first_right
 
@@ -784,8 +885,6 @@
 
     in_moved = None
     everything = [*feeds, *firsts]
-    query_cols, key_cols = query_weight.shape[1], key_weight.shape[1]
-
     bits = 2
 
     def finish():

time: 924 us -> 888 us (0.961)
  local copies, waits for them, and re-layouts: 88.6 us -> 69 us
  waiting for transfers between devices: 368 us -> 382 us
  other arithmetic: 93.2 us -> 79.3 us
  matrix products: 199 us -> 188 us
    pallas_call x0 -> x2, Pallas kernels: none -> 16.3 us  [the longest x1 8.24 us: attention_forward(): pl.pallas_call(attention_forward_kernel, out_shape=tuple((jax.ShapeDtypeS...]
    pallas_call x1, Pallas kernels: 36.3 us -> 21 us  [state_forward(): pl.pallas_call(state_forward_kernel, out_shape=(jax.ShapeDtypeStruct((tot...]
    all_gather x2, waiting for transfers between devices: 31.7 us -> 42.1 us  [local(): lax.all_gather(jnp.concatenate(list(group_weights.values()), axis=1), 'dp...]
    dot_general x16 -> x14, matrix products: 70.9 us -> 68.5 us  [project(): return jnp.dot(left, right, preferred_element_type=f32)]
  transfers between devices with their start and end apart: 37 -> 37, of which waited for: 14 -> 16; matrix products, arithmetic and copies ran while one was open for 31% -> 28% of each run, Pallas kernels for 9% -> 9%
where the time goes in v8:
time: 888 us; the launch traced here: 877 us
  waiting for transfers between devices  382 us (43%)
  matrix products  188 us (21%)
  Pallas kernels  82.6 us (9%)
  other arithmetic  79.3 us (9%)
  local copies, waits for them, and re-layouts  69 us (8%)
  starting transfers between devices  58.6 us (7%)
  between operations  15.7 us (2%)
    ppermute x19, waiting for transfers between devices, other_group(): return lax.ppermute(values, 'dp', [(i, i ^ bits) for i in range(groups)])  174 us
    ppermute x10, waiting for transfers between devices, other_lane(): return lax.ppermute(values, 'tensor', swap_lane)  92.4 us
    all_to_all x4, waiting for transfers between devices, exchange(): lax.all_to_all(buffer.reshape(groups, micro * per, width), 'dp', split_ax...  73.3 us
    dot_general x14, matrix products, project(): return jnp.dot(left, right, preferred_element_type=f32)  68.5 us
    dot_general x12, matrix products, outer_sum(): lax.dot_general(left, right, (((0,), (0,)), ((), ())), preferred_element_...  67.9 us
    dot_general x6, matrix products, project_back(): lax.dot_general(left, right, (((1,), (1,)), ((), ())), preferred_element_...  51.5 us
    all_gather x2, waiting for transfers between devices, local(): lax.all_gather(jnp.concatenate(list(group_weights.values()), axis=1), 'dp...  42.1 us
    pallas_call x1, Pallas kernels, state_backward(): pl.pallas_call(state_backward_kernel, out_shape=(jax.ShapeDtypeStruct((to...  34.4 us
  transfers between devices with their start and end apart: 37, of which 16 were waited for; matrix products, arithmetic and copies ran while one was open for 28% of the time, Pallas kernels for 9%

profile of v8, /device:TPU:0, one launch (start us, length us, event | category | flops | bytes accessed | tf_op | source)
XLA Modules:
  0.0 877.1 jit_solution(18018945389962614196)
XLA Ops:
  18.8 4.9 select_reduce_fusion
  25.4 7.4 all-to-all-start
  34.5 38.2 %all-to-all-done = bf16[16,16,2048]{2,1,0:T(8,128)(2,1)S(1)} async-done(((bf16[16,16,2048]{2,1,0:T(8,128)(2,1)}), bf16[16,16,2048]{2,1,0:T(8,128)(2,1)S(1)}, u32[]{:S(2)}, u32[]{:S(2)}) %all-to-all-start) | async-done | bytes 1048608 | tf_op jit(solution)/shard_map/all_to_all | solution.py:598
  72.7 3.7 all-to-all-start.1
  81.0 35.1 %all-to-all-done.1 = bf16[16,16,2048]{2,1,0:T(8,128)(2,1)S(1)} async-done(((bf16[16,16,2048]{2,1,0:T(8,128)(2,1)}), bf16[16,16,2048]{2,1,0:T(8,128)(2,1)S(1)}, u32[]{:S(2)}, u32[]{:S(2)}) %all-to-all-start.1) | async-done | bytes 1048608 | tf_op jit(solution)/shard_map/all_to_all | solution.py:598
  120.1 21.3 %collective-permute-done.1 = bf16[256,2048]{1,0:T(8,128)(2,1)S(1)} collective-permute-done((bf16[256,2048]{1,0:T(8,128)(2,1)S(1)}, bf16[256,2048]{1,0:T(8,128)(2,1)S(1)}, u32[]{:S(2)}, u32[]{:S(2)}) %collective-permute-start.1) | collective-permute-done | bytes 1048608 | tf_op jit(solution)/shard_map/ppermute | solution.py:550
  146.5 6.9 pick_halves.3
  153.4 35.5 %all-gather.5.cloned.1.call-done = bf16[2048,6528]{1,0:T(8,128)(2,1)} async-done(((bf16[128,6528]{1,0:T(8,128)(2,1)}), bf16[2048,6528]{1,0:T(8,128)(2,1)}) %all-gather.5.cloned.1.call-update) | async-done | bytes 26738704 | tf_op jit(solution)/shard_map/all_gather | solution.py:567
  200.1 8.1 fusion.55.gate_ref
  208.2 7.9 fusion.57.signal_ref
  216.1 21.0 %state_forward.1 = (f32[512,1536]{1,0:T(8,128)}, f32[512,128]{1,0:T(8,128)}) custom-call(f32[512,1536]{1,0:T(8,128)} %fusion.57.signal_ref, f32[512,1536]{1,0:T(8,128)} %fusion.55.gate_ref, f32[5,1536]{1,0:T(8,128)S(1)} %copy-done.46, f32[1,1536]{1,0:T(1,128)S(1)} %broadcast_in_dim_reshape.2.skip_ref, bf16[512,512]{1,0:T(8,128)(2,1)S(1)} %copy-done.12, ...), custom_call_target="tpu_custom_call" | custom-call | flops 1610612736 | bytes 9437184 | tf_op jit(solution)/shard_map/state_forward/pallas_call | solution.py:451
  240.0 5.0 fusion.59.query_ref.key_ref.value_ref
  245.0 8.2 attention_forward.1
  253.2 4.2 multiply_convert_fusion.5
  257.4 6.3 fusion.53
  268.4 46.0 %collective-permute-done.3 = bf16[512,2048]{1,0:T(8,128)(2,1)} collective-permute-done((bf16[512,2048]{1,0:T(8,128)(2,1)S(1)}, bf16[512,2048]{1,0:T(8,128)(2,1)}, u32[]{:S(2)}, u32[]{:S(2)}) %collective-permute-start.3) | collective-permute-done | bytes 2097184 | tf_op jit(solution)/shard_map/ppermute | solution.py:550
  314.4 6.2 fusion.81
  322.5 6.6 all-gather.3.cloned.1.call-done
  329.6 55.3 %conditional.13 = (f32[2048]{0:T(1024)S(1)}, bf16[512,2048]{1,0:T(8,128)(2,1)}, bf16[512,2048]{1,0:T(8,128)(2,1)}, bf16[512,2048]{1,0:T(8,128)(2,1)}, bf16[512,2...) conditional(s32[]{:T(128)} %convert_element_type.475, () %tuple.133, (bf16[2048,6144]{1,0:T(8,128)(2,1)}, ...), branch_computations={%region_7.8_spmd, %region_8.11_spmd} | conditional | flops 25802309632 | bytes 241219728 | solution.py:689
  329.6 7.7 fusion
  337.3 3.5 copy-done.79
  340.9 6.2 fusion.4
  347.0 10.8 %multiply_convert_fusion = (bf16[512,2048]{1,0:T(8,128)(2,1)}, bf16[512,2048]{1,0:T(8,128)(2,1)}, bf16[512,2048]{1,0:T(8,128)(2,1)}) fusion(f32[512,2048]{1,0:T(8,128)} %fusion.4, f32[512,2048]{1,0:T(8,128)S(1)} %fusion, bf16[512,2048]{1,0:T(8,128)(2,1)S(1)} %get-tuple-element.308, bf16[2048,6144]{1,0:T(8,128)(2,1)} %get-tuple-element.307), kind=kOutput, calls=%fused_computation.11 | convolution fusion | flops 4310695936 | bytes 25165824 | tf_op jit(solution)/shard_map/cond/branch_1_fun/dot_general | solution.py:26
  357.8 7.8 fusion.2
  365.6 8.5 multiply_reduce_fusion
  376.2 8.4 convert_bitcast_fusion
  387.0 26.5 %conditional.14 = (bf16[256,2048]{1,0:T(8,128)(2,1)S(1)}, bf16[256,2048]{1,0:T(8,128)(2,1)}, bf16[512,1024]{1,0:T(8,128)(2,1)}, bf16[1024,2048]{1,0:T(8,128)(2,1)}, bf16[1024,2048]{1,0:T(8,128)(2,1)}) conditional(s32[]{:T(128)} %convert_element_type.501, () %tuple.137, (bf16[2048,6144]{1,0:T(8,128)(2,1)}, bf16[512,2048]{1,0:T(8,128)(2,1)}, ...), branch_computations={%region_11.12_spmd, %region_12.13_spmd} | conditional | flops 8595177472 | bytes 39846044 | solution.py:689
  387.0 8.5 fusion.18
  396.7 4.0 pick_halves.2
  400.7 6.6 convolution_convert_fusion
  407.4 6.1 convolution_convert_fusion.1
  414.6 19.7 %collective-permute-done.4.values_ref = bf16[512,2048]{1,0:T(8,128)(2,1)} collective-permute-done((bf16[512,2048]{1,0:T(8,128)(2,1)}, bf16[512,2048]{1,0:T(8,128)(2,1)}, u32[]{:S(2)}, u32[]{:S(2)}) %collective-permute-start.4) | collective-permute-done | bytes 2097184 | tf_op jit(solution)/shard_map/ppermute | solution.py:550
  434.4 16.5 %conditional.15 = (bf16[512,2048]{1,0:T(8,128)(2,1)}, bf16[1,2,2,128,2048]{4,3,2,1,0:T(8,128)(2,1)}, bf16[512,2048]{1,0:T(8,128)(2,1)}, bf16[2,1,2,128,2048]{4,3,2,1,0:T(8,128)(2,1)}) conditional(s32[]{:T(128)} %convert_element_type.502, () %tuple.140, (bf16[512,1024]{1,0:T(8,128)(2,1)}, bf16[512,2048]{1,0:T(8,128)(2,1)}, ...), branch_computations={%region_13.14_spmd, %region_14.15_spmd} | conditional | flops 4307550208 | bytes 39845920 | solution.py:689
  434.6 5.7 add_convert_fusion
  442.9 5.6 add_convert_fusion.1
  452.2 5.6 collective-permute-start.10
  458.0 30.6 %conditional.16 = (f32[512]{0:T(512)}, f32[256,2048]{1,0:T(8,128)}, f32[512,1536]{1,0:T(8,128)}, bf16[512,2048]{1,0:T(8,128)(2,1)}, bf16[512,768]{1,0:T(8,128)(2,1)S(1)}) conditional(s32[]{:T(128)} %convert_element_type.503, () %tuple.144, (bf16[512,2048]{1,0:T(8,128)(2,1)}, bf16[512,2048]{1,0:T(8,128)(2,1)}, bf16[512,2048]{1,0:T(8,128)(2,1)}, ...), branch_computations={%region_15.16_spmd, %region_16.18_spmd} | conditional | flops 4978900480 | bytes 66592900 | solution.py:689
  458.0 5.9 fusion.80
  466.6 9.7 %multiply_reduce_fusion.2 = (f32[512]{0:T(512)}, f32[512,1536]{1,0:T(8,128)}) fusion(f32[512,1536]{1,0:T(8,128)S(1)} %copy-done.10, f32[512,1536]{1,0:T(8,128)S(1)} %copy-done.4, f32[1536]{0:T(1024)S(1)} %get-tuple-element.332, bf16[512,2048]{1,0:T(8,128)(2,1)} %get-tuple-element.1058, bf16[2048,6528]{1,0:T(8,128)(2,1)} %get-tuple-element.331), kind=kOutput, calls=%fused_computation.36 | convolution fusion | flops 3227516416 | bytes 17833984 | tf_op jit(solution)/shard_map/cond/branch_1_fun/dot_general | solution.py:26
  476.2 4.3 fusion.25.grad_ref
  480.5 8.0 attention_backward.1
  489.4 12.2 %conditional.17 = (bf16[2048,2048]{1,0:T(8,128)(2,1)}, bf16[256,2048]{0,1:T(8,128)(2,1)S(1)}) conditional(s32[]{:T(128)} %convert_element_type.504, () %tuple.147, (bf16[512,1536]{1,0:T(8,128)(2,1)}, bf16[512,512]{1,0:T(8,128)(2,1)}, bf16[512,2048]{1,0:T(8,128)(2,1)}, bf16[512,2048]{1,0:T(8,128)(2,1)S(1)}, s32[]{:T(128)}, ...), branch_computations={%region_18.19_spmd, %region_19.20_spmd} | conditional | flops 4575461376 | bytes 31588488 | solution.py:689
  493.1 8.5 convert_bitcast_fusion.1
  503.0 3.7 all-to-all-start.2
  511.1 45.2 %conditional.18 = (f32[2,8,1536]{2,1,0:T(8,128)}, f32[2,8,512]{2,1,0:T(8,128)}, f32[2,24,2]{2,1,0:T(8,128)}, bf16[512,4480]{1,0:T(8,128)(2,1)}) conditional(s32[]{:T(128)} %convert_element_type.506, () %tuple.150, (f32[1536]{0:T(1024)}, f32[512]{0:T(512)}, f32[512]{0:T(512)}, f32[512]{0:T(512)}, f32[512,2]{0,1:T(2,128)S(1)}, ...), branch_computations={%region_20.21_spmd, %region_21.22_spmd} | conditional | flops 4026587648 | bytes 16101700 | solution.py:689
  521.9 34.4 %state_backward.1 = (bf16[512,4480]{1,0:T(8,128)(2,1)}, f32[2,8,1536]{2,1,0:T(8,128)}, f32[2,8,512]{2,1,0:T(8,128)}, f32[2,24,2]{2,1,0:T(8,128)}) custom-call(f32[512,1536]{1,0:T(8,128)} %get-tuple-element.351.grad_ref, f32[512,1536]{1,0:T(8,128)} %get-tuple-element.352.out_ref, f32[512,1536]{1,0:T(8,128)} %get-tuple-element.353.gate_ref, ...), custom_call_target="tpu_custom_call" | custom-call | flops 4026531840 | bytes 15728640 | tf_op jit(solution)/shard_map/cond/branch_1_fun/state_backward/pallas_call | solution.py:476
  556.4 19.7 %conditional.19 = (bf16[1024,4480]{1,0:T(8,128)(2,1)}, bf16[256,2048]{1,0:T(8,128)(2,1)}, bf16[1,1,2,128,2048]{4,3,2,1,0:T(8,128)(2,1)S(1)}, bf16[256,2048]{1,0:...) conditional(s32[]{:T(128)} %convert_element_type.507, () %tuple.154, ...), branch_computations={%region_23.24_spmd, %region_24.25_spmd} | conditional | flops 4979556352 | bytes 42205260 | solution.py:689
  565.0 9.8 %convolution_convert_fusion.3 = bf16[1024,4480]{1,0:T(8,128)(2,1)} fusion(bf16[512,1024]{1,0:T(8,128)(2,1)S(1)} %copy-done.80, bf16[512,4480]{1,0:T(8,128)(2,1)} %get-tuple-element.379), kind=kOutput, calls=%fused_computation.56 | convolution fusion | flops 4702208000 | bytes 14811136 | tf_op jit(solution)/shard_map/cond/branch_1_fun/dot_general | solution.py:34
  579.6 22.8 %conditional.20 = (f32[2048]{0:T(1024)S(1)}, bf16[256,2048]{1,0:T(8,128)(2,1)}, bf16[256,2048]{1,0:T(8,128)(2,1)S(1)}) conditional(s32[]{:T(128)} %convert_element_type.509, () %tuple.157, (bf16[2048,6528]{1,0:T(8,128)(2,1)}, bf16[512,4480]{1,0:T(8,128)(2,1)}, f32[512,2048]{1,0:T(8,128)}, f32[2,2,128]{2,1,0:T(2,128)S(1)}, f32[512,1]{0,1:T(1,128)S(1)}, ...), branch_computations={%region_25.26_spmd, %region_26.29_spmd} | conditional | flops 9406776320 | bytes 46053484 | solution.py:689
  579.6 17.5 %multiply_reduce_fusion.3 = (f32[512]{0:T(512)S(1)}, f32[2048]{0:T(1024)S(1)}, f32[512,2048]{1,0:T(8,128)}) fusion(f32[512,2048]{1,0:T(8,128)} %get-tuple-element.388, f32[2048]{0:T(1024)S(1)} %get-tuple-element.392, f32[512]{0:T(512)S(1)} %bitcast.295, bf16[512,4480]{1,0:T(8,128)(2,1)} %get-tuple-element.386, bf16[2048,6528]{1,0:T(8,128)(2,1)} %get-tuple-element.387), kind=kOutput, calls=%fused_computation.65 | convolution fusion | flops 9401530368 | bytes 31346688 | tf_op jit(solution)/shard_map/cond/branch_1_fun/dot_general | solution.py:30
  597.1 4.2 subtract_convert_fusion.1
  602.4 8.0 collective-permute-done.12
  610.4 4.5 collective-permute-done.13
  614.9 23.1 %conditional.21 = (bf16[512,2176]{1,0:T(8,128)(2,1)}, bf16[1,2,2,128,2176]{4,3,2,1,0:T(8,128)(2,1)}, bf16[512,2304]{1,0:T(8,128)(2,1)}, bf16[2,1,2,128,2304]{4,3...) conditional(s32[]{:T(128)} %convert_element_type.510, ...), branch_computations={%region_29.30_spmd, %region_30.34_spmd} | conditional | flops 4715790336 | bytes 59525208 | solution.py:689
  615.0 9.5 %add_convert_fusion.2 = bf16[1024,4480]{1,0:T(8,128)(2,1)S(1)} fusion(bf16[1024,4480]{1,0:T(8,128)(2,1)} %get-tuple-element.396, bf16[512,1024]{1,0:T(8,128)(2,1)} %get-tuple-element.394, bf16[512,4480]{1,0:T(8,128)(2,1)} %get-tuple-element.395), kind=kOutput, calls=%fused_computation.73 | convolution fusion | flops 4711383040 | bytes 23986176 | tf_op jit(solution)/shard_map/cond/branch_1_fun/dot_general | solution.py:34
  646.2 55.5 %collective-permute-done.15 = bf16[128,2048]{1,0:T(8,128)(2,1)} collective-permute-done((bf16[128,2048]{1,0:T(8,128)(2,1)}, bf16[128,2048]{1,0:T(8,128)(2,1)}, u32[]{:S(2)}, u32[]{:S(2)}) %collective-permute-start.15) | collective-permute-done | bytes 524320 | tf_op jit(solution)/shard_map/ppermute | solution.py:553
  703.2 8.1 collective-permute-done.16
  713.5 13.0 %conditional.23 = (bf16[256,2176]{1,0:T(8,128)(2,1)}, bf16[1,1,2,128,2176]{4,3,2,1,0:T(8,128)(2,1)}, bf16[256,2304]{1,0:T(8,128)(2,1)}, bf16[1,1,2,128,2304]{4,3...) conditional(s32[]{:T(128)} %convert_element_type.512, () %tuple.167, ...), branch_computations={%region_37.38_spmd, %region_38.39_spmd} | conditional | flops 280788992 | bytes 38142112 | solution.py:689
  727.9 5.1 all-to-all-start.3
  737.0 42.7 %collective-permute-done.23 = f32[16,2048]{1,0:T(8,128)S(1)} collective-permute-done((f32[16,2048]{1,0:T(8,128)}, f32[16,2048]{1,0:T(8,128)S(1)}, u32[]{:S(2)}, u32[]{:S(2)}) %collective-permute-start.23) | collective-permute-done | bytes 131104 | tf_op jit(solution)/shard_map/ppermute | solution.py:553
  779.7 11.5 %conditional.24 = (f32[128,2048]{1,0:T(8,128)}, f32[128,2048]{1,0:T(8,128)}, bf16[128,2176]{1,0:T(8,128)(2,1)}, bf16[1,1,1,128,2176]{4,3,2,1,0:T(8,128)(2,1)S(1)...) conditional(s32[]{:T(128)} %convert_element_type.513, ...), branch_computations={%region_39.40_spmd, %region_40.41_spmd} | conditional | flops 6455296 | bytes 24969408 | solution.py:689
  784.9 3.3 fusion.49
  796.7 52.7 %collective-permute-done.24 = f32[16,2048]{1,0:T(8,128)S(1)} collective-permute-done((f32[16,2048]{1,0:T(8,128)S(1)}, f32[16,2048]{1,0:T(8,128)S(1)}, u32[]{:S(2)}, u32[]{:S(2)}) %collective-permute-start.24) | collective-permute-done | bytes 131104 | tf_op jit(solution)/shard_map/ppermute | solution.py:553
  849.4 8.1 conditional.25
  (387 shorter events, 179.0 us)
Async XLA Ops:
  7.2 16.8 %copy-start = (bf16[2,128,2048]{2,1,0:T(8,128)(2,1)S(1)}, bf16[2,128,2048]{2,1,0:T(8,128)(2,1)}, u32[]{:S(2)}) copy-start(bf16[2,128,2048]{2,1,0:T(8,128)(2,1)} %param.52) | copy-start | bytes 3145732
  7.2 181.7 %all-gather.5.cloned.1.call-start = ((), (), s32[]{:S(2)}) async-start(), calls=%async_computation.7 | async-start | bytes 28409856 | tf_op jit(solution)/shard_map/all_gather | solution.py:567
  16.0 313.0 %all-gather.3.cloned.1.call-start = ((), (), s32[]{:S(2)}) async-start(), calls=%async_computation.6 | async-start | bytes 26738688 | tf_op jit(solution)/shard_map/all_gather | solution.py:567
  18.6 14.2 %copy-start.68 = (s32[2,256]{1,0:T(2,128)S(1)}, s32[2,256]{1,0:T(2,128)}, u32[]{:S(2)}) copy-start(s32[2,256]{1,0:T(2,128)} %param.54) | copy-start | bytes 6148
  18.6 14.5 %copy-start.31 = (bf16[2,128,2048]{2,1,0:T(8,128)(2,1)S(1)}, bf16[2,128,2048]{2,1,0:T(8,128)(2,1)}, u32[]{:S(2)}) copy-start(bf16[2,128,2048]{2,1,0:T(8,128)(2,1)} %param.51) | copy-start | bytes 3145732
  24.0 92.2 %copy-start.74 = (s32[256]{0:T(256)}, s32[256]{0:T(256)S(1)}, u32[]{:S(2)}) copy-start(s32[256]{0:T(256)S(1)} %get-tuple-element.1012) | copy-start | bytes 3076
  25.4 47.3 %all-to-all-start = ((bf16[16,16,2048]{2,1,0:T(8,128)(2,1)}), bf16[16,16,2048]{2,1,0:T(8,128)(2,1)S(1)}, u32[]{:S(2)}, u32[]{:S(2)}) async-start(bf16[16,16,2048]{2,1,0:T(8,128)(2,1)} %bitcast.74), calls=%async_computation | async-start | bytes 2097152 | tf_op jit(solution)/shard_map/all_to_all | solution.py:598
  32.8 43.9 %copy-start.78 = (f32[24]{0:T(128)S(1)}, f32[24]{0:T(128)}, u32[]{:S(2)}) copy-start(f32[24]{0:T(128)} %param.74) | copy-start | bytes 292
  72.7 43.5 %all-to-all-start.1 = ((bf16[16,16,2048]{2,1,0:T(8,128)(2,1)}), bf16[16,16,2048]{2,1,0:T(8,128)(2,1)S(1)}, u32[]{:S(2)}, u32[]{:S(2)}) async-start(bf16[16,16,2048]{2,1,0:T(8,128)(2,1)} %bitcast.80), calls=%async_computation.1 | async-start | bytes 2097152 | tf_op jit(solution)/shard_map/all_to_all | solution.py:598
  76.3 480.1 %reduce-scatter.3.cloned.1.call-start = ((), (), s32[]{:S(2)}) async-start(), calls=%async_computation.8 | async-start | bytes 8912896 | tf_op jit(solution)/shard_map/reduce_scatter | solution.py:764
  76.6 168.3 %copy-start.52 = (f32[2,1,256]{2,1,0:T(1,128)}, f32[2,1,256]{2,1,0:T(1,128)S(1)}, u32[]{:S(2)}) copy-start(f32[2,1,256]{2,1,0:T(1,128)S(1)} %convert_element_type.489.seg_row_ref) | copy-start | bytes 6148
  76.9 139.2 %copy-start.50 = (f32[1,1536]{1,0:T(1,128)}, f32[1,1536]{1,0:T(1,128)S(1)}, u32[]{:S(2)}) copy-start(f32[1,1536]{1,0:T(1,128)S(1)} %broadcast_in_dim_reshape.2.skip_ref) | copy-start | bytes 18436
  76.9 168.0 %copy-start.14 = (f32[512,8]{1,0:T(8,128)}, f32[512,8]{1,0:T(8,128)S(1)}, u32[]{:S(2)}) copy-start(f32[512,8]{1,0:T(8,128)S(1)} %pad.21.columns_ref) | copy-start | bytes 49156
  77.9 40.2 %copy-start.82 = (f32[24]{0:T(128)S(1)}, f32[24]{0:T(128)}, u32[]{:S(2)}) copy-start(f32[24]{0:T(128)} %param.73) | copy-start | bytes 292
  78.4 39.8 %collective-permute-start = (bf16[256,2048]{1,0:T(8,128)(2,1)S(1)}, bf16[256,2048]{1,0:T(8,128)(2,1)S(1)}, u32[]{:S(2)}, u32[]{:S(2)}) collective-permute-start(bf16[256,2048]{1,0:T(8,128)(2,1)S(1)} %convolution_convert_fusion.9), channel_id=1, source_target_pairs={{0,1},{1,0},{2,3},{3,2},{4,5},{5,4},{6,7},{7,6},{8,9},{9,8},{10,11... | collective-permute-start | bytes 3145736 | tf_op jit(solution)/shard_map/ppermute | solution.py:550
  116.6 24.7 %collective-permute-start.1 = (bf16[256,2048]{1,0:T(8,128)(2,1)S(1)}, bf16[256,2048]{1,0:T(8,128)(2,1)S(1)}, u32[]{:S(2)}, u32[]{:S(2)}) collective-permute-start(bf16[256,2048]{1,0:T(8,128)(2,1)S(1)} %convolution_convert_fusion.7), channel_id=1, source_target_pairs={{0,1},{1,0},{2,3},{3,2},{4,5},{5,4},{6,7},{7,6},{8,9},{9,8},{10,11... | collective-permute-start | bytes 3145736 | tf_op jit(solution)/shard_map/ppermute | solution.py:550
  118.2 73.1 %copy-start.77 = (f32[24]{0:T(128)}, f32[24]{0:T(128)S(1)}, u32[]{:S(2)}) copy-start(f32[24]{0:T(128)S(1)} %exponential_negate_fusion) | copy-start | bytes 292
  146.5 42.5 %copy-start.3 = (bf16[512,2048]{1,0:T(8,128)(2,1)S(1)}, bf16[512,2048]{1,0:T(8,128)(2,1)}, u32[]{:S(2)}) copy-start(bf16[512,2048]{1,0:T(8,128)(2,1)} %multiply_convert_fusion.4.first_ref.second_ref) | copy-start | bytes 6291460
  146.5 42.5 %copy-start.76 = (f32[24]{0:T(128)S(1)}, f32[24]{0:T(128)}, u32[]{:S(2)}) copy-start(f32[24]{0:T(128)} %param.72) | copy-start | bytes 292
  195.1 20.9 %copy-start.43 = (f32[2,12,2,256]{3,2,1,0:T(2,128)}, f32[2,12,2,256]{3,2,1,0:T(2,128)S(1)}, u32[]{:S(2)}) copy-start(f32[2,12,2,256]{3,2,1,0:T(2,128)S(1)} %reshape.692.step_ref) | copy-start | bytes 147460
  238.2 15.0 %collective-permute-start.2 = (f32[512]{0:T(512)S(1)}, f32[512]{0:T(512)S(1)}, u32[]{:S(2)}, u32[]{:S(2)}) collective-permute-start(f32[512]{0:T(512)S(1)} %reduce_sum.159), channel_id=1, source_target_pairs={{0,1},{1,0},{2,3},{3,2},{4,5},{5,4},{6,7},{7,6},{8,9},{9,8},{10,11... | collective-permute-start | bytes 6152 | tf_op jit(solution)/shard_map/ppermute | solution.py:550
  266.7 47.8 %collective-permute-start.3 = (bf16[512,2048]{1,0:T(8,128)(2,1)S(1)}, bf16[512,2048]{1,0:T(8,128)(2,1)}, u32[]{:S(2)}, u32[]{:S(2)}) collective-permute-start(bf16[512,2048]{1,0:T(8,128)(2,1)S(1)} %add_convert_fusion.6), channel_id=1, source_target_pairs={{0,1},{1,0},{2,3},{3,2},{4,5},{5,4},{6,7},{7,6},{8,9},{9,8},{10,11... | collective-permute-start | bytes 6291464 | tf_op jit(solution)/shard_map/ppermute | solution.py:550
  268.4 53.5 %copy-start.63 = (f32[2048]{0:T(1024)S(1)}, f32[2048]{0:T(1024)}, u32[]{:S(2)}) copy-start(f32[2048]{0:T(1024)} %param.68) | copy-start | bytes 24580
  385.6 48.8 %collective-permute-start.4 = (bf16[512,2048]{1,0:T(8,128)(2,1)}, bf16[512,2048]{1,0:T(8,128)(2,1)}, u32[]{:S(2)}, u32[]{:S(2)}) collective-permute-start(bf16[512,2048]{1,0:T(8,128)(2,1)} %get-tuple-element.591), channel_id=1, source_target_pairs={{0,1},{1,0},{2,3},{3,2},{4,5},{5,4},{6,7},{7,6},{8,9},{9,8},{10,11... | collective-permute-start | bytes 6291464 | tf_op jit(solution)/shard_map/ppermute | solution.py:550
  413.5 20.8 %copy-start.16 = (bf16[256,2048]{1,0:T(8,128)(2,1)}, bf16[256,2048]{1,0:T(8,128)(2,1)S(1)}, u32[]{:S(2)}) copy-start(bf16[256,2048]{1,0:T(8,128)(2,1)S(1)} %get-tuple-element.605) | copy-start | bytes 3145732
  413.5 20.8 %collective-permute-start.5 = (bf16[1024,2048]{1,0:T(8,128)(2,1)}, bf16[1024,2048]{1,0:T(8,128)(2,1)}, u32[]{:S(2)}, u32[]{:S(2)}) collective-permute-start(bf16[1024,2048]{1,0:T(8,128)(2,1)} %get-tuple-element.592), channel_id=1, source_target_pairs={{0,2},{2,0},{4,6},{6,4},{8,10},{10,8},{12,14},{14,12},{16,18},{18,... | collective-permute-start | bytes 12582920 | tf_op jit(solution)/shard_map/ppermute | solution.py:553
  413.6 20.8 %collective-permute-start.6 = (bf16[1024,2048]{1,0:T(8,128)(2,1)}, bf16[1024,2048]{1,0:T(8,128)(2,1)}, u32[]{:S(2)}, u32[]{:S(2)}) collective-permute-start(bf16[1024,2048]{1,0:T(8,128)(2,1)} %get-tuple-element.593), channel_id=1, source_target_pairs={{0,2},{2,0},{4,6},{6,4},{8,10},{10,8},{12,14},{14,12},{16,18},{18,... | collective-permute-start | bytes 12582920 | tf_op jit(solution)/shard_map/ppermute | solution.py:553
  414.0 74.5 %collective-permute-start.7 = (bf16[256,2048]{1,0:T(8,128)(2,1)}, bf16[256,2048]{1,0:T(8,128)(2,1)}, u32[]{:S(2)}, u32[]{:S(2)}) collective-permute-start(bf16[256,2048]{1,0:T(8,128)(2,1)} %get-tuple-element.606), channel_id=1, source_target_pairs={{0,1},{1,0},{2,3},{3,2},{4,5},{5,4},{6,7},{7,6},{8,9},{9,8},{10,11... | collective-permute-start | bytes 3145736 | tf_op jit(solution)/shard_map/ppermute | solution.py:550
  434.4 23.4 %copy-start.75 = (s32[256]{0:T(256)S(1)}, s32[256]{0:T(256)}, u32[]{:S(2)}) copy-start(s32[256]{0:T(256)} %copy-done.74) | copy-start | bytes 3076
  434.4 23.5 %copy-start.15 = (f32[512,8]{1,0:T(8,128)S(1)}, f32[512,8]{1,0:T(8,128)}, u32[]{:S(2)}) copy-start(f32[512,8]{1,0:T(8,128)} %copy-done.14) | copy-start | bytes 49156
  434.4 23.5 %copy-start.24 = (f32[512,128]{1,0:T(8,128)S(1)}, f32[512,128]{1,0:T(8,128)}, u32[]{:S(2)}) copy-start(f32[512,128]{1,0:T(8,128)} %get-tuple-element.1018.cosine_ref) | copy-start | bytes 786436
  434.4 23.5 %copy-start.53 = (f32[2,1,256]{2,1,0:T(1,128)S(1)}, f32[2,1,256]{2,1,0:T(1,128)}, u32[]{:S(2)}) copy-start(f32[2,1,256]{2,1,0:T(1,128)} %copy-done.52) | copy-start | bytes 6148
  434.4 23.5 %copy-start.59 = (f32[1536]{0:T(1024)S(1)}, f32[1536]{0:T(1024)}, u32[]{:S(2)}) copy-start(f32[1536]{0:T(1024)} %param.71) | copy-start | bytes 18436
  450.9 105.4 %collective-permute-start.9 = (bf16[512,2048]{1,0:T(8,128)(2,1)}, bf16[512,2048]{1,0:T(8,128)(2,1)}, u32[]{:S(2)}, u32[]{:S(2)}) collective-permute-start(bf16[512,2048]{1,0:T(8,128)(2,1)} %get-tuple-element.618), channel_id=1, source_target_pairs={{0,4},{2,6},{4,0},{6,2},{8,12},{10,14},{12,8},{14,10},{16,20},{18,... | collective-permute-start | bytes 6291464 | tf_op jit(solution)/shard_map/ppermute | solution.py:553
  452.2 104.2 %collective-permute-start.10 = (bf16[512,2048]{1,0:T(8,128)(2,1)}, bf16[512,2048]{1,0:T(8,128)(2,1)}, u32[]{:S(2)}, u32[]{:S(2)}) collective-permute-start(bf16[512,2048]{1,0:T(8,128)(2,1)} %get-tuple-element.620), channel_id=1, source_target_pairs={{0,8},{2,10},{4,12},{6,14},{8,0},{10,2},{12,4},{14,6},{16,24},{18,... | collective-permute-start | bytes 6291464 | tf_op jit(solution)/shard_map/ppermute | solution.py:553
  457.9 30.7 %copy-start.29 = (bf16[256,256]{1,0:T(8,128)(2,1)}, bf16[256,256]{1,0:T(8,128)(2,1)S(1)}, u32[]{:S(2)}) copy-start(bf16[256,256]{1,0:T(8,128)(2,1)S(1)} %fusion.67) | copy-start | bytes 393220
  458.0 30.6 %copy-start.8 = (bf16[512,2048]{1,0:T(8,128)(2,1)S(1)}, bf16[512,2048]{1,0:T(8,128)(2,1)}, u32[]{:S(2)}) copy-start(bf16[512,2048]{1,0:T(8,128)(2,1)} %copy-done.7) | copy-start | bytes 6291460
  503.0 53.3 %all-to-all-start.2 = ((bf16[16,16,2048]{2,1,0:T(8,128)(2,1)}), bf16[16,16,2048]{2,1,0:T(8,128)(2,1)S(1)}, u32[]{:S(2)}, u32[]{:S(2)}) async-start(bf16[16,16,2048]{2,1,0:T(8,128)(2,1)} %bitcast.97), calls=%async_computation.3 | async-start | bytes 2097152 | tf_op jit(solution)/shard_map/all_to_all | solution.py:598
  506.7 196.6 %reduce-scatter.5.cloned.1.call-start = ((), (), s32[]{:S(2)}) async-start(), calls=%async_computation.9 | async-start | bytes 8912896 | tf_op jit(solution)/shard_map/reduce_scatter | solution.py:827
  507.3 3.8 collective-permute-start.8
  556.4 23.1 %copy-start.65 = (f32[2048]{0:T(1024)S(1)}, f32[2048]{0:T(1024)}, u32[]{:S(2)}) copy-start(f32[2048]{0:T(1024)} %param.67) | copy-start | bytes 24580
  556.4 23.1 %copy-start.67 = (f32[2,2,128]{2,1,0:T(2,128)S(1)}, f32[2,2,128]{2,1,0:T(2,128)}, u32[]{:S(2)}) copy-start(f32[2,2,128]{2,1,0:T(2,128)} %copy-done.66) | copy-start | bytes 6148
  556.4 23.1 %copy-start.70 = (f32[512,1]{0,1:T(1,128)S(1)}, f32[512,1]{0,1:T(1,128)}, u32[]{:S(2)}) copy-start(f32[512,1]{0,1:T(1,128)} %copy-done.69) | copy-start | bytes 6148
  556.4 23.1 %copy-start.72 = (f32[512,1]{0,1:T(1,128)S(1)}, f32[512,1]{0,1:T(1,128)}, u32[]{:S(2)}) copy-start(f32[512,1]{0,1:T(1,128)} %copy-done.71) | copy-start | bytes 6148
  576.2 38.7 %collective-permute-start.11 = (bf16[1024,4480]{1,0:T(8,128)(2,1)}, bf16[1024,4480]{1,0:T(8,128)(2,1)}, u32[]{:S(2)}, u32[]{:S(2)}) collective-permute-start(bf16[1024,4480]{1,0:T(8,128)(2,1)} %get-tuple-element.627), channel_id=1, source_target_pairs={{0,2},{2,0},{4,6},{6,4},{8,10},{10,8},{12,14},{14,12},{16,18},{18,... | collective-permute-start | bytes 27525128 | tf_op jit(solution)/shard_map/ppermute | solution.py:553
  576.2 34.2 %collective-permute-start.12 = (bf16[256,2048]{1,0:T(8,128)(2,1)}, bf16[256,2048]{1,0:T(8,128)(2,1)}, u32[]{:S(2)}, u32[]{:S(2)}) collective-permute-start(bf16[256,2048]{1,0:T(8,128)(2,1)} %get-tuple-element.630), channel_id=1, source_target_pairs={{0,8},{2,10},{4,12},{6,14},{8,0},{10,2},{12,4},{14,6},{16,24},{18,... | collective-permute-start | bytes 3145736 | tf_op jit(solution)/shard_map/ppermute | solution.py:553
  578.0 36.8 %collective-permute-start.13 = (bf16[256,2048]{1,0:T(8,128)(2,1)}, bf16[256,2048]{1,0:T(8,128)(2,1)}, u32[]{:S(2)}, u32[]{:S(2)}) collective-permute-start(bf16[256,2048]{1,0:T(8,128)(2,1)} %get-tuple-element.632), channel_id=1, source_target_pairs={{0,4},{2,6},{4,0},{6,2},{8,12},{10,14},{12,8},{14,10},{16,20},{18,... | collective-permute-start | bytes 3145736 | tf_op jit(solution)/shard_map/ppermute | solution.py:553
  579.5 35.3 %copy-start.62 = (f32[2048]{0:T(1024)S(1)}, f32[2048]{0:T(1024)}, u32[]{:S(2)}) copy-start(f32[2048]{0:T(1024)} %copy-done.61) | copy-start | bytes 24580
  638.0 75.4 %collective-permute-start.18 = (bf16[512,2304]{1,0:T(8,128)(2,1)}, bf16[512,2304]{1,0:T(8,128)(2,1)}, u32[]{:S(2)}, u32[]{:S(2)}) collective-permute-start(bf16[512,2304]{1,0:T(8,128)(2,1)} %get-tuple-element.649), channel_id=1, source_target_pairs={{0,8},{2,10},{4,12},{6,14},{8,0},{10,2},{12,4},{14,6},{16,24},{18,... | collective-permute-start | bytes 7077896 | tf_op jit(solution)/shard_map/ppermute | solution.py:553
  638.4 72.9 %collective-permute-start.17 = (bf16[512,2176]{1,0:T(8,128)(2,1)}, bf16[512,2176]{1,0:T(8,128)(2,1)}, u32[]{:S(2)}, u32[]{:S(2)}) collective-permute-start(bf16[512,2176]{1,0:T(8,128)(2,1)} %get-tuple-element.647), channel_id=1, source_target_pairs={{0,4},{2,6},{4,0},{6,2},{8,12},{10,14},{12,8},{14,10},{16,20},{18,... | collective-permute-start | bytes 6684680 | tf_op jit(solution)/shard_map/ppermute | solution.py:553
  640.0 71.3 %collective-permute-start.20 = (bf16[256,2048]{1,0:T(8,128)(2,1)}, bf16[256,2048]{1,0:T(8,128)(2,1)S(1)}, u32[]{:S(2)}, u32[]{:S(2)}) collective-permute-start(bf16[256,2048]{1,0:T(8,128)(2,1)} %get-tuple-element.652), channel_id=1, source_target_pairs={{0,1},{1,0},{2,3},{3,2},{4,5},{5,4},{6,7},{7,6},{8,9},{9,8},{10,11... | collective-permute-start | bytes 3145736 | tf_op jit(solution)/shard_map/ppermute | solution.py:550
  640.6 2.3 collective-permute-start.14
  640.6 61.1 %collective-permute-start.15 = (bf16[128,2048]{1,0:T(8,128)(2,1)}, bf16[128,2048]{1,0:T(8,128)(2,1)}, u32[]{:S(2)}, u32[]{:S(2)}) collective-permute-start(bf16[128,2048]{1,0:T(8,128)(2,1)} %get-tuple-element.642), channel_id=1, source_target_pairs={{0,16},{2,18},{4,20},{6,22},{8,24},{10,26},{12,28},{14,30},{16,0},... | collective-permute-start | bytes 1572872 | tf_op jit(solution)/shard_map/ppermute | solution.py:553
  642.9 68.4 %collective-permute-start.16 = (bf16[128,2048]{1,0:T(8,128)(2,1)}, bf16[128,2048]{1,0:T(8,128)(2,1)}, u32[]{:S(2)}, u32[]{:S(2)}) collective-permute-start(bf16[128,2048]{1,0:T(8,128)(2,1)} %get-tuple-element.643), channel_id=1, source_target_pairs={{0,16},{2,18},{4,20},{6,22},{8,24},{10,26},{12,28},{14,30},{16,0},... | collective-permute-start | bytes 1572872 | tf_op jit(solution)/shard_map/ppermute | solution.py:553
  701.6 9.7 %collective-permute-start.19 = (f32[16,2048]{1,0:T(8,128)}, f32[16,2048]{1,0:T(8,128)}, u32[]{:S(2)}, u32[]{:S(2)}) collective-permute-start(f32[16,2048]{1,0:T(8,128)} %get-tuple-element.1162), channel_id=1, source_target_pairs={{0,4},{2,6},{4,0},{6,2},{8,12},{10,14},{12,8},{14,10},{16,20},{18,... | collective-permute-start | bytes 393224 | tf_op jit(solution)/shard_map/ppermute | solution.py:553
  727.9 121.5 %all-to-all-start.3 = ((bf16[16,16,2048]{2,1,0:T(8,128)(2,1)}), bf16[16,16,2048]{2,1,0:T(8,128)(2,1)S(1)}, u32[]{:S(2)}, u32[]{:S(2)}) async-start(bf16[16,16,2048]{2,1,0:T(8,128)(2,1)} %bitcast.98), calls=%async_computation.5 | async-start | bytes 2097152 | tf_op jit(solution)/shard_map/all_to_all | solution.py:598
  733.0 46.7 %collective-permute-start.22 = (bf16[256,2304]{1,0:T(8,128)(2,1)}, bf16[256,2304]{1,0:T(8,128)(2,1)S(1)}, u32[]{:S(2)}, u32[]{:S(2)}) collective-permute-start(bf16[256,2304]{1,0:T(8,128)(2,1)} %get-tuple-element.663), channel_id=1, source_target_pairs={{0,4},{2,6},{4,0},{6,2},{8,12},{10,14},{12,8},{14,10},{16,20},{18,... | collective-permute-start | bytes 3538952 | tf_op jit(solution)/shard_map/ppermute | solution.py:553
  735.0 44.7 %collective-permute-start.21 = (bf16[256,2176]{1,0:T(8,128)(2,1)}, bf16[256,2176]{1,0:T(8,128)(2,1)}, u32[]{:S(2)}, u32[]{:S(2)}) collective-permute-start(bf16[256,2176]{1,0:T(8,128)(2,1)} %get-tuple-element.661), channel_id=1, source_target_pairs={{0,8},{2,10},{4,12},{6,14},{8,0},{10,2},{12,4},{14,6},{16,24},{18,... | collective-permute-start | bytes 3342344 | tf_op jit(solution)/shard_map/ppermute | solution.py:553
  736.4 43.3 %collective-permute-start.23 = (f32[16,2048]{1,0:T(8,128)}, f32[16,2048]{1,0:T(8,128)S(1)}, u32[]{:S(2)}, u32[]{:S(2)}) collective-permute-start(f32[16,2048]{1,0:T(8,128)} %get-tuple-element.664), channel_id=1, source_target_pairs={{0,8},{2,10},{4,12},{6,14},{8,0},{10,2},{12,4},{14,6},{16,24},{18,... | collective-permute-start | bytes 393224 | tf_op jit(solution)/shard_map/ppermute | solution.py:553
  791.2 58.2 %collective-permute-start.26 = (bf16[128,2304]{1,0:T(8,128)(2,1)}, bf16[128,2304]{1,0:T(8,128)(2,1)S(1)}, u32[]{:S(2)}, u32[]{:S(2)}) collective-permute-start(bf16[128,2304]{1,0:T(8,128)(2,1)} %get-tuple-element.673), channel_id=1, source_target_pairs={{0,16},{2,18},{4,20},{6,22},{8,24},{10,26},{12,28},{14,30},{16,0},... | collective-permute-start | bytes 1769480 | tf_op jit(solution)/shard_map/ppermute | solution.py:553
  793.8 55.6 %collective-permute-start.25 = (bf16[128,2176]{1,0:T(8,128)(2,1)}, bf16[128,2176]{1,0:T(8,128)(2,1)}, u32[]{:S(2)}, u32[]{:S(2)}) collective-permute-start(bf16[128,2176]{1,0:T(8,128)(2,1)} %get-tuple-element.671), channel_id=1, source_target_pairs={{0,16},{2,18},{4,20},{6,22},{8,24},{10,26},{12,28},{14,30},{16,0},... | collective-permute-start | bytes 1671176 | tf_op jit(solution)/shard_map/ppermute | solution.py:553
  794.2 55.2 %collective-permute-start.24 = (f32[16,2048]{1,0:T(8,128)S(1)}, f32[16,2048]{1,0:T(8,128)S(1)}, u32[]{:S(2)}, u32[]{:S(2)}) collective-permute-start(f32[16,2048]{1,0:T(8,128)S(1)} %get-tuple-element.669), channel_id=1, source_target_pairs={{0,16},{2,18},{4,20},{6,22},{8,24},{10,26},{12,28},{14,30},{16,0},... | collective-permute-start | bytes 393224 | tf_op jit(solution)/shard_map/ppermute | solution.py:553
  857.5 6.5 collective-permute-start.28
  857.5 12.1 %collective-permute-start.27 = (f32[64,512]{1,0:T(8,128)}, f32[64,512]{1,0:T(8,128)S(1)}, u32[]{:S(2)}, u32[]{:S(2)}) collective-permute-start(f32[64,512]{1,0:T(8,128)} %get-tuple-element.685), channel_id=1, source_target_pairs={{0,1},{1,0},{2,3},{3,2},{4,5},{5,4},{6,7},{7,6},{8,9},{9,8},{10,11... | collective-permute-start | bytes 393224 | tf_op jit(solution)/shard_map/ppermute | solution.py:550
  (57 other events, 232.2 us)
Sparse Core Ops, SparseCore 0:
  16.1 172.8 all-gather.4
  190.5 138.4 all-gather.2
  385.1 129.0 reduce-scatter.2
  518.2 117.8 reduce-scatter.4

commit v9 on v8

--- a/solution.py
+++ b/solution.py
@@ -825,14 +825,15 @@
     part_branch, out_sent = unit(branch_partial)
     out_moved = exchange(out_sent)
     sum_branch = lax.psum_scatter(part_branch, "dp", scatter_dimension=0, tiled=True)
+    step_sig = jax.nn.sigmoid(raw_step + step_bias).reshape(micro, rows, heads).transpose(0, 2, 1)
+    gain_row, rate_column = mixer_gain[None, :], rate[:, None]
 
     def state_space_backward():
         cross = (inv_rms**3) * ((cross_own + cross_other)[:, None] / inner_width)
-        step_sig = jax.nn.sigmoid(raw_step + step_bias).reshape(micro, rows, heads).transpose(0, 2, 1)
         columns = jnp.pad(jnp.concatenate([row_facts, inv_rms, cross], axis=1), ((0, 0), (0, 4)))
         first_right, column_sums, state_sums, head_sums = state_backward(
-            grad_gated_norm, ssm_out, gate_z, ssm_in, kernel_inner, skip_wide, mixer_gain[None, :], *layout, columns,
-            state_raw, kernel_state, step_heads, step_sig, rate[:, None], joint_low,
+            grad_gated_norm, ssm_out, gate_z, ssm_in, kernel_inner, skip_wide, gain_row, *layout, columns,
+            state_raw, kernel_state, step_heads, step_sig, rate_column, joint_low,
         )
         return column_sums, state_sums, head_sums, first_right
 
@@ -860,32 +861,30 @@
 
     def first_moves():
         moves = keep_first(normed_left[0], first_right, first_came, firsts, first_sizes)
+        return moves, lax.optimization_barrier(in_send), [red.step() for red in feeds]
+
+    moves, in_send, steps = unit(first_moves)
+    settle(feeds, steps)
+    for red, move in zip(firsts, moves):
+        red.move(*move)
+    in_other = hand_over(other_lane(in_send), 6)
+
+    def small_block():
         head_row = (jnp.sum(head_sums, axis=0).T * jnp.stack([rate, jnp.ones_like(rate)])).reshape(1, -1)
-        flat = jnp.concatenate(
+        return jnp.concatenate(
             [
                 jnp.concatenate([jnp.sum(column_sums, axis=0), jnp.sum(state_sums, axis=0)], axis=1),
                 grad_gain_in[None, :], grad_gain_mid[None, :], jnp.pad(head_row, ((0, 5), (0, width - head_row.shape[1]))),
             ]
         )
-        return moves, lax.optimization_barrier(in_send), [red.step() for red in feeds], flat
-
-    moves, in_send, steps, flat = unit(first_moves)
+    flat = unit(small_block)
     flat_moved = other_group(flat, masks[0])
-    settle(feeds, steps)
-    for red, move in zip(firsts, moves):
-        red.move(*move)
-    in_other = hand_over(other_lane(in_send), 6)
-
-    flat = unit(lambda: flat + flat_moved)
-    flat_moved = other_group(flat, masks[1])
 
     def send_input():
         in_sum = in_own.astype(f32) + in_other.astype(f32)
         return deal_order_rows((in_sum + grad_middle_own).astype(bf16))
 
-    in_moved = None
-    everything = [*feeds, *firsts]
-    bits = 2
+    bits = 1
 
     def finish():
         low, high = red_low.result, red_high.result
@@ -902,41 +901,39 @@
     order[0], arrived = lax.optimization_barrier((order[0], arrived))
     for red, came in zip(feeds, arrived):
         red.came = came
-    wides = None
-    while pending := [red for red in everything if not hasattr(red, "result")]:
+    sum_branch = arrived[-1]
+    in_moved = None
+    while red_low.stage < len(red_low.places):
+        moving = [red for red in (*firsts, *feeds) if red.stage < len(red.places)]
+        steps, flat, sent = unit(
+            lambda: (
+                [red.next() for red in moving],
+                flat + flat_moved if flat_moved is not None else flat,
+                send_input() if in_moved is None else (),
+            )
+        )
+        settle(moving, steps)
+        flat_moved = other_group(flat, masks[bits]) if bits < len(masks) else None
+        bits += 1
         if in_moved is None:
-            pending = list(firsts)
-        widen = in_moved is not None and wides is None
-        last = all(red.stage == len(red.places) for red in pending) and in_moved is not None
-
-        def round_work():
-            steps = [red.step() for red in pending]
-            added = flat + flat_moved if bits <= len(masks) else flat
-            wide = [arrived[-1].astype(f32), total_fdown_low[0].astype(f32)] if widen else ()
-            if last:
-                for red, step in zip(pending, steps):
-                    red.result = step
-                return steps, added, wide, finish()
-            return steps, added, wide, send_input() if in_moved is None else ()
-
-        steps, flat, wide, other = unit(round_work)
-        if widen:
-            wides = wide
-        if bits < len(masks):
-            flat_moved = other_group(flat, masks[bits])
-        bits += 1
-        if last:
-            break
-        settle(pending, steps)
-        if in_moved is None:
-            in_moved = exchange(other)
-    for red, step in zip(pending, steps):
-        red.result = step
-    (total_gate, total_step, (total_input, total_query, total_key, total_value), states), grad_input = other
-    while bits <= len(masks):
-        flat = flat + flat_moved
-        if bits < len(masks):
-            flat_moved = other_group(flat, masks[bits])
+            in_moved = exchange(sent)
+    totals, flat = unit(
+        lambda: (
+            [red.last() for red in feeds] + [sum_branch.astype(f32), total_fdown_low[0].astype(f32)],
+            flat + flat_moved if flat_moved is not None else flat,
+        )
+    )
+    total_fgate, total_fup, total_branch, total_fdown = totals
+    flat_moved = other_group(flat, masks[bits]) if bits < len(masks) else None
+    bits += 1
+
+    def last_work():
+        red_low.result, red_high.result = red_low.last(), red_high.last()
+        return finish(), flat + flat_moved if flat_moved is not None else flat
+
+    ((total_gate, total_step, (total_input, total_query, total_key, total_value), states), grad_input), flat = unit(last_work)
+    while bits < len(masks):
+        flat = flat + other_group(flat, masks[bits])
         bits += 1
     theirs = other_lane(flat)
     low, high = jnp.where(lane == 0, flat, theirs), jnp.where(lane == 0, theirs, flat)
@@ -953,8 +950,6 @@
     sum_bias = joined(10, heads, heads)
     sum_rate = joined(10, 0, heads)
 
-    total_fgate, total_fup = red_fgate.result, red_fup.result
-    total_branch, total_fdown = wides
     total_mix, total_attn = total_branch[:, :gate_cols], total_branch[:, gate_cols:]
     state_lane = states[0] + other_lane(states[1])
     return (

time: 888 us -> 876 us (0.986)
  waiting for transfers between devices: 382 us -> 367 us
    ppermute x19, waiting for transfers between devices: 174 us -> 160 us  [other_group(): return lax.ppermute(values, 'dp', [(i, i ^ bits) for i in range(groups)])]
  transfers between devices with their start and end apart: 37 -> 37, of which waited for: 16 -> 18; matrix products, arithmetic and copies ran while one was open for 28% -> 28% of each run, Pallas kernels for 9% -> 10%
where the time goes in v9:
time: 876 us; the launch traced here: 865 us
  waiting for transfers between devices  367 us (42%)
  matrix products  188 us (21%)
  other arithmetic  82.4 us (9%)
  Pallas kernels  82.3 us (9%)
  local copies, waits for them, and re-layouts  72.9 us (8%)
  starting transfers between devices  55.6 us (6%)
  between operations  15.7 us (2%)
    ppermute x19, waiting for transfers between devices, other_group(): return lax.ppermute(values, 'dp', [(i, i ^ bits) for i in range(groups)])  160 us
    ppermute x10, waiting for transfers between devices, other_lane(): return lax.ppermute(values, 'tensor', swap_lane)  91 us
    all_to_all x4, waiting for transfers between devices, exchange(): lax.all_to_all(buffer.reshape(groups, micro * per, width), 'dp', split_ax...  73.3 us
    dot_general x14, matrix products, project(): return jnp.dot(left, right, preferred_element_type=f32)  68.3 us
    dot_general x12, matrix products, outer_sum(): lax.dot_general(left, right, (((0,), (0,)), ((), ())), preferred_element_...  67.7 us
    dot_general x6, matrix products, project_back(): lax.dot_general(left, right, (((1,), (1,)), ((), ())), preferred_element_...  51.5 us
    all_gather x2, waiting for transfers between devices, local(): lax.all_gather(jnp.concatenate(list(group_weights.values()), axis=1), 'dp...  42.1 us
    pallas_call x1, Pallas kernels, state_backward(): pl.pallas_call(state_backward_kernel, out_shape=(jax.ShapeDtypeStruct((to...  34.2 us
  transfers between devices with their start and end apart: 37, of which 18 were waited for; matrix products, arithmetic and copies ran while one was open for 28% of the time, Pallas kernels for 10%

profile of v9, /device:TPU:0, one launch (start us, length us, event | category | flops | bytes accessed | tf_op | source)
XLA Modules:
  0.0 865.3 jit_solution(219031715790490673)
XLA Ops:
  18.8 4.9 select_reduce_fusion
  25.4 7.4 all-to-all-start
  34.5 38.2 %all-to-all-done = bf16[16,16,2048]{2,1,0:T(8,128)(2,1)S(1)} async-done(((bf16[16,16,2048]{2,1,0:T(8,128)(2,1)}), bf16[16,16,2048]{2,1,0:T(8,128)(2,1)S(1)}, u32[]{:S(2)}, u32[]{:S(2)}) %all-to-all-start) | async-done | bytes 1048608 | tf_op jit(solution)/shard_map/all_to_all | solution.py:598
  72.7 3.7 all-to-all-start.1
  81.0 35.1 %all-to-all-done.1 = bf16[16,16,2048]{2,1,0:T(8,128)(2,1)S(1)} async-done(((bf16[16,16,2048]{2,1,0:T(8,128)(2,1)}), bf16[16,16,2048]{2,1,0:T(8,128)(2,1)S(1)}, u32[]{:S(2)}, u32[]{:S(2)}) %all-to-all-start.1) | async-done | bytes 1048608 | tf_op jit(solution)/shard_map/all_to_all | solution.py:598
  120.1 21.3 %collective-permute-done.1 = bf16[256,2048]{1,0:T(8,128)(2,1)S(1)} collective-permute-done((bf16[256,2048]{1,0:T(8,128)(2,1)S(1)}, bf16[256,2048]{1,0:T(8,128)(2,1)S(1)}, u32[]{:S(2)}, u32[]{:S(2)}) %collective-permute-start.1) | collective-permute-done | bytes 1048608 | tf_op jit(solution)/shard_map/ppermute | solution.py:550
  146.6 6.9 pick_halves.3
  153.5 35.5 %all-gather.5.cloned.1.call-done = bf16[2048,6528]{1,0:T(8,128)(2,1)} async-done(((bf16[128,6528]{1,0:T(8,128)(2,1)}), bf16[2048,6528]{1,0:T(8,128)(2,1)}) %all-gather.5.cloned.1.call-update) | async-done | bytes 26738704 | tf_op jit(solution)/shard_map/all_gather | solution.py:567
  200.1 8.1 fusion.55.gate_ref
  208.2 7.9 fusion.57.signal_ref
  216.1 21.0 %state_forward.1 = (f32[512,1536]{1,0:T(8,128)}, f32[512,128]{1,0:T(8,128)}) custom-call(f32[512,1536]{1,0:T(8,128)} %fusion.57.signal_ref, f32[512,1536]{1,0:T(8,128)} %fusion.55.gate_ref, f32[5,1536]{1,0:T(8,128)S(1)} %copy-done.46, f32[1,1536]{1,0:T(1,128)S(1)} %broadcast_in_dim_reshape.2.skip_ref, bf16[512,512]{1,0:T(8,128)(2,1)S(1)} %copy-done.12, ...), custom_call_target="tpu_custom_call" | custom-call | flops 1610612736 | bytes 9437184 | tf_op jit(solution)/shard_map/state_forward/pallas_call | solution.py:451
  240.0 5.0 fusion.59.query_ref.key_ref.value_ref
  244.9 8.2 attention_forward.1
  253.2 4.2 multiply_convert_fusion.5
  257.4 6.3 fusion.53
  268.4 46.0 %collective-permute-done.3 = bf16[512,2048]{1,0:T(8,128)(2,1)} collective-permute-done((bf16[512,2048]{1,0:T(8,128)(2,1)S(1)}, bf16[512,2048]{1,0:T(8,128)(2,1)}, u32[]{:S(2)}, u32[]{:S(2)}) %collective-permute-start.3) | collective-permute-done | bytes 2097184 | tf_op jit(solution)/shard_map/ppermute | solution.py:550
  314.4 6.2 fusion.80
  322.4 6.6 all-gather.3.cloned.1.call-done
  329.6 55.3 %conditional.14 = (f32[2048]{0:T(1024)S(1)}, bf16[512,2048]{1,0:T(8,128)(2,1)}, bf16[512,2048]{1,0:T(8,128)(2,1)}, bf16[512,2048]{1,0:T(8,128)(2,1)}, bf16[512,2...) conditional(s32[]{:T(128)} %convert_element_type.472, () %tuple.142, (bf16[2048,6144]{1,0:T(8,128)(2,1)}, ...), branch_computations={%region_7.8_spmd, %region_8.11_spmd} | conditional | flops 25802309632 | bytes 241219728 | solution.py:689
  329.6 7.7 fusion
  340.9 6.2 fusion.4
  347.1 10.8 %multiply_convert_fusion = (bf16[512,2048]{1,0:T(8,128)(2,1)}, bf16[512,2048]{1,0:T(8,128)(2,1)}, bf16[512,2048]{1,0:T(8,128)(2,1)}) fusion(f32[512,2048]{1,0:T(8,128)} %fusion.4, f32[512,2048]{1,0:T(8,128)S(1)} %fusion, bf16[512,2048]{1,0:T(8,128)(2,1)S(1)} %get-tuple-element.296, bf16[2048,6144]{1,0:T(8,128)(2,1)} %get-tuple-element.295), kind=kOutput, calls=%fused_computation.11 | convolution fusion | flops 4310695936 | bytes 25165824 | tf_op jit(solution)/shard_map/cond/branch_1_fun/dot_general | solution.py:26
  357.9 7.8 fusion.2
  365.7 8.5 multiply_reduce_fusion
  376.3 8.3 convert_bitcast_fusion
  387.0 26.5 %conditional.15 = (bf16[256,2048]{1,0:T(8,128)(2,1)S(1)}, bf16[256,2048]{1,0:T(8,128)(2,1)}, bf16[512,1024]{1,0:T(8,128)(2,1)}, bf16[1024,2048]{1,0:T(8,128)(2,1)}, bf16[1024,2048]{1,0:T(8,128)(2,1)}) conditional(s32[]{:T(128)} %convert_element_type.498, () %tuple.146, (bf16[2048,6144]{1,0:T(8,128)(2,1)}, bf16[512,2048]{1,0:T(8,128)(2,1)}, ...), branch_computations={%region_11.12_spmd, %region_12.13_spmd} | conditional | flops 8595177472 | bytes 39846044 | solution.py:689
  387.0 8.5 fusion.18
  396.7 4.0 pick_halves.2
  400.7 6.7 convolution_convert_fusion
  407.4 6.2 convolution_convert_fusion.1
  414.6 19.7 %collective-permute-done.4.values_ref = bf16[512,2048]{1,0:T(8,128)(2,1)} collective-permute-done((bf16[512,2048]{1,0:T(8,128)(2,1)}, bf16[512,2048]{1,0:T(8,128)(2,1)}, u32[]{:S(2)}, u32[]{:S(2)}) %collective-permute-start.4) | collective-permute-done | bytes 2097184 | tf_op jit(solution)/shard_map/ppermute | solution.py:550
  434.4 16.6 %conditional.16 = (bf16[512,2048]{1,0:T(8,128)(2,1)}, bf16[1,2,2,128,2048]{4,3,2,1,0:T(8,128)(2,1)}, bf16[512,2048]{1,0:T(8,128)(2,1)}, bf16[2,1,2,128,2048]{4,3,2,1,0:T(8,128)(2,1)}) conditional(s32[]{:T(128)} %convert_element_type.499, () %tuple.149, (bf16[512,1024]{1,0:T(8,128)(2,1)}, bf16[512,2048]{1,0:T(8,128)(2,1)}, ...), branch_computations={%region_13.14_spmd, %region_14.15_spmd} | conditional | flops 4307550208 | bytes 39845920 | solution.py:689
  434.6 5.7 add_convert_fusion
  442.9 5.6 add_convert_fusion.1
  452.2 5.6 collective-permute-start.10
  458.0 30.4 %conditional.17 = (f32[512]{0:T(512)}, f32[256,2048]{1,0:T(8,128)}, f32[512,1536]{1,0:T(8,128)}, bf16[512,2048]{1,0:T(8,128)(2,1)}, bf16[512,768]{1,0:T(8,128)(2,1)S(1)}) conditional(s32[]{:T(128)} %convert_element_type.500, () %tuple.153, (bf16[512,2048]{1,0:T(8,128)(2,1)}, bf16[512,2048]{1,0:T(8,128)(2,1)}, bf16[512,2048]{1,0:T(8,128)(2,1)}, ...), branch_computations={%region_15.16_spmd, %region_16.18_spmd} | conditional | flops 4978900480 | bytes 66592900 | solution.py:689
  458.0 5.9 fusion.79
  466.6 9.5 %multiply_reduce_fusion.2 = (f32[512]{0:T(512)}, f32[512,1536]{1,0:T(8,128)}) fusion(f32[512,1536]{1,0:T(8,128)S(1)} %copy-done.10, f32[512,1536]{1,0:T(8,128)S(1)} %copy-done.4, f32[1536]{0:T(1024)S(1)} %get-tuple-element.320, bf16[512,2048]{1,0:T(8,128)(2,1)} %get-tuple-element.1013, bf16[2048,6528]{1,0:T(8,128)(2,1)} %get-tuple-element.319), kind=kOutput, calls=%fused_computation.36 | convolution fusion | flops 3227516416 | bytes 17833984 | tf_op jit(solution)/shard_map/cond/branch_1_fun/dot_general | solution.py:26
  476.0 4.3 fusion.25.grad_ref
  480.3 8.0 attention_backward.1
  489.2 12.2 %conditional.18 = (bf16[2048,2048]{1,0:T(8,128)(2,1)}, bf16[256,2048]{0,1:T(8,128)(2,1)S(1)}) conditional(s32[]{:T(128)} %convert_element_type.501, () %tuple.156, (bf16[512,1536]{1,0:T(8,128)(2,1)}, bf16[512,512]{1,0:T(8,128)(2,1)}, bf16[512,2048]{1,0:T(8,128)(2,1)}, bf16[512,2048]{1,0:T(8,128)(2,1)S(1)}, s32[]{:T(128)}, ...), branch_computations={%region_18.19_spmd, %region_19.20_spmd} | conditional | flops 4575461376 | bytes 31588488 | solution.py:689
  492.9 8.5 convert_bitcast_fusion.1
  502.8 3.7 all-to-all-start.2
  510.9 43.4 %conditional.19 = (f32[2,8,1536]{2,1,0:T(8,128)}, f32[2,8,512]{2,1,0:T(8,128)}, f32[2,24,2]{2,1,0:T(8,128)}, bf16[512,4480]{1,0:T(8,128)(2,1)}) conditional(s32[]{:T(128)} %convert_element_type.503, () %tuple.159, (f32[1536]{0:T(1024)}, f32[512]{0:T(512)}, f32[512]{0:T(512)}, f32[512]{0:T(512)}, f32[512,2]{0,1:T(2,128)S(1)}, ...), branch_computations={%region_20.21_spmd, %region_21.22_spmd} | conditional | flops 4026538496 | bytes 15904996 | solution.py:689
  520.2 34.2 %state_backward.1 = (bf16[512,4480]{1,0:T(8,128)(2,1)}, f32[2,8,1536]{2,1,0:T(8,128)}, f32[2,8,512]{2,1,0:T(8,128)}, f32[2,24,2]{2,1,0:T(8,128)}) custom-call(f32[512,1536]{1,0:T(8,128)} %get-tuple-element.339.grad_ref, f32[512,1536]{1,0:T(8,128)} %get-tuple-element.340.out_ref, f32[512,1536]{1,0:T(8,128)} %get-tuple-element.341.gate_ref, ...), custom_call_target="tpu_custom_call" | custom-call | flops 4026531840 | bytes 15728640 | tf_op jit(solution)/shard_map/cond/branch_1_fun/state_backward/pallas_call | solution.py:476
  554.4 19.7 %conditional.20 = (bf16[1024,4480]{1,0:T(8,128)(2,1)}, bf16[256,2048]{1,0:T(8,128)(2,1)}, bf16[1,1,2,128,2048]{4,3,2,1,0:T(8,128)(2,1)S(1)}, bf16[256,2048]{1,0:...) conditional(s32[]{:T(128)} %convert_element_type.504, () %tuple.163, ...), branch_computations={%region_23.24_spmd, %region_24.25_spmd} | conditional | flops 4979556352 | bytes 42205260 | solution.py:689
  563.0 9.7 %convolution_convert_fusion.3 = bf16[1024,4480]{1,0:T(8,128)(2,1)} fusion(bf16[512,1024]{1,0:T(8,128)(2,1)S(1)} %copy-done.80, bf16[512,4480]{1,0:T(8,128)(2,1)} %get-tuple-element.366), kind=kOutput, calls=%fused_computation.54 | convolution fusion | flops 4702208000 | bytes 14811136 | tf_op jit(solution)/shard_map/cond/branch_1_fun/dot_general | solution.py:34
  577.5 23.0 %conditional.21 = (f32[2048]{0:T(1024)S(1)}, bf16[256,2048]{1,0:T(8,128)(2,1)}, bf16[256,2048]{1,0:T(8,128)(2,1)S(1)}) conditional(s32[]{:T(128)} %convert_element_type.506, () %tuple.166, (bf16[2048,6528]{1,0:T(8,128)(2,1)}, bf16[512,4480]{1,0:T(8,128)(2,1)}, f32[512,2048]{1,0:T(8,128)}, f32[2,2,128]{2,1,0:T(2,128)S(1)}, f32[512,1]{0,1:T(1,128)S(1)}, ...), branch_computations={%region_25.26_spmd, %region_26.29_spmd} | conditional | flops 9406776320 | bytes 46053484 | solution.py:689
  577.5 17.5 %multiply_reduce_fusion.3 = (f32[512]{0:T(512)S(1)}, f32[2048]{0:T(1024)S(1)}, f32[512,2048]{1,0:T(8,128)}) fusion(f32[512,2048]{1,0:T(8,128)} %get-tuple-element.375, f32[2048]{0:T(1024)S(1)} %get-tuple-element.379, f32[512]{0:T(512)S(1)} %bitcast.295, bf16[512,4480]{1,0:T(8,128)(2,1)} %get-tuple-element.373, bf16[2048,6528]{1,0:T(8,128)(2,1)} %get-tuple-element.374), kind=kOutput, calls=%fused_computation.63 | convolution fusion | flops 9401530368 | bytes 31346688 | tf_op jit(solution)/shard_map/cond/branch_1_fun/dot_general | solution.py:30
  595.0 4.3 subtract_convert_fusion.1
  600.4 9.8 %collective-permute-done.12 = bf16[256,2048]{1,0:T(8,128)(2,1)} collective-permute-done((bf16[256,2048]{1,0:T(8,128)(2,1)}, bf16[256,2048]{1,0:T(8,128)(2,1)}, u32[]{:S(2)}, u32[]{:S(2)}) %collective-permute-start.12) | collective-permute-done | bytes 1048608 | tf_op jit(solution)/shard_map/ppermute | solution.py:553
  612.9 19.6 %conditional.22 = (bf16[512,2176]{1,0:T(8,128)(2,1)}, bf16[1,2,2,128,2176]{4,3,2,1,0:T(8,128)(2,1)}, bf16[512,2304]{1,0:T(8,128)(2,1)}, bf16[2,1,2,128,2304]{4,3...) conditional(s32[]{:T(128)} %convert_element_type.507, ...), branch_computations={%region_29.30_spmd, %region_30.31_spmd} | conditional | flops 4715577344 | bytes 59113572 | solution.py:689
  613.0 9.3 %add_convert_fusion.2 = bf16[1024,4480]{1,0:T(8,128)(2,1)S(1)} fusion(bf16[1024,4480]{1,0:T(8,128)(2,1)} %get-tuple-element.383, bf16[512,1024]{1,0:T(8,128)(2,1)} %get-tuple-element.381, bf16[512,4480]{1,0:T(8,128)(2,1)} %get-tuple-element.382), kind=kOutput, calls=%fused_computation.71 | convolution fusion | flops 4711383040 | bytes 23986176 | tf_op jit(solution)/shard_map/cond/branch_1_fun/dot_general | solution.py:34
  637.9 9.0 %conditional.23 = (f32[16,2048]{1,0:T(8,128)}) conditional(s32[]{:T(128)} %convert_element_type.508, () %tuple.172, (f32[2,8,1536]{2,1,0:T(8,128)}, f32[2,8,512]{2,1,0:T(8,128)}, f32[2048]{0:T(1024)}, f32[2048]{0:T(1024)}, f32[2,24,2]{2,1,0:T(8,128)}, /*index=5*/f32[24]{0:T(128)}) %tuple.324), branch_computations={%region_31.32_spmd, %region_32.36_spmd} | conditional | flops 213088 | bytes 411636 | solution.py:689
  646.9 49.3 %collective-permute-done.14 = bf16[128,2048]{1,0:T(8,128)(2,1)} collective-permute-done((bf16[128,2048]{1,0:T(8,128)(2,1)}, bf16[128,2048]{1,0:T(8,128)(2,1)}, u32[]{:S(2)}, u32[]{:S(2)}) %collective-permute-start.14) | collective-permute-done | bytes 524320 | tf_op jit(solution)/shard_map/ppermute | solution.py:553
  696.2 10.6 %collective-permute-done.15 = bf16[128,2048]{1,0:T(8,128)(2,1)} collective-permute-done((bf16[128,2048]{1,0:T(8,128)(2,1)}, bf16[128,2048]{1,0:T(8,128)(2,1)}, u32[]{:S(2)}, u32[]{:S(2)}) %collective-permute-start.15) | collective-permute-done | bytes 524320 | tf_op jit(solution)/shard_map/ppermute | solution.py:553
  709.0 13.0 %conditional.24 = (bf16[256,2176]{1,0:T(8,128)(2,1)}, bf16[1,1,2,128,2176]{4,3,2,1,0:T(8,128)(2,1)}, bf16[256,2304]{1,0:T(8,128)(2,1)}, bf16[1,1,2,128,2304]{4,3...) conditional(s32[]{:T(128)} %convert_element_type.509, () %tuple.176, ...), branch_computations={%region_37.38_spmd, %region_38.39_spmd} | conditional | flops 280788992 | bytes 38142112 | solution.py:689
  723.5 4.8 all-to-all-start.3
  732.2 38.5 %collective-permute-done.22 = f32[16,2048]{1,0:T(8,128)S(1)} collective-permute-done((f32[16,2048]{1,0:T(8,128)}, f32[16,2048]{1,0:T(8,128)S(1)}, u32[]{:S(2)}, u32[]{:S(2)}) %collective-permute-start.22) | collective-permute-done | bytes 131104 | tf_op jit(solution)/shard_map/ppermute | solution.py:553
  772.2 6.2 conditional.25
  782.2 26.2 %collective-permute-done.23 = f32[16,2048]{1,0:T(8,128)} collective-permute-done((f32[16,2048]{1,0:T(8,128)S(1)}, f32[16,2048]{1,0:T(8,128)}, u32[]{:S(2)}, u32[]{:S(2)}) %collective-permute-start.23) | collective-permute-done | bytes 131104 | tf_op jit(solution)/shard_map/ppermute | solution.py:553
  808.4 6.3 conditional.26
  817.4 19.2 %collective-permute-done.26 = f32[16,2048]{1,0:T(8,128)S(1)} collective-permute-done((f32[16,2048]{1,0:T(8,128)S(1)}, f32[16,2048]{1,0:T(8,128)S(1)}, u32[]{:S(2)}, u32[]{:S(2)}) %collective-permute-start.26) | collective-permute-done | bytes 131104 | tf_op jit(solution)/shard_map/ppermute | solution.py:553
  836.6 9.2 %conditional.27 = (f32[128,1536]{1,0:T(8,128)}, f32[128,24]{1,0:T(8,128)}, f32[128,1536]{1,0:T(8,128)}, f32[128,512]{1,0:T(8,128)}, f32[128,128]{1,0:T(8,128)}, ...) conditional(s32[]{:T(128)} %convert_element_type.512, ...), branch_computations={%region_43.44_spmd, %region_44.45_spmd} | conditional | flops 270712832 | bytes 13263072 | solution.py:689
  (387 shorter events, 191.1 us)
Async XLA Ops:
  7.2 16.8 %copy-start = (bf16[2,128,2048]{2,1,0:T(8,128)(2,1)S(1)}, bf16[2,128,2048]{2,1,0:T(8,128)(2,1)}, u32[]{:S(2)}) copy-start(bf16[2,128,2048]{2,1,0:T(8,128)(2,1)} %param.54) | copy-start | bytes 3145732
  7.2 181.7 %all-gather.5.cloned.1.call-start = ((), (), s32[]{:S(2)}) async-start(), calls=%async_computation.7 | async-start | bytes 28409856 | tf_op jit(solution)/shard_map/all_gather | solution.py:567
  16.0 313.1 %all-gather.3.cloned.1.call-start = ((), (), s32[]{:S(2)}) async-start(), calls=%async_computation.6 | async-start | bytes 26738688 | tf_op jit(solution)/shard_map/all_gather | solution.py:567
  18.6 14.5 %copy-start.31 = (bf16[2,128,2048]{2,1,0:T(8,128)(2,1)S(1)}, bf16[2,128,2048]{2,1,0:T(8,128)(2,1)}, u32[]{:S(2)}) copy-start(bf16[2,128,2048]{2,1,0:T(8,128)(2,1)} %param.53) | copy-start | bytes 3145732
  24.0 92.2 %copy-start.74 = (s32[256]{0:T(256)}, s32[256]{0:T(256)S(1)}, u32[]{:S(2)}) copy-start(s32[256]{0:T(256)S(1)} %get-tuple-element.969) | copy-start | bytes 3076
  25.4 47.3 %all-to-all-start = ((bf16[16,16,2048]{2,1,0:T(8,128)(2,1)}), bf16[16,16,2048]{2,1,0:T(8,128)(2,1)S(1)}, u32[]{:S(2)}, u32[]{:S(2)}) async-start(bf16[16,16,2048]{2,1,0:T(8,128)(2,1)} %bitcast.73), calls=%async_computation | async-start | bytes 2097152 | tf_op jit(solution)/shard_map/all_to_all | solution.py:598
  32.8 43.9 %copy-start.78 = (f32[24]{0:T(128)S(1)}, f32[24]{0:T(128)}, u32[]{:S(2)}) copy-start(f32[24]{0:T(128)} %param.76) | copy-start | bytes 292
  72.7 43.5 %all-to-all-start.1 = ((bf16[16,16,2048]{2,1,0:T(8,128)(2,1)}), bf16[16,16,2048]{2,1,0:T(8,128)(2,1)S(1)}, u32[]{:S(2)}, u32[]{:S(2)}) async-start(bf16[16,16,2048]{2,1,0:T(8,128)(2,1)} %bitcast.79), calls=%async_computation.1 | async-start | bytes 2097152 | tf_op jit(solution)/shard_map/all_to_all | solution.py:598
  76.3 478.1 %reduce-scatter.3.cloned.1.call-start = ((), (), s32[]{:S(2)}) async-start(), calls=%async_computation.8 | async-start | bytes 8912896 | tf_op jit(solution)/shard_map/reduce_scatter | solution.py:764
  76.6 168.3 %copy-start.52 = (f32[2,1,256]{2,1,0:T(1,128)}, f32[2,1,256]{2,1,0:T(1,128)S(1)}, u32[]{:S(2)}) copy-start(f32[2,1,256]{2,1,0:T(1,128)S(1)} %convert_element_type.486.seg_row_ref) | copy-start | bytes 6148
  76.9 139.2 %copy-start.50 = (f32[1,1536]{1,0:T(1,128)}, f32[1,1536]{1,0:T(1,128)S(1)}, u32[]{:S(2)}) copy-start(f32[1,1536]{1,0:T(1,128)S(1)} %broadcast_in_dim_reshape.2.skip_ref) | copy-start | bytes 18436
  76.9 168.0 %copy-start.14 = (f32[512,8]{1,0:T(8,128)}, f32[512,8]{1,0:T(8,128)S(1)}, u32[]{:S(2)}) copy-start(f32[512,8]{1,0:T(8,128)S(1)} %pad.21.columns_ref) | copy-start | bytes 49156
  77.9 40.3 %copy-start.82 = (f32[24]{0:T(128)S(1)}, f32[24]{0:T(128)}, u32[]{:S(2)}) copy-start(f32[24]{0:T(128)} %param.75) | copy-start | bytes 292
  78.4 39.8 %collective-permute-start = (bf16[256,2048]{1,0:T(8,128)(2,1)S(1)}, bf16[256,2048]{1,0:T(8,128)(2,1)S(1)}, u32[]{:S(2)}, u32[]{:S(2)}) collective-permute-start(bf16[256,2048]{1,0:T(8,128)(2,1)S(1)} %convolution_convert_fusion.9), channel_id=1, source_target_pairs={{0,1},{1,0},{2,3},{3,2},{4,5},{5,4},{6,7},{7,6},{8,9},{9,8},{10,11... | collective-permute-start | bytes 3145736 | tf_op jit(solution)/shard_map/ppermute | solution.py:550
  116.6 24.7 %collective-permute-start.1 = (bf16[256,2048]{1,0:T(8,128)(2,1)S(1)}, bf16[256,2048]{1,0:T(8,128)(2,1)S(1)}, u32[]{:S(2)}, u32[]{:S(2)}) collective-permute-start(bf16[256,2048]{1,0:T(8,128)(2,1)S(1)} %convolution_convert_fusion.7), channel_id=1, source_target_pairs={{0,1},{1,0},{2,3},{3,2},{4,5},{5,4},{6,7},{7,6},{8,9},{9,8},{10,11... | collective-permute-start | bytes 3145736 | tf_op jit(solution)/shard_map/ppermute | solution.py:550
  118.2 73.1 %copy-start.76 = (f32[24]{0:T(128)}, f32[24]{0:T(128)S(1)}, u32[]{:S(2)}) copy-start(f32[24]{0:T(128)S(1)} %exponential_negate_fusion) | copy-start | bytes 292
  146.6 42.4 %copy-start.3 = (bf16[512,2048]{1,0:T(8,128)(2,1)S(1)}, bf16[512,2048]{1,0:T(8,128)(2,1)}, u32[]{:S(2)}) copy-start(bf16[512,2048]{1,0:T(8,128)(2,1)} %multiply_convert_fusion.4.first_ref.second_ref) | copy-start | bytes 6291460
  146.6 42.4 %copy-start.77 = (f32[24]{0:T(128)S(1)}, f32[24]{0:T(128)}, u32[]{:S(2)}) copy-start(f32[24]{0:T(128)} %param.74) | copy-start | bytes 292
  195.1 20.9 %copy-start.43 = (f32[2,12,2,256]{3,2,1,0:T(2,128)}, f32[2,12,2,256]{3,2,1,0:T(2,128)S(1)}, u32[]{:S(2)}) copy-start(f32[2,12,2,256]{3,2,1,0:T(2,128)S(1)} %reshape.687.step_ref) | copy-start | bytes 147460
  238.2 15.0 %collective-permute-start.2 = (f32[512]{0:T(512)S(1)}, f32[512]{0:T(512)S(1)}, u32[]{:S(2)}, u32[]{:S(2)}) collective-permute-start(f32[512]{0:T(512)S(1)} %reduce_sum.159), channel_id=1, source_target_pairs={{0,1},{1,0},{2,3},{3,2},{4,5},{5,4},{6,7},{7,6},{8,9},{9,8},{10,11... | collective-permute-start | bytes 6152 | tf_op jit(solution)/shard_map/ppermute | solution.py:550
  266.6 47.8 %collective-permute-start.3 = (bf16[512,2048]{1,0:T(8,128)(2,1)S(1)}, bf16[512,2048]{1,0:T(8,128)(2,1)}, u32[]{:S(2)}, u32[]{:S(2)}) collective-permute-start(bf16[512,2048]{1,0:T(8,128)(2,1)S(1)} %add_convert_fusion.6), channel_id=1, source_target_pairs={{0,1},{1,0},{2,3},{3,2},{4,5},{5,4},{6,7},{7,6},{8,9},{9,8},{10,11... | collective-permute-start | bytes 6291464 | tf_op jit(solution)/shard_map/ppermute | solution.py:550
  268.4 53.5 %copy-start.63 = (f32[2048]{0:T(1024)S(1)}, f32[2048]{0:T(1024)}, u32[]{:S(2)}) copy-start(f32[2048]{0:T(1024)} %param.70) | copy-start | bytes 24580
  385.6 48.8 %collective-permute-start.4 = (bf16[512,2048]{1,0:T(8,128)(2,1)}, bf16[512,2048]{1,0:T(8,128)(2,1)}, u32[]{:S(2)}, u32[]{:S(2)}) collective-permute-start(bf16[512,2048]{1,0:T(8,128)(2,1)} %get-tuple-element.580), channel_id=1, source_target_pairs={{0,1},{1,0},{2,3},{3,2},{4,5},{5,4},{6,7},{7,6},{8,9},{9,8},{10,11... | collective-permute-start | bytes 6291464 | tf_op jit(solution)/shard_map/ppermute | solution.py:550
  413.5 20.8 %copy-start.16 = (bf16[256,2048]{1,0:T(8,128)(2,1)}, bf16[256,2048]{1,0:T(8,128)(2,1)S(1)}, u32[]{:S(2)}) copy-start(bf16[256,2048]{1,0:T(8,128)(2,1)S(1)} %get-tuple-element.594) | copy-start | bytes 3145732
  413.5 20.8 %collective-permute-start.5 = (bf16[1024,2048]{1,0:T(8,128)(2,1)}, bf16[1024,2048]{1,0:T(8,128)(2,1)}, u32[]{:S(2)}, u32[]{:S(2)}) collective-permute-start(bf16[1024,2048]{1,0:T(8,128)(2,1)} %get-tuple-element.581), channel_id=1, source_target_pairs={{0,2},{2,0},{4,6},{6,4},{8,10},{10,8},{12,14},{14,12},{16,18},{18,... | collective-permute-start | bytes 12582920 | tf_op jit(solution)/shard_map/ppermute | solution.py:553
  413.5 20.8 %collective-permute-start.6 = (bf16[1024,2048]{1,0:T(8,128)(2,1)}, bf16[1024,2048]{1,0:T(8,128)(2,1)}, u32[]{:S(2)}, u32[]{:S(2)}) collective-permute-start(bf16[1024,2048]{1,0:T(8,128)(2,1)} %get-tuple-element.582), channel_id=1, source_target_pairs={{0,2},{2,0},{4,6},{6,4},{8,10},{10,8},{12,14},{14,12},{16,18},{18,... | collective-permute-start | bytes 12582920 | tf_op jit(solution)/shard_map/ppermute | solution.py:553
  414.1 74.3 %collective-permute-start.7 = (bf16[256,2048]{1,0:T(8,128)(2,1)}, bf16[256,2048]{1,0:T(8,128)(2,1)}, u32[]{:S(2)}, u32[]{:S(2)}) collective-permute-start(bf16[256,2048]{1,0:T(8,128)(2,1)} %get-tuple-element.595), channel_id=1, source_target_pairs={{0,1},{1,0},{2,3},{3,2},{4,5},{5,4},{6,7},{7,6},{8,9},{9,8},{10,11... | collective-permute-start | bytes 3145736 | tf_op jit(solution)/shard_map/ppermute | solution.py:550
  434.4 23.4 %copy-start.75 = (s32[256]{0:T(256)S(1)}, s32[256]{0:T(256)}, u32[]{:S(2)}) copy-start(s32[256]{0:T(256)} %copy-done.74) | copy-start | bytes 3076
  434.4 23.6 %copy-start.15 = (f32[512,8]{1,0:T(8,128)S(1)}, f32[512,8]{1,0:T(8,128)}, u32[]{:S(2)}) copy-start(f32[512,8]{1,0:T(8,128)} %copy-done.14) | copy-start | bytes 49156
  434.4 23.6 %copy-start.24 = (f32[512,128]{1,0:T(8,128)S(1)}, f32[512,128]{1,0:T(8,128)}, u32[]{:S(2)}) copy-start(f32[512,128]{1,0:T(8,128)} %get-tuple-element.973.cosine_ref) | copy-start | bytes 786436
  434.4 23.6 %copy-start.53 = (f32[2,1,256]{2,1,0:T(1,128)S(1)}, f32[2,1,256]{2,1,0:T(1,128)}, u32[]{:S(2)}) copy-start(f32[2,1,256]{2,1,0:T(1,128)} %copy-done.52) | copy-start | bytes 6148
  434.4 23.6 %copy-start.59 = (f32[1536]{0:T(1024)S(1)}, f32[1536]{0:T(1024)}, u32[]{:S(2)}) copy-start(f32[1536]{0:T(1024)} %param.73) | copy-start | bytes 18436
  451.0 103.4 %collective-permute-start.9 = (bf16[512,2048]{1,0:T(8,128)(2,1)}, bf16[512,2048]{1,0:T(8,128)(2,1)}, u32[]{:S(2)}, u32[]{:S(2)}) collective-permute-start(bf16[512,2048]{1,0:T(8,128)(2,1)} %get-tuple-element.607), channel_id=1, source_target_pairs={{0,4},{2,6},{4,0},{6,2},{8,12},{10,14},{12,8},{14,10},{16,20},{18,... | collective-permute-start | bytes 6291464 | tf_op jit(solution)/shard_map/ppermute | solution.py:553
  452.2 102.1 %collective-permute-start.10 = (bf16[512,2048]{1,0:T(8,128)(2,1)}, bf16[512,2048]{1,0:T(8,128)(2,1)}, u32[]{:S(2)}, u32[]{:S(2)}) collective-permute-start(bf16[512,2048]{1,0:T(8,128)(2,1)} %get-tuple-element.609), channel_id=1, source_target_pairs={{0,8},{2,10},{4,12},{6,14},{8,0},{10,2},{12,4},{14,6},{16,24},{18,... | collective-permute-start | bytes 6291464 | tf_op jit(solution)/shard_map/ppermute | solution.py:553
  457.9 30.5 %copy-start.29 = (bf16[256,256]{1,0:T(8,128)(2,1)}, bf16[256,256]{1,0:T(8,128)(2,1)S(1)}, u32[]{:S(2)}) copy-start(bf16[256,256]{1,0:T(8,128)(2,1)S(1)} %fusion.66) | copy-start | bytes 393220
  458.0 30.4 %copy-start.8 = (bf16[512,2048]{1,0:T(8,128)(2,1)S(1)}, bf16[512,2048]{1,0:T(8,128)(2,1)}, u32[]{:S(2)}) copy-start(bf16[512,2048]{1,0:T(8,128)(2,1)} %copy-done.7) | copy-start | bytes 6291460
  502.8 51.5 %all-to-all-start.2 = ((bf16[16,16,2048]{2,1,0:T(8,128)(2,1)}), bf16[16,16,2048]{2,1,0:T(8,128)(2,1)S(1)}, u32[]{:S(2)}, u32[]{:S(2)}) async-start(bf16[16,16,2048]{2,1,0:T(8,128)(2,1)} %bitcast.97), calls=%async_computation.3 | async-start | bytes 2097152 | tf_op jit(solution)/shard_map/all_to_all | solution.py:598
  506.5 189.7 %reduce-scatter.5.cloned.1.call-start = ((), (), s32[]{:S(2)}) async-start(), calls=%async_computation.9 | async-start | bytes 8912896 | tf_op jit(solution)/shard_map/reduce_scatter | solution.py:827
  507.1 3.8 collective-permute-start.8
  554.4 23.0 %copy-start.65 = (f32[2048]{0:T(1024)S(1)}, f32[2048]{0:T(1024)}, u32[]{:S(2)}) copy-start(f32[2048]{0:T(1024)} %param.69) | copy-start | bytes 24580
  554.4 23.0 %copy-start.67 = (f32[2,2,128]{2,1,0:T(2,128)S(1)}, f32[2,2,128]{2,1,0:T(2,128)}, u32[]{:S(2)}) copy-start(f32[2,2,128]{2,1,0:T(2,128)} %copy-done.66) | copy-start | bytes 6148
  554.4 23.0 %copy-start.70 = (f32[512,1]{0,1:T(1,128)S(1)}, f32[512,1]{0,1:T(1,128)}, u32[]{:S(2)}) copy-start(f32[512,1]{0,1:T(1,128)} %copy-done.69) | copy-start | bytes 6148
  554.4 23.0 %copy-start.72 = (f32[512,1]{0,1:T(1,128)S(1)}, f32[512,1]{0,1:T(1,128)}, u32[]{:S(2)}) copy-start(f32[512,1]{0,1:T(1,128)} %copy-done.71) | copy-start | bytes 6148
  574.2 38.7 %collective-permute-start.11 = (bf16[1024,4480]{1,0:T(8,128)(2,1)}, bf16[1024,4480]{1,0:T(8,128)(2,1)}, u32[]{:S(2)}, u32[]{:S(2)}) collective-permute-start(bf16[1024,4480]{1,0:T(8,128)(2,1)} %get-tuple-element.616), channel_id=1, source_target_pairs={{0,2},{2,0},{4,6},{6,4},{8,10},{10,8},{12,14},{14,12},{16,18},{18,... | collective-permute-start | bytes 27525128 | tf_op jit(solution)/shard_map/ppermute | solution.py:553
  574.2 36.1 %collective-permute-start.12 = (bf16[256,2048]{1,0:T(8,128)(2,1)}, bf16[256,2048]{1,0:T(8,128)(2,1)}, u32[]{:S(2)}, u32[]{:S(2)}) collective-permute-start(bf16[256,2048]{1,0:T(8,128)(2,1)} %get-tuple-element.619), channel_id=1, source_target_pairs={{0,8},{2,10},{4,12},{6,14},{8,0},{10,2},{12,4},{14,6},{16,24},{18,... | collective-permute-start | bytes 3145736 | tf_op jit(solution)/shard_map/ppermute | solution.py:553
  576.0 36.8 %collective-permute-start.13 = (bf16[256,2048]{1,0:T(8,128)(2,1)}, bf16[256,2048]{1,0:T(8,128)(2,1)}, u32[]{:S(2)}, u32[]{:S(2)}) collective-permute-start(bf16[256,2048]{1,0:T(8,128)(2,1)} %get-tuple-element.621), channel_id=1, source_target_pairs={{0,4},{2,6},{4,0},{6,2},{8,12},{10,14},{12,8},{14,10},{16,20},{18,... | collective-permute-start | bytes 3145736 | tf_op jit(solution)/shard_map/ppermute | solution.py:553
  632.5 76.5 %collective-permute-start.17 = (bf16[512,2304]{1,0:T(8,128)(2,1)}, bf16[512,2304]{1,0:T(8,128)(2,1)}, u32[]{:S(2)}, u32[]{:S(2)}) collective-permute-start(bf16[512,2304]{1,0:T(8,128)(2,1)} %get-tuple-element.637), channel_id=1, source_target_pairs={{0,8},{2,10},{4,12},{6,14},{8,0},{10,2},{12,4},{14,6},{16,24},{18,... | collective-permute-start | bytes 7077896 | tf_op jit(solution)/shard_map/ppermute | solution.py:553
  632.7 74.1 %collective-permute-start.16 = (bf16[512,2176]{1,0:T(8,128)(2,1)}, bf16[512,2176]{1,0:T(8,128)(2,1)}, u32[]{:S(2)}, u32[]{:S(2)}) collective-permute-start(bf16[512,2176]{1,0:T(8,128)(2,1)} %get-tuple-element.635), channel_id=1, source_target_pairs={{0,4},{2,6},{4,0},{6,2},{8,12},{10,14},{12,8},{14,10},{16,20},{18,... | collective-permute-start | bytes 6684680 | tf_op jit(solution)/shard_map/ppermute | solution.py:553
  634.4 72.4 %collective-permute-start.19 = (bf16[256,2048]{1,0:T(8,128)(2,1)}, bf16[256,2048]{1,0:T(8,128)(2,1)S(1)}, u32[]{:S(2)}, u32[]{:S(2)}) collective-permute-start(bf16[256,2048]{1,0:T(8,128)(2,1)} %get-tuple-element.640), channel_id=1, source_target_pairs={{0,1},{1,0},{2,3},{3,2},{4,5},{5,4},{6,7},{7,6},{8,9},{9,8},{10,11... | collective-permute-start | bytes 3145736 | tf_op jit(solution)/shard_map/ppermute | solution.py:550
  635.0 61.2 %collective-permute-start.14 = (bf16[128,2048]{1,0:T(8,128)(2,1)}, bf16[128,2048]{1,0:T(8,128)(2,1)}, u32[]{:S(2)}, u32[]{:S(2)}) collective-permute-start(bf16[128,2048]{1,0:T(8,128)(2,1)} %get-tuple-element.630), channel_id=1, source_target_pairs={{0,16},{2,18},{4,20},{6,22},{8,24},{10,26},{12,28},{14,30},{16,0},... | collective-permute-start | bytes 1572872 | tf_op jit(solution)/shard_map/ppermute | solution.py:553
  637.5 69.4 %collective-permute-start.15 = (bf16[128,2048]{1,0:T(8,128)(2,1)}, bf16[128,2048]{1,0:T(8,128)(2,1)}, u32[]{:S(2)}, u32[]{:S(2)}) collective-permute-start(bf16[128,2048]{1,0:T(8,128)(2,1)} %get-tuple-element.631), channel_id=1, source_target_pairs={{0,16},{2,18},{4,20},{6,22},{8,24},{10,26},{12,28},{14,30},{16,0},... | collective-permute-start | bytes 1572872 | tf_op jit(solution)/shard_map/ppermute | solution.py:553
  696.2 10.7 %collective-permute-start.18 = (f32[16,2048]{1,0:T(8,128)}, f32[16,2048]{1,0:T(8,128)}, u32[]{:S(2)}, u32[]{:S(2)}) collective-permute-start(f32[16,2048]{1,0:T(8,128)} %get-tuple-element.1117), channel_id=1, source_target_pairs={{0,2},{2,0},{4,6},{6,4},{8,10},{10,8},{12,14},{14,12},{16,18},{18,... | collective-permute-start | bytes 393224 | tf_op jit(solution)/shard_map/ppermute | solution.py:553
  723.5 113.2 %all-to-all-start.3 = ((bf16[16,16,2048]{2,1,0:T(8,128)(2,1)}), bf16[16,16,2048]{2,1,0:T(8,128)(2,1)S(1)}, u32[]{:S(2)}, u32[]{:S(2)}) async-start(bf16[16,16,2048]{2,1,0:T(8,128)(2,1)} %bitcast.98), calls=%async_computation.5 | async-start | bytes 2097152 | tf_op jit(solution)/shard_map/all_to_all | solution.py:598
  728.2 44.0 %collective-permute-start.21 = (bf16[256,2304]{1,0:T(8,128)(2,1)}, bf16[256,2304]{1,0:T(8,128)(2,1)S(1)}, u32[]{:S(2)}, u32[]{:S(2)}) collective-permute-start(bf16[256,2304]{1,0:T(8,128)(2,1)} %get-tuple-element.647), channel_id=1, source_target_pairs={{0,4},{2,6},{4,0},{6,2},{8,12},{10,14},{12,8},{14,10},{16,20},{18,... | collective-permute-start | bytes 3538952 | tf_op jit(solution)/shard_map/ppermute | solution.py:553
  730.2 42.0 %collective-permute-start.20 = (bf16[256,2176]{1,0:T(8,128)(2,1)}, bf16[256,2176]{1,0:T(8,128)(2,1)}, u32[]{:S(2)}, u32[]{:S(2)}) collective-permute-start(bf16[256,2176]{1,0:T(8,128)(2,1)} %get-tuple-element.645), channel_id=1, source_target_pairs={{0,8},{2,10},{4,12},{6,14},{8,0},{10,2},{12,4},{14,6},{16,24},{18,... | collective-permute-start | bytes 3342344 | tf_op jit(solution)/shard_map/ppermute | solution.py:553
  731.6 39.1 %collective-permute-start.22 = (f32[16,2048]{1,0:T(8,128)}, f32[16,2048]{1,0:T(8,128)S(1)}, u32[]{:S(2)}, u32[]{:S(2)}) collective-permute-start(f32[16,2048]{1,0:T(8,128)} %get-tuple-element.648), channel_id=1, source_target_pairs={{0,4},{2,6},{4,0},{6,2},{8,12},{10,14},{12,8},{14,10},{16,20},{18,... | collective-permute-start | bytes 393224 | tf_op jit(solution)/shard_map/ppermute | solution.py:553
  772.2 36.2 %copy-start.26 = (bf16[128,2048]{1,0:T(8,128)(2,1)S(1)}, bf16[128,2048]{1,0:T(8,128)(2,1)}, u32[]{:S(2)}) copy-start(bf16[128,2048]{1,0:T(8,128)(2,1)} %reduce-scatter.5.cloned.1.call-done) | copy-start | bytes 1572868
  772.2 36.2 %copy-start.35 = (bf16[128,2048]{1,0:T(8,128)(2,1)S(1)}, bf16[128,2048]{1,0:T(8,128)(2,1)}, u32[]{:S(2)}) copy-start(bf16[128,2048]{1,0:T(8,128)(2,1)} %reduce-scatter.3.cloned.1.call-done) | copy-start | bytes 1572868
  778.4 58.2 %collective-permute-start.25 = (bf16[128,2304]{1,0:T(8,128)(2,1)}, bf16[128,2304]{1,0:T(8,128)(2,1)}, u32[]{:S(2)}, u32[]{:S(2)}) collective-permute-start(bf16[128,2304]{1,0:T(8,128)(2,1)} %get-tuple-element.663), channel_id=1, source_target_pairs={{0,16},{2,18},{4,20},{6,22},{8,24},{10,26},{12,28},{14,30},{16,0},... | collective-permute-start | bytes 1769480 | tf_op jit(solution)/shard_map/ppermute | solution.py:553
  781.0 55.6 %collective-permute-start.24 = (bf16[128,2176]{1,0:T(8,128)(2,1)}, bf16[128,2176]{1,0:T(8,128)(2,1)}, u32[]{:S(2)}, u32[]{:S(2)}) collective-permute-start(bf16[128,2176]{1,0:T(8,128)(2,1)} %get-tuple-element.661), channel_id=1, source_target_pairs={{0,16},{2,18},{4,20},{6,22},{8,24},{10,26},{12,28},{14,30},{16,0},... | collective-permute-start | bytes 1671176 | tf_op jit(solution)/shard_map/ppermute | solution.py:553
  781.4 27.0 %collective-permute-start.23 = (f32[16,2048]{1,0:T(8,128)S(1)}, f32[16,2048]{1,0:T(8,128)}, u32[]{:S(2)}, u32[]{:S(2)}) collective-permute-start(f32[16,2048]{1,0:T(8,128)S(1)} %get-tuple-element.656), channel_id=1, source_target_pairs={{0,8},{2,10},{4,12},{6,14},{8,0},{10,2},{12,4},{14,6},{16,24},{18,... | collective-permute-start | bytes 393224 | tf_op jit(solution)/shard_map/ppermute | solution.py:553
  815.4 21.2 %collective-permute-start.26 = (f32[16,2048]{1,0:T(8,128)S(1)}, f32[16,2048]{1,0:T(8,128)S(1)}, u32[]{:S(2)}, u32[]{:S(2)}) collective-permute-start(f32[16,2048]{1,0:T(8,128)S(1)} %get-tuple-element.665), channel_id=1, source_target_pairs={{0,16},{2,18},{4,20},{6,22},{8,24},{10,26},{12,28},{14,30},{16,0},... | collective-permute-start | bytes 393224 | tf_op jit(solution)/shard_map/ppermute | solution.py:553
  845.8 6.5 collective-permute-start.28
  847.3 10.7 %collective-permute-start.27 = (f32[64,512]{1,0:T(8,128)}, f32[64,512]{1,0:T(8,128)S(1)}, u32[]{:S(2)}, u32[]{:S(2)}) collective-permute-start(f32[64,512]{1,0:T(8,128)} %get-tuple-element.676), channel_id=1, source_target_pairs={{0,1},{1,0},{2,3},{3,2},{4,5},{5,4},{6,7},{7,6},{8,9},{9,8},{10,11... | collective-permute-start | bytes 393224 | tf_op jit(solution)/shard_map/ppermute | solution.py:550
  (57 other events, 251.8 us)
Sparse Core Ops, SparseCore 0:
  16.1 172.8 all-gather.4
  190.5 138.4 all-gather.2
  385.1 129.1 reduce-scatter.2
  518.3 118.8 reduce-scatter.4

commit v10 on v9

--- a/solution.py
+++ b/solution.py
@@ -117,6 +117,24 @@
         cost_estimate=pl.CostEstimate(flops=0, transcendentals=0, bytes_accessed=4 * height * width),
         name="pick_halves",
     )(order, values, values)
+
+
+def join_columns(pieces):
+    height = pieces[0].shape[0]
+    width = sum(piece.shape[1] for piece in pieces)
+
+    def put_all(*refs):
+        start = 0
+        for source in refs[:-1]:
+            refs[-1][:, start : start + source.shape[1]] = source[...]
+            start += source.shape[1]
+
+    return pl.pallas_call(
+        put_all,
+        out_shape=jax.ShapeDtypeStruct((height, width), pieces[0].dtype),
+        cost_estimate=pl.CostEstimate(flops=0, transcendentals=0, bytes_accessed=4 * height * width),
+        name="join_columns",
+    )(*pieces)
 
 
 def hand_over(values, microseconds):
@@ -552,6 +570,9 @@
     def other_group(values, bits):
         return lax.ppermute(values, "dp", [(i, i ^ bits) for i in range(groups)])
 
+    def after(value, *others):
+        return lax.optimization_barrier((value, others))[0]
+
     step_padded = jnp.pad(step_weight, ((0, 0), (0, STEP_PAD - step_weight.shape[1])))
     early = dict(
         gate=mamba_gate, state=state_weight, step=step_padded, input=mamba_input, query=query_weight, key=key_weight,
@@ -564,7 +585,7 @@
         for name, weight in group_weights.items():
             places_of[name] = (label, start, weight.shape[1])
             start += weight.shape[1]
-        whole[label] = lax.all_gather(jnp.concatenate(list(group_weights.values()), axis=1), "dp", axis=0, tiled=True)
+        whole[label] = lax.all_gather(join_columns(list(group_weights.values())), "dp", axis=0, tiled=True)
 
     def full(name):
         label, start, size = places_of[name]
@@ -693,9 +714,6 @@
         least = min(range(len(leaves)), key=lambda place: leaves[place].size)
         leaves[least], order[0] = lax.optimization_barrier((leaves[least], order[0]))
         return jax.tree.unflatten(form, leaves)
-
-    def after(value, *others):
-        return lax.optimization_barrier((value, others))[0]
 
     in32 = whole_in.astype(f32)
     in_scale = rms_scale(in32)
@@ -755,24 +773,37 @@
         grad_hidden = project(whole_grad, full("fdown"))
         gate_ff_low = (grad_hidden * up_ff * (sig_ff * (1.0 + gate_ff * (1.0 - sig_ff)))).astype(bf16)
         up_ff_low = (grad_hidden * (gate_ff * sig_ff)).astype(bf16)
-        grad_mid_norm = project_back(gate_ff_low, full("fgate")) + project_back(up_ff_low, full("fup"))
-        grad_gain_mid = jnp.sum(grad_mid_norm * mid32 * mid_scale, axis=0)
-        mid_part = rms_back(grad_mid_norm, mid32, mid_scale, gain_middle).astype(bf16)
-        return grad_gain_mid, mid_part, hidden_low, (gate_ff_low, up_ff_low), outer_low(whole_grad, hidden_low)
-
-    grad_gain_mid, mid_part, hidden_low, feed_low, part_fdown = unit(feed_forward)
+        feed_low = (gate_ff_low, up_ff_low)
+        return hidden_low, feed_low, feed_back(feed_low, 0), outer_low(whole_grad, hidden_low)
+
+    half = total // 2
+
+    def feed_back(feed_low, start):
+        gate_part, up_part, values, scale = [
+            lax.slice_in_dim(array, start, start + half) for array in (*feed_low, mid32, mid_scale)
+        ]
+        grad_mid_norm = project_back(gate_part, full("fgate")) + project_back(up_part, full("fup"))
+        grad_gain = jnp.sum(grad_mid_norm * values * scale, axis=0)
+        return rms_back(grad_mid_norm, values, scale, gain_middle).astype(bf16), grad_gain
+
+    hidden_low, feed_low, (mid_part_low, gain_mid_low), part_fdown = unit(feed_forward)
+    mid_other_low = hand_over(other_lane(mid_part_low), 2)
+    mid_part_high, gain_mid_high = unit(lambda: feed_back(feed_low, half))
+    mid_other_high = hand_over(other_lane(mid_part_high), 45)
     sum_fdown = lax.psum_scatter(part_fdown, "dp", scatter_dimension=0, tiled=True)
-    mid_other = hand_over(other_lane(mid_part), 45)
+    grad_gain_mid = gain_mid_low + gain_mid_high
 
     def feed_output():
         ffn_part = project_back(hidden_low, full("fdown")).astype(bf16)
+        return lane_rows(ffn_part, lane), lane_rows(ffn_part, 1 - lane)
+
+    def feed_sends():
         mid_left = split_left(mid_low)
-        return (
-            lane_rows(ffn_part, lane), lane_rows(ffn_part, 1 - lane), mid_left[0],
-            [core_send(mid_left, right) for right in feed_low],
-        )
-
-    ffn_own, ffn_send, mid_keep, send_feed = unit(feed_output)
+        return mid_left[0], [core_send(mid_left, right) for right in feed_low]
+
+    mid_keep, send_feed = unit(feed_sends)
+    order[0], mid_other_low = lax.optimization_barrier((order[0], mid_other_low))
+    ffn_own, ffn_send = unit(feed_output)
     feed_came = [other_group(send, 1) for send in send_feed]
 
     def keep_first(keep, right, came, reductions, sizes):
@@ -791,7 +822,7 @@
             else:
                 red.result = step
 
-    mid_other, feed_came = lax.optimization_barrier((mid_other, feed_came))
+    mid_other_high, feed_came = lax.optimization_barrier((mid_other_high, feed_came))
     moves = unit(
         lambda: [
             keep_first(mid_keep, right, came, (red,), (ff_cols,))[0] for red, right, came in zip(feeds, feed_low, feed_came)
@@ -801,7 +832,11 @@
         red.move(*move)
 
     def branch_backward():
-        grad_middle = whole_grad.astype(f32) + (mid_part.astype(f32) + mid_other.astype(f32))
+        mid_sums = [
+            mine.astype(f32) + other.astype(f32)
+            for mine, other in ((mid_part_low, mid_other_low), (mid_part_high, mid_other_high))
+        ]
+        grad_middle = whole_grad.astype(f32) + jnp.concatenate(mid_sums)
         whole_branch = grad_middle.astype(bf16)
         grad_gated_norm = project(whole_branch, full("mix"))
         cross_own = jnp.sum(grad_gated_norm * mixer_gain * (ssm_out * jax.nn.silu(gate_z)), axis=1)

time: 876 us -> 872 us (level)
  matrix products: 188 us -> 207 us
  waiting for transfers between devices: 367 us -> 349 us
  local copies, waits for them, and re-layouts: 72.9 us -> 62.1 us
    dot_general x6 -> x8, matrix products: 51.5 us -> 71.4 us  [project_back(): lax.dot_general(left, right, (((1,), (1,)), ((), ())), preferred_element_...]
    ppermute x10 -> x11, waiting for transfers between devices: 91 us -> 74.7 us  [other_lane(): return lax.ppermute(values, 'tensor', swap_lane)]
  transfers between devices with their start and end apart: 37 -> 38, of which waited for: 18 -> 16; matrix products, arithmetic and copies ran while one was open for 28% -> 31% of each run, Pallas kernels for 10% -> 10%
where the time goes in v10:
time: 872 us; the launch traced here: 867 us
  waiting for transfers between devices  349 us (40%)
  matrix products  207 us (24%)
  Pallas kernels  87.7 us (10%)
  other arithmetic  79.9 us (9%)
  starting transfers between devices  64 us (7%)
  local copies, waits for them, and re-layouts  62.1 us (7%)
  between operations  15.6 us (2%)
    ppermute x19, waiting for transfers between devices, other_group(): return lax.ppermute(values, 'dp', [(i, i ^ bits) for i in range(groups)])  165 us
    ppermute x11, waiting for transfers between devices, other_lane(): return lax.ppermute(values, 'tensor', swap_lane)  74.7 us
    all_to_all x4, waiting for transfers between devices, exchange(): lax.all_to_all(buffer.reshape(groups, micro * per, width), 'dp', split_ax...  73.3 us
    dot_general x8, matrix products, project_back(): lax.dot_general(left, right, (((1,), (1,)), ((), ())), preferred_element_...  71.4 us
    dot_general x14, matrix products, project(): return jnp.dot(left, right, preferred_element_type=f32)  68 us
    dot_general x12, matrix products, outer_sum(): lax.dot_general(left, right, (((0,), (0,)), ((), ())), preferred_element_...  67.7 us
    all_gather x2, waiting for transfers between devices, local(): lax.all_gather(join_columns(list(group_weights.values())), 'dp', axis=0,...  35.6 us
    pallas_call x1, Pallas kernels, state_backward(): pl.pallas_call(state_backward_kernel, out_shape=(jax.ShapeDtypeStruct((to...  34 us
  transfers between devices with their start and end apart: 38, of which 16 were waited for; matrix products, arithmetic and copies ran while one was open for 31% of the time, Pallas kernels for 10%

profile of v10, /device:TPU:0, one launch (start us, length us, event | category | flops | bytes accessed | tf_op | source)
XLA Modules:
  0.0 867.3 jit_solution(12236067977396840882)
XLA Ops:
  14.4 4.9 select_reduce_fusion
  21.1 7.4 all-to-all-start.1
  30.1 38.2 %all-to-all-done.1 = bf16[16,16,2048]{2,1,0:T(8,128)(2,1)S(1)} async-done(((bf16[16,16,2048]{2,1,0:T(8,128)(2,1)}), bf16[16,16,2048]{2,1,0:T(8,128)(2,1)S(1)}, u32[]{:S(2)}, u32[]{:S(2)}) %all-to-all-start.1) | async-done | bytes 1048608 | tf_op jit(solution)/shard_map/all_to_all | solution.py:619
  76.7 35.1 %all-to-all-done = bf16[16,16,2048]{2,1,0:T(8,128)(2,1)S(1)} async-done(((bf16[16,16,2048]{2,1,0:T(8,128)(2,1)}), bf16[16,16,2048]{2,1,0:T(8,128)(2,1)S(1)}, u32[]{:S(2)}, u32[]{:S(2)}) %all-to-all-start) | async-done | bytes 1048608 | tf_op jit(solution)/shard_map/all_to_all | solution.py:619
  115.8 21.2 %collective-permute-done = bf16[256,2048]{1,0:T(8,128)(2,1)S(1)} collective-permute-done((bf16[256,2048]{1,0:T(8,128)(2,1)S(1)}, bf16[256,2048]{1,0:T(8,128)(2,1)S(1)}, u32[]{:S(2)}, u32[]{:S(2)}) %collective-permute-start) | collective-permute-done | bytes 1048608 | tf_op jit(solution)/shard_map/ppermute | solution.py:568
  142.2 6.7 pick_halves.3
  148.9 35.6 %all-gather.5.cloned.1.call-done = bf16[2048,6528]{1,0:T(8,128)(2,1)} async-done(((bf16[128,6528]{1,0:T(8,128)(2,1)}), bf16[2048,6528]{1,0:T(8,128)(2,1)}) %all-gather.5.cloned.1.call-update) | async-done | bytes 26738704 | tf_op jit(solution)/shard_map/all_gather | solution.py:588
  195.7 8.0 fusion.68.gate_ref
  203.7 8.1 fusion.70.signal_ref
  211.8 21.1 %state_forward.1 = (f32[512,1536]{1,0:T(8,128)}, f32[512,128]{1,0:T(8,128)}) custom-call(f32[512,1536]{1,0:T(8,128)} %fusion.70.signal_ref, f32[512,1536]{1,0:T(8,128)} %fusion.68.gate_ref, f32[5,1536]{1,0:T(8,128)S(1)} %copy-done.47, f32[1,1536]{1,0:T(1,128)S(1)} %broadcast_in_dim_reshape.2.skip_ref, bf16[512,512]{1,0:T(8,128)(2,1)S(1)} %copy-done.14, ...), custom_call_target="tpu_custom_call" | custom-call | flops 1610612736 | bytes 9437184 | tf_op jit(solution)/shard_map/state_forward/pallas_call | solution.py:469
  235.7 5.0 fusion.72.query_ref.key_ref.value_ref
  240.7 8.2 attention_forward.1
  249.0 4.2 multiply_convert_fusion.5
  253.2 17.6 %fusion.66 = f32[512,2048]{1,0:T(8,128)S(1)} fusion(bf16[512,1536]{1,0:T(8,128)(2,1)S(1)} %multiply_convert_fusion.5, bf16[2048,6528]{1,0:T(8,128)(2,1)} %all-gather.5.cloned.1.call-done), kind=kOutput, calls=%fused_computation.121 | convolution fusion | flops 3221225472 | bytes 12058624 | tf_op jit(solution)/shard_map/dot_general | solution.py:30
  275.7 45.7 %collective-permute-done.3 = bf16[512,2048]{1,0:T(8,128)(2,1)} collective-permute-done((bf16[512,2048]{1,0:T(8,128)(2,1)S(1)}, bf16[512,2048]{1,0:T(8,128)(2,1)}, u32[]{:S(2)}, u32[]{:S(2)}) %collective-permute-start.3) | collective-permute-done | bytes 2097184 | tf_op jit(solution)/shard_map/ppermute | solution.py:568
  321.4 6.1 fusion.93
  329.4 45.8 %conditional.16 = (bf16[512,2048]{1,0:T(8,128)(2,1)}, bf16[512,2048]{1,0:T(8,128)(2,1)}, bf16[512,2048]{1,0:T(8,128)(2,1)}, bf16[256,2048]{1,0:T(8,128)(2,1)S(1)...) conditional(s32[]{:T(128)} %convert_element_type.487, () %tuple.161, (bf16[2048,6144]{1,0:T(8,128)(2,1)}, ...), branch_computations={%region_7.8_spmd, %region_8.11_spmd} | conditional | flops 21501050880 | bytes 124814440 | solution.py:710
  329.4 6.9 fusion.4
  336.3 7.0 fusion.8
  343.3 10.2 %multiply_convert_fusion = (bf16[512,2048]{1,0:T(8,128)(2,1)}, bf16[512,2048]{1,0:T(8,128)(2,1)}, bf16[512,2048]{1,0:T(8,128)(2,1)}) fusion(f32[512,2048]{1,0:T(8,128)S(1)} %fusion.8, f32[512,2048]{1,0:T(8,128)S(1)} %fusion.4, bf16[512,2048]{1,0:T(8,128)(2,1)S(1)} %copy-done.12, bf16[2048,6144]{1,0:T(8,128)(2,1)} %get-tuple-element.306), kind=kOutput, calls=%fused_computation.11 | convolution fusion | flops 4310695936 | bytes 25165824 | tf_op jit(solution)/shard_map/cond/branch_1_fun/dot_general | solution.py:26
  353.5 6.2 fusion.2
  359.8 6.3 multiply_reduce_fusion
  366.5 8.3 convert_bitcast_fusion
  376.6 13.9 %conditional.17 = (bf16[256,2048]{1,0:T(8,128)(2,1)}, f32[2048]{0:T(1024)}) conditional(s32[]{:T(128)} %convert_element_type.513, () %tuple.165, (f32[512,1]{0,1:T(1,128)S(1)}, bf16[512,2048]{1,0:T(8,128)(2,1)}, bf16[2048,6144]{1,0:T(8,128)(2,1)}, bf16[512,2048]{1,0:T(8,128)(2,1)}, f32[2048]{0:T(1024)S(1)}, ...), branch_computations={%region_11.12_spmd, %region_12.15_spmd} | conditional | flops 4301257728 | bytes 49316908 | solution.py:710
  376.6 6.2 fusion.18
  382.8 6.3 multiply_reduce_fusion.2
  392.0 16.9 %conditional.18 = (bf16[512,1024]{1,0:T(8,128)(2,1)}, bf16[1024,2048]{1,0:T(8,128)(2,1)}, bf16[1024,2048]{1,0:T(8,128)(2,1)}) conditional(s32[]{:T(128)} %convert_element_type.514, () %tuple.168, (s32[16]{0:T(128)S(1)}, bf16[512,2048]{1,0:T(8,128)(2,1)S(1)}, bf16[512,2048]{1,0:T(8,128)(2,1)}, bf16[512,2048]{1,0:T(8,128)(2,1)}) %tuple.169), branch_computations={%region_15.16_spmd, %region_16.17_spmd} | conditional | flops 4299161600 | bytes 23068724 | solution.py:710
  392.0 4.1 pick_halves.2
  396.1 6.7 convolution_convert_fusion
  402.8 6.1 convolution_convert_fusion.1
  409.4 9.9 %conditional.19 = (bf16[256,2048]{1,0:T(8,128)(2,1)S(1)}, bf16[256,2048]{1,0:T(8,128)(2,1)}) conditional(s32[]{:T(128)} %convert_element_type.515, () %tuple.172, (bf16[2048,6144]{1,0:T(8,128)(2,1)}, bf16[512,2048]{1,0:T(8,128)(2,1)}, s32[]{:T(128)}) %tuple.173), branch_computations={%region_17.18_spmd, %region_18.19_spmd} | conditional | flops 4296015872 | bytes 16777320 | solution.py:710
  409.6 8.5 fusion.31
  423.1 16.3 %conditional.20 = (bf16[512,2048]{1,0:T(8,128)(2,1)}, bf16[1,2,2,128,2048]{4,3,2,1,0:T(8,128)(2,1)}, bf16[512,2048]{1,0:T(8,128)(2,1)}, bf16[2,1,2,128,2048]{4,3,2,1,0:T(8,128)(2,1)}) conditional(s32[]{:T(128)} %convert_element_type.516, () %tuple.175, (bf16[512,1024]{1,0:T(8,128)(2,1)}, bf16[512,2048]{1,0:T(8,128)(2,1)}, ...), branch_computations={%region_19.20_spmd, %region_20.21_spmd} | conditional | flops 4307550208 | bytes 39845920 | solution.py:710
  423.1 5.6 add_convert_fusion.1
  431.3 5.6 add_convert_fusion
  441.0 12.0 %collective-permute-start.11 = (bf16[512,2048]{1,0:T(8,128)(2,1)}, bf16[512,2048]{1,0:T(8,128)(2,1)}, u32[]{:S(2)}, u32[]{:S(2)}) collective-permute-start(bf16[512,2048]{1,0:T(8,128)(2,1)} %get-tuple-element.642), channel_id=1, source_target_pairs={{0,8},{2,10},{4,12},{6,14},{8,0},{10,2},{12,4},{14,6},{16,24},{18,... | collective-permute-start | bytes 6291464 | tf_op jit(solution)/shard_map/ppermute | solution.py:571
  453.2 30.5 %conditional.21 = (f32[512]{0:T(512)}, f32[256,2048]{1,0:T(8,128)}, f32[512,1536]{1,0:T(8,128)}, bf16[512,2048]{1,0:T(8,128)(2,1)}, bf16[512,768]{1,0:T(8,128)(2,1)S(1)}) conditional(s32[]{:T(128)} %convert_element_type.517, () %tuple.179, (bf16[512,2048]{1,0:T(8,128)(2,1)}, bf16[256,2048]{1,0:T(8,128)(2,1)}, bf16[256,2048]{1,0:T(8,128)(2,1)}, ...), branch_computations={%region_21.22_spmd, %region_22.24_spmd} | conditional | flops 4979949056 | bytes 83370136 | solution.py:710
  461.8 9.4 %multiply_reduce_fusion.4 = (f32[512]{0:T(512)}, f32[512,1536]{1,0:T(8,128)}) fusion(f32[512,1536]{1,0:T(8,128)S(1)} %copy-done.11, f32[512,1536]{1,0:T(8,128)S(1)} %copy-done.4, f32[1536]{0:T(1024)S(1)} %get-tuple-element.337, bf16[512,2048]{1,0:T(8,128)(2,1)} %get-tuple-element.1062, bf16[2048,6528]{1,0:T(8,128)(2,1)} %get-tuple-element.336), kind=kOutput, calls=%fused_computation.50 | convolution fusion | flops 3227516416 | bytes 17833984 | tf_op jit(solution)/shard_map/cond/branch_1_fun/dot_general | solution.py:26
  471.2 4.4 fusion.38.grad_ref
  475.6 8.2 attention_backward.1
  484.6 12.0 %conditional.22 = (bf16[2048,2048]{1,0:T(8,128)(2,1)}, bf16[256,2048]{0,1:T(8,128)(2,1)S(1)}) conditional(s32[]{:T(128)} %convert_element_type.518, () %tuple.182, (bf16[512,1536]{1,0:T(8,128)(2,1)}, bf16[512,512]{1,0:T(8,128)(2,1)}, bf16[512,2048]{1,0:T(8,128)(2,1)}, bf16[512,2048]{1,0:T(8,128)(2,1)S(1)}, s32[]{:T(128)}, ...), branch_computations={%region_24.25_spmd, %region_25.26_spmd} | conditional | flops 4575461376 | bytes 31588488 | solution.py:710
  488.1 8.5 convert_bitcast_fusion.1
  498.0 4.1 all-to-all-start.2
  506.7 43.7 %conditional.23 = (f32[2,8,1536]{2,1,0:T(8,128)}, f32[2,8,512]{2,1,0:T(8,128)}, f32[2,24,2]{2,1,0:T(8,128)}, bf16[512,4480]{1,0:T(8,128)(2,1)}) conditional(s32[]{:T(128)} %convert_element_type.520, () %tuple.185, (f32[1536]{0:T(1024)}, f32[512]{0:T(512)}, f32[512]{0:T(512)}, f32[512]{0:T(512)}, f32[512,2]{0,1:T(2,128)S(1)}, ...), branch_computations={%region_26.27_spmd, %region_27.28_spmd} | conditional | flops 4026538496 | bytes 15904996 | solution.py:710
  516.3 34.0 %state_backward.1 = (bf16[512,4480]{1,0:T(8,128)(2,1)}, f32[2,8,1536]{2,1,0:T(8,128)}, f32[2,8,512]{2,1,0:T(8,128)}, f32[2,24,2]{2,1,0:T(8,128)}) custom-call(f32[512,1536]{1,0:T(8,128)} %get-tuple-element.356.grad_ref, f32[512,1536]{1,0:T(8,128)} %get-tuple-element.357.out_ref, f32[512,1536]{1,0:T(8,128)} %get-tuple-element.358.gate_ref, ...), custom_call_target="tpu_custom_call" | custom-call | flops 4026531840 | bytes 15728640 | tf_op jit(solution)/shard_map/cond/branch_1_fun/state_backward/pallas_call | solution.py:494
  550.4 19.6 %conditional.24 = (bf16[1024,4480]{1,0:T(8,128)(2,1)}, bf16[256,2048]{1,0:T(8,128)(2,1)}, bf16[1,1,2,128,2048]{4,3,2,1,0:T(8,128)(2,1)S(1)}, bf16[256,2048]{1,0:...) conditional(s32[]{:T(128)} %convert_element_type.521, () %tuple.189, ...), branch_computations={%region_29.30_spmd, %region_30.31_spmd} | conditional | flops 4979556352 | bytes 42205260 | solution.py:710
  558.8 9.8 %convolution_convert_fusion.3 = bf16[1024,4480]{1,0:T(8,128)(2,1)} fusion(bf16[512,1024]{1,0:T(8,128)(2,1)S(1)} %copy-done.74, bf16[512,4480]{1,0:T(8,128)(2,1)} %get-tuple-element.383), kind=kOutput, calls=%fused_computation.70 | convolution fusion | flops 4702208000 | bytes 14811136 | tf_op jit(solution)/shard_map/cond/branch_1_fun/dot_general | solution.py:34
  573.5 22.9 %conditional.25 = (f32[2048]{0:T(1024)S(1)}, bf16[256,2048]{1,0:T(8,128)(2,1)}, bf16[256,2048]{1,0:T(8,128)(2,1)S(1)}) conditional(s32[]{:T(128)} %convert_element_type.523, () %tuple.192, (bf16[2048,6528]{1,0:T(8,128)(2,1)}, bf16[512,4480]{1,0:T(8,128)(2,1)}, f32[512,2048]{1,0:T(8,128)}, f32[2,2,128]{2,1,0:T(2,128)S(1)}, f32[]{:T(128)}, ...), branch_computations={%region_31.32_spmd, %region_32.35_spmd} | conditional | flops 9406776320 | bytes 46049396 | solution.py:710
  573.7 17.4 %multiply_reduce_fusion.5 = (f32[512]{0:T(512)S(1)}, f32[2048]{0:T(1024)S(1)}, f32[512,2048]{1,0:T(8,128)}) fusion(f32[512,2048]{1,0:T(8,128)} %get-tuple-element.392, f32[2048]{0:T(1024)S(1)} %get-tuple-element.396, f32[512]{0:T(512)S(1)} %bitcast.294, bf16[512,4480]{1,0:T(8,128)(2,1)} %get-tuple-element.390, bf16[2048,6528]{1,0:T(8,128)(2,1)} %get-tuple-element.391), kind=kOutput, calls=%fused_computation.79 | convolution fusion | flops 9401530368 | bytes 31346688 | tf_op jit(solution)/shard_map/cond/branch_1_fun/dot_general | solution.py:30
  591.1 4.2 subtract_convert_fusion.2
  596.4 14.4 %collective-permute-done.13 = bf16[256,2048]{1,0:T(8,128)(2,1)} collective-permute-done((bf16[256,2048]{1,0:T(8,128)(2,1)}, bf16[256,2048]{1,0:T(8,128)(2,1)}, u32[]{:S(2)}, u32[]{:S(2)}) %collective-permute-start.13) | collective-permute-done | bytes 1048608 | tf_op jit(solution)/shard_map/ppermute | solution.py:571
  610.8 19.3 %conditional.26 = (bf16[512,2176]{1,0:T(8,128)(2,1)}, bf16[1,2,2,128,2176]{4,3,2,1,0:T(8,128)(2,1)}, bf16[512,2304]{1,0:T(8,128)(2,1)}, bf16[2,1,2,128,2304]{4,3...) conditional(s32[]{:T(128)} %convert_element_type.524, ...), branch_computations={%region_35.36_spmd, %region_36.37_spmd} | conditional | flops 4715577344 | bytes 59113572 | solution.py:710
  610.8 9.3 %add_convert_fusion.2 = bf16[1024,4480]{1,0:T(8,128)(2,1)S(1)} fusion(bf16[1024,4480]{1,0:T(8,128)(2,1)} %get-tuple-element.400, bf16[512,1024]{1,0:T(8,128)(2,1)} %get-tuple-element.398, bf16[512,4480]{1,0:T(8,128)(2,1)} %get-tuple-element.399), kind=kOutput, calls=%fused_computation.87 | convolution fusion | flops 4711383040 | bytes 23986176 | tf_op jit(solution)/shard_map/cond/branch_1_fun/dot_general | solution.py:34
  636.4 9.7 %conditional.27 = (f32[16,2048]{1,0:T(8,128)}) conditional(s32[]{:T(128)} %convert_element_type.525, () %tuple.198, (f32[2,8,1536]{2,1,0:T(8,128)}, f32[2,8,512]{2,1,0:T(8,128)}, f32[2048]{0:T(1024)}, f32[2048]{0:T(1024)}, f32[2048]{0:T(1024)}, /*index=5*/f32[2,24,2]{2,1,0:T(8,128)}, f32[24]{0:T(128)}) %tuple.358), branch_computations={%region_37.38_spmd, %region_38.42_spmd} | conditional | flops 215136 | bytes 436212 | solution.py:710
  646.1 51.5 %collective-permute-done.15 = bf16[128,2048]{1,0:T(8,128)(2,1)} collective-permute-done((bf16[128,2048]{1,0:T(8,128)(2,1)}, bf16[128,2048]{1,0:T(8,128)(2,1)}, u32[]{:S(2)}, u32[]{:S(2)}) %collective-permute-start.15) | collective-permute-done | bytes 524320 | tf_op jit(solution)/shard_map/ppermute | solution.py:571
  697.6 11.0 %collective-permute-done.16 = bf16[128,2048]{1,0:T(8,128)(2,1)} collective-permute-done((bf16[128,2048]{1,0:T(8,128)(2,1)}, bf16[128,2048]{1,0:T(8,128)(2,1)}, u32[]{:S(2)}, u32[]{:S(2)}) %collective-permute-start.16) | collective-permute-done | bytes 524320 | tf_op jit(solution)/shard_map/ppermute | solution.py:571
  710.8 13.2 %conditional.28 = (bf16[256,2176]{1,0:T(8,128)(2,1)}, bf16[1,1,2,128,2176]{4,3,2,1,0:T(8,128)(2,1)}, bf16[256,2304]{1,0:T(8,128)(2,1)}, bf16[1,1,2,128,2304]{4,3...) conditional(s32[]{:T(128)} %convert_element_type.526, () %tuple.202, ...), branch_computations={%region_43.44_spmd, %region_44.45_spmd} | conditional | flops 280788992 | bytes 38142112 | solution.py:710
  725.4 4.8 all-to-all-start.3
  734.1 38.5 %collective-permute-done.23 = f32[16,2048]{1,0:T(8,128)S(1)} collective-permute-done((f32[16,2048]{1,0:T(8,128)}, f32[16,2048]{1,0:T(8,128)S(1)}, u32[]{:S(2)}, u32[]{:S(2)}) %collective-permute-start.23) | collective-permute-done | bytes 131104 | tf_op jit(solution)/shard_map/ppermute | solution.py:571
  774.1 6.2 conditional.29
  784.1 26.2 %collective-permute-done.24 = f32[16,2048]{1,0:T(8,128)} collective-permute-done((f32[16,2048]{1,0:T(8,128)S(1)}, f32[16,2048]{1,0:T(8,128)}, u32[]{:S(2)}, u32[]{:S(2)}) %collective-permute-start.24) | collective-permute-done | bytes 131104 | tf_op jit(solution)/shard_map/ppermute | solution.py:571
  810.4 6.3 conditional.30
  819.4 19.2 %collective-permute-done.27 = f32[16,2048]{1,0:T(8,128)S(1)} collective-permute-done((f32[16,2048]{1,0:T(8,128)S(1)}, f32[16,2048]{1,0:T(8,128)S(1)}, u32[]{:S(2)}, u32[]{:S(2)}) %collective-permute-start.27) | collective-permute-done | bytes 131104 | tf_op jit(solution)/shard_map/ppermute | solution.py:571
  838.6 9.2 %conditional.31 = (f32[128,1536]{1,0:T(8,128)}, f32[128,24]{1,0:T(8,128)}, f32[128,1536]{1,0:T(8,128)}, f32[128,512]{1,0:T(8,128)}, f32[128,128]{1,0:T(8,128)}, ...) conditional(s32[]{:T(128)} %convert_element_type.529, ...), branch_computations={%region_49.50_spmd, %region_50.51_spmd} | conditional | flops 270712832 | bytes 13263072 | solution.py:710
  (378 shorter events, 195.7 us)
Async XLA Ops:
  7.2 177.3 %all-gather.5.cloned.1.call-start = ((), (), s32[]{:S(2)}) async-start(), calls=%async_computation.7 | async-start | bytes 28409856 | tf_op jit(solution)/shard_map/all_gather | solution.py:588
  11.5 317.8 %all-gather.3.cloned.1.call-start = ((), (), s32[]{:S(2)}) async-start(), calls=%async_computation.6 | async-start | bytes 26738688 | tf_op jit(solution)/shard_map/all_gather | solution.py:588
  14.3 14.5 %copy-start.33 = (bf16[2,128,2048]{2,1,0:T(8,128)(2,1)S(1)}, bf16[2,128,2048]{2,1,0:T(8,128)(2,1)}, u32[]{:S(2)}) copy-start(bf16[2,128,2048]{2,1,0:T(8,128)(2,1)} %param.57) | copy-start | bytes 3145732
  19.6 92.2 %copy-start.69 = (s32[256]{0:T(256)}, s32[256]{0:T(256)S(1)}, u32[]{:S(2)}) copy-start(s32[256]{0:T(256)S(1)} %get-tuple-element.1014) | copy-start | bytes 3076
  21.1 47.3 %all-to-all-start.1 = ((bf16[16,16,2048]{2,1,0:T(8,128)(2,1)}), bf16[16,16,2048]{2,1,0:T(8,128)(2,1)S(1)}, u32[]{:S(2)}, u32[]{:S(2)}) async-start(bf16[16,16,2048]{2,1,0:T(8,128)(2,1)} %bitcast.84), calls=%async_computation.1 | async-start | bytes 2097152 | tf_op jit(solution)/shard_map/all_to_all | solution.py:619
  28.7 43.6 %copy-start.73 = (f32[24]{0:T(128)S(1)}, f32[24]{0:T(128)}, u32[]{:S(2)}) copy-start(f32[24]{0:T(128)} %param.80) | copy-start | bytes 292
  68.3 43.5 %all-to-all-start = ((bf16[16,16,2048]{2,1,0:T(8,128)(2,1)}), bf16[16,16,2048]{2,1,0:T(8,128)(2,1)S(1)}, u32[]{:S(2)}, u32[]{:S(2)}) async-start(bf16[16,16,2048]{2,1,0:T(8,128)(2,1)} %bitcast.75), calls=%async_computation | async-start | bytes 2097152 | tf_op jit(solution)/shard_map/all_to_all | solution.py:619
  72.0 478.4 %reduce-scatter.3.cloned.1.call-start = ((), (), s32[]{:S(2)}) async-start(), calls=%async_computation.8 | async-start | bytes 8912896 | tf_op jit(solution)/shard_map/reduce_scatter | solution.py:793
  72.3 168.4 %copy-start.53 = (f32[2,1,256]{2,1,0:T(1,128)}, f32[2,1,256]{2,1,0:T(1,128)S(1)}, u32[]{:S(2)}) copy-start(f32[2,1,256]{2,1,0:T(1,128)S(1)} %convert_element_type.501.seg_row_ref) | copy-start | bytes 6148
  72.5 139.3 %copy-start.51 = (f32[1,1536]{1,0:T(1,128)}, f32[1,1536]{1,0:T(1,128)S(1)}, u32[]{:S(2)}) copy-start(f32[1,1536]{1,0:T(1,128)S(1)} %broadcast_in_dim_reshape.2.skip_ref) | copy-start | bytes 18436
  72.5 168.2 %copy-start.16 = (f32[512,8]{1,0:T(8,128)}, f32[512,8]{1,0:T(8,128)S(1)}, u32[]{:S(2)}) copy-start(f32[512,8]{1,0:T(8,128)S(1)} %pad.21.columns_ref) | copy-start | bytes 49156
  74.1 39.8 %copy-start.76 = (f32[24]{0:T(128)S(1)}, f32[24]{0:T(128)}, u32[]{:S(2)}) copy-start(f32[24]{0:T(128)} %param.79) | copy-start | bytes 292
  74.1 39.8 %collective-permute-start.1 = (bf16[256,2048]{1,0:T(8,128)(2,1)S(1)}, bf16[256,2048]{1,0:T(8,128)(2,1)S(1)}, u32[]{:S(2)}, u32[]{:S(2)}) collective-permute-start(bf16[256,2048]{1,0:T(8,128)(2,1)S(1)} %convolution_convert_fusion.7), channel_id=1, source_target_pairs={{0,1},{1,0},{2,3},{3,2},{4,5},{5,4},{6,7},{7,6},{8,9},{9,8},{10,11... | collective-permute-start | bytes 3145736 | tf_op jit(solution)/shard_map/ppermute | solution.py:568
  112.3 24.7 %collective-permute-start = (bf16[256,2048]{1,0:T(8,128)(2,1)S(1)}, bf16[256,2048]{1,0:T(8,128)(2,1)S(1)}, u32[]{:S(2)}, u32[]{:S(2)}) collective-permute-start(bf16[256,2048]{1,0:T(8,128)(2,1)S(1)} %convolution_convert_fusion.9), channel_id=1, source_target_pairs={{0,1},{1,0},{2,3},{3,2},{4,5},{5,4},{6,7},{7,6},{8,9},{9,8},{10,11... | collective-permute-start | bytes 3145736 | tf_op jit(solution)/shard_map/ppermute | solution.py:568
  113.8 73.0 %copy-start.71 = (f32[24]{0:T(128)}, f32[24]{0:T(128)S(1)}, u32[]{:S(2)}) copy-start(f32[24]{0:T(128)S(1)} %exponential_negate_fusion) | copy-start | bytes 292
  142.2 42.3 %copy-start.3 = (bf16[512,2048]{1,0:T(8,128)(2,1)S(1)}, bf16[512,2048]{1,0:T(8,128)(2,1)}, u32[]{:S(2)}) copy-start(bf16[512,2048]{1,0:T(8,128)(2,1)} %multiply_convert_fusion.4.first_ref.second_ref) | copy-start | bytes 6291460
  142.2 42.3 %copy-start.72 = (f32[24]{0:T(128)S(1)}, f32[24]{0:T(128)}, u32[]{:S(2)}) copy-start(f32[24]{0:T(128)} %param.78) | copy-start | bytes 292
  190.7 21.0 %copy-start.44 = (f32[2,12,2,256]{3,2,1,0:T(2,128)}, f32[2,12,2,256]{3,2,1,0:T(2,128)S(1)}, u32[]{:S(2)}) copy-start(f32[2,12,2,256]{3,2,1,0:T(2,128)S(1)} %reshape.700.step_ref) | copy-start | bytes 147460
  234.0 15.0 %collective-permute-start.2 = (f32[512]{0:T(512)S(1)}, f32[512]{0:T(512)S(1)}, u32[]{:S(2)}, u32[]{:S(2)}) collective-permute-start(f32[512]{0:T(512)S(1)} %reduce_sum.175), channel_id=1, source_target_pairs={{0,1},{1,0},{2,3},{3,2},{4,5},{5,4},{6,7},{7,6},{8,9},{9,8},{10,11... | collective-permute-start | bytes 6152 | tf_op jit(solution)/shard_map/ppermute | solution.py:568
  249.0 21.9 %copy-start.38 = (bf16[512,512]{1,0:T(8,128)(2,1)}, bf16[512,512]{1,0:T(8,128)(2,1)S(1)}, u32[]{:S(2)}) copy-start(bf16[512,512]{1,0:T(8,128)(2,1)S(1)} %get-tuple-element.597) | copy-start | bytes 1572868
  253.2 17.7 %copy-start.29 = (bf16[512,1536]{1,0:T(8,128)(2,1)}, bf16[512,1536]{1,0:T(8,128)(2,1)S(1)}, u32[]{:S(2)}) copy-start(bf16[512,1536]{1,0:T(8,128)(2,1)S(1)} %multiply_convert_fusion.5) | copy-start | bytes 4718596
  273.7 47.6 %collective-permute-start.3 = (bf16[512,2048]{1,0:T(8,128)(2,1)S(1)}, bf16[512,2048]{1,0:T(8,128)(2,1)}, u32[]{:S(2)}, u32[]{:S(2)}) collective-permute-start(bf16[512,2048]{1,0:T(8,128)(2,1)S(1)} %add_convert_fusion.6), channel_id=1, source_target_pairs={{0,1},{1,0},{2,3},{3,2},{4,5},{5,4},{6,7},{7,6},{8,9},{9,8},{10,11... | collective-permute-start | bytes 6291464 | tf_op jit(solution)/shard_map/ppermute | solution.py:568
  275.7 53.1 %copy-start.50 = (f32[2048]{0:T(1024)S(1)}, f32[2048]{0:T(1024)}, u32[]{:S(2)}) copy-start(f32[2048]{0:T(1024)} %param.74) | copy-start | bytes 24580
  376.1 33.3 %collective-permute-start.4 = (bf16[256,2048]{1,0:T(8,128)(2,1)S(1)}, bf16[256,2048]{1,0:T(8,128)(2,1)}, u32[]{:S(2)}, u32[]{:S(2)}) collective-permute-start(bf16[256,2048]{1,0:T(8,128)(2,1)S(1)} %get-tuple-element.606), channel_id=1, source_target_pairs={{0,1},{1,0},{2,3},{3,2},{4,5},{5,4},{6,7},{7,6},{8,9},{9,8},{10,11... | collective-permute-start | bytes 3145736 | tf_op jit(solution)/shard_map/ppermute | solution.py:568
  390.4 32.6 %collective-permute-start.5 = (bf16[256,2048]{1,0:T(8,128)(2,1)}, bf16[256,2048]{1,0:T(8,128)(2,1)}, u32[]{:S(2)}, u32[]{:S(2)}) collective-permute-start(bf16[256,2048]{1,0:T(8,128)(2,1)} %get-tuple-element.612), channel_id=1, source_target_pairs={{0,1},{1,0},{2,3},{3,2},{4,5},{5,4},{6,7},{7,6},{8,9},{9,8},{10,11... | collective-permute-start | bytes 3145736 | tf_op jit(solution)/shard_map/ppermute | solution.py:568
  408.9 14.2 %collective-permute-start.6 = (bf16[1024,2048]{1,0:T(8,128)(2,1)}, bf16[1024,2048]{1,0:T(8,128)(2,1)}, u32[]{:S(2)}, u32[]{:S(2)}) collective-permute-start(bf16[1024,2048]{1,0:T(8,128)(2,1)} %get-tuple-element.613), channel_id=1, source_target_pairs={{0,2},{2,0},{4,6},{6,4},{8,10},{10,8},{12,14},{14,12},{16,18},{18,... | collective-permute-start | bytes 12582920 | tf_op jit(solution)/shard_map/ppermute | solution.py:571
  408.9 14.2 %collective-permute-start.7 = (bf16[1024,2048]{1,0:T(8,128)(2,1)}, bf16[1024,2048]{1,0:T(8,128)(2,1)}, u32[]{:S(2)}, u32[]{:S(2)}) collective-permute-start(bf16[1024,2048]{1,0:T(8,128)(2,1)} %get-tuple-element.614), channel_id=1, source_target_pairs={{0,2},{2,0},{4,6},{6,4},{8,10},{10,8},{12,14},{14,12},{16,18},{18,... | collective-permute-start | bytes 12582920 | tf_op jit(solution)/shard_map/ppermute | solution.py:571
  419.3 64.5 %collective-permute-start.8 = (bf16[256,2048]{1,0:T(8,128)(2,1)}, bf16[256,2048]{1,0:T(8,128)(2,1)}, u32[]{:S(2)}, u32[]{:S(2)}) collective-permute-start(bf16[256,2048]{1,0:T(8,128)(2,1)} %get-tuple-element.628), channel_id=1, source_target_pairs={{0,1},{1,0},{2,3},{3,2},{4,5},{5,4},{6,7},{7,6},{8,9},{9,8},{10,11... | collective-permute-start | bytes 3145736 | tf_op jit(solution)/shard_map/ppermute | solution.py:568
  423.1 30.0 %copy-start.70 = (s32[256]{0:T(256)S(1)}, s32[256]{0:T(256)}, u32[]{:S(2)}) copy-start(s32[256]{0:T(256)} %copy-done.69) | copy-start | bytes 3076
  423.1 30.1 %copy-start.17 = (f32[512,8]{1,0:T(8,128)S(1)}, f32[512,8]{1,0:T(8,128)}, u32[]{:S(2)}) copy-start(f32[512,8]{1,0:T(8,128)} %copy-done.16) | copy-start | bytes 49156
  423.1 30.1 %copy-start.26 = (f32[512,128]{1,0:T(8,128)S(1)}, f32[512,128]{1,0:T(8,128)}, u32[]{:S(2)}) copy-start(f32[512,128]{1,0:T(8,128)} %get-tuple-element.1018.cosine_ref) | copy-start | bytes 786436
  423.1 30.1 %copy-start.54 = (f32[2,1,256]{2,1,0:T(1,128)S(1)}, f32[2,1,256]{2,1,0:T(1,128)}, u32[]{:S(2)}) copy-start(f32[2,1,256]{2,1,0:T(1,128)} %copy-done.53) | copy-start | bytes 6148
  423.1 30.1 %copy-start.60 = (f32[1536]{0:T(1024)S(1)}, f32[1536]{0:T(1024)}, u32[]{:S(2)}) copy-start(f32[1536]{0:T(1024)} %param.77) | copy-start | bytes 18436
  439.4 111.0 %collective-permute-start.10 = (bf16[512,2048]{1,0:T(8,128)(2,1)}, bf16[512,2048]{1,0:T(8,128)(2,1)}, u32[]{:S(2)}, u32[]{:S(2)}) collective-permute-start(bf16[512,2048]{1,0:T(8,128)(2,1)} %get-tuple-element.640), channel_id=1, source_target_pairs={{0,4},{2,6},{4,0},{6,2},{8,12},{10,14},{12,8},{14,10},{16,20},{18,... | collective-permute-start | bytes 6291464 | tf_op jit(solution)/shard_map/ppermute | solution.py:571
  441.0 109.4 %collective-permute-start.11 = (bf16[512,2048]{1,0:T(8,128)(2,1)}, bf16[512,2048]{1,0:T(8,128)(2,1)}, u32[]{:S(2)}, u32[]{:S(2)}) collective-permute-start(bf16[512,2048]{1,0:T(8,128)(2,1)} %get-tuple-element.642), channel_id=1, source_target_pairs={{0,8},{2,10},{4,12},{6,14},{8,0},{10,2},{12,4},{14,6},{16,24},{18,... | collective-permute-start | bytes 6291464 | tf_op jit(solution)/shard_map/ppermute | solution.py:571
  453.1 30.7 %copy-start.31 = (bf16[256,256]{1,0:T(8,128)(2,1)}, bf16[256,256]{1,0:T(8,128)(2,1)S(1)}, u32[]{:S(2)}) copy-start(bf16[256,256]{1,0:T(8,128)(2,1)S(1)} %fusion.79) | copy-start | bytes 393220
  453.2 30.6 %copy-start.8 = (bf16[512,2048]{1,0:T(8,128)(2,1)S(1)}, bf16[512,2048]{1,0:T(8,128)(2,1)}, u32[]{:S(2)}) copy-start(bf16[512,2048]{1,0:T(8,128)(2,1)} %copy-done.7) | copy-start | bytes 6291460
  498.0 52.4 %all-to-all-start.2 = ((bf16[16,16,2048]{2,1,0:T(8,128)(2,1)}), bf16[16,16,2048]{2,1,0:T(8,128)(2,1)S(1)}, u32[]{:S(2)}, u32[]{:S(2)}) async-start(bf16[16,16,2048]{2,1,0:T(8,128)(2,1)} %bitcast.100), calls=%async_computation.3 | async-start | bytes 2097152 | tf_op jit(solution)/shard_map/all_to_all | solution.py:619
  502.1 195.5 %reduce-scatter.5.cloned.1.call-start = ((), (), s32[]{:S(2)}) async-start(), calls=%async_computation.9 | async-start | bytes 8912896 | tf_op jit(solution)/shard_map/reduce_scatter | solution.py:862
  502.7 4.0 collective-permute-start.9
  550.4 23.0 %copy-start.64 = (f32[2048]{0:T(1024)S(1)}, f32[2048]{0:T(1024)}, u32[]{:S(2)}) copy-start(f32[2048]{0:T(1024)} %param.73) | copy-start | bytes 24580
  550.4 23.0 %copy-start.66 = (f32[2,2,128]{2,1,0:T(2,128)S(1)}, f32[2,2,128]{2,1,0:T(2,128)}, u32[]{:S(2)}) copy-start(f32[2,2,128]{2,1,0:T(2,128)} %copy-done.65) | copy-start | bytes 6148
  570.1 40.7 %collective-permute-start.12 = (bf16[1024,4480]{1,0:T(8,128)(2,1)}, bf16[1024,4480]{1,0:T(8,128)(2,1)}, u32[]{:S(2)}, u32[]{:S(2)}) collective-permute-start(bf16[1024,4480]{1,0:T(8,128)(2,1)} %get-tuple-element.649), channel_id=1, source_target_pairs={{0,2},{2,0},{4,6},{6,4},{8,10},{10,8},{12,14},{14,12},{16,18},{18,... | collective-permute-start | bytes 27525128 | tf_op jit(solution)/shard_map/ppermute | solution.py:571
  570.1 40.7 %collective-permute-start.13 = (bf16[256,2048]{1,0:T(8,128)(2,1)}, bf16[256,2048]{1,0:T(8,128)(2,1)}, u32[]{:S(2)}, u32[]{:S(2)}) collective-permute-start(bf16[256,2048]{1,0:T(8,128)(2,1)} %get-tuple-element.652), channel_id=1, source_target_pairs={{0,8},{2,10},{4,12},{6,14},{8,0},{10,2},{12,4},{14,6},{16,24},{18,... | collective-permute-start | bytes 3145736 | tf_op jit(solution)/shard_map/ppermute | solution.py:571
  572.1 38.7 %collective-permute-start.14 = (bf16[256,2048]{1,0:T(8,128)(2,1)}, bf16[256,2048]{1,0:T(8,128)(2,1)}, u32[]{:S(2)}, u32[]{:S(2)}) collective-permute-start(bf16[256,2048]{1,0:T(8,128)(2,1)} %get-tuple-element.654), channel_id=1, source_target_pairs={{0,4},{2,6},{4,0},{6,2},{8,12},{10,14},{12,8},{14,10},{16,20},{18,... | collective-permute-start | bytes 3145736 | tf_op jit(solution)/shard_map/ppermute | solution.py:571
  596.4 14.4 %copy-start.62 = (f32[2048]{0:T(1024)}, f32[2048]{0:T(1024)S(1)}, u32[]{:S(2)}) copy-start(f32[2048]{0:T(1024)S(1)} %get-tuple-element.659) | copy-start | bytes 24580
  630.1 80.7 %collective-permute-start.18 = (bf16[512,2304]{1,0:T(8,128)(2,1)}, bf16[512,2304]{1,0:T(8,128)(2,1)}, u32[]{:S(2)}, u32[]{:S(2)}) collective-permute-start(bf16[512,2304]{1,0:T(8,128)(2,1)} %get-tuple-element.671), channel_id=1, source_target_pairs={{0,8},{2,10},{4,12},{6,14},{8,0},{10,2},{12,4},{14,6},{16,24},{18,... | collective-permute-start | bytes 7077896 | tf_op jit(solution)/shard_map/ppermute | solution.py:571
  630.6 78.0 %collective-permute-start.17 = (bf16[512,2176]{1,0:T(8,128)(2,1)}, bf16[512,2176]{1,0:T(8,128)(2,1)}, u32[]{:S(2)}, u32[]{:S(2)}) collective-permute-start(bf16[512,2176]{1,0:T(8,128)(2,1)} %get-tuple-element.669), channel_id=1, source_target_pairs={{0,4},{2,6},{4,0},{6,2},{8,12},{10,14},{12,8},{14,10},{16,20},{18,... | collective-permute-start | bytes 6684680 | tf_op jit(solution)/shard_map/ppermute | solution.py:571
  632.1 76.5 %collective-permute-start.20 = (bf16[256,2048]{1,0:T(8,128)(2,1)}, bf16[256,2048]{1,0:T(8,128)(2,1)S(1)}, u32[]{:S(2)}, u32[]{:S(2)}) collective-permute-start(bf16[256,2048]{1,0:T(8,128)(2,1)} %get-tuple-element.674), channel_id=1, source_target_pairs={{0,1},{1,0},{2,3},{3,2},{4,5},{5,4},{6,7},{7,6},{8,9},{9,8},{10,11... | collective-permute-start | bytes 3145736 | tf_op jit(solution)/shard_map/ppermute | solution.py:568
  633.5 64.2 %collective-permute-start.15 = (bf16[128,2048]{1,0:T(8,128)(2,1)}, bf16[128,2048]{1,0:T(8,128)(2,1)}, u32[]{:S(2)}, u32[]{:S(2)}) collective-permute-start(bf16[128,2048]{1,0:T(8,128)(2,1)} %get-tuple-element.664), channel_id=1, source_target_pairs={{0,16},{2,18},{4,20},{6,22},{8,24},{10,26},{12,28},{14,30},{16,0},... | collective-permute-start | bytes 1572872 | tf_op jit(solution)/shard_map/ppermute | solution.py:571
  635.9 72.7 %collective-permute-start.16 = (bf16[128,2048]{1,0:T(8,128)(2,1)}, bf16[128,2048]{1,0:T(8,128)(2,1)}, u32[]{:S(2)}, u32[]{:S(2)}) collective-permute-start(bf16[128,2048]{1,0:T(8,128)(2,1)} %get-tuple-element.665), channel_id=1, source_target_pairs={{0,16},{2,18},{4,20},{6,22},{8,24},{10,26},{12,28},{14,30},{16,0},... | collective-permute-start | bytes 1572872 | tf_op jit(solution)/shard_map/ppermute | solution.py:571
  697.6 11.0 %collective-permute-start.19 = (f32[16,2048]{1,0:T(8,128)}, f32[16,2048]{1,0:T(8,128)}, u32[]{:S(2)}, u32[]{:S(2)}) collective-permute-start(f32[16,2048]{1,0:T(8,128)} %get-tuple-element.1166), channel_id=1, source_target_pairs={{0,2},{2,0},{4,6},{6,4},{8,10},{10,8},{12,14},{14,12},{16,18},{18,... | collective-permute-start | bytes 393224 | tf_op jit(solution)/shard_map/ppermute | solution.py:571
  725.4 113.2 %all-to-all-start.3 = ((bf16[16,16,2048]{2,1,0:T(8,128)(2,1)}), bf16[16,16,2048]{2,1,0:T(8,128)(2,1)S(1)}, u32[]{:S(2)}, u32[]{:S(2)}) async-start(bf16[16,16,2048]{2,1,0:T(8,128)(2,1)} %bitcast.101), calls=%async_computation.5 | async-start | bytes 2097152 | tf_op jit(solution)/shard_map/all_to_all | solution.py:619
  730.2 44.0 %collective-permute-start.22 = (bf16[256,2304]{1,0:T(8,128)(2,1)}, bf16[256,2304]{1,0:T(8,128)(2,1)S(1)}, u32[]{:S(2)}, u32[]{:S(2)}) collective-permute-start(bf16[256,2304]{1,0:T(8,128)(2,1)} %get-tuple-element.681), channel_id=1, source_target_pairs={{0,4},{2,6},{4,0},{6,2},{8,12},{10,14},{12,8},{14,10},{16,20},{18,... | collective-permute-start | bytes 3538952 | tf_op jit(solution)/shard_map/ppermute | solution.py:571
  732.1 42.0 %collective-permute-start.21 = (bf16[256,2176]{1,0:T(8,128)(2,1)}, bf16[256,2176]{1,0:T(8,128)(2,1)}, u32[]{:S(2)}, u32[]{:S(2)}) collective-permute-start(bf16[256,2176]{1,0:T(8,128)(2,1)} %get-tuple-element.679), channel_id=1, source_target_pairs={{0,8},{2,10},{4,12},{6,14},{8,0},{10,2},{12,4},{14,6},{16,24},{18,... | collective-permute-start | bytes 3342344 | tf_op jit(solution)/shard_map/ppermute | solution.py:571
  733.6 39.1 %collective-permute-start.23 = (f32[16,2048]{1,0:T(8,128)}, f32[16,2048]{1,0:T(8,128)S(1)}, u32[]{:S(2)}, u32[]{:S(2)}) collective-permute-start(f32[16,2048]{1,0:T(8,128)} %get-tuple-element.682), channel_id=1, source_target_pairs={{0,4},{2,6},{4,0},{6,2},{8,12},{10,14},{12,8},{14,10},{16,20},{18,... | collective-permute-start | bytes 393224 | tf_op jit(solution)/shard_map/ppermute | solution.py:571
  774.1 36.2 %copy-start.28 = (bf16[128,2048]{1,0:T(8,128)(2,1)S(1)}, bf16[128,2048]{1,0:T(8,128)(2,1)}, u32[]{:S(2)}) copy-start(bf16[128,2048]{1,0:T(8,128)(2,1)} %reduce-scatter.5.cloned.1.call-done) | copy-start | bytes 1572868
  774.1 36.2 %copy-start.37 = (bf16[128,2048]{1,0:T(8,128)(2,1)S(1)}, bf16[128,2048]{1,0:T(8,128)(2,1)}, u32[]{:S(2)}) copy-start(bf16[128,2048]{1,0:T(8,128)(2,1)} %reduce-scatter.3.cloned.1.call-done) | copy-start | bytes 1572868
  780.4 58.2 %collective-permute-start.26 = (bf16[128,2304]{1,0:T(8,128)(2,1)}, bf16[128,2304]{1,0:T(8,128)(2,1)}, u32[]{:S(2)}, u32[]{:S(2)}) collective-permute-start(bf16[128,2304]{1,0:T(8,128)(2,1)} %get-tuple-element.697), channel_id=1, source_target_pairs={{0,16},{2,18},{4,20},{6,22},{8,24},{10,26},{12,28},{14,30},{16,0},... | collective-permute-start | bytes 1769480 | tf_op jit(solution)/shard_map/ppermute | solution.py:571
  783.0 55.6 %collective-permute-start.25 = (bf16[128,2176]{1,0:T(8,128)(2,1)}, bf16[128,2176]{1,0:T(8,128)(2,1)}, u32[]{:S(2)}, u32[]{:S(2)}) collective-permute-start(bf16[128,2176]{1,0:T(8,128)(2,1)} %get-tuple-element.695), channel_id=1, source_target_pairs={{0,16},{2,18},{4,20},{6,22},{8,24},{10,26},{12,28},{14,30},{16,0},... | collective-permute-start | bytes 1671176 | tf_op jit(solution)/shard_map/ppermute | solution.py:571
  783.4 27.0 %collective-permute-start.24 = (f32[16,2048]{1,0:T(8,128)S(1)}, f32[16,2048]{1,0:T(8,128)}, u32[]{:S(2)}, u32[]{:S(2)}) collective-permute-start(f32[16,2048]{1,0:T(8,128)S(1)} %get-tuple-element.690), channel_id=1, source_target_pairs={{0,8},{2,10},{4,12},{6,14},{8,0},{10,2},{12,4},{14,6},{16,24},{18,... | collective-permute-start | bytes 393224 | tf_op jit(solution)/shard_map/ppermute | solution.py:571
  817.4 21.2 %collective-permute-start.27 = (f32[16,2048]{1,0:T(8,128)S(1)}, f32[16,2048]{1,0:T(8,128)S(1)}, u32[]{:S(2)}, u32[]{:S(2)}) collective-permute-start(f32[16,2048]{1,0:T(8,128)S(1)} %get-tuple-element.699), channel_id=1, source_target_pairs={{0,16},{2,18},{4,20},{6,22},{8,24},{10,26},{12,28},{14,30},{16,0},... | collective-permute-start | bytes 393224 | tf_op jit(solution)/shard_map/ppermute | solution.py:571
  847.8 6.5 collective-permute-start.29
  849.2 10.7 %collective-permute-start.28 = (f32[64,512]{1,0:T(8,128)}, f32[64,512]{1,0:T(8,128)S(1)}, u32[]{:S(2)}, u32[]{:S(2)}) collective-permute-start(f32[64,512]{1,0:T(8,128)} %get-tuple-element.710), channel_id=1, source_target_pairs={{0,1},{1,0},{2,3},{3,2},{4,5},{5,4},{6,7},{7,6},{8,9},{9,8},{10,11... | collective-permute-start | bytes 393224 | tf_op jit(solution)/shard_map/ppermute | solution.py:568
  (52 other events, 219.8 us)
Sparse Core Ops, SparseCore 0:
  11.6 172.8 all-gather.4
  186.1 138.4 all-gather.2
  375.3 139.5 reduce-scatter.2
  518.8 144.4 reduce-scatter.4

commit v11 on v10

--- a/solution.py
+++ b/solution.py
@@ -272,23 +272,24 @@
     )
 
 
-def attention_forward(joint, query_cols, key_cols, tables):
+def attention_forward(query, key_value, tables):
     micro, _, rows = tables[3].shape
-    total = joint.shape[0]
+    total, query_cols = query.shape
+    key_cols = key_value.shape[1] // 2
     heads, kv_heads = query_cols // HEAD, key_cols // HEAD
     by_head, by_kv, table_specs = attention_specs(rows, heads // kv_heads)
     return pl.pallas_call(
         attention_forward_kernel,
         out_shape=tuple(jax.ShapeDtypeStruct((total, size), bf16) for size in (query_cols, query_cols, key_cols, key_cols)),
         grid=(micro, heads),
-        in_specs=[by_head(0), by_kv(heads), by_kv(heads + kv_heads)] + table_specs,
+        in_specs=[by_head(0), by_kv(0), by_kv(kv_heads)] + table_specs,
         out_specs=(by_head(0), by_head(0), by_kv(0), by_kv(0)),
         scratch_shapes=[pltpu.VMEM((rows, rows), f32)],
         cost_estimate=pl.CostEstimate(
             flops=4 * total * rows * query_cols, transcendentals=total * rows * heads, bytes_accessed=8 * total * query_cols
         ),
         name="attention_forward",
-    )(joint, joint, joint, *tables)
+    )(query, key_value, key_value, *tables)
 
 
 def attention_backward(grad, query, key, value, tables):
@@ -354,9 +355,12 @@
     grad_ref, out_ref, gate_ref, signal_ref, taps_ref, skip_ref, gain_ref, state_ref, seg_row_ref, run_row_ref, run_col_ref,
     step_ref, columns_ref, state_raw_ref, state_taps_ref, step_all_ref, step_sig_ref, rate_ref, others_ref,
     first_ref, sums_ref, state_sums_ref, head_sums_ref,
-    inner_ref, mask_ref, grad_inner_ref, direct_ref, along_ref,
+    inner_ref, mask_ref, grad_inner_ref, direct_ref, along_ref, *, query_cols,
 ):
     rows = signal_ref.shape[0]
+    rest = taps_ref.shape[1]
+    after_rest = rest + 2 * NS + STEP_PAD
+    input_start = after_rest + query_cols
     pair = pl.program_id(1)
     block = pl.ds(pl.multiple_of(pair * 2 * SHD, 2 * SHD), 2 * SHD)
     taps_ref, skip_ref, gain_ref = taps_ref.at[:, block], skip_ref.at[:, block], gain_ref.at[:, block]
@@ -373,8 +377,6 @@
     grad, out, gate, signal = grad_ref[...], out_ref[...], gate_ref[...], signal_ref[...]
     position, scale, cross = columns_ref[:, 1:2], columns_ref[:, 2:3], columns_ref[:, 3:4]
     here = pl.multiple_of(pair * 2 * SHD, 2 * SHD)
-    rest = first_ref.shape[1] // 2 - others_ref.shape[1] // 2 - NS - STEP_PAD // 2
-    after_rest = rest + 2 * NS + STEP_PAD
     sig = sigmoid_of(gate)
     silu = gate * sig
     gated = out * silu
@@ -414,7 +416,7 @@
     sums_ref[0, CONV + 1 : CONV + 2, :] = jnp.sum(scaled * gated, axis=0, keepdims=True)
     sums_ref[0, CONV + 2 : CONV + 3, :] = jnp.sum(grad_out * cols, axis=0, keepdims=True)
     sums_ref[0, CONV + 3 : CONV + 4, :] = jnp.zeros((1, cols.shape[1]), f32)
-    first_ref[:, pl.ds(pl.multiple_of(after_rest + here, 2 * SHD), 2 * SHD)] = grad_signal.astype(bf16)
+    first_ref[:, pl.ds(pl.multiple_of(input_start + here, 2 * SHD), 2 * SHD)] = grad_signal.astype(bf16)
 
     @pl.when(pair == pl.num_programs(1) - 1)
     def _():
@@ -445,7 +447,8 @@
         head_sums_ref[0, :, 1:2] = jnp.sum(grad_raw, axis=1, keepdims=True)
         wide = jnp.concatenate([grad_raw, jnp.zeros((STEP_PAD - heads, rows), f32)], axis=0)
         first_ref[:, rest + 2 * NS : after_rest] = wide.T.astype(bf16)
-        first_ref[:, first_ref.shape[1] - others_ref.shape[1] :] = others_ref[...]
+        first_ref[:, after_rest:input_start] = others_ref[:, :query_cols]
+        first_ref[:, input_start + rest :] = others_ref[:, query_cols:]
 
 
 def state_specs(rows, pairs):
@@ -483,7 +486,7 @@
 
 def state_backward(
     grad, out, gate, signal, taps, skip, gain, state, seg_row, run_row, run_col, step, columns,
-    state_raw, state_taps, step_all, step_sig, rate, others,
+    state_raw, state_taps, step_all, step_sig, rate, others, query_cols,
 ):
     micro, pairs, _, rows = run_row.shape
     heads = 2 * pairs
@@ -492,7 +495,7 @@
     joint = 2 * width + 2 * NS + STEP_PAD + others.shape[1]
     heads_block = pl.BlockSpec((1, heads, rows), lambda m, p: (m, 0, 0))
     return pl.pallas_call(
-        state_backward_kernel,
+        functools.partial(state_backward_kernel, query_cols=query_cols),
         out_shape=(
             jax.ShapeDtypeStruct((total, joint), bf16),
             jax.ShapeDtypeStruct((micro, 8, width), f32),
@@ -575,7 +578,7 @@
 
     step_padded = jnp.pad(step_weight, ((0, 0), (0, STEP_PAD - step_weight.shape[1])))
     early = dict(
-        gate=mamba_gate, state=state_weight, step=step_padded, input=mamba_input, query=query_weight, key=key_weight,
+        gate=mamba_gate, state=state_weight, step=step_padded, query=query_weight, input=mamba_input, key=key_weight,
         value=value_weight, mix=mamba_out, attn=attention_out,
     )
     late = dict(fgate=feed_gate, fup=feed_up, fdown=feed_down)
@@ -743,11 +746,11 @@
     row_columns = jnp.pad(row_facts, ((0, 0), (0, 6)))
     query_cols, key_cols = query_weight.shape[1], key_weight.shape[1]
     attention_tables = (*rope_tables(position), row_columns, layout[1])
-    joint_start = places_of["query"][1]
-    joint_weight = lax.slice_in_dim(whole["early"], joint_start, joint_start + query_cols + 2 * key_cols, axis=1)
+    pair_start = places_of["key"][1]
+    pair_weight = lax.slice_in_dim(whole["early"], pair_start, pair_start + 2 * key_cols, axis=1)
     ssm_out, squares = state_forward(ssm_in, gate_z, kernel_inner, skip_wide, *layout, row_columns)
     attended_low, query_low, key_low, value_low = attention_forward(
-        project(normed_low, joint_weight), query_cols, key_cols, attention_tables
+        project(normed_low, full("query")), project(normed_low, pair_weight), attention_tables
     )
     square_own = jnp.sum(squares, axis=1)
     square_sum = square_own + other_lane(square_own)
@@ -868,7 +871,7 @@
         columns = jnp.pad(jnp.concatenate([row_facts, inv_rms, cross], axis=1), ((0, 0), (0, 4)))
         first_right, column_sums, state_sums, head_sums = state_backward(
             grad_gated_norm, ssm_out, gate_z, ssm_in, kernel_inner, skip_wide, gain_row, *layout, columns,
-            state_raw, kernel_state, step_heads, step_sig, rate_column, joint_low,
+            state_raw, kernel_state, step_heads, step_sig, rate_column, joint_low, query_cols,
         )
         return column_sums, state_sums, head_sums, first_right
 
@@ -891,7 +894,7 @@
     grad_gain_in, in_own, in_send = unit(input_gradient)
 
     firsts = (red_low, red_high)
-    low_size = gate_cols + 2 * NS + STEP_PAD
+    low_size = gate_cols + 2 * NS + STEP_PAD + query_cols
     first_sizes = (low_size, first_right.shape[1] - low_size)
 
     def first_moves():
@@ -924,10 +927,10 @@
     def finish():
         low, high = red_low.result, red_high.result
         state_rows = low[:, gate_cols : gate_cols + 2 * NS].reshape(lanes, shard // lanes, 2 * NS)
-        cut = [0, gate_cols, gate_cols + query_cols, gate_cols + query_cols + key_cols, high.shape[1]]
+        cut = [0, gate_cols, gate_cols + key_cols, high.shape[1]]
         pieces = (
             low[:, :gate_cols], low[:, gate_cols + 2 * NS : gate_cols + 2 * NS + heads],
-            [high[:, start:stop] for start, stop in zip(cut, cut[1:])],
+            low[:, gate_cols + 2 * NS + STEP_PAD :], [high[:, start:stop] for start, stop in zip(cut, cut[1:])],
             [lax.dynamic_index_in_dim(state_rows, which, 0, keepdims=False) for which in (lane, 1 - lane)],
         )
         return pieces, deal_take(in_moved)
@@ -966,7 +969,7 @@
         red_low.result, red_high.result = red_low.last(), red_high.last()
         return finish(), flat + flat_moved if flat_moved is not None else flat
 
-    ((total_gate, total_step, (total_input, total_query, total_key, total_value), states), grad_input), flat = unit(last_work)
+    ((total_gate, total_step, total_query, (total_input, total_key, total_value), states), grad_input), flat = unit(last_work)
     while bits < len(masks):
         flat = flat + other_group(flat, masks[bits])
         bits += 1

time: 872 us -> 854 us (0.979)
  waiting for transfers between devices: 349 us -> 339 us
    ppermute x19, waiting for transfers between devices: 165 us -> 153 us  [other_group(): return lax.ppermute(values, 'dp', [(i, i ^ bits) for i in range(groups)])]
    dot_general x14 -> x15, matrix products: 68 us -> 69.6 us  [project(): return jnp.dot(left, right, preferred_element_type=f32)]
where the time goes in v11:
time: 854 us; the launch traced here: 850 us
  waiting for transfers between devices  339 us (40%)
  matrix products  209 us (24%)
  Pallas kernels  87.5 us (10%)
  other arithmetic  73.6 us (9%)
  local copies, waits for them, and re-layouts  61.1 us (7%)
  starting transfers between devices  61.1 us (7%)
  between operations  15.7 us (2%)
    ppermute x19, waiting for transfers between devices, other_group(): return lax.ppermute(values, 'dp', [(i, i ^ bits) for i in range(groups)])  153 us
    ppermute x11, waiting for transfers between devices, other_lane(): return lax.ppermute(values, 'tensor', swap_lane)  76.3 us
    all_to_all x4, waiting for transfers between devices, exchange(): lax.all_to_all(buffer.reshape(groups, micro * per, width), 'dp', split_ax...  73.3 us
    dot_general x8, matrix products, project_back(): lax.dot_general(left, right, (((1,), (1,)), ((), ())), preferred_element_...  71.7 us
    dot_general x15, matrix products, project(): return jnp.dot(left, right, preferred_element_type=f32)  69.6 us
    dot_general x12, matrix products, outer_sum(): lax.dot_general(left, right, (((0,), (0,)), ((), ())), preferred_element_...  67.7 us
    all_gather x2, waiting for transfers between devices, local(): lax.all_gather(join_columns(list(group_weights.values())), 'dp', axis=0,...  35.7 us
    pallas_call x1, Pallas kernels, state_backward(): pl.pallas_call(functools.partial(state_backward_kernel, query_cols=query_...  34.1 us
  transfers between devices with their start and end apart: 38, of which 16 were waited for; matrix products, arithmetic and copies ran while one was open for 31% of the time, Pallas kernels for 10%

profile of v11, /device:TPU:0, one launch (start us, length us, event | category | flops | bytes accessed | tf_op | source)
XLA Modules:
  0.0 849.5 jit_solution(7641411647665765595)
XLA Ops:
  14.4 4.9 select_reduce_fusion
  21.1 7.4 all-to-all-start.1
  30.2 38.2 %all-to-all-done.1 = bf16[16,16,2048]{2,1,0:T(8,128)(2,1)S(1)} async-done(((bf16[16,16,2048]{2,1,0:T(8,128)(2,1)}), bf16[16,16,2048]{2,1,0:T(8,128)(2,1)S(1)}, u32[]{:S(2)}, u32[]{:S(2)}) %all-to-all-start.1) | async-done | bytes 1048608 | tf_op jit(solution)/shard_map/all_to_all | solution.py:622
  76.7 35.1 %all-to-all-done = bf16[16,16,2048]{2,1,0:T(8,128)(2,1)S(1)} async-done(((bf16[16,16,2048]{2,1,0:T(8,128)(2,1)}), bf16[16,16,2048]{2,1,0:T(8,128)(2,1)S(1)}, u32[]{:S(2)}, u32[]{:S(2)}) %all-to-all-start) | async-done | bytes 1048608 | tf_op jit(solution)/shard_map/all_to_all | solution.py:622
  115.8 21.2 %collective-permute-done = bf16[256,2048]{1,0:T(8,128)(2,1)S(1)} collective-permute-done((bf16[256,2048]{1,0:T(8,128)(2,1)S(1)}, bf16[256,2048]{1,0:T(8,128)(2,1)S(1)}, u32[]{:S(2)}, u32[]{:S(2)}) %collective-permute-start) | collective-permute-done | bytes 1048608 | tf_op jit(solution)/shard_map/ppermute | solution.py:571
  142.2 6.7 pick_halves.3
  148.9 35.6 %all-gather.5.cloned.1.call-done = bf16[2048,6528]{1,0:T(8,128)(2,1)} async-done(((bf16[128,6528]{1,0:T(8,128)(2,1)}), bf16[2048,6528]{1,0:T(8,128)(2,1)}) %all-gather.5.cloned.1.call-update) | async-done | bytes 26738704 | tf_op jit(solution)/shard_map/all_gather | solution.py:591
  195.7 8.0 fusion.68.gate_ref
  203.7 7.9 fusion.70.signal_ref
  211.7 21.0 %state_forward.1 = (f32[512,1536]{1,0:T(8,128)}, f32[512,128]{1,0:T(8,128)}) custom-call(f32[512,1536]{1,0:T(8,128)} %fusion.70.signal_ref, f32[512,1536]{1,0:T(8,128)} %fusion.68.gate_ref, f32[5,1536]{1,0:T(8,128)S(1)} %copy-done.53, f32[1,1536]{1,0:T(1,128)S(1)} %broadcast_in_dim_reshape.2.skip_ref, bf16[512,512]{1,0:T(8,128)(2,1)S(1)} %copy-done.14, ...), custom_call_target="tpu_custom_call" | custom-call | flops 1610612736 | bytes 9437184 | tf_op jit(solution)/shard_map/state_forward/pallas_call | solution.py:472
  238.5 4.0 fusion.73.query_ref
  242.5 8.2 attention_forward.1
  250.8 4.4 multiply_convert_fusion.5
  255.1 17.8 %fusion.66 = f32[512,2048]{1,0:T(8,128)S(1)} fusion(bf16[512,1536]{1,0:T(8,128)(2,1)S(1)} %multiply_convert_fusion.5, bf16[2048,6528]{1,0:T(8,128)(2,1)} %all-gather.5.cloned.1.call-done), kind=kOutput, calls=%fused_computation.121 | convolution fusion | flops 3221225472 | bytes 12058624 | tf_op jit(solution)/shard_map/dot_general | solution.py:30
  277.1 46.4 %collective-permute-done.3 = bf16[512,2048]{1,0:T(8,128)(2,1)} collective-permute-done((bf16[512,2048]{1,0:T(8,128)(2,1)S(1)}, bf16[512,2048]{1,0:T(8,128)(2,1)}, u32[]{:S(2)}, u32[]{:S(2)}) %collective-permute-start.3) | collective-permute-done | bytes 2097184 | tf_op jit(solution)/shard_map/ppermute | solution.py:571
  323.5 6.0 fusion.95
  331.4 45.8 %conditional.16 = (bf16[512,2048]{1,0:T(8,128)(2,1)}, bf16[512,2048]{1,0:T(8,128)(2,1)}, bf16[512,2048]{1,0:T(8,128)(2,1)}, bf16[256,2048]{1,0:T(8,128)(2,1)S(1)...) conditional(s32[]{:T(128)} %convert_element_type.487, () %tuple.161, (bf16[2048,6144]{1,0:T(8,128)(2,1)}, ...), branch_computations={%region_7.8_spmd, %region_8.11_spmd} | conditional | flops 21501050880 | bytes 124814440 | solution.py:713
  331.4 6.9 fusion.4
  338.3 7.0 fusion.8
  345.4 10.2 %multiply_convert_fusion = (bf16[512,2048]{1,0:T(8,128)(2,1)}, bf16[512,2048]{1,0:T(8,128)(2,1)}, bf16[512,2048]{1,0:T(8,128)(2,1)}) fusion(f32[512,2048]{1,0:T(8,128)S(1)} %fusion.8, f32[512,2048]{1,0:T(8,128)S(1)} %fusion.4, bf16[512,2048]{1,0:T(8,128)(2,1)S(1)} %copy-done.12, bf16[2048,6144]{1,0:T(8,128)(2,1)} %get-tuple-element.306), kind=kOutput, calls=%fused_computation.11 | convolution fusion | flops 4310695936 | bytes 25165824 | tf_op jit(solution)/shard_map/cond/branch_1_fun/dot_general | solution.py:26
  355.6 6.2 fusion.2
  361.8 6.3 multiply_reduce_fusion
  368.5 8.3 convert_bitcast_fusion
  378.6 13.9 %conditional.17 = (bf16[256,2048]{1,0:T(8,128)(2,1)}, f32[2048]{0:T(1024)}) conditional(s32[]{:T(128)} %convert_element_type.513, () %tuple.165, (f32[512,1]{0,1:T(1,128)S(1)}, bf16[512,2048]{1,0:T(8,128)(2,1)}, bf16[2048,6144]{1,0:T(8,128)(2,1)}, bf16[512,2048]{1,0:T(8,128)(2,1)}, f32[2048]{0:T(1024)S(1)}, ...), branch_computations={%region_11.12_spmd, %region_12.15_spmd} | conditional | flops 4301257728 | bytes 49316908 | solution.py:713
  378.6 6.2 fusion.18
  384.8 6.3 multiply_reduce_fusion.2
  394.1 16.9 %conditional.18 = (bf16[512,1024]{1,0:T(8,128)(2,1)}, bf16[1024,2048]{1,0:T(8,128)(2,1)}, bf16[1024,2048]{1,0:T(8,128)(2,1)}) conditional(s32[]{:T(128)} %convert_element_type.514, () %tuple.168, (s32[16]{0:T(128)S(1)}, bf16[512,2048]{1,0:T(8,128)(2,1)S(1)}, bf16[512,2048]{1,0:T(8,128)(2,1)}, bf16[512,2048]{1,0:T(8,128)(2,1)}) %tuple.169), branch_computations={%region_15.16_spmd, %region_16.17_spmd} | conditional | flops 4299161600 | bytes 23068724 | solution.py:713
  394.1 4.1 pick_halves.2
  398.1 6.7 convolution_convert_fusion
  404.9 6.1 convolution_convert_fusion.1
  411.5 9.8 %conditional.19 = (bf16[256,2048]{1,0:T(8,128)(2,1)S(1)}, bf16[256,2048]{1,0:T(8,128)(2,1)}) conditional(s32[]{:T(128)} %convert_element_type.515, () %tuple.172, (bf16[2048,6144]{1,0:T(8,128)(2,1)}, bf16[512,2048]{1,0:T(8,128)(2,1)}, s32[]{:T(128)}) %tuple.173), branch_computations={%region_17.18_spmd, %region_18.19_spmd} | conditional | flops 4296015872 | bytes 16777320 | solution.py:713
  411.6 8.5 %fusion.31 = bf16[512,2048]{1,0:T(8,128)(2,1)S(1)} fusion(bf16[512,2048]{1,0:T(8,128)(2,1)} %get-tuple-element.323, bf16[2048,6144]{1,0:T(8,128)(2,1)} %get-tuple-element.324), kind=kOutput, calls=%fused_computation.42 | convolution fusion | flops 4296015872 | bytes 12582912 | tf_op jit(solution)/shard_map/cond/branch_1_fun/dot_general | solution.py:30
  421.7 4.0 collective-permute-done.5.values_ref
  425.8 16.4 %conditional.20 = (bf16[512,2048]{1,0:T(8,128)(2,1)}, bf16[1,2,2,128,2048]{4,3,2,1,0:T(8,128)(2,1)}, bf16[512,2048]{1,0:T(8,128)(2,1)}, bf16[2,1,2,128,2048]{4,3,2,1,0:T(8,128)(2,1)}) conditional(s32[]{:T(128)} %convert_element_type.516, () %tuple.175, (bf16[512,1024]{1,0:T(8,128)(2,1)}, bf16[512,2048]{1,0:T(8,128)(2,1)}, ...), branch_computations={%region_19.20_spmd, %region_20.21_spmd} | conditional | flops 4307550208 | bytes 39845920 | solution.py:713
  425.8 5.6 add_convert_fusion.1
  433.9 5.6 add_convert_fusion
  443.1 10.8 %collective-permute-start.11 = (bf16[512,2048]{1,0:T(8,128)(2,1)}, bf16[512,2048]{1,0:T(8,128)(2,1)}, u32[]{:S(2)}, u32[]{:S(2)}) collective-permute-start(bf16[512,2048]{1,0:T(8,128)(2,1)} %get-tuple-element.642), channel_id=1, source_target_pairs={{0,8},{2,10},{4,12},{6,14},{8,0},{10,2},{12,4},{14,6},{16,24},{18,... | collective-permute-start | bytes 6291464 | tf_op jit(solution)/shard_map/ppermute | solution.py:574
  454.1 30.4 %conditional.21 = (f32[512]{0:T(512)}, f32[256,2048]{1,0:T(8,128)}, f32[512,1536]{1,0:T(8,128)}, bf16[512,2048]{1,0:T(8,128)(2,1)}, bf16[512,768]{1,0:T(8,128)(2,1)S(1)}) conditional(s32[]{:T(128)} %convert_element_type.517, () %tuple.179, (bf16[512,2048]{1,0:T(8,128)(2,1)}, bf16[256,2048]{1,0:T(8,128)(2,1)}, bf16[256,2048]{1,0:T(8,128)(2,1)}, ...), branch_computations={%region_21.22_spmd, %region_22.24_spmd} | conditional | flops 4979949056 | bytes 83370136 | solution.py:713
  462.7 9.4 %multiply_reduce_fusion.4 = (f32[512]{0:T(512)}, f32[512,1536]{1,0:T(8,128)}) fusion(f32[512,1536]{1,0:T(8,128)S(1)} %copy-done.11, f32[512,1536]{1,0:T(8,128)S(1)} %copy-done.4, f32[1536]{0:T(1024)S(1)} %get-tuple-element.337, bf16[512,2048]{1,0:T(8,128)(2,1)} %get-tuple-element.1064, bf16[2048,6528]{1,0:T(8,128)(2,1)} %get-tuple-element.336), kind=kOutput, calls=%fused_computation.50 | convolution fusion | flops 3227516416 | bytes 17833984 | tf_op jit(solution)/shard_map/cond/branch_1_fun/dot_general | solution.py:26
  472.1 4.3 fusion.38.grad_ref
  476.4 8.0 attention_backward.1
  485.4 12.1 %conditional.22 = (bf16[2048,2048]{1,0:T(8,128)(2,1)}, bf16[256,2048]{0,1:T(8,128)(2,1)S(1)}) conditional(s32[]{:T(128)} %convert_element_type.518, () %tuple.182, (bf16[512,1536]{1,0:T(8,128)(2,1)}, bf16[512,512]{1,0:T(8,128)(2,1)}, bf16[512,2048]{1,0:T(8,128)(2,1)}, bf16[512,2048]{1,0:T(8,128)(2,1)S(1)}, s32[]{:T(128)}, ...), branch_computations={%region_24.25_spmd, %region_25.26_spmd} | conditional | flops 4575461376 | bytes 31588488 | solution.py:713
  489.0 8.5 %convert_bitcast_fusion.1 = bf16[2048,2048]{1,0:T(8,128)(2,1)} fusion(bf16[512,2048]{1,0:T(8,128)(2,1)} %get-tuple-element.350, bf16[512,512]{1,0:T(8,128)(2,1)S(1)} %copy-done.45, bf16[512,1536]{1,0:T(8,128)(2,1)S(1)} %copy-done.30), kind=kOutput, calls=%fused_computation.57 | convolution fusion | flops 4303355904 | bytes 12582912 | tf_op jit(solution)/shard_map/cond/branch_1_fun/dot_general | solution.py:34
  498.9 4.0 all-to-all-start.2
  507.5 43.8 %conditional.23 = (f32[2,8,1536]{2,1,0:T(8,128)}, f32[2,8,512]{2,1,0:T(8,128)}, f32[2,24,2]{2,1,0:T(8,128)}, bf16[512,4480]{1,0:T(8,128)(2,1)}) conditional(s32[]{:T(128)} %convert_element_type.520, () %tuple.185, (f32[1536]{0:T(1024)}, f32[512]{0:T(512)}, f32[512]{0:T(512)}, f32[512]{0:T(512)}, f32[512,2]{0,1:T(2,128)S(1)}, ...), branch_computations={%region_26.27_spmd, %region_27.28_spmd} | conditional | flops 4026538496 | bytes 15904996 | solution.py:713
  517.2 34.1 %state_backward.1 = (bf16[512,4480]{1,0:T(8,128)(2,1)}, f32[2,8,1536]{2,1,0:T(8,128)}, f32[2,8,512]{2,1,0:T(8,128)}, f32[2,24,2]{2,1,0:T(8,128)}) custom-call(f32[512,1536]{1,0:T(8,128)} %get-tuple-element.356.grad_ref, f32[512,1536]{1,0:T(8,128)} %get-tuple-element.357.out_ref, f32[512,1536]{1,0:T(8,128)} %get-tuple-element.358.gate_ref, ...), custom_call_target="tpu_custom_call" | custom-call | flops 4026531840 | bytes 15728640 | tf_op jit(solution)/shard_map/cond/branch_1_fun/state_backward/pallas_call | solution.py:497
  551.4 19.4 %conditional.24 = (bf16[1024,4480]{1,0:T(8,128)(2,1)}, bf16[256,2048]{1,0:T(8,128)(2,1)}, bf16[1,1,2,128,2048]{4,3,2,1,0:T(8,128)(2,1)S(1)}, bf16[256,2048]{1,0:...) conditional(s32[]{:T(128)} %convert_element_type.521, () %tuple.189, ...), branch_computations={%region_29.30_spmd, %region_30.31_spmd} | conditional | flops 4979556352 | bytes 42205260 | solution.py:713
  559.6 9.8 %convolution_convert_fusion.3 = bf16[1024,4480]{1,0:T(8,128)(2,1)} fusion(bf16[512,1024]{1,0:T(8,128)(2,1)S(1)} %copy-done.82, bf16[512,4480]{1,0:T(8,128)(2,1)} %get-tuple-element.383), kind=kOutput, calls=%fused_computation.70 | convolution fusion | flops 4702208000 | bytes 14811136 | tf_op jit(solution)/shard_map/cond/branch_1_fun/dot_general | solution.py:34
  574.2 23.1 %conditional.25 = (f32[2048]{0:T(1024)S(1)}, bf16[256,2048]{1,0:T(8,128)(2,1)}, bf16[256,2048]{1,0:T(8,128)(2,1)S(1)}) conditional(s32[]{:T(128)} %convert_element_type.523, () %tuple.192, (bf16[2048,6528]{1,0:T(8,128)(2,1)}, bf16[512,4480]{1,0:T(8,128)(2,1)}, f32[512,2048]{1,0:T(8,128)}, f32[2,2,128]{2,1,0:T(2,128)S(1)}, f32[]{:T(128)}, ...), branch_computations={%region_31.32_spmd, %region_32.35_spmd} | conditional | flops 9406776320 | bytes 46049396 | solution.py:713
  574.4 17.4 %multiply_reduce_fusion.5 = (f32[512]{0:T(512)S(1)}, f32[2048]{0:T(1024)S(1)}, f32[512,2048]{1,0:T(8,128)}) fusion(f32[512,2048]{1,0:T(8,128)} %get-tuple-element.392, f32[2048]{0:T(1024)S(1)} %get-tuple-element.396, f32[512]{0:T(512)S(1)} %bitcast.296, bf16[512,4480]{1,0:T(8,128)(2,1)} %get-tuple-element.390, bf16[2048,6528]{1,0:T(8,128)(2,1)} %get-tuple-element.391), kind=kOutput, calls=%fused_computation.79 | convolution fusion | flops 9401530368 | bytes 31346688 | tf_op jit(solution)/shard_map/cond/branch_1_fun/dot_general | solution.py:30
  591.8 4.3 subtract_convert_fusion.2
  597.2 15.1 %collective-permute-done.13 = bf16[256,2048]{1,0:T(8,128)(2,1)} collective-permute-done((bf16[256,2048]{1,0:T(8,128)(2,1)}, bf16[256,2048]{1,0:T(8,128)(2,1)}, u32[]{:S(2)}, u32[]{:S(2)}) %collective-permute-start.13) | collective-permute-done | bytes 1048608 | tf_op jit(solution)/shard_map/ppermute | solution.py:574
  612.4 19.3 %conditional.26 = (bf16[512,2688]{1,0:T(8,128)(2,1)}, bf16[1,2,2,128,2688]{4,3,2,1,0:T(8,128)(2,1)}, bf16[512,1792]{1,0:T(8,128)(2,1)}, bf16[2,1,2,128,1792]{4,3...) conditional(s32[]{:T(128)} %convert_element_type.524, ...), branch_computations={%region_35.36_spmd, %region_36.37_spmd} | conditional | flops 4715577344 | bytes 59113572 | solution.py:713
  612.4 9.2 %add_convert_fusion.2 = bf16[1024,4480]{1,0:T(8,128)(2,1)S(1)} fusion(bf16[1024,4480]{1,0:T(8,128)(2,1)} %get-tuple-element.400, bf16[512,1024]{1,0:T(8,128)(2,1)} %get-tuple-element.398, bf16[512,4480]{1,0:T(8,128)(2,1)} %get-tuple-element.399), kind=kOutput, calls=%fused_computation.87 | convolution fusion | flops 4711383040 | bytes 23986176 | tf_op jit(solution)/shard_map/cond/branch_1_fun/dot_general | solution.py:34
  641.5 46.7 %collective-permute-done.15 = bf16[128,2048]{1,0:T(8,128)(2,1)} collective-permute-done((bf16[128,2048]{1,0:T(8,128)(2,1)}, bf16[128,2048]{1,0:T(8,128)(2,1)}, u32[]{:S(2)}, u32[]{:S(2)}) %collective-permute-start.15) | collective-permute-done | bytes 524320 | tf_op jit(solution)/shard_map/ppermute | solution.py:574
  688.2 10.8 %collective-permute-done.16 = bf16[128,2048]{1,0:T(8,128)(2,1)} collective-permute-done((bf16[128,2048]{1,0:T(8,128)(2,1)}, bf16[128,2048]{1,0:T(8,128)(2,1)}, u32[]{:S(2)}, u32[]{:S(2)}) %collective-permute-start.16) | collective-permute-done | bytes 524320 | tf_op jit(solution)/shard_map/ppermute | solution.py:574
  701.2 11.7 %conditional.28 = (bf16[256,2688]{1,0:T(8,128)(2,1)}, bf16[1,1,2,128,2688]{4,3,2,1,0:T(8,128)(2,1)}, bf16[256,1792]{1,0:T(8,128)(2,1)S(1)}, bf16[1,1,2,128,1792]...) conditional(s32[]{:T(128)} %convert_element_type.526, () %tuple.202, ...), branch_computations={%region_43.44_spmd, %region_44.45_spmd} | conditional | flops 280788992 | bytes 37093480 | solution.py:713
  725.1 29.1 %collective-permute-done.23 = f32[16,2048]{1,0:T(8,128)} collective-permute-done((f32[16,2048]{1,0:T(8,128)S(1)}, f32[16,2048]{1,0:T(8,128)}, u32[]{:S(2)}, u32[]{:S(2)}) %collective-permute-start.23) | collective-permute-done | bytes 131104 | tf_op jit(solution)/shard_map/ppermute | solution.py:574
  754.3 5.7 collective-permute-done.21
  761.1 6.7 conditional.29
  770.8 24.0 %collective-permute-done.24 = f32[16,2048]{1,0:T(8,128)S(1)} collective-permute-done((f32[16,2048]{1,0:T(8,128)S(1)}, f32[16,2048]{1,0:T(8,128)S(1)}, u32[]{:S(2)}, u32[]{:S(2)}) %collective-permute-start.24) | collective-permute-done | bytes 131104 | tf_op jit(solution)/shard_map/ppermute | solution.py:574
  794.7 6.9 conditional.30
  802.8 19.8 %collective-permute-done.27 = f32[16,2048]{1,0:T(8,128)S(1)} collective-permute-done((f32[16,2048]{1,0:T(8,128)}, f32[16,2048]{1,0:T(8,128)S(1)}, u32[]{:S(2)}, u32[]{:S(2)}) %collective-permute-start.27) | collective-permute-done | bytes 131104 | tf_op jit(solution)/shard_map/ppermute | solution.py:574
  822.7 8.3 conditional.31
  (394 shorter events, 192.9 us)
Async XLA Ops:
  7.2 177.3 %all-gather.5.cloned.1.call-start = ((), (), s32[]{:S(2)}) async-start(), calls=%async_computation.7 | async-start | bytes 28409856 | tf_op jit(solution)/shard_map/all_gather | solution.py:591
  11.6 319.8 %all-gather.3.cloned.1.call-start = ((), (), s32[]{:S(2)}) async-start(), calls=%async_computation.6 | async-start | bytes 26738688 | tf_op jit(solution)/shard_map/all_gather | solution.py:591
  19.6 92.2 %copy-start.76 = (s32[256]{0:T(256)}, s32[256]{0:T(256)S(1)}, u32[]{:S(2)}) copy-start(s32[256]{0:T(256)S(1)} %get-tuple-element.1016) | copy-start | bytes 3076
  21.1 47.3 %all-to-all-start.1 = ((bf16[16,16,2048]{2,1,0:T(8,128)(2,1)}), bf16[16,16,2048]{2,1,0:T(8,128)(2,1)S(1)}, u32[]{:S(2)}, u32[]{:S(2)}) async-start(bf16[16,16,2048]{2,1,0:T(8,128)(2,1)} %bitcast.84), calls=%async_computation.1 | async-start | bytes 2097152 | tf_op jit(solution)/shard_map/all_to_all | solution.py:622
  28.7 43.6 %copy-start.81 = (f32[24]{0:T(128)S(1)}, f32[24]{0:T(128)}, u32[]{:S(2)}) copy-start(f32[24]{0:T(128)} %param.80) | copy-start | bytes 292
  68.3 43.5 %all-to-all-start = ((bf16[16,16,2048]{2,1,0:T(8,128)(2,1)}), bf16[16,16,2048]{2,1,0:T(8,128)(2,1)S(1)}, u32[]{:S(2)}, u32[]{:S(2)}) async-start(bf16[16,16,2048]{2,1,0:T(8,128)(2,1)} %bitcast.75), calls=%async_computation | async-start | bytes 2097152 | tf_op jit(solution)/shard_map/all_to_all | solution.py:622
  72.0 479.4 %reduce-scatter.3.cloned.1.call-start = ((), (), s32[]{:S(2)}) async-start(), calls=%async_computation.8 | async-start | bytes 8912896 | tf_op jit(solution)/shard_map/reduce_scatter | solution.py:796
  72.3 170.2 %copy-start.61 = (f32[2,1,256]{2,1,0:T(1,128)}, f32[2,1,256]{2,1,0:T(1,128)S(1)}, u32[]{:S(2)}) copy-start(f32[2,1,256]{2,1,0:T(1,128)S(1)} %convert_element_type.501.seg_row_ref) | copy-start | bytes 6148
  72.5 139.2 %copy-start.59 = (f32[1,1536]{1,0:T(1,128)}, f32[1,1536]{1,0:T(1,128)S(1)}, u32[]{:S(2)}) copy-start(f32[1,1536]{1,0:T(1,128)S(1)} %broadcast_in_dim_reshape.2.skip_ref) | copy-start | bytes 18436
  72.5 170.0 %copy-start.16 = (f32[512,8]{1,0:T(8,128)}, f32[512,8]{1,0:T(8,128)S(1)}, u32[]{:S(2)}) copy-start(f32[512,8]{1,0:T(8,128)S(1)} %pad.21.columns_ref) | copy-start | bytes 49156
  74.1 39.8 %copy-start.84 = (f32[24]{0:T(128)S(1)}, f32[24]{0:T(128)}, u32[]{:S(2)}) copy-start(f32[24]{0:T(128)} %param.79) | copy-start | bytes 292
  74.1 39.8 %collective-permute-start.1 = (bf16[256,2048]{1,0:T(8,128)(2,1)S(1)}, bf16[256,2048]{1,0:T(8,128)(2,1)S(1)}, u32[]{:S(2)}, u32[]{:S(2)}) collective-permute-start(bf16[256,2048]{1,0:T(8,128)(2,1)S(1)} %convolution_convert_fusion.7), channel_id=1, source_target_pairs={{0,1},{1,0},{2,3},{3,2},{4,5},{5,4},{6,7},{7,6},{8,9},{9,8},{10,11... | collective-permute-start | bytes 3145736 | tf_op jit(solution)/shard_map/ppermute | solution.py:571
  112.3 24.7 %collective-permute-start = (bf16[256,2048]{1,0:T(8,128)(2,1)S(1)}, bf16[256,2048]{1,0:T(8,128)(2,1)S(1)}, u32[]{:S(2)}, u32[]{:S(2)}) collective-permute-start(bf16[256,2048]{1,0:T(8,128)(2,1)S(1)} %convolution_convert_fusion.9), channel_id=1, source_target_pairs={{0,1},{1,0},{2,3},{3,2},{4,5},{5,4},{6,7},{7,6},{8,9},{9,8},{10,11... | collective-permute-start | bytes 3145736 | tf_op jit(solution)/shard_map/ppermute | solution.py:571
  113.9 73.0 %copy-start.78 = (f32[24]{0:T(128)}, f32[24]{0:T(128)S(1)}, u32[]{:S(2)}) copy-start(f32[24]{0:T(128)S(1)} %exponential_negate_fusion) | copy-start | bytes 292
  142.2 42.4 %copy-start.3 = (bf16[512,2048]{1,0:T(8,128)(2,1)S(1)}, bf16[512,2048]{1,0:T(8,128)(2,1)}, u32[]{:S(2)}) copy-start(bf16[512,2048]{1,0:T(8,128)(2,1)} %multiply_convert_fusion.4.first_ref.second_ref) | copy-start | bytes 6291460
  142.2 42.4 %copy-start.80 = (f32[24]{0:T(128)S(1)}, f32[24]{0:T(128)}, u32[]{:S(2)}) copy-start(f32[24]{0:T(128)} %param.78) | copy-start | bytes 292
  190.8 20.9 %copy-start.50 = (f32[2,12,2,256]{3,2,1,0:T(2,128)}, f32[2,12,2,256]{3,2,1,0:T(2,128)S(1)}, u32[]{:S(2)}) copy-start(f32[2,12,2,256]{3,2,1,0:T(2,128)S(1)} %reshape.700.step_ref) | copy-start | bytes 147460
  233.8 16.9 %collective-permute-start.2 = (f32[512]{0:T(512)S(1)}, f32[512]{0:T(512)S(1)}, u32[]{:S(2)}, u32[]{:S(2)}) collective-permute-start(f32[512]{0:T(512)S(1)} %reduce_sum.175), channel_id=1, source_target_pairs={{0,1},{1,0},{2,3},{3,2},{4,5},{5,4},{6,7},{7,6},{8,9},{9,8},{10,11... | collective-permute-start | bytes 6152 | tf_op jit(solution)/shard_map/ppermute | solution.py:571
  250.7 22.2 %copy-start.44 = (bf16[512,512]{1,0:T(8,128)(2,1)}, bf16[512,512]{1,0:T(8,128)(2,1)S(1)}, u32[]{:S(2)}) copy-start(bf16[512,512]{1,0:T(8,128)(2,1)S(1)} %get-tuple-element.597) | copy-start | bytes 1572868
  275.9 47.7 %collective-permute-start.3 = (bf16[512,2048]{1,0:T(8,128)(2,1)S(1)}, bf16[512,2048]{1,0:T(8,128)(2,1)}, u32[]{:S(2)}, u32[]{:S(2)}) collective-permute-start(bf16[512,2048]{1,0:T(8,128)(2,1)S(1)} %add_convert_fusion.6), channel_id=1, source_target_pairs={{0,1},{1,0},{2,3},{3,2},{4,5},{5,4},{6,7},{7,6},{8,9},{9,8},{10,11... | collective-permute-start | bytes 6291464 | tf_op jit(solution)/shard_map/ppermute | solution.py:571
  378.2 33.3 %collective-permute-start.4 = (bf16[256,2048]{1,0:T(8,128)(2,1)S(1)}, bf16[256,2048]{1,0:T(8,128)(2,1)}, u32[]{:S(2)}, u32[]{:S(2)}) collective-permute-start(bf16[256,2048]{1,0:T(8,128)(2,1)S(1)} %get-tuple-element.606), channel_id=1, source_target_pairs={{0,1},{1,0},{2,3},{3,2},{4,5},{5,4},{6,7},{7,6},{8,9},{9,8},{10,11... | collective-permute-start | bytes 3145736 | tf_op jit(solution)/shard_map/ppermute | solution.py:571
  392.4 33.3 %collective-permute-start.5 = (bf16[256,2048]{1,0:T(8,128)(2,1)}, bf16[256,2048]{1,0:T(8,128)(2,1)}, u32[]{:S(2)}, u32[]{:S(2)}) collective-permute-start(bf16[256,2048]{1,0:T(8,128)(2,1)} %get-tuple-element.612), channel_id=1, source_target_pairs={{0,1},{1,0},{2,3},{3,2},{4,5},{5,4},{6,7},{7,6},{8,9},{9,8},{10,11... | collective-permute-start | bytes 3145736 | tf_op jit(solution)/shard_map/ppermute | solution.py:571
  411.0 14.8 %collective-permute-start.6 = (bf16[1024,2048]{1,0:T(8,128)(2,1)}, bf16[1024,2048]{1,0:T(8,128)(2,1)}, u32[]{:S(2)}, u32[]{:S(2)}) collective-permute-start(bf16[1024,2048]{1,0:T(8,128)(2,1)} %get-tuple-element.613), channel_id=1, source_target_pairs={{0,2},{2,0},{4,6},{6,4},{8,10},{10,8},{12,14},{14,12},{16,18},{18,... | collective-permute-start | bytes 12582920 | tf_op jit(solution)/shard_map/ppermute | solution.py:574
  411.0 14.8 %collective-permute-start.7 = (bf16[1024,2048]{1,0:T(8,128)(2,1)}, bf16[1024,2048]{1,0:T(8,128)(2,1)}, u32[]{:S(2)}, u32[]{:S(2)}) collective-permute-start(bf16[1024,2048]{1,0:T(8,128)(2,1)} %get-tuple-element.614), channel_id=1, source_target_pairs={{0,2},{2,0},{4,6},{6,4},{8,10},{10,8},{12,14},{14,12},{16,18},{18,... | collective-permute-start | bytes 12582920 | tf_op jit(solution)/shard_map/ppermute | solution.py:574
  421.3 63.2 %collective-permute-start.8 = (bf16[256,2048]{1,0:T(8,128)(2,1)}, bf16[256,2048]{1,0:T(8,128)(2,1)}, u32[]{:S(2)}, u32[]{:S(2)}) collective-permute-start(bf16[256,2048]{1,0:T(8,128)(2,1)} %get-tuple-element.628), channel_id=1, source_target_pairs={{0,1},{1,0},{2,3},{3,2},{4,5},{5,4},{6,7},{7,6},{8,9},{9,8},{10,11... | collective-permute-start | bytes 3145736 | tf_op jit(solution)/shard_map/ppermute | solution.py:571
  425.7 28.2 %copy-start.77 = (s32[256]{0:T(256)S(1)}, s32[256]{0:T(256)}, u32[]{:S(2)}) copy-start(s32[256]{0:T(256)} %copy-done.76) | copy-start | bytes 3076
  425.7 28.3 %copy-start.17 = (f32[512,8]{1,0:T(8,128)S(1)}, f32[512,8]{1,0:T(8,128)}, u32[]{:S(2)}) copy-start(f32[512,8]{1,0:T(8,128)} %copy-done.16) | copy-start | bytes 49156
  425.8 28.3 %copy-start.26 = (f32[512,128]{1,0:T(8,128)S(1)}, f32[512,128]{1,0:T(8,128)}, u32[]{:S(2)}) copy-start(f32[512,128]{1,0:T(8,128)} %get-tuple-element.1020.cosine_ref) | copy-start | bytes 786436
  425.8 28.3 %copy-start.62 = (f32[2,1,256]{2,1,0:T(1,128)S(1)}, f32[2,1,256]{2,1,0:T(1,128)}, u32[]{:S(2)}) copy-start(f32[2,1,256]{2,1,0:T(1,128)} %copy-done.61) | copy-start | bytes 6148
  425.8 28.3 %copy-start.68 = (f32[1536]{0:T(1024)S(1)}, f32[1536]{0:T(1024)}, u32[]{:S(2)}) copy-start(f32[1536]{0:T(1024)} %param.77) | copy-start | bytes 18436
  442.2 109.2 %collective-permute-start.10 = (bf16[512,2048]{1,0:T(8,128)(2,1)}, bf16[512,2048]{1,0:T(8,128)(2,1)}, u32[]{:S(2)}, u32[]{:S(2)}) collective-permute-start(bf16[512,2048]{1,0:T(8,128)(2,1)} %get-tuple-element.640), channel_id=1, source_target_pairs={{0,4},{2,6},{4,0},{6,2},{8,12},{10,14},{12,8},{14,10},{16,20},{18,... | collective-permute-start | bytes 6291464 | tf_op jit(solution)/shard_map/ppermute | solution.py:574
  443.1 108.2 %collective-permute-start.11 = (bf16[512,2048]{1,0:T(8,128)(2,1)}, bf16[512,2048]{1,0:T(8,128)(2,1)}, u32[]{:S(2)}, u32[]{:S(2)}) collective-permute-start(bf16[512,2048]{1,0:T(8,128)(2,1)} %get-tuple-element.642), channel_id=1, source_target_pairs={{0,8},{2,10},{4,12},{6,14},{8,0},{10,2},{12,4},{14,6},{16,24},{18,... | collective-permute-start | bytes 6291464 | tf_op jit(solution)/shard_map/ppermute | solution.py:574
  454.0 30.5 %copy-start.34 = (bf16[256,256]{1,0:T(8,128)(2,1)}, bf16[256,256]{1,0:T(8,128)(2,1)S(1)}, u32[]{:S(2)}) copy-start(bf16[256,256]{1,0:T(8,128)(2,1)S(1)} %fusion.81) | copy-start | bytes 393220
  454.1 30.4 %copy-start.8 = (bf16[512,2048]{1,0:T(8,128)(2,1)S(1)}, bf16[512,2048]{1,0:T(8,128)(2,1)}, u32[]{:S(2)}) copy-start(bf16[512,2048]{1,0:T(8,128)(2,1)} %copy-done.7) | copy-start | bytes 6291460
  498.9 52.4 %all-to-all-start.2 = ((bf16[16,16,2048]{2,1,0:T(8,128)(2,1)}), bf16[16,16,2048]{2,1,0:T(8,128)(2,1)S(1)}, u32[]{:S(2)}, u32[]{:S(2)}) async-start(bf16[16,16,2048]{2,1,0:T(8,128)(2,1)} %bitcast.100), calls=%async_computation.3 | async-start | bytes 2097152 | tf_op jit(solution)/shard_map/all_to_all | solution.py:622
  502.9 185.3 %reduce-scatter.5.cloned.1.call-start = ((), (), s32[]{:S(2)}) async-start(), calls=%async_computation.9 | async-start | bytes 8912896 | tf_op jit(solution)/shard_map/reduce_scatter | solution.py:865
  503.5 4.0 collective-permute-start.9
  505.0 46.4 %copy-start.32 = (bf16[256,256]{1,0:T(8,128)(2,1)}, bf16[256,256]{1,0:T(8,128)(2,1)S(1)}, u32[]{:S(2)}) copy-start(bf16[256,256]{1,0:T(8,128)(2,1)S(1)} %fusion.80) | copy-start | bytes 393220
  551.4 22.8 %copy-start.71 = (f32[2048]{0:T(1024)S(1)}, f32[2048]{0:T(1024)}, u32[]{:S(2)}) copy-start(f32[2048]{0:T(1024)} %param.73) | copy-start | bytes 24580
  551.4 22.8 %copy-start.73 = (f32[2,2,128]{2,1,0:T(2,128)S(1)}, f32[2,2,128]{2,1,0:T(2,128)}, u32[]{:S(2)}) copy-start(f32[2,2,128]{2,1,0:T(2,128)} %copy-done.72) | copy-start | bytes 6148
  570.8 41.5 %collective-permute-start.12 = (bf16[1024,4480]{1,0:T(8,128)(2,1)}, bf16[1024,4480]{1,0:T(8,128)(2,1)}, u32[]{:S(2)}, u32[]{:S(2)}) collective-permute-start(bf16[1024,4480]{1,0:T(8,128)(2,1)} %get-tuple-element.649), channel_id=1, source_target_pairs={{0,2},{2,0},{4,6},{6,4},{8,10},{10,8},{12,14},{14,12},{16,18},{18,... | collective-permute-start | bytes 27525128 | tf_op jit(solution)/shard_map/ppermute | solution.py:574
  570.8 41.5 %collective-permute-start.13 = (bf16[256,2048]{1,0:T(8,128)(2,1)}, bf16[256,2048]{1,0:T(8,128)(2,1)}, u32[]{:S(2)}, u32[]{:S(2)}) collective-permute-start(bf16[256,2048]{1,0:T(8,128)(2,1)} %get-tuple-element.652), channel_id=1, source_target_pairs={{0,8},{2,10},{4,12},{6,14},{8,0},{10,2},{12,4},{14,6},{16,24},{18,... | collective-permute-start | bytes 3145736 | tf_op jit(solution)/shard_map/ppermute | solution.py:574
  572.7 39.6 %collective-permute-start.14 = (bf16[256,2048]{1,0:T(8,128)(2,1)}, bf16[256,2048]{1,0:T(8,128)(2,1)}, u32[]{:S(2)}, u32[]{:S(2)}) collective-permute-start(bf16[256,2048]{1,0:T(8,128)(2,1)} %get-tuple-element.654), channel_id=1, source_target_pairs={{0,4},{2,6},{4,0},{6,2},{8,12},{10,14},{12,8},{14,10},{16,20},{18,... | collective-permute-start | bytes 3145736 | tf_op jit(solution)/shard_map/ppermute | solution.py:574
  612.4 25.8 %copy-start.79 = (f32[24]{0:T(128)S(1)}, f32[24]{0:T(128)}, u32[]{:S(2)}) copy-start(f32[24]{0:T(128)} %copy-done.78) | copy-start | bytes 292
  631.7 69.5 %collective-permute-start.17 = (bf16[512,2688]{1,0:T(8,128)(2,1)}, bf16[512,2688]{1,0:T(8,128)(2,1)}, u32[]{:S(2)}, u32[]{:S(2)}) collective-permute-start(bf16[512,2688]{1,0:T(8,128)(2,1)} %get-tuple-element.669), channel_id=1, source_target_pairs={{0,4},{2,6},{4,0},{6,2},{8,12},{10,14},{12,8},{14,10},{16,20},{18,... | collective-permute-start | bytes 8257544 | tf_op jit(solution)/shard_map/ppermute | solution.py:574
  633.2 68.0 %collective-permute-start.18 = (bf16[512,1792]{1,0:T(8,128)(2,1)}, bf16[512,1792]{1,0:T(8,128)(2,1)}, u32[]{:S(2)}, u32[]{:S(2)}) collective-permute-start(bf16[512,1792]{1,0:T(8,128)(2,1)} %get-tuple-element.671), channel_id=1, source_target_pairs={{0,8},{2,10},{4,12},{6,14},{8,0},{10,2},{12,4},{14,6},{16,24},{18,... | collective-permute-start | bytes 5505032 | tf_op jit(solution)/shard_map/ppermute | solution.py:574
  633.7 65.3 %collective-permute-start.20 = (bf16[256,2048]{1,0:T(8,128)(2,1)}, bf16[256,2048]{1,0:T(8,128)(2,1)S(1)}, u32[]{:S(2)}, u32[]{:S(2)}) collective-permute-start(bf16[256,2048]{1,0:T(8,128)(2,1)} %get-tuple-element.674), channel_id=1, source_target_pairs={{0,1},{1,0},{2,3},{3,2},{4,5},{5,4},{6,7},{7,6},{8,9},{9,8},{10,11... | collective-permute-start | bytes 3145736 | tf_op jit(solution)/shard_map/ppermute | solution.py:571
  635.2 53.0 %collective-permute-start.15 = (bf16[128,2048]{1,0:T(8,128)(2,1)}, bf16[128,2048]{1,0:T(8,128)(2,1)}, u32[]{:S(2)}, u32[]{:S(2)}) collective-permute-start(bf16[128,2048]{1,0:T(8,128)(2,1)} %get-tuple-element.664), channel_id=1, source_target_pairs={{0,16},{2,18},{4,20},{6,22},{8,24},{10,26},{12,28},{14,30},{16,0},... | collective-permute-start | bytes 1572872 | tf_op jit(solution)/shard_map/ppermute | solution.py:574
  637.6 61.4 %collective-permute-start.16 = (bf16[128,2048]{1,0:T(8,128)(2,1)}, bf16[128,2048]{1,0:T(8,128)(2,1)}, u32[]{:S(2)}, u32[]{:S(2)}) collective-permute-start(bf16[128,2048]{1,0:T(8,128)(2,1)} %get-tuple-element.665), channel_id=1, source_target_pairs={{0,16},{2,18},{4,20},{6,22},{8,24},{10,26},{12,28},{14,30},{16,0},... | collective-permute-start | bytes 1572872 | tf_op jit(solution)/shard_map/ppermute | solution.py:574
  688.2 10.9 %collective-permute-start.19 = (f32[16,2048]{1,0:T(8,128)S(1)}, f32[16,2048]{1,0:T(8,128)S(1)}, u32[]{:S(2)}, u32[]{:S(2)}) collective-permute-start(f32[16,2048]{1,0:T(8,128)S(1)} %get-tuple-element.1168), channel_id=1, source_target_pairs={{0,2},{2,0},{4,6},{6,4},{8,10},{10,8},{12,14},{14,12},{16,18},{18,... | collective-permute-start | bytes 393224 | tf_op jit(solution)/shard_map/ppermute | solution.py:574
  714.5 45.5 %collective-permute-start.21 = (bf16[256,2688]{1,0:T(8,128)(2,1)}, bf16[256,2688]{1,0:T(8,128)(2,1)S(1)}, u32[]{:S(2)}, u32[]{:S(2)}) collective-permute-start(bf16[256,2688]{1,0:T(8,128)(2,1)} %get-tuple-element.679), channel_id=1, source_target_pairs={{0,8},{2,10},{4,12},{6,14},{8,0},{10,2},{12,4},{14,6},{16,24},{18,... | collective-permute-start | bytes 4128776 | tf_op jit(solution)/shard_map/ppermute | solution.py:574
  719.2 103.4 %all-to-all-start.3 = ((bf16[16,16,2048]{2,1,0:T(8,128)(2,1)}), bf16[16,16,2048]{2,1,0:T(8,128)(2,1)S(1)}, u32[]{:S(2)}, u32[]{:S(2)}) async-start(bf16[16,16,2048]{2,1,0:T(8,128)(2,1)} %bitcast.101), calls=%async_computation.5 | async-start | bytes 2097152 | tf_op jit(solution)/shard_map/all_to_all | solution.py:622
  723.0 31.2 %collective-permute-start.22 = (bf16[256,1792]{1,0:T(8,128)(2,1)S(1)}, bf16[256,1792]{1,0:T(8,128)(2,1)}, u32[]{:S(2)}, u32[]{:S(2)}) collective-permute-start(bf16[256,1792]{1,0:T(8,128)(2,1)S(1)} %copy-done.41), channel_id=1, source_target_pairs={{0,4},{2,6},{4,0},{6,2},{8,12},{10,14},{12,8},{14,10},{16,20},{18,... | collective-permute-start | bytes 2752520 | tf_op jit(solution)/shard_map/ppermute | solution.py:574
  724.9 29.3 %collective-permute-start.23 = (f32[16,2048]{1,0:T(8,128)S(1)}, f32[16,2048]{1,0:T(8,128)}, u32[]{:S(2)}, u32[]{:S(2)}) collective-permute-start(f32[16,2048]{1,0:T(8,128)S(1)} %copy-done.47), channel_id=1, source_target_pairs={{0,4},{2,6},{4,0},{6,2},{8,12},{10,14},{12,8},{14,10},{16,20},{18,... | collective-permute-start | bytes 393224 | tf_op jit(solution)/shard_map/ppermute | solution.py:574
  761.1 33.6 %copy-start.28 = (bf16[128,2048]{1,0:T(8,128)(2,1)S(1)}, bf16[128,2048]{1,0:T(8,128)(2,1)}, u32[]{:S(2)}) copy-start(bf16[128,2048]{1,0:T(8,128)(2,1)} %reduce-scatter.5.cloned.1.call-done) | copy-start | bytes 1572868
  767.7 27.0 %copy-start.48 = (f32[16,2048]{1,0:T(8,128)}, f32[16,2048]{1,0:T(8,128)S(1)}, u32[]{:S(2)}) copy-start(f32[16,2048]{1,0:T(8,128)S(1)} %get-tuple-element.690) | copy-start | bytes 393220
  767.8 54.9 %collective-permute-start.25 = (bf16[128,2688]{1,0:T(8,128)(2,1)}, bf16[128,2688]{1,0:T(8,128)(2,1)}, u32[]{:S(2)}, u32[]{:S(2)}) collective-permute-start(bf16[128,2688]{1,0:T(8,128)(2,1)} %get-tuple-element.695), channel_id=1, source_target_pairs={{0,16},{2,18},{4,20},{6,22},{8,24},{10,26},{12,28},{14,30},{16,0},... | collective-permute-start | bytes 2064392 | tf_op jit(solution)/shard_map/ppermute | solution.py:574
  767.8 54.8 %collective-permute-start.26 = (bf16[128,1792]{1,0:T(8,128)(2,1)}, bf16[128,1792]{1,0:T(8,128)(2,1)}, u32[]{:S(2)}, u32[]{:S(2)}) collective-permute-start(bf16[128,1792]{1,0:T(8,128)(2,1)} %get-tuple-element.697), channel_id=1, source_target_pairs={{0,16},{2,18},{4,20},{6,22},{8,24},{10,26},{12,28},{14,30},{16,0},... | collective-permute-start | bytes 1376264 | tf_op jit(solution)/shard_map/ppermute | solution.py:574
  770.8 24.0 %collective-permute-start.24 = (f32[16,2048]{1,0:T(8,128)S(1)}, f32[16,2048]{1,0:T(8,128)S(1)}, u32[]{:S(2)}, u32[]{:S(2)}) collective-permute-start(f32[16,2048]{1,0:T(8,128)S(1)} %get-tuple-element.690), channel_id=1, source_target_pairs={{0,8},{2,10},{4,12},{6,14},{8,0},{10,2},{12,4},{14,6},{16,24},{18,... | collective-permute-start | bytes 393224 | tf_op jit(solution)/shard_map/ppermute | solution.py:574
  794.7 27.9 %copy-start.33 = (bf16[256,256]{1,0:T(8,128)(2,1)S(1)}, bf16[256,256]{1,0:T(8,128)(2,1)}, u32[]{:S(2)}) copy-start(bf16[256,256]{1,0:T(8,128)(2,1)} %copy-done.32) | copy-start | bytes 393220
  801.7 21.0 %copy-start.36 = (f32[128,2048]{1,0:T(8,128)}, f32[128,2048]{1,0:T(8,128)S(1)}, u32[]{:S(2)}) copy-start(f32[128,2048]{1,0:T(8,128)S(1)} %get-tuple-element.911) | copy-start | bytes 3145732
  801.7 21.0 %collective-permute-start.27 = (f32[16,2048]{1,0:T(8,128)}, f32[16,2048]{1,0:T(8,128)S(1)}, u32[]{:S(2)}, u32[]{:S(2)}) collective-permute-start(f32[16,2048]{1,0:T(8,128)} %get-tuple-element.699), channel_id=1, source_target_pairs={{0,16},{2,18},{4,20},{6,22},{8,24},{10,26},{12,28},{14,30},{16,0},... | collective-permute-start | bytes 393224 | tf_op jit(solution)/shard_map/ppermute | solution.py:574
  831.0 6.4 collective-permute-start.29
  832.5 9.6 %collective-permute-start.28 = (f32[64,512]{1,0:T(8,128)}, f32[64,512]{1,0:T(8,128)S(1)}, u32[]{:S(2)}, u32[]{:S(2)}) collective-permute-start(f32[64,512]{1,0:T(8,128)} %get-tuple-element.710), channel_id=1, source_target_pairs={{0,1},{1,0},{2,3},{3,2},{4,5},{5,4},{6,7},{7,6},{8,9},{9,8},{10,11... | collective-permute-start | bytes 393224 | tf_op jit(solution)/shard_map/ppermute | solution.py:571
  (60 other events, 252.1 us)
Sparse Core Ops, SparseCore 0:
  11.7 172.8 all-gather.4
  186.1 138.4 all-gather.2
  377.3 139.0 reduce-scatter.2
  520.4 143.9 reduce-scatter.4

commit v12 on v11

--- a/solution.py
+++ b/solution.py
@@ -392,23 +392,32 @@
     lanes = lax.broadcasted_iota(jnp.int32, cols.shape, 1)
     zero = jnp.zeros_like(grad_low)
     grad_cols = []
+    cut = rows // 2
     for head in range(2):
-        step_row = step_ref[0, pair, head : head + 1, :]
-        inner = inner_ref[...]
-        decay, mixing = mixing_block(
-            inner, mask_ref[...], run_col_ref[0, pair, :, head : head + 1], run_row_ref[0, pair, head : head + 1, :], step_row
-        )
-        grad_cols.append(
-            lax.dot_general(mixing, grad_low, (((0,), (0,)), ((), ())), preferred_element_type=f32)
-        )
         grad_head = jnp.where((lanes < SHD) == (head == 0), grad_low, zero)
-        grad_decay = lax.dot_general(
-            grad_head, cols_low, (((1,), (1,)), ((), ())), preferred_element_type=f32
-        ) * decay
-        stepped = grad_decay * step_row
-        grad_inner_ref[...] += stepped
-        direct_ref[pl.ds(2 * pair + head, 1), :] = jnp.sum(grad_decay * inner, axis=0, keepdims=True)
-        along = jnp.sum(stepped * inner, axis=1, keepdims=True)
+        partial_cols, directs, alongs = [], [], []
+        for start, stop in ((0, cut), (cut, rows)):
+            step_row = step_ref[0, pair, head : head + 1, :stop]
+            inner = inner_ref[start:stop, :stop]
+            decay, mixing = mixing_block(
+                inner, mask_ref[start:stop, :stop], run_col_ref[0, pair, start:stop, head : head + 1],
+                run_row_ref[0, pair, head : head + 1, :stop], step_row,
+            )
+            partial_cols.append(
+                lax.dot_general(mixing, grad_low[start:stop], (((0,), (0,)), ((), ())), preferred_element_type=f32)
+            )
+            grad_decay = lax.dot_general(
+                grad_head[start:stop], cols_low[:stop], (((1,), (1,)), ((), ())), preferred_element_type=f32
+            ) * decay
+            stepped = grad_decay * step_row
+            grad_inner_ref[start:stop, :stop] += stepped
+            directs.append(jnp.sum(grad_decay * inner, axis=0, keepdims=True))
+            alongs.append(jnp.sum(stepped * inner, axis=1, keepdims=True))
+        grad_cols.append(jnp.concatenate([partial_cols[0] + partial_cols[1][:cut], partial_cols[1][cut:]], axis=0))
+        direct_ref[pl.ds(2 * pair + head, 1), :] = jnp.concatenate(
+            [directs[0] + directs[1][:, :cut], directs[1][:, cut:]], axis=1
+        )
+        along = jnp.concatenate(alongs, axis=0)
         along_ref[...] = jnp.where(lanes == 2 * pair + head, along, along_ref[...])
     grad_cols = jnp.where(lanes < SHD, grad_cols[0], grad_cols[1]) + skip_ref[...] * grad_out
     grad_sum = grad_cols * (sig * (1.0 + summed * (1.0 - sig)))
@@ -878,10 +887,8 @@
     column_sums, state_sums, head_sums, first_right = unit(state_space_backward)
 
     total_fdown_low = [sum_fdown]
-    order[0], total_fdown_low = lax.optimization_barrier((order[0], total_fdown_low))
-    send_first, steps, block_out = unit(
-        lambda: (core_send(normed_left, first_right), [red.step() for red in feeds], deal_take(out_moved))
-    )
+    order[0], total_fdown_low, out_moved = lax.optimization_barrier((order[0], total_fdown_low, out_moved))
+    send_first, steps = unit(lambda: (core_send(normed_left, first_right), [red.step() for red in feeds]))
     settle(feeds, steps)
     first_came = other_group(send_first, 1)
 
@@ -955,9 +962,10 @@
         bits += 1
         if in_moved is None:
             in_moved = exchange(sent)
-    totals, flat = unit(
+    totals, block_out, flat = unit(
         lambda: (
             [red.last() for red in feeds] + [sum_branch.astype(f32), total_fdown_low[0].astype(f32)],
+            deal_take(out_moved),
             flat + flat_moved if flat_moved is not None else flat,
         )
     )

time: 854 us -> 854 us (level)
  transfers between devices with their start and end apart: 38 -> 38, of which waited for: 16 -> 17; matrix products, arithmetic and copies ran while one was open for 31% -> 31% of each run, Pallas kernels for 10% -> 11%
where the time goes in v12:
time: 854 us; the launch traced here: 849 us
  waiting for transfers between devices  333 us (39%)
  matrix products  209 us (24%)
  Pallas kernels  94.3 us (11%)
  other arithmetic  74.8 us (9%)
  local copies, waits for them, and re-layouts  61.3 us (7%)
  starting transfers between devices  58.9 us (7%)
  between operations  15.7 us (2%)
    ppermute x19, waiting for transfers between devices, other_group(): return lax.ppermute(values, 'dp', [(i, i ^ bits) for i in range(groups)])  147 us
    ppermute x11, waiting for transfers between devices, other_lane(): return lax.ppermute(values, 'tensor', swap_lane)  77 us
    all_to_all x4, waiting for transfers between devices, exchange(): lax.all_to_all(buffer.reshape(groups, micro * per, width), 'dp', split_ax...  73.3 us
    dot_general x8, matrix products, project_back(): lax.dot_general(left, right, (((1,), (1,)), ((), ())), preferred_element_...  71.7 us
    dot_general x15, matrix products, project(): return jnp.dot(left, right, preferred_element_type=f32)  69 us
    dot_general x12, matrix products, outer_sum(): lax.dot_general(left, right, (((0,), (0,)), ((), ())), preferred_element_...  68.1 us
    pallas_call x1, Pallas kernels, state_backward(): pl.pallas_call(functools.partial(state_backward_kernel, query_cols=query_...  40.9 us
    all_gather x2, waiting for transfers between devices, local(): lax.all_gather(join_columns(list(group_weights.values())), 'dp', axis=0,...  35.7 us
  transfers between devices with their start and end apart: 38, of which 17 were waited for; matrix products, arithmetic and copies ran while one was open for 31% of the time, Pallas kernels for 11%

profile of v12, /device:TPU:0, one launch (start us, length us, event | category | flops | bytes accessed | tf_op | source)
XLA Modules:
  0.0 849.2 jit_solution(4499354341313954026)
XLA Ops:
  14.4 4.9 select_reduce_fusion
  21.1 7.4 all-to-all-start.1
  30.2 38.2 %all-to-all-done.1 = bf16[16,16,2048]{2,1,0:T(8,128)(2,1)S(1)} async-done(((bf16[16,16,2048]{2,1,0:T(8,128)(2,1)}), bf16[16,16,2048]{2,1,0:T(8,128)(2,1)S(1)}, u32[]{:S(2)}, u32[]{:S(2)}) %all-to-all-start.1) | async-done | bytes 1048608 | tf_op jit(solution)/shard_map/all_to_all | solution.py:631
  76.7 35.1 %all-to-all-done = bf16[16,16,2048]{2,1,0:T(8,128)(2,1)S(1)} async-done(((bf16[16,16,2048]{2,1,0:T(8,128)(2,1)}), bf16[16,16,2048]{2,1,0:T(8,128)(2,1)S(1)}, u32[]{:S(2)}, u32[]{:S(2)}) %all-to-all-start) | async-done | bytes 1048608 | tf_op jit(solution)/shard_map/all_to_all | solution.py:631
  115.8 21.2 %collective-permute-done = bf16[256,2048]{1,0:T(8,128)(2,1)S(1)} collective-permute-done((bf16[256,2048]{1,0:T(8,128)(2,1)S(1)}, bf16[256,2048]{1,0:T(8,128)(2,1)S(1)}, u32[]{:S(2)}, u32[]{:S(2)}) %collective-permute-start) | collective-permute-done | bytes 1048608 | tf_op jit(solution)/shard_map/ppermute | solution.py:580
  142.2 6.7 pick_halves.3
  148.9 35.6 %all-gather.5.cloned.1.call-done = bf16[2048,6528]{1,0:T(8,128)(2,1)} async-done(((bf16[128,6528]{1,0:T(8,128)(2,1)}), bf16[2048,6528]{1,0:T(8,128)(2,1)}) %all-gather.5.cloned.1.call-update) | async-done | bytes 26738704 | tf_op jit(solution)/shard_map/all_gather | solution.py:600
  195.7 8.0 fusion.68.gate_ref
  203.7 7.9 fusion.70.signal_ref
  211.7 20.9 %state_forward.1 = (f32[512,1536]{1,0:T(8,128)}, f32[512,128]{1,0:T(8,128)}) custom-call(f32[512,1536]{1,0:T(8,128)} %fusion.70.signal_ref, f32[512,1536]{1,0:T(8,128)} %fusion.68.gate_ref, f32[5,1536]{1,0:T(8,128)S(1)} %copy-done.49, f32[1,1536]{1,0:T(1,128)S(1)} %broadcast_in_dim_reshape.2.skip_ref, bf16[512,512]{1,0:T(8,128)(2,1)S(1)} %copy-done.14, ...), custom_call_target="tpu_custom_call" | custom-call | flops 1610612736 | bytes 9437184 | tf_op jit(solution)/shard_map/state_forward/pallas_call | solution.py:481
  238.5 4.0 fusion.73.query_ref
  242.5 8.2 attention_forward.1
  250.8 4.4 multiply_convert_fusion.5
  255.1 17.8 %fusion.66 = f32[512,2048]{1,0:T(8,128)S(1)} fusion(bf16[512,1536]{1,0:T(8,128)(2,1)S(1)} %multiply_convert_fusion.5, bf16[2048,6528]{1,0:T(8,128)(2,1)} %all-gather.5.cloned.1.call-done), kind=kOutput, calls=%fused_computation.121 | convolution fusion | flops 3221225472 | bytes 12058624 | tf_op jit(solution)/shard_map/dot_general | solution.py:30
  277.1 46.4 %collective-permute-done.3 = bf16[512,2048]{1,0:T(8,128)(2,1)} collective-permute-done((bf16[512,2048]{1,0:T(8,128)(2,1)S(1)}, bf16[512,2048]{1,0:T(8,128)(2,1)}, u32[]{:S(2)}, u32[]{:S(2)}) %collective-permute-start.3) | collective-permute-done | bytes 2097184 | tf_op jit(solution)/shard_map/ppermute | solution.py:580
  323.5 6.0 fusion.95
  331.4 45.8 %conditional.16 = (bf16[512,2048]{1,0:T(8,128)(2,1)}, bf16[512,2048]{1,0:T(8,128)(2,1)}, bf16[512,2048]{1,0:T(8,128)(2,1)}, bf16[256,2048]{1,0:T(8,128)(2,1)S(1)...) conditional(s32[]{:T(128)} %convert_element_type.488, () %tuple.161, (bf16[2048,6144]{1,0:T(8,128)(2,1)}, ...), branch_computations={%region_7.8_spmd, %region_8.11_spmd} | conditional | flops 21501050880 | bytes 124814440 | solution.py:722
  331.4 6.9 fusion.4
  338.3 7.0 fusion.8
  345.4 10.2 %multiply_convert_fusion = (bf16[512,2048]{1,0:T(8,128)(2,1)}, bf16[512,2048]{1,0:T(8,128)(2,1)}, bf16[512,2048]{1,0:T(8,128)(2,1)}) fusion(f32[512,2048]{1,0:T(8,128)S(1)} %fusion.8, f32[512,2048]{1,0:T(8,128)S(1)} %fusion.4, bf16[512,2048]{1,0:T(8,128)(2,1)S(1)} %copy-done.12, bf16[2048,6144]{1,0:T(8,128)(2,1)} %get-tuple-element.309), kind=kOutput, calls=%fused_computation.11 | convolution fusion | flops 4310695936 | bytes 25165824 | tf_op jit(solution)/shard_map/cond/branch_1_fun/dot_general | solution.py:26
  355.5 6.2 fusion.2
  361.8 6.3 multiply_reduce_fusion
  368.5 8.3 convert_bitcast_fusion
  378.6 13.9 %conditional.17 = (bf16[256,2048]{1,0:T(8,128)(2,1)}, f32[2048]{0:T(1024)}) conditional(s32[]{:T(128)} %convert_element_type.514, () %tuple.165, (f32[512,1]{0,1:T(1,128)S(1)}, bf16[512,2048]{1,0:T(8,128)(2,1)}, bf16[2048,6144]{1,0:T(8,128)(2,1)}, bf16[512,2048]{1,0:T(8,128)(2,1)}, f32[2048]{0:T(1024)S(1)}, ...), branch_computations={%region_11.12_spmd, %region_12.15_spmd} | conditional | flops 4301257728 | bytes 49316908 | solution.py:722
  378.6 6.2 fusion.18
  384.8 6.3 multiply_reduce_fusion.2
  394.0 16.9 %conditional.18 = (bf16[512,1024]{1,0:T(8,128)(2,1)}, bf16[1024,2048]{1,0:T(8,128)(2,1)}, bf16[1024,2048]{1,0:T(8,128)(2,1)}) conditional(s32[]{:T(128)} %convert_element_type.515, () %tuple.168, (s32[16]{0:T(128)S(1)}, bf16[512,2048]{1,0:T(8,128)(2,1)S(1)}, bf16[512,2048]{1,0:T(8,128)(2,1)}, bf16[512,2048]{1,0:T(8,128)(2,1)}) %tuple.169), branch_computations={%region_15.16_spmd, %region_16.17_spmd} | conditional | flops 4299161600 | bytes 23068724 | solution.py:722
  394.0 4.1 pick_halves.2
  398.1 6.7 convolution_convert_fusion
  404.8 6.1 convolution_convert_fusion.1
  411.5 9.9 %conditional.19 = (bf16[256,2048]{1,0:T(8,128)(2,1)S(1)}, bf16[256,2048]{1,0:T(8,128)(2,1)}) conditional(s32[]{:T(128)} %convert_element_type.516, () %tuple.172, (bf16[2048,6144]{1,0:T(8,128)(2,1)}, bf16[512,2048]{1,0:T(8,128)(2,1)}, s32[]{:T(128)}) %tuple.173), branch_computations={%region_17.18_spmd, %region_18.19_spmd} | conditional | flops 4296015872 | bytes 16777320 | solution.py:722
  411.6 8.5 %fusion.31 = bf16[512,2048]{1,0:T(8,128)(2,1)S(1)} fusion(bf16[512,2048]{1,0:T(8,128)(2,1)} %get-tuple-element.326, bf16[2048,6144]{1,0:T(8,128)(2,1)} %get-tuple-element.327), kind=kOutput, calls=%fused_computation.42 | convolution fusion | flops 4296015872 | bytes 12582912 | tf_op jit(solution)/shard_map/cond/branch_1_fun/dot_general | solution.py:30
  421.8 3.9 collective-permute-done.5.values_ref
  425.8 16.4 %conditional.20 = (bf16[512,2048]{1,0:T(8,128)(2,1)}, bf16[1,2,2,128,2048]{4,3,2,1,0:T(8,128)(2,1)}, bf16[512,2048]{1,0:T(8,128)(2,1)}, bf16[2,1,2,128,2048]{4,3,2,1,0:T(8,128)(2,1)}) conditional(s32[]{:T(128)} %convert_element_type.517, () %tuple.175, (bf16[512,1024]{1,0:T(8,128)(2,1)}, bf16[512,2048]{1,0:T(8,128)(2,1)}, ...), branch_computations={%region_19.20_spmd, %region_20.21_spmd} | conditional | flops 4307550208 | bytes 39845920 | solution.py:722
  425.8 5.6 add_convert_fusion.1
  434.0 5.6 add_convert_fusion
  443.1 10.9 %collective-permute-start.11 = (bf16[512,2048]{1,0:T(8,128)(2,1)}, bf16[512,2048]{1,0:T(8,128)(2,1)}, u32[]{:S(2)}, u32[]{:S(2)}) collective-permute-start(bf16[512,2048]{1,0:T(8,128)(2,1)} %get-tuple-element.647), channel_id=1, source_target_pairs={{0,8},{2,10},{4,12},{6,14},{8,0},{10,2},{12,4},{14,6},{16,24},{18,... | collective-permute-start | bytes 6291464 | tf_op jit(solution)/shard_map/ppermute | solution.py:583
  454.2 29.8 %conditional.21 = (f32[512]{0:T(512)S(1)}, f32[256,2048]{1,0:T(8,128)}, f32[512,1536]{1,0:T(8,128)}, bf16[512,2048]{1,0:T(8,128)(2,1)}, bf16[512,768]{1,0:T(8,128)(2,1)S(1)}) conditional(s32[]{:T(128)} %convert_element_type.518, () %tuple.179, (bf16[512,2048]{1,0:T(8,128)(2,1)}, bf16[256,2048]{1,0:T(8,128)(2,1)}, bf16[256,2048]{1,0:T(8,128)(2,1)}, ...), branch_computations={%region_21.22_spmd, %region_22.24_spmd} | conditional | flops 4979949056 | bytes 83370136 | solution.py:722
  462.8 8.9 %multiply_reduce_fusion.4 = (f32[512]{0:T(512)S(1)}, f32[512,1536]{1,0:T(8,128)}) fusion(f32[512,1536]{1,0:T(8,128)S(1)} %copy-done.11, f32[512,1536]{1,0:T(8,128)S(1)} %copy-done.4, f32[1536]{0:T(1024)S(1)} %get-tuple-element.340, bf16[512,2048]{1,0:T(8,128)(2,1)} %get-tuple-element.1069, bf16[2048,6528]{1,0:T(8,128)(2,1)} %get-tuple-element.339), kind=kOutput, calls=%fused_computation.50 | convolution fusion | flops 3227516416 | bytes 17833984 | tf_op jit(solution)/shard_map/cond/branch_1_fun/dot_general | solution.py:26
  471.7 4.3 fusion.38.grad_ref
  476.0 8.0 attention_backward.1
  484.9 12.1 %conditional.22 = (bf16[2048,2048]{1,0:T(8,128)(2,1)}, bf16[256,2048]{0,1:T(8,128)(2,1)S(1)}) conditional(s32[]{:T(128)} %convert_element_type.519, () %tuple.182, (bf16[512,1536]{1,0:T(8,128)(2,1)}, bf16[512,512]{1,0:T(8,128)(2,1)}, bf16[512,2048]{1,0:T(8,128)(2,1)}, bf16[512,2048]{1,0:T(8,128)(2,1)S(1)}, s32[]{:T(128)}, ...), branch_computations={%region_24.25_spmd, %region_25.26_spmd} | conditional | flops 4575461376 | bytes 31588488 | solution.py:722
  488.5 8.5 %convert_bitcast_fusion.1 = bf16[2048,2048]{1,0:T(8,128)(2,1)} fusion(bf16[512,2048]{1,0:T(8,128)(2,1)} %get-tuple-element.353, bf16[512,512]{1,0:T(8,128)(2,1)S(1)} %copy-done.42, bf16[512,1536]{1,0:T(8,128)(2,1)S(1)} %copy-done.32), kind=kOutput, calls=%fused_computation.57 | convolution fusion | flops 4303355904 | bytes 12582912 | tf_op jit(solution)/shard_map/cond/branch_1_fun/dot_general | solution.py:34
  498.4 3.9 all-to-all-start.2
  506.9 50.6 %conditional.23 = (f32[2,8,1536]{2,1,0:T(8,128)}, f32[2,8,512]{2,1,0:T(8,128)}, f32[2,24,2]{2,1,0:T(8,128)}, bf16[512,4480]{1,0:T(8,128)(2,1)}) conditional(s32[]{:T(128)} %convert_element_type.521, () %tuple.185, (f32[1536]{0:T(1024)}, f32[512]{0:T(512)}, f32[512]{0:T(512)}, f32[512]{0:T(512)}, f32[512,2]{0,1:T(2,128)S(1)}, ...), branch_computations={%region_26.27_spmd, %region_27.28_spmd} | conditional | flops 4026538496 | bytes 15904996 | solution.py:722
  516.6 40.9 %state_backward.1 = (bf16[512,4480]{1,0:T(8,128)(2,1)}, f32[2,8,1536]{2,1,0:T(8,128)}, f32[2,8,512]{2,1,0:T(8,128)}, f32[2,24,2]{2,1,0:T(8,128)}) custom-call(f32[512,1536]{1,0:T(8,128)} %get-tuple-element.359.grad_ref, f32[512,1536]{1,0:T(8,128)} %get-tuple-element.360.out_ref, f32[512,1536]{1,0:T(8,128)} %get-tuple-element.361.gate_ref, ...), custom_call_target="tpu_custom_call" | custom-call | flops 4026531840 | bytes 15728640 | tf_op jit(solution)/shard_map/cond/branch_1_fun/state_backward/pallas_call | solution.py:506
  558.6 17.9 %conditional.24 = (bf16[1024,4480]{1,0:T(8,128)(2,1)}, bf16[256,2048]{1,0:T(8,128)(2,1)}, bf16[1,1,2,128,2048]{4,3,2,1,0:T(8,128)(2,1)S(1)}, bf16[256,2048]{1,0:T(8,128)(2,1)}, bf16[1,1,2,128,2048]{4,3,2,1,0:T(8,128)(2,1)}) conditional(s32[]{:T(128)} %convert_element_type.522, () %tuple.189, (bf16[512,1024]{1,0:T(8,128)(2,1)}, ...), branch_computations={%region_29.30_spmd, %region_30.31_spmd} | conditional | flops 4710596608 | bytes 39977028 | solution.py:722
  566.7 9.8 %convolution_convert_fusion.3 = bf16[1024,4480]{1,0:T(8,128)(2,1)} fusion(bf16[512,1024]{1,0:T(8,128)(2,1)S(1)} %copy-done.76, bf16[512,4480]{1,0:T(8,128)(2,1)} %get-tuple-element.386), kind=kOutput, calls=%fused_computation.70 | convolution fusion | flops 4702208000 | bytes 14811136 | tf_op jit(solution)/shard_map/cond/branch_1_fun/dot_general | solution.py:34
  580.0 23.0 %conditional.25 = (f32[2048]{0:T(1024)S(1)}, bf16[256,2048]{1,0:T(8,128)(2,1)}, bf16[256,2048]{1,0:T(8,128)(2,1)S(1)}) conditional(s32[]{:T(128)} %convert_element_type.523, () %tuple.192, (bf16[2048,6528]{1,0:T(8,128)(2,1)}, bf16[512,4480]{1,0:T(8,128)(2,1)}, f32[512,2048]{1,0:T(8,128)}, f32[2,2,128]{2,1,0:T(2,128)S(1)}, f32[]{:T(128)}, ...), branch_computations={%region_31.32_spmd, %region_32.35_spmd} | conditional | flops 9406776320 | bytes 46049396 | solution.py:722
  580.2 17.5 %multiply_reduce_fusion.5 = (f32[512]{0:T(512)S(1)}, f32[2048]{0:T(1024)S(1)}, f32[512,2048]{1,0:T(8,128)}) fusion(f32[512,2048]{1,0:T(8,128)} %get-tuple-element.393, f32[2048]{0:T(1024)S(1)} %get-tuple-element.397, f32[512]{0:T(512)S(1)} %bitcast.296, bf16[512,4480]{1,0:T(8,128)(2,1)} %get-tuple-element.391, bf16[2048,6528]{1,0:T(8,128)(2,1)} %get-tuple-element.392), kind=kOutput, calls=%fused_computation.78 | convolution fusion | flops 9401530368 | bytes 31346688 | tf_op jit(solution)/shard_map/cond/branch_1_fun/dot_general | solution.py:30
  597.8 4.2 subtract_convert_fusion.2
  603.1 9.2 %collective-permute-done.13 = bf16[256,2048]{1,0:T(8,128)(2,1)} collective-permute-done((bf16[256,2048]{1,0:T(8,128)(2,1)}, bf16[256,2048]{1,0:T(8,128)(2,1)}, u32[]{:S(2)}, u32[]{:S(2)}) %collective-permute-start.13) | collective-permute-done | bytes 1048608 | tf_op jit(solution)/shard_map/ppermute | solution.py:583
  615.4 19.7 %conditional.26 = (bf16[512,2688]{1,0:T(8,128)(2,1)}, bf16[1,2,2,128,2688]{4,3,2,1,0:T(8,128)(2,1)}, bf16[512,1792]{1,0:T(8,128)(2,1)}, bf16[2,1,2,128,1792]{4,3...) conditional(s32[]{:T(128)} %convert_element_type.524, ...), branch_computations={%region_35.36_spmd, %region_36.37_spmd} | conditional | flops 4715577344 | bytes 59113572 | solution.py:722
  615.4 9.5 %add_convert_fusion.2 = bf16[1024,4480]{1,0:T(8,128)(2,1)S(1)} fusion(bf16[1024,4480]{1,0:T(8,128)(2,1)} %get-tuple-element.401, bf16[512,1024]{1,0:T(8,128)(2,1)} %get-tuple-element.399, bf16[512,4480]{1,0:T(8,128)(2,1)} %get-tuple-element.400), kind=kOutput, calls=%fused_computation.86 | convolution fusion | flops 4711383040 | bytes 23986176 | tf_op jit(solution)/shard_map/cond/branch_1_fun/dot_general | solution.py:34
  643.7 45.0 %collective-permute-done.15 = bf16[128,2048]{1,0:T(8,128)(2,1)} collective-permute-done((bf16[128,2048]{1,0:T(8,128)(2,1)}, bf16[128,2048]{1,0:T(8,128)(2,1)}, u32[]{:S(2)}, u32[]{:S(2)}) %collective-permute-start.15) | collective-permute-done | bytes 524320 | tf_op jit(solution)/shard_map/ppermute | solution.py:583
  688.7 9.3 %collective-permute-done.16 = bf16[128,2048]{1,0:T(8,128)(2,1)} collective-permute-done((bf16[128,2048]{1,0:T(8,128)(2,1)}, bf16[128,2048]{1,0:T(8,128)(2,1)}, u32[]{:S(2)}, u32[]{:S(2)}) %collective-permute-start.16) | collective-permute-done | bytes 524320 | tf_op jit(solution)/shard_map/ppermute | solution.py:583
  700.0 11.7 %conditional.28 = (bf16[256,2688]{1,0:T(8,128)(2,1)}, bf16[1,1,2,128,2688]{4,3,2,1,0:T(8,128)(2,1)}, bf16[256,1792]{1,0:T(8,128)(2,1)S(1)}, bf16[1,1,2,128,1792]...) conditional(s32[]{:T(128)} %convert_element_type.526, () %tuple.202, ...), branch_computations={%region_43.44_spmd, %region_44.45_spmd} | conditional | flops 280788992 | bytes 37093480 | solution.py:722
  723.0 30.5 %collective-permute-done.23 = f32[16,2048]{1,0:T(8,128)} collective-permute-done((f32[16,2048]{1,0:T(8,128)S(1)}, f32[16,2048]{1,0:T(8,128)}, u32[]{:S(2)}, u32[]{:S(2)}) %collective-permute-start.23) | collective-permute-done | bytes 131104 | tf_op jit(solution)/shard_map/ppermute | solution.py:583
  753.5 4.2 collective-permute-done.21
  758.8 7.4 conditional.29
  769.1 25.6 %collective-permute-done.24 = f32[16,2048]{1,0:T(8,128)} collective-permute-done((f32[16,2048]{1,0:T(8,128)}, f32[16,2048]{1,0:T(8,128)}, u32[]{:S(2)}, u32[]{:S(2)}) %collective-permute-start.24) | collective-permute-done | bytes 131104 | tf_op jit(solution)/shard_map/ppermute | solution.py:583
  794.7 9.0 %conditional.30 = (f32[128,2048]{1,0:T(8,128)}, f32[128,2048]{1,0:T(8,128)}, f32[128,2048]{1,0:T(8,128)}, bf16[2,128,2048]{2,1,0:T(8,128)(2,1)}, f32[16,2048]{1,...) conditional(s32[]{:T(128)} %convert_element_type.528, () %tuple.208, ...), branch_computations={%region_47.48_spmd, %region_48.49_spmd} | conditional | flops 270827520 | bytes 12582996 | solution.py:722
  804.8 17.6 %collective-permute-done.27 = f32[16,2048]{1,0:T(8,128)S(1)} collective-permute-done((f32[16,2048]{1,0:T(8,128)}, f32[16,2048]{1,0:T(8,128)S(1)}, u32[]{:S(2)}, u32[]{:S(2)}) %collective-permute-start.27) | collective-permute-done | bytes 131104 | tf_op jit(solution)/shard_map/ppermute | solution.py:583
  822.5 8.2 conditional.31
  (382 shorter events, 196.2 us)
Async XLA Ops:
  7.2 12.4 %copy-start = (bf16[2,128,2048]{2,1,0:T(8,128)(2,1)S(1)}, bf16[2,128,2048]{2,1,0:T(8,128)(2,1)}, u32[]{:S(2)}) copy-start(bf16[2,128,2048]{2,1,0:T(8,128)(2,1)} %param.58) | copy-start | bytes 3145732
  7.2 177.3 %all-gather.5.cloned.1.call-start = ((), (), s32[]{:S(2)}) async-start(), calls=%async_computation.7 | async-start | bytes 28409856 | tf_op jit(solution)/shard_map/all_gather | solution.py:600
  11.6 319.8 %all-gather.3.cloned.1.call-start = ((), (), s32[]{:S(2)}) async-start(), calls=%async_computation.6 | async-start | bytes 26738688 | tf_op jit(solution)/shard_map/all_gather | solution.py:600
  19.6 92.2 %copy-start.69 = (s32[256]{0:T(256)}, s32[256]{0:T(256)S(1)}, u32[]{:S(2)}) copy-start(s32[256]{0:T(256)S(1)} %get-tuple-element.1021) | copy-start | bytes 3076
  21.1 47.3 %all-to-all-start.1 = ((bf16[16,16,2048]{2,1,0:T(8,128)(2,1)}), bf16[16,16,2048]{2,1,0:T(8,128)(2,1)S(1)}, u32[]{:S(2)}, u32[]{:S(2)}) async-start(bf16[16,16,2048]{2,1,0:T(8,128)(2,1)} %bitcast.83), calls=%async_computation.1 | async-start | bytes 2097152 | tf_op jit(solution)/shard_map/all_to_all | solution.py:631
  28.7 43.6 %copy-start.75 = (f32[24]{0:T(128)S(1)}, f32[24]{0:T(128)}, u32[]{:S(2)}) copy-start(f32[24]{0:T(128)} %param.80) | copy-start | bytes 292
  68.3 43.5 %all-to-all-start = ((bf16[16,16,2048]{2,1,0:T(8,128)(2,1)}), bf16[16,16,2048]{2,1,0:T(8,128)(2,1)S(1)}, u32[]{:S(2)}, u32[]{:S(2)}) async-start(bf16[16,16,2048]{2,1,0:T(8,128)(2,1)} %bitcast.74), calls=%async_computation | async-start | bytes 2097152 | tf_op jit(solution)/shard_map/all_to_all | solution.py:631
  72.0 485.6 %reduce-scatter.3.cloned.1.call-start = ((), (), s32[]{:S(2)}) async-start(), calls=%async_computation.8 | async-start | bytes 8912896 | tf_op jit(solution)/shard_map/reduce_scatter | solution.py:805
  72.3 170.2 %copy-start.53 = (f32[2,1,256]{2,1,0:T(1,128)}, f32[2,1,256]{2,1,0:T(1,128)S(1)}, u32[]{:S(2)}) copy-start(f32[2,1,256]{2,1,0:T(1,128)S(1)} %convert_element_type.502.seg_row_ref) | copy-start | bytes 6148
  72.5 139.2 %copy-start.51 = (f32[1,1536]{1,0:T(1,128)}, f32[1,1536]{1,0:T(1,128)S(1)}, u32[]{:S(2)}) copy-start(f32[1,1536]{1,0:T(1,128)S(1)} %broadcast_in_dim_reshape.2.skip_ref) | copy-start | bytes 18436
  72.6 169.9 %copy-start.16 = (f32[512,8]{1,0:T(8,128)}, f32[512,8]{1,0:T(8,128)S(1)}, u32[]{:S(2)}) copy-start(f32[512,8]{1,0:T(8,128)S(1)} %pad.21.columns_ref) | copy-start | bytes 49156
  74.1 39.8 %copy-start.78 = (f32[24]{0:T(128)S(1)}, f32[24]{0:T(128)}, u32[]{:S(2)}) copy-start(f32[24]{0:T(128)} %param.79) | copy-start | bytes 292
  74.1 39.8 %collective-permute-start.1 = (bf16[256,2048]{1,0:T(8,128)(2,1)S(1)}, bf16[256,2048]{1,0:T(8,128)(2,1)S(1)}, u32[]{:S(2)}, u32[]{:S(2)}) collective-permute-start(bf16[256,2048]{1,0:T(8,128)(2,1)S(1)} %convolution_convert_fusion.7), channel_id=1, source_target_pairs={{0,1},{1,0},{2,3},{3,2},{4,5},{5,4},{6,7},{7,6},{8,9},{9,8},{10,11... | collective-permute-start | bytes 3145736 | tf_op jit(solution)/shard_map/ppermute | solution.py:580
  112.3 24.7 %collective-permute-start = (bf16[256,2048]{1,0:T(8,128)(2,1)S(1)}, bf16[256,2048]{1,0:T(8,128)(2,1)S(1)}, u32[]{:S(2)}, u32[]{:S(2)}) collective-permute-start(bf16[256,2048]{1,0:T(8,128)(2,1)S(1)} %convolution_convert_fusion.9), channel_id=1, source_target_pairs={{0,1},{1,0},{2,3},{3,2},{4,5},{5,4},{6,7},{7,6},{8,9},{9,8},{10,11... | collective-permute-start | bytes 3145736 | tf_op jit(solution)/shard_map/ppermute | solution.py:580
  113.9 73.0 %copy-start.72 = (f32[24]{0:T(128)}, f32[24]{0:T(128)S(1)}, u32[]{:S(2)}) copy-start(f32[24]{0:T(128)S(1)} %exponential_negate_fusion) | copy-start | bytes 292
  142.2 42.3 %copy-start.3 = (bf16[512,2048]{1,0:T(8,128)(2,1)S(1)}, bf16[512,2048]{1,0:T(8,128)(2,1)}, u32[]{:S(2)}) copy-start(bf16[512,2048]{1,0:T(8,128)(2,1)} %multiply_convert_fusion.4.first_ref.second_ref) | copy-start | bytes 6291460
  142.2 42.3 %copy-start.74 = (f32[24]{0:T(128)S(1)}, f32[24]{0:T(128)}, u32[]{:S(2)}) copy-start(f32[24]{0:T(128)} %param.78) | copy-start | bytes 292
  190.8 20.9 %copy-start.46 = (f32[2,12,2,256]{3,2,1,0:T(2,128)}, f32[2,12,2,256]{3,2,1,0:T(2,128)S(1)}, u32[]{:S(2)}) copy-start(f32[2,12,2,256]{3,2,1,0:T(2,128)S(1)} %reshape.700.step_ref) | copy-start | bytes 147460
  233.8 17.0 %collective-permute-start.2 = (f32[512]{0:T(512)S(1)}, f32[512]{0:T(512)S(1)}, u32[]{:S(2)}, u32[]{:S(2)}) collective-permute-start(f32[512]{0:T(512)S(1)} %reduce_sum.175), channel_id=1, source_target_pairs={{0,1},{1,0},{2,3},{3,2},{4,5},{5,4},{6,7},{7,6},{8,9},{9,8},{10,11... | collective-permute-start | bytes 6152 | tf_op jit(solution)/shard_map/ppermute | solution.py:580
  250.7 22.2 %copy-start.41 = (bf16[512,512]{1,0:T(8,128)(2,1)}, bf16[512,512]{1,0:T(8,128)(2,1)S(1)}, u32[]{:S(2)}) copy-start(bf16[512,512]{1,0:T(8,128)(2,1)S(1)} %get-tuple-element.601) | copy-start | bytes 1572868
  255.1 17.8 %copy-start.31 = (bf16[512,1536]{1,0:T(8,128)(2,1)}, bf16[512,1536]{1,0:T(8,128)(2,1)S(1)}, u32[]{:S(2)}) copy-start(bf16[512,1536]{1,0:T(8,128)(2,1)S(1)} %multiply_convert_fusion.5) | copy-start | bytes 4718596
  275.9 47.7 %collective-permute-start.3 = (bf16[512,2048]{1,0:T(8,128)(2,1)S(1)}, bf16[512,2048]{1,0:T(8,128)(2,1)}, u32[]{:S(2)}, u32[]{:S(2)}) collective-permute-start(bf16[512,2048]{1,0:T(8,128)(2,1)S(1)} %add_convert_fusion.6), channel_id=1, source_target_pairs={{0,1},{1,0},{2,3},{3,2},{4,5},{5,4},{6,7},{7,6},{8,9},{9,8},{10,11... | collective-permute-start | bytes 6291464 | tf_op jit(solution)/shard_map/ppermute | solution.py:580
  378.1 33.3 %collective-permute-start.4 = (bf16[256,2048]{1,0:T(8,128)(2,1)S(1)}, bf16[256,2048]{1,0:T(8,128)(2,1)}, u32[]{:S(2)}, u32[]{:S(2)}) collective-permute-start(bf16[256,2048]{1,0:T(8,128)(2,1)S(1)} %get-tuple-element.610), channel_id=1, source_target_pairs={{0,1},{1,0},{2,3},{3,2},{4,5},{5,4},{6,7},{7,6},{8,9},{9,8},{10,11... | collective-permute-start | bytes 3145736 | tf_op jit(solution)/shard_map/ppermute | solution.py:580
  392.4 33.3 %collective-permute-start.5 = (bf16[256,2048]{1,0:T(8,128)(2,1)}, bf16[256,2048]{1,0:T(8,128)(2,1)}, u32[]{:S(2)}, u32[]{:S(2)}) collective-permute-start(bf16[256,2048]{1,0:T(8,128)(2,1)} %get-tuple-element.616), channel_id=1, source_target_pairs={{0,1},{1,0},{2,3},{3,2},{4,5},{5,4},{6,7},{7,6},{8,9},{9,8},{10,11... | collective-permute-start | bytes 3145736 | tf_op jit(solution)/shard_map/ppermute | solution.py:580
  410.9 14.8 %collective-permute-start.6 = (bf16[1024,2048]{1,0:T(8,128)(2,1)}, bf16[1024,2048]{1,0:T(8,128)(2,1)}, u32[]{:S(2)}, u32[]{:S(2)}) collective-permute-start(bf16[1024,2048]{1,0:T(8,128)(2,1)} %get-tuple-element.617), channel_id=1, source_target_pairs={{0,2},{2,0},{4,6},{6,4},{8,10},{10,8},{12,14},{14,12},{16,18},{18,... | collective-permute-start | bytes 12582920 | tf_op jit(solution)/shard_map/ppermute | solution.py:583
  410.9 14.8 %collective-permute-start.7 = (bf16[1024,2048]{1,0:T(8,128)(2,1)}, bf16[1024,2048]{1,0:T(8,128)(2,1)}, u32[]{:S(2)}, u32[]{:S(2)}) collective-permute-start(bf16[1024,2048]{1,0:T(8,128)(2,1)} %get-tuple-element.618), channel_id=1, source_target_pairs={{0,2},{2,0},{4,6},{6,4},{8,10},{10,8},{12,14},{14,12},{16,18},{18,... | collective-permute-start | bytes 12582920 | tf_op jit(solution)/shard_map/ppermute | solution.py:583
  421.3 62.8 %collective-permute-start.8 = (bf16[256,2048]{1,0:T(8,128)(2,1)}, bf16[256,2048]{1,0:T(8,128)(2,1)}, u32[]{:S(2)}, u32[]{:S(2)}) collective-permute-start(bf16[256,2048]{1,0:T(8,128)(2,1)} %get-tuple-element.632), channel_id=1, source_target_pairs={{0,1},{1,0},{2,3},{3,2},{4,5},{5,4},{6,7},{7,6},{8,9},{9,8},{10,11... | collective-permute-start | bytes 3145736 | tf_op jit(solution)/shard_map/ppermute | solution.py:580
  425.7 28.4 %copy-start.70 = (s32[256]{0:T(256)S(1)}, s32[256]{0:T(256)}, u32[]{:S(2)}) copy-start(s32[256]{0:T(256)} %copy-done.69) | copy-start | bytes 3076
  425.7 28.5 %copy-start.17 = (f32[512,8]{1,0:T(8,128)S(1)}, f32[512,8]{1,0:T(8,128)}, u32[]{:S(2)}) copy-start(f32[512,8]{1,0:T(8,128)} %copy-done.16) | copy-start | bytes 49156
  425.7 28.5 %copy-start.28 = (f32[512,128]{1,0:T(8,128)S(1)}, f32[512,128]{1,0:T(8,128)}, u32[]{:S(2)}) copy-start(f32[512,128]{1,0:T(8,128)} %get-tuple-element.1025.cosine_ref) | copy-start | bytes 786436
  425.7 28.5 %copy-start.54 = (f32[2,1,256]{2,1,0:T(1,128)S(1)}, f32[2,1,256]{2,1,0:T(1,128)}, u32[]{:S(2)}) copy-start(f32[2,1,256]{2,1,0:T(1,128)} %copy-done.53) | copy-start | bytes 6148
  425.8 28.5 %copy-start.60 = (f32[1536]{0:T(1024)S(1)}, f32[1536]{0:T(1024)}, u32[]{:S(2)}) copy-start(f32[1536]{0:T(1024)} %param.77) | copy-start | bytes 18436
  442.2 115.4 %collective-permute-start.10 = (bf16[512,2048]{1,0:T(8,128)(2,1)}, bf16[512,2048]{1,0:T(8,128)(2,1)}, u32[]{:S(2)}, u32[]{:S(2)}) collective-permute-start(bf16[512,2048]{1,0:T(8,128)(2,1)} %get-tuple-element.645), channel_id=1, source_target_pairs={{0,4},{2,6},{4,0},{6,2},{8,12},{10,14},{12,8},{14,10},{16,20},{18,... | collective-permute-start | bytes 6291464 | tf_op jit(solution)/shard_map/ppermute | solution.py:583
  443.1 114.4 %collective-permute-start.11 = (bf16[512,2048]{1,0:T(8,128)(2,1)}, bf16[512,2048]{1,0:T(8,128)(2,1)}, u32[]{:S(2)}, u32[]{:S(2)}) collective-permute-start(bf16[512,2048]{1,0:T(8,128)(2,1)} %get-tuple-element.647), channel_id=1, source_target_pairs={{0,8},{2,10},{4,12},{6,14},{8,0},{10,2},{12,4},{14,6},{16,24},{18,... | collective-permute-start | bytes 6291464 | tf_op jit(solution)/shard_map/ppermute | solution.py:583
  454.2 29.9 %copy-start.8 = (bf16[512,2048]{1,0:T(8,128)(2,1)S(1)}, bf16[512,2048]{1,0:T(8,128)(2,1)}, u32[]{:S(2)}) copy-start(bf16[512,2048]{1,0:T(8,128)(2,1)} %copy-done.7) | copy-start | bytes 6291460
  498.4 59.1 %all-to-all-start.2 = ((bf16[16,16,2048]{2,1,0:T(8,128)(2,1)}), bf16[16,16,2048]{2,1,0:T(8,128)(2,1)S(1)}, u32[]{:S(2)}, u32[]{:S(2)}) async-start(bf16[16,16,2048]{2,1,0:T(8,128)(2,1)} %bitcast.99), calls=%async_computation.3 | async-start | bytes 2097152 | tf_op jit(solution)/shard_map/all_to_all | solution.py:631
  502.4 186.3 %reduce-scatter.5.cloned.1.call-start = ((), (), s32[]{:S(2)}) async-start(), calls=%async_computation.9 | async-start | bytes 8912896 | tf_op jit(solution)/shard_map/reduce_scatter | solution.py:874
  502.9 4.0 collective-permute-start.9
  557.6 22.4 %copy-start.63 = (f32[2048]{0:T(1024)S(1)}, f32[2048]{0:T(1024)}, u32[]{:S(2)}) copy-start(f32[2048]{0:T(1024)} %param.73) | copy-start | bytes 24580
  557.6 22.4 %copy-start.65 = (f32[2,2,128]{2,1,0:T(2,128)S(1)}, f32[2,2,128]{2,1,0:T(2,128)}, u32[]{:S(2)}) copy-start(f32[2,2,128]{2,1,0:T(2,128)} %copy-done.64) | copy-start | bytes 6148
  576.5 38.9 %collective-permute-start.12 = (bf16[1024,4480]{1,0:T(8,128)(2,1)}, bf16[1024,4480]{1,0:T(8,128)(2,1)}, u32[]{:S(2)}, u32[]{:S(2)}) collective-permute-start(bf16[1024,4480]{1,0:T(8,128)(2,1)} %get-tuple-element.652), channel_id=1, source_target_pairs={{0,2},{2,0},{4,6},{6,4},{8,10},{10,8},{12,14},{14,12},{16,18},{18,... | collective-permute-start | bytes 27525128 | tf_op jit(solution)/shard_map/ppermute | solution.py:583
  576.5 35.8 %collective-permute-start.13 = (bf16[256,2048]{1,0:T(8,128)(2,1)}, bf16[256,2048]{1,0:T(8,128)(2,1)}, u32[]{:S(2)}, u32[]{:S(2)}) collective-permute-start(bf16[256,2048]{1,0:T(8,128)(2,1)} %get-tuple-element.655), channel_id=1, source_target_pairs={{0,8},{2,10},{4,12},{6,14},{8,0},{10,2},{12,4},{14,6},{16,24},{18,... | collective-permute-start | bytes 3145736 | tf_op jit(solution)/shard_map/ppermute | solution.py:583
  578.6 36.8 %collective-permute-start.14 = (bf16[256,2048]{1,0:T(8,128)(2,1)}, bf16[256,2048]{1,0:T(8,128)(2,1)}, u32[]{:S(2)}, u32[]{:S(2)}) collective-permute-start(bf16[256,2048]{1,0:T(8,128)(2,1)} %get-tuple-element.657), channel_id=1, source_target_pairs={{0,4},{2,6},{4,0},{6,2},{8,12},{10,14},{12,8},{14,10},{16,20},{18,... | collective-permute-start | bytes 3145736 | tf_op jit(solution)/shard_map/ppermute | solution.py:583
  615.4 24.9 %copy-start.73 = (f32[24]{0:T(128)S(1)}, f32[24]{0:T(128)}, u32[]{:S(2)}) copy-start(f32[24]{0:T(128)} %copy-done.72) | copy-start | bytes 292
  635.1 64.9 %collective-permute-start.17 = (bf16[512,2688]{1,0:T(8,128)(2,1)}, bf16[512,2688]{1,0:T(8,128)(2,1)}, u32[]{:S(2)}, u32[]{:S(2)}) collective-permute-start(bf16[512,2688]{1,0:T(8,128)(2,1)} %get-tuple-element.672), channel_id=1, source_target_pairs={{0,4},{2,6},{4,0},{6,2},{8,12},{10,14},{12,8},{14,10},{16,20},{18,... | collective-permute-start | bytes 8257544 | tf_op jit(solution)/shard_map/ppermute | solution.py:583
  636.3 63.7 %collective-permute-start.18 = (bf16[512,1792]{1,0:T(8,128)(2,1)}, bf16[512,1792]{1,0:T(8,128)(2,1)}, u32[]{:S(2)}, u32[]{:S(2)}) collective-permute-start(bf16[512,1792]{1,0:T(8,128)(2,1)} %get-tuple-element.674), channel_id=1, source_target_pairs={{0,8},{2,10},{4,12},{6,14},{8,0},{10,2},{12,4},{14,6},{16,24},{18,... | collective-permute-start | bytes 5505032 | tf_op jit(solution)/shard_map/ppermute | solution.py:583
  636.7 61.3 %collective-permute-start.20 = (bf16[256,2048]{1,0:T(8,128)(2,1)}, bf16[256,2048]{1,0:T(8,128)(2,1)S(1)}, u32[]{:S(2)}, u32[]{:S(2)}) collective-permute-start(bf16[256,2048]{1,0:T(8,128)(2,1)} %get-tuple-element.677), channel_id=1, source_target_pairs={{0,1},{1,0},{2,3},{3,2},{4,5},{5,4},{6,7},{7,6},{8,9},{9,8},{10,11... | collective-permute-start | bytes 3145736 | tf_op jit(solution)/shard_map/ppermute | solution.py:580
  637.4 51.3 %collective-permute-start.15 = (bf16[128,2048]{1,0:T(8,128)(2,1)}, bf16[128,2048]{1,0:T(8,128)(2,1)}, u32[]{:S(2)}, u32[]{:S(2)}) collective-permute-start(bf16[128,2048]{1,0:T(8,128)(2,1)} %get-tuple-element.667), channel_id=1, source_target_pairs={{0,16},{2,18},{4,20},{6,22},{8,24},{10,26},{12,28},{14,30},{16,0},... | collective-permute-start | bytes 1572872 | tf_op jit(solution)/shard_map/ppermute | solution.py:583
  639.7 58.3 %collective-permute-start.16 = (bf16[128,2048]{1,0:T(8,128)(2,1)}, bf16[128,2048]{1,0:T(8,128)(2,1)}, u32[]{:S(2)}, u32[]{:S(2)}) collective-permute-start(bf16[128,2048]{1,0:T(8,128)(2,1)} %get-tuple-element.668), channel_id=1, source_target_pairs={{0,16},{2,18},{4,20},{6,22},{8,24},{10,26},{12,28},{14,30},{16,0},... | collective-permute-start | bytes 1572872 | tf_op jit(solution)/shard_map/ppermute | solution.py:583
  688.7 9.3 %collective-permute-start.19 = (f32[16,2048]{1,0:T(8,128)S(1)}, f32[16,2048]{1,0:T(8,128)S(1)}, u32[]{:S(2)}, u32[]{:S(2)}) collective-permute-start(f32[16,2048]{1,0:T(8,128)S(1)} %get-tuple-element.1173), channel_id=1, source_target_pairs={{0,2},{2,0},{4,6},{6,4},{8,10},{10,8},{12,14},{14,12},{16,18},{18,... | collective-permute-start | bytes 393224 | tf_op jit(solution)/shard_map/ppermute | solution.py:583
  713.3 44.3 %collective-permute-start.21 = (bf16[256,2688]{1,0:T(8,128)(2,1)}, bf16[256,2688]{1,0:T(8,128)(2,1)S(1)}, u32[]{:S(2)}, u32[]{:S(2)}) collective-permute-start(bf16[256,2688]{1,0:T(8,128)(2,1)} %get-tuple-element.682), channel_id=1, source_target_pairs={{0,8},{2,10},{4,12},{6,14},{8,0},{10,2},{12,4},{14,6},{16,24},{18,... | collective-permute-start | bytes 4128776 | tf_op jit(solution)/shard_map/ppermute | solution.py:583
  717.1 105.4 %all-to-all-start.3 = ((bf16[16,16,2048]{2,1,0:T(8,128)(2,1)}), bf16[16,16,2048]{2,1,0:T(8,128)(2,1)S(1)}, u32[]{:S(2)}, u32[]{:S(2)}) async-start(bf16[16,16,2048]{2,1,0:T(8,128)(2,1)} %bitcast.101), calls=%async_computation.5 | async-start | bytes 2097152 | tf_op jit(solution)/shard_map/all_to_all | solution.py:631
  720.9 32.6 %collective-permute-start.22 = (bf16[256,1792]{1,0:T(8,128)(2,1)S(1)}, bf16[256,1792]{1,0:T(8,128)(2,1)}, u32[]{:S(2)}, u32[]{:S(2)}) collective-permute-start(bf16[256,1792]{1,0:T(8,128)(2,1)S(1)} %copy-done.38), channel_id=1, source_target_pairs={{0,4},{2,6},{4,0},{6,2},{8,12},{10,14},{12,8},{14,10},{16,20},{18,... | collective-permute-start | bytes 2752520 | tf_op jit(solution)/shard_map/ppermute | solution.py:583
  722.8 30.7 %collective-permute-start.23 = (f32[16,2048]{1,0:T(8,128)S(1)}, f32[16,2048]{1,0:T(8,128)}, u32[]{:S(2)}, u32[]{:S(2)}) collective-permute-start(f32[16,2048]{1,0:T(8,128)S(1)} %copy-done.44), channel_id=1, source_target_pairs={{0,4},{2,6},{4,0},{6,2},{8,12},{10,14},{12,8},{14,10},{16,20},{18,... | collective-permute-start | bytes 393224 | tf_op jit(solution)/shard_map/ppermute | solution.py:583
  758.8 36.0 %copy-start.19 = (bf16[16,16,2048]{2,1,0:T(8,128)(2,1)S(1)}, bf16[16,16,2048]{2,1,0:T(8,128)(2,1)}, u32[]{:S(2)}) copy-start(bf16[16,16,2048]{2,1,0:T(8,128)(2,1)} %copy-done.18) | copy-start | bytes 3145732
  758.8 36.0 %copy-start.30 = (bf16[128,2048]{1,0:T(8,128)(2,1)S(1)}, bf16[128,2048]{1,0:T(8,128)(2,1)}, u32[]{:S(2)}) copy-start(bf16[128,2048]{1,0:T(8,128)(2,1)} %reduce-scatter.5.cloned.1.call-done) | copy-start | bytes 1572868
  766.2 56.3 %collective-permute-start.25 = (bf16[128,2688]{1,0:T(8,128)(2,1)}, bf16[128,2688]{1,0:T(8,128)(2,1)}, u32[]{:S(2)}, u32[]{:S(2)}) collective-permute-start(bf16[128,2688]{1,0:T(8,128)(2,1)} %get-tuple-element.700), channel_id=1, source_target_pairs={{0,16},{2,18},{4,20},{6,22},{8,24},{10,26},{12,28},{14,30},{16,0},... | collective-permute-start | bytes 2064392 | tf_op jit(solution)/shard_map/ppermute | solution.py:583
  767.2 55.2 %collective-permute-start.26 = (bf16[128,1792]{1,0:T(8,128)(2,1)}, bf16[128,1792]{1,0:T(8,128)(2,1)}, u32[]{:S(2)}, u32[]{:S(2)}) collective-permute-start(bf16[128,1792]{1,0:T(8,128)(2,1)} %get-tuple-element.702), channel_id=1, source_target_pairs={{0,16},{2,18},{4,20},{6,22},{8,24},{10,26},{12,28},{14,30},{16,0},... | collective-permute-start | bytes 1376264 | tf_op jit(solution)/shard_map/ppermute | solution.py:583
  769.1 25.6 %collective-permute-start.24 = (f32[16,2048]{1,0:T(8,128)}, f32[16,2048]{1,0:T(8,128)}, u32[]{:S(2)}, u32[]{:S(2)}) collective-permute-start(f32[16,2048]{1,0:T(8,128)} %get-tuple-element.694), channel_id=1, source_target_pairs={{0,8},{2,10},{4,12},{6,14},{8,0},{10,2},{12,4},{14,6},{16,24},{18,... | collective-permute-start | bytes 393224 | tf_op jit(solution)/shard_map/ppermute | solution.py:583
  803.8 18.7 %collective-permute-start.27 = (f32[16,2048]{1,0:T(8,128)}, f32[16,2048]{1,0:T(8,128)S(1)}, u32[]{:S(2)}, u32[]{:S(2)}) collective-permute-start(f32[16,2048]{1,0:T(8,128)} %get-tuple-element.704), channel_id=1, source_target_pairs={{0,16},{2,18},{4,20},{6,22},{8,24},{10,26},{12,28},{14,30},{16,0},... | collective-permute-start | bytes 393224 | tf_op jit(solution)/shard_map/ppermute | solution.py:583
  830.6 11.8 %copy-start.48 = (f32[128,512]{1,0:T(8,128)}, f32[128,512]{1,0:T(8,128)S(1)}, u32[]{:S(2)}) copy-start(f32[128,512]{1,0:T(8,128)S(1)} %get-tuple-element.907) | copy-start | bytes 786436
  830.7 11.8 %copy-start.1 = (bf16[2,128,2048]{2,1,0:T(8,128)(2,1)S(1)}, bf16[2,128,2048]{2,1,0:T(8,128)(2,1)}, u32[]{:S(2)}) copy-start(bf16[2,128,2048]{2,1,0:T(8,128)(2,1)} %param.58) | copy-start | bytes 3145732
  830.7 6.4 collective-permute-start.29
  830.7 11.0 %collective-permute-start.28 = (f32[64,512]{1,0:T(8,128)}, f32[64,512]{1,0:T(8,128)S(1)}, u32[]{:S(2)}, u32[]{:S(2)}) collective-permute-start(f32[64,512]{1,0:T(8,128)} %get-tuple-element.715), channel_id=1, source_target_pairs={{0,1},{1,0},{2,3},{3,2},{4,5},{5,4},{6,7},{7,6},{8,9},{9,8},{10,11... | collective-permute-start | bytes 393224 | tf_op jit(solution)/shard_map/ppermute | solution.py:580
  (54 other events, 202.0 us)
Sparse Core Ops, SparseCore 0:
  11.7 172.8 all-gather.4
  186.1 138.4 all-gather.2
  377.3 139.0 reduce-scatter.2
  520.3 118.4 reduce-scatter.4
